TPU v7x, 32 devices: a whole 2x2x4 slice. The times are simulated.
32 devices in a mesh: wide: 8 (over z, y), narrow: 4 (over x, core).
Axes of the slice: x: 2, y: 2, z: 4, core: 2. Of those that a mesh axis runs over, the one named last changes fastest.
Arguments:
- tokens: bfloat16 [8, 1024, 2048], P('wide', 'narrow'), may hold values from -6 to 6
- w_in: bfloat16 [3, 2048, 2048], P(None, None, ('wide', 'narrow')), may hold values from -0.125 to 0.125
- w_out: bfloat16 [2048, 2048], P(('wide', 'narrow')), may hold values from -0.125 to 0.125
- gain_one: bfloat16 [2048], P(('wide', 'narrow')), may hold values from 0.5 to 1.5
- short_kernel: bfloat16 [3, 3, 2048], P(None, None, ('wide', 'narrow')), may hold values from -3 to 3
- decay_rate: bfloat16 [2048, 16], P(('wide', 'narrow')), may hold values from 0.00024414062 to 0.099609375
- pole_angle: bfloat16 [2048, 16], P(('wide', 'narrow')), may hold values from -3.140625 to 3.140625
- residue: bfloat16 [2048, 32], P(('wide', 'narrow')), may hold values from -0.1796875 to 0.1796875
- gain_two: bfloat16 [2048], P(('wide', 'narrow')), may hold values from 0.5 to 1.5
- w_gate: bfloat16 [2048, 5632], P(None, ('wide', 'narrow')), may hold values from -0.125 to 0.125
- w_up: bfloat16 [2048, 5632], P(None, ('wide', 'narrow')), may hold values from -0.125 to 0.125
- w_down: bfloat16 [2048, 5632], P(None, ('wide', 'narrow')), may hold values from -0.078125 to 0.078125
- doc_blocks: int32 [8, 3], P('wide'), may hold values from 1 to 4, 8 in all within a row
- doc_pad: int32 [8, 3], P('wide'), may hold values from 0 to 127
- cotangent: bfloat16 [8, 1024, 2048], P('wide', 'narrow'), may hold values from -6 to 6
Outputs:
- block_output: bfloat16 [8, 1024, 2048], P('wide', 'narrow')
- input_grad: bfloat16 [8, 1024, 2048], P('wide', 'narrow')
- grad_w_in: float32 [3, 2048, 2048], P(None, None, ('wide', 'narrow'))
- grad_w_out: float32 [2048, 2048], P(('wide', 'narrow'))
- grad_gain_one: float32 [2048], P(('wide', 'narrow'))
- grad_short_kernel: float32 [3, 3, 2048], P(None, None, ('wide', 'narrow'))
- grad_decay_rate: float32 [2048, 16], P(('wide', 'narrow'))
- grad_pole_angle: float32 [2048, 16], P(('wide', 'narrow'))
- grad_residue: float32 [2048, 32], P(('wide', 'narrow'))
- grad_gain_two: float32 [2048], P(('wide', 'narrow'))
- grad_w_gate: float32 [2048, 5632], P(None, ('wide', 'narrow'))
- grad_w_up: float32 [2048, 5632], P(None, ('wide', 'narrow'))
- grad_w_down: float32 [2048, 5632], P(None, ('wide', 'narrow'))
Inputs may be any that keep to these rules, and one draw needn't show every extreme that they name: `doc_blocks`: each row's 3 counts sum to 8, and the largest is exactly 4.
All inputs are finite; a program needn't handle non-finite values.
Results may differ from a plain program's by a relative error of at most 0.02.
Values may be sent and summed in bfloat16 or wider, within the bound.
No kernel may reach another device: no remote copies, remote signals or barrier semaphores. Data moves between devices by JAX's collectives and lax.ppermute only.
A program may use at most 216 MiB of HBM per device.

v0:
```python
from functools import partial

import jax
import jax.numpy as jnp
from jax import lax
from jax.sharding import PartitionSpec as P

BLOCK = 128


epsilon = 1e-06
highest = lax.Precision.HIGHEST
rows_only = (((0,), (0,)), ((), ()))
last_only = (((1,), (1,)), ((), ()))


def layout(doc_blocks, doc_pad, slots):
    block_ends = jnp.cumsum(doc_blocks) * BLOCK
    starts = block_ends - doc_blocks * BLOCK
    places = jnp.arange(slots, dtype=jnp.int32)
    living = (places[None, :] >= starts[:, None]) & (
        places[None, :] < (block_ends - doc_pad)[:, None]
    )
    live_mask = jnp.sum(living.astype(jnp.float32), axis=0)
    opening = jnp.sum((places[None, :] == starts[:, None]).astype(jnp.float32), axis=0)
    return (live_mask, opening)


def rms_norm(values, gain):
    return values * lax.rsqrt(jnp.mean(values * values, axis=-1, keepdims=True) + epsilon) * gain


def earlier(values):
    return jnp.concatenate([jnp.zeros_like(values[:1]), values[:-1]], axis=0)


def short_mix(masked, kernel_taps, opening):
    keep_one = (1.0 - opening)[:, None]
    keep_two = keep_one * earlier(keep_one)
    once = earlier(masked)
    return (
        kernel_taps[0] * masked
        + kernel_taps[1] * keep_one * once
        + kernel_taps[2] * keep_two * earlier(once)
    )


def powers(decay_rate, pole_angle, steps):
    lag_steps = jnp.arange(steps, dtype=jnp.float32)
    fading = jnp.exp(-decay_rate[:, :, None] * lag_steps)
    turning = pole_angle[:, :, None] * lag_steps
    return (fading * jnp.cos(turning), fading * jnp.sin(turning))


def long_conv(signal, decay_rate, pole_angle, residue, opening):
    pole_count = decay_rate.shape[1]
    block_count = signal.shape[0] // BLOCK
    power_re, power_im = powers(decay_rate, pole_angle, BLOCK + 1)
    resid_re = residue[:, :pole_count, None]
    resid_im = -residue[:, pole_count:, None]
    coeff_re = resid_re * power_re - resid_im * power_im
    coeff_im = resid_re * power_im + resid_im * power_re
    lag_index = jnp.arange(BLOCK, dtype=jnp.int32)
    onehot = (
        lag_index[:, None, None] == lag_index[None, :, None] - lag_index[None, None, :]
    ).astype(jnp.float32)
    toeplitz = jnp.einsum(
        "cl,lts->cts", jnp.sum(coeff_re[:, :, :BLOCK], axis=1), onehot, precision=highest
    )
    blocked = signal.reshape(block_count, BLOCK, signal.shape[1])
    within = jnp.einsum("cts,nsc->ntc", toeplitz, blocked, precision=highest)
    back_re = power_re[:, :, BLOCK - 1 :: -1]
    back_im = power_im[:, :, BLOCK - 1 :: -1]
    end_re = jnp.einsum("cjs,nsc->ncj", back_re, blocked, precision=highest)
    end_im = jnp.einsum("cjs,nsc->ncj", back_im, blocked, precision=highest)
    step_re = power_re[:, :, BLOCK]
    step_im = power_im[:, :, BLOCK]
    restarts = opening.reshape(block_count, BLOCK)[:, 0]

    def advance(state, pieces):
        carried_re, carried_im = state
        add_re, add_im, restart = pieces
        enter_re = carried_re * (1.0 - restart)
        enter_im = carried_im * (1.0 - restart)
        next_re = step_re * enter_re - step_im * enter_im + add_re
        next_im = step_re * enter_im + step_im * enter_re + add_im
        return ((next_re, next_im), (enter_re, enter_im))

    empty = jnp.zeros(step_re.shape, jnp.float32)
    _, (state_re, state_im) = lax.scan(advance, (empty, empty), (end_re, end_im, restarts))
    across = jnp.einsum(
        "cjt,ncj->ntc", coeff_re[:, :, 1:], state_re, precision=highest
    ) - jnp.einsum("cjt,ncj->ntc", coeff_im[:, :, 1:], state_im, precision=highest)
    return (within + across).reshape(signal.shape)


def mixer(opening, masked, kernel_taps, decay_rate, pole_angle, residue):
    channels = masked.shape[1] // 3
    short = short_mix(masked, kernel_taps, opening)
    streams = short[:, channels : 2 * channels] * short[:, 2 * channels :]
    return short[:, :channels] * long_conv(streams, decay_rate, pole_angle, residue, opening)


def fetch_mixer(w_in, w_out, short_kernel, decay_rate, pole_angle, residue):
    return tuple(
        (
            lax.all_gather(w_in, "wide", axis=2, tiled=True),
            lax.all_gather(w_out, "wide", axis=0, tiled=True),
            lax.all_gather(short_kernel, "wide", axis=2, tiled=True),
            lax.all_gather(decay_rate, "wide", axis=0, tiled=True),
            lax.all_gather(pole_angle, "wide", axis=0, tiled=True),
            lax.all_gather(residue, "wide", axis=0, tiled=True),
        )
    )


def fetch_mlp(w_gate, w_up, w_down):
    return tuple(
        (
            lax.all_gather(w_gate, "wide", axis=1, tiled=True),
            lax.all_gather(w_up, "wide", axis=1, tiled=True),
            lax.all_gather(w_down, "wide", axis=1, tiled=True),
        )
    )


def spread_rows(values):
    return lax.all_gather(values, "narrow", axis=1, tiled=True)


def sum_rows(values):
    return lax.psum_scatter(
        values.astype(jnp.bfloat16), "narrow", scatter_dimension=1, tiled=True
    ).astype(jnp.float32)


def body(
    tokens,
    w_in,
    w_out,
    gain_one,
    short_kernel,
    decay_rate,
    pole_angle,
    residue,
    gain_two,
    w_gate,
    w_up,
    w_down,
    doc_blocks,
    doc_pad,
    cotangent,
):
    group, local_rows, width = tokens.shape
    slots = local_rows * lax.axis_size("narrow")
    flat = group * slots
    live_mask, opening = jax.vmap(partial(layout, slots=slots))(doc_blocks, doc_pad)
    gain_first_low, gain_last_low = (
        lax.all_gather(gain_one, ("wide", "narrow"), axis=0, tiled=True),
        lax.all_gather(gain_two, ("wide", "narrow"), axis=0, tiled=True),
    )
    gain_first = gain_first_low.astype(jnp.float32)
    gain_last = gain_last_low.astype(jnp.float32)
    source = tokens.astype(jnp.float32)
    normed, first_pull = jax.vjp(rms_norm, source, gain_first)
    low_first = normed.astype(jnp.bfloat16)
    flat_first = spread_rows(low_first).reshape(flat, width)
    mixer_set = fetch_mixer(w_in, w_out, short_kernel, decay_rate, pole_angle, residue)
    in_all, out_all = (mixer_set[0], mixer_set[1])
    kernel_all, decay_all, angle_all, residue_all = tuple(
        (member.astype(jnp.float32) for member in mixer_set[2:])
    )
    channels = in_all.shape[2]
    projected = jnp.einsum("rd,sdc->rsc", flat_first, in_all, preferred_element_type=jnp.float32)
    masked = projected.reshape(group, slots, 3 * channels) * live_mask[:, :, None]
    taps = kernel_all.reshape(3, 3 * channels)
    mixer_rows = jax.vmap(mixer, in_axes=(0, 0, None, None, None, None))
    gated, mixer_pull = jax.vjp(
        partial(mixer_rows, opening), masked, taps, decay_all, angle_all, residue_all
    )
    flat_gated = gated.astype(jnp.bfloat16).reshape(flat, channels)
    mixer_out = sum_rows(
        jnp.dot(flat_gated, out_all, preferred_element_type=jnp.float32).reshape(
            group, slots, width
        )
    )
    middle = source + mixer_out
    gate_all, up_all, down_all = fetch_mlp(w_gate, w_up, w_down)
    normed_two, second_pull = jax.vjp(rms_norm, middle, gain_last)
    flat_second = spread_rows(normed_two.astype(jnp.bfloat16)).reshape(flat, width)
    gate_pre = jnp.dot(flat_second, gate_all, preferred_element_type=jnp.float32)
    up_pre = jnp.dot(flat_second, up_all, preferred_element_type=jnp.float32)
    sigmoid_gate = jax.nn.sigmoid(gate_pre)
    silu_gate = gate_pre * sigmoid_gate
    low_hidden = (silu_gate * up_pre).astype(jnp.bfloat16)
    down_out = sum_rows(
        lax.dot_general(
            low_hidden, down_all, last_only, preferred_element_type=jnp.float32
        ).reshape(group, slots, width)
    )
    block_output = (middle + down_out).astype(jnp.bfloat16)
    upstream = cotangent.astype(jnp.float32)
    flat_upstream = spread_rows(upstream.astype(jnp.bfloat16)).reshape(flat, width)
    gate_back, up_back, down_back = fetch_mlp(w_gate, w_up, w_down)
    d_hidden = jnp.dot(flat_upstream, down_back, preferred_element_type=jnp.float32)
    grad_down = lax.dot_general(
        flat_upstream, low_hidden, rows_only, preferred_element_type=jnp.float32
    )
    low_dgate = (d_hidden * up_pre * sigmoid_gate * (1.0 + gate_pre * (1.0 - sigmoid_gate))).astype(
        jnp.bfloat16
    )
    low_dup = (d_hidden * silu_gate).astype(jnp.bfloat16)
    grad_gate = lax.dot_general(
        flat_second, low_dgate, rows_only, preferred_element_type=jnp.float32
    )
    grad_up = lax.dot_general(flat_second, low_dup, rows_only, preferred_element_type=jnp.float32)
    d_second_part = lax.dot_general(
        low_dgate, gate_back, last_only, preferred_element_type=jnp.float32
    ) + lax.dot_general(low_dup, up_back, last_only, preferred_element_type=jnp.float32)
    d_normed_two = sum_rows(d_second_part.reshape(group, slots, width))
    d_middle_norm, grad_gain_two = second_pull(d_normed_two)
    d_middle = upstream + d_middle_norm
    gate_share, up_share, down_share = (
        lax.psum_scatter(
            grad_gate.astype(jnp.bfloat16), "wide", scatter_dimension=1, tiled=True
        ).astype(jnp.float32),
        lax.psum_scatter(
            grad_up.astype(jnp.bfloat16), "wide", scatter_dimension=1, tiled=True
        ).astype(jnp.float32),
        lax.psum_scatter(
            grad_down.astype(jnp.bfloat16), "wide", scatter_dimension=1, tiled=True
        ).astype(jnp.float32),
    )
    mixer_again = fetch_mixer(w_in, w_out, short_kernel, decay_rate, pole_angle, residue)
    in_back, out_back = (mixer_again[0], mixer_again[1])
    flat_dmiddle = spread_rows(d_middle.astype(jnp.bfloat16)).reshape(flat, width)
    d_gated = lax.dot_general(flat_dmiddle, out_back, last_only, preferred_element_type=jnp.float32)
    grad_out = lax.dot_general(
        flat_gated, flat_dmiddle, rows_only, preferred_element_type=jnp.float32
    )
    d_masked, grad_taps, grad_decay, grad_angle, grad_residue = mixer_pull(
        d_gated.reshape(group, slots, channels)
    )
    low_dz = (d_masked * live_mask[:, :, None]).astype(jnp.bfloat16).reshape(flat, 3, channels)
    grad_in = jnp.einsum("rd,rsc->sdc", flat_first, low_dz, preferred_element_type=jnp.float32)
    d_normed = sum_rows(
        jnp.einsum("rsc,sdc->rd", low_dz, in_back, preferred_element_type=jnp.float32).reshape(
            group, slots, width
        )
    )
    d_source_norm, grad_gain_one = first_pull(d_normed)
    input_grad = (d_middle + d_source_norm).astype(jnp.bfloat16)
    grad_kernel = grad_taps.reshape(3, 3, channels)
    in_share, out_share, kernel_share, decay_share, angle_share, residue_share = (
        lax.psum_scatter(
            grad_in.astype(jnp.bfloat16), "wide", scatter_dimension=2, tiled=True
        ).astype(jnp.float32),
        lax.psum_scatter(
            grad_out.astype(jnp.bfloat16), "wide", scatter_dimension=0, tiled=True
        ).astype(jnp.float32),
        lax.psum_scatter(
            grad_kernel.astype(jnp.bfloat16), "wide", scatter_dimension=2, tiled=True
        ).astype(jnp.float32),
        lax.psum_scatter(
            grad_decay.astype(jnp.bfloat16), "wide", scatter_dimension=0, tiled=True
        ).astype(jnp.float32),
        lax.psum_scatter(
            grad_angle.astype(jnp.bfloat16), "wide", scatter_dimension=0, tiled=True
        ).astype(jnp.float32),
        lax.psum_scatter(
            grad_residue.astype(jnp.bfloat16), "wide", scatter_dimension=0, tiled=True
        ).astype(jnp.float32),
    )
    gain_one_share, gain_two_share = (
        lax.psum_scatter(grad_gain_one, ("wide", "narrow"), scatter_dimension=0, tiled=True),
        lax.psum_scatter(grad_gain_two, ("wide", "narrow"), scatter_dimension=0, tiled=True),
    )
    return (
        block_output,
        input_grad,
        in_share,
        out_share,
        gain_one_share,
        kernel_share,
        decay_share,
        angle_share,
        residue_share,
        gain_two_share,
        gate_share,
        up_share,
        down_share,
    )


def solution(mesh):
    return jax.shard_map(
        body,
        mesh=mesh,
        in_specs=(
            P("wide", "narrow", None),
            P(None, None, ("wide", "narrow")),
            P(("wide", "narrow"), None),
            P(("wide", "narrow")),
            P(None, None, ("wide", "narrow")),
            P(("wide", "narrow"), None),
            P(("wide", "narrow"), None),
            P(("wide", "narrow"), None),
            P(("wide", "narrow")),
            P(None, ("wide", "narrow")),
            P(None, ("wide", "narrow")),
            P(None, ("wide", "narrow")),
            P("wide", None),
            P("wide", None),
            P("wide", "narrow", None),
        ),
        out_specs=(
            P("wide", "narrow", None),
            P("wide", "narrow", None),
            P(None, None, ("wide", "narrow")),
            P(("wide", "narrow"), None),
            P(("wide", "narrow")),
            P(None, None, ("wide", "narrow")),
            P(("wide", "narrow"), None),
            P(("wide", "narrow"), None),
            P(("wide", "narrow"), None),
            P(("wide", "narrow")),
            P(None, ("wide", "narrow")),
            P(None, ("wide", "narrow")),
            P(None, ("wide", "narrow")),
        ),
        check_vma=False,
    )
```

profile of v0, /device:TPU:0, one launch (start us, length us, event | category | flops | bytes accessed | tf_op | source)
XLA Modules:
  0.0 1931.2 jit_solution(3491222357846574946)
XLA Ops:
  9.0 42.1 %all-reduce.24 = (bf16[2048]{0:T(1024)(128)(2,1)S(1)}, bf16[2048]{0:T(1024)(128)(2,1)S(1)}) all-reduce(bf16[2048]{0:T(1024)(128)(2,1)S(1)} %dynamic-update-slice, bf16[2048]{0:T(1024)(128)(2,1)S(1)} %dynamic-update-slice.1), channel_id=1, replica_groups=mesh['wide'=8,'narrow'=4] {'wide','narrow'}, use_global_device_ids=true, to_apply=%add.19 | all-reduce | flops 4096 | bytes 16384
  57.9 30.6 %all-gather.2 = bf16[8,64,16]{1,2,0:T(8,128)(2,1)S(1)} all-gather(bf16[1,64,16]{1,2,0:T(8,128)(2,1)S(1)} %bitcast.316), channel_id=1, replica_groups=mesh['wide'=8,'narrow'=4] {'wide'}, dimensions={0}, use_global_device_ids=true | all-gather | bytes 18432 | tf_op jit(solution)/shard_map/all_gather | solution.py:111
  88.6 31.4 %all-gather.1 = bf16[8,64,16]{1,2,0:T(8,128)(2,1)S(1)} all-gather(bf16[1,64,16]{1,2,0:T(8,128)(2,1)S(1)} %bitcast.317), channel_id=1, replica_groups=mesh['wide'=8,'narrow'=4] {'wide'}, dimensions={0}, use_global_device_ids=true | all-gather | bytes 18432 | tf_op jit(solution)/shard_map/all_gather | solution.py:110
  120.2 31.5 %all-gather = bf16[8,64,32]{1,2,0:T(8,128)(2,1)S(1)} all-gather(bf16[1,64,32]{1,2,0:T(8,128)(2,1)S(1)} %bitcast.315), channel_id=1, replica_groups=mesh['wide'=8,'narrow'=4] {'wide'}, dimensions={0}, use_global_device_ids=true | all-gather | bytes 36864 | tf_op jit(solution)/shard_map/all_gather | solution.py:112
  152.1 33.8 %fusion.21 = (f32[512,16,129]{2,1,0:T(8,128)S(1)}, f32[512,16,129]{2,1,0:T(8,128)}, f32[512,16,129]{2,1,0:T(8,128)S(1)}) fusion(f32[512,16]{1,0:T(8,128)S(1)} %bitcast.302, f32[512,16]{1,0:T(8,128)S(1)} %bitcast.300, f32[512,16]{1,0:T(8,128)S(1)} %copy.293, f32[512,16]{1,0:T(8,128)S(1)} %copy.288), kind=kLoop, calls=%fused_computation.55 | loop fusion | flops 7397376 | bytes 12812288 | tf_op jit(solution)/shard_map/jvp(vmap())/mul | solution.py:52
  201.3 32.5 %all_gather.50 = bf16[3,3,512]{1,0,2:T(4,128)(2,1)S(1)} all-gather(bf16[3,3,64]{1,0,2:T(4,128)(2,1)S(1)} %copy.283), channel_id=1, replica_groups=mesh['wide'=8,'narrow'=4] {'wide'}, dimensions={2}, use_global_device_ids=true | all-gather | bytes 10368 | tf_op jit(solution)/shard_map/all_gather | solution.py:109
  240.7 7.2 rev.12
  247.9 7.2 rev.13
  255.2 17.1 fusion.17
  272.3 10.1 fusion.41
  288.8 10.0 broadcast_multiply_fusion.1
  305.1 10.1 convolution_bitcast_fusion.1
  317.3 9.4 convolution_bitcast_fusion
  329.6 26.9 %while.49 = (s32[]{:T(128)}, f32[1,512,16]{1,2,0:T(8,128)S(1)}, f32[1,512,16]{1,2,0:T(8,128)S(1)}, f32[8,1,512,16]{2,3,1,0:T(8,128)S(1)}, f32[8,1,512,16]{2,3,1,...) while((s32[]{:T(128)}, f32[1,512,16]{1,2,0:T(8,128)S(1)}, ...), condition=%wide.region_6.7_spmd.clone, body=%wide.region_5.6_spmd.clone.sunk | while | flops 131076 | bytes 393400 | solution.py:90
  360.6 11.4 fusion.94
  372.1 74.3 %fusion.8 = f32[512,8,128]{2,1,0:T(8,128)S(1)} fusion(f32[8,128,512]{1,0,2:T(8,128)S(1)} %copy.294, f32[512,128,128]{2,0,1:T(8,128)} %fusion.17), kind=kOutput, calls=%fused_computation.28 | convolution fusion | flops 805306368 | bytes 37748736 | tf_op jit(solution)/shard_map/jvp(vmap(cts,nsc->ntc))/dot_general | solution.py:71
  446.4 6.0 bitcast_add_fusion.9
  457.1 6.2 convert_bitcast_fusion.2
  464.0 43.9 %reduce-scatter.22.cloned.1.call-done = bf16[1,256,2048]{2,1,0:T(8,128)(2,1)} async-done(((bf16[1,1024,2048]{2,1,0:T(8,128)(2,1)}), bf16[1,256,2048]{2,1,0:T(8,128)(2,1)}) %reduce-scatter.22.cloned.1.call-update) | async-done | bytes 1048592 | tf_op jit(solution)/shard_map/reduce_scatter | solution.py:132
  514.5 87.8 %all-gather.21.cloned.1.call-done = bf16[2048,1408]{0,1:T(8,128)(2,1)} async-done(((bf16[2048,176]{0,1:T(8,128)(2,1)}), bf16[2048,1408]{0,1:T(8,128)(2,1)}) %all-gather.21.cloned.1.call-update) | async-done | bytes 5767184 | tf_op jit(solution)/shard_map/all_gather | solution.py:120
  602.3 34.7 %all-gather.19.cloned.1.call-done = bf16[1,1024,2048]{2,1,0:T(8,128)(2,1)} async-done(((bf16[1,256,2048]{2,1,0:T(8,128)(2,1)}), bf16[1,1024,2048]{2,1,0:T(8,128)(2,1)}) %all-gather.19.cloned.1.call-update) | async-done | bytes 4194320 | tf_op jit(solution)/shard_map/all_gather | solution.py:128
  637.0 12.2 fusion.39
  649.2 82.3 %all-gather.23.cloned.1.call-done = bf16[2048,1408]{0,1:T(8,128)(2,1)} async-done(((bf16[2048,176]{0,1:T(8,128)(2,1)}), bf16[2048,1408]{0,1:T(8,128)(2,1)}) %all-gather.23.cloned.1.call-update) | async-done | bytes 5767184 | tf_op jit(solution)/shard_map/all_gather | solution.py:121
  731.5 11.8 fusion.37
  743.3 22.5 %all-gather.27.cloned.1.call-done = bf16[1,1024,2048]{2,1,0:T(8,128)(2,1)} async-done(((bf16[1,256,2048]{2,1,0:T(8,128)(2,1)}), bf16[1,1024,2048]{2,1,0:T(8,128)(2,1)}) %all-gather.27.cloned.1.call-update) | async-done | bytes 4194320 | tf_op jit(solution)/shard_map/all_gather | solution.py:128
  765.8 94.5 %all-gather.25.cloned.1.call-done = bf16[2048,1408]{0,1:T(8,128)(2,1)} async-done(((bf16[2048,176]{0,1:T(8,128)(2,1)}), bf16[2048,1408]{0,1:T(8,128)(2,1)}) %all-gather.25.cloned.1.call-update) | async-done | bytes 5767184 | tf_op jit(solution)/shard_map/all_gather | solution.py:122
  860.3 15.7 multiply_convert_fusion.1
  876.0 10.9 fusion.106
  886.9 8.5 fusion.25
  895.5 42.9 %reduce-scatter.26.cloned.1.call-done = bf16[1,256,2048]{2,1,0:T(8,128)(2,1)} async-done(((bf16[1,1024,2048]{2,1,0:T(8,128)(2,1)}), bf16[1,256,2048]{2,1,0:T(8,128)(2,1)}) %reduce-scatter.26.cloned.1.call-update) | async-done | bytes 1048592 | tf_op jit(solution)/shard_map/reduce_scatter | solution.py:132
  945.0 10.6 convolution_convert_fusion.2
  957.3 10.6 convolution_convert_fusion.1
  968.1 10.5 fusion.22
  980.2 7.5 bitcast_multiply_fusion.6
  989.7 53.4 %fusion.6 = f32[512,8,128]{2,1,0:T(8,128)} fusion(f32[512,128,128]{2,0,1:T(8,128)} %fusion.17, f32[1,8,128,512]{2,1,3,0:T(8,128)S(1)} %copy.307), kind=kOutput, calls=%fused_computation.26 | convolution fusion | flops 805306368 | bytes 37748736 | tf_op jit(solution)/shard_map/transpose(jvp(vmap(cts,nsc->ntc)))/dot_general | solution.py:71
  1043.2 10.2 fusion.84
  1053.4 14.5 fusion.79
  1073.8 23.3 %while.50 = (s32[]{:T(128)}, f32[512,16]{0,1:T(8,128)S(1)}, f32[512,16]{0,1:T(8,128)S(1)}, f32[1,512,16]{1,2,0:T(8,128)S(1)}, f32[1,512,16]{1,2,0:T(8,128)S(1)},...) while((s32[]{:T(128)}, f32[512,16]{0,1:T(8,128)S(1)}, ...), condition=%wide.region_13.14_spmd.clone, body=%wide.region_12.13_spmd.clone.sunk | while | flops 229380 | bytes 657108 | solution.py:90
  1099.0 7.8 fusion.107
  1108.8 9.1 add_bitcast_fusion
  1131.9 9.0 slice_multiply_fusion.1
  1141.0 10.5 pad_add_fusion.1
  1153.1 9.1 multiply_reduce_fusion.6
  1163.5 9.9 fusion.109
  1173.4 7.2 rev.15
  1184.1 9.8 fusion.108
  1193.9 7.2 rev.14
  1204.7 8.5 fusion.69
  1213.3 6.9 fusion.72
  1220.3 56.6 %fusion.66 = f32[512,128,128]{2,1,0:T(8,128)} fusion(f32[8,128,512]{1,0,2:T(8,128)S(1)} %copy-done.1, f32[1,8,128,512]{2,1,3,0:T(8,128)S(1)} %copy.307), kind=kOutput, calls=%fused_computation.137 | convolution fusion | flops 805306368 | bytes 37748736 | tf_op jit(solution)/shard_map/transpose(jvp(vmap(cts,nsc->ntc)))/dot_general | solution.py:71
  1276.9 41.9 %fusion.89 = f32[512,128]{1,0:T(8,128)S(1)} fusion(s32[128,128]{1,0:T(8,128)S(1)} %copy-done.42, f32[512,128,128]{2,1,0:T(8,128)} %fusion.66), kind=kOutput, calls=%fused_computation.164 | convolution fusion | flops 12886999040 | bytes 33882112 | tf_op jit(solution)/shard_map/transpose(jvp(vmap(cl,lts->cts)))/dot_general | solution.py:67
  1321.2 57.6 %multiply_reduce_fusion.1 = (f32[512,16]{1,0:T(8,128)S(1)}, f32[512,16]{1,0:T(8,128)S(1)}, f32[512,16]{1,0:T(8,128)S(1)}, f32[512,16]{1,0:T(8,128)S(1)}, f32[512,16]{1,0:T(8,128)S(1)}, /*index=5*/bf16[512,16]{1,0:T(8,128)(2,1)S(1)}) fusion(f32[512,16,128]{2,1,0:T(8,128)S(1)} %broadcast_in_dim.101, f32[512,16,128]{2,1,0:T(8,128)S(1)} %fusion.69, ...), kind=kLoop, calls=%fused_computation.42 | loop fusion | flops 40108032 | bytes 21348352 | tf_op jit(solution)/shard_map/transpose(jvp(vmap()))/reduce_sum | solution.py:61
  1382.0 6.3 fusion.50
  1391.3 11.2 fusion.49
  1404.4 11.1 convert_bitcast_fusion.1
  1417.4 10.7 convert_bitcast_fusion
  1435.6 5.8 reduce-scatter.40.cloned.1.call-done
  1442.9 63.1 %reduce-scatter.42.cloned.1.call-done = bf16[64,16]{1,0:T(8,128)(2,1)} async-done(((bf16[512,16]{1,0:T(8,128)(2,1)}), bf16[64,16]{1,0:T(8,128)(2,1)}) %reduce-scatter.42.cloned.1.call-update) | async-done | bytes 2064
  1507.4 63.2 %reduce-scatter.44.cloned.1.call-done = bf16[64,16]{1,0:T(8,128)(2,1)} async-done(((bf16[512,16]{1,0:T(8,128)(2,1)}), bf16[64,16]{1,0:T(8,128)(2,1)}) %reduce-scatter.44.cloned.1.call-update) | async-done | bytes 2064
  1572.1 62.7 %reduce-scatter.46.cloned.1.call-done = bf16[64,32]{1,0:T(8,128)(2,1)} async-done(((bf16[512,32]{1,0:T(8,128)(2,1)}), bf16[64,32]{1,0:T(8,128)(2,1)}) %reduce-scatter.46.cloned.1.call-update) | async-done | bytes 4112
  1636.1 69.4 %reduce-scatter.32.cloned.1.call-done = bf16[64,2048]{1,0:T(8,128)(2,1)} async-done(((bf16[512,2048]{1,0:T(8,128)(2,1)}), bf16[64,2048]{1,0:T(8,128)(2,1)}) %reduce-scatter.32.cloned.1.call-update) | async-done | bytes 262160 | tf_op jit(solution)/shard_map/reduce_scatter | solution.py:258
  1707.3 44.3 %reduce-scatter.28.cloned.1.call-done = bf16[1,256,2048]{2,1,0:T(8,128)(2,1)} async-done(((bf16[1,1024,2048]{2,1,0:T(8,128)(2,1)}), bf16[1,256,2048]{2,1,0:T(8,128)(2,1)}) %reduce-scatter.28.cloned.1.call-update) | async-done | bytes 1048592 | tf_op jit(solution)/shard_map/reduce_scatter | solution.py:132
  1753.9 40.0 %all-reduce.23 = (f32[2048]{0:T(1024)S(1)}, f32[2048]{0:T(1024)S(1)}) all-reduce(f32[2048]{0:T(1024)S(1)} %get-tuple-element.764, f32[2048]{0:T(1024)S(1)} %copy-done.55), channel_id=8, replica_groups=mesh['wide'=8,'narrow'=4] {'wide','narrow'}, use_global_device_ids=true, to_apply=%region_19.20.clone | all-reduce | flops 4096 | bytes 32768
  1804.3 117.2 %reduce-scatter.30.cloned.1.call-done = bf16[3,2048,64]{1,2,0:T(8,128)(2,1)} async-done(((bf16[3,2048,512]{1,2,0:T(8,128)(2,1)}), bf16[3,2048,64]{1,2,0:T(8,128)(2,1)}) %reduce-scatter.30.cloned.1.call-update) | async-done | bytes 786448 | tf_op jit(solution)/shard_map/reduce_scatter | solution.py:255
  (410 shorter events, 202.7 us)
Async XLA Ops:
  7.2 50.7 %copy-start.65 = (bf16[64,16]{0,1:T(8,128)(2,1)S(1)}, bf16[64,16]{0,1:T(8,128)(2,1)}, u32[]{:S(2)}) copy-start(bf16[64,16]{0,1:T(8,128)(2,1)} %param.25) | copy-start | bytes 6148
  7.2 81.4 %copy-start.66 = (bf16[64,16]{0,1:T(8,128)(2,1)S(1)}, bf16[64,16]{0,1:T(8,128)(2,1)}, u32[]{:S(2)}) copy-start(bf16[64,16]{0,1:T(8,128)(2,1)} %param.24) | copy-start | bytes 6148
  7.2 113.0 %copy-start.64 = (bf16[64,32]{0,1:T(8,128)(2,1)S(1)}, bf16[64,32]{0,1:T(8,128)(2,1)}, u32[]{:S(2)}) copy-start(bf16[64,32]{0,1:T(8,128)(2,1)} %param.26) | copy-start | bytes 12292
  7.2 265.1 %all-gather.13.cloned.1.call-start = ((), (), s32[]{:S(2)}) async-start(), calls=%async_computation.13 | async-start | bytes 5242880 | tf_op jit(solution)/shard_map/all_gather | solution.py:128
  56.3 216.0 %all-gather.15.cloned.1.call-start = ((), (), s32[]{:S(2)}) async-start(), calls=%async_computation.14 | async-start | bytes 7077888 | tf_op jit(solution)/shard_map/all_gather | solution.py:107
  57.0 400.1 %all-gather.17.cloned.1.call-start = ((), (), s32[]{:S(2)}) async-start(), calls=%async_computation.15 | async-start | bytes 2359296 | tf_op jit(solution)/shard_map/all_gather | solution.py:108
  57.8 450.2 %reduce-scatter.22.cloned.1.call-start = ((), (), s32[]{:S(2)}) async-start(), calls=%async_computation.16 | async-start | bytes 5242880 | tf_op jit(solution)/shard_map/reduce_scatter | solution.py:132
  57.8 197.4 %copy-start.41 = (s32[128,128]{1,0:T(8,128)}, s32[128,128]{1,0:T(8,128)S(1)}, u32[]{:S(2)}) copy-start(s32[128,128]{1,0:T(8,128)S(1)} %iota_subtract_fusion) | copy-start | bytes 196612
  88.6 97.3 %copy-start.36 = (f32[8,64,16]{2,1,0:T(8,128)}, f32[8,64,16]{2,1,0:T(8,128)S(1)}, u32[]{:S(2)}) copy-start(f32[8,64,16]{2,1,0:T(8,128)S(1)} %copy.336) | copy-start | bytes 98308
  120.1 65.7 %copy-start.34 = (f32[8,64,16]{2,1,0:T(8,128)}, f32[8,64,16]{2,1,0:T(8,128)S(1)}, u32[]{:S(2)}) copy-start(f32[8,64,16]{2,1,0:T(8,128)S(1)} %copy.335) | copy-start | bytes 98308
  151.9 208.7 %copy-start.25 = (f32[512,16]{1,0:T(8,128)}, f32[512,16]{1,0:T(8,128)S(1)}, u32[]{:S(2)}) copy-start(f32[512,16]{1,0:T(8,128)S(1)} %copy.293) | copy-start | bytes 98308
  152.1 208.5 %copy-start.27 = (f32[512,16]{1,0:T(8,128)}, f32[512,16]{1,0:T(8,128)S(1)}, u32[]{:S(2)}) copy-start(f32[512,16]{1,0:T(8,128)S(1)} %copy.288) | copy-start | bytes 98308
  198.3 88.4 %copy-start.47 = (f32[1024]{0:T(1024)}, f32[1024]{0:T(1024)S(1)}, u32[]{:S(2)}) copy-start(f32[1024]{0:T(1024)S(1)} %get-tuple-element.769) | copy-start | bytes 12292
  198.3 88.4 %copy-start.51 = (f32[1024]{0:T(1024)}, f32[1024]{0:T(1024)S(1)}, u32[]{:S(2)}) copy-start(f32[1024]{0:T(1024)S(1)} %broadcast_subtract_fusion) | copy-start | bytes 12292
  234.7 52.0 %copy-start.49 = (f32[1536]{0:T(1024)}, f32[1536]{0:T(1024)S(1)}, u32[]{:S(2)}) copy-start(f32[1536]{0:T(1024)S(1)} %mul.607) | copy-start | bytes 18436
  255.2 31.5 %copy-start.53 = (f32[1024]{0:T(1024)}, f32[1024]{0:T(1024)S(1)}, u32[]{:S(2)}) copy-start(f32[1024]{0:T(1024)S(1)} %maximum_multiply_fusion) | copy-start | bytes 12292
  305.1 66.9 %copy-start = (f32[8,128,512]{1,0,2:T(8,128)}, f32[8,128,512]{1,0,2:T(8,128)S(1)}, u32[]{:S(2)}) copy-start(f32[8,128,512]{1,0,2:T(8,128)S(1)} %copy.294) | copy-start | bytes 6291460
  356.6 15.4 copy-start.31
  356.6 15.4 copy-start.38
  356.6 15.4 copy-start.39
  360.6 85.8 %slice-start.6 = ((s8[8388608]{0:T(1024)(128)(4,1)}), s8[4194304]{0:T(1024)(128)(4,1)S(1)}, s32[]{:S(2)}) async-start(s8[8388608]{0:T(1024)(128)(4,1)} %bitcast.291), calls=%async_computation.41 | async-start | bytes 8388608
  372.0 74.3 %slice-start.7 = ((s8[8388608]{0:T(1024)(128)(4,1)}), s8[4194304]{0:T(1024)(128)(4,1)S(1)}, s32[]{:S(2)}) async-start(s8[8388608]{0:T(1024)(128)(4,1)} %bitcast.291), calls=%async_computation.42 | async-start | bytes 8388608
  372.1 74.3 %copy-start.16 = (f32[8,512,16]{2,0,1:T(8,128)S(1)}, f32[8,512,16]{2,0,1:T(8,128)}, u32[]{:S(2)}) copy-start(f32[8,512,16]{2,0,1:T(8,128)} %copy.303) | copy-start | bytes 786436
  463.4 44.6 %copy-start.5 = (bf16[1,256,2048]{2,1,0:T(8,128)(2,1)S(1)}, bf16[1,256,2048]{2,1,0:T(8,128)(2,1)}, u32[]{:S(2)}) copy-start(bf16[1,256,2048]{2,1,0:T(8,128)(2,1)} %param.19) | copy-start | bytes 3145732
  463.4 139.0 %all-gather.21.cloned.1.call-start = ((), (), s32[]{:S(2)}) async-start(), calls=%async_computation.18 | async-start | bytes 6488064 | tf_op jit(solution)/shard_map/all_gather | solution.py:120
  464.0 173.0 %all-gather.19.cloned.1.call-start = ((), (), s32[]{:S(2)}) async-start(), calls=%async_computation.17 | async-start | bytes 5242880 | tf_op jit(solution)/shard_map/all_gather | solution.py:128
  464.0 477.1 %copy-start.43 = (f32[2048]{0:T(1024)}, f32[2048]{0:T(1024)S(1)}, u32[]{:S(2)}) copy-start(f32[2048]{0:T(1024)S(1)} %convert_element_type.190) | copy-start | bytes 24580
  509.6 431.5 %copy-start.56 = (f32[256]{0:T(256)}, f32[256]{0:T(256)S(1)}, u32[]{:S(2)}) copy-start(f32[256]{0:T(256)S(1)} %fusion.101) | copy-start | bytes 3076
  512.2 219.3 %all-gather.23.cloned.1.call-start = ((), (), s32[]{:S(2)}) async-start(), calls=%async_computation.19 | async-start | bytes 6488064 | tf_op jit(solution)/shard_map/all_gather | solution.py:121
  513.0 252.8 %all-gather.27.cloned.1.call-start = ((), (), s32[]{:S(2)}) async-start(), calls=%async_computation.22 | async-start | bytes 5242880 | tf_op jit(solution)/shard_map/all_gather | solution.py:128
  513.7 346.6 %all-gather.25.cloned.1.call-start = ((), (), s32[]{:S(2)}) async-start(), calls=%async_computation.20 | async-start | bytes 6488064 | tf_op jit(solution)/shard_map/all_gather | solution.py:122
  514.5 423.9 %reduce-scatter.26.cloned.1.call-start = ((), (), s32[]{:S(2)}) async-start(), calls=%async_computation.23 | async-start | bytes 5242880 | tf_op jit(solution)/shard_map/reduce_scatter | solution.py:132
  895.4 42.9 %copy-start.8 = (bf16[1,256,2048]{2,1,0:T(8,128)(2,1)S(1)}, bf16[1,256,2048]{2,1,0:T(8,128)(2,1)}, u32[]{:S(2)}) copy-start(bf16[1,256,2048]{2,1,0:T(8,128)(2,1)} %reduce-scatter.22.cloned.1.call-done) | copy-start | bytes 3145732
  895.4 46.3 %copy-start.22 = (bf16[1,256,2048]{2,1,0:T(8,128)(2,1)S(1)}, bf16[1,256,2048]{2,1,0:T(8,128)(2,1)}, u32[]{:S(2)}) copy-start(bf16[1,256,2048]{2,1,0:T(8,128)(2,1)} %param.33) | copy-start | bytes 3145732
  895.4 84.1 %all-gather.29.cloned.1.call-start = ((), (), s32[]{:S(2)}) async-start(), calls=%async_computation.24 | async-start | bytes 5242880 | tf_op jit(solution)/shard_map/all_gather | solution.py:128
  944.9 483.2 %reduce-scatter.34.cloned.1.call-start = ((), (), s32[]{:S(2)}) async-start(), calls=%async_computation.28 | async-start | bytes 6488064 | tf_op jit(solution)/shard_map/reduce_scatter | solution.py:224
  955.5 475.1 %reduce-scatter.36.cloned.1.call-start = ((), (), s32[]{:S(2)}) async-start(), calls=%async_computation.29 | async-start | bytes 6488064 | tf_op jit(solution)/shard_map/reduce_scatter | solution.py:227
  968.0 465.2 %reduce-scatter.38.cloned.1.call-start = ((), (), s32[]{:S(2)}) async-start(), calls=%async_computation.30 | async-start | bytes 6488064 | tf_op jit(solution)/shard_map/reduce_scatter | solution.py:230
  978.6 462.8 %reduce-scatter.40.cloned.1.call-start = ((), (), s32[]{:S(2)}) async-start(), calls=%async_computation.31 | async-start | bytes 147456
  1131.9 19.5 %slice-start = ((s8[6291456]{0:T(1024)(128)(4,1)}), s8[2097152]{0:T(1024)(128)(4,1)S(1)}, s32[]{:S(2)}) async-start(s8[6291456]{0:T(1024)(128)(4,1)} %bitcast.284), calls=%async_computation.35 | async-start | bytes 4194304
  1131.9 19.5 %slice-start.2 = ((s8[6291456]{0:T(1024)(128)(4,1)}), s8[4194304]{0:T(1024)(128)(4,1)S(1)}, s32[]{:S(2)}) async-start(s8[6291456]{0:T(1024)(128)(4,1)} %bitcast.287), calls=%async_computation.37 | async-start | bytes 8388608
  1131.9 19.5 %slice-start.4 = ((s8[6291456]{0:T(1024)(128)(4,1)}), s8[4194304]{0:T(1024)(128)(4,1)S(1)}, s32[]{:S(2)}) async-start(s8[6291456]{0:T(1024)(128)(4,1)} %bitcast.289), calls=%async_computation.39 | async-start | bytes 8388608
  1220.2 56.7 %copy-start.42 = (s32[128,128]{1,0:T(8,128)S(1)}, s32[128,128]{1,0:T(8,128)}, u32[]{:S(2)}) copy-start(s32[128,128]{1,0:T(8,128)} %copy-done.41) | copy-start | bytes 196612
  1276.9 42.3 %copy-start.18 = (f32[512,16,1]{2,1,0:T(8,128)S(1)}, f32[512,16,1]{2,1,0:T(8,128)}, u32[]{:S(2)}) copy-start(f32[512,16,1]{2,1,0:T(8,128)} %copy.325) | copy-start | bytes 98308
  1276.9 42.3 %copy-start.19 = (f32[512,16,128]{2,1,0:T(8,128)S(1)}, f32[512,16,128]{2,1,0:T(8,128)}, u32[]{:S(2)}) copy-start(f32[512,16,128]{2,1,0:T(8,128)} %rev.14) | copy-start | bytes 12582916
  1276.9 42.3 %copy-start.20 = (f32[512,16,1]{2,1,0:T(8,128)S(1)}, f32[512,16,1]{2,1,0:T(8,128)}, u32[]{:S(2)}) copy-start(f32[512,16,1]{2,1,0:T(8,128)} %copy.318) | copy-start | bytes 98308
  1276.9 42.3 %copy-start.37 = (f32[8,64,16]{2,1,0:T(8,128)S(1)}, f32[8,64,16]{2,1,0:T(8,128)}, u32[]{:S(2)}) copy-start(f32[8,64,16]{2,1,0:T(8,128)} %copy-done.36) | copy-start | bytes 98308
  1378.9 127.2 %reduce-scatter.42.cloned.1.call-start = ((), (), s32[]{:S(2)}) async-start(), calls=%async_computation.32 | async-start | bytes 147456
  1379.7 190.9 %reduce-scatter.44.cloned.1.call-start = ((), (), s32[]{:S(2)}) async-start(), calls=%async_computation.33 | async-start | bytes 147456
  1381.1 253.7 %reduce-scatter.46.cloned.1.call-start = ((), (), s32[]{:S(2)}) async-start(), calls=%async_computation.34 | async-start | bytes 147456
  1381.9 323.6 %reduce-scatter.32.cloned.1.call-start = ((), (), s32[]{:S(2)}) async-start(), calls=%async_computation.27 | async-start | bytes 2359296 | tf_op jit(solution)/shard_map/reduce_scatter | solution.py:258
  1388.4 363.2 %reduce-scatter.28.cloned.1.call-start = ((), (), s32[]{:S(2)}) async-start(), calls=%async_computation.25 | async-start | bytes 5242880 | tf_op jit(solution)/shard_map/reduce_scatter | solution.py:132
  1402.6 396.8 %reduce-scatter.24.cloned.1.call-start = ((), (), s32[]{:S(2)}) async-start(), calls=%async_computation.21 | async-start | bytes 5242880 | tf_op jit(solution)/shard_map/reduce_scatter | solution.py:132
  1415.5 506.0 %reduce-scatter.30.cloned.1.call-start = ((), (), s32[]{:S(2)}) async-start(), calls=%async_computation.26 | async-start | bytes 7077888 | tf_op jit(solution)/shard_map/reduce_scatter | solution.py:255
  1428.1 323.5 %copy-start.6 = (bf16[1,256,2048]{2,1,0:T(8,128)(2,1)S(1)}, bf16[1,256,2048]{2,1,0:T(8,128)(2,1)}, u32[]{:S(2)}) copy-start(bf16[1,256,2048]{2,1,0:T(8,128)(2,1)} %param.19) | copy-start | bytes 3145732
  1428.1 323.5 %copy-start.46 = (f32[2048]{0:T(1024)S(1)}, f32[2048]{0:T(1024)}, u32[]{:S(2)}) copy-start(f32[2048]{0:T(1024)} %copy-done.45) | copy-start | bytes 24580
  1428.1 323.5 %copy-start.59 = (f32[256]{0:T(256)S(1)}, f32[256]{0:T(256)}, u32[]{:S(2)}) copy-start(f32[256]{0:T(256)} %copy-done.58) | copy-start | bytes 3076
  1430.6 323.2 %copy-start.55 = (f32[2048]{0:T(1024)S(1)}, f32[2048]{0:T(1024)}, u32[]{:S(2)}) copy-start(f32[2048]{0:T(1024)} %get-tuple-element.762) | copy-start | bytes 24580
  1430.6 364.5 %copy-start.61 = (f32[256]{0:T(256)S(1)}, f32[256]{0:T(256)}, u32[]{:S(2)}) copy-start(f32[256]{0:T(256)} %copy-done.60) | copy-start | bytes 3076
  1430.6 368.8 %copy-start.9 = (bf16[1,256,2048]{2,1,0:T(8,128)(2,1)S(1)}, bf16[1,256,2048]{2,1,0:T(8,128)(2,1)}, u32[]{:S(2)}) copy-start(bf16[1,256,2048]{2,1,0:T(8,128)(2,1)} %reduce-scatter.22.cloned.1.call-done) | copy-start | bytes 3145732
  1430.6 368.8 %copy-start.23 = (bf16[1,256,2048]{2,1,0:T(8,128)(2,1)S(1)}, bf16[1,256,2048]{2,1,0:T(8,128)(2,1)}, u32[]{:S(2)}) copy-start(bf16[1,256,2048]{2,1,0:T(8,128)(2,1)} %param.33) | copy-start | bytes 3145732
  1430.6 368.8 %copy-start.44 = (f32[2048]{0:T(1024)S(1)}, f32[2048]{0:T(1024)}, u32[]{:S(2)}) copy-start(f32[2048]{0:T(1024)} %copy-done.43) | copy-start | bytes 24580
  1430.6 368.8 %copy-start.57 = (f32[256]{0:T(256)S(1)}, f32[256]{0:T(256)}, u32[]{:S(2)}) copy-start(f32[256]{0:T(256)} %copy-done.56) | copy-start | bytes 3076
  1430.6 368.8 %copy-start.63 = (f32[256]{0:T(256)S(1)}, f32[256]{0:T(256)}, u32[]{:S(2)}) copy-start(f32[256]{0:T(256)} %copy-done.62) | copy-start | bytes 3076
  (44 other events, 293.1 us)
Sparse Core Ops, SparseCore 0:
  56.4 34.2 all-gather.12
  92.9 100.4 all-gather.14
  195.5 49.6 all-gather.16
  463.5 44.3 reduce-scatter.21
  510.0 92.3 all-gather.20
  604.3 32.6 all-gather.18
  639.2 92.3 all-gather.22
  733.1 32.6 all-gather.26
  767.9 92.3 all-gather.24
  895.5 42.7 reduce-scatter.25
  945.0 34.4 all-gather.28
  983.0 110.6 reduce-scatter.33
  1097.3 109.9 reduce-scatter.35
  1210.8 109.9 reduce-scatter.37
  1379.0 62.3 reduce-scatter.39
  1445.1 60.8 reduce-scatter.41
  1509.8 60.8 reduce-scatter.43
  1573.8 60.8 reduce-scatter.45
  1638.2 67.2 reduce-scatter.31
  1707.9 43.6 reduce-scatter.27
  1754.1 45.2 reduce-scatter.23
  1803.0 118.4 reduce-scatter.29
where the time goes:
time: 1940 us; the launch traced here: 1930 us
  waiting for transfers between devices  844 us (44%)
  matrix products  511 us (26%)
  other arithmetic  225 us (12%)
  blocking collectives  208 us (11%)
  local copies, waits for them, and re-layouts  126 us (6%)
    unnamed x26, waiting for transfers between devices  199 us
    dot_general x3, matrix products, long_conv(): within = jnp.einsum('cts,nsc->ntc', toeplitz, blocked, precision=highest)  184 us
    reduce_scatter x4, waiting for transfers between devices, sum_rows(): lax.psum_scatter(values.astype(jnp.bfloat16), 'narrow', scatter_dimension...  135 us
    reduce_scatter x1, waiting for transfers between devices, body(): lax.psum_scatter(grad_in.astype(jnp.bfloat16), 'wide', scatter_dimension=...  117 us
    all_gather x1, waiting for transfers between devices, fetch_mlp(): lax.all_gather(w_down, 'wide', axis=1, tiled=True)  94.5 us
    all_gather x1, waiting for transfers between devices, fetch_mlp(): lax.all_gather(w_gate, 'wide', axis=1, tiled=True)  87.8 us
    all_gather x1, waiting for transfers between devices, fetch_mlp(): lax.all_gather(w_up, 'wide', axis=1, tiled=True)  82.3 us
    unnamed x2, blocking collectives  82.1 us
  transfers between devices with their start and end apart: 22, of which 16 were waited for; matrix products, arithmetic and copies ran while one was open for 41% of the time, Pallas kernels for 0%

commit v1 on v0

v1 whole, which is shorter than its diff:
```python
from functools import partial

import jax
import jax.numpy as jnp
import numpy as np
from jax import lax
from jax.experimental import pallas as pl
from jax.experimental.pallas import tpu as pltpu
from jax.sharding import PartitionSpec as P

BLOCK = 128
LONGEST = 4
SPAN = LONGEST * BLOCK
FREQ = SPAN

epsilon = 1e-06
bf16 = jnp.bfloat16
f32 = jnp.float32


def transform():
    k = np.arange(FREQ)[:, None] * 2 + 1
    t = np.arange(SPAN)[None, :]
    turn = (k * t % (4 * SPAN)) * (2 * np.pi / (4 * SPAN))
    return np.concatenate([np.cos(turn), -np.sin(turn)], axis=0).astype(np.float32)


def nn(a, b):
    return lax.dot_general(a, b, (((1,), (0,)), ((), ())), preferred_element_type=f32)


def nt(a, b):
    return lax.dot_general(a, b, (((1,), (1,)), ((), ())), preferred_element_type=f32)


def tn(a, b):
    return lax.dot_general(a, b, (((0,), (0,)), ((), ())), preferred_element_type=f32)


def swap(values, axis, shift):
    size = lax.axis_size(axis)
    return lax.ppermute(values, axis, [(i, i ^ shift) for i in range(size)])


def gather_wide(piece, axis=0):
    size = lax.axis_size("wide")
    parts = [piece] + [swap(piece, "wide", k) for k in range(2, size, 2)]
    near = jnp.concatenate(parts, axis=axis)
    return near, swap(near, "wide", 1)


def scatter_wide(near, far, axis=0):
    size = lax.axis_size("wide")
    got = swap(far, "wide", 1)
    total = near.astype(f32) + got.astype(f32)
    chunks = jnp.split(total, size // 2, axis=axis)
    out = chunks[0]
    for k in range(1, size // 2):
        out = out + swap(chunks[k].astype(bf16), "wide", 2 * k).astype(f32)
    return out


def gather_rows(own):
    size = lax.axis_size("narrow")
    even = jnp.concatenate([own] + [swap(own, "narrow", k) for k in range(2, size, 2)], axis=0)
    return jnp.concatenate([even, swap(even, "narrow", 1)], axis=0)


def scatter_rows(even, odd):
    size = lax.axis_size("narrow")
    got = swap(odd, "narrow", 1)
    total = even.astype(f32) + got.astype(f32)
    rows = total.shape[0] // (size // 2)
    out = total[:rows]
    for k in range(1, size // 2):
        chunk = total[k * rows : (k + 1) * rows].astype(bf16)
        out = out + swap(chunk, "narrow", 2 * k).astype(f32)
    return out


def inverse_rms(values):
    return lax.rsqrt(jnp.mean(values * values, axis=-1, keepdims=True) + epsilon)


def norm_back(values, rate, gain, grad):
    a = grad * gain
    inner = jnp.mean(a * values, axis=-1, keepdims=True)
    return rate * a - values * (rate * rate * rate) * inner


def filter_kernel(base_re, base_im, step_re, step_im, out):
    poles = base_re.shape[0]
    width = out.shape[1]
    for g in range(width // 128 if width % 128 == 0 else 1):
        lanes = pl.ds(g * 128, min(128, width))
        start = tuple(base_re[j, :, lanes] for j in range(poles)) + tuple(
            base_im[j, :, lanes] for j in range(poles)
        )

        def step(b, state):
            total = state[0]
            for j in range(1, poles):
                total = total + state[j]
            out[pl.ds(pl.multiple_of(b * 8, 8), 8), lanes] = total
            new_re, new_im = [], []
            for j in range(poles):
                sr = step_re[j, :, lanes]
                si = step_im[j, :, lanes]
                new_re.append(state[j] * sr - state[poles + j] * si)
                new_im.append(state[j] * si + state[poles + j] * sr)
            return tuple(new_re) + tuple(new_im)

        lax.fori_loop(0, SPAN // 8, step, start)


def filter_taps(base_re, base_im, step_re, step_im):
    width = base_re.shape[2]
    return pl.pallas_call(
        filter_kernel,
        out_shape=jax.ShapeDtypeStruct((SPAN, width), f32),
        cost_estimate=pl.CostEstimate(
            flops=16 * 7 * SPAN * width, bytes_accessed=4 * SPAN * width, transcendentals=0
        ),
        name="taps",
    )(base_re, base_im, step_re, step_im)


def moment_kernel(grad, step_re, step_im, sum_re, sum_im, mom_re, mom_im):
    poles = step_re.shape[0]
    width = grad.shape[1]
    per = 8
    for g in range(width // 128 if width % 128 == 0 else 1):
        lanes = pl.ds(g * 128, min(128, width))
        for j0 in range(0, poles, per):
            zero = jnp.zeros((8, min(128, width)), f32)

            def step(i, state):
                b = SPAN // 8 - 1 - i
                value = grad[pl.ds(pl.multiple_of(b * 8, 8), 8), lanes]
                new = []
                for n in range(per):
                    sr = step_re[j0 + n, :, lanes]
                    si = step_im[j0 + n, :, lanes]
                    pr, pi, qr, qi = state[4 * n : 4 * n + 4]
                    ur, ui = pr + qr, pi + qi
                    new += [
                        pr * sr - pi * si + value,
                        pr * si + pi * sr,
                        ur * sr - ui * si,
                        ur * si + ui * sr,
                    ]
                return tuple(new)

            state = lax.fori_loop(0, SPAN // 8, step, (zero,) * (4 * per))
            for n in range(per):
                sum_re[j0 + n, :, lanes] = state[4 * n]
                sum_im[j0 + n, :, lanes] = state[4 * n + 1]
                mom_re[j0 + n, :, lanes] = state[4 * n + 2]
                mom_im[j0 + n, :, lanes] = state[4 * n + 3]


def filter_moments(grad, step_re, step_im):
    poles, _, width = step_re.shape
    shape = jax.ShapeDtypeStruct((poles, 8, width), f32)
    return pl.pallas_call(
        moment_kernel,
        out_shape=(shape,) * 4,
        cost_estimate=pl.CostEstimate(
            flops=16 * 15 * SPAN * width, bytes_accessed=4 * SPAN * width, transcendentals=0
        ),
        name="moments",
    )(grad, step_re, step_im)


LIVE, KEEP_ONE, KEEP_TWO = 0, 1, 2


def load_masked(order, proj, table, m_scr):
    pieces, rows, _ = proj.shape
    m_scr[0:8, :] = jnp.zeros_like(m_scr[0:8, :])

    def piece(b, _):
        p = order[b]
        at = pl.multiple_of(b * rows, rows)
        live = table[pl.ds(at, rows), LIVE : LIVE + 1]
        m_scr[pl.ds(pl.multiple_of(at + 8, 8), rows), :] = proj[p] * live
        return 0

    lax.fori_loop(0, pieces, piece, 0)


def short_block(m_scr, taps, table, at):
    window = m_scr[pl.ds(at, BLOCK + 8), :]
    one = table[pl.ds(at, BLOCK), KEEP_ONE : KEEP_ONE + 1]
    two = table[pl.ds(at, BLOCK), KEEP_TWO : KEEP_TWO + 1]
    here = window[8:]
    once = window[7 : BLOCK + 7] * one
    twice = window[6 : BLOCK + 6] * two
    short = taps[0:1, :] * here + taps[1:2, :] * once + taps[2:3, :] * twice
    return short, here, once, twice


def pack_document(source, packed, first, count):
    blocks = source.shape[0] // BLOCK
    for kb in range(LONGEST):
        at = pl.multiple_of(jnp.minimum(first + kb, blocks - 1) * BLOCK, BLOCK)
        inside = (kb < count).astype(f32)
        packed[kb * BLOCK : (kb + 1) * BLOCK, :] = (source[pl.ds(at, BLOCK), :] * inside).astype(bf16)


def place_document(result, target, first, count):
    for kb in range(LONGEST):

        @pl.when(kb < count)
        def _():
            at = pl.multiple_of((first + kb) * BLOCK, BLOCK)
            target[pl.ds(at, BLOCK), :] = result[kb * BLOCK : (kb + 1) * BLOCK, :]


def forward_kernel(
    order, first, count, proj, taps, table, spectrum, fwd, inv, gated, long_out, seen, m_scr, u_scr, q_scr, packed
):
    width = long_out.shape[1]
    pieces, rows, _ = proj.shape
    blocks = long_out.shape[0] // BLOCK
    load_masked(order, proj, table, m_scr)

    def block(n, _):
        at = pl.multiple_of(n * BLOCK, BLOCK)
        short, _, _, _ = short_block(m_scr, taps, table, at)
        q_scr[pl.ds(at, BLOCK), :] = short[:, :width]
        u_scr[pl.ds(at, BLOCK), :] = short[:, width : 2 * width] * short[:, 2 * width :]
        return 0

    lax.fori_loop(0, blocks, block, 0)

    def document(d, _):
        pack_document(u_scr, packed, first[d], count[d])
        both = jnp.dot(fwd[...], packed[...], preferred_element_type=f32)
        seen[d] = both.astype(bf16)
        re, im = both[:FREQ], both[FREQ:]
        hr, hi = spectrum[:FREQ], spectrum[FREQ:]
        answer = jnp.concatenate([re * hr - im * hi, re * hi + im * hr], axis=0).astype(bf16)
        result = jnp.dot(inv[...], answer, preferred_element_type=f32)
        place_document(result, long_out, first[d], count[d])
        return 0

    lax.fori_loop(0, seen.shape[0], document, 0)

    def piece(b, _):
        at = pl.multiple_of(b * rows, rows)
        gated[order[b]] = (q_scr[pl.ds(at, rows), :] * long_out[pl.ds(at, rows), :]).astype(bf16)
        return 0

    lax.fori_loop(0, pieces, piece, 0)


def backward_kernel(
    order, first, count, proj, d_gated, long_out, seen, taps, table, spectrum, fwd, inv,
    dz, d_filter, d_taps, m_scr, dy_scr, k_scr, v_scr, ds_scr, packed, d_spec,
):
    width = long_out.shape[1]
    pieces, rows, _ = proj.shape
    slots = long_out.shape[0]
    blocks = slots // BLOCK
    per_piece = rows // BLOCK
    load_masked(order, proj, table, m_scr)
    ds_scr[slots : slots + 8, :] = jnp.zeros_like(ds_scr[slots : slots + 8, :])

    def block(n, _):
        at = pl.multiple_of(n * BLOCK, BLOCK)
        short, _, _, _ = short_block(m_scr, taps, table, at)
        within = pl.multiple_of((n % per_piece) * BLOCK, BLOCK)
        dg = d_gated[order[n // per_piece], pl.ds(within, BLOCK), :]
        dy_scr[pl.ds(at, BLOCK), :] = dg * short[:, :width]
        ds_scr[pl.ds(at, BLOCK), :width] = dg * long_out[pl.ds(at, BLOCK), :]
        k_scr[pl.ds(at, BLOCK), :] = short[:, width : 2 * width]
        v_scr[pl.ds(at, BLOCK), :] = short[:, 2 * width :]
        return 0

    lax.fori_loop(0, blocks, block, 0)
    d_spec[...] = jnp.zeros_like(d_spec)

    def document(d, _):
        pack_document(dy_scr, packed, first[d], count[d])
        both = jnp.dot(fwd[...], packed[...], preferred_element_type=f32)
        re, im = both[:FREQ], both[FREQ:]
        hr, hi = spectrum[:FREQ], spectrum[FREQ:]
        answer = jnp.concatenate([re * hr + im * hi, im * hr - re * hi], axis=0).astype(bf16)
        result = jnp.dot(inv[...], answer, preferred_element_type=f32)
        ur, ui = seen[d, :FREQ].astype(f32), seen[d, FREQ:].astype(f32)
        d_spec[:FREQ] += re * ur + im * ui
        d_spec[FREQ:] += im * ur - re * ui
        for kb in range(LONGEST):

            @pl.when(kb < count[d])
            def _():
                at = pl.multiple_of((first[d] + kb) * BLOCK, BLOCK)
                du = result[kb * BLOCK : (kb + 1) * BLOCK, :]
                ds_scr[pl.ds(at, BLOCK), width : 2 * width] = du * v_scr[pl.ds(at, BLOCK), :]
                ds_scr[pl.ds(at, BLOCK), 2 * width :] = du * k_scr[pl.ds(at, BLOCK), :]

        return 0

    lax.fori_loop(0, seen.shape[0], document, 0)
    d_filter[...] = jnp.dot(inv[...], d_spec[...].astype(bf16), preferred_element_type=f32)
    d_taps[...] = jnp.zeros_like(d_taps)

    def back(n, _):
        at = pl.multiple_of(n * BLOCK, BLOCK)
        window = m_scr[pl.ds(at, BLOCK + 8), :]
        ahead = ds_scr[pl.ds(at, BLOCK + 8), :]
        one = table[pl.ds(at, BLOCK + 8), KEEP_ONE : KEEP_ONE + 1]
        two = table[pl.ds(at, BLOCK + 8), KEEP_TWO : KEEP_TWO + 1]
        live = table[pl.ds(at, BLOCK), LIVE : LIVE + 1]
        ds = ahead[:BLOCK]
        ahead_one = ahead * one
        ahead_two = ahead * two
        dm = (
            taps[0:1, :] * ds
            + taps[1:2, :] * ahead_one[1 : BLOCK + 1]
            + taps[2:3, :] * ahead_two[2 : BLOCK + 2]
        )
        d_taps[0:1, :] += jnp.sum(window[8:] * ds, axis=0, keepdims=True)
        d_taps[1:2, :] += jnp.sum(window[7 : BLOCK + 7] * ahead_one[:BLOCK], axis=0, keepdims=True)
        d_taps[2:3, :] += jnp.sum(window[6 : BLOCK + 6] * ahead_two[:BLOCK], axis=0, keepdims=True)
        within = pl.multiple_of((n % per_piece) * BLOCK, BLOCK)
        dz[order[n // per_piece], pl.ds(within, BLOCK), :] = (dm * live).astype(bf16)
        return 0

    lax.fori_loop(0, blocks, back, 0)


smem = pl.BlockSpec(memory_space=pltpu.SMEM)
vmem = pl.BlockSpec(memory_space=pltpu.VMEM)


def mixer_forward(order, first, count, proj, taps, table, spectrum, fwd, inv):
    pieces, rows, three = proj.shape
    width = three // 3
    slots = pieces * rows
    docs = first.shape[0]
    return pl.pallas_call(
        forward_kernel,
        out_shape=(
            jax.ShapeDtypeStruct((pieces, rows, width), bf16),
            jax.ShapeDtypeStruct((slots, width), f32),
            jax.ShapeDtypeStruct((docs, 2 * FREQ, width), bf16),
        ),
        in_specs=[smem] * 3 + [vmem] * 6,
        out_specs=(vmem,) * 3,
        scratch_shapes=[
            pltpu.VMEM((slots + 8, three), f32),
            pltpu.VMEM((slots, width), f32),
            pltpu.VMEM((slots, width), f32),
            pltpu.VMEM((SPAN, width), bf16),
        ],
        compiler_params=pltpu.CompilerParams(vmem_limit_bytes=40 * 2**20),
        cost_estimate=pl.CostEstimate(
            flops=docs * 8 * FREQ * SPAN * width,
            bytes_accessed=slots * three * 4 + 8 * slots * width,
            transcendentals=0,
        ),
        name="mixer_forward",
    )(order, first, count, proj, taps, table, spectrum, fwd, inv)


def mixer_backward(order, first, count, proj, d_gated, long_out, seen, taps, table, spectrum, fwd, inv):
    pieces, rows, three = proj.shape
    width = three // 3
    slots = pieces * rows
    docs = first.shape[0]
    return pl.pallas_call(
        backward_kernel,
        out_shape=(
            jax.ShapeDtypeStruct((pieces, rows, three), bf16),
            jax.ShapeDtypeStruct((SPAN, width), f32),
            jax.ShapeDtypeStruct((8, three), f32),
        ),
        in_specs=[smem] * 3 + [vmem] * 9,
        out_specs=(vmem,) * 3,
        scratch_shapes=[
            pltpu.VMEM((slots + 8, three), f32),
            pltpu.VMEM((slots, width), f32),
            pltpu.VMEM((slots, width), f32),
            pltpu.VMEM((slots, width), f32),
            pltpu.VMEM((slots + 8, three), f32),
            pltpu.VMEM((SPAN, width), bf16),
            pltpu.VMEM((2 * FREQ, width), f32),
        ],
        compiler_params=pltpu.CompilerParams(vmem_limit_bytes=48 * 2**20),
        cost_estimate=pl.CostEstimate(
            flops=docs * 10 * FREQ * SPAN * width,
            bytes_accessed=slots * three * 8 + 8 * slots * width,
            transcendentals=0,
        ),
        name="mixer_backward",
    )(order, first, count, proj, d_gated, long_out, seen, taps, table, spectrum, fwd, inv)


def layout(doc_blocks, doc_pad, slots):
    block_ends = jnp.cumsum(doc_blocks) * BLOCK
    starts = block_ends - doc_blocks * BLOCK
    places = jnp.arange(slots, dtype=jnp.int32)
    living = (places[None, :] >= starts[:, None]) & (
        places[None, :] < (block_ends - doc_pad)[:, None]
    )
    live = jnp.sum(living.astype(f32), axis=0)
    opening = jnp.sum((places[None, :] == starts[:, None]).astype(f32), axis=0)
    one = 1.0 - opening
    one = one * (places > 0)
    two = one * jnp.concatenate([jnp.zeros((1,), f32), one[:-1]])
    table = jnp.stack([live, one, two], axis=1)
    table = jnp.concatenate([table, jnp.zeros((8, 3), f32)], axis=0)
    return table, starts // BLOCK


def picked(index, count, values):
    hot = index[:, None] == jnp.arange(count)[None, :]
    shape = hot.shape + (1,) * (values.ndim - 1)
    return jnp.sum(jnp.where(hot.reshape(shape), values[None], 0), axis=1)


def body(
    tokens, w_in, w_out, gain_one, short_kernel, decay_rate, pole_angle, residue,
    gain_two, w_gate, w_up, w_down, doc_blocks, doc_pad, cotangent,
):
    wide, narrow = lax.axis_size("wide"), lax.axis_size("narrow")
    wide_at, narrow_at = lax.axis_index("wide"), lax.axis_index("narrow")
    _, local_rows, width = tokens.shape
    slots = local_rows * narrow
    source = tokens[0].astype(f32)
    upstream_low = cotangent[0]
    poles = decay_rate.shape[1]
    own = w_in.shape[2]
    half = own * wide // 2

    small = jnp.concatenate(
        [
            short_kernel.reshape(9, own),
            decay_rate.T,
            pole_angle.T,
            residue.T,
            gain_one[None],
            gain_two[None],
        ],
        axis=0,
    )
    small_halves = gather_wide(small, axis=1)
    count_small = small.shape[0]
    gains = jnp.stack([s[count_small - 2 :].reshape(2, wide // 2, own) for s in small_halves], axis=2)
    gains = gains.reshape(2, wide, own).transpose(1, 0, 2)
    gains = picked(jnp.arange(wide) ^ wide_at, wide, gains.astype(f32)).astype(bf16)
    gain_parts = gather_rows(gains[None])
    offsets = list(range(0, narrow, 2)) + list(range(1, narrow, 2))
    place_of = np.argsort(np.array(offsets))
    order = jnp.asarray(place_of, jnp.int32)
    order = picked(jnp.arange(narrow) ^ narrow_at, narrow, order)
    gain_all = picked(order, narrow, gain_parts.astype(f32))
    gain_all = gain_all.transpose(2, 1, 0, 3).reshape(2, width)
    gain_first, gain_last = gain_all[0], gain_all[1]

    table, first = layout(doc_blocks[0], doc_pad[0], slots)
    count = doc_blocks[0]

    in_piece = w_in.transpose(0, 2, 1)
    out_piece = w_out
    gate_piece, up_piece, down_piece = w_gate.T, w_up.T, w_down.T
    in_halves = gather_wide(in_piece, axis=1)
    out_halves = gather_wide(out_piece)
    gate_halves = gather_wide(gate_piece)
    up_halves = gather_wide(up_piece)
    down_halves = gather_wide(down_piece)

    rate_first = inverse_rms(source)
    low_first = (source * rate_first * gain_first).astype(bf16)
    rows_first = gather_rows(low_first)
    rows_upstream = gather_rows(upstream_low)

    matrix = transform()
    fwd = jnp.asarray(matrix, bf16)
    inv = jnp.asarray(matrix.T / SPAN, bf16)

    tables, kept = [], []
    for s in range(2):
        block = small_halves[s].astype(f32)
        taps = block[:9].reshape(3, 3 * half)
        taps = jnp.concatenate([taps, jnp.zeros((5, 3 * half), f32)], axis=0)
        decay = block[9 : 9 + poles][:, None, :]
        angle = block[9 + poles : 9 + 2 * poles][:, None, :]
        res_re = block[9 + 2 * poles : 9 + 3 * poles][:, None, :]
        res_im = -block[9 + 3 * poles : 9 + 4 * poles][:, None, :]
        lag = jnp.arange(8, dtype=f32)[None, :, None]
        fade = jnp.exp(-decay * lag)
        power_re, power_im = fade * jnp.cos(angle * lag), fade * jnp.sin(angle * lag)
        fade_step = jnp.exp(-decay * 8.0)
        step_re = jnp.broadcast_to(fade_step * jnp.cos(angle * 8.0), power_re.shape)
        step_im = jnp.broadcast_to(fade_step * jnp.sin(angle * 8.0), power_re.shape)
        filt = filter_taps(
            res_re * power_re - res_im * power_im,
            res_re * power_im + res_im * power_re,
            step_re,
            step_im,
        )
        spectrum = lax.dot_general(
            jnp.asarray(matrix),
            filt,
            (((1,), (0,)), ((), ())),
            precision=lax.Precision.HIGHEST,
            preferred_element_type=f32,
        )
        tables.append((taps, spectrum))
        kept.append((power_re, power_im, step_re, step_im, res_re[:, 0], -res_im[:, 0]))

    even = slots // 2
    mixed = []
    for s in range(2):
        taps, spectrum = tables[s]
        weight = in_halves[s].reshape(3 * half, width)
        proj = nt(rows_first, weight).reshape(narrow, local_rows, 3 * half)
        gated, long_out, seen = mixer_forward(
            order, first, count, proj, taps, table, spectrum, fwd, inv
        )
        mixed.append((proj, gated.reshape(slots, half), long_out, seen))
    share_odd = sum(nn(mixed[s][1][even:], out_halves[s]) for s in range(2)).astype(bf16)
    share_even = sum(nn(mixed[s][1][:even], out_halves[s]) for s in range(2)).astype(bf16)
    middle = source + scatter_rows(share_even, share_odd)
    rate_last = inverse_rms(middle)
    rows_second = gather_rows((middle * rate_last * gain_last).astype(bf16))

    down_even, down_odd = 0.0, 0.0
    second_even, second_odd = 0.0, 0.0
    shares = []
    for s in range(2):
        gate_pre = nt(rows_second, gate_halves[s])
        up_pre = nt(rows_second, up_halves[s])
        sig = jax.nn.sigmoid(gate_pre)
        silu = gate_pre * sig
        hidden = (silu * up_pre).astype(bf16)
        d_hidden = nt(rows_upstream, down_halves[s])
        d_gate = (d_hidden * up_pre * sig * (1.0 + gate_pre * (1.0 - sig))).astype(bf16)
        d_up = (d_hidden * silu).astype(bf16)
        second_odd = second_odd + nn(d_gate[even:], gate_halves[s]) + nn(d_up[even:], up_halves[s])
        second_even = second_even + nn(d_gate[:even], gate_halves[s]) + nn(d_up[:even], up_halves[s])
        down_odd = down_odd + nn(hidden[even:], down_halves[s])
        down_even = down_even + nn(hidden[:even], down_halves[s])
        shares.append(
            (
                tn(d_gate, rows_second).astype(bf16),
                tn(d_up, rows_second).astype(bf16),
                tn(hidden, rows_upstream).astype(bf16),
            )
        )
    d_second = scatter_rows(second_even.astype(bf16), second_odd.astype(bf16))
    down_out = scatter_rows(down_even.astype(bf16), down_odd.astype(bf16))
    block_output = (middle + down_out).astype(bf16)
    upstream = upstream_low.astype(f32)
    d_middle = upstream + norm_back(middle, rate_last, gain_last, d_second)
    grad_gain_two = jnp.sum(d_second * middle * rate_last, axis=0)
    gate_share, up_share, down_share = (
        scatter_wide(shares[0][i], shares[1][i]) for i in range(3)
    )

    rows_dmiddle = gather_rows(d_middle.astype(bf16))
    out_parts, in_parts, small_parts = [], [], []
    normed_even, normed_odd = 0.0, 0.0
    for s in range(2):
        proj, gated, long_out, seen = mixed[s]
        taps, spectrum = tables[s]
        d_gated = nt(rows_dmiddle, out_halves[s]).reshape(narrow, local_rows, half)
        out_parts.append(tn(gated, rows_dmiddle).astype(bf16))
        dz, d_filter, d_taps = mixer_backward(
            order, first, count, proj, d_gated, long_out, seen, taps, table, spectrum, fwd, inv
        )
        dz = dz.reshape(slots, 3 * half)
        weight = in_halves[s].reshape(3 * half, width)
        normed_odd = normed_odd + nn(dz[even:], weight)
        normed_even = normed_even + nn(dz[:even], weight)
        in_parts.append(tn(dz, rows_first).astype(bf16).reshape(3, half, width))
        power_re, power_im, step_re, step_im, res_re, res_im = kept[s]
        sum_re, sum_im, mom_re, mom_im = filter_moments(d_filter, step_re, step_im)
        lag = jnp.arange(8, dtype=f32)[None, :, None]
        full_re = lag * sum_re + 8.0 * mom_re
        full_im = lag * sum_im + 8.0 * mom_im
        grad_re = jnp.sum(power_re * sum_re - power_im * sum_im, axis=1)
        grad_im = jnp.sum(power_re * sum_im + power_im * sum_re, axis=1)
        lag_re = jnp.sum(power_re * full_re - power_im * full_im, axis=1)
        lag_im = jnp.sum(power_re * full_im + power_im * full_re, axis=1)
        small_parts.append(
            jnp.concatenate(
                [
                    d_taps[:3].reshape(9, half),
                    -(res_re * lag_re + res_im * lag_im),
                    res_im * lag_re - res_re * lag_im,
                    grad_re,
                    grad_im,
                ],
                axis=0,
            ).astype(bf16)
        )
    d_normed = scatter_rows(normed_even.astype(bf16), normed_odd.astype(bf16))
    out_share = scatter_wide(out_parts[0], out_parts[1])
    in_share = scatter_wide(in_parts[0], in_parts[1], axis=1)
    small_share = scatter_wide(small_parts[0], small_parts[1], axis=1)
    input_grad = (d_middle + norm_back(source, rate_first, gain_first, d_normed)).astype(bf16)
    grad_gain_one = jnp.sum(d_normed * source * rate_first, axis=0)

    grads = jnp.stack([grad_gain_one, grad_gain_two]).reshape(2, wide, narrow, own)
    grads = picked(jnp.arange(narrow) ^ narrow_at, narrow, grads.transpose(2, 1, 0, 3))
    grads = jnp.stack([grads[k] for k in offsets])
    even_places = narrow // 2
    total = grads[:even_places] + swap(grads[even_places:], "narrow", 1)
    summed = total[0]
    for k in range(1, even_places):
        summed = summed + swap(total[k], "narrow", 2 * k)
    summed = picked(jnp.arange(wide) ^ wide_at, wide, summed)
    pairs = summed.reshape(wide // 2, 2, 2, own)
    total = pairs[:, 0] + swap(pairs[:, 1], "wide", 1)
    gain_share = total[0]
    for k in range(1, wide // 2):
        gain_share = gain_share + swap(total[k], "wide", 2 * k)

    at = 9 + poles
    return (
        block_output[None],
        input_grad[None],
        in_share.transpose(0, 2, 1),
        out_share,
        gain_share[0],
        small_share[:9].reshape(3, 3, own),
        small_share[9:at].T,
        small_share[at : at + poles].T,
        small_share[at + poles :].T,
        gain_share[1],
        gate_share.T,
        up_share.T,
        down_share.T,
    )


def solution(mesh):
    both = ("wide", "narrow")
    return jax.shard_map(
        body,
        mesh=mesh,
        in_specs=(
            P("wide", "narrow", None),
            P(None, None, both),
            P(both, None),
            P(both),
            P(None, None, both),
            P(both, None),
            P(both, None),
            P(both, None),
            P(both),
            P(None, both),
            P(None, both),
            P(None, both),
            P("wide", None),
            P("wide", None),
            P("wide", "narrow", None),
        ),
        out_specs=(
            P("wide", "narrow", None),
            P("wide", "narrow", None),
            P(None, None, both),
            P(both, None),
            P(both),
            P(None, None, both),
            P(both, None),
            P(both, None),
            P(both, None),
            P(both),
            P(None, both),
            P(None, both),
            P(None, both),
        ),
        check_vma=False,
    )
```

time: 1940 us -> 1080 us (0.56)
  waiting for transfers between devices: 844 us -> 457 us
  matrix products: 511 us -> 182 us
  starting transfers between devices: 0.89 us -> 235 us
  blocking collectives: 208 us -> 0 us
  other arithmetic: 225 us -> 87.1 us
  local copies, waits for them, and re-layouts: 126 us -> 36 us
  Pallas kernels: 0 us -> 69.6 us
    ppermute x0 -> x72, waiting for transfers between devices: none -> 457 us  [swap(): return lax.ppermute(values, axis, [(i, i ^ shift) for i in range(size)])]
    dot_general x32 -> x42, matrix products: 511 us -> 182 us  [the longest x20 64.2 us: nn(): lax.dot_general(a, b, (((1,), (0,)), ((), ())), preferred_element_type=f32)]
    all_gather x9 -> x0, waiting for transfers between devices: 323 us -> none  [the longest x1 94.5 us: fetch_mlp(): lax.all_gather(w_down, 'wide', axis=1, tiled=True)]
    reduce_scatter x9 -> x0, waiting for transfers between devices: 322 us -> none  [the longest x4 135 us: sum_rows(): lax.psum_scatter(values.astype(jnp.bfloat16), 'narrow', scatter_dimension...]
    ppermute x0 -> x72, starting transfers between devices: none -> 235 us  [swap(): return lax.ppermute(values, axis, [(i, i ^ shift) for i in range(size)])]
    unnamed x26 -> x0, waiting for transfers between devices: 199 us -> none
    all_gather x4 -> x0, blocking collectives: 126 us -> none  [the longest x1 32.5 us: fetch_mixer(): lax.all_gather(short_kernel, 'wide', axis=2, tiled=True)]
    unnamed x2 -> x0, blocking collectives: 82.1 us -> none
  transfers between devices with their start and end apart: 22 -> 72, of which waited for: 16 -> 25; matrix products, arithmetic and copies ran while one was open for 41% -> 25% of each run, Pallas kernels for 0% -> 2%
where the time goes in v1:
time: 1080 us; the launch traced here: 1070 us
  waiting for transfers between devices  457 us (42%)
  starting transfers between devices  235 us (22%)
  matrix products  182 us (17%)
  other arithmetic  87.1 us (8%)
  Pallas kernels  69.6 us (6%)
  local copies, waits for them, and re-layouts  36 us (3%)
    ppermute x72, waiting for transfers between devices, swap(): return lax.ppermute(values, axis, [(i, i ^ shift) for i in range(size)])  457 us
    ppermute x72, starting transfers between devices, swap(): return lax.ppermute(values, axis, [(i, i ^ shift) for i in range(size)])  235 us
    dot_general x20, matrix products, nn(): lax.dot_general(a, b, (((1,), (0,)), ((), ())), preferred_element_type=f32)  64.2 us
    dot_general x10, matrix products, nt(): lax.dot_general(a, b, (((1,), (1,)), ((), ())), preferred_element_type=f32)  59.5 us
    dot_general x10, matrix products, tn(): lax.dot_general(a, b, (((0,), (0,)), ((), ())), preferred_element_type=f32)  53.1 us
    pallas_call x2, Pallas kernels, mixer_backward(): pl.pallas_call(backward_kernel, out_shape=(jax.ShapeDtypeStruct((pieces,...  31.2 us
    another operation x8, other arithmetic  25.1 us
  transfers between devices with their start and end apart: 72, of which 25 were waited for; matrix products, arithmetic and copies ran while one was open for 25% of the time, Pallas kernels for 2%

profile of v1, /device:TPU:0, one launch (start us, length us, event | category | flops | bytes accessed | tf_op | source)
XLA Modules:
  0.0 1069.4 jit_solution(13277089353720780119)
XLA Ops:
  34.8 21.5 %collective-permute-done.6 = bf16[256,2048]{1,0:T(8,128)(2,1)S(1)} collective-permute-done((bf16[256,2048]{1,0:T(8,128)(2,1)S(1)}, bf16[256,2048]{1,0:T(8,128)(2,1)S(1)}, u32[]{:S(2)}, u32[]{:S(2)}) %collective-permute-start.6) | collective-permute-done | bytes 1048608 | tf_op jit(solution)/shard_map/ppermute | solution.py:42
  60.5 4.1 taps.2
  67.4 10.0 collective-permute-start.13
  77.5 15.8 %collective-permute-done.9 = bf16[3,64,2048]{2,1,0:T(8,128)(2,1)} collective-permute-done((bf16[3,64,2048]{2,1,0:T(8,128)(2,1)}, bf16[3,64,2048]{2,1,0:T(8,128)(2,1)}, u32[]{:S(2)}, u32[]{:S(2)}) %collective-permute-start.9) | collective-permute-done | bytes 786464 | tf_op jit(solution)/shard_map/ppermute | solution.py:42
  103.3 4.1 taps.3
  118.8 5.5 fusion.94.proj
  124.4 7.3 mixer_forward.2
  132.9 34.9 %collective-permute-done.14 = bf16[3,256,2048]{2,1,0:T(8,128)(2,1)} collective-permute-done((bf16[3,256,2048]{2,1,0:T(8,128)(2,1)}, bf16[3,256,2048]{2,1,0:T(8,128)(2,1)}, u32[]{:S(2)}, u32[]{:S(2)}) %collective-permute-start.14) | collective-permute-done | bytes 3145760 | tf_op jit(solution)/shard_map/ppermute | solution.py:42
  167.8 5.3 fusion.96.proj
  173.1 7.0 mixer_forward.3
  180.3 6.3 collective-permute-done.15
  202.3 19.1 %collective-permute-done.17 = bf16[256,2048]{1,0:T(8,128)(2,1)} collective-permute-done((bf16[256,2048]{1,0:T(8,128)(2,1)S(1)}, bf16[256,2048]{1,0:T(8,128)(2,1)}, u32[]{:S(2)}, u32[]{:S(2)}) %collective-permute-start.17) | collective-permute-done | bytes 1048608 | tf_op jit(solution)/shard_map/ppermute | solution.py:42
  226.5 5.8 collective-permute-done.23
  232.3 16.7 %collective-permute-done.24 = bf16[176,2048]{1,0:T(8,128)(2,1)} collective-permute-done((bf16[176,2048]{1,0:T(8,128)(2,1)}, bf16[176,2048]{1,0:T(8,128)(2,1)}, u32[]{:S(2)}, u32[]{:S(2)}) %collective-permute-start.24) | collective-permute-done | bytes 720928 | tf_op jit(solution)/shard_map/ppermute | solution.py:42
  254.7 7.8 collective-permute-done.20
  262.4 37.0 %collective-permute-start.26 = (bf16[176,2048]{1,0:T(8,128)(2,1)S(1)}, bf16[176,2048]{1,0:T(8,128)(2,1)S(1)}, u32[]{:S(2)}, u32[]{:S(2)}) collective-permute-start(bf16[176,2048]{1,0:T(8,128)(2,1)S(1)} %bitcast.185), channel_id=1, source_target_pairs={{0,8},{4,12},{8,0},{12,4},{16,24},{20,28},{24,16},{28,20},{1,9},{5... | collective-permute-start | bytes 2162696 | tf_op jit(solution)/shard_map/ppermute | solution.py:42
  299.4 11.3 %collective-permute-done.21 = bf16[176,2048]{1,0:T(8,128)(2,1)S(1)} collective-permute-done((bf16[176,2048]{1,0:T(8,128)(2,1)}, bf16[176,2048]{1,0:T(8,128)(2,1)S(1)}, u32[]{:S(2)}, u32[]{:S(2)}) %collective-permute-start.21) | collective-permute-done | bytes 720928 | tf_op jit(solution)/shard_map/ppermute | solution.py:42
  317.4 55.2 %collective-permute-done.27 = bf16[176,2048]{1,0:T(8,128)(2,1)S(1)} collective-permute-done((bf16[176,2048]{1,0:T(8,128)(2,1)S(1)}, bf16[176,2048]{1,0:T(8,128)(2,1)S(1)}, u32[]{:S(2)}, u32[]{:S(2)}) %collective-permute-start.27) | collective-permute-done | bytes 720928 | tf_op jit(solution)/shard_map/ppermute | solution.py:42
  376.2 19.4 %collective-permute-done.34 = bf16[256,2048]{1,0:T(8,128)(2,1)S(1)} collective-permute-done((bf16[256,2048]{1,0:T(8,128)(2,1)S(1)}, bf16[256,2048]{1,0:T(8,128)(2,1)S(1)}, u32[]{:S(2)}, u32[]{:S(2)}) %collective-permute-start.34) | collective-permute-done | bytes 1048608 | tf_op jit(solution)/shard_map/ppermute | solution.py:42
  396.5 4.8 fusion.73
  401.2 4.8 fusion.74
  406.0 32.4 %collective-permute-done.31 = bf16[704,2048]{1,0:T(8,128)(2,1)S(1)} collective-permute-done((bf16[704,2048]{1,0:T(8,128)(2,1)S(1)}, bf16[704,2048]{1,0:T(8,128)(2,1)S(1)}, u32[]{:S(2)}, u32[]{:S(2)}) %collective-permute-start.31) | collective-permute-done | bytes 2883616 | tf_op jit(solution)/shard_map/ppermute | solution.py:42
  438.5 8.1 multiply_convert_fusion
  446.6 4.5 convolution_convert_fusion.2
  452.7 4.5 convolution_convert_fusion.4
  457.7 4.6 convolution_convert_fusion.6
  463.9 6.5 fusion.71
  470.5 6.1 fusion.72
  478.5 10.8 %multiply_convert_fusion.2 = (bf16[1024,704]{0,1:T(8,128)(2,1)}, bf16[1024,704]{0,1:T(8,128)(2,1)}, bf16[1024,704]{0,1:T(8,128)(2,1)}) fusion(f32[1024,704]{0,1:T(8,128)} %fusion.72, f32[1024,704]{0,1:T(8,128)} %fusion.71, bf16[176,2048]{1,0:T(8,128)(2,1)} %copy-done.81, bf16[176,2048]{1,0:T(8,128)(2,1)} %copy-done.79, bf16[176,2048]{1,0:T(8,128)(2,1)} %copy-done.77, ...), kind=kOutput, calls=%fused_computation.40 | convolution fusion | flops 2987720704 | bytes 17170432 | tf_op jit(solution)/shard_map/dot_general | solution.py:33
  489.2 5.4 add_convert_fusion.4
  506.8 7.3 convolution_convert_fusion.3
  514.1 4.6 convolution_convert_fusion.5
  520.6 5.8 fusion.44
  532.7 5.3 fusion.46
  542.0 4.5 convolution_convert_fusion.7
  549.2 9.0 convert_add_fusion.6
  559.0 6.7 fusion.65
  566.8 45.9 %collective-permute-start.69 = (bf16[176,2048]{1,0:T(8,128)(2,1)S(1)}, bf16[176,2048]{1,0:T(8,128)(2,1)S(1)}, u32[]{:S(2)}, u32[]{:S(2)}) collective-permute-start(bf16[176,2048]{1,0:T(8,128)(2,1)S(1)} %get-tuple-element.96), channel_id=1, source_target_pairs={{0,8},{4,12},{8,0},{12,4},{16,24},{20,28},{24,16},{28,20},{1,9},{5... | collective-permute-start | bytes 2162696 | tf_op jit(solution)/shard_map/ppermute | solution.py:42
  612.7 12.1 %collective-permute-start.70 = (bf16[176,2048]{1,0:T(8,128)(2,1)S(1)}, bf16[176,2048]{1,0:T(8,128)(2,1)S(1)}, u32[]{:S(2)}, u32[]{:S(2)}) collective-permute-start(bf16[176,2048]{1,0:T(8,128)(2,1)S(1)} %get-tuple-element.98), channel_id=1, source_target_pairs={{0,16},{4,20},{8,24},{12,28},{16,0},{20,4},{24,8},{28,12},{1,17},{... | collective-permute-start | bytes 2162696 | tf_op jit(solution)/shard_map/ppermute | solution.py:42
  624.8 5.7 fusion.64
  633.6 4.0 fusion.75
  639.5 42.7 %collective-permute-start.65 = (bf16[176,2048]{1,0:T(8,128)(2,1)}, bf16[176,2048]{1,0:T(8,128)(2,1)S(1)}, u32[]{:S(2)}, u32[]{:S(2)}) collective-permute-start(bf16[176,2048]{1,0:T(8,128)(2,1)} %get-tuple-element.99), channel_id=1, source_target_pairs={{0,8},{4,12},{8,0},{12,4},{16,24},{20,28},{24,16},{28,20},{1,9},{5... | collective-permute-start | bytes 2162696 | tf_op jit(solution)/shard_map/ppermute | solution.py:42
  682.2 5.6 fusion.63
  694.6 15.2 %collective-permute-done.65 = bf16[176,2048]{1,0:T(8,128)(2,1)S(1)} collective-permute-done((bf16[176,2048]{1,0:T(8,128)(2,1)}, bf16[176,2048]{1,0:T(8,128)(2,1)S(1)}, u32[]{:S(2)}, u32[]{:S(2)}) %collective-permute-start.65) | collective-permute-done | bytes 720928 | tf_op jit(solution)/shard_map/ppermute | solution.py:42
  709.8 29.1 %collective-permute-done.66 = bf16[176,2048]{1,0:T(8,128)(2,1)S(1)} collective-permute-done((bf16[176,2048]{1,0:T(8,128)(2,1)}, bf16[176,2048]{1,0:T(8,128)(2,1)S(1)}, u32[]{:S(2)}, u32[]{:S(2)}) %collective-permute-start.66) | collective-permute-done | bytes 720928 | tf_op jit(solution)/shard_map/ppermute | solution.py:42
  747.0 53.0 %collective-permute-done.62 = bf16[176,2048]{1,0:T(8,128)(2,1)S(1)} collective-permute-done((bf16[176,2048]{1,0:T(8,128)(2,1)}, bf16[176,2048]{1,0:T(8,128)(2,1)S(1)}, u32[]{:S(2)}, u32[]{:S(2)}) %collective-permute-start.62) | collective-permute-done | bytes 720928 | tf_op jit(solution)/shard_map/ppermute | solution.py:42
  806.8 15.5 %mixer_backward.2 = (bf16[4,256,768]{2,1,0:T(8,128)(2,1)}, f32[512,256]{1,0:T(8,128)S(1)}, f32[8,768]{1,0:T(8,128)S(1)}) custom-call(s32[4]{0:T(128)S(1)} %copy-done.28, s32[3]{0:T(128)S(1)} %copy-done.26, s32[3]{0:T(128)S(1)} %bitcast.158, f32[4,256,768]{2,1,0:T(8,128)} %copy-done.6, f32[4,256,256]{2,1,0:T(8,128)S(1)} %bitcast.152, ...), custom_call_target="tpu_custom_call" | custom-call | flops 2013265920 | bytes 8388608 | tf_op jit(solution)/shard_map/mixer_backward/pallas_call | solution.py:373
  823.2 7.9 moments.2
  835.0 15.6 %mixer_backward.3 = (bf16[4,256,768]{2,1,0:T(8,128)(2,1)}, f32[512,256]{1,0:T(8,128)S(1)}, f32[8,768]{1,0:T(8,128)S(1)}) custom-call(s32[4]{0:T(128)S(1)} %copy-done.28, s32[3]{0:T(128)S(1)} %copy-done.26, s32[3]{0:T(128)S(1)} %bitcast.159, f32[4,256,768]{2,1,0:T(8,128)} %copy-done.5, f32[4,256,256]{2,1,0:T(8,128)S(1)} %bitcast.151, ...), custom_call_target="tpu_custom_call" | custom-call | flops 2013265920 | bytes 8388608 | tf_op jit(solution)/shard_map/mixer_backward/pallas_call | solution.py:373
  851.5 8.1 moments.3
  869.8 5.3 add_convert_fusion
  875.2 4.0 convolution_convert_fusion.8
  880.4 6.9 convolution_convert_fusion.1
  887.3 6.8 convolution_convert_fusion
  894.2 6.0 fusion.100
  901.7 11.5 %collective-permute-start.57 = (bf16[73,64]{1,0:T(8,128)(2,1)S(1)}, bf16[73,64]{1,0:T(8,128)(2,1)S(1)}, u32[]{:S(2)}, u32[]{:S(2)}) collective-permute-start(bf16[73,64]{1,0:T(8,128)(2,1)S(1)} %get-tuple-element.137), channel_id=1, source_target_pairs={{0,8},{4,12},{8,0},{12,4},{16,24},{20,28},{24,16},{28,20},{1,9},{5... | collective-permute-start | bytes 28040 | tf_op jit(solution)/shard_map/ppermute | solution.py:42
  915.6 4.9 add_convert_fusion.1
  930.2 5.3 fusion.93
  940.6 12.5 %collective-permute-done.41 = bf16[256,2048]{1,0:T(8,128)(2,1)S(1)} collective-permute-done((bf16[256,2048]{1,0:T(8,128)(2,1)}, bf16[256,2048]{1,0:T(8,128)(2,1)S(1)}, u32[]{:S(2)}, u32[]{:S(2)}) %collective-permute-start.41) | collective-permute-done | bytes 1048608 | tf_op jit(solution)/shard_map/ppermute | solution.py:42
  954.2 4.4 collective-permute-done.48
  962.2 28.5 %collective-permute-done.42 = bf16[3,256,2048]{2,1,0:T(8,128)(2,1)} collective-permute-done((bf16[3,256,2048]{2,1,0:T(8,128)(2,1)}, bf16[3,256,2048]{2,1,0:T(8,128)(2,1)}, u32[]{:S(2)}, u32[]{:S(2)}) %collective-permute-start.42) | collective-permute-done | bytes 3145760 | tf_op jit(solution)/shard_map/ppermute | solution.py:42
  990.7 4.5 fusion.66
  1004.0 43.1 %collective-permute-done.53 = f32[2,64]{1,0:T(2,128)S(1)} collective-permute-done((f32[2,64]{1,0:T(2,128)S(1)}, f32[2,64]{1,0:T(2,128)S(1)}, u32[]{:S(2)}, u32[]{:S(2)}) %collective-permute-start.53) | collective-permute-done | bytes 544 | tf_op jit(solution)/shard_map/ppermute | solution.py:42
  1050.4 16.6 %collective-permute-done.54 = f32[2,64]{1,0:T(2,128)S(1)} collective-permute-done((f32[2,64]{1,0:T(2,128)S(1)}, f32[2,64]{1,0:T(2,128)S(1)}, u32[]{:S(2)}, u32[]{:S(2)}) %collective-permute-start.54) | collective-permute-done | bytes 544 | tf_op jit(solution)/shard_map/ppermute | solution.py:42
  (507 shorter events, 216.1 us)
Async XLA Ops:
  4.5 13.2 %collective-permute-start = (bf16[75,64]{1,0:T(8,128)(2,1)S(1)}, bf16[75,64]{1,0:T(8,128)(2,1)S(1)}, u32[]{:S(2)}, u32[]{:S(2)}) collective-permute-start(bf16[75,64]{1,0:T(8,128)(2,1)S(1)} %concatenate.92), channel_id=1, source_target_pairs={{0,8},{4,12},{8,0},{12,4},{16,24},{20,28},{24,16},{28,20},{1,9},{5... | collective-permute-start | bytes 28808 | tf_op jit(solution)/shard_map/ppermute | solution.py:42
  7.6 10.8 %collective-permute-start.1 = (bf16[75,64]{1,0:T(8,128)(2,1)S(1)}, bf16[75,64]{1,0:T(8,128)(2,1)S(1)}, u32[]{:S(2)}, u32[]{:S(2)}) collective-permute-start(bf16[75,64]{1,0:T(8,128)(2,1)S(1)} %concatenate.92), channel_id=1, source_target_pairs={{0,16},{4,20},{8,24},{12,28},{16,0},{20,4},{24,8},{28,12},{1,17},{... | collective-permute-start | bytes 28808 | tf_op jit(solution)/shard_map/ppermute | solution.py:42
  10.2 9.7 collective-permute-start.2
  10.2 54.3 %collective-permute-start.10 = (bf16[3,64,2048]{2,1,0:T(8,128)(2,1)}, bf16[3,64,2048]{2,1,0:T(8,128)(2,1)}, u32[]{:S(2)}, u32[]{:S(2)}) collective-permute-start(bf16[3,64,2048]{2,1,0:T(8,128)(2,1)} %bitcast.175), channel_id=1, source_target_pairs={{0,24},{4,28},{8,16},{12,20},{16,8},{20,12},{24,0},{28,4},{1,25},{... | collective-permute-start | bytes 2359304 | tf_op jit(solution)/shard_map/ppermute | solution.py:42
  14.0 53.4 %collective-permute-start.8 = (bf16[3,64,2048]{2,1,0:T(8,128)(2,1)}, bf16[3,64,2048]{2,1,0:T(8,128)(2,1)}, u32[]{:S(2)}, u32[]{:S(2)}) collective-permute-start(bf16[3,64,2048]{2,1,0:T(8,128)(2,1)} %bitcast.176), channel_id=1, source_target_pairs={{0,8},{4,12},{8,0},{12,4},{16,24},{20,28},{24,16},{28,20},{1,9},{5... | collective-permute-start | bytes 2359304 | tf_op jit(solution)/shard_map/ppermute | solution.py:42
  17.7 75.5 %collective-permute-start.9 = (bf16[3,64,2048]{2,1,0:T(8,128)(2,1)}, bf16[3,64,2048]{2,1,0:T(8,128)(2,1)}, u32[]{:S(2)}, u32[]{:S(2)}) collective-permute-start(bf16[3,64,2048]{2,1,0:T(8,128)(2,1)} %bitcast.177), channel_id=1, source_target_pairs={{0,16},{4,20},{8,24},{12,28},{16,0},{20,4},{24,8},{28,12},{1,17},{... | collective-permute-start | bytes 2359304 | tf_op jit(solution)/shard_map/ppermute | solution.py:42
  18.4 92.5 %collective-permute-start.11 = (bf16[64,2048]{1,0:T(8,128)(2,1)}, bf16[64,2048]{1,0:T(8,128)(2,1)}, u32[]{:S(2)}, u32[]{:S(2)}) collective-permute-start(bf16[64,2048]{1,0:T(8,128)(2,1)} %param.21), channel_id=1, source_target_pairs={{0,8},{4,12},{8,0},{12,4},{16,24},{20,28},{24,16},{28,20},{1,9},{5... | collective-permute-start | bytes 786440 | tf_op jit(solution)/shard_map/ppermute | solution.py:42
  31.0 25.3 %collective-permute-start.6 = (bf16[256,2048]{1,0:T(8,128)(2,1)S(1)}, bf16[256,2048]{1,0:T(8,128)(2,1)S(1)}, u32[]{:S(2)}, u32[]{:S(2)}) collective-permute-start(bf16[256,2048]{1,0:T(8,128)(2,1)S(1)} %fusion.6), channel_id=1, source_target_pairs={{0,2},{1,3},{2,0},{3,1},{4,6},{5,7},{6,4},{7,5},{8,10},{9,11},{10,... | collective-permute-start | bytes 3145736 | tf_op jit(solution)/shard_map/ppermute | solution.py:42
  57.9 58.5 %collective-permute-start.7 = (bf16[512,2048]{1,0:T(8,128)(2,1)}, bf16[512,2048]{1,0:T(8,128)(2,1)}, u32[]{:S(2)}, u32[]{:S(2)}) collective-permute-start(bf16[512,2048]{1,0:T(8,128)(2,1)} %pad_maximum_fusion.8), channel_id=1, source_target_pairs={{0,1},{1,0},{2,3},{3,2},{4,5},{5,4},{6,7},{7,6},{8,9},{9,8},{10,11... | collective-permute-start | bytes 6291464 | tf_op jit(solution)/shard_map/ppermute | solution.py:42
  64.5 48.1 %collective-permute-start.12 = (bf16[64,2048]{1,0:T(8,128)(2,1)}, bf16[64,2048]{1,0:T(8,128)(2,1)}, u32[]{:S(2)}, u32[]{:S(2)}) collective-permute-start(bf16[64,2048]{1,0:T(8,128)(2,1)} %param.21), channel_id=1, source_target_pairs={{0,16},{4,20},{8,24},{12,28},{16,0},{20,4},{24,8},{28,12},{1,17},{... | collective-permute-start | bytes 786440 | tf_op jit(solution)/shard_map/ppermute | solution.py:42
  67.4 46.8 %collective-permute-start.13 = (bf16[64,2048]{1,0:T(8,128)(2,1)}, bf16[64,2048]{1,0:T(8,128)(2,1)}, u32[]{:S(2)}, u32[]{:S(2)}) collective-permute-start(bf16[64,2048]{1,0:T(8,128)(2,1)} %param.21), channel_id=1, source_target_pairs={{0,24},{4,28},{8,16},{12,20},{16,8},{20,12},{24,0},{28,4},{1,25},{... | collective-permute-start | bytes 786440 | tf_op jit(solution)/shard_map/ppermute | solution.py:42
  96.4 71.4 %collective-permute-start.14 = (bf16[3,256,2048]{2,1,0:T(8,128)(2,1)}, bf16[3,256,2048]{2,1,0:T(8,128)(2,1)}, u32[]{:S(2)}, u32[]{:S(2)}) collective-permute-start(bf16[3,256,2048]{2,1,0:T(8,128)(2,1)} %pad_maximum_fusion.4), channel_id=1, source_target_pairs={{0,4},{4,0},{8,12},{12,8},{16,20},{20,16},{24,28},{28,24},{1,5},{5... | collective-permute-start | bytes 9437192 | tf_op jit(solution)/shard_map/ppermute | solution.py:42
  115.9 70.6 %collective-permute-start.15 = (bf16[256,2048]{1,0:T(8,128)(2,1)}, bf16[256,2048]{1,0:T(8,128)(2,1)S(1)}, u32[]{:S(2)}, u32[]{:S(2)}) collective-permute-start(bf16[256,2048]{1,0:T(8,128)(2,1)} %constant_dynamic-update-slice_fusion), channel_id=1, source_target_pairs={{0,4},{4,0},{8,12},{12,8},{16,20},{20,16},{24,28},{28,24},{1,5},{5... | collective-permute-start | bytes 3145736 | tf_op jit(solution)/shard_map/ppermute | solution.py:42
  196.1 25.4 %collective-permute-start.17 = (bf16[256,2048]{1,0:T(8,128)(2,1)S(1)}, bf16[256,2048]{1,0:T(8,128)(2,1)}, u32[]{:S(2)}, u32[]{:S(2)}) collective-permute-start(bf16[256,2048]{1,0:T(8,128)(2,1)S(1)} %slice.440), channel_id=1, source_target_pairs={{0,2},{1,3},{2,0},{3,1},{4,6},{5,7},{6,4},{7,5},{8,10},{9,11},{10,... | collective-permute-start | bytes 3145736 | tf_op jit(solution)/shard_map/ppermute | solution.py:42
  197.9 34.5 %collective-permute-start.23 = (bf16[176,2048]{1,0:T(8,128)(2,1)}, bf16[176,2048]{1,0:T(8,128)(2,1)}, u32[]{:S(2)}, u32[]{:S(2)}) collective-permute-start(bf16[176,2048]{1,0:T(8,128)(2,1)} %bitcast.29), channel_id=1, source_target_pairs={{0,8},{4,12},{8,0},{12,4},{16,24},{20,28},{24,16},{28,20},{1,9},{5... | collective-permute-start | bytes 2162696 | tf_op jit(solution)/shard_map/ppermute | solution.py:42
  197.9 51.2 %collective-permute-start.24 = (bf16[176,2048]{1,0:T(8,128)(2,1)}, bf16[176,2048]{1,0:T(8,128)(2,1)}, u32[]{:S(2)}, u32[]{:S(2)}) collective-permute-start(bf16[176,2048]{1,0:T(8,128)(2,1)} %bitcast.29), channel_id=1, source_target_pairs={{0,16},{4,20},{8,24},{12,28},{16,0},{20,4},{24,8},{28,12},{1,17},{... | collective-permute-start | bytes 2162696 | tf_op jit(solution)/shard_map/ppermute | solution.py:42
  200.6 50.6 %collective-permute-start.25 = (bf16[176,2048]{1,0:T(8,128)(2,1)}, bf16[176,2048]{1,0:T(8,128)(2,1)}, u32[]{:S(2)}, u32[]{:S(2)}) collective-permute-start(bf16[176,2048]{1,0:T(8,128)(2,1)} %bitcast.29), channel_id=1, source_target_pairs={{0,24},{4,28},{8,16},{12,20},{16,8},{20,12},{24,0},{28,4},{1,25},{... | collective-permute-start | bytes 2162696 | tf_op jit(solution)/shard_map/ppermute | solution.py:42
  202.2 60.2 %collective-permute-start.20 = (bf16[176,2048]{1,0:T(8,128)(2,1)}, bf16[176,2048]{1,0:T(8,128)(2,1)}, u32[]{:S(2)}, u32[]{:S(2)}) collective-permute-start(bf16[176,2048]{1,0:T(8,128)(2,1)} %bitcast.28), channel_id=1, source_target_pairs={{0,8},{4,12},{8,0},{12,4},{16,24},{20,28},{24,16},{28,20},{1,9},{5... | collective-permute-start | bytes 2162696 | tf_op jit(solution)/shard_map/ppermute | solution.py:42
  224.8 89.7 %collective-permute-start.18 = (bf16[256,2048]{1,0:T(8,128)(2,1)S(1)}, bf16[256,2048]{1,0:T(8,128)(2,1)S(1)}, u32[]{:S(2)}, u32[]{:S(2)}) collective-permute-start(bf16[256,2048]{1,0:T(8,128)(2,1)S(1)} %multiply_convert_fusion.6), channel_id=1, source_target_pairs={{0,2},{1,3},{2,0},{3,1},{4,6},{5,7},{6,4},{7,5},{8,10},{9,11},{10,... | collective-permute-start | bytes 3145736 | tf_op jit(solution)/shard_map/ppermute | solution.py:42
  232.3 78.4 %collective-permute-start.21 = (bf16[176,2048]{1,0:T(8,128)(2,1)}, bf16[176,2048]{1,0:T(8,128)(2,1)S(1)}, u32[]{:S(2)}, u32[]{:S(2)}) collective-permute-start(bf16[176,2048]{1,0:T(8,128)(2,1)} %bitcast.28), channel_id=1, source_target_pairs={{0,16},{4,20},{8,24},{12,28},{16,0},{20,4},{24,8},{28,12},{1,17},{... | collective-permute-start | bytes 2162696 | tf_op jit(solution)/shard_map/ppermute | solution.py:42
  249.0 61.7 %collective-permute-start.22 = (bf16[176,2048]{1,0:T(8,128)(2,1)}, bf16[176,2048]{1,0:T(8,128)(2,1)S(1)}, u32[]{:S(2)}, u32[]{:S(2)}) collective-permute-start(bf16[176,2048]{1,0:T(8,128)(2,1)} %bitcast.28), channel_id=1, source_target_pairs={{0,24},{4,28},{8,16},{12,20},{16,8},{20,12},{24,0},{28,4},{1,25},{... | collective-permute-start | bytes 2162696 | tf_op jit(solution)/shard_map/ppermute | solution.py:42
  253.1 143.4 %collective-permute-start.30 = (bf16[704,2048]{1,0:T(8,128)(2,1)S(1)}, bf16[704,2048]{1,0:T(8,128)(2,1)S(1)}, u32[]{:S(2)}, u32[]{:S(2)}) collective-permute-start(bf16[704,2048]{1,0:T(8,128)(2,1)S(1)} %pad_maximum_fusion.6), channel_id=1, source_target_pairs={{0,4},{4,0},{8,12},{12,8},{16,20},{20,16},{24,28},{28,24},{1,5},{5... | collective-permute-start | bytes 8650760 | tf_op jit(solution)/shard_map/ppermute | solution.py:42
  262.4 55.0 %collective-permute-start.26 = (bf16[176,2048]{1,0:T(8,128)(2,1)S(1)}, bf16[176,2048]{1,0:T(8,128)(2,1)S(1)}, u32[]{:S(2)}, u32[]{:S(2)}) collective-permute-start(bf16[176,2048]{1,0:T(8,128)(2,1)S(1)} %bitcast.185), channel_id=1, source_target_pairs={{0,8},{4,12},{8,0},{12,4},{16,24},{20,28},{24,16},{28,20},{1,9},{5... | collective-permute-start | bytes 2162696 | tf_op jit(solution)/shard_map/ppermute | solution.py:42
  310.8 61.8 %collective-permute-start.27 = (bf16[176,2048]{1,0:T(8,128)(2,1)S(1)}, bf16[176,2048]{1,0:T(8,128)(2,1)S(1)}, u32[]{:S(2)}, u32[]{:S(2)}) collective-permute-start(bf16[176,2048]{1,0:T(8,128)(2,1)S(1)} %bitcast.186), channel_id=1, source_target_pairs={{0,16},{4,20},{8,24},{12,28},{16,0},{20,4},{24,8},{28,12},{1,17},{... | collective-permute-start | bytes 2162696 | tf_op jit(solution)/shard_map/ppermute | solution.py:42
  310.8 62.1 %collective-permute-start.28 = (bf16[176,2048]{1,0:T(8,128)(2,1)S(1)}, bf16[176,2048]{1,0:T(8,128)(2,1)S(1)}, u32[]{:S(2)}, u32[]{:S(2)}) collective-permute-start(bf16[176,2048]{1,0:T(8,128)(2,1)S(1)} %bitcast.187), channel_id=1, source_target_pairs={{0,24},{4,28},{8,16},{12,20},{16,8},{20,12},{24,0},{28,4},{1,25},{... | collective-permute-start | bytes 2162696 | tf_op jit(solution)/shard_map/ppermute | solution.py:42
  314.5 86.7 %collective-permute-start.29 = (bf16[704,2048]{1,0:T(8,128)(2,1)S(1)}, bf16[704,2048]{1,0:T(8,128)(2,1)S(1)}, u32[]{:S(2)}, u32[]{:S(2)}) collective-permute-start(bf16[704,2048]{1,0:T(8,128)(2,1)S(1)} %pad_maximum_fusion.5), channel_id=1, source_target_pairs={{0,4},{4,0},{8,12},{12,8},{16,20},{20,16},{24,28},{28,24},{1,5},{5... | collective-permute-start | bytes 8650760 | tf_op jit(solution)/shard_map/ppermute | solution.py:42
  317.4 79.1 %collective-permute-start.19 = (bf16[512,2048]{1,0:T(8,128)(2,1)S(1)}, bf16[512,2048]{1,0:T(8,128)(2,1)S(1)}, u32[]{:S(2)}, u32[]{:S(2)}) collective-permute-start(bf16[512,2048]{1,0:T(8,128)(2,1)S(1)} %pad_maximum_fusion.9), channel_id=1, source_target_pairs={{0,1},{1,0},{2,3},{3,2},{4,5},{5,4},{6,7},{7,6},{8,9},{9,8},{10,11... | collective-permute-start | bytes 6291464 | tf_op jit(solution)/shard_map/ppermute | solution.py:42
  372.6 23.0 %collective-permute-start.34 = (bf16[256,2048]{1,0:T(8,128)(2,1)S(1)}, bf16[256,2048]{1,0:T(8,128)(2,1)S(1)}, u32[]{:S(2)}, u32[]{:S(2)}) collective-permute-start(bf16[256,2048]{1,0:T(8,128)(2,1)S(1)} %bitcast.162), channel_id=1, source_target_pairs={{0,2},{1,3},{2,0},{3,1},{4,6},{5,7},{6,4},{7,5},{8,10},{9,11},{10,... | collective-permute-start | bytes 3145736 | tf_op jit(solution)/shard_map/ppermute | solution.py:42
  374.5 64.0 %collective-permute-start.31 = (bf16[704,2048]{1,0:T(8,128)(2,1)S(1)}, bf16[704,2048]{1,0:T(8,128)(2,1)S(1)}, u32[]{:S(2)}, u32[]{:S(2)}) collective-permute-start(bf16[704,2048]{1,0:T(8,128)(2,1)S(1)} %pad_maximum_fusion.7), channel_id=1, source_target_pairs={{0,4},{4,0},{8,12},{12,8},{16,20},{20,16},{24,28},{28,24},{1,5},{5... | collective-permute-start | bytes 8650760 | tf_op jit(solution)/shard_map/ppermute | solution.py:42
  395.8 10.3 collective-permute-start.35
  451.2 107.9 %collective-permute-start.68 = (bf16[704,2048]{1,0:T(8,128)(2,1)}, bf16[704,2048]{1,0:T(8,128)(2,1)}, u32[]{:S(2)}, u32[]{:S(2)}) collective-permute-start(bf16[704,2048]{1,0:T(8,128)(2,1)} %convolution_convert_fusion.2), channel_id=1, source_target_pairs={{0,4},{4,0},{8,12},{12,8},{16,20},{20,16},{24,28},{28,24},{1,5},{5... | collective-permute-start | bytes 8650760 | tf_op jit(solution)/shard_map/ppermute | solution.py:42
  457.2 155.5 %collective-permute-start.64 = (bf16[704,2048]{1,0:T(8,128)(2,1)}, bf16[704,2048]{1,0:T(8,128)(2,1)}, u32[]{:S(2)}, u32[]{:S(2)}) collective-permute-start(bf16[704,2048]{1,0:T(8,128)(2,1)} %convolution_convert_fusion.4), channel_id=1, source_target_pairs={{0,4},{4,0},{8,12},{12,8},{16,20},{20,16},{24,28},{28,24},{1,5},{5... | collective-permute-start | bytes 8650760 | tf_op jit(solution)/shard_map/ppermute | solution.py:42
  462.3 177.2 %collective-permute-start.60 = (bf16[704,2048]{1,0:T(8,128)(2,1)}, bf16[704,2048]{1,0:T(8,128)(2,1)}, u32[]{:S(2)}, u32[]{:S(2)}) collective-permute-start(bf16[704,2048]{1,0:T(8,128)(2,1)} %convolution_convert_fusion.6), channel_id=1, source_target_pairs={{0,4},{4,0},{8,12},{12,8},{16,20},{20,16},{24,28},{28,24},{1,5},{5... | collective-permute-start | bytes 8650760 | tf_op jit(solution)/shard_map/ppermute | solution.py:42
  494.6 51.9 %collective-permute-start.32 = (bf16[512,2048]{1,0:T(8,128)(2,1)}, bf16[512,2048]{1,0:T(8,128)(2,1)S(1)}, u32[]{:S(2)}, u32[]{:S(2)}) collective-permute-start(bf16[512,2048]{1,0:T(8,128)(2,1)} %add_convert_fusion.4), channel_id=1, source_target_pairs={{0,1},{1,0},{2,3},{3,2},{4,5},{5,4},{6,7},{7,6},{8,9},{9,8},{10,11... | collective-permute-start | bytes 6291464 | tf_op jit(solution)/shard_map/ppermute | solution.py:42
  506.2 43.0 %collective-permute-start.36 = (bf16[512,2048]{1,0:T(8,128)(2,1)S(1)}, bf16[512,2048]{1,0:T(8,128)(2,1)}, u32[]{:S(2)}, u32[]{:S(2)}) collective-permute-start(bf16[512,2048]{1,0:T(8,128)(2,1)S(1)} %add_convert_fusion.2), channel_id=1, source_target_pairs={{0,1},{1,0},{2,3},{3,2},{4,5},{5,4},{6,7},{7,6},{8,9},{9,8},{10,11... | collective-permute-start | bytes 6291464 | tf_op jit(solution)/shard_map/ppermute | solution.py:42
  547.4 86.1 %collective-permute-start.33 = (bf16[256,2048]{1,0:T(8,128)(2,1)S(1)}, bf16[256,2048]{1,0:T(8,128)(2,1)}, u32[]{:S(2)}, u32[]{:S(2)}) collective-permute-start(bf16[256,2048]{1,0:T(8,128)(2,1)S(1)} %slice.439), channel_id=1, source_target_pairs={{0,2},{1,3},{2,0},{3,1},{4,6},{5,7},{6,4},{7,5},{8,10},{9,11},{10,... | collective-permute-start | bytes 3145736 | tf_op jit(solution)/shard_map/ppermute | solution.py:42
  558.4 72.1 %collective-permute-start.37 = (bf16[256,2048]{1,0:T(8,128)(2,1)S(1)}, bf16[256,2048]{1,0:T(8,128)(2,1)S(1)}, u32[]{:S(2)}, u32[]{:S(2)}) collective-permute-start(bf16[256,2048]{1,0:T(8,128)(2,1)S(1)} %slice.438), channel_id=1, source_target_pairs={{0,2},{1,3},{2,0},{3,1},{4,6},{5,7},{6,4},{7,5},{8,10},{9,11},{10,... | collective-permute-start | bytes 3145736 | tf_op jit(solution)/shard_map/ppermute | solution.py:42
  566.8 122.9 %collective-permute-start.69 = (bf16[176,2048]{1,0:T(8,128)(2,1)S(1)}, bf16[176,2048]{1,0:T(8,128)(2,1)S(1)}, u32[]{:S(2)}, u32[]{:S(2)}) collective-permute-start(bf16[176,2048]{1,0:T(8,128)(2,1)S(1)} %get-tuple-element.96), channel_id=1, source_target_pairs={{0,8},{4,12},{8,0},{12,4},{16,24},{20,28},{24,16},{28,20},{1,9},{5... | collective-permute-start | bytes 2162696 | tf_op jit(solution)/shard_map/ppermute | solution.py:42
  612.7 79.1 %collective-permute-start.70 = (bf16[176,2048]{1,0:T(8,128)(2,1)S(1)}, bf16[176,2048]{1,0:T(8,128)(2,1)S(1)}, u32[]{:S(2)}, u32[]{:S(2)}) collective-permute-start(bf16[176,2048]{1,0:T(8,128)(2,1)S(1)} %get-tuple-element.98), channel_id=1, source_target_pairs={{0,16},{4,20},{8,24},{12,28},{16,0},{20,4},{24,8},{28,12},{1,17},{... | collective-permute-start | bytes 2162696 | tf_op jit(solution)/shard_map/ppermute | solution.py:42
  630.5 62.9 %collective-permute-start.71 = (bf16[176,2048]{1,0:T(8,128)(2,1)}, bf16[176,2048]{1,0:T(8,128)(2,1)}, u32[]{:S(2)}, u32[]{:S(2)}) collective-permute-start(bf16[176,2048]{1,0:T(8,128)(2,1)} %get-tuple-element.97), channel_id=1, source_target_pairs={{0,24},{4,28},{8,16},{12,20},{16,8},{20,12},{24,0},{28,4},{1,25},{... | collective-permute-start | bytes 2162696 | tf_op jit(solution)/shard_map/ppermute | solution.py:42
  637.6 50.3 %collective-permute-start.38 = (bf16[256,2048]{1,0:T(8,128)(2,1)S(1)}, bf16[256,2048]{1,0:T(8,128)(2,1)S(1)}, u32[]{:S(2)}, u32[]{:S(2)}) collective-permute-start(bf16[256,2048]{1,0:T(8,128)(2,1)S(1)} %get-tuple-element.71), channel_id=1, source_target_pairs={{0,2},{1,3},{2,0},{3,1},{4,6},{5,7},{6,4},{7,5},{8,10},{9,11},{10,... | collective-permute-start | bytes 3145736 | tf_op jit(solution)/shard_map/ppermute | solution.py:42
  639.5 70.3 %collective-permute-start.65 = (bf16[176,2048]{1,0:T(8,128)(2,1)}, bf16[176,2048]{1,0:T(8,128)(2,1)S(1)}, u32[]{:S(2)}, u32[]{:S(2)}) collective-permute-start(bf16[176,2048]{1,0:T(8,128)(2,1)} %get-tuple-element.99), channel_id=1, source_target_pairs={{0,8},{4,12},{8,0},{12,4},{16,24},{20,28},{24,16},{28,20},{1,9},{5... | collective-permute-start | bytes 2162696 | tf_op jit(solution)/shard_map/ppermute | solution.py:42
  687.9 51.0 %collective-permute-start.66 = (bf16[176,2048]{1,0:T(8,128)(2,1)}, bf16[176,2048]{1,0:T(8,128)(2,1)S(1)}, u32[]{:S(2)}, u32[]{:S(2)}) collective-permute-start(bf16[176,2048]{1,0:T(8,128)(2,1)} %get-tuple-element.101), channel_id=1, source_target_pairs={{0,16},{4,20},{8,24},{12,28},{16,0},{20,4},{24,8},{28,12},{1,17},{... | collective-permute-start | bytes 2162696 | tf_op jit(solution)/shard_map/ppermute | solution.py:42
  689.7 54.4 %collective-permute-start.67 = (bf16[176,2048]{1,0:T(8,128)(2,1)}, bf16[176,2048]{1,0:T(8,128)(2,1)S(1)}, u32[]{:S(2)}, u32[]{:S(2)}) collective-permute-start(bf16[176,2048]{1,0:T(8,128)(2,1)} %get-tuple-element.100), channel_id=1, source_target_pairs={{0,24},{4,28},{8,16},{12,20},{16,8},{20,12},{24,0},{28,4},{1,25},{... | collective-permute-start | bytes 2162696 | tf_op jit(solution)/shard_map/ppermute | solution.py:42
  691.8 111.2 %collective-permute-start.39 = (bf16[512,2048]{1,0:T(8,128)(2,1)}, bf16[512,2048]{1,0:T(8,128)(2,1)}, u32[]{:S(2)}, u32[]{:S(2)}) collective-permute-start(bf16[512,2048]{1,0:T(8,128)(2,1)} %pad_maximum_fusion.11), channel_id=1, source_target_pairs={{0,1},{1,0},{2,3},{3,2},{4,5},{5,4},{6,7},{7,6},{8,9},{9,8},{10,11... | collective-permute-start | bytes 6291464 | tf_op jit(solution)/shard_map/ppermute | solution.py:42
  693.4 53.6 %collective-permute-start.61 = (bf16[176,2048]{1,0:T(8,128)(2,1)}, bf16[176,2048]{1,0:T(8,128)(2,1)S(1)}, u32[]{:S(2)}, u32[]{:S(2)}) collective-permute-start(bf16[176,2048]{1,0:T(8,128)(2,1)} %get-tuple-element.102), channel_id=1, source_target_pairs={{0,8},{4,12},{8,0},{12,4},{16,24},{20,28},{24,16},{28,20},{1,9},{5... | collective-permute-start | bytes 2162696 | tf_op jit(solution)/shard_map/ppermute | solution.py:42
  709.8 90.2 %collective-permute-start.62 = (bf16[176,2048]{1,0:T(8,128)(2,1)}, bf16[176,2048]{1,0:T(8,128)(2,1)S(1)}, u32[]{:S(2)}, u32[]{:S(2)}) collective-permute-start(bf16[176,2048]{1,0:T(8,128)(2,1)} %get-tuple-element.104), channel_id=1, source_target_pairs={{0,16},{4,20},{8,24},{12,28},{16,0},{20,4},{24,8},{28,12},{1,17},{... | collective-permute-start | bytes 2162696 | tf_op jit(solution)/shard_map/ppermute | solution.py:42
  738.9 61.1 %collective-permute-start.63 = (bf16[176,2048]{1,0:T(8,128)(2,1)}, bf16[176,2048]{1,0:T(8,128)(2,1)S(1)}, u32[]{:S(2)}, u32[]{:S(2)}) collective-permute-start(bf16[176,2048]{1,0:T(8,128)(2,1)} %get-tuple-element.103), channel_id=1, source_target_pairs={{0,24},{4,28},{8,16},{12,20},{16,8},{20,12},{24,0},{28,4},{1,25},{... | collective-permute-start | bytes 2162696 | tf_op jit(solution)/shard_map/ppermute | solution.py:42
  862.9 38.7 %collective-permute-start.56 = (bf16[73,256]{1,0:T(8,128)(2,1)S(1)}, bf16[73,256]{1,0:T(8,128)(2,1)S(1)}, u32[]{:S(2)}, u32[]{:S(2)}) collective-permute-start(bf16[73,256]{1,0:T(8,128)(2,1)S(1)} %concatenate.115), channel_id=1, source_target_pairs={{0,4},{4,0},{8,12},{12,8},{16,20},{20,16},{24,28},{28,24},{1,5},{5... | collective-permute-start | bytes 112136 | tf_op jit(solution)/shard_map/ppermute | solution.py:42
  875.1 47.8 %collective-permute-start.40 = (bf16[512,2048]{1,0:T(8,128)(2,1)}, bf16[512,2048]{1,0:T(8,128)(2,1)}, u32[]{:S(2)}, u32[]{:S(2)}) collective-permute-start(bf16[512,2048]{1,0:T(8,128)(2,1)} %add_convert_fusion), channel_id=1, source_target_pairs={{0,1},{1,0},{2,3},{3,2},{4,5},{5,4},{6,7},{7,6},{8,9},{9,8},{10,11... | collective-permute-start | bytes 6291464 | tf_op jit(solution)/shard_map/ppermute | solution.py:42
  879.2 51.0 %collective-permute-start.46 = (bf16[256,2048]{1,0:T(8,128)(2,1)}, bf16[256,2048]{1,0:T(8,128)(2,1)}, u32[]{:S(2)}, u32[]{:S(2)}) collective-permute-start(bf16[256,2048]{1,0:T(8,128)(2,1)} %convolution_convert_fusion.8), channel_id=1, source_target_pairs={{0,4},{4,0},{8,12},{12,8},{16,20},{20,16},{24,28},{28,24},{1,5},{5... | collective-permute-start | bytes 3145736 | tf_op jit(solution)/shard_map/ppermute | solution.py:42
  901.7 18.9 %collective-permute-start.57 = (bf16[73,64]{1,0:T(8,128)(2,1)S(1)}, bf16[73,64]{1,0:T(8,128)(2,1)S(1)}, u32[]{:S(2)}, u32[]{:S(2)}) collective-permute-start(bf16[73,64]{1,0:T(8,128)(2,1)S(1)} %get-tuple-element.137), channel_id=1, source_target_pairs={{0,8},{4,12},{8,0},{12,4},{16,24},{20,28},{24,16},{28,20},{1,9},{5... | collective-permute-start | bytes 28040 | tf_op jit(solution)/shard_map/ppermute | solution.py:42
  920.6 70.0 %collective-permute-start.42 = (bf16[3,256,2048]{2,1,0:T(8,128)(2,1)}, bf16[3,256,2048]{2,1,0:T(8,128)(2,1)}, u32[]{:S(2)}, u32[]{:S(2)}) collective-permute-start(bf16[3,256,2048]{2,1,0:T(8,128)(2,1)} %bitcast.43), channel_id=1, source_target_pairs={{0,4},{4,0},{8,12},{12,8},{16,20},{20,16},{24,28},{28,24},{1,5},{5... | collective-permute-start | bytes 9437192 | tf_op jit(solution)/shard_map/ppermute | solution.py:42
  928.5 24.6 %collective-permute-start.41 = (bf16[256,2048]{1,0:T(8,128)(2,1)}, bf16[256,2048]{1,0:T(8,128)(2,1)S(1)}, u32[]{:S(2)}, u32[]{:S(2)}) collective-permute-start(bf16[256,2048]{1,0:T(8,128)(2,1)} %slice.437), channel_id=1, source_target_pairs={{0,2},{1,3},{2,0},{3,1},{4,6},{5,7},{6,4},{7,5},{8,10},{9,11},{10,... | collective-permute-start | bytes 3145736 | tf_op jit(solution)/shard_map/ppermute | solution.py:42
  936.3 18.0 %collective-permute-start.47 = (bf16[64,2048]{1,0:T(8,128)(2,1)}, bf16[64,2048]{1,0:T(8,128)(2,1)S(1)}, u32[]{:S(2)}, u32[]{:S(2)}) collective-permute-start(bf16[64,2048]{1,0:T(8,128)(2,1)} %get-tuple-element.110), channel_id=1, source_target_pairs={{0,8},{4,12},{8,0},{12,4},{16,24},{20,28},{24,16},{28,20},{1,9},{5... | collective-permute-start | bytes 786440 | tf_op jit(solution)/shard_map/ppermute | solution.py:42
  937.3 21.3 %collective-permute-start.48 = (bf16[64,2048]{1,0:T(8,128)(2,1)S(1)}, bf16[64,2048]{1,0:T(8,128)(2,1)S(1)}, u32[]{:S(2)}, u32[]{:S(2)}) collective-permute-start(bf16[64,2048]{1,0:T(8,128)(2,1)S(1)} %get-tuple-element.112), channel_id=1, source_target_pairs={{0,16},{4,20},{8,24},{12,28},{16,0},{20,4},{24,8},{28,12},{1,17},{... | collective-permute-start | bytes 786440 | tf_op jit(solution)/shard_map/ppermute | solution.py:42
  938.5 20.1 %collective-permute-start.49 = (bf16[64,2048]{1,0:T(8,128)(2,1)S(1)}, bf16[64,2048]{1,0:T(8,128)(2,1)S(1)}, u32[]{:S(2)}, u32[]{:S(2)}) collective-permute-start(bf16[64,2048]{1,0:T(8,128)(2,1)S(1)} %get-tuple-element.111), channel_id=1, source_target_pairs={{0,24},{4,28},{8,16},{12,20},{16,8},{20,12},{24,0},{28,4},{1,25},{... | collective-permute-start | bytes 786440 | tf_op jit(solution)/shard_map/ppermute | solution.py:42
  960.6 34.6 %collective-permute-start.51 = (f32[8,2,64]{2,0,1:T(8,128)S(1)}, f32[8,2,64]{2,0,1:T(8,128)S(1)}, u32[]{:S(2)}, u32[]{:S(2)}) collective-permute-start(f32[8,2,64]{2,0,1:T(8,128)S(1)} %slice_bitcast_fusion.3), channel_id=1, source_target_pairs={{0,2},{1,3},{2,0},{3,1},{4,6},{5,7},{6,4},{7,5},{8,10},{9,11},{10,... | collective-permute-start | bytes 12296 | tf_op jit(solution)/shard_map/ppermute | solution.py:42
  997.2 70.4 %collective-permute-start.43 = (bf16[3,64,2048]{2,1,0:T(8,128)(2,1)S(1)}, bf16[3,64,2048]{2,1,0:T(8,128)(2,1)S(1)}, u32[]{:S(2)}, u32[]{:S(2)}) collective-permute-start(bf16[3,64,2048]{2,1,0:T(8,128)(2,1)S(1)} %get-tuple-element.93), channel_id=1, source_target_pairs={{0,8},{4,12},{8,0},{12,4},{16,24},{20,28},{24,16},{28,20},{1,9},{5... | collective-permute-start | bytes 2359304 | tf_op jit(solution)/shard_map/ppermute | solution.py:42
  998.1 69.5 %collective-permute-start.44 = (bf16[3,64,2048]{2,1,0:T(8,128)(2,1)S(1)}, bf16[3,64,2048]{2,1,0:T(8,128)(2,1)S(1)}, u32[]{:S(2)}, u32[]{:S(2)}) collective-permute-start(bf16[3,64,2048]{2,1,0:T(8,128)(2,1)S(1)} %get-tuple-element.95), channel_id=1, source_target_pairs={{0,16},{4,20},{8,24},{12,28},{16,0},{20,4},{24,8},{28,12},{1,17},{... | collective-permute-start | bytes 2359304 | tf_op jit(solution)/shard_map/ppermute | solution.py:42
  999.5 68.1 %collective-permute-start.45 = (bf16[3,64,2048]{2,1,0:T(8,128)(2,1)S(1)}, bf16[3,64,2048]{2,1,0:T(8,128)(2,1)S(1)}, u32[]{:S(2)}, u32[]{:S(2)}) collective-permute-start(bf16[3,64,2048]{2,1,0:T(8,128)(2,1)S(1)} %get-tuple-element.94), channel_id=1, source_target_pairs={{0,24},{4,28},{8,16},{12,20},{16,8},{20,12},{24,0},{28,4},{1,25},{... | collective-permute-start | bytes 2359304 | tf_op jit(solution)/shard_map/ppermute | solution.py:42
  1001.7 45.4 %collective-permute-start.53 = (f32[2,64]{1,0:T(2,128)S(1)}, f32[2,64]{1,0:T(2,128)S(1)}, u32[]{:S(2)}, u32[]{:S(2)}) collective-permute-start(f32[2,64]{1,0:T(2,128)S(1)} %bitcast.207), channel_id=1, source_target_pairs={{0,8},{4,12},{8,0},{12,4},{16,24},{20,28},{24,16},{28,20},{1,9},{5... | collective-permute-start | bytes 1544 | tf_op jit(solution)/shard_map/ppermute | solution.py:42
  1001.8 65.3 %collective-permute-start.54 = (f32[2,64]{1,0:T(2,128)S(1)}, f32[2,64]{1,0:T(2,128)S(1)}, u32[]{:S(2)}, u32[]{:S(2)}) collective-permute-start(f32[2,64]{1,0:T(2,128)S(1)} %bitcast.206), channel_id=1, source_target_pairs={{0,16},{4,20},{8,24},{12,28},{16,0},{20,4},{24,8},{28,12},{1,17},{... | collective-permute-start | bytes 1544 | tf_op jit(solution)/shard_map/ppermute | solution.py:42
  1047.1 20.0 %collective-permute-start.55 = (f32[2,64]{1,0:T(2,128)S(1)}, f32[2,64]{1,0:T(2,128)S(1)}, u32[]{:S(2)}, u32[]{:S(2)}) collective-permute-start(f32[2,64]{1,0:T(2,128)S(1)} %bitcast.205), channel_id=1, source_target_pairs={{0,24},{4,28},{8,16},{12,20},{16,8},{20,12},{24,0},{28,4},{1,25},{... | collective-permute-start | bytes 1544 | tf_op jit(solution)/shard_map/ppermute | solution.py:42
  (130 other events, 2884.3 us)

commit v2 on v1

--- a/solution.py
+++ b/solution.py
@@ -42,40 +42,117 @@
     return lax.ppermute(values, axis, [(i, i ^ shift) for i in range(size)])
 
 
-def gather_wide(piece, axis=0):
-    size = lax.axis_size("wide")
-    parts = [piece] + [swap(piece, "wide", k) for k in range(2, size, 2)]
-    near = jnp.concatenate(parts, axis=axis)
-    return near, swap(near, "wide", 1)
-
-
-def scatter_wide(near, far, axis=0):
-    size = lax.axis_size("wide")
-    got = swap(far, "wide", 1)
-    total = near.astype(f32) + got.astype(f32)
-    chunks = jnp.split(total, size // 2, axis=axis)
-    out = chunks[0]
-    for k in range(1, size // 2):
-        out = out + swap(chunks[k].astype(bf16), "wide", 2 * k).astype(f32)
-    return out
+def ring_of(size):
+    return list(range(0, size, 2)) + list(range(size - 1, 0, -2))
+
+
+def along(values, step):
+    outer = lax.axis_size("wide") // 2
+    ring = ring_of(outer)
+    pairs = [
+        (ring[p] * 2 + side, ring[(p + step) % outer] * 2 + side)
+        for p in range(outer)
+        for side in range(2)
+    ]
+    return lax.ppermute(values, "wide", pairs)
+
+
+def ring_offsets(outer):
+    near = [sign * h for h in range(1, outer // 2) for sign in (-1, 1)]
+    return [0] + near + [outer // 2]
+
+
+def cut_of(rows):
+    cut = (rows // 2 + 15) // 16 * 16
+    return cut if cut < rows else rows // 2
+
+
+def two_parts(values, axis):
+    cut = cut_of(values.shape[axis])
+    return (
+        lax.slice_in_dim(values, 0, cut, axis=axis),
+        lax.slice_in_dim(values, cut, values.shape[axis], axis=axis),
+    )
+
+
+def gather_ring(own, axis=0, halves=True):
+    outer = lax.axis_size("wide") // 2
+    before, after = [own], [own]
+    for _ in range(1, outer // 2):
+        before.append(along(before[-1], 1))
+        after.append(along(after[-1], -1))
+    if halves:
+        top, _ = two_parts(before[-1], axis)
+        _, bottom = two_parts(after[-1], axis)
+        opposite = [along(top, 1), along(bottom, -1)]
+    else:
+        opposite = [along(before[-1], 1)]
+    near = [piece for h in range(1, outer // 2) for piece in (before[h], after[h])]
+    return [own] + near + opposite, near
+
+
+def scatter_ring(full, axis=0, halves=True):
+    outer = lax.axis_size("wide") // 2
+    wire = full.dtype
+    chunks = jnp.split(full, outer, axis=axis)
+    total = chunks[0].astype(f32)
+    most = outer // 2 - 1
+    behind = {h: chunks[2 * h - 1].astype(f32) for h in range(1, most + 1)}
+    ahead = {h: chunks[2 * h].astype(f32) for h in range(1, most + 1)}
+    if halves:
+        top, bottom = two_parts(chunks[-1], axis)
+        far_top, far_bottom = two_parts(ahead[most], axis)
+        got = along(top, 1).astype(f32)
+        ahead[most] = jnp.concatenate([far_top + got, far_bottom], axis=axis)
+        far_top, far_bottom = two_parts(behind[most], axis)
+        got = along(bottom, -1).astype(f32)
+        behind[most] = jnp.concatenate([far_top, far_bottom + got], axis=axis)
+    else:
+        ahead[most] = ahead[most] + along(chunks[-1], 1).astype(f32)
+    for h in range(most, 0, -1):
+        got = along(ahead[h].astype(wire), 1).astype(f32)
+        back = along(behind[h].astype(wire), -1).astype(f32)
+        if h > 1:
+            ahead[h - 1] = ahead[h - 1] + got
+            behind[h - 1] = behind[h - 1] + back
+        else:
+            total = total + got + back
+    return total
 
 
 def gather_rows(own):
     size = lax.axis_size("narrow")
-    even = jnp.concatenate([own] + [swap(own, "narrow", k) for k in range(2, size, 2)], axis=0)
-    return jnp.concatenate([even, swap(even, "narrow", 1)], axis=0)
-
-
-def scatter_rows(even, odd):
+    half = own.shape[0] // 2
+    across = [swap(own, "narrow", k) for k in range(2, size, 2)]
+    beside = swap(own, "wide", 1)
+    even = jnp.concatenate([own] + across, axis=0)
+    odd = swap(even, "narrow", 1)
+    parts = [beside]
+    for n, k in enumerate(range(2, size, 2)):
+        parts.append(swap(across[n][:half], "wide", 1))
+        parts.append(swap(beside[half:], "narrow", k))
+    other_even = jnp.concatenate(parts, axis=0)
+    other_odd = swap(other_even, "narrow", 1)
+    return even, odd, other_even, other_odd
+
+
+def scatter_rows(even, odd, other_even, other_odd):
     size = lax.axis_size("narrow")
-    got = swap(odd, "narrow", 1)
-    total = even.astype(f32) + got.astype(f32)
-    rows = total.shape[0] // (size // 2)
-    out = total[:rows]
-    for k in range(1, size // 2):
-        chunk = total[k * rows : (k + 1) * rows].astype(bf16)
-        out = out + swap(chunk, "narrow", 2 * k).astype(f32)
-    return out
+    rows = even.shape[0] // (size // 2)
+    half = rows // 2
+    other = other_even.astype(f32) + swap(other_odd, "narrow", 1).astype(f32)
+    mine = even.astype(f32) + swap(odd, "narrow", 1).astype(f32)
+    beside_top, beside_bottom = other[:half], other[half:rows]
+    out = mine[:rows]
+    for n, k in enumerate(range(2, size, 2)):
+        at = (n + 1) * rows
+        top = swap(other[at : at + half].astype(bf16), "wide", 1).astype(f32)
+        bottom = swap(other[at + half : at + rows].astype(bf16), "narrow", k).astype(f32)
+        beside_bottom = beside_bottom + bottom
+        across = jnp.concatenate([mine[at : at + half] + top, mine[at + half : at + rows]], axis=0)
+        out = out + swap(across.astype(bf16), "narrow", k).astype(f32)
+    beside = jnp.concatenate([beside_top, beside_bottom], axis=0)
+    return out + swap(beside.astype(bf16), "wide", 1).astype(f32)
 
 
 def inverse_rms(values):
@@ -427,13 +504,27 @@
 ):
     wide, narrow = lax.axis_size("wide"), lax.axis_size("narrow")
     wide_at, narrow_at = lax.axis_index("wide"), lax.axis_index("narrow")
+    outer = wide // 2
     _, local_rows, width = tokens.shape
     slots = local_rows * narrow
+    even = slots // 2
     source = tokens[0].astype(f32)
     upstream_low = cotangent[0]
     poles = decay_rate.shape[1]
     own = w_in.shape[2]
-    half = own * wide // 2
+    channels = own * outer
+    hidden_units = w_gate.shape[1] * outer
+
+    ring = np.array(ring_of(outer))
+    ring_place = np.argsort(ring)
+    tour = picked((wide_at // 2)[None], outer, jnp.asarray(ring_place, jnp.int32))[0]
+    piece_places = (tour + jnp.asarray(ring_offsets(outer), jnp.int32)) % outer
+    piece_outer = picked(piece_places, outer, jnp.asarray(ring, jnp.int32))
+    sides = jnp.arange(2) ^ (wide_at % 2)
+    offsets = list(range(0, narrow, 2)) + list(range(1, narrow, 2))
+    place_of = np.argsort(np.array(offsets))
+    order = picked(jnp.arange(narrow) ^ narrow_at, narrow, jnp.asarray(place_of, jnp.int32))
+    narrow_of = jnp.asarray(offsets, jnp.int32) ^ narrow_at
 
     small = jnp.concatenate(
         [
@@ -446,179 +537,178 @@
         ],
         axis=0,
     )
-    small_halves = gather_wide(small, axis=1)
-    count_small = small.shape[0]
-    gains = jnp.stack([s[count_small - 2 :].reshape(2, wide // 2, own) for s in small_halves], axis=2)
-    gains = gains.reshape(2, wide, own).transpose(1, 0, 2)
-    gains = picked(jnp.arange(wide) ^ wide_at, wide, gains.astype(f32)).astype(bf16)
-    gain_parts = gather_rows(gains[None])
-    offsets = list(range(0, narrow, 2)) + list(range(1, narrow, 2))
-    place_of = np.argsort(np.array(offsets))
-    order = jnp.asarray(place_of, jnp.int32)
-    order = picked(jnp.arange(narrow) ^ narrow_at, narrow, order)
-    gain_all = picked(order, narrow, gain_parts.astype(f32))
-    gain_all = gain_all.transpose(2, 1, 0, 3).reshape(2, width)
+    small_all = jnp.concatenate(gather_ring(small, axis=1, halves=False)[0], axis=1)
+    gains = small_all[small.shape[0] - 2 :].reshape(2, outer, own)
+    gains = jnp.stack([gains, swap(gains, "wide", 1)])
+    gains = jnp.stack([gains] + [swap(gains, "narrow", k) for k in range(2, narrow, 2)])
+    gains = jnp.concatenate([gains, swap(gains, "narrow", 1)], axis=0).astype(f32)
+    gains = picked(order, narrow, gains).transpose(1, 3, 0, 2, 4)
+    gains = picked(sides, 2, gains).transpose(1, 0, 2, 3, 4)
+    hot = piece_outer[None, :] == jnp.arange(outer)[:, None]
+    gains = jnp.sum(jnp.where(hot[:, :, None, None, None, None], gains[None], 0), axis=1)
+    gain_all = gains.transpose(3, 0, 1, 2, 4).reshape(2, width)
     gain_first, gain_last = gain_all[0], gain_all[1]
 
-    table, first = layout(doc_blocks[0], doc_pad[0], slots)
-    count = doc_blocks[0]
-
-    in_piece = w_in.transpose(0, 2, 1)
-    out_piece = w_out
-    gate_piece, up_piece, down_piece = w_gate.T, w_up.T, w_down.T
-    in_halves = gather_wide(in_piece, axis=1)
-    out_halves = gather_wide(out_piece)
-    gate_halves = gather_wide(gate_piece)
-    up_halves = gather_wide(up_piece)
-    down_halves = gather_wide(down_piece)
+    def reduce_gain(values):
+        values = values.reshape(outer, 2, narrow, own)
+        values = picked(piece_outer, outer, values).transpose(1, 0, 2, 3)
+        values = picked(sides, 2, values).transpose(2, 0, 1, 3)
+        values = picked(narrow_of, narrow, values)
+        total = values[: narrow // 2] + swap(values[narrow // 2 :], "narrow", 1)
+        summed = total[0]
+        for k in range(1, narrow // 2):
+            summed = summed + swap(total[k], "narrow", 2 * k)
+        summed = summed[0] + swap(summed[1], "wide", 1)
+        return scatter_ring(summed, halves=False)[0]
+
+    documents = jnp.concatenate([doc_blocks, doc_pad], axis=0)
+    documents = (documents, swap(documents, "wide", 1))
+    tables = [layout(rules[0], rules[1], slots) for rules in documents]
+
+    in_pieces, sent = gather_ring(w_in.transpose(0, 2, 1), axis=1)
+    out_own, gate_own, up_own, down_own = w_out, w_gate.T, w_up.T, w_down.T
+    out_own, gate_own, *_ = lax.optimization_barrier((out_own, gate_own, *sent))
+    out_pieces, _ = gather_ring(out_own)
+    gate_pieces, sent = gather_ring(gate_own)
+    up_own, *_ = lax.optimization_barrier((up_own, *sent))
+    up_pieces, sent = gather_ring(up_own)
+    down_own, *_ = lax.optimization_barrier((down_own, *sent))
+    down_pieces, _ = gather_ring(down_own)
 
     rate_first = inverse_rms(source)
     low_first = (source * rate_first * gain_first).astype(bf16)
-    rows_first = gather_rows(low_first)
-    rows_upstream = gather_rows(upstream_low)
+    first_parts = gather_rows(low_first)
+    rows_first = [jnp.concatenate(first_parts[:2], axis=0), jnp.concatenate(first_parts[2:], axis=0)]
 
     matrix = transform()
     fwd = jnp.asarray(matrix, bf16)
     inv = jnp.asarray(matrix.T / SPAN, bf16)
 
-    tables, kept = [], []
-    for s in range(2):
-        block = small_halves[s].astype(f32)
-        taps = block[:9].reshape(3, 3 * half)
-        taps = jnp.concatenate([taps, jnp.zeros((5, 3 * half), f32)], axis=0)
-        decay = block[9 : 9 + poles][:, None, :]
-        angle = block[9 + poles : 9 + 2 * poles][:, None, :]
-        res_re = block[9 + 2 * poles : 9 + 3 * poles][:, None, :]
-        res_im = -block[9 + 3 * poles : 9 + 4 * poles][:, None, :]
-        lag = jnp.arange(8, dtype=f32)[None, :, None]
-        fade = jnp.exp(-decay * lag)
-        power_re, power_im = fade * jnp.cos(angle * lag), fade * jnp.sin(angle * lag)
-        fade_step = jnp.exp(-decay * 8.0)
-        step_re = jnp.broadcast_to(fade_step * jnp.cos(angle * 8.0), power_re.shape)
-        step_im = jnp.broadcast_to(fade_step * jnp.sin(angle * 8.0), power_re.shape)
-        filt = filter_taps(
-            res_re * power_re - res_im * power_im,
-            res_re * power_im + res_im * power_re,
-            step_re,
-            step_im,
+    block = small_all.astype(f32)
+    taps = block[:9].reshape(3, 3 * channels)
+    taps = jnp.concatenate([taps, jnp.zeros((5, 3 * channels), f32)], axis=0)
+    decay = block[9 : 9 + poles][:, None, :]
+    angle = block[9 + poles : 9 + 2 * poles][:, None, :]
+    res_re = block[9 + 2 * poles : 9 + 3 * poles][:, None, :]
+    res_im = -block[9 + 3 * poles : 9 + 4 * poles][:, None, :]
+    lag = jnp.arange(8, dtype=f32)[None, :, None]
+    fade = jnp.exp(-decay * lag)
+    power_re, power_im = fade * jnp.cos(angle * lag), fade * jnp.sin(angle * lag)
+    fade_step = jnp.exp(-decay * 8.0)
+    step_re = jnp.broadcast_to(fade_step * jnp.cos(angle * 8.0), power_re.shape)
+    step_im = jnp.broadcast_to(fade_step * jnp.sin(angle * 8.0), power_re.shape)
+    filt = filter_taps(
+        res_re * power_re - res_im * power_im,
+        res_re * power_im + res_im * power_re,
+        step_re,
+        step_im,
+    )
+    spectrum = lax.dot_general(
+        jnp.asarray(matrix),
+        filt,
+        (((1,), (0,)), ((), ())),
+        precision=lax.Precision.HIGHEST,
+        preferred_element_type=f32,
+    )
+    res_re, res_im = res_re[:, 0], -res_im[:, 0]
+
+    in_all = jnp.concatenate(in_pieces, axis=1).reshape(3 * channels, width)
+    mixed = []
+    for r in range(2):
+        table, first = tables[r]
+        proj = nt(rows_first[r], in_all).reshape(narrow, local_rows, 3 * channels)
+        gated, long_out, seen = mixer_forward(
+            order, first, documents[r][0], proj, taps, table, spectrum, fwd, inv
         )
-        spectrum = lax.dot_general(
-            jnp.asarray(matrix),
-            filt,
-            (((1,), (0,)), ((), ())),
-            precision=lax.Precision.HIGHEST,
-            preferred_element_type=f32,
-        )
-        tables.append((taps, spectrum))
-        kept.append((power_re, power_im, step_re, step_im, res_re[:, 0], -res_im[:, 0]))
-
-    even = slots // 2
-    mixed = []
-    for s in range(2):
-        taps, spectrum = tables[s]
-        weight = in_halves[s].reshape(3 * half, width)
-        proj = nt(rows_first, weight).reshape(narrow, local_rows, 3 * half)
-        gated, long_out, seen = mixer_forward(
-            order, first, count, proj, taps, table, spectrum, fwd, inv
-        )
-        mixed.append((proj, gated.reshape(slots, half), long_out, seen))
-    share_odd = sum(nn(mixed[s][1][even:], out_halves[s]) for s in range(2)).astype(bf16)
-    share_even = sum(nn(mixed[s][1][:even], out_halves[s]) for s in range(2)).astype(bf16)
-    middle = source + scatter_rows(share_even, share_odd)
+        mixed.append((proj, gated.reshape(slots, channels), long_out, seen))
+    out_all = jnp.concatenate(out_pieces, axis=0)
+    shares = []
+    for r in (1, 0):
+        share = nn(mixed[r][1], out_all).astype(bf16)
+        shares = [share[:even], share[even:]] + shares
+    middle = source + scatter_rows(*shares)
     rate_last = inverse_rms(middle)
-    rows_second = gather_rows((middle * rate_last * gain_last).astype(bf16))
-
-    down_even, down_odd = 0.0, 0.0
-    second_even, second_odd = 0.0, 0.0
+    rows_upstream = jnp.concatenate(gather_rows(upstream_low), axis=0)
+    rows_second = jnp.concatenate(
+        gather_rows((middle * rate_last * gain_last).astype(bf16)), axis=0
+    )
+
+    gate_up = jnp.concatenate(gate_pieces + up_pieces, axis=0)
+    down_all = jnp.concatenate(down_pieces, axis=0)
+    pre = nt(gate_up, rows_second)
+    gate_pre, up_pre = pre[:hidden_units], pre[hidden_units:]
+    sig = jax.nn.sigmoid(gate_pre)
+    silu = gate_pre * sig
+    hidden = (silu * up_pre).astype(bf16)
+    d_hidden = nt(down_all, rows_upstream)
+    d_gate = (d_hidden * up_pre * sig * (1.0 + gate_pre * (1.0 - sig))).astype(bf16)
+    d_up = (d_hidden * silu).astype(bf16)
+    d_pre = jnp.concatenate([d_gate, d_up], axis=0)
     shares = []
-    for s in range(2):
-        gate_pre = nt(rows_second, gate_halves[s])
-        up_pre = nt(rows_second, up_halves[s])
-        sig = jax.nn.sigmoid(gate_pre)
-        silu = gate_pre * sig
-        hidden = (silu * up_pre).astype(bf16)
-        d_hidden = nt(rows_upstream, down_halves[s])
-        d_gate = (d_hidden * up_pre * sig * (1.0 + gate_pre * (1.0 - sig))).astype(bf16)
-        d_up = (d_hidden * silu).astype(bf16)
-        second_odd = second_odd + nn(d_gate[even:], gate_halves[s]) + nn(d_up[even:], up_halves[s])
-        second_even = second_even + nn(d_gate[:even], gate_halves[s]) + nn(d_up[:even], up_halves[s])
-        down_odd = down_odd + nn(hidden[even:], down_halves[s])
-        down_even = down_even + nn(hidden[:even], down_halves[s])
-        shares.append(
-            (
-                tn(d_gate, rows_second).astype(bf16),
-                tn(d_up, rows_second).astype(bf16),
-                tn(hidden, rows_upstream).astype(bf16),
-            )
-        )
-    d_second = scatter_rows(second_even.astype(bf16), second_odd.astype(bf16))
-    down_out = scatter_rows(down_even.astype(bf16), down_odd.astype(bf16))
-    block_output = (middle + down_out).astype(bf16)
+    for r in (1, 0):
+        share = tn(d_pre[:, r * slots : (r + 1) * slots], gate_up).astype(bf16)
+        shares = [share[:even], share[even:]] + shares
+    d_second = scatter_rows(*shares)
     upstream = upstream_low.astype(f32)
     d_middle = upstream + norm_back(middle, rate_last, gain_last, d_second)
+    rows_dmiddle = gather_rows(d_middle.astype(bf16))
+    rows_dmiddle = [
+        jnp.concatenate(rows_dmiddle[:2], axis=0),
+        jnp.concatenate(rows_dmiddle[2:], axis=0),
+    ]
+    down_share = scatter_ring(nn(hidden, rows_upstream).astype(bf16))
+    grad_pre = nn(d_pre, rows_second).astype(bf16)
+    gate_share = scatter_ring(grad_pre[:hidden_units])
+    up_share = scatter_ring(grad_pre[hidden_units:])
+    shares = []
+    for r in (1, 0):
+        share = tn(hidden[:, r * slots : (r + 1) * slots], down_all).astype(bf16)
+        shares = [share[:even], share[even:]] + shares
+    block_output = (middle + scatter_rows(*shares)).astype(bf16)
     grad_gain_two = jnp.sum(d_second * middle * rate_last, axis=0)
-    gate_share, up_share, down_share = (
-        scatter_wide(shares[0][i], shares[1][i]) for i in range(3)
-    )
-
-    rows_dmiddle = gather_rows(d_middle.astype(bf16))
-    out_parts, in_parts, small_parts = [], [], []
-    normed_even, normed_odd = 0.0, 0.0
-    for s in range(2):
-        proj, gated, long_out, seen = mixed[s]
-        taps, spectrum = tables[s]
-        d_gated = nt(rows_dmiddle, out_halves[s]).reshape(narrow, local_rows, half)
-        out_parts.append(tn(gated, rows_dmiddle).astype(bf16))
-        dz, d_filter, d_taps = mixer_backward(
-            order, first, count, proj, d_gated, long_out, seen, taps, table, spectrum, fwd, inv
+
+    grad_out, grad_in, d_filter, d_taps = 0.0, 0.0, 0.0, 0.0
+    shares, grad_gain_one = [], 0.0
+    for r in (1, 0):
+        proj, gated, long_out, seen = mixed[r]
+        table, first = tables[r]
+        d_gated = nt(rows_dmiddle[r], out_all).reshape(narrow, local_rows, channels)
+        grad_out = grad_out + tn(gated, rows_dmiddle[r])
+        dz, d_filter_row, d_taps_row = mixer_backward(
+            order, first, documents[r][0], proj, d_gated, long_out, seen, taps, table,
+            spectrum, fwd, inv,
         )
-        dz = dz.reshape(slots, 3 * half)
-        weight = in_halves[s].reshape(3 * half, width)
-        normed_odd = normed_odd + nn(dz[even:], weight)
-        normed_even = normed_even + nn(dz[:even], weight)
-        in_parts.append(tn(dz, rows_first).astype(bf16).reshape(3, half, width))
-        power_re, power_im, step_re, step_im, res_re, res_im = kept[s]
-        sum_re, sum_im, mom_re, mom_im = filter_moments(d_filter, step_re, step_im)
-        lag = jnp.arange(8, dtype=f32)[None, :, None]
-        full_re = lag * sum_re + 8.0 * mom_re
-        full_im = lag * sum_im + 8.0 * mom_im
-        grad_re = jnp.sum(power_re * sum_re - power_im * sum_im, axis=1)
-        grad_im = jnp.sum(power_re * sum_im + power_im * sum_re, axis=1)
-        lag_re = jnp.sum(power_re * full_re - power_im * full_im, axis=1)
-        lag_im = jnp.sum(power_re * full_im + power_im * full_re, axis=1)
-        small_parts.append(
-            jnp.concatenate(
-                [
-                    d_taps[:3].reshape(9, half),
-                    -(res_re * lag_re + res_im * lag_im),
-                    res_im * lag_re - res_re * lag_im,
-                    grad_re,
-                    grad_im,
-                ],
-                axis=0,
-            ).astype(bf16)
+        dz = dz.reshape(slots, 3 * channels)
+        d_filter, d_taps = d_filter + d_filter_row, d_taps + d_taps_row
+        share = nn(dz, in_all).astype(bf16)
+        shares = [share[:even], share[even:]] + shares
+        grad_gain_one = grad_gain_one + jnp.sum(
+            share.astype(f32) * rows_first[r].astype(f32), axis=0
         )
-    d_normed = scatter_rows(normed_even.astype(bf16), normed_odd.astype(bf16))
-    out_share = scatter_wide(out_parts[0], out_parts[1])
-    in_share = scatter_wide(in_parts[0], in_parts[1], axis=1)
-    small_share = scatter_wide(small_parts[0], small_parts[1], axis=1)
+        grad_in = grad_in + tn(dz, rows_first[r])
+    d_normed = scatter_rows(*shares)
     input_grad = (d_middle + norm_back(source, rate_first, gain_first, d_normed)).astype(bf16)
-    grad_gain_one = jnp.sum(d_normed * source * rate_first, axis=0)
-
-    grads = jnp.stack([grad_gain_one, grad_gain_two]).reshape(2, wide, narrow, own)
-    grads = picked(jnp.arange(narrow) ^ narrow_at, narrow, grads.transpose(2, 1, 0, 3))
-    grads = jnp.stack([grads[k] for k in offsets])
-    even_places = narrow // 2
-    total = grads[:even_places] + swap(grads[even_places:], "narrow", 1)
-    summed = total[0]
-    for k in range(1, even_places):
-        summed = summed + swap(total[k], "narrow", 2 * k)
-    summed = picked(jnp.arange(wide) ^ wide_at, wide, summed)
-    pairs = summed.reshape(wide // 2, 2, 2, own)
-    total = pairs[:, 0] + swap(pairs[:, 1], "wide", 1)
-    gain_share = total[0]
-    for k in range(1, wide // 2):
-        gain_share = gain_share + swap(total[k], "wide", 2 * k)
+    out_share = scatter_ring(grad_out.astype(bf16))
+    in_share = scatter_ring(grad_in.astype(bf16).reshape(3, channels, width), axis=1)
+
+    sum_re, sum_im, mom_re, mom_im = filter_moments(d_filter, step_re, step_im)
+    full_re = lag * sum_re + 8.0 * mom_re
+    full_im = lag * sum_im + 8.0 * mom_im
+    grad_re = jnp.sum(power_re * sum_re - power_im * sum_im, axis=1)
+    grad_im = jnp.sum(power_re * sum_im + power_im * sum_re, axis=1)
+    lag_re = jnp.sum(power_re * full_re - power_im * full_im, axis=1)
+    lag_im = jnp.sum(power_re * full_im + power_im * full_re, axis=1)
+    small_grad = jnp.concatenate(
+        [
+            d_taps[:3].reshape(9, channels),
+            -(res_re * lag_re + res_im * lag_im),
+            res_im * lag_re - res_re * lag_im,
+            grad_re,
+            grad_im,
+        ],
+        axis=0,
+    ).astype(bf16)
+    small_share = scatter_ring(small_grad, axis=1, halves=False)
 
     at = 9 + poles
     return (
@@ -626,12 +716,12 @@
         input_grad[None],
         in_share.transpose(0, 2, 1),
         out_share,
-        gain_share[0],
+        reduce_gain(grad_gain_one / gain_first),
         small_share[:9].reshape(3, 3, own),
         small_share[9:at].T,
         small_share[at : at + poles].T,
         small_share[at + poles :].T,
-        gain_share[1],
+        reduce_gain(grad_gain_two),
         gate_share.T,
         up_share.T,
         down_share.T,

time: 1080 us -> 853 us (0.79)
  waiting for transfers between devices: 457 us -> 342 us
  starting transfers between devices: 235 us -> 127 us
  local copies, waits for them, and re-layouts: 36 us -> 78.9 us
  matrix products: 182 us -> 151 us
  Pallas kernels: 69.6 us -> 57 us
    ppermute x72 -> x58, waiting for transfers between devices: 457 us -> 186 us  [swap(): return lax.ppermute(values, axis, [(i, i ^ shift) for i in range(size)])]
    ppermute x72 -> x58, starting transfers between devices: 235 us -> 50.9 us  [swap(): return lax.ppermute(values, axis, [(i, i ^ shift) for i in range(size)])]
    ppermute x0 -> x52, waiting for transfers between devices: none -> 156 us  [along(): return lax.ppermute(values, 'wide', pairs)]
    ppermute x0 -> x52, starting transfers between devices: none -> 75.6 us  [along(): return lax.ppermute(values, 'wide', pairs)]
    unnamed x247 -> x212, local copies, waits for them, and re-layouts: 14.4 us -> 41.1 us
    slice x17 -> x44, local copies, waits for them, and re-layouts: 3.96 us -> 24.7 us  [the longest x8 8.67 us: body(): shares = [share[:even], share[even:]] + shares]
    dot_general x20 -> x6, matrix products: 64.2 us -> 44.7 us  [nn(): lax.dot_general(a, b, (((1,), (0,)), ((), ())), preferred_element_type=f32)]
    another operation x10 -> x23, other arithmetic: 25.1 us -> 11.7 us
  transfers between devices with their start and end apart: 72 -> 110, of which waited for: 25 -> 47; matrix products, arithmetic and copies ran while one was open for 25% -> 24% of each run, Pallas kernels for 2% -> 7%
where the time goes in v2:
time: 853 us; the launch traced here: 840 us
  waiting for transfers between devices  342 us (40%)
  matrix products  151 us (18%)
  starting transfers between devices  127 us (15%)
  other arithmetic  81.1 us (10%)
  local copies, waits for them, and re-layouts  78.9 us (9%)
  Pallas kernels  57 us (7%)
    ppermute x58, waiting for transfers between devices, swap(): return lax.ppermute(values, axis, [(i, i ^ shift) for i in range(size)])  186 us
    ppermute x52, waiting for transfers between devices, along(): return lax.ppermute(values, 'wide', pairs)  156 us
    ppermute x52, starting transfers between devices, along(): return lax.ppermute(values, 'wide', pairs)  75.6 us
    dot_general x8, matrix products, tn(): lax.dot_general(a, b, (((0,), (0,)), ((), ())), preferred_element_type=f32)  56.1 us
    ppermute x58, starting transfers between devices, swap(): return lax.ppermute(values, axis, [(i, i ^ shift) for i in range(size)])  50.9 us
    dot_general x6, matrix products, nt(): lax.dot_general(a, b, (((1,), (1,)), ((), ())), preferred_element_type=f32)  47.1 us
    dot_general x6, matrix products, nn(): lax.dot_general(a, b, (((1,), (0,)), ((), ())), preferred_element_type=f32)  44.7 us
    unnamed x212, local copies, waits for them, and re-layouts  41.1 us
  transfers between devices with their start and end apart: 110, of which 47 were waited for; matrix products, arithmetic and copies ran while one was open for 24% of the time, Pallas kernels for 7%

profile of v2, /device:TPU:0, one launch (start us, length us, event | category | flops | bytes accessed | tf_op | source)
XLA Modules:
  0.0 839.7 jit_solution(7113369836387290601)
XLA Ops:
  1.3 3.1 concatenate.193
  31.7 14.5 %collective-permute-done.2 = bf16[75,64]{1,0:T(8,128)(2,1)S(1)} collective-permute-done((bf16[75,64]{1,0:T(8,128)(2,1)S(1)}, bf16[75,64]{1,0:T(8,128)(2,1)S(1)}, u32[]{:S(2)}, u32[]{:S(2)}) %collective-permute-start.2) | collective-permute-done | bytes 9632 | tf_op jit(solution)/shard_map/ppermute | solution.py:57
  56.4 4.1 taps.1
  76.5 11.5 %collective-permute-done.18 = bf16[256,2048]{1,0:T(8,128)(2,1)} collective-permute-done((bf16[256,2048]{1,0:T(8,128)(2,1)S(1)}, bf16[256,2048]{1,0:T(8,128)(2,1)}, u32[]{:S(2)}, u32[]{:S(2)}) %collective-permute-start.18) | collective-permute-done | bytes 1048608 | tf_op jit(solution)/shard_map/ppermute | solution.py:42
  94.9 3.1 pad_maximum_fusion.8
  102.9 7.4 collective-permute-done.53
  114.1 7.0 collective-permute-done.19
  124.0 4.1 collective-permute-done.14
  129.0 5.4 collective-permute-done.15
  134.4 3.2 collective-permute-start.27
  137.7 23.2 %collective-permute-done.11 = bf16[3,32,2048]{2,1,0:T(8,128)(2,1)S(1)} collective-permute-done((bf16[3,32,2048]{2,1,0:T(8,128)(2,1)S(1)}, bf16[3,32,2048]{2,1,0:T(8,128)(2,1)S(1)}, u32[]{:S(2)}, u32[]{:S(2)}) %collective-permute-start.11) | collective-permute-done | bytes 393248 | tf_op jit(solution)/shard_map/ppermute | solution.py:57
  165.1 3.4 fusion.76.proj
  168.6 6.9 mixer_forward.3
  179.5 3.4 fusion.74.proj
  183.0 6.9 mixer_forward.2
  211.1 11.5 %collective-permute-done.25 = bf16[128,2048]{1,0:T(8,128)(2,1)S(1)} collective-permute-done((bf16[128,2048]{1,0:T(8,128)(2,1)S(1)}, bf16[128,2048]{1,0:T(8,128)(2,1)S(1)}, u32[]{:S(2)}, u32[]{:S(2)}) %collective-permute-start.25) | collective-permute-done | bytes 524320 | tf_op jit(solution)/shard_map/ppermute | solution.py:42
  224.0 11.0 %collective-permute-done.23 = bf16[128,2048]{1,0:T(8,128)(2,1)S(1)} collective-permute-done((bf16[128,2048]{1,0:T(8,128)(2,1)S(1)}, bf16[128,2048]{1,0:T(8,128)(2,1)S(1)}, u32[]{:S(2)}, u32[]{:S(2)}) %collective-permute-start.23) | collective-permute-done | bytes 524320 | tf_op jit(solution)/shard_map/ppermute | solution.py:42
  236.2 6.6 collective-permute-done.29
  250.5 7.1 collective-permute-done.26
  257.7 10.3 %collective-permute-done.24 = bf16[256,2048]{1,0:T(8,128)(2,1)S(1)} collective-permute-done((bf16[256,2048]{1,0:T(8,128)(2,1)S(1)}, bf16[256,2048]{1,0:T(8,128)(2,1)S(1)}, u32[]{:S(2)}, u32[]{:S(2)}) %collective-permute-start.24) | collective-permute-done | bytes 1048608 | tf_op jit(solution)/shard_map/ppermute | solution.py:42
  272.0 16.7 %collective-permute-done.34 = bf16[80,2048]{1,0:T(8,128)(2,1)S(1)} collective-permute-done((bf16[80,2048]{1,0:T(8,128)(2,1)S(1)}, bf16[80,2048]{1,0:T(8,128)(2,1)S(1)}, u32[]{:S(2)}, u32[]{:S(2)}) %collective-permute-start.34) | collective-permute-done | bytes 327712 | tf_op jit(solution)/shard_map/ppermute | solution.py:57
  289.7 6.4 collective-permute-done.33
  301.8 11.4 %collective-permute-done.37 = bf16[256,2048]{1,0:T(8,128)(2,1)S(1)} collective-permute-done((bf16[256,2048]{1,0:T(8,128)(2,1)S(1)}, bf16[256,2048]{1,0:T(8,128)(2,1)S(1)}, u32[]{:S(2)}, u32[]{:S(2)}) %collective-permute-start.37) | collective-permute-done | bytes 1048608 | tf_op jit(solution)/shard_map/ppermute | solution.py:42
  314.3 7.9 collective-permute-done.35
  325.0 6.8 collective-permute-done.39
  334.7 7.2 collective-permute-done.43
  350.9 19.1 %fusion.77 = f32[1408,2048]{1,0:T(8,128)} fusion(bf16[1408,2048]{1,0:T(8,128)(2,1)} %constant_dynamic-update-slice_fusion.14, bf16[2048,2048]{1,0:T(8,128)(2,1)} %constant_dynamic-update-slice_fusion.24), kind=kOutput, calls=%fused_computation.331 | convolution fusion | flops 11811160064 | bytes 25690112 | tf_op jit(solution)/shard_map/dot_general | solution.py:33
  370.0 15.1 %multiply_convert_fusion = (bf16[704,2048]{1,0:T(8,128)(2,1)}, bf16[704,2048]{1,0:T(8,128)(2,1)}, bf16[704,2048]{1,0:T(8,128)(2,1)S(1)}) fusion(f32[1408,2048]{1,0:T(8,128)} %fusion.77, bf16[704,2048]{1,0:T(8,128)(2,1)S(1)} %copy-done.66, bf16[2048,2048]{1,0:T(8,128)(2,1)} %copy-done.72), kind=kOutput, calls=%fused_computation.9 | convolution fusion | flops 5927206912 | bytes 31457280 | tf_op jit(solution)/shard_map/dot_general | solution.py:33
  385.1 9.5 %convolution_convert_fusion.9 = bf16[704,2048]{1,0:T(8,128)(2,1)S(1)} fusion(bf16[704,2048]{1,0:T(8,128)(2,1)S(1)} %get-tuple-element.85, bf16[2048,2048]{1,0:T(8,128)(2,1)} %copy-done.72), kind=kOutput, calls=%fused_computation.37 | convolution fusion | flops 5907021824 | bytes 14155776 | tf_op jit(solution)/shard_map/dot_general | solution.py:29
  395.7 17.0 %convolution_convert_fusion = bf16[1408,2048]{1,0:T(8,128)(2,1)S(1)} fusion(bf16[2048,2048]{1,0:T(8,128)(2,1)} %constant_dynamic-update-slice_fusion.24, bf16[704,2048]{1,0:T(8,128)(2,1)} %get-tuple-element.83, bf16[704,2048]{1,0:T(8,128)(2,1)} %get-tuple-element.84), kind=kOutput, calls=%fused_computation.2 | convolution fusion | flops 11825577984 | bytes 19922944 | tf_op jit(solution)/shard_map/dot_general | solution.py:29
  412.7 12.2 %convolution_convert_fusion.2 = bf16[1024,2048]{1,0:T(8,128)(2,1)S(1)} fusion(bf16[1408,2048]{1,0:T(8,128)(2,1)} %constant_dynamic-update-slice_fusion.14, bf16[704,2048]{1,0:T(8,128)(2,1)} %get-tuple-element.84, bf16[704,2048]{1,0:T(8,128)(2,1)} %get-tuple-element.83), kind=kOutput, calls=%fused_computation.30 | convolution fusion | flops 5913444352 | bytes 15728640 | tf_op jit(solution)/shard_map/dot_general | solution.py:37
  424.9 10.9 %convolution_convert_fusion.1 = bf16[1024,2048]{1,0:T(8,128)(2,1)S(1)} fusion(bf16[1408,2048]{1,0:T(8,128)(2,1)} %constant_dynamic-update-slice_fusion.14, bf16[704,2048]{1,0:T(8,128)(2,1)} %get-tuple-element.84, bf16[704,2048]{1,0:T(8,128)(2,1)S(1)} %copy-done.84), kind=kOutput, calls=%fused_computation.29 | convolution fusion | flops 5913444352 | bytes 15728640 | tf_op jit(solution)/shard_map/dot_general | solution.py:37
  435.8 5.5 convolution_convert_fusion.3
  441.4 5.7 convolution_convert_fusion.4
  459.9 6.6 collective-permute-done.108
  467.6 6.7 collective-permute-done.104
  474.3 7.0 collective-permute-done.100
  496.3 6.0 collective-permute-done.59
  507.1 7.9 collective-permute-done.47
  523.2 17.9 %collective-permute-done.62 = bf16[256,2048]{1,0:T(8,128)(2,1)S(1)} collective-permute-done((bf16[256,2048]{1,0:T(8,128)(2,1)S(1)}, bf16[256,2048]{1,0:T(8,128)(2,1)S(1)}, u32[]{:S(2)}, u32[]{:S(2)}) %collective-permute-start.62) | collective-permute-done | bytes 1048608 | tf_op jit(solution)/shard_map/ppermute | solution.py:42
  547.2 13.5 %collective-permute-done.50 = bf16[256,2048]{1,0:T(8,128)(2,1)S(1)} collective-permute-done((bf16[256,2048]{1,0:T(8,128)(2,1)S(1)}, bf16[256,2048]{1,0:T(8,128)(2,1)S(1)}, u32[]{:S(2)}, u32[]{:S(2)}) %collective-permute-start.50) | collective-permute-done | bytes 1048608 | tf_op jit(solution)/shard_map/ppermute | solution.py:42
  564.6 5.1 fusion.59
  576.9 14.9 %collective-permute-done.63 = bf16[256,2048]{1,0:T(8,128)(2,1)S(1)} collective-permute-done((bf16[256,2048]{1,0:T(8,128)(2,1)S(1)}, bf16[256,2048]{1,0:T(8,128)(2,1)S(1)}, u32[]{:S(2)}, u32[]{:S(2)}) %collective-permute-start.63) | collective-permute-done | bytes 1048608 | tf_op jit(solution)/shard_map/ppermute | solution.py:42
  595.0 23.5 %collective-permute-done.103 = bf16[176,2048]{1,0:T(8,128)(2,1)S(1)} collective-permute-done((bf16[176,2048]{1,0:T(8,128)(2,1)S(1)}, bf16[176,2048]{1,0:T(8,128)(2,1)S(1)}, u32[]{:S(2)}, u32[]{:S(2)}) %collective-permute-start.103) | collective-permute-done | bytes 720928 | tf_op jit(solution)/shard_map/ppermute | solution.py:57
  618.5 3.8 add_bitcast_fusion.2
  626.8 5.7 collective-permute-done.107
  636.5 3.3 pad_maximum_fusion.11
  642.1 4.7 fusion.22
  646.8 15.6 %mixer_backward.2 = (bf16[4,256,768]{2,1,0:T(8,128)(2,1)}, f32[512,256]{1,0:T(8,128)S(1)}, f32[8,768]{1,0:T(8,128)S(1)}) custom-call(s32[4]{0:T(128)S(1)} %select_reduce_fusion.10.order, s32[3]{0:T(128)S(1)} %copy-done.18, s32[3]{0:T(128)S(1)} %bitcast.179, f32[4,256,768]{2,1,0:T(8,128)} %copy-done.4, f32[4,256,256]{2,1,0:T(8,128)S(1)} %bitcast.176, ...), custom_call_target="tpu_custom_call" | custom-call | flops 2013265920 | bytes 8388608 | tf_op jit(solution)/shard_map/mixer_backward/pallas_call | solution.py:450
  662.4 6.7 multiply_reduce_fusion
  671.3 3.8 fusion.21
  675.1 7.6 fusion.58
  688.1 15.5 %mixer_backward.3 = (bf16[4,256,768]{2,1,0:T(8,128)(2,1)}, f32[512,256]{1,0:T(8,128)S(1)}, f32[8,768]{1,0:T(8,128)S(1)}) custom-call(s32[4]{0:T(128)S(1)} %select_reduce_fusion.10.order, s32[3]{0:T(128)S(1)} %copy-done.16, s32[3]{0:T(128)S(1)} %copy-done.20, f32[4,256,768]{2,1,0:T(8,128)} %copy-done.3, f32[4,256,256]{2,1,0:T(8,128)S(1)} %bitcast.175, ...), custom_call_target="tpu_custom_call" | custom-call | flops 2013265920 | bytes 8388608 | tf_op jit(solution)/shard_map/mixer_backward/pallas_call | solution.py:450
  704.5 7.9 moments.1
  718.7 9.0 %multiply_reduce_fusion.1 = (f32[2048]{0:T(1024)S(1)}, bf16[1024,2048]{1,0:T(8,128)(2,1)}) fusion(bf16[1024,2048]{1,0:T(8,128)(2,1)} %copy-done.56, bf16[1024,768]{1,0:T(8,128)(2,1)} %bitcast.218, bf16[768,2048]{1,0:T(8,128)(2,1)} %bitcast.197), kind=kOutput, calls=%fused_computation.1 | convolution fusion | flops 3231709184 | bytes 13115392 | tf_op jit(solution)/shard_map/dot_general | solution.py:29
  728.3 8.1 add_convert_fusion
  761.1 3.2 collective-permute-done.96
  777.6 6.6 collective-permute-done.77
  790.8 4.7 collective-permute-start.73
  798.0 6.2 collective-permute-done.73
  807.1 8.9 %collective-permute-done.71 = bf16[128,2048]{1,0:T(8,128)(2,1)S(1)} collective-permute-done((bf16[128,2048]{1,0:T(8,128)(2,1)S(1)}, bf16[128,2048]{1,0:T(8,128)(2,1)S(1)}, u32[]{:S(2)}, u32[]{:S(2)}) %collective-permute-start.71) | collective-permute-done | bytes 524320 | tf_op jit(solution)/shard_map/ppermute | solution.py:42
  823.0 6.2 collective-permute-done.76
  829.2 3.2 add_bitcast_fusion
  832.3 4.3 collective-permute-done.74
  (600 shorter events, 286.8 us)
Async XLA Ops:
  4.5 27.3 %collective-permute-start.1 = (bf16[75,64]{1,0:T(8,128)(2,1)S(1)}, bf16[75,64]{1,0:T(8,128)(2,1)S(1)}, u32[]{:S(2)}, u32[]{:S(2)}) collective-permute-start(bf16[75,64]{1,0:T(8,128)(2,1)S(1)} %concatenate.193), channel_id=1, source_target_pairs={{0,8},{4,12},{16,0},{20,4},{24,16},{28,20},{8,24},{12,28},{1,9},{5... | collective-permute-start | bytes 28808 | tf_op jit(solution)/shard_map/ppermute | solution.py:57
  7.5 22.9 %collective-permute-start = (bf16[75,64]{1,0:T(8,128)(2,1)S(1)}, bf16[75,64]{1,0:T(8,128)(2,1)S(1)}, u32[]{:S(2)}, u32[]{:S(2)}) collective-permute-start(bf16[75,64]{1,0:T(8,128)(2,1)S(1)} %concatenate.193), channel_id=1, source_target_pairs={{0,16},{4,20},{16,24},{20,28},{24,8},{28,12},{8,0},{12,4},{1,17},{... | collective-permute-start | bytes 28808 | tf_op jit(solution)/shard_map/ppermute | solution.py:57
  8.6 59.2 %collective-permute-start.9 = (bf16[3,64,2048]{2,1,0:T(8,128)(2,1)}, bf16[3,64,2048]{2,1,0:T(8,128)(2,1)}, u32[]{:S(2)}, u32[]{:S(2)}) collective-permute-start(bf16[3,64,2048]{2,1,0:T(8,128)(2,1)} %bitcast.184), channel_id=1, source_target_pairs={{0,8},{4,12},{16,0},{20,4},{24,16},{28,20},{8,24},{12,28},{1,9},{5... | collective-permute-start | bytes 2359304 | tf_op jit(solution)/shard_map/ppermute | solution.py:57
  10.1 58.2 %collective-permute-start.8 = (bf16[3,64,2048]{2,1,0:T(8,128)(2,1)}, bf16[3,64,2048]{2,1,0:T(8,128)(2,1)}, u32[]{:S(2)}, u32[]{:S(2)}) collective-permute-start(bf16[3,64,2048]{2,1,0:T(8,128)(2,1)} %bitcast.185), channel_id=1, source_target_pairs={{0,16},{4,20},{16,24},{20,28},{24,8},{28,12},{8,0},{12,4},{1,17},{... | collective-permute-start | bytes 2359304 | tf_op jit(solution)/shard_map/ppermute | solution.py:57
  28.5 64.8 %collective-permute-start.51 = (bf16[256,2048]{1,0:T(8,128)(2,1)}, bf16[256,2048]{1,0:T(8,128)(2,1)}, u32[]{:S(2)}, u32[]{:S(2)}) collective-permute-start(bf16[256,2048]{1,0:T(8,128)(2,1)} %bitcast.39), channel_id=1, source_target_pairs={{0,2},{1,3},{2,0},{3,1},{4,6},{5,7},{6,4},{7,5},{8,10},{9,11},{10,... | collective-permute-start | bytes 3145736 | tf_op jit(solution)/shard_map/ppermute | solution.py:42
  61.8 26.2 %collective-permute-start.18 = (bf16[256,2048]{1,0:T(8,128)(2,1)S(1)}, bf16[256,2048]{1,0:T(8,128)(2,1)}, u32[]{:S(2)}, u32[]{:S(2)}) collective-permute-start(bf16[256,2048]{1,0:T(8,128)(2,1)S(1)} %fusion.8), channel_id=1, source_target_pairs={{0,4},{4,0},{8,12},{12,8},{16,20},{20,16},{24,28},{28,24},{1,5},{5... | collective-permute-start | bytes 3145736 | tf_op jit(solution)/shard_map/ppermute | solution.py:42
  63.4 27.1 %collective-permute-start.6 = (bf16[256,2048]{1,0:T(8,128)(2,1)S(1)}, bf16[256,2048]{1,0:T(8,128)(2,1)}, u32[]{:S(2)}, u32[]{:S(2)}) collective-permute-start(bf16[256,2048]{1,0:T(8,128)(2,1)S(1)} %fusion.8), channel_id=1, source_target_pairs={{0,2},{1,3},{2,0},{3,1},{4,6},{5,7},{6,4},{7,5},{8,10},{9,11},{10,... | collective-permute-start | bytes 3145736 | tf_op jit(solution)/shard_map/ppermute | solution.py:42
  67.8 42.5 %collective-permute-start.53 = (bf16[256,2048]{1,0:T(8,128)(2,1)}, bf16[256,2048]{1,0:T(8,128)(2,1)S(1)}, u32[]{:S(2)}, u32[]{:S(2)}) collective-permute-start(bf16[256,2048]{1,0:T(8,128)(2,1)} %bitcast.39), channel_id=1, source_target_pairs={{0,4},{4,0},{8,12},{12,8},{16,20},{20,16},{24,28},{28,24},{1,5},{5... | collective-permute-start | bytes 3145736 | tf_op jit(solution)/shard_map/ppermute | solution.py:42
  68.4 31.5 %collective-permute-start.13 = (bf16[64,2048]{1,0:T(8,128)(2,1)S(1)}, bf16[64,2048]{1,0:T(8,128)(2,1)S(1)}, u32[]{:S(2)}, u32[]{:S(2)}) collective-permute-start(bf16[64,2048]{1,0:T(8,128)(2,1)S(1)} %copy-done.59), channel_id=1, source_target_pairs={{0,8},{4,12},{16,0},{20,4},{24,16},{28,20},{8,24},{12,28},{1,9},{5... | collective-permute-start | bytes 786440 | tf_op jit(solution)/shard_map/ppermute | solution.py:57
  90.5 23.5 %collective-permute-start.20 = (bf16[128,2048]{1,0:T(8,128)(2,1)S(1)}, bf16[128,2048]{1,0:T(8,128)(2,1)S(1)}, u32[]{:S(2)}, u32[]{:S(2)}) collective-permute-start(bf16[128,2048]{1,0:T(8,128)(2,1)S(1)} %slice.635), channel_id=1, source_target_pairs={{0,2},{1,3},{2,0},{3,1},{4,6},{5,7},{6,4},{7,5},{8,10},{9,11},{10,... | collective-permute-start | bytes 1572872 | tf_op jit(solution)/shard_map/ppermute | solution.py:42
  93.3 27.8 %collective-permute-start.19 = (bf16[128,2048]{1,0:T(8,128)(2,1)S(1)}, bf16[128,2048]{1,0:T(8,128)(2,1)S(1)}, u32[]{:S(2)}, u32[]{:S(2)}) collective-permute-start(bf16[128,2048]{1,0:T(8,128)(2,1)S(1)} %slice.634), channel_id=1, source_target_pairs={{0,4},{4,0},{8,12},{12,8},{16,20},{20,16},{24,28},{28,24},{1,5},{5... | collective-permute-start | bytes 1572872 | tf_op jit(solution)/shard_map/ppermute | solution.py:42
  99.9 92.0 %collective-permute-start.28 = (bf16[176,2048]{1,0:T(8,128)(2,1)}, bf16[176,2048]{1,0:T(8,128)(2,1)}, u32[]{:S(2)}, u32[]{:S(2)}) collective-permute-start(bf16[176,2048]{1,0:T(8,128)(2,1)} %bitcast.25), channel_id=1, source_target_pairs={{0,8},{4,12},{16,0},{20,4},{24,16},{28,20},{8,24},{12,28},{1,9},{5... | collective-permute-start | bytes 2162696 | tf_op jit(solution)/shard_map/ppermute | solution.py:57
  100.4 34.0 %collective-permute-start.10 = (bf16[3,32,2048]{2,1,0:T(8,128)(2,1)S(1)}, bf16[3,32,2048]{2,1,0:T(8,128)(2,1)S(1)}, u32[]{:S(2)}, u32[]{:S(2)}) collective-permute-start(bf16[3,32,2048]{2,1,0:T(8,128)(2,1)S(1)} %slice.621), channel_id=1, source_target_pairs={{0,16},{4,20},{16,24},{20,28},{24,8},{28,12},{8,0},{12,4},{1,17},{... | collective-permute-start | bytes 1179656 | tf_op jit(solution)/shard_map/ppermute | solution.py:57
  114.0 47.6 %collective-permute-start.7 = (bf16[512,2048]{1,0:T(8,128)(2,1)S(1)}, bf16[512,2048]{1,0:T(8,128)(2,1)S(1)}, u32[]{:S(2)}, u32[]{:S(2)}) collective-permute-start(bf16[512,2048]{1,0:T(8,128)(2,1)S(1)} %pad_maximum_fusion.4), channel_id=1, source_target_pairs={{0,1},{1,0},{2,3},{3,2},{4,5},{5,4},{6,7},{7,6},{8,9},{9,8},{10,11... | collective-permute-start | bytes 6291464 | tf_op jit(solution)/shard_map/ppermute | solution.py:42
  122.6 42.2 %collective-permute-start.21 = (bf16[512,2048]{1,0:T(8,128)(2,1)S(1)}, bf16[512,2048]{1,0:T(8,128)(2,1)S(1)}, u32[]{:S(2)}, u32[]{:S(2)}) collective-permute-start(bf16[512,2048]{1,0:T(8,128)(2,1)S(1)} %pad_maximum_fusion.5), channel_id=1, source_target_pairs={{0,1},{1,0},{2,3},{3,2},{4,5},{5,4},{6,7},{7,6},{8,9},{9,8},{10,11... | collective-permute-start | bytes 6291464 | tf_op jit(solution)/shard_map/ppermute | solution.py:42
  134.4 26.5 %collective-permute-start.11 = (bf16[3,32,2048]{2,1,0:T(8,128)(2,1)S(1)}, bf16[3,32,2048]{2,1,0:T(8,128)(2,1)S(1)}, u32[]{:S(2)}, u32[]{:S(2)}) collective-permute-start(bf16[3,32,2048]{2,1,0:T(8,128)(2,1)S(1)} %slice.622), channel_id=1, source_target_pairs={{0,8},{4,12},{16,0},{20,4},{24,16},{28,20},{8,24},{12,28},{1,9},{5... | collective-permute-start | bytes 1179656 | tf_op jit(solution)/shard_map/ppermute | solution.py:57
  134.4 59.9 %collective-permute-start.27 = (bf16[176,2048]{1,0:T(8,128)(2,1)}, bf16[176,2048]{1,0:T(8,128)(2,1)}, u32[]{:S(2)}, u32[]{:S(2)}) collective-permute-start(bf16[176,2048]{1,0:T(8,128)(2,1)} %bitcast.25), channel_id=1, source_target_pairs={{0,16},{4,20},{16,24},{20,28},{24,8},{28,12},{8,0},{12,4},{1,17},{... | collective-permute-start | bytes 2162696 | tf_op jit(solution)/shard_map/ppermute | solution.py:57
  160.9 39.6 %collective-permute-start.54 = (bf16[128,2048]{1,0:T(8,128)(2,1)}, bf16[128,2048]{1,0:T(8,128)(2,1)}, u32[]{:S(2)}, u32[]{:S(2)}) collective-permute-start(bf16[128,2048]{1,0:T(8,128)(2,1)} %slice.667), channel_id=1, source_target_pairs={{0,4},{4,0},{8,12},{12,8},{16,20},{20,16},{24,28},{28,24},{1,5},{5... | collective-permute-start | bytes 1572872 | tf_op jit(solution)/shard_map/ppermute | solution.py:42
  161.7 41.8 %collective-permute-start.55 = (bf16[128,2048]{1,0:T(8,128)(2,1)}, bf16[128,2048]{1,0:T(8,128)(2,1)}, u32[]{:S(2)}, u32[]{:S(2)}) collective-permute-start(bf16[128,2048]{1,0:T(8,128)(2,1)} %slice.668), channel_id=1, source_target_pairs={{0,2},{1,3},{2,0},{3,1},{4,6},{5,7},{6,4},{7,5},{8,10},{9,11},{10,... | collective-permute-start | bytes 1572872 | tf_op jit(solution)/shard_map/ppermute | solution.py:42
  178.4 26.9 %collective-permute-start.22 = (bf16[512,2048]{1,0:T(8,128)(2,1)}, bf16[512,2048]{1,0:T(8,128)(2,1)S(1)}, u32[]{:S(2)}, u32[]{:S(2)}) collective-permute-start(bf16[512,2048]{1,0:T(8,128)(2,1)} %slice.637), channel_id=1, source_target_pairs={{0,1},{1,0},{2,3},{3,2},{4,5},{5,4},{6,7},{7,6},{8,9},{9,8},{10,11... | collective-permute-start | bytes 6291464 | tf_op jit(solution)/shard_map/ppermute | solution.py:42
  194.4 52.1 %collective-permute-start.32 = (bf16[176,2048]{1,0:T(8,128)(2,1)S(1)}, bf16[176,2048]{1,0:T(8,128)(2,1)S(1)}, u32[]{:S(2)}, u32[]{:S(2)}) collective-permute-start(bf16[176,2048]{1,0:T(8,128)(2,1)S(1)} %bitcast.186), channel_id=1, source_target_pairs={{0,8},{4,12},{16,0},{20,4},{24,16},{28,20},{8,24},{12,28},{1,9},{5... | collective-permute-start | bytes 2162696 | tf_op jit(solution)/shard_map/ppermute | solution.py:57
  200.5 45.9 %collective-permute-start.31 = (bf16[176,2048]{1,0:T(8,128)(2,1)S(1)}, bf16[176,2048]{1,0:T(8,128)(2,1)S(1)}, u32[]{:S(2)}, u32[]{:S(2)}) collective-permute-start(bf16[176,2048]{1,0:T(8,128)(2,1)S(1)} %bitcast.187), channel_id=1, source_target_pairs={{0,16},{4,20},{16,24},{20,28},{24,8},{28,12},{8,0},{12,4},{1,17},{... | collective-permute-start | bytes 2162696 | tf_op jit(solution)/shard_map/ppermute | solution.py:57
  203.5 41.3 %collective-permute-start.30 = (bf16[80,2048]{1,0:T(8,128)(2,1)S(1)}, bf16[80,2048]{1,0:T(8,128)(2,1)S(1)}, u32[]{:S(2)}, u32[]{:S(2)}) collective-permute-start(bf16[80,2048]{1,0:T(8,128)(2,1)S(1)} %slice.644), channel_id=1, source_target_pairs={{0,8},{4,12},{16,0},{20,4},{24,16},{28,20},{8,24},{12,28},{1,9},{5... | collective-permute-start | bytes 983048 | tf_op jit(solution)/shard_map/ppermute | solution.py:57
  205.3 37.5 %collective-permute-start.29 = (bf16[96,2048]{1,0:T(8,128)(2,1)S(1)}, bf16[96,2048]{1,0:T(8,128)(2,1)S(1)}, u32[]{:S(2)}, u32[]{:S(2)}) collective-permute-start(bf16[96,2048]{1,0:T(8,128)(2,1)S(1)} %slice.643), channel_id=1, source_target_pairs={{0,16},{4,20},{16,24},{20,28},{24,8},{28,12},{8,0},{12,4},{1,17},{... | collective-permute-start | bytes 1179656 | tf_op jit(solution)/shard_map/ppermute | solution.py:57
  234.9 22.7 %collective-permute-start.26 = (bf16[256,2048]{1,0:T(8,128)(2,1)S(1)}, bf16[256,2048]{1,0:T(8,128)(2,1)S(1)}, u32[]{:S(2)}, u32[]{:S(2)}) collective-permute-start(bf16[256,2048]{1,0:T(8,128)(2,1)S(1)} %pad_maximum_fusion.15), channel_id=1, source_target_pairs={{0,4},{4,0},{8,12},{12,8},{16,20},{20,16},{24,28},{28,24},{1,5},{5... | collective-permute-start | bytes 3145736 | tf_op jit(solution)/shard_map/ppermute | solution.py:42
  242.8 25.1 %collective-permute-start.24 = (bf16[256,2048]{1,0:T(8,128)(2,1)S(1)}, bf16[256,2048]{1,0:T(8,128)(2,1)S(1)}, u32[]{:S(2)}, u32[]{:S(2)}) collective-permute-start(bf16[256,2048]{1,0:T(8,128)(2,1)S(1)} %pad_maximum_fusion.14), channel_id=1, source_target_pairs={{0,2},{1,3},{2,0},{3,1},{4,6},{5,7},{6,4},{7,5},{8,10},{9,11},{10,... | collective-permute-start | bytes 3145736 | tf_op jit(solution)/shard_map/ppermute | solution.py:42
  244.8 78.7 %collective-permute-start.52 = (bf16[512,2048]{1,0:T(8,128)(2,1)S(1)}, bf16[512,2048]{1,0:T(8,128)(2,1)S(1)}, u32[]{:S(2)}, u32[]{:S(2)}) collective-permute-start(bf16[512,2048]{1,0:T(8,128)(2,1)S(1)} %copy-done.45), channel_id=1, source_target_pairs={{0,1},{1,0},{2,3},{3,2},{4,5},{5,4},{6,7},{7,6},{8,9},{9,8},{10,11... | collective-permute-start | bytes 6291464 | tf_op jit(solution)/shard_map/ppermute | solution.py:42
  246.5 53.3 %collective-permute-start.42 = (bf16[176,2048]{1,0:T(8,128)(2,1)S(1)}, bf16[176,2048]{1,0:T(8,128)(2,1)S(1)}, u32[]{:S(2)}, u32[]{:S(2)}) collective-permute-start(bf16[176,2048]{1,0:T(8,128)(2,1)S(1)} %bitcast.189), channel_id=1, source_target_pairs={{0,8},{4,12},{16,0},{20,4},{24,16},{28,20},{8,24},{12,28},{1,9},{5... | collective-permute-start | bytes 2162696 | tf_op jit(solution)/shard_map/ppermute | solution.py:57
  247.0 52.8 %collective-permute-start.41 = (bf16[176,2048]{1,0:T(8,128)(2,1)S(1)}, bf16[176,2048]{1,0:T(8,128)(2,1)S(1)}, u32[]{:S(2)}, u32[]{:S(2)}) collective-permute-start(bf16[176,2048]{1,0:T(8,128)(2,1)S(1)} %bitcast.190), channel_id=1, source_target_pairs={{0,16},{4,20},{16,24},{20,28},{24,8},{28,12},{8,0},{12,4},{1,17},{... | collective-permute-start | bytes 2162696 | tf_op jit(solution)/shard_map/ppermute | solution.py:57
  257.7 31.0 %collective-permute-start.34 = (bf16[80,2048]{1,0:T(8,128)(2,1)S(1)}, bf16[80,2048]{1,0:T(8,128)(2,1)S(1)}, u32[]{:S(2)}, u32[]{:S(2)}) collective-permute-start(bf16[80,2048]{1,0:T(8,128)(2,1)S(1)} %slice.646), channel_id=1, source_target_pairs={{0,8},{4,12},{16,0},{20,4},{24,16},{28,20},{8,24},{12,28},{1,9},{5... | collective-permute-start | bytes 983048 | tf_op jit(solution)/shard_map/ppermute | solution.py:57
  268.0 28.2 %collective-permute-start.33 = (bf16[96,2048]{1,0:T(8,128)(2,1)S(1)}, bf16[96,2048]{1,0:T(8,128)(2,1)S(1)}, u32[]{:S(2)}, u32[]{:S(2)}) collective-permute-start(bf16[96,2048]{1,0:T(8,128)(2,1)S(1)} %slice.645), channel_id=1, source_target_pairs={{0,16},{4,20},{16,24},{20,28},{24,8},{28,12},{8,0},{12,4},{1,17},{... | collective-permute-start | bytes 1179656 | tf_op jit(solution)/shard_map/ppermute | solution.py:57
  288.6 24.6 %collective-permute-start.37 = (bf16[256,2048]{1,0:T(8,128)(2,1)S(1)}, bf16[256,2048]{1,0:T(8,128)(2,1)S(1)}, u32[]{:S(2)}, u32[]{:S(2)}) collective-permute-start(bf16[256,2048]{1,0:T(8,128)(2,1)S(1)} %get-tuple-element.74), channel_id=1, source_target_pairs={{0,4},{4,0},{8,12},{12,8},{16,20},{20,16},{24,28},{28,24},{1,5},{5... | collective-permute-start | bytes 3145736 | tf_op jit(solution)/shard_map/ppermute | solution.py:42
  296.1 26.0 %collective-permute-start.35 = (bf16[256,2048]{1,0:T(8,128)(2,1)S(1)}, bf16[256,2048]{1,0:T(8,128)(2,1)S(1)}, u32[]{:S(2)}, u32[]{:S(2)}) collective-permute-start(bf16[256,2048]{1,0:T(8,128)(2,1)S(1)} %get-tuple-element.74), channel_id=1, source_target_pairs={{0,2},{1,3},{2,0},{3,1},{4,6},{5,7},{6,4},{7,5},{8,10},{9,11},{10,... | collective-permute-start | bytes 3145736 | tf_op jit(solution)/shard_map/ppermute | solution.py:42
  299.7 42.3 %collective-permute-start.56 = (bf16[512,2048]{1,0:T(8,128)(2,1)S(1)}, bf16[512,2048]{1,0:T(8,128)(2,1)S(1)}, u32[]{:S(2)}, u32[]{:S(2)}) collective-permute-start(bf16[512,2048]{1,0:T(8,128)(2,1)S(1)} %pad_maximum_fusion.9), channel_id=1, source_target_pairs={{0,1},{1,0},{2,3},{3,2},{4,5},{5,4},{6,7},{7,6},{8,9},{9,8},{10,11... | collective-permute-start | bytes 6291464 | tf_op jit(solution)/shard_map/ppermute | solution.py:42
  299.8 42.2 %collective-permute-start.44 = (bf16[80,2048]{1,0:T(8,128)(2,1)S(1)}, bf16[80,2048]{1,0:T(8,128)(2,1)S(1)}, u32[]{:S(2)}, u32[]{:S(2)}) collective-permute-start(bf16[80,2048]{1,0:T(8,128)(2,1)S(1)} %slice.654), channel_id=1, source_target_pairs={{0,8},{4,12},{16,0},{20,4},{24,16},{28,20},{8,24},{12,28},{1,9},{5... | collective-permute-start | bytes 983048 | tf_op jit(solution)/shard_map/ppermute | solution.py:57
  323.5 20.4 %collective-permute-start.36 = (bf16[512,2048]{1,0:T(8,128)(2,1)S(1)}, bf16[512,2048]{1,0:T(8,128)(2,1)S(1)}, u32[]{:S(2)}, u32[]{:S(2)}) collective-permute-start(bf16[512,2048]{1,0:T(8,128)(2,1)S(1)} %pad_maximum_fusion.6), channel_id=1, source_target_pairs={{0,1},{1,0},{2,3},{3,2},{4,5},{5,4},{6,7},{7,6},{8,9},{9,8},{10,11... | collective-permute-start | bytes 6291464 | tf_op jit(solution)/shard_map/ppermute | solution.py:42
  449.8 122.6 %collective-permute-start.106 = (bf16[96,2048]{1,0:T(8,128)(2,1)}, bf16[96,2048]{1,0:T(8,128)(2,1)}, u32[]{:S(2)}, u32[]{:S(2)}) collective-permute-start(bf16[96,2048]{1,0:T(8,128)(2,1)} %get-tuple-element.114), channel_id=1, source_target_pairs={{0,16},{4,20},{16,24},{20,28},{24,8},{28,12},{8,0},{12,4},{1,17},{... | collective-permute-start | bytes 1179656 | tf_op jit(solution)/shard_map/ppermute | solution.py:57
  451.1 23.2 %collective-permute-start.104 = (bf16[80,2048]{1,0:T(8,128)(2,1)S(1)}, bf16[80,2048]{1,0:T(8,128)(2,1)S(1)}, u32[]{:S(2)}, u32[]{:S(2)}) collective-permute-start(bf16[80,2048]{1,0:T(8,128)(2,1)S(1)} %get-tuple-element.103), channel_id=1, source_target_pairs={{0,8},{4,12},{16,0},{20,4},{24,16},{28,20},{8,24},{12,28},{1,9},{5... | collective-permute-start | bytes 983048 | tf_op jit(solution)/shard_map/ppermute | solution.py:57
  452.9 28.4 %collective-permute-start.100 = (bf16[80,2048]{1,0:T(8,128)(2,1)S(1)}, bf16[80,2048]{1,0:T(8,128)(2,1)S(1)}, u32[]{:S(2)}, u32[]{:S(2)}) collective-permute-start(bf16[80,2048]{1,0:T(8,128)(2,1)S(1)} %get-tuple-element.104), channel_id=1, source_target_pairs={{0,8},{4,12},{16,0},{20,4},{24,16},{28,20},{8,24},{12,28},{1,9},{5... | collective-permute-start | bytes 983048 | tf_op jit(solution)/shard_map/ppermute | solution.py:57
  455.6 27.7 %collective-permute-start.58 = (bf16[512,2048]{1,0:T(8,128)(2,1)S(1)}, bf16[512,2048]{1,0:T(8,128)(2,1)S(1)}, u32[]{:S(2)}, u32[]{:S(2)}) collective-permute-start(bf16[512,2048]{1,0:T(8,128)(2,1)S(1)} %slice.678), channel_id=1, source_target_pairs={{0,1},{1,0},{2,3},{3,2},{4,5},{5,4},{6,7},{7,6},{8,9},{9,8},{10,11... | collective-permute-start | bytes 6291464 | tf_op jit(solution)/shard_map/ppermute | solution.py:42
  466.5 53.0 %collective-permute-start.102 = (bf16[96,2048]{1,0:T(8,128)(2,1)}, bf16[96,2048]{1,0:T(8,128)(2,1)}, u32[]{:S(2)}, u32[]{:S(2)}) collective-permute-start(bf16[96,2048]{1,0:T(8,128)(2,1)} %get-tuple-element.98), channel_id=1, source_target_pairs={{0,16},{4,20},{16,24},{20,28},{24,8},{28,12},{8,0},{12,4},{1,17},{... | collective-permute-start | bytes 1179656 | tf_op jit(solution)/shard_map/ppermute | solution.py:57
  485.1 35.5 %collective-permute-start.98 = (bf16[96,2048]{1,0:T(8,128)(2,1)}, bf16[96,2048]{1,0:T(8,128)(2,1)}, u32[]{:S(2)}, u32[]{:S(2)}) collective-permute-start(bf16[96,2048]{1,0:T(8,128)(2,1)} %get-tuple-element.101), channel_id=1, source_target_pairs={{0,16},{4,20},{16,24},{20,28},{24,8},{28,12},{8,0},{12,4},{1,17},{... | collective-permute-start | bytes 1179656 | tf_op jit(solution)/shard_map/ppermute | solution.py:57
  515.1 26.0 %collective-permute-start.62 = (bf16[256,2048]{1,0:T(8,128)(2,1)S(1)}, bf16[256,2048]{1,0:T(8,128)(2,1)S(1)}, u32[]{:S(2)}, u32[]{:S(2)}) collective-permute-start(bf16[256,2048]{1,0:T(8,128)(2,1)S(1)} %pad_maximum_fusion.19), channel_id=1, source_target_pairs={{0,4},{4,0},{8,12},{12,8},{16,20},{20,16},{24,28},{28,24},{1,5},{5... | collective-permute-start | bytes 3145736 | tf_op jit(solution)/shard_map/ppermute | solution.py:42
  518.3 26.0 %collective-permute-start.60 = (bf16[256,2048]{1,0:T(8,128)(2,1)S(1)}, bf16[256,2048]{1,0:T(8,128)(2,1)S(1)}, u32[]{:S(2)}, u32[]{:S(2)}) collective-permute-start(bf16[256,2048]{1,0:T(8,128)(2,1)S(1)} %pad_maximum_fusion.18), channel_id=1, source_target_pairs={{0,2},{1,3},{2,0},{3,1},{4,6},{5,7},{6,4},{7,5},{8,10},{9,11},{10,... | collective-permute-start | bytes 3145736 | tf_op jit(solution)/shard_map/ppermute | solution.py:42
  519.6 41.1 %collective-permute-start.50 = (bf16[256,2048]{1,0:T(8,128)(2,1)S(1)}, bf16[256,2048]{1,0:T(8,128)(2,1)S(1)}, u32[]{:S(2)}, u32[]{:S(2)}) collective-permute-start(bf16[256,2048]{1,0:T(8,128)(2,1)S(1)} %pad_maximum_fusion.17), channel_id=1, source_target_pairs={{0,4},{4,0},{8,12},{12,8},{16,20},{20,16},{24,28},{28,24},{1,5},{5... | collective-permute-start | bytes 3145736 | tf_op jit(solution)/shard_map/ppermute | solution.py:42
  520.6 43.0 %collective-permute-start.48 = (bf16[256,2048]{1,0:T(8,128)(2,1)S(1)}, bf16[256,2048]{1,0:T(8,128)(2,1)S(1)}, u32[]{:S(2)}, u32[]{:S(2)}) collective-permute-start(bf16[256,2048]{1,0:T(8,128)(2,1)S(1)} %pad_maximum_fusion.16), channel_id=1, source_target_pairs={{0,2},{1,3},{2,0},{3,1},{4,6},{5,7},{6,4},{7,5},{8,10},{9,11},{10,... | collective-permute-start | bytes 3145736 | tf_op jit(solution)/shard_map/ppermute | solution.py:42
  541.1 34.5 %collective-permute-start.101 = (bf16[176,2048]{1,0:T(8,128)(2,1)}, bf16[176,2048]{1,0:T(8,128)(2,1)}, u32[]{:S(2)}, u32[]{:S(2)}) collective-permute-start(bf16[176,2048]{1,0:T(8,128)(2,1)} %pad_maximum_fusion.25), channel_id=1, source_target_pairs={{0,8},{4,12},{16,0},{20,4},{24,16},{28,20},{8,24},{12,28},{1,9},{5... | collective-permute-start | bytes 2162696 | tf_op jit(solution)/shard_map/ppermute | solution.py:57
  544.3 32.3 %collective-permute-start.105 = (bf16[176,2048]{1,0:T(8,128)(2,1)}, bf16[176,2048]{1,0:T(8,128)(2,1)S(1)}, u32[]{:S(2)}, u32[]{:S(2)}) collective-permute-start(bf16[176,2048]{1,0:T(8,128)(2,1)} %pad_maximum_fusion.27), channel_id=1, source_target_pairs={{0,8},{4,12},{16,0},{20,4},{24,16},{28,20},{8,24},{12,28},{1,9},{5... | collective-permute-start | bytes 2162696 | tf_op jit(solution)/shard_map/ppermute | solution.py:57
  569.7 22.1 %collective-permute-start.63 = (bf16[256,2048]{1,0:T(8,128)(2,1)S(1)}, bf16[256,2048]{1,0:T(8,128)(2,1)S(1)}, u32[]{:S(2)}, u32[]{:S(2)}) collective-permute-start(bf16[256,2048]{1,0:T(8,128)(2,1)S(1)} %get-tuple-element.71), channel_id=1, source_target_pairs={{0,2},{1,3},{2,0},{3,1},{4,6},{5,7},{6,4},{7,5},{8,10},{9,11},{10,... | collective-permute-start | bytes 3145736 | tf_op jit(solution)/shard_map/ppermute | solution.py:42
  570.6 24.3 %collective-permute-start.99 = (bf16[176,2048]{1,0:T(8,128)(2,1)S(1)}, bf16[176,2048]{1,0:T(8,128)(2,1)S(1)}, u32[]{:S(2)}, u32[]{:S(2)}) collective-permute-start(bf16[176,2048]{1,0:T(8,128)(2,1)S(1)} %pad_maximum_fusion.24), channel_id=1, source_target_pairs={{0,16},{4,20},{16,24},{20,28},{24,8},{28,12},{8,0},{12,4},{1,17},{... | collective-permute-start | bytes 2162696 | tf_op jit(solution)/shard_map/ppermute | solution.py:57
  572.5 46.0 %collective-permute-start.103 = (bf16[176,2048]{1,0:T(8,128)(2,1)S(1)}, bf16[176,2048]{1,0:T(8,128)(2,1)S(1)}, u32[]{:S(2)}, u32[]{:S(2)}) collective-permute-start(bf16[176,2048]{1,0:T(8,128)(2,1)S(1)} %pad_maximum_fusion.26), channel_id=1, source_target_pairs={{0,16},{4,20},{16,24},{20,28},{24,8},{28,12},{8,0},{12,4},{1,17},{... | collective-permute-start | bytes 2162696 | tf_op jit(solution)/shard_map/ppermute | solution.py:57
  575.6 46.7 %collective-permute-start.66 = (bf16[256,2048]{1,0:T(8,128)(2,1)S(1)}, bf16[256,2048]{1,0:T(8,128)(2,1)}, u32[]{:S(2)}, u32[]{:S(2)}) collective-permute-start(bf16[256,2048]{1,0:T(8,128)(2,1)S(1)} %get-tuple-element.71), channel_id=1, source_target_pairs={{0,4},{4,0},{8,12},{12,8},{16,20},{20,16},{24,28},{28,24},{1,5},{5... | collective-permute-start | bytes 3145736 | tf_op jit(solution)/shard_map/ppermute | solution.py:42
  576.6 50.2 %collective-permute-start.109 = (bf16[176,2048]{1,0:T(8,128)(2,1)S(1)}, bf16[176,2048]{1,0:T(8,128)(2,1)S(1)}, u32[]{:S(2)}, u32[]{:S(2)}) collective-permute-start(bf16[176,2048]{1,0:T(8,128)(2,1)S(1)} %copy-done.54), channel_id=1, source_target_pairs={{0,8},{4,12},{16,0},{20,4},{24,16},{28,20},{8,24},{12,28},{1,9},{5... | collective-permute-start | bytes 2162696 | tf_op jit(solution)/shard_map/ppermute | solution.py:57
  591.8 40.7 %collective-permute-start.107 = (bf16[176,2048]{1,0:T(8,128)(2,1)S(1)}, bf16[176,2048]{1,0:T(8,128)(2,1)S(1)}, u32[]{:S(2)}, u32[]{:S(2)}) collective-permute-start(bf16[176,2048]{1,0:T(8,128)(2,1)S(1)} %pad_maximum_fusion.28), channel_id=1, source_target_pairs={{0,16},{4,20},{16,24},{20,28},{24,8},{28,12},{8,0},{12,4},{1,17},{... | collective-permute-start | bytes 2162696 | tf_op jit(solution)/shard_map/ppermute | solution.py:57
  595.0 47.1 %collective-permute-start.64 = (bf16[512,2048]{1,0:T(8,128)(2,1)}, bf16[512,2048]{1,0:T(8,128)(2,1)}, u32[]{:S(2)}, u32[]{:S(2)}) collective-permute-start(bf16[512,2048]{1,0:T(8,128)(2,1)} %pad_maximum_fusion.10), channel_id=1, source_target_pairs={{0,1},{1,0},{2,3},{3,2},{4,5},{5,4},{6,7},{7,6},{8,9},{9,8},{10,11... | collective-permute-start | bytes 6291464 | tf_op jit(solution)/shard_map/ppermute | solution.py:42
  639.8 42.9 %collective-permute-start.69 = (bf16[512,2048]{1,0:T(8,128)(2,1)}, bf16[512,2048]{1,0:T(8,128)(2,1)}, u32[]{:S(2)}, u32[]{:S(2)}) collective-permute-start(bf16[512,2048]{1,0:T(8,128)(2,1)} %pad_maximum_fusion.11), channel_id=1, source_target_pairs={{0,1},{1,0},{2,3},{3,2},{4,5},{5,4},{6,7},{7,6},{8,9},{9,8},{10,11... | collective-permute-start | bytes 6291464 | tf_op jit(solution)/shard_map/ppermute | solution.py:42
  670.8 120.1 %collective-permute-start.65 = (bf16[512,2048]{1,0:T(8,128)(2,1)}, bf16[512,2048]{1,0:T(8,128)(2,1)}, u32[]{:S(2)}, u32[]{:S(2)}) collective-permute-start(bf16[512,2048]{1,0:T(8,128)(2,1)} %slice.685), channel_id=1, source_target_pairs={{0,1},{1,0},{2,3},{3,2},{4,5},{5,4},{6,7},{7,6},{8,9},{9,8},{10,11... | collective-permute-start | bytes 6291464 | tf_op jit(solution)/shard_map/ppermute | solution.py:42
  715.7 43.9 %collective-permute-start.89 = (bf16[73,64]{1,0:T(8,128)(2,1)S(1)}, bf16[73,64]{1,0:T(8,128)(2,1)S(1)}, u32[]{:S(2)}, u32[]{:S(2)}) collective-permute-start(bf16[73,64]{1,0:T(8,128)(2,1)S(1)} %get-tuple-element.147), channel_id=1, source_target_pairs={{0,16},{4,20},{16,24},{20,28},{24,8},{28,12},{8,0},{12,4},{1,17},{... | collective-permute-start | bytes 28040 | tf_op jit(solution)/shard_map/ppermute | solution.py:57
  717.8 49.9 %collective-permute-start.91 = (bf16[73,64]{1,0:T(8,128)(2,1)S(1)}, bf16[73,64]{1,0:T(8,128)(2,1)S(1)}, u32[]{:S(2)}, u32[]{:S(2)}) collective-permute-start(bf16[73,64]{1,0:T(8,128)(2,1)S(1)} %get-tuple-element.148), channel_id=1, source_target_pairs={{0,8},{4,12},{16,0},{20,4},{24,16},{28,20},{8,24},{12,28},{1,9},{5... | collective-permute-start | bytes 28040 | tf_op jit(solution)/shard_map/ppermute | solution.py:57
  771.9 46.9 %collective-permute-start.82 = (bf16[64,2048]{1,0:T(8,128)(2,1)S(1)}, bf16[64,2048]{1,0:T(8,128)(2,1)S(1)}, u32[]{:S(2)}, u32[]{:S(2)}) collective-permute-start(bf16[64,2048]{1,0:T(8,128)(2,1)S(1)} %pad_maximum_fusion.31), channel_id=1, source_target_pairs={{0,8},{4,12},{16,0},{20,4},{24,16},{28,20},{8,24},{12,28},{1,9},{5... | collective-permute-start | bytes 786440 | tf_op jit(solution)/shard_map/ppermute | solution.py:57
  776.0 45.0 %collective-permute-start.80 = (bf16[64,2048]{1,0:T(8,128)(2,1)}, bf16[64,2048]{1,0:T(8,128)(2,1)}, u32[]{:S(2)}, u32[]{:S(2)}) collective-permute-start(bf16[64,2048]{1,0:T(8,128)(2,1)} %pad_maximum_fusion.30), channel_id=1, source_target_pairs={{0,16},{4,20},{16,24},{20,28},{24,8},{28,12},{8,0},{12,4},{1,17},{... | collective-permute-start | bytes 786440 | tf_op jit(solution)/shard_map/ppermute | solution.py:57
  785.4 37.6 %collective-permute-start.78 = (bf16[3,64,2048]{2,1,0:T(8,128)(2,1)}, bf16[3,64,2048]{2,1,0:T(8,128)(2,1)}, u32[]{:S(2)}, u32[]{:S(2)}) collective-permute-start(bf16[3,64,2048]{2,1,0:T(8,128)(2,1)} %pad_maximum_fusion.23), channel_id=1, source_target_pairs={{0,8},{4,12},{16,0},{20,4},{24,16},{28,20},{8,24},{12,28},{1,9},{5... | collective-permute-start | bytes 2359304 | tf_op jit(solution)/shard_map/ppermute | solution.py:57
  787.3 41.9 %collective-permute-start.76 = (bf16[3,64,2048]{2,1,0:T(8,128)(2,1)}, bf16[3,64,2048]{2,1,0:T(8,128)(2,1)}, u32[]{:S(2)}, u32[]{:S(2)}) collective-permute-start(bf16[3,64,2048]{2,1,0:T(8,128)(2,1)} %pad_maximum_fusion.22), channel_id=1, source_target_pairs={{0,16},{4,20},{16,24},{20,28},{24,8},{28,12},{8,0},{12,4},{1,17},{... | collective-permute-start | bytes 2359304 | tf_op jit(solution)/shard_map/ppermute | solution.py:57
  816.0 20.6 %collective-permute-start.74 = (bf16[256,2048]{1,0:T(8,128)(2,1)}, bf16[256,2048]{1,0:T(8,128)(2,1)S(1)}, u32[]{:S(2)}, u32[]{:S(2)}) collective-permute-start(bf16[256,2048]{1,0:T(8,128)(2,1)} %pad_maximum_fusion.21), channel_id=1, source_target_pairs={{0,4},{4,0},{8,12},{12,8},{16,20},{20,16},{24,28},{28,24},{1,5},{5... | collective-permute-start | bytes 3145736 | tf_op jit(solution)/shard_map/ppermute | solution.py:42
  (133 other events, 2077.0 us)

commit v3 on v2

--- a/solution.py
+++ b/solution.py
@@ -40,6 +40,13 @@
 def swap(values, axis, shift):
     size = lax.axis_size(axis)
     return lax.ppermute(values, axis, [(i, i ^ shift) for i in range(size)])
+
+
+def after(values, tokens):
+    if not tokens:
+        return values
+    joined = lax.optimization_barrier(tuple(values) + tuple(tokens))
+    return list(joined[: len(values)])
 
 
 def ring_of(size):
@@ -75,23 +82,28 @@
     )
 
 
-def gather_ring(own, axis=0, halves=True):
+def gather_ring(own, axis=0, halves=True, tokens=(), later=()):
     outer = lax.axis_size("wide") // 2
-    before, after = [own], [own]
-    for _ in range(1, outer // 2):
-        before.append(along(before[-1], 1))
-        after.append(along(after[-1], -1))
+    [own] = after([own], list(tokens))
+    before, behind = [own], [own]
+    for h in range(1, outer // 2):
+        one, two = along(before[-1], 1), along(behind[-1], -1)
+        if halves:
+            one, two = lax.optimization_barrier((one, two))
+        before.append(one)
+        behind.append(two)
     if halves:
         top, _ = two_parts(before[-1], axis)
-        _, bottom = two_parts(after[-1], axis)
+        _, bottom = two_parts(behind[-1], axis)
+        top, bottom = after([top, bottom], later)
         opposite = [along(top, 1), along(bottom, -1)]
     else:
         opposite = [along(before[-1], 1)]
-    near = [piece for h in range(1, outer // 2) for piece in (before[h], after[h])]
-    return [own] + near + opposite, near
-
-
-def scatter_ring(full, axis=0, halves=True):
+    near = [piece for h in range(1, outer // 2) for piece in (before[h], behind[h])]
+    return [own] + near + opposite, opposite
+
+
+def scatter_ring(full, axis=0, halves=True, tokens=(), later=()):
     outer = lax.axis_size("wide") // 2
     wire = full.dtype
     chunks = jnp.split(full, outer, axis=axis)
@@ -100,7 +112,7 @@
     behind = {h: chunks[2 * h - 1].astype(f32) for h in range(1, most + 1)}
     ahead = {h: chunks[2 * h].astype(f32) for h in range(1, most + 1)}
     if halves:
-        top, bottom = two_parts(chunks[-1], axis)
+        top, bottom = after(two_parts(chunks[-1], axis), tokens)
         far_top, far_bottom = two_parts(ahead[most], axis)
         got = along(top, 1).astype(f32)
         ahead[most] = jnp.concatenate([far_top + got, far_bottom], axis=axis)
@@ -110,49 +122,71 @@
     else:
         ahead[most] = ahead[most] + along(chunks[-1], 1).astype(f32)
     for h in range(most, 0, -1):
-        got = along(ahead[h].astype(wire), 1).astype(f32)
-        back = along(behind[h].astype(wire), -1).astype(f32)
+        one, two = ahead[h].astype(wire), behind[h].astype(wire)
+        if halves:
+            one, two = lax.optimization_barrier((one, two, *later))[:2]
+        one, two = along(one, 1), along(two, -1)
+        got, back = one.astype(f32), two.astype(f32)
         if h > 1:
             ahead[h - 1] = ahead[h - 1] + got
             behind[h - 1] = behind[h - 1] + back
         else:
             total = total + got + back
-    return total
-
-
-def gather_rows(own):
+    return total, (one, two)
+
+
+def gather_rows(own, tokens=()):
     size = lax.axis_size("narrow")
     half = own.shape[0] // 2
+    [own] = after([own], tokens)
     across = [swap(own, "narrow", k) for k in range(2, size, 2)]
     beside = swap(own, "wide", 1)
-    even = jnp.concatenate([own] + across, axis=0)
-    odd = swap(even, "narrow", 1)
-    parts = [beside]
+    stage_one = across + [beside]
+    corner, stage_two = [], []
     for n, k in enumerate(range(2, size, 2)):
-        parts.append(swap(across[n][:half], "wide", 1))
-        parts.append(swap(beside[half:], "narrow", k))
-    other_even = jnp.concatenate(parts, axis=0)
-    other_odd = swap(other_even, "narrow", 1)
-    return even, odd, other_even, other_odd
-
-
-def scatter_rows(even, odd, other_even, other_odd):
+        ends = [swap(across[n][:half], "wide", 1), swap(beside[half:], "narrow", k)]
+        corner.append(jnp.concatenate(ends, axis=0))
+        stage_two += ends
+    [own_again] = after([own], stage_one)
+    odd = [swap(piece, "narrow", 1) for piece in [own_again] + across]
+    other_odd = [swap(piece, "narrow", 1) for piece in [beside] + corner]
+    pieces = [own] + across + odd, [beside] + corner + other_odd
+    return pieces, (stage_one, stage_two, odd + other_odd)
+
+
+def scatter_rows(even, odd, other_even, other_odd, tokens=()):
     size = lax.axis_size("narrow")
     rows = even.shape[0] // (size // 2)
     half = rows // 2
-    other = other_even.astype(f32) + swap(other_odd, "narrow", 1).astype(f32)
-    mine = even.astype(f32) + swap(odd, "narrow", 1).astype(f32)
+    stage_one = [swap(other_odd, "narrow", 1), swap(odd, "narrow", 1)]
+    other = other_even.astype(f32) + stage_one[0].astype(f32)
+    mine = even.astype(f32) + stage_one[1].astype(f32)
     beside_top, beside_bottom = other[:half], other[half:rows]
     out = mine[:rows]
+    corners = other[rows:].astype(bf16)
+    [corners] = after([corners], tokens)
+    spread, stage_two, stage_three = [], [], []
     for n, k in enumerate(range(2, size, 2)):
-        at = (n + 1) * rows
-        top = swap(other[at : at + half].astype(bf16), "wide", 1).astype(f32)
-        bottom = swap(other[at + half : at + rows].astype(bf16), "narrow", k).astype(f32)
-        beside_bottom = beside_bottom + bottom
-        across = jnp.concatenate([mine[at : at + half] + top, mine[at + half : at + rows]], axis=0)
-        out = out + swap(across.astype(bf16), "narrow", k).astype(f32)
-    beside = jnp.concatenate([beside_top, beside_bottom], axis=0)
-    return out + swap(beside.astype(bf16), "wide", 1).astype(f32)
+        at = n * rows
+        ends = [
+            swap(corners[at : at + half], "wide", 1),
+            swap(corners[at + half : at + rows], "narrow", k),
+        ]
+        stage_two += ends
+        beside_bottom = beside_bottom + ends[1].astype(f32)
+        at = at + rows
+        spread.append(
+            jnp.concatenate(
+                [mine[at : at + half] + ends[0].astype(f32), mine[at + half : at + rows]], axis=0
+            ).astype(bf16)
+        )
+    spread.append(jnp.concatenate([beside_top, beside_bottom], axis=0).astype(bf16))
+    spread = lax.optimization_barrier(tuple(spread))
+    for n, k in enumerate(range(2, size, 2)):
+        stage_three.append(swap(spread[n], "narrow", k))
+        out = out + stage_three[-1].astype(f32)
+    stage_three.append(swap(spread[-1], "wide", 1))
+    return out + stage_three[-1].astype(f32), (stage_one, stage_two, stage_three)
 
 
 def inverse_rms(values):
@@ -526,6 +560,8 @@
     order = picked(jnp.arange(narrow) ^ narrow_at, narrow, jnp.asarray(place_of, jnp.int32))
     narrow_of = jnp.asarray(offsets, jnp.int32) ^ narrow_at
 
+    (first_own, first_other), first_stages = gather_rows(tokens[0])
+
     small = jnp.concatenate(
         [
             short_kernel.reshape(9, own),
@@ -539,6 +575,7 @@
     )
     small_all = jnp.concatenate(gather_ring(small, axis=1, halves=False)[0], axis=1)
     gains = small_all[small.shape[0] - 2 :].reshape(2, outer, own)
+    [gains] = after([gains], first_stages[0])
     gains = jnp.stack([gains, swap(gains, "wide", 1)])
     gains = jnp.stack([gains] + [swap(gains, "narrow", k) for k in range(2, narrow, 2)])
     gains = jnp.concatenate([gains, swap(gains, "narrow", 1)], axis=0).astype(f32)
@@ -550,35 +587,32 @@
     gain_first, gain_last = gain_all[0], gain_all[1]
 
     def reduce_gain(values):
-        values = values.reshape(outer, 2, narrow, own)
-        values = picked(piece_outer, outer, values).transpose(1, 0, 2, 3)
-        values = picked(sides, 2, values).transpose(2, 0, 1, 3)
+        values = values.reshape(2, outer, 2, narrow, own).transpose(1, 2, 3, 0, 4)
+        values = picked(piece_outer, outer, values).transpose(1, 0, 2, 3, 4)
+        values = picked(sides, 2, values).transpose(2, 0, 1, 3, 4)
         values = picked(narrow_of, narrow, values)
         total = values[: narrow // 2] + swap(values[narrow // 2 :], "narrow", 1)
         summed = total[0]
         for k in range(1, narrow // 2):
             summed = summed + swap(total[k], "narrow", 2 * k)
         summed = summed[0] + swap(summed[1], "wide", 1)
-        return scatter_ring(summed, halves=False)[0]
+        return scatter_ring(summed, halves=False)[0][0]
 
     documents = jnp.concatenate([doc_blocks, doc_pad], axis=0)
+    [documents] = after([documents], first_stages[0])
     documents = (documents, swap(documents, "wide", 1))
     tables = [layout(rules[0], rules[1], slots) for rules in documents]
 
-    in_pieces, sent = gather_ring(w_in.transpose(0, 2, 1), axis=1)
-    out_own, gate_own, up_own, down_own = w_out, w_gate.T, w_up.T, w_down.T
-    out_own, gate_own, *_ = lax.optimization_barrier((out_own, gate_own, *sent))
-    out_pieces, _ = gather_ring(out_own)
-    gate_pieces, sent = gather_ring(gate_own)
-    up_own, *_ = lax.optimization_barrier((up_own, *sent))
-    up_pieces, sent = gather_ring(up_own)
-    down_own, *_ = lax.optimization_barrier((down_own, *sent))
-    down_pieces, _ = gather_ring(down_own)
+    in_pieces, last = gather_ring(w_in.transpose(0, 2, 1), axis=1)
+    out_pieces, last = gather_ring(w_out, tokens=list(last) + first_stages[2])
+
+    def normed(pieces):
+        values = jnp.concatenate(pieces, axis=0).astype(f32)
+        return (values * inverse_rms(values) * gain_first).astype(bf16)
 
     rate_first = inverse_rms(source)
-    low_first = (source * rate_first * gain_first).astype(bf16)
-    first_parts = gather_rows(low_first)
-    rows_first = [jnp.concatenate(first_parts[:2], axis=0), jnp.concatenate(first_parts[2:], axis=0)]
+    rows_first = [normed(first_own), normed(first_other)]
+    (upstream_own, upstream_other), _ = gather_rows(upstream_low, first_stages[1])
 
     matrix = transform()
     fwd = jnp.asarray(matrix, bf16)
@@ -622,74 +656,85 @@
         )
         mixed.append((proj, gated.reshape(slots, channels), long_out, seen))
     out_all = jnp.concatenate(out_pieces, axis=0)
-    shares = []
-    for r in (1, 0):
-        share = nn(mixed[r][1], out_all).astype(bf16)
-        shares = [share[:even], share[even:]] + shares
-    middle = source + scatter_rows(*shares)
+    parts = [slice(0, even), slice(even, slots)]
+    shares = [nn(mixed[r][1][p], out_all).astype(bf16) for r in range(2) for p in parts]
+    mixer_out, stages = scatter_rows(*shares)
+    middle = source + mixer_out
     rate_last = inverse_rms(middle)
-    rows_upstream = jnp.concatenate(gather_rows(upstream_low), axis=0)
-    rows_second = jnp.concatenate(
-        gather_rows((middle * rate_last * gain_last).astype(bf16)), axis=0
+    rows_upstream = jnp.concatenate(upstream_own + upstream_other, axis=0)
+    (second_own, second_other), second_stages = gather_rows(
+        (middle * rate_last * gain_last).astype(bf16)
+    )
+    rows_second = jnp.concatenate(second_own + second_other, axis=0)
+    down_pieces, last = gather_ring(w_down.T, tokens=last, later=stages[0])
+    gate_pieces, last = gather_ring(w_gate.T, tokens=last + stages[1], later=stages[2])
+    up_pieces, last = gather_ring(
+        w_up.T, tokens=last + second_stages[0], later=second_stages[1]
     )
 
     gate_up = jnp.concatenate(gate_pieces + up_pieces, axis=0)
     down_all = jnp.concatenate(down_pieces, axis=0)
+    d_hidden = nt(down_all, rows_upstream)
     pre = nt(gate_up, rows_second)
     gate_pre, up_pre = pre[:hidden_units], pre[hidden_units:]
     sig = jax.nn.sigmoid(gate_pre)
     silu = gate_pre * sig
     hidden = (silu * up_pre).astype(bf16)
-    d_hidden = nt(down_all, rows_upstream)
     d_gate = (d_hidden * up_pre * sig * (1.0 + gate_pre * (1.0 - sig))).astype(bf16)
     d_up = (d_hidden * silu).astype(bf16)
     d_pre = jnp.concatenate([d_gate, d_up], axis=0)
-    shares = []
-    for r in (1, 0):
-        share = tn(d_pre[:, r * slots : (r + 1) * slots], gate_up).astype(bf16)
-        shares = [share[:even], share[even:]] + shares
-    d_second = scatter_rows(*shares)
+    grad_down = nn(hidden, rows_upstream).astype(bf16)
+    d_pre, *_ = after([d_pre], [grad_down])
+    parts = [slice(p, p + even) for p in range(0, 2 * slots, even)]
+    shares = [tn(d_pre[:, p], gate_up).astype(bf16) for p in parts]
+    d_second, stages = scatter_rows(*shares)
     upstream = upstream_low.astype(f32)
     d_middle = upstream + norm_back(middle, rate_last, gain_last, d_second)
-    rows_dmiddle = gather_rows(d_middle.astype(bf16))
-    rows_dmiddle = [
-        jnp.concatenate(rows_dmiddle[:2], axis=0),
-        jnp.concatenate(rows_dmiddle[2:], axis=0),
-    ]
-    down_share = scatter_ring(nn(hidden, rows_upstream).astype(bf16))
-    grad_pre = nn(d_pre, rows_second).astype(bf16)
-    gate_share = scatter_ring(grad_pre[:hidden_units])
-    up_share = scatter_ring(grad_pre[hidden_units:])
-    shares = []
-    for r in (1, 0):
-        share = tn(hidden[:, r * slots : (r + 1) * slots], down_all).astype(bf16)
-        shares = [share[:even], share[even:]] + shares
-    block_output = (middle + scatter_rows(*shares)).astype(bf16)
+    (middle_own, middle_other), middle_stages = gather_rows(d_middle.astype(bf16))
+    rows_dmiddle = [jnp.concatenate(middle_own, axis=0), jnp.concatenate(middle_other, axis=0)]
+    down_share, last = scatter_ring(grad_down, later=stages[1])
+    [d_gate] = after([d_gate], stages[0])
+    [d_up] = after([d_up], stages[1])
+    grad_pre = jnp.stack([nn(d, rows_second).astype(bf16) for d in (d_gate, d_up)])
+    pre_share, last = scatter_ring(
+        grad_pre, axis=1, tokens=list(last) + stages[2], later=middle_stages[1]
+    )
+    [hidden] = after([hidden], [shares[1], shares[3]])
+    down_shares = [tn(hidden[:, p], down_all).astype(bf16) for p in parts]
+    down_out, _ = scatter_rows(*down_shares, tokens=middle_stages[1])
+    block_output = (middle + down_out).astype(bf16)
     grad_gain_two = jnp.sum(d_second * middle * rate_last, axis=0)
 
-    grad_out, grad_in, d_filter, d_taps = 0.0, 0.0, 0.0, 0.0
-    shares, grad_gain_one = [], 0.0
-    for r in (1, 0):
+    halves = (slice(0, even), slice(even, slots))
+    shares, d_rows, grad_gain_one, d_filter, d_taps = [None, None], [None, None], 0.0, 0.0, 0.0
+    for r in range(2):
         proj, gated, long_out, seen = mixed[r]
         table, first = tables[r]
         d_gated = nt(rows_dmiddle[r], out_all).reshape(narrow, local_rows, channels)
-        grad_out = grad_out + tn(gated, rows_dmiddle[r])
         dz, d_filter_row, d_taps_row = mixer_backward(
             order, first, documents[r][0], proj, d_gated, long_out, seen, taps, table,
             spectrum, fwd, inv,
         )
-        dz = dz.reshape(slots, 3 * channels)
+        d_rows[r] = dz.reshape(slots, 3 * channels)
         d_filter, d_taps = d_filter + d_filter_row, d_taps + d_taps_row
-        share = nn(dz, in_all).astype(bf16)
-        shares = [share[:even], share[even:]] + shares
-        grad_gain_one = grad_gain_one + jnp.sum(
-            share.astype(f32) * rows_first[r].astype(f32), axis=0
-        )
-        grad_in = grad_in + tn(dz, rows_first[r])
-    d_normed = scatter_rows(*shares)
+        shares[r] = [nn(d_rows[r][p], in_all).astype(bf16) for p in halves]
+        for n, share in enumerate(shares[r]):
+            rows = rows_first[r][n * even : (n + 1) * even]
+            grad_gain_one = grad_gain_one + jnp.sum(share.astype(f32) * rows.astype(f32), axis=0)
+    d_normed, stages = scatter_rows(*shares[0], *shares[1])
     input_grad = (d_middle + norm_back(source, rate_first, gain_first, d_normed)).astype(bf16)
-    out_share = scatter_ring(grad_out.astype(bf16))
-    in_share = scatter_ring(grad_in.astype(bf16).reshape(3, channels, width), axis=1)
+    done = shares[0] + shares[1]
+    d_rows = after(d_rows, done)
+    grad_in = sum(tn(d_rows[r], rows_first[r]) for r in range(2)).astype(bf16)
+    d_filter, *_ = after([d_filter], [grad_in])
+    gated = after([mixed[0][1], mixed[1][1]], stages[1])
+    grad_out = sum(tn(gated[r], rows_dmiddle[r]) for r in range(2)).astype(bf16)
+    in_share, last = scatter_ring(
+        grad_in.reshape(3, channels, width), axis=1, tokens=list(last) + stages[0]
+    )
+    out_share, _ = scatter_ring(grad_out, tokens=last)
+    gain_grads = after([jnp.stack([grad_gain_one / gain_first, grad_gain_two])], stages[1])
+    gain_share = reduce_gain(gain_grads[0])
 
     sum_re, sum_im, mom_re, mom_im = filter_moments(d_filter, step_re, step_im)
     full_re = lag * sum_re + 8.0 * mom_re
@@ -708,7 +753,8 @@
         ],
         axis=0,
     ).astype(bf16)
-    small_share = scatter_ring(small_grad, axis=1, halves=False)
+    [small_grad] = after([small_grad], stages[1])
+    small_share, _ = scatter_ring(small_grad, axis=1, halves=False)
 
     at = 9 + poles
     return (
@@ -716,14 +762,14 @@
         input_grad[None],
         in_share.transpose(0, 2, 1),
         out_share,
-        reduce_gain(grad_gain_one / gain_first),
+        gain_share[0],
         small_share[:9].reshape(3, 3, own),
         small_share[9:at].T,
         small_share[at : at + poles].T,
         small_share[at + poles :].T,
-        reduce_gain(grad_gain_two),
-        gate_share.T,
-        up_share.T,
+        gain_share[1],
+        pre_share[0].T,
+        pre_share[1].T,
         down_share.T,
     )
 

time: 853 us -> 742 us (0.87)
  waiting for transfers between devices: 342 us -> 267 us
  starting transfers between devices: 127 us -> 101 us
  matrix products: 151 us -> 138 us
    ppermute x58 -> x63, waiting for transfers between devices: 186 us -> 60.3 us  [swap(): return lax.ppermute(values, axis, [(i, i ^ shift) for i in range(size)])]
    ppermute x52 -> x45, waiting for transfers between devices: 156 us -> 207 us  [along(): return lax.ppermute(values, 'wide', pairs)]
    ppermute x52 -> x45, starting transfers between devices: 75.6 us -> 56.9 us  [along(): return lax.ppermute(values, 'wide', pairs)]
    dot_general x8 -> x12, matrix products: 56.1 us -> 47.1 us  [tn(): lax.dot_general(a, b, (((0,), (0,)), ((), ())), preferred_element_type=f32)]
    ppermute x58 -> x63, starting transfers between devices: 50.9 us -> 43.7 us  [swap(): return lax.ppermute(values, axis, [(i, i ^ shift) for i in range(size)])]
    concatenate x17 -> x13, other arithmetic: 17.6 us -> 13.4 us  [the longest x1 7.05 us: body(): d_pre = jnp.concatenate([d_gate, d_up], axis=0)]
    dot_general x6 -> x11, matrix products: 44.7 us -> 44.4 us  [nn(): lax.dot_general(a, b, (((1,), (0,)), ((), ())), preferred_element_type=f32)]
    unnamed x212 -> x252, local copies, waits for them, and re-layouts: 41.1 us -> 40.9 us
  transfers between devices with their start and end apart: 110 -> 108, of which waited for: 47 -> 35; matrix products, arithmetic and copies ran while one was open for 24% -> 29% of each run, Pallas kernels for 7% -> 7%
where the time goes in v3:
time: 742 us; the launch traced here: 734 us
  waiting for transfers between devices  267 us (36%)
  matrix products  138 us (19%)
  starting transfers between devices  101 us (14%)
  other arithmetic  87 us (12%)
  local copies, waits for them, and re-layouts  79.6 us (11%)
  Pallas kernels  58.4 us (8%)
    ppermute x45, waiting for transfers between devices, along(): return lax.ppermute(values, 'wide', pairs)  207 us
    ppermute x63, waiting for transfers between devices, swap(): return lax.ppermute(values, axis, [(i, i ^ shift) for i in range(size)])  60.3 us
    ppermute x45, starting transfers between devices, along(): return lax.ppermute(values, 'wide', pairs)  56.9 us
    dot_general x12, matrix products, tn(): lax.dot_general(a, b, (((0,), (0,)), ((), ())), preferred_element_type=f32)  47.1 us
    dot_general x11, matrix products, nn(): lax.dot_general(a, b, (((1,), (0,)), ((), ())), preferred_element_type=f32)  44.4 us
    ppermute x63, starting transfers between devices, swap(): return lax.ppermute(values, axis, [(i, i ^ shift) for i in range(size)])  43.7 us
    dot_general x6, matrix products, nt(): lax.dot_general(a, b, (((1,), (1,)), ((), ())), preferred_element_type=f32)  42.6 us
    unnamed x252, local copies, waits for them, and re-layouts  40.9 us
  transfers between devices with their start and end apart: 108, of which 35 were waited for; matrix products, arithmetic and copies ran while one was open for 29% of the time, Pallas kernels for 7%

profile of v3, /device:TPU:0, one launch (start us, length us, event | category | flops | bytes accessed | tf_op | source)
XLA Modules:
  0.0 733.7 jit_solution(2298994619328645938)
XLA Ops:
  0.6 3.0 collective-permute-start
  5.9 3.1 concatenate.173
  25.7 7.5 %collective-permute-done.6 = bf16[75,64]{1,0:T(8,128)(2,1)S(1)} collective-permute-done((bf16[75,64]{1,0:T(8,128)(2,1)S(1)}, bf16[75,64]{1,0:T(8,128)(2,1)S(1)}, u32[]{:S(2)}, u32[]{:S(2)}) %collective-permute-start.6) | collective-permute-done | bytes 9632 | tf_op jit(solution)/shard_map/ppermute | solution.py:64
  36.5 4.1 taps.1
  40.5 3.5 fusion.89.spectrum
  44.0 5.9 collective-permute-done.11
  70.2 10.4 %collective-permute-done.8 = bf16[2,2,4,64]{3,2,1,0:T(4,128)(2,1)S(1)} collective-permute-done((bf16[2,2,4,64]{3,2,1,0:T(4,128)(2,1)S(1)}, bf16[2,2,4,64]{3,2,1,0:T(4,128)(2,1)S(1)}, u32[]{:S(2)}, u32[]{:S(2)}) %collective-permute-start.8) | collective-permute-done | bytes 2080 | tf_op jit(solution)/shard_map/ppermute | solution.py:42
  97.5 3.0 fusion
  103.8 8.9 %fusion.5 = (bf16[1024,2048]{1,0:T(8,128)(2,1)S(1)}, bf16[1024,2048]{1,0:T(8,128)(2,1)S(1)}) fusion(bf16[1024,2048]{1,0:T(8,128)(2,1)S(1)} %constant_dynamic-update-slice_fusion.10, f32[1024]{0:T(1024)S(1)} %add_rsqrt_fusion, f32[2048]{0:T(1024)S(1)} %mul.468, f32[1024]{0:T(1024)S(1)} %add_rsqrt_fusion.1, bf16[256,2048]{1,0:T(8,128)(2,1)S(1)} %collective-permute-done.3, ...), kind=kLoop, calls=%fused_computation.9 | loop fusion | flops 31457280 | bytes 16793600 | tf_op jit(solution)/shard_map/convert_element_type | solution.py:611
  114.7 3.5 fusion.90.proj
  118.2 3.5 fusion.88.proj
  127.5 7.1 mixer_forward.3
  136.5 4.3 collective-permute-done.20
  143.3 3.6 collective-permute-done.21
  150.1 7.1 mixer_forward.2
  169.6 11.6 %collective-permute-done.26 = bf16[128,2048]{1,0:T(8,128)(2,1)S(1)} collective-permute-done((bf16[128,2048]{1,0:T(8,128)(2,1)S(1)}, bf16[128,2048]{1,0:T(8,128)(2,1)S(1)}, u32[]{:S(2)}, u32[]{:S(2)}) %collective-permute-start.26) | collective-permute-done | bytes 524320 | tf_op jit(solution)/shard_map/ppermute | solution.py:42
  182.7 11.4 %collective-permute-done.25 = bf16[128,2048]{1,0:T(8,128)(2,1)S(1)} collective-permute-done((bf16[128,2048]{1,0:T(8,128)(2,1)S(1)}, bf16[128,2048]{1,0:T(8,128)(2,1)S(1)}, u32[]{:S(2)}, u32[]{:S(2)}) %collective-permute-start.25) | collective-permute-done | bytes 524320 | tf_op jit(solution)/shard_map/ppermute | solution.py:42
  202.1 14.6 %collective-permute-done.32 = bf16[80,2048]{1,0:T(8,128)(2,1)S(1)} collective-permute-done((bf16[80,2048]{1,0:T(8,128)(2,1)S(1)}, bf16[80,2048]{1,0:T(8,128)(2,1)S(1)}, u32[]{:S(2)}, u32[]{:S(2)}) %collective-permute-start.32) | collective-permute-done | bytes 327712 | tf_op jit(solution)/shard_map/ppermute | solution.py:64
  223.3 12.8 %collective-permute-done.33 = bf16[176,2048]{1,0:T(8,128)(2,1)S(1)} collective-permute-done((bf16[176,2048]{1,0:T(8,128)(2,1)S(1)}, bf16[176,2048]{1,0:T(8,128)(2,1)S(1)}, u32[]{:S(2)}, u32[]{:S(2)}) %collective-permute-start.33) | collective-permute-done | bytes 720928 | tf_op jit(solution)/shard_map/ppermute | solution.py:64
  236.2 14.1 %collective-permute-done.34 = bf16[176,2048]{1,0:T(8,128)(2,1)S(1)} collective-permute-done((bf16[176,2048]{1,0:T(8,128)(2,1)S(1)}, bf16[176,2048]{1,0:T(8,128)(2,1)S(1)}, u32[]{:S(2)}, u32[]{:S(2)}) %collective-permute-start.34) | collective-permute-done | bytes 720928 | tf_op jit(solution)/shard_map/ppermute | solution.py:64
  253.3 9.0 %collective-permute-done.35 = bf16[96,2048]{1,0:T(8,128)(2,1)S(1)} collective-permute-done((bf16[96,2048]{1,0:T(8,128)(2,1)S(1)}, bf16[96,2048]{1,0:T(8,128)(2,1)S(1)}, u32[]{:S(2)}, u32[]{:S(2)}) %collective-permute-start.35) | collective-permute-done | bytes 393248 | tf_op jit(solution)/shard_map/ppermute | solution.py:64
  263.9 4.9 collective-permute-done.36
  274.7 13.6 %collective-permute-done.39 = bf16[176,2048]{1,0:T(8,128)(2,1)S(1)} collective-permute-done((bf16[176,2048]{1,0:T(8,128)(2,1)S(1)}, bf16[176,2048]{1,0:T(8,128)(2,1)S(1)}, u32[]{:S(2)}, u32[]{:S(2)}) %collective-permute-start.39) | collective-permute-done | bytes 720928 | tf_op jit(solution)/shard_map/ppermute | solution.py:64
  288.3 14.1 %collective-permute-done.40 = bf16[176,2048]{1,0:T(8,128)(2,1)S(1)} collective-permute-done((bf16[176,2048]{1,0:T(8,128)(2,1)S(1)}, bf16[176,2048]{1,0:T(8,128)(2,1)S(1)}, u32[]{:S(2)}, u32[]{:S(2)}) %collective-permute-start.40) | collective-permute-done | bytes 720928 | tf_op jit(solution)/shard_map/ppermute | solution.py:64
  311.2 3.2 collective-permute-done.43
  314.4 6.5 collective-permute-done.44
  323.7 17.5 %fusion.91 = f32[1408,2048]{1,0:T(8,128)} fusion(bf16[1408,2048]{1,0:T(8,128)(2,1)S(1)} %constant_dynamic-update-slice_fusion.15, bf16[2048,2048]{1,0:T(8,128)(2,1)} %constant_dynamic-update-slice_fusion.25), kind=kOutput, calls=%fused_computation.356 | convolution fusion | flops 11811160064 | bytes 25690112 | tf_op jit(solution)/shard_map/dot_general | solution.py:33
  341.2 15.6 %multiply_convert_fusion.1 = (bf16[704,2048]{1,0:T(8,128)(2,1)}, bf16[704,2048]{1,0:T(8,128)(2,1)}, bf16[704,2048]{1,0:T(8,128)(2,1)}) fusion(f32[1408,2048]{1,0:T(8,128)} %fusion.91, bf16[704,2048]{1,0:T(8,128)(2,1)S(1)} %copy-done.81, bf16[2048,2048]{1,0:T(8,128)(2,1)} %constant_dynamic-update-slice_fusion.39), kind=kOutput, calls=%fused_computation.13 | convolution fusion | flops 5927206912 | bytes 31457280 | tf_op jit(solution)/shard_map/dot_general | solution.py:33
  356.8 9.6 %convolution_convert_fusion.2 = bf16[704,2048]{1,0:T(8,128)(2,1)S(1)} fusion(bf16[704,2048]{1,0:T(8,128)(2,1)} %get-tuple-element.121, bf16[2048,2048]{1,0:T(8,128)(2,1)} %constant_dynamic-update-slice_fusion.39), kind=kOutput, calls=%fused_computation.39 | convolution fusion | flops 5907021824 | bytes 14155776 | tf_op jit(solution)/shard_map/dot_general | solution.py:29
  366.6 7.1 pad_maximum_fusion
  373.6 6.7 convolution_convert_fusion.17
  380.4 4.8 convolution_convert_fusion.18
  391.7 4.3 convolution_convert_fusion.14
  396.0 3.1 collective-permute-start.83
  399.2 4.3 convolution_convert_fusion.13
  403.5 12.0 %collective-permute-done.84 = bf16[80,2048]{1,0:T(8,128)(2,1)S(1)} collective-permute-done((bf16[80,2048]{1,0:T(8,128)(2,1)S(1)}, bf16[80,2048]{1,0:T(8,128)(2,1)S(1)}, u32[]{:S(2)}, u32[]{:S(2)}) %collective-permute-start.84) | collective-permute-done | bytes 327712 | tf_op jit(solution)/shard_map/ppermute | solution.py:64
  420.7 3.6 fusion.87
  427.6 3.7 convert_add_fusion.3
  431.3 8.7 %fusion.9 = bf16[1,704,2048]{2,1,0:T(8,128)(2,1)S(1)} fusion(bf16[704,2048]{1,0:T(8,128)(2,1)S(1)} %copy-done.49, bf16[2048,2048]{1,0:T(8,128)(2,1)} %constant_dynamic-update-slice_fusion.25), kind=kOutput, calls=%fused_computation.56 | convolution fusion | flops 5907021824 | bytes 14155776 | tf_op jit(solution)/shard_map/dot_general | solution.py:29
  440.1 3.3 convert_add_fusion.5
  451.5 8.6 %fusion.10 = bf16[1,704,2048]{2,1,0:T(8,128)(2,1)S(1)} fusion(bf16[704,2048]{1,0:T(8,128)(2,1)S(1)} %copy-done.48, bf16[2048,2048]{1,0:T(8,128)(2,1)} %constant_dynamic-update-slice_fusion.25), kind=kOutput, calls=%fused_computation.57 | convolution fusion | flops 5907021824 | bytes 14155776 | tf_op jit(solution)/shard_map/dot_general | solution.py:29
  460.3 3.4 collective-permute-done.85
  463.7 14.7 %collective-permute-done.86 = bf16[176,2048]{1,0:T(8,128)(2,1)S(1)} collective-permute-done((bf16[176,2048]{1,0:T(8,128)(2,1)}, bf16[176,2048]{1,0:T(8,128)(2,1)S(1)}, u32[]{:S(2)}, u32[]{:S(2)}) %collective-permute-start.86) | collective-permute-done | bytes 720928 | tf_op jit(solution)/shard_map/ppermute | solution.py:64
  479.8 3.7 fusion.69
  490.5 22.4 %collective-permute-done.88 = bf16[2,80,2048]{2,1,0:T(8,128)(2,1)S(1)} collective-permute-done((bf16[2,80,2048]{2,1,0:T(8,128)(2,1)S(1)}, bf16[2,80,2048]{2,1,0:T(8,128)(2,1)S(1)}, u32[]{:S(2)}, u32[]{:S(2)}) %collective-permute-start.88) | collective-permute-done | bytes 655392 | tf_op jit(solution)/shard_map/ppermute | solution.py:64
  518.0 8.6 %collective-permute-done.66 = bf16[128,2048]{1,0:T(8,128)(2,1)S(1)} collective-permute-done((bf16[128,2048]{1,0:T(8,128)(2,1)S(1)}, bf16[128,2048]{1,0:T(8,128)(2,1)S(1)}, u32[]{:S(2)}, u32[]{:S(2)}) %collective-permute-start.66) | collective-permute-done | bytes 524320 | tf_op jit(solution)/shard_map/ppermute | solution.py:42
  532.9 15.8 %mixer_backward.2 = (bf16[4,256,768]{2,1,0:T(8,128)(2,1)}, f32[512,256]{1,0:T(8,128)S(1)}, f32[8,768]{1,0:T(8,128)S(1)}) custom-call(s32[4]{0:T(128)S(1)} %copy-done.12, s32[3]{0:T(128)S(1)} %copy-done.16, s32[3]{0:T(128)S(1)} %copy-done.20, f32[4,256,768]{2,1,0:T(8,128)} %copy-done.4, f32[4,256,256]{2,1,0:T(8,128)S(1)} %bitcast.194, ...), custom_call_target="tpu_custom_call" | custom-call | flops 2013265920 | bytes 8388608 | tf_op jit(solution)/shard_map/mixer_backward/pallas_call | solution.py:484
  553.2 3.2 convolution_convert_fusion.9
  557.4 7.5 %collective-permute-done.69 = bf16[128,2048]{1,0:T(8,128)(2,1)S(1)} collective-permute-done((bf16[128,2048]{1,0:T(8,128)(2,1)S(1)}, bf16[128,2048]{1,0:T(8,128)(2,1)S(1)}, u32[]{:S(2)}, u32[]{:S(2)}) %collective-permute-start.69) | collective-permute-done | bytes 524320 | tf_op jit(solution)/shard_map/ppermute | solution.py:42
  571.7 16.3 %mixer_backward.3 = (bf16[4,256,768]{2,1,0:T(8,128)(2,1)}, f32[512,256]{1,0:T(8,128)S(1)}, f32[8,768]{1,0:T(8,128)S(1)}) custom-call(s32[4]{0:T(128)S(1)} %copy-done.12, s32[3]{0:T(128)S(1)} %copy-done.14, s32[3]{0:T(128)S(1)} %copy-done.18, f32[4,256,768]{2,1,0:T(8,128)} %copy-done.3, f32[4,256,256]{2,1,0:T(8,128)S(1)} %bitcast.193, ...), custom_call_target="tpu_custom_call" | custom-call | flops 2013265920 | bytes 8388608 | tf_op jit(solution)/shard_map/mixer_backward/pallas_call | solution.py:484
  598.7 3.6 fusion.37
  602.3 5.0 multiply_reduce_fusion.1
  607.4 4.6 fusion.8
  612.1 3.5 fusion.93
  615.6 5.1 add_convert_fusion
  620.7 8.0 %moments.1 = (f32[16,8,256]{2,1,0:T(8,128)}, f32[16,8,256]{2,1,0:T(8,128)}, f32[16,8,256]{2,1,0:T(8,128)}, f32[16,8,256]{2,1,0:T(8,128)}) custom-call(f32[512,256]{1,0:T(8,128)} %add.365.grad, f32[16,8,256]{2,1,0:T(8,128)} %broadcast_in_dim.201.step_re, f32[16,8,256]{2,1,0:T(8,128)} %broadcast_in_dim.202.step_im), custom_call_target="tpu_custom_call" | custom-call | flops 31457280 | bytes 524288 | tf_op jit(solution)/shard_map/moments/pallas_call | solution.py:276
  638.8 6.5 collective-permute-done.91
  645.3 9.4 %collective-permute-done.92 = bf16[3,32,2048]{2,1,0:T(8,128)(2,1)} collective-permute-done((bf16[3,32,2048]{2,1,0:T(8,128)(2,1)S(1)}, bf16[3,32,2048]{2,1,0:T(8,128)(2,1)}, u32[]{:S(2)}, u32[]{:S(2)}) %collective-permute-start.92) | collective-permute-done | bytes 393248 | tf_op jit(solution)/shard_map/ppermute | solution.py:64
  662.0 3.6 fusion.94
  681.5 13.2 %collective-permute-done.102 = f32[1,2,64]{2,0,1:T(1,128)S(1)} collective-permute-done((f32[1,2,64]{2,0,1:T(1,128)S(1)}, f32[1,2,64]{2,0,1:T(1,128)S(1)}, u32[]{:S(2)}, u32[]{:S(2)}) %collective-permute-start.102) | collective-permute-done | bytes 544 | tf_op jit(solution)/shard_map/ppermute | solution.py:64
  708.4 3.1 add_bitcast_fusion
  711.5 5.9 collective-permute-done.96
  720.6 4.0 collective-permute-done.82
  730.1 3.1 fusion.38
  (627 shorter events, 248.7 us)
Async XLA Ops:
  0.6 59.0 %collective-permute-start = (bf16[256,2048]{1,0:T(8,128)(2,1)}, bf16[256,2048]{1,0:T(8,128)(2,1)S(1)}, u32[]{:S(2)}, u32[]{:S(2)}) collective-permute-start(bf16[256,2048]{1,0:T(8,128)(2,1)} %bitcast.199), channel_id=1, source_target_pairs={{0,2},{1,3},{2,0},{3,1},{4,6},{5,7},{6,4},{7,5},{8,10},{9,11},{10,... | collective-permute-start | bytes 3145736 | tf_op jit(solution)/shard_map/ppermute | solution.py:42
  3.7 56.0 %collective-permute-start.1 = (bf16[256,2048]{1,0:T(8,128)(2,1)}, bf16[256,2048]{1,0:T(8,128)(2,1)}, u32[]{:S(2)}, u32[]{:S(2)}) collective-permute-start(bf16[256,2048]{1,0:T(8,128)(2,1)} %bitcast.200), channel_id=1, source_target_pairs={{0,4},{4,0},{8,12},{12,8},{16,20},{20,16},{24,28},{28,24},{1,5},{5... | collective-permute-start | bytes 3145736 | tf_op jit(solution)/shard_map/ppermute | solution.py:42
  11.6 32.4 %collective-permute-start.10 = (bf16[3,64,2048]{2,1,0:T(8,128)(2,1)}, bf16[3,64,2048]{2,1,0:T(8,128)(2,1)}, u32[]{:S(2)}, u32[]{:S(2)}) collective-permute-start(bf16[3,64,2048]{2,1,0:T(8,128)(2,1)} %bitcast.215), channel_id=1, source_target_pairs={{0,16},{4,20},{16,24},{20,28},{24,8},{28,12},{8,0},{12,4},{1,17},{... | collective-permute-start | bytes 2359304 | tf_op jit(solution)/shard_map/ppermute | solution.py:64
  24.3 25.6 %collective-permute-start.11 = (bf16[3,64,2048]{2,1,0:T(8,128)(2,1)}, bf16[3,64,2048]{2,1,0:T(8,128)(2,1)}, u32[]{:S(2)}, u32[]{:S(2)}) collective-permute-start(bf16[3,64,2048]{2,1,0:T(8,128)(2,1)} %bitcast.216), channel_id=1, source_target_pairs={{0,8},{4,12},{16,0},{20,4},{24,16},{28,20},{8,24},{12,28},{1,9},{5... | collective-permute-start | bytes 2359304 | tf_op jit(solution)/shard_map/ppermute | solution.py:64
  51.6 33.4 %collective-permute-start.12 = (bf16[3,32,2048]{2,1,0:T(8,128)(2,1)}, bf16[3,32,2048]{2,1,0:T(8,128)(2,1)}, u32[]{:S(2)}, u32[]{:S(2)}) collective-permute-start(bf16[3,32,2048]{2,1,0:T(8,128)(2,1)} %slice.479), channel_id=1, source_target_pairs={{0,16},{4,20},{16,24},{20,28},{24,8},{28,12},{8,0},{12,4},{1,17},{... | collective-permute-start | bytes 1179656 | tf_op jit(solution)/shard_map/ppermute | solution.py:64
  54.0 33.0 %collective-permute-start.13 = (bf16[3,32,2048]{2,1,0:T(8,128)(2,1)}, bf16[3,32,2048]{2,1,0:T(8,128)(2,1)}, u32[]{:S(2)}, u32[]{:S(2)}) collective-permute-start(bf16[3,32,2048]{2,1,0:T(8,128)(2,1)} %slice.480), channel_id=1, source_target_pairs={{0,8},{4,12},{16,0},{20,4},{24,16},{28,20},{8,24},{12,28},{1,9},{5... | collective-permute-start | bytes 1179656 | tf_op jit(solution)/shard_map/ppermute | solution.py:64
  63.0 26.4 %collective-permute-start.15 = (bf16[128,2048]{1,0:T(8,128)(2,1)}, bf16[128,2048]{1,0:T(8,128)(2,1)}, u32[]{:S(2)}, u32[]{:S(2)}) collective-permute-start(bf16[128,2048]{1,0:T(8,128)(2,1)} %slice.621), channel_id=1, source_target_pairs={{0,4},{4,0},{8,12},{12,8},{16,20},{20,16},{24,28},{28,24},{1,5},{5... | collective-permute-start | bytes 1572872 | tf_op jit(solution)/shard_map/ppermute | solution.py:42
  67.7 21.7 %collective-permute-start.16 = (bf16[128,2048]{1,0:T(8,128)(2,1)}, bf16[128,2048]{1,0:T(8,128)(2,1)}, u32[]{:S(2)}, u32[]{:S(2)}) collective-permute-start(bf16[128,2048]{1,0:T(8,128)(2,1)} %slice.622), channel_id=1, source_target_pairs={{0,2},{1,3},{2,0},{3,1},{4,6},{5,7},{6,4},{7,5},{8,10},{9,11},{10,... | collective-permute-start | bytes 1572872 | tf_op jit(solution)/shard_map/ppermute | solution.py:42
  90.8 30.9 %collective-permute-start.49 = (bf16[256,2048]{1,0:T(8,128)(2,1)}, bf16[256,2048]{1,0:T(8,128)(2,1)}, u32[]{:S(2)}, u32[]{:S(2)}) collective-permute-start(bf16[256,2048]{1,0:T(8,128)(2,1)} %bitcast.40), channel_id=1, source_target_pairs={{0,2},{1,3},{2,0},{3,1},{4,6},{5,7},{6,4},{7,5},{8,10},{9,11},{10,... | collective-permute-start | bytes 3145736 | tf_op jit(solution)/shard_map/ppermute | solution.py:42
  96.0 25.7 %collective-permute-start.50 = (bf16[256,2048]{1,0:T(8,128)(2,1)}, bf16[256,2048]{1,0:T(8,128)(2,1)S(1)}, u32[]{:S(2)}, u32[]{:S(2)}) collective-permute-start(bf16[256,2048]{1,0:T(8,128)(2,1)} %bitcast.40), channel_id=1, source_target_pairs={{0,4},{4,0},{8,12},{12,8},{16,20},{20,16},{24,28},{28,24},{1,5},{5... | collective-permute-start | bytes 3145736 | tf_op jit(solution)/shard_map/ppermute | solution.py:42
  100.6 34.1 %collective-permute-start.18 = (bf16[64,2048]{1,0:T(8,128)(2,1)S(1)}, bf16[64,2048]{1,0:T(8,128)(2,1)S(1)}, u32[]{:S(2)}, u32[]{:S(2)}) collective-permute-start(bf16[64,2048]{1,0:T(8,128)(2,1)S(1)} %copy-done.75), channel_id=1, source_target_pairs={{0,16},{4,20},{16,24},{20,28},{24,8},{28,12},{8,0},{12,4},{1,17},{... | collective-permute-start | bytes 786440 | tf_op jit(solution)/shard_map/ppermute | solution.py:64
  101.8 33.0 %collective-permute-start.19 = (bf16[64,2048]{1,0:T(8,128)(2,1)S(1)}, bf16[64,2048]{1,0:T(8,128)(2,1)S(1)}, u32[]{:S(2)}, u32[]{:S(2)}) collective-permute-start(bf16[64,2048]{1,0:T(8,128)(2,1)S(1)} %copy-done.75), channel_id=1, source_target_pairs={{0,8},{4,12},{16,0},{20,4},{24,16},{28,20},{8,24},{12,28},{1,9},{5... | collective-permute-start | bytes 786440 | tf_op jit(solution)/shard_map/ppermute | solution.py:64
  121.7 38.1 %collective-permute-start.51 = (bf16[256,2048]{1,0:T(8,128)(2,1)}, bf16[256,2048]{1,0:T(8,128)(2,1)S(1)}, u32[]{:S(2)}, u32[]{:S(2)}) collective-permute-start(bf16[256,2048]{1,0:T(8,128)(2,1)} %bitcast.40), channel_id=1, source_target_pairs={{0,1},{1,0},{2,3},{3,2},{4,5},{5,4},{6,7},{7,6},{8,9},{9,8},{10,11... | collective-permute-start | bytes 3145736 | tf_op jit(solution)/shard_map/ppermute | solution.py:42
  124.1 34.0 %collective-permute-start.53 = (bf16[128,2048]{1,0:T(8,128)(2,1)}, bf16[128,2048]{1,0:T(8,128)(2,1)S(1)}, u32[]{:S(2)}, u32[]{:S(2)}) collective-permute-start(bf16[128,2048]{1,0:T(8,128)(2,1)} %slice.635), channel_id=1, source_target_pairs={{0,4},{4,0},{8,12},{12,8},{16,20},{20,16},{24,28},{28,24},{1,5},{5... | collective-permute-start | bytes 1572872 | tf_op jit(solution)/shard_map/ppermute | solution.py:42
  126.0 33.7 %collective-permute-start.54 = (bf16[128,2048]{1,0:T(8,128)(2,1)}, bf16[128,2048]{1,0:T(8,128)(2,1)S(1)}, u32[]{:S(2)}, u32[]{:S(2)}) collective-permute-start(bf16[128,2048]{1,0:T(8,128)(2,1)} %slice.636), channel_id=1, source_target_pairs={{0,2},{1,3},{2,0},{3,1},{4,6},{5,7},{6,4},{7,5},{8,10},{9,11},{10,... | collective-permute-start | bytes 1572872 | tf_op jit(solution)/shard_map/ppermute | solution.py:42
  134.7 27.9 %collective-permute-start.52 = (bf16[256,2048]{1,0:T(8,128)(2,1)}, bf16[256,2048]{1,0:T(8,128)(2,1)}, u32[]{:S(2)}, u32[]{:S(2)}) collective-permute-start(bf16[256,2048]{1,0:T(8,128)(2,1)} %collective-permute-done.49), channel_id=1, source_target_pairs={{0,1},{1,0},{2,3},{3,2},{4,5},{5,4},{6,7},{7,6},{8,9},{9,8},{10,11... | collective-permute-start | bytes 3145736 | tf_op jit(solution)/shard_map/ppermute | solution.py:42
  159.2 35.7 %collective-permute-start.55 = (bf16[256,2048]{1,0:T(8,128)(2,1)S(1)}, bf16[256,2048]{1,0:T(8,128)(2,1)S(1)}, u32[]{:S(2)}, u32[]{:S(2)}) collective-permute-start(bf16[256,2048]{1,0:T(8,128)(2,1)S(1)} %copy-done.51), channel_id=1, source_target_pairs={{0,1},{1,0},{2,3},{3,2},{4,5},{5,4},{6,7},{7,6},{8,9},{9,8},{10,11... | collective-permute-start | bytes 3145736 | tf_op jit(solution)/shard_map/ppermute | solution.py:42
  159.9 38.2 %collective-permute-start.29 = (bf16[176,2048]{1,0:T(8,128)(2,1)S(1)}, bf16[176,2048]{1,0:T(8,128)(2,1)S(1)}, u32[]{:S(2)}, u32[]{:S(2)}) collective-permute-start(bf16[176,2048]{1,0:T(8,128)(2,1)S(1)} %bitcast.222), channel_id=1, source_target_pairs={{0,16},{4,20},{16,24},{20,28},{24,8},{28,12},{8,0},{12,4},{1,17},{... | collective-permute-start | bytes 2162696 | tf_op jit(solution)/shard_map/ppermute | solution.py:64
  162.6 35.5 %collective-permute-start.30 = (bf16[176,2048]{1,0:T(8,128)(2,1)S(1)}, bf16[176,2048]{1,0:T(8,128)(2,1)S(1)}, u32[]{:S(2)}, u32[]{:S(2)}) collective-permute-start(bf16[176,2048]{1,0:T(8,128)(2,1)S(1)} %bitcast.223), channel_id=1, source_target_pairs={{0,8},{4,12},{16,0},{20,4},{24,16},{28,20},{8,24},{12,28},{1,9},{5... | collective-permute-start | bytes 2162696 | tf_op jit(solution)/shard_map/ppermute | solution.py:64
  168.8 32.2 %collective-permute-start.56 = (bf16[256,2048]{1,0:T(8,128)(2,1)S(1)}, bf16[256,2048]{1,0:T(8,128)(2,1)S(1)}, u32[]{:S(2)}, u32[]{:S(2)}) collective-permute-start(bf16[256,2048]{1,0:T(8,128)(2,1)S(1)} %pad_maximum_fusion.8), channel_id=1, source_target_pairs={{0,1},{1,0},{2,3},{3,2},{4,5},{5,4},{6,7},{7,6},{8,9},{9,8},{10,11... | collective-permute-start | bytes 3145736 | tf_op jit(solution)/shard_map/ppermute | solution.py:42
  194.3 24.5 %collective-permute-start.27 = (bf16[256,2048]{1,0:T(8,128)(2,1)S(1)}, bf16[256,2048]{1,0:T(8,128)(2,1)S(1)}, u32[]{:S(2)}, u32[]{:S(2)}) collective-permute-start(bf16[256,2048]{1,0:T(8,128)(2,1)S(1)} %pad_maximum_fusion.5), channel_id=1, source_target_pairs={{0,2},{1,3},{2,0},{3,1},{4,6},{5,7},{6,4},{7,5},{8,10},{9,11},{10,... | collective-permute-start | bytes 3145736 | tf_op jit(solution)/shard_map/ppermute | solution.py:42
  194.9 23.9 %collective-permute-start.28 = (bf16[256,2048]{1,0:T(8,128)(2,1)S(1)}, bf16[256,2048]{1,0:T(8,128)(2,1)S(1)}, u32[]{:S(2)}, u32[]{:S(2)}) collective-permute-start(bf16[256,2048]{1,0:T(8,128)(2,1)S(1)} %pad_maximum_fusion.6), channel_id=1, source_target_pairs={{0,4},{4,0},{8,12},{12,8},{16,20},{20,16},{24,28},{28,24},{1,5},{5... | collective-permute-start | bytes 3145736 | tf_op jit(solution)/shard_map/ppermute | solution.py:42
  216.8 19.4 %collective-permute-start.33 = (bf16[176,2048]{1,0:T(8,128)(2,1)S(1)}, bf16[176,2048]{1,0:T(8,128)(2,1)S(1)}, u32[]{:S(2)}, u32[]{:S(2)}) collective-permute-start(bf16[176,2048]{1,0:T(8,128)(2,1)S(1)} %bitcast.224), channel_id=1, source_target_pairs={{0,16},{4,20},{16,24},{20,28},{24,8},{28,12},{8,0},{12,4},{1,17},{... | collective-permute-start | bytes 2162696 | tf_op jit(solution)/shard_map/ppermute | solution.py:64
  217.4 32.9 %collective-permute-start.34 = (bf16[176,2048]{1,0:T(8,128)(2,1)S(1)}, bf16[176,2048]{1,0:T(8,128)(2,1)S(1)}, u32[]{:S(2)}, u32[]{:S(2)}) collective-permute-start(bf16[176,2048]{1,0:T(8,128)(2,1)S(1)} %bitcast.225), channel_id=1, source_target_pairs={{0,8},{4,12},{16,0},{20,4},{24,16},{28,20},{8,24},{12,28},{1,9},{5... | collective-permute-start | bytes 2162696 | tf_op jit(solution)/shard_map/ppermute | solution.py:64
  221.0 31.5 %collective-permute-start.37 = (bf16[256,2048]{1,0:T(8,128)(2,1)S(1)}, bf16[256,2048]{1,0:T(8,128)(2,1)S(1)}, u32[]{:S(2)}, u32[]{:S(2)}) collective-permute-start(bf16[256,2048]{1,0:T(8,128)(2,1)S(1)} %get-tuple-element.117), channel_id=1, source_target_pairs={{0,2},{1,3},{2,0},{3,1},{4,6},{5,7},{6,4},{7,5},{8,10},{9,11},{10,... | collective-permute-start | bytes 3145736 | tf_op jit(solution)/shard_map/ppermute | solution.py:42
  222.6 39.8 %collective-permute-start.38 = (bf16[256,2048]{1,0:T(8,128)(2,1)S(1)}, bf16[256,2048]{1,0:T(8,128)(2,1)S(1)}, u32[]{:S(2)}, u32[]{:S(2)}) collective-permute-start(bf16[256,2048]{1,0:T(8,128)(2,1)S(1)} %get-tuple-element.117), channel_id=1, source_target_pairs={{0,4},{4,0},{8,12},{12,8},{16,20},{20,16},{24,28},{28,24},{1,5},{5... | collective-permute-start | bytes 3145736 | tf_op jit(solution)/shard_map/ppermute | solution.py:42
  252.7 19.3 %collective-permute-start.41 = (bf16[128,2048]{1,0:T(8,128)(2,1)S(1)}, bf16[128,2048]{1,0:T(8,128)(2,1)S(1)}, u32[]{:S(2)}, u32[]{:S(2)}) collective-permute-start(bf16[128,2048]{1,0:T(8,128)(2,1)S(1)} %slice.631), channel_id=1, source_target_pairs={{0,4},{4,0},{8,12},{12,8},{16,20},{20,16},{24,28},{28,24},{1,5},{5... | collective-permute-start | bytes 1572872 | tf_op jit(solution)/shard_map/ppermute | solution.py:42
  268.8 19.4 %collective-permute-start.39 = (bf16[176,2048]{1,0:T(8,128)(2,1)S(1)}, bf16[176,2048]{1,0:T(8,128)(2,1)S(1)}, u32[]{:S(2)}, u32[]{:S(2)}) collective-permute-start(bf16[176,2048]{1,0:T(8,128)(2,1)S(1)} %bitcast.227), channel_id=1, source_target_pairs={{0,16},{4,20},{16,24},{20,28},{24,8},{28,12},{8,0},{12,4},{1,17},{... | collective-permute-start | bytes 2162696 | tf_op jit(solution)/shard_map/ppermute | solution.py:64
  269.5 32.9 %collective-permute-start.40 = (bf16[176,2048]{1,0:T(8,128)(2,1)S(1)}, bf16[176,2048]{1,0:T(8,128)(2,1)S(1)}, u32[]{:S(2)}, u32[]{:S(2)}) collective-permute-start(bf16[176,2048]{1,0:T(8,128)(2,1)S(1)} %bitcast.228), channel_id=1, source_target_pairs={{0,8},{4,12},{16,0},{20,4},{24,16},{28,20},{8,24},{12,28},{1,9},{5... | collective-permute-start | bytes 2162696 | tf_op jit(solution)/shard_map/ppermute | solution.py:64
  270.9 32.3 %collective-permute-start.45 = (bf16[256,2048]{1,0:T(8,128)(2,1)S(1)}, bf16[256,2048]{1,0:T(8,128)(2,1)S(1)}, u32[]{:S(2)}, u32[]{:S(2)}) collective-permute-start(bf16[256,2048]{1,0:T(8,128)(2,1)S(1)} %get-tuple-element.117), channel_id=1, source_target_pairs={{0,1},{1,0},{2,3},{3,2},{4,5},{5,4},{6,7},{7,6},{8,9},{9,8},{10,11... | collective-permute-start | bytes 3145736 | tf_op jit(solution)/shard_map/ppermute | solution.py:42
  272.0 34.3 %collective-permute-start.46 = (bf16[256,2048]{1,0:T(8,128)(2,1)S(1)}, bf16[256,2048]{1,0:T(8,128)(2,1)S(1)}, u32[]{:S(2)}, u32[]{:S(2)}) collective-permute-start(bf16[256,2048]{1,0:T(8,128)(2,1)S(1)} %collective-permute-done.37), channel_id=1, source_target_pairs={{0,1},{1,0},{2,3},{3,2},{4,5},{5,4},{6,7},{7,6},{8,9},{9,8},{10,11... | collective-permute-start | bytes 3145736 | tf_op jit(solution)/shard_map/ppermute | solution.py:42
  274.6 35.5 %collective-permute-start.47 = (bf16[256,2048]{1,0:T(8,128)(2,1)S(1)}, bf16[256,2048]{1,0:T(8,128)(2,1)S(1)}, u32[]{:S(2)}, u32[]{:S(2)}) collective-permute-start(bf16[256,2048]{1,0:T(8,128)(2,1)S(1)} %collective-permute-done.38), channel_id=1, source_target_pairs={{0,1},{1,0},{2,3},{3,2},{4,5},{5,4},{6,7},{7,6},{8,9},{9,8},{10,11... | collective-permute-start | bytes 3145736 | tf_op jit(solution)/shard_map/ppermute | solution.py:42
  288.3 32.7 %collective-permute-start.48 = (bf16[256,2048]{1,0:T(8,128)(2,1)S(1)}, bf16[256,2048]{1,0:T(8,128)(2,1)S(1)}, u32[]{:S(2)}, u32[]{:S(2)}) collective-permute-start(bf16[256,2048]{1,0:T(8,128)(2,1)S(1)} %pad_maximum_fusion.7), channel_id=1, source_target_pairs={{0,1},{1,0},{2,3},{3,2},{4,5},{5,4},{6,7},{7,6},{8,9},{9,8},{10,11... | collective-permute-start | bytes 3145736 | tf_op jit(solution)/shard_map/ppermute | solution.py:42
  385.1 35.6 %collective-permute-start.60 = (bf16[512,2048]{1,0:T(8,128)(2,1)S(1)}, bf16[512,2048]{1,0:T(8,128)(2,1)S(1)}, u32[]{:S(2)}, u32[]{:S(2)}) collective-permute-start(bf16[512,2048]{1,0:T(8,128)(2,1)S(1)} %convolution_convert_fusion.17), channel_id=1, source_target_pairs={{0,1},{1,0},{2,3},{3,2},{4,5},{5,4},{6,7},{7,6},{8,9},{9,8},{10,11... | collective-permute-start | bytes 6291464 | tf_op jit(solution)/shard_map/ppermute | solution.py:42
  385.2 42.4 %collective-permute-start.59 = (bf16[512,2048]{1,0:T(8,128)(2,1)}, bf16[512,2048]{1,0:T(8,128)(2,1)S(1)}, u32[]{:S(2)}, u32[]{:S(2)}) collective-permute-start(bf16[512,2048]{1,0:T(8,128)(2,1)} %convolution_convert_fusion.18), channel_id=1, source_target_pairs={{0,1},{1,0},{2,3},{3,2},{4,5},{5,4},{6,7},{7,6},{8,9},{9,8},{10,11... | collective-permute-start | bytes 6291464 | tf_op jit(solution)/shard_map/ppermute | solution.py:42
  391.6 25.9 %collective-permute-start.58 = (bf16[512,2048]{1,0:T(8,128)(2,1)S(1)}, bf16[512,2048]{1,0:T(8,128)(2,1)S(1)}, u32[]{:S(2)}, u32[]{:S(2)}) collective-permute-start(bf16[512,2048]{1,0:T(8,128)(2,1)S(1)} %convolution_convert_fusion.11), channel_id=1, source_target_pairs={{0,1},{1,0},{2,3},{3,2},{4,5},{5,4},{6,7},{7,6},{8,9},{9,8},{10,11... | collective-permute-start | bytes 6291464 | tf_op jit(solution)/shard_map/ppermute | solution.py:42
  396.0 19.5 %collective-permute-start.84 = (bf16[80,2048]{1,0:T(8,128)(2,1)S(1)}, bf16[80,2048]{1,0:T(8,128)(2,1)S(1)}, u32[]{:S(2)}, u32[]{:S(2)}) collective-permute-start(bf16[80,2048]{1,0:T(8,128)(2,1)S(1)} %get-tuple-element.216), channel_id=1, source_target_pairs={{0,8},{4,12},{16,0},{20,4},{24,16},{28,20},{8,24},{12,28},{1,9},{5... | collective-permute-start | bytes 983048 | tf_op jit(solution)/shard_map/ppermute | solution.py:64
  396.0 20.5 %collective-permute-start.83 = (bf16[96,2048]{1,0:T(8,128)(2,1)S(1)}, bf16[96,2048]{1,0:T(8,128)(2,1)S(1)}, u32[]{:S(2)}, u32[]{:S(2)}) collective-permute-start(bf16[96,2048]{1,0:T(8,128)(2,1)S(1)} %get-tuple-element.215), channel_id=1, source_target_pairs={{0,16},{4,20},{16,24},{20,28},{24,8},{28,12},{8,0},{12,4},{1,17},{... | collective-permute-start | bytes 1179656 | tf_op jit(solution)/shard_map/ppermute | solution.py:64
  415.5 24.6 %collective-permute-start.57 = (bf16[512,2048]{1,0:T(8,128)(2,1)}, bf16[512,2048]{1,0:T(8,128)(2,1)}, u32[]{:S(2)}, u32[]{:S(2)}) collective-permute-start(bf16[512,2048]{1,0:T(8,128)(2,1)} %convolution_convert_fusion.13), channel_id=1, source_target_pairs={{0,1},{1,0},{2,3},{3,2},{4,5},{5,4},{6,7},{7,6},{8,9},{9,8},{10,11... | collective-permute-start | bytes 6291464 | tf_op jit(solution)/shard_map/ppermute | solution.py:42
  444.3 19.4 %collective-permute-start.85 = (bf16[176,2048]{1,0:T(8,128)(2,1)}, bf16[176,2048]{1,0:T(8,128)(2,1)S(1)}, u32[]{:S(2)}, u32[]{:S(2)}) collective-permute-start(bf16[176,2048]{1,0:T(8,128)(2,1)} %pad_maximum_fusion.19), channel_id=1, source_target_pairs={{0,16},{4,20},{16,24},{20,28},{24,8},{28,12},{8,0},{12,4},{1,17},{... | collective-permute-start | bytes 2162696 | tf_op jit(solution)/shard_map/ppermute | solution.py:64
  444.8 33.6 %collective-permute-start.86 = (bf16[176,2048]{1,0:T(8,128)(2,1)}, bf16[176,2048]{1,0:T(8,128)(2,1)S(1)}, u32[]{:S(2)}, u32[]{:S(2)}) collective-permute-start(bf16[176,2048]{1,0:T(8,128)(2,1)} %pad_maximum_fusion.20), channel_id=1, source_target_pairs={{0,8},{4,12},{16,0},{20,4},{24,16},{28,20},{8,24},{12,28},{1,9},{5... | collective-permute-start | bytes 2162696 | tf_op jit(solution)/shard_map/ppermute | solution.py:64
  449.5 28.9 %collective-permute-start.63 = (bf16[256,2048]{1,0:T(8,128)(2,1)S(1)}, bf16[256,2048]{1,0:T(8,128)(2,1)S(1)}, u32[]{:S(2)}, u32[]{:S(2)}) collective-permute-start(bf16[256,2048]{1,0:T(8,128)(2,1)S(1)} %pad_maximum_fusion.9), channel_id=1, source_target_pairs={{0,2},{1,3},{2,0},{3,1},{4,6},{5,7},{6,4},{7,5},{8,10},{9,11},{10,... | collective-permute-start | bytes 3145736 | tf_op jit(solution)/shard_map/ppermute | solution.py:42
  450.1 28.3 %collective-permute-start.64 = (bf16[256,2048]{1,0:T(8,128)(2,1)S(1)}, bf16[256,2048]{1,0:T(8,128)(2,1)S(1)}, u32[]{:S(2)}, u32[]{:S(2)}) collective-permute-start(bf16[256,2048]{1,0:T(8,128)(2,1)S(1)} %pad_maximum_fusion.10), channel_id=1, source_target_pairs={{0,4},{4,0},{8,12},{12,8},{16,20},{20,16},{24,28},{28,24},{1,5},{5... | collective-permute-start | bytes 3145736 | tf_op jit(solution)/shard_map/ppermute | solution.py:42
  478.4 34.5 %collective-permute-start.88 = (bf16[2,80,2048]{2,1,0:T(8,128)(2,1)S(1)}, bf16[2,80,2048]{2,1,0:T(8,128)(2,1)S(1)}, u32[]{:S(2)}, u32[]{:S(2)}) collective-permute-start(bf16[2,80,2048]{2,1,0:T(8,128)(2,1)S(1)} %pad_maximum_fusion.23), channel_id=1, source_target_pairs={{0,8},{4,12},{16,0},{20,4},{24,16},{28,20},{8,24},{12,28},{1,9},{5... | collective-permute-start | bytes 1966088 | tf_op jit(solution)/shard_map/ppermute | solution.py:64
  483.5 30.0 %collective-permute-start.65 = (bf16[256,2048]{1,0:T(8,128)(2,1)S(1)}, bf16[256,2048]{1,0:T(8,128)(2,1)S(1)}, u32[]{:S(2)}, u32[]{:S(2)}) collective-permute-start(bf16[256,2048]{1,0:T(8,128)(2,1)S(1)} %get-tuple-element.127), channel_id=1, source_target_pairs={{0,2},{1,3},{2,0},{3,1},{4,6},{5,7},{6,4},{7,5},{8,10},{9,11},{10,... | collective-permute-start | bytes 3145736 | tf_op jit(solution)/shard_map/ppermute | solution.py:42
  484.0 31.0 %collective-permute-start.67 = (bf16[256,2048]{1,0:T(8,128)(2,1)S(1)}, bf16[256,2048]{1,0:T(8,128)(2,1)S(1)}, u32[]{:S(2)}, u32[]{:S(2)}) collective-permute-start(bf16[256,2048]{1,0:T(8,128)(2,1)S(1)} %get-tuple-element.127), channel_id=1, source_target_pairs={{0,4},{4,0},{8,12},{12,8},{16,20},{20,16},{24,28},{28,24},{1,5},{5... | collective-permute-start | bytes 3145736 | tf_op jit(solution)/shard_map/ppermute | solution.py:42
  485.5 27.7 %collective-permute-start.87 = (bf16[2,96,2048]{2,1,0:T(8,128)(2,1)S(1)}, bf16[2,96,2048]{2,1,0:T(8,128)(2,1)S(1)}, u32[]{:S(2)}, u32[]{:S(2)}) collective-permute-start(bf16[2,96,2048]{2,1,0:T(8,128)(2,1)S(1)} %pad_maximum_fusion.16), channel_id=1, source_target_pairs={{0,16},{4,20},{16,24},{20,28},{24,8},{28,12},{8,0},{12,4},{1,17},{... | collective-permute-start | bytes 2359304 | tf_op jit(solution)/shard_map/ppermute | solution.py:64
  517.4 50.0 %collective-permute-start.76 = (bf16[256,2048]{1,0:T(8,128)(2,1)S(1)}, bf16[256,2048]{1,0:T(8,128)(2,1)S(1)}, u32[]{:S(2)}, u32[]{:S(2)}) collective-permute-start(bf16[256,2048]{1,0:T(8,128)(2,1)S(1)} %collective-permute-done.67), channel_id=1, source_target_pairs={{0,1},{1,0},{2,3},{3,2},{4,5},{5,4},{6,7},{7,6},{8,9},{9,8},{10,11... | collective-permute-start | bytes 3145736 | tf_op jit(solution)/shard_map/ppermute | solution.py:42
  527.9 64.6 %collective-permute-start.89 = (bf16[2,176,2048]{2,1,0:T(8,128)(2,1)}, bf16[2,176,2048]{2,1,0:T(8,128)(2,1)}, u32[]{:S(2)}, u32[]{:S(2)}) collective-permute-start(bf16[2,176,2048]{2,1,0:T(8,128)(2,1)} %get-tuple-element.144), channel_id=1, source_target_pairs={{0,16},{4,20},{16,24},{20,28},{24,8},{28,12},{8,0},{12,4},{1,17},{... | collective-permute-start | bytes 4325384 | tf_op jit(solution)/shard_map/ppermute | solution.py:64
  527.9 64.7 %collective-permute-start.90 = (bf16[2,176,2048]{2,1,0:T(8,128)(2,1)}, bf16[2,176,2048]{2,1,0:T(8,128)(2,1)}, u32[]{:S(2)}, u32[]{:S(2)}) collective-permute-start(bf16[2,176,2048]{2,1,0:T(8,128)(2,1)} %get-tuple-element.145), channel_id=1, source_target_pairs={{0,8},{4,12},{16,0},{20,4},{24,16},{28,20},{8,24},{12,28},{1,9},{5... | collective-permute-start | bytes 4325384 | tf_op jit(solution)/shard_map/ppermute | solution.py:64
  530.4 38.5 %collective-permute-start.77 = (bf16[256,2048]{1,0:T(8,128)(2,1)S(1)}, bf16[256,2048]{1,0:T(8,128)(2,1)S(1)}, u32[]{:S(2)}, u32[]{:S(2)}) collective-permute-start(bf16[256,2048]{1,0:T(8,128)(2,1)S(1)} %pad_maximum_fusion.13), channel_id=1, source_target_pairs={{0,1},{1,0},{2,3},{3,2},{4,5},{5,4},{6,7},{7,6},{8,9},{9,8},{10,11... | collective-permute-start | bytes 3145736 | tf_op jit(solution)/shard_map/ppermute | solution.py:42
  530.6 20.7 %collective-permute-start.70 = (bf16[128,2048]{1,0:T(8,128)(2,1)S(1)}, bf16[128,2048]{1,0:T(8,128)(2,1)S(1)}, u32[]{:S(2)}, u32[]{:S(2)}) collective-permute-start(bf16[128,2048]{1,0:T(8,128)(2,1)S(1)} %get-tuple-element.240), channel_id=1, source_target_pairs={{0,2},{1,3},{2,0},{3,1},{4,6},{5,7},{6,4},{7,5},{8,10},{9,11},{10,... | collective-permute-start | bytes 1572872 | tf_op jit(solution)/shard_map/ppermute | solution.py:42
  564.9 37.4 %collective-permute-start.75 = (bf16[512,2048]{1,0:T(8,128)(2,1)}, bf16[512,2048]{1,0:T(8,128)(2,1)}, u32[]{:S(2)}, u32[]{:S(2)}) collective-permute-start(bf16[512,2048]{1,0:T(8,128)(2,1)} %convolution_convert_fusion.9), channel_id=1, source_target_pairs={{0,1},{1,0},{2,3},{3,2},{4,5},{5,4},{6,7},{7,6},{8,9},{9,8},{10,11... | collective-permute-start | bytes 6291464 | tf_op jit(solution)/shard_map/ppermute | solution.py:42
  567.4 30.4 %collective-permute-start.71 = (bf16[256,2048]{1,0:T(8,128)(2,1)}, bf16[256,2048]{1,0:T(8,128)(2,1)}, u32[]{:S(2)}, u32[]{:S(2)}) collective-permute-start(bf16[256,2048]{1,0:T(8,128)(2,1)} %pad_maximum_fusion.11), channel_id=1, source_target_pairs={{0,2},{1,3},{2,0},{3,1},{4,6},{5,7},{6,4},{7,5},{8,10},{9,11},{10,... | collective-permute-start | bytes 3145736 | tf_op jit(solution)/shard_map/ppermute | solution.py:42
  568.9 28.9 %collective-permute-start.72 = (bf16[256,2048]{1,0:T(8,128)(2,1)}, bf16[256,2048]{1,0:T(8,128)(2,1)}, u32[]{:S(2)}, u32[]{:S(2)}) collective-permute-start(bf16[256,2048]{1,0:T(8,128)(2,1)} %pad_maximum_fusion.12), channel_id=1, source_target_pairs={{0,4},{4,0},{8,12},{12,8},{16,20},{20,16},{24,28},{28,24},{1,5},{5... | collective-permute-start | bytes 3145736 | tf_op jit(solution)/shard_map/ppermute | solution.py:42
  631.5 27.8 %collective-permute-start.79 = (bf16[128,2048]{1,0:T(8,128)(2,1)}, bf16[128,2048]{1,0:T(8,128)(2,1)}, u32[]{:S(2)}, u32[]{:S(2)}) collective-permute-start(bf16[128,2048]{1,0:T(8,128)(2,1)} %get-tuple-element.223), channel_id=1, source_target_pairs={{0,4},{4,0},{8,12},{12,8},{16,20},{20,16},{24,28},{28,24},{1,5},{5... | collective-permute-start | bytes 1572872 | tf_op jit(solution)/shard_map/ppermute | solution.py:42
  632.9 26.3 %collective-permute-start.80 = (bf16[128,2048]{1,0:T(8,128)(2,1)}, bf16[128,2048]{1,0:T(8,128)(2,1)}, u32[]{:S(2)}, u32[]{:S(2)}) collective-permute-start(bf16[128,2048]{1,0:T(8,128)(2,1)} %get-tuple-element.222), channel_id=1, source_target_pairs={{0,2},{1,3},{2,0},{3,1},{4,6},{5,7},{6,4},{7,5},{8,10},{9,11},{10,... | collective-permute-start | bytes 1572872 | tf_op jit(solution)/shard_map/ppermute | solution.py:42
  635.2 19.5 %collective-permute-start.92 = (bf16[3,32,2048]{2,1,0:T(8,128)(2,1)S(1)}, bf16[3,32,2048]{2,1,0:T(8,128)(2,1)}, u32[]{:S(2)}, u32[]{:S(2)}) collective-permute-start(bf16[3,32,2048]{2,1,0:T(8,128)(2,1)S(1)} %get-tuple-element.147), channel_id=1, source_target_pairs={{0,8},{4,12},{16,0},{20,4},{24,16},{28,20},{8,24},{12,28},{1,9},{5... | collective-permute-start | bytes 1179656 | tf_op jit(solution)/shard_map/ppermute | solution.py:64
  657.2 48.8 %collective-permute-start.93 = (bf16[3,64,2048]{2,1,0:T(8,128)(2,1)}, bf16[3,64,2048]{2,1,0:T(8,128)(2,1)}, u32[]{:S(2)}, u32[]{:S(2)}) collective-permute-start(bf16[3,64,2048]{2,1,0:T(8,128)(2,1)} %pad_maximum_fusion.17), channel_id=1, source_target_pairs={{0,16},{4,20},{16,24},{20,28},{24,8},{28,12},{8,0},{12,4},{1,17},{... | collective-permute-start | bytes 2359304 | tf_op jit(solution)/shard_map/ppermute | solution.py:64
  657.8 48.2 %collective-permute-start.94 = (bf16[3,64,2048]{2,1,0:T(8,128)(2,1)S(1)}, bf16[3,64,2048]{2,1,0:T(8,128)(2,1)}, u32[]{:S(2)}, u32[]{:S(2)}) collective-permute-start(bf16[3,64,2048]{2,1,0:T(8,128)(2,1)S(1)} %pad_maximum_fusion.18), channel_id=1, source_target_pairs={{0,8},{4,12},{16,0},{20,4},{24,16},{28,20},{8,24},{12,28},{1,9},{5... | collective-permute-start | bytes 2359304 | tf_op jit(solution)/shard_map/ppermute | solution.py:64
  659.3 36.5 %collective-permute-start.105 = (bf16[73,64]{1,0:T(8,128)(2,1)S(1)}, bf16[73,64]{1,0:T(8,128)(2,1)S(1)}, u32[]{:S(2)}, u32[]{:S(2)}) collective-permute-start(bf16[73,64]{1,0:T(8,128)(2,1)S(1)} %get-tuple-element.256), channel_id=1, source_target_pairs={{0,16},{4,20},{16,24},{20,28},{24,8},{28,12},{8,0},{12,4},{1,17},{... | collective-permute-start | bytes 28040 | tf_op jit(solution)/shard_map/ppermute | solution.py:64
  660.9 41.5 %collective-permute-start.107 = (bf16[73,64]{1,0:T(8,128)(2,1)S(1)}, bf16[73,64]{1,0:T(8,128)(2,1)S(1)}, u32[]{:S(2)}, u32[]{:S(2)}) collective-permute-start(bf16[73,64]{1,0:T(8,128)(2,1)S(1)} %get-tuple-element.257), channel_id=1, source_target_pairs={{0,8},{4,12},{16,0},{20,4},{24,16},{28,20},{8,24},{12,28},{1,9},{5... | collective-permute-start | bytes 28040 | tf_op jit(solution)/shard_map/ppermute | solution.py:64
  698.3 22.3 %collective-permute-start.81 = (bf16[256,2048]{1,0:T(8,128)(2,1)}, bf16[256,2048]{1,0:T(8,128)(2,1)S(1)}, u32[]{:S(2)}, u32[]{:S(2)}) collective-permute-start(bf16[256,2048]{1,0:T(8,128)(2,1)} %pad_maximum_fusion.14), channel_id=1, source_target_pairs={{0,2},{1,3},{2,0},{3,1},{4,6},{5,7},{6,4},{7,5},{8,10},{9,11},{10,... | collective-permute-start | bytes 3145736 | tf_op jit(solution)/shard_map/ppermute | solution.py:42
  702.3 22.2 %collective-permute-start.82 = (bf16[256,2048]{1,0:T(8,128)(2,1)}, bf16[256,2048]{1,0:T(8,128)(2,1)}, u32[]{:S(2)}, u32[]{:S(2)}) collective-permute-start(bf16[256,2048]{1,0:T(8,128)(2,1)} %pad_maximum_fusion.15), channel_id=1, source_target_pairs={{0,4},{4,0},{8,12},{12,8},{16,20},{20,16},{24,28},{28,24},{1,5},{5... | collective-permute-start | bytes 3145736 | tf_op jit(solution)/shard_map/ppermute | solution.py:42
  (148 other events, 2420.1 us)

commit v4 on v3

--- a/solution.py
+++ b/solution.py
@@ -82,57 +82,89 @@
     )
 
 
-def gather_ring(own, axis=0, halves=True, tokens=(), later=()):
+class Gather:
+    def __init__(self, own):
+        self.most = lax.axis_size("wide") // 4 - 1
+        self.before, self.behind, self.opposite = [own], [own], []
+
+    def sends(self):
+        if len(self.before) <= self.most:
+            return self.before[-1], self.behind[-1]
+        return two_parts(self.before[-1], 0)[0], two_parts(self.behind[-1], 0)[1]
+
+    def take(self, got, back):
+        if len(self.before) <= self.most:
+            self.before.append(got)
+            self.behind.append(back)
+        else:
+            self.opposite = [got, back]
+
+    def pieces(self):
+        near = [piece for pair in zip(self.before[1:], self.behind[1:]) for piece in pair]
+        return [self.before[0]] + near + [jnp.concatenate(self.opposite, axis=0)]
+
+
+class Scatter:
+    def __init__(self, chunks):
+        self.left = len(chunks) // 2 - 1
+        self.wire = chunks[0].dtype
+        self.total = chunks[0].astype(f32)
+        self.behind = [chunk.astype(f32) for chunk in chunks[1:-1:2]]
+        self.ahead = [chunk.astype(f32) for chunk in chunks[2:-1:2]]
+        self.last = chunks[-1]
+
+    def sends(self):
+        if self.last is not None:
+            return two_parts(self.last, 0)
+        h = self.left - 1
+        return self.ahead[h].astype(self.wire), self.behind[h].astype(self.wire)
+
+    def take(self, got, back):
+        got, back = got.astype(f32), back.astype(f32)
+        h = self.left - 1
+        if self.last is not None:
+            top, bottom = two_parts(self.ahead[h], 0)
+            self.ahead[h] = jnp.concatenate([top + got, bottom], axis=0)
+            top, bottom = two_parts(self.behind[h], 0)
+            self.behind[h] = jnp.concatenate([top, bottom + back], axis=0)
+            self.last = None
+            return
+        self.left = h
+        if h:
+            self.ahead[h - 1] = self.ahead[h - 1] + got
+            self.behind[h - 1] = self.behind[h - 1] + back
+        else:
+            self.total = self.total + got + back
+
+
+def ring_step(items, tokens=()):
+    sends = [item.sends() for item in items]
+    ways = [one[0] if len(one) == 1 else jnp.concatenate(one, axis=0) for one in zip(*sends)]
+    ways = after(ways, list(tokens)) if tokens else lax.optimization_barrier(tuple(ways))
+    got, back = along(ways[0], 1), along(ways[1], -1)
+    at = [0, 0]
+    for item, (ahead, behind) in zip(items, sends):
+        ends = [at[0] + ahead.shape[0], at[1] + behind.shape[0]]
+        item.take(got[at[0] : ends[0]], back[at[1] : ends[1]])
+        at = ends
+    return [got, back]
+
+
+def gather_small(own):
     outer = lax.axis_size("wide") // 2
-    [own] = after([own], list(tokens))
-    before, behind = [own], [own]
-    for h in range(1, outer // 2):
-        one, two = along(before[-1], 1), along(behind[-1], -1)
-        if halves:
-            one, two = lax.optimization_barrier((one, two))
-        before.append(one)
-        behind.append(two)
-    if halves:
-        top, _ = two_parts(before[-1], axis)
-        _, bottom = two_parts(behind[-1], axis)
-        top, bottom = after([top, bottom], later)
-        opposite = [along(top, 1), along(bottom, -1)]
-    else:
-        opposite = [along(before[-1], 1)]
-    near = [piece for h in range(1, outer // 2) for piece in (before[h], behind[h])]
-    return [own] + near + opposite, opposite
-
-
-def scatter_ring(full, axis=0, halves=True, tokens=(), later=()):
-    outer = lax.axis_size("wide") // 2
-    wire = full.dtype
-    chunks = jnp.split(full, outer, axis=axis)
+    pieces = [own]
+    for _ in range(1, outer):
+        pieces.append(along(pieces[-1], 1))
+    order = [-offset % outer for offset in ring_offsets(outer)]
+    return jnp.concatenate([pieces[k] for k in order], axis=1)
+
+
+def scatter_small(chunks):
+    offsets = ring_offsets(len(chunks))
     total = chunks[0].astype(f32)
-    most = outer // 2 - 1
-    behind = {h: chunks[2 * h - 1].astype(f32) for h in range(1, most + 1)}
-    ahead = {h: chunks[2 * h].astype(f32) for h in range(1, most + 1)}
-    if halves:
-        top, bottom = after(two_parts(chunks[-1], axis), tokens)
-        far_top, far_bottom = two_parts(ahead[most], axis)
-        got = along(top, 1).astype(f32)
-        ahead[most] = jnp.concatenate([far_top + got, far_bottom], axis=axis)
-        far_top, far_bottom = two_parts(behind[most], axis)
-        got = along(bottom, -1).astype(f32)
-        behind[most] = jnp.concatenate([far_top, far_bottom + got], axis=axis)
-    else:
-        ahead[most] = ahead[most] + along(chunks[-1], 1).astype(f32)
-    for h in range(most, 0, -1):
-        one, two = ahead[h].astype(wire), behind[h].astype(wire)
-        if halves:
-            one, two = lax.optimization_barrier((one, two, *later))[:2]
-        one, two = along(one, 1), along(two, -1)
-        got, back = one.astype(f32), two.astype(f32)
-        if h > 1:
-            ahead[h - 1] = ahead[h - 1] + got
-            behind[h - 1] = behind[h - 1] + back
-        else:
-            total = total + got + back
-    return total, (one, two)
+    for chunk, offset in zip(chunks[1:], offsets[1:]):
+        total = total + along(chunk, offset).astype(f32)
+    return total
 
 
 def gather_rows(own, tokens=()):
@@ -142,25 +174,23 @@
     across = [swap(own, "narrow", k) for k in range(2, size, 2)]
     beside = swap(own, "wide", 1)
     stage_one = across + [beside]
-    corner, stage_two = [], []
+    parts, stage_two = [beside], []
     for n, k in enumerate(range(2, size, 2)):
         ends = [swap(across[n][:half], "wide", 1), swap(beside[half:], "narrow", k)]
-        corner.append(jnp.concatenate(ends, axis=0))
+        parts += ends
         stage_two += ends
-    [own_again] = after([own], stage_one)
-    odd = [swap(piece, "narrow", 1) for piece in [own_again] + across]
-    other_odd = [swap(piece, "narrow", 1) for piece in [beside] + corner]
-    pieces = [own] + across + odd, [beside] + corner + other_odd
-    return pieces, (stage_one, stage_two, odd + other_odd)
+    even = jnp.concatenate([own] + across, axis=0)
+    other_even = jnp.concatenate(parts, axis=0)
+    odd, other_odd = swap(even, "narrow", 1), swap(other_even, "narrow", 1)
+    return ([even, odd], [other_even, other_odd]), (stage_one, stage_two, [odd, other_odd])
 
 
 def scatter_rows(even, odd, other_even, other_odd, tokens=()):
     size = lax.axis_size("narrow")
     rows = even.shape[0] // (size // 2)
     half = rows // 2
-    stage_one = [swap(other_odd, "narrow", 1), swap(odd, "narrow", 1)]
-    other = other_even.astype(f32) + stage_one[0].astype(f32)
-    mine = even.astype(f32) + stage_one[1].astype(f32)
+    other = other_even.astype(f32) + other_odd.astype(f32)
+    mine = even.astype(f32) + odd.astype(f32)
     beside_top, beside_bottom = other[:half], other[half:rows]
     out = mine[:rows]
     corners = other[rows:].astype(bf16)
@@ -186,11 +216,42 @@
         stage_three.append(swap(spread[n], "narrow", k))
         out = out + stage_three[-1].astype(f32)
     stage_three.append(swap(spread[-1], "wide", 1))
-    return out + stage_three[-1].astype(f32), (stage_one, stage_two, stage_three)
+    return out + stage_three[-1].astype(f32), (stage_two, stage_three)
 
 
 def inverse_rms(values):
     return lax.rsqrt(jnp.mean(values * values, axis=-1, keepdims=True) + epsilon)
+
+
+def norm_kernel(*refs):
+    pieces, gain, out = refs[:-2], refs[-2], refs[-1]
+    rows = pieces[0].shape[0]
+    step = 32 if rows % 32 == 0 else rows
+    for n, piece in enumerate(pieces):
+
+        def part(b, _):
+            at = pl.multiple_of(b * step, step)
+            values = piece[pl.ds(at, step), :].astype(f32)
+            rate = lax.rsqrt(jnp.mean(values * values, axis=-1, keepdims=True) + epsilon)
+            to = pl.multiple_of(n * rows + at, step)
+            out[pl.ds(to, step), :] = (values * rate * gain[...]).astype(bf16)
+            return 0
+
+        lax.fori_loop(0, rows // step, part, 0)
+
+
+def normed_rows(pieces, gain):
+    rows, width = pieces[0].shape
+    return pl.pallas_call(
+        norm_kernel,
+        out_shape=jax.ShapeDtypeStruct((rows * len(pieces), width), bf16),
+        cost_estimate=pl.CostEstimate(
+            flops=6 * rows * len(pieces) * width,
+            bytes_accessed=4 * rows * len(pieces) * width,
+            transcendentals=0,
+        ),
+        name="norm",
+    )(*pieces, gain.reshape(1, width))
 
 
 def norm_back(values, rate, gain, grad):
@@ -573,7 +634,7 @@
         ],
         axis=0,
     )
-    small_all = jnp.concatenate(gather_ring(small, axis=1, halves=False)[0], axis=1)
+    small_all = gather_small(small)
     gains = small_all[small.shape[0] - 2 :].reshape(2, outer, own)
     [gains] = after([gains], first_stages[0])
     gains = jnp.stack([gains, swap(gains, "wide", 1)])
@@ -586,7 +647,7 @@
     gain_all = gains.transpose(3, 0, 1, 2, 4).reshape(2, width)
     gain_first, gain_last = gain_all[0], gain_all[1]
 
-    def reduce_gain(values):
+    def reduce_gain(values, tokens):
         values = values.reshape(2, outer, 2, narrow, own).transpose(1, 2, 3, 0, 4)
         values = picked(piece_outer, outer, values).transpose(1, 0, 2, 3, 4)
         values = picked(sides, 2, values).transpose(2, 0, 1, 3, 4)
@@ -596,23 +657,30 @@
         for k in range(1, narrow // 2):
             summed = summed + swap(total[k], "narrow", 2 * k)
         summed = summed[0] + swap(summed[1], "wide", 1)
-        return scatter_ring(summed, halves=False)[0][0]
+        [summed] = after([summed], tokens)
+        return scatter_small([summed[j] for j in range(outer)])
 
     documents = jnp.concatenate([doc_blocks, doc_pad], axis=0)
     [documents] = after([documents], first_stages[0])
     documents = (documents, swap(documents, "wide", 1))
     tables = [layout(rules[0], rules[1], slots) for rules in documents]
 
-    in_pieces, last = gather_ring(w_in.transpose(0, 2, 1), axis=1)
-    out_pieces, last = gather_ring(w_out, tokens=list(last) + first_stages[2])
-
-    def normed(pieces):
-        values = jnp.concatenate(pieces, axis=0).astype(f32)
-        return (values * inverse_rms(values) * gain_first).astype(bf16)
-
+    shards = [w_in.transpose(0, 2, 1).reshape(3 * own, width), w_out, w_down.T, w_gate.T, w_up.T]
+    weights = [Gather(shard) for shard in shards]
+    steps = outer // 2
+
+    def weight_step(at, tokens):
+        active = [weights[i] for i in range(len(weights)) if 0 <= at - i < steps]
+        return ring_step(active, tokens)
+
+    last = []
+    for at in range(steps - 1):
+        last = weight_step(at, last)
+    last = weight_step(steps - 1, last + first_stages[0])
+    last = weight_step(steps, last + first_stages[1])
+    rows_first = [normed_rows(first_own, gain_first), normed_rows(first_other, gain_first)]
     rate_first = inverse_rms(source)
-    rows_first = [normed(first_own), normed(first_other)]
-    (upstream_own, upstream_other), _ = gather_rows(upstream_low, first_stages[1])
+    (upstream_own, upstream_other), _ = gather_rows(upstream_low, first_stages[2])
 
     matrix = transform()
     fwd = jnp.asarray(matrix, bf16)
@@ -646,6 +714,7 @@
     )
     res_re, res_im = res_re[:, 0], -res_im[:, 0]
 
+    in_pieces = [piece.reshape(3, own, width) for piece in weights[0].pieces()]
     in_all = jnp.concatenate(in_pieces, axis=1).reshape(3 * channels, width)
     mixed = []
     for r in range(2):
@@ -655,10 +724,11 @@
             order, first, documents[r][0], proj, taps, table, spectrum, fwd, inv
         )
         mixed.append((proj, gated.reshape(slots, channels), long_out, seen))
-    out_all = jnp.concatenate(out_pieces, axis=0)
+    out_all = jnp.concatenate(weights[1].pieces(), axis=0)
     parts = [slice(0, even), slice(even, slots)]
     shares = [nn(mixed[r][1][p], out_all).astype(bf16) for r in range(2) for p in parts]
-    mixer_out, stages = scatter_rows(*shares)
+    cores = [swap(shares[n], "narrow", 1) for n in (1, 3)]
+    mixer_out, stages = scatter_rows(shares[0], cores[0], shares[2], cores[1])
     middle = source + mixer_out
     rate_last = inverse_rms(middle)
     rows_upstream = jnp.concatenate(upstream_own + upstream_other, axis=0)
@@ -666,75 +736,104 @@
         (middle * rate_last * gain_last).astype(bf16)
     )
     rows_second = jnp.concatenate(second_own + second_other, axis=0)
-    down_pieces, last = gather_ring(w_down.T, tokens=last, later=stages[0])
-    gate_pieces, last = gather_ring(w_gate.T, tokens=last + stages[1], later=stages[2])
-    up_pieces, last = gather_ring(
-        w_up.T, tokens=last + second_stages[0], later=second_stages[1]
-    )
-
-    gate_up = jnp.concatenate(gate_pieces + up_pieces, axis=0)
-    down_all = jnp.concatenate(down_pieces, axis=0)
+    last = weight_step(steps + 1, last + cores)
+    last = weight_step(steps + 2, last + stages[1])
+    last = weight_step(steps + 3, last + second_stages[1])
+    for at in range(steps + 4, steps + len(weights) - 1):
+        last = weight_step(at, last)
+
+    down_all, gate_all = [jnp.concatenate(weights[i].pieces(), axis=0) for i in (2, 3)]
     d_hidden = nt(down_all, rows_upstream)
-    pre = nt(gate_up, rows_second)
-    gate_pre, up_pre = pre[:hidden_units], pre[hidden_units:]
+    gate_pre = nt(gate_all, rows_second)
+    up_pieces = after(weights[4].pieces(), [d_hidden, gate_pre])
+    up_all = jnp.concatenate(up_pieces, axis=0)
+    up_pre = nt(up_all, rows_second)
     sig = jax.nn.sigmoid(gate_pre)
     silu = gate_pre * sig
     hidden = (silu * up_pre).astype(bf16)
     d_gate = (d_hidden * up_pre * sig * (1.0 + gate_pre * (1.0 - sig))).astype(bf16)
     d_up = (d_hidden * silu).astype(bf16)
-    d_pre = jnp.concatenate([d_gate, d_up], axis=0)
     grad_down = nn(hidden, rows_upstream).astype(bf16)
-    d_pre, *_ = after([d_pre], [grad_down])
+    d_gate, d_up = after([d_gate, d_up], [grad_down])
+    grads = [Scatter(jnp.split(grad_down, outer, axis=0))]
+    last = ring_step(grads)
     parts = [slice(p, p + even) for p in range(0, 2 * slots, even)]
-    shares = [tn(d_pre[:, p], gate_up).astype(bf16) for p in parts]
-    d_second, stages = scatter_rows(*shares)
+
+    def second_share(n, tokens=()):
+        one, two = after([d_gate, d_up], tokens)
+        p = parts[n]
+        return (tn(one[:, p], gate_all) + tn(two[:, p], up_all)).astype(bf16)
+
+    odds = [second_share(n) for n in (1, 3)]
+    cores = [swap(odd, "narrow", 1) for odd in odds]
+    evens = [second_share(n, last) for n in (0, 2)]
+    d_second, stages = scatter_rows(evens[0], cores[0], evens[1], cores[1])
     upstream = upstream_low.astype(f32)
     d_middle = upstream + norm_back(middle, rate_last, gain_last, d_second)
     (middle_own, middle_other), middle_stages = gather_rows(d_middle.astype(bf16))
     rows_dmiddle = [jnp.concatenate(middle_own, axis=0), jnp.concatenate(middle_other, axis=0)]
-    down_share, last = scatter_ring(grad_down, later=stages[1])
-    [d_gate] = after([d_gate], stages[0])
-    [d_up] = after([d_up], stages[1])
-    grad_pre = jnp.stack([nn(d, rows_second).astype(bf16) for d in (d_gate, d_up)])
-    pre_share, last = scatter_ring(
-        grad_pre, axis=1, tokens=list(last) + stages[2], later=middle_stages[1]
+    d_gate, d_up = after([d_gate, d_up], cores)
+    for d in (d_gate, d_up):
+        grads.append(Scatter(jnp.split(nn(d, rows_second).astype(bf16), outer, axis=0)))
+    for at in range(1, steps):
+        last = ring_step(grads[:1], last + cores)
+    down_last = last
+    last = ring_step(grads[1:], last + stages[0])
+    for at in range(1, steps):
+        last = ring_step(grads[1:], last + stages[1])
+    [hidden] = after([hidden], stages[0] + down_last)
+    down_shares = [tn(hidden[:, p], down_all).astype(bf16) for p in parts]
+    down_shares = after(down_shares, middle_stages[2])
+    down_cores = [swap(down_shares[n], "narrow", 1) for n in (1, 3)]
+    down_out, down_stages = scatter_rows(
+        down_shares[0], down_cores[0], down_shares[2], down_cores[1]
     )
-    [hidden] = after([hidden], [shares[1], shares[3]])
-    down_shares = [tn(hidden[:, p], down_all).astype(bf16) for p in parts]
-    down_out, _ = scatter_rows(*down_shares, tokens=middle_stages[1])
     block_output = (middle + down_out).astype(bf16)
     grad_gain_two = jnp.sum(d_second * middle * rate_last, axis=0)
 
+    grad_out = sum(tn(mixed[r][1], rows_dmiddle[r]) for r in range(2)).astype(bf16)
+    out_sum = Scatter(jnp.split(grad_out, outer, axis=0))
+    out_last = []
+    for at in range(steps):
+        last = ring_step([out_sum], last)
+        out_last.append(last)
     halves = (slice(0, even), slice(even, slots))
     shares, d_rows, grad_gain_one, d_filter, d_taps = [None, None], [None, None], 0.0, 0.0, 0.0
     for r in range(2):
         proj, gated, long_out, seen = mixed[r]
         table, first = tables[r]
         d_gated = nt(rows_dmiddle[r], out_all).reshape(narrow, local_rows, channels)
+        if r == 1:
+            [d_gated] = after([d_gated], [grad_out, *shares[0], *down_cores])
         dz, d_filter_row, d_taps_row = mixer_backward(
             order, first, documents[r][0], proj, d_gated, long_out, seen, taps, table,
             spectrum, fwd, inv,
         )
         d_rows[r] = dz.reshape(slots, 3 * channels)
         d_filter, d_taps = d_filter + d_filter_row, d_taps + d_taps_row
-        shares[r] = [nn(d_rows[r][p], in_all).astype(bf16) for p in halves]
-        for n, share in enumerate(shares[r]):
+        if r == 0:
+            shares[r] = [nn(d_rows[r][p], in_all).astype(bf16) for p in halves]
+    [ready] = after([d_rows[1]], out_last[0] + down_stages[0])
+    odd = nn(ready[halves[1]], in_all).astype(bf16)
+    cores = [swap(shares[0][1], "narrow", 1), swap(odd, "narrow", 1)]
+    ready = after(d_rows, [odd])
+    grad_in = sum(tn(ready[r], rows_first[r]) for r in range(2)).astype(bf16)
+    [ready] = after([d_rows[1]], [grad_in] + cores + out_last[-1] + down_stages[1])
+    shares[1] = [nn(ready[halves[0]], in_all).astype(bf16), odd]
+    d_normed, stages = scatter_rows(shares[0][0], cores[0], shares[1][0], cores[1])
+    input_grad = (d_middle + norm_back(source, rate_first, gain_first, d_normed)).astype(bf16)
+    for r in range(2):
+        for n, share in enumerate(after(shares[r], [shares[1][0]])):
             rows = rows_first[r][n * even : (n + 1) * even]
             grad_gain_one = grad_gain_one + jnp.sum(share.astype(f32) * rows.astype(f32), axis=0)
-    d_normed, stages = scatter_rows(*shares[0], *shares[1])
-    input_grad = (d_middle + norm_back(source, rate_first, gain_first, d_normed)).astype(bf16)
-    done = shares[0] + shares[1]
-    d_rows = after(d_rows, done)
-    grad_in = sum(tn(d_rows[r], rows_first[r]) for r in range(2)).astype(bf16)
-    d_filter, *_ = after([d_filter], [grad_in])
-    gated = after([mixed[0][1], mixed[1][1]], stages[1])
-    grad_out = sum(tn(gated[r], rows_dmiddle[r]) for r in range(2)).astype(bf16)
-    in_share, last = scatter_ring(
-        grad_in.reshape(3, channels, width), axis=1, tokens=list(last) + stages[0]
-    )
-    out_share, _ = scatter_ring(grad_out, tokens=last)
-    gain_grads = after([jnp.stack([grad_gain_one / gain_first, grad_gain_two])], stages[1])
-    gain_share = reduce_gain(gain_grads[0])
+    chunks = grad_in.reshape(3, outer, own, width)
+    in_sum = Scatter([chunks[:, j].reshape(3 * own, width) for j in range(outer)])
+    last = ring_step([in_sum], last)
+    d_filter, *_ = after([d_filter], last + stages[0])
+    for at in range(1, steps):
+        last = ring_step([in_sum], last + stages[0])
+    gain_grads = after([jnp.stack([grad_gain_one / gain_first, grad_gain_two])], stages[0])
+    gain_share = reduce_gain(gain_grads[0], stages[1])
 
     sum_re, sum_im, mom_re, mom_im = filter_moments(d_filter, step_re, step_im)
     full_re = lag * sum_re + 8.0 * mom_re
@@ -754,23 +853,23 @@
         axis=0,
     ).astype(bf16)
     [small_grad] = after([small_grad], stages[1])
-    small_share, _ = scatter_ring(small_grad, axis=1, halves=False)
+    small_share = scatter_small(jnp.split(small_grad, outer, axis=1))
 
     at = 9 + poles
     return (
         block_output[None],
         input_grad[None],
-        in_share.transpose(0, 2, 1),
-        out_share,
+        in_sum.total.reshape(3, own, width).transpose(0, 2, 1),
+        out_sum.total,
         gain_share[0],
         small_share[:9].reshape(3, 3, own),
         small_share[9:at].T,
         small_share[at : at + poles].T,
         small_share[at + poles :].T,
         gain_share[1],
-        pre_share[0].T,
-        pre_share[1].T,
-        down_share.T,
+        grads[1].total.T,
+        grads[2].total.T,
+        grads[0].total.T,
     )
 
 

time: 742 us -> 796 us (1.073)
  waiting for transfers between devices: 267 us -> 318 us
  other arithmetic: 87 us -> 70.1 us
  Pallas kernels: 58.4 us -> 74.9 us
  matrix products: 138 us -> 147 us
    ppermute x63 -> x55, waiting for transfers between devices: 60.3 us -> 106 us  [swap(): return lax.ppermute(values, axis, [(i, i ^ shift) for i in range(size)])]
    pallas_call x0 -> x2, Pallas kernels: none -> 16.8 us  [normed_rows(): pl.pallas_call(norm_kernel, out_shape=jax.ShapeDtypeStruct((rows * len(pi...]
    convert_element_type x2 -> x0, other arithmetic: 8.92 us -> none  [the longest x1 8.91 us: normed(): return (values * inverse_rms(values) * gain_first).astype(bf16)]
    dot_general x6 -> x7, matrix products: 42.6 us -> 49.7 us  [nt(): lax.dot_general(a, b, (((1,), (1,)), ((), ())), preferred_element_type=f32)]
    ppermute x45 -> x37, starting transfers between devices: 56.9 us -> 51.1 us  [along(): return lax.ppermute(values, 'wide', pairs)]
    ppermute x45 -> x37, waiting for transfers between devices: 207 us -> 212 us  [along(): return lax.ppermute(values, 'wide', pairs)]
    unnamed x252 -> x228, local copies, waits for them, and re-layouts: 40.9 us -> 35.8 us
    ppermute x63 -> x55, starting transfers between devices: 43.7 us -> 48.4 us  [swap(): return lax.ppermute(values, axis, [(i, i ^ shift) for i in range(size)])]
  transfers between devices with their start and end apart: 108 -> 92, of which waited for: 35 -> 37; matrix products, arithmetic and copies ran while one was open for 29% -> 25% of each run, Pallas kernels for 7% -> 8%
where the time goes in v4:
time: 796 us; the launch traced here: 787 us
  waiting for transfers between devices  318 us (40%)
  matrix products  147 us (18%)
  starting transfers between devices  99.6 us (13%)
  Pallas kernels  74.9 us (9%)
  local copies, waits for them, and re-layouts  74.6 us (9%)
  other arithmetic  70.1 us (9%)
    ppermute x37, waiting for transfers between devices, along(): return lax.ppermute(values, 'wide', pairs)  212 us
    ppermute x55, waiting for transfers between devices, swap(): return lax.ppermute(values, axis, [(i, i ^ shift) for i in range(size)])  106 us
    ppermute x37, starting transfers between devices, along(): return lax.ppermute(values, 'wide', pairs)  51.1 us
    dot_general x7, matrix products, nt(): lax.dot_general(a, b, (((1,), (1,)), ((), ())), preferred_element_type=f32)  49.7 us
    ppermute x55, starting transfers between devices, swap(): return lax.ppermute(values, axis, [(i, i ^ shift) for i in range(size)])  48.4 us
    dot_general x16, matrix products, tn(): lax.dot_general(a, b, (((0,), (0,)), ((), ())), preferred_element_type=f32)  47.9 us
    dot_general x11, matrix products, nn(): lax.dot_general(a, b, (((1,), (0,)), ((), ())), preferred_element_type=f32)  45.5 us
    unnamed x228, local copies, waits for them, and re-layouts  35.8 us
  transfers between devices with their start and end apart: 92, of which 37 were waited for; matrix products, arithmetic and copies ran while one was open for 25% of the time, Pallas kernels for 8%

profile of v4, /device:TPU:0, one launch (start us, length us, event | category | flops | bytes accessed | tf_op | source)
XLA Modules:
  0.0 787.5 jit_solution(14593508157071663543)
XLA Ops:
  0.7 3.1 collective-permute-start.1
  5.9 3.1 concatenate.223
  26.9 20.7 %collective-permute-done.4 = bf16[75,64]{1,0:T(8,128)(2,1)S(1)} collective-permute-done((bf16[75,64]{1,0:T(8,128)(2,1)S(1)}, bf16[75,64]{1,0:T(8,128)(2,1)S(1)}, u32[]{:S(2)}, u32[]{:S(2)}) %collective-permute-start.4) | collective-permute-done | bytes 9632 | tf_op jit(solution)/shard_map/ppermute | solution.py:64
  54.7 4.1 taps.1
  58.8 3.5 fusion.88.spectrum
  73.0 3.2 collective-permute-start.11
  95.2 6.1 collective-permute-done.12
  106.8 3.1 pad_maximum_fusion.1
  111.8 10.6 %collective-permute-done.15 = bf16[208,2048]{1,0:T(8,128)(2,1)S(1)} collective-permute-done((bf16[208,2048]{1,0:T(8,128)(2,1)S(1)}, bf16[208,2048]{1,0:T(8,128)(2,1)S(1)}, u32[]{:S(2)}, u32[]{:S(2)}) %collective-permute-start.15) | collective-permute-done | bytes 852000 | tf_op jit(solution)/shard_map/ppermute | solution.py:64
  122.4 20.8 %collective-permute-done.16 = bf16[208,2048]{1,0:T(8,128)(2,1)S(1)} collective-permute-done((bf16[208,2048]{1,0:T(8,128)(2,1)S(1)}, bf16[208,2048]{1,0:T(8,128)(2,1)S(1)}, u32[]{:S(2)}, u32[]{:S(2)}) %collective-permute-start.16) | collective-permute-done | bytes 852000 | tf_op jit(solution)/shard_map/ppermute | solution.py:64
  146.3 8.4 %norm.2 = bf16[1024,2048]{1,0:T(8,128)(2,1)} custom-call(bf16[512,2048]{1,0:T(8,128)(2,1)} %pad_maximum_fusion.2.refs_0_, bf16[512,2048]{1,0:T(8,128)(2,1)} %collective-permute-done.2.refs_1_, f32[1,2048]{1,0:T(1,128)} %slice.603.refs_2_), custom_call_target="tpu_custom_call" | custom-call | flops 12582912 | bytes 8388608 | tf_op jit(solution)/shard_map/norm/pallas_call | solution.py:245
  154.7 8.4 %norm.3 = bf16[1024,2048]{1,0:T(8,128)(2,1)} custom-call(bf16[512,2048]{1,0:T(8,128)(2,1)} %constant_dynamic-update-slice_fusion.1.refs_0_, bf16[512,2048]{1,0:T(8,128)(2,1)} %collective-permute-done.19.refs_1_, f32[1,2048]{1,0:T(1,128)} %slice.603.refs_2_), custom_call_target="tpu_custom_call" | custom-call | flops 12582912 | bytes 8388608 | tf_op jit(solution)/shard_map/norm/pallas_call | solution.py:245
  163.1 6.4 fusion.89.proj
  169.5 7.0 mixer_forward.3
  180.0 3.4 fusion.87.proj
  183.5 7.0 mixer_forward.2
  195.7 20.0 %collective-permute-done.39 = bf16[256,2048]{1,0:T(8,128)(2,1)S(1)} collective-permute-done((bf16[256,2048]{1,0:T(8,128)(2,1)S(1)}, bf16[256,2048]{1,0:T(8,128)(2,1)S(1)}, u32[]{:S(2)}, u32[]{:S(2)}) %collective-permute-start.39) | collective-permute-done | bytes 1048608 | tf_op jit(solution)/shard_map/ppermute | solution.py:42
  221.9 8.7 %collective-permute-done.41 = bf16[128,2048]{1,0:T(8,128)(2,1)S(1)} collective-permute-done((bf16[128,2048]{1,0:T(8,128)(2,1)S(1)}, bf16[128,2048]{1,0:T(8,128)(2,1)S(1)}, u32[]{:S(2)}, u32[]{:S(2)}) %collective-permute-start.41) | collective-permute-done | bytes 524320 | tf_op jit(solution)/shard_map/ppermute | solution.py:42
  232.2 3.0 collective-permute-start.25
  235.2 4.8 collective-permute-done.22
  241.8 10.4 %collective-permute-done.21 = bf16[128,2048]{1,0:T(8,128)(2,1)S(1)} collective-permute-done((bf16[128,2048]{1,0:T(8,128)(2,1)S(1)}, bf16[128,2048]{1,0:T(8,128)(2,1)S(1)}, u32[]{:S(2)}, u32[]{:S(2)}) %collective-permute-start.21) | collective-permute-done | bytes 524320 | tf_op jit(solution)/shard_map/ppermute | solution.py:42
  259.9 20.7 %collective-permute-done.25 = bf16[272,2048]{1,0:T(8,128)(2,1)S(1)} collective-permute-done((bf16[272,2048]{1,0:T(8,128)(2,1)S(1)}, bf16[272,2048]{1,0:T(8,128)(2,1)S(1)}, u32[]{:S(2)}, u32[]{:S(2)}) %collective-permute-start.25) | collective-permute-done | bytes 1114144 | tf_op jit(solution)/shard_map/ppermute | solution.py:64
  292.1 17.9 %collective-permute-done.31 = bf16[256,2048]{1,0:T(8,128)(2,1)S(1)} collective-permute-done((bf16[256,2048]{1,0:T(8,128)(2,1)S(1)}, bf16[256,2048]{1,0:T(8,128)(2,1)S(1)}, u32[]{:S(2)}, u32[]{:S(2)}) %collective-permute-start.31) | collective-permute-done | bytes 1048608 | tf_op jit(solution)/shard_map/ppermute | solution.py:42
  314.7 22.4 %collective-permute-done.28 = bf16[256,2048]{1,0:T(8,128)(2,1)S(1)} collective-permute-done((bf16[256,2048]{1,0:T(8,128)(2,1)S(1)}, bf16[256,2048]{1,0:T(8,128)(2,1)S(1)}, u32[]{:S(2)}, u32[]{:S(2)}) %collective-permute-start.28) | collective-permute-done | bytes 1048608 | tf_op jit(solution)/shard_map/ppermute | solution.py:64
  340.5 11.2 %fusion.91 = f32[704,2048]{1,0:T(8,128)} fusion(bf16[704,2048]{1,0:T(8,128)(2,1)} %get-tuple-element.261, bf16[2048,2048]{1,0:T(8,128)(2,1)} %constant_dynamic-update-slice_fusion.13), kind=kOutput, calls=%fused_computation.347 | convolution fusion | flops 5905580032 | bytes 17039360 | tf_op jit(solution)/shard_map/dot_general | solution.py:33
  352.7 3.5 collective-permute-done.35
  362.3 10.3 %fusion.90 = f32[704,2048]{1,0:T(8,128)} fusion(bf16[704,2048]{1,0:T(8,128)(2,1)S(1)} %get-tuple-element.258, bf16[2048,2048]{1,0:T(8,128)(2,1)} %constant_dynamic-update-slice_fusion.5), kind=kOutput, calls=%fused_computation.346 | convolution fusion | flops 5905580032 | bytes 17039360 | tf_op jit(solution)/shard_map/dot_general | solution.py:33
  373.9 15.8 %multiply_convert_fusion = (bf16[704,2048]{1,0:T(8,128)(2,1)}, bf16[704,2048]{1,0:T(8,128)(2,1)}, bf16[704,2048]{1,0:T(8,128)(2,1)}) fusion(f32[704,2048]{1,0:T(8,128)} %fusion.91, f32[704,2048]{1,0:T(8,128)} %fusion.90, bf16[704,2048]{1,0:T(8,128)(2,1)S(1)} %constant_dynamic-update-slice_fusion.20, bf16[2048,2048]{1,0:T(8,128)(2,1)} %constant_dynamic-update-slice_fusion.5), kind=kOutput, calls=%fused_computation.1 | convolution fusion | flops 5927206912 | bytes 31457280 | tf_op jit(solution)/shard_map/dot_general | solution.py:33
  389.7 9.6 %convolution_convert_fusion.2 = bf16[704,2048]{1,0:T(8,128)(2,1)S(1)} fusion(bf16[704,2048]{1,0:T(8,128)(2,1)} %get-tuple-element.127, bf16[2048,2048]{1,0:T(8,128)(2,1)} %constant_dynamic-update-slice_fusion.13), kind=kOutput, calls=%fused_computation.29 | convolution fusion | flops 5907021824 | bytes 14155776 | tf_op jit(solution)/shard_map/dot_general | solution.py:29
  412.4 11.5 %collective-permute-done.44 = bf16[80,2048]{1,0:T(8,128)(2,1)S(1)} collective-permute-done((bf16[80,2048]{1,0:T(8,128)(2,1)S(1)}, bf16[80,2048]{1,0:T(8,128)(2,1)S(1)}, u32[]{:S(2)}, u32[]{:S(2)}) %collective-permute-start.44) | collective-permute-done | bytes 327712 | tf_op jit(solution)/shard_map/ppermute | solution.py:64
  429.7 9.3 %convolution_convert_fusion = bf16[704,2048]{1,0:T(8,128)(2,1)S(1)} fusion(bf16[704,2048]{1,0:T(8,128)(2,1)S(1)} %copy-done.56, bf16[2048,2048]{1,0:T(8,128)(2,1)} %constant_dynamic-update-slice_fusion.5), kind=kOutput, calls=%fused_computation.27 | convolution fusion | flops 5907021824 | bytes 14155776 | tf_op jit(solution)/shard_map/dot_general | solution.py:29
  439.9 3.2 fusion.86
  445.2 9.5 %convolution_convert_fusion.1 = bf16[704,2048]{1,0:T(8,128)(2,1)S(1)} fusion(bf16[704,2048]{1,0:T(8,128)(2,1)} %get-tuple-element.143, bf16[2048,2048]{1,0:T(8,128)(2,1)} %constant_dynamic-update-slice_fusion.5), kind=kOutput, calls=%fused_computation.28 | convolution fusion | flops 5907021824 | bytes 14155776 | tf_op jit(solution)/shard_map/dot_general | solution.py:29
  457.3 3.0 convert_add_fusion.4
  466.8 5.8 collective-permute-done.49
  472.7 13.0 %collective-permute-done.50 = bf16[176,2048]{1,0:T(8,128)(2,1)S(1)} collective-permute-done((bf16[176,2048]{1,0:T(8,128)(2,1)}, bf16[176,2048]{1,0:T(8,128)(2,1)S(1)}, u32[]{:S(2)}, u32[]{:S(2)}) %collective-permute-start.50) | collective-permute-done | bytes 720928 | tf_op jit(solution)/shard_map/ppermute | solution.py:64
  485.7 5.3 convolution_convert_fusion.11
  491.0 4.9 convolution_convert_fusion.12
  500.9 5.0 convolution_convert_fusion.13
  509.1 5.0 convolution_convert_fusion.14
  516.7 7.8 collective-permute-done.53
  524.8 15.2 %collective-permute-done.67 = bf16[160,2048]{1,0:T(8,128)(2,1)S(1)} collective-permute-done((bf16[160,2048]{1,0:T(8,128)(2,1)S(1)}, bf16[160,2048]{1,0:T(8,128)(2,1)S(1)}, u32[]{:S(2)}, u32[]{:S(2)}) %collective-permute-start.67) | collective-permute-done | bytes 655392 | tf_op jit(solution)/shard_map/ppermute | solution.py:64
  547.7 3.0 collective-permute-done.57
  557.6 15.7 %mixer_backward.2 = (bf16[4,256,768]{2,1,0:T(8,128)(2,1)}, f32[512,256]{1,0:T(8,128)S(1)}, f32[8,768]{1,0:T(8,128)S(1)}) custom-call(s32[4]{0:T(128)S(1)} %copy-done.12, s32[3]{0:T(128)S(1)} %copy-done.16, s32[3]{0:T(128)S(1)} %copy-done.20, f32[4,256,768]{2,1,0:T(8,128)} %copy-done.4, f32[4,256,256]{2,1,0:T(8,128)S(1)} %bitcast.205, ...), custom_call_target="tpu_custom_call" | custom-call | flops 2013265920 | bytes 8388608 | tf_op jit(solution)/shard_map/mixer_backward/pallas_call | solution.py:545
  582.6 23.3 %collective-permute-done.69 = bf16[352,2048]{1,0:T(8,128)(2,1)} collective-permute-done((bf16[352,2048]{1,0:T(8,128)(2,1)}, bf16[352,2048]{1,0:T(8,128)(2,1)}, u32[]{:S(2)}, u32[]{:S(2)}) %collective-permute-start.69) | collective-permute-done | bytes 1441824 | tf_op jit(solution)/shard_map/ppermute | solution.py:64
  607.9 4.5 add_bitcast_fusion.1
  618.1 5.4 collective-permute-done.73
  623.4 5.1 collective-permute-done.74
  629.4 3.1 convert_add_fusion.1
  633.5 3.1 convert_add_fusion.2
  642.0 16.3 %mixer_backward.3 = (bf16[4,256,768]{2,1,0:T(8,128)(2,1)}, f32[512,256]{1,0:T(8,128)S(1)}, f32[8,768]{1,0:T(8,128)S(1)}) custom-call(s32[4]{0:T(128)S(1)} %copy-done.12, s32[3]{0:T(128)S(1)} %copy-done.14, s32[3]{0:T(128)S(1)} %copy-done.18, f32[4,256,768]{2,1,0:T(8,128)} %copy-done.3, f32[4,256,256]{2,1,0:T(8,128)S(1)} %bitcast.204, ...), custom_call_target="tpu_custom_call" | custom-call | flops 2013265920 | bytes 8388608 | tf_op jit(solution)/shard_map/mixer_backward/pallas_call | solution.py:545
  659.3 4.1 convolution_convert_fusion.8
  663.5 3.5 fusion.94
  667.0 4.0 add_convert_fusion
  679.3 4.7 collective-permute-done.79
  685.0 7.9 %collective-permute-done.80 = bf16[96,2048]{1,0:T(8,128)(2,1)S(1)} collective-permute-done((bf16[96,2048]{1,0:T(8,128)(2,1)S(1)}, bf16[96,2048]{1,0:T(8,128)(2,1)S(1)}, u32[]{:S(2)}, u32[]{:S(2)}) %collective-permute-start.80) | collective-permute-done | bytes 393248 | tf_op jit(solution)/shard_map/ppermute | solution.py:64
  693.9 8.0 %collective-permute-done.63 = bf16[256,2048]{1,0:T(8,128)(2,1)S(1)} collective-permute-done((bf16[256,2048]{1,0:T(8,128)(2,1)S(1)}, bf16[256,2048]{1,0:T(8,128)(2,1)S(1)}, u32[]{:S(2)}, u32[]{:S(2)}) %collective-permute-start.63) | collective-permute-done | bytes 1048608 | tf_op jit(solution)/shard_map/ppermute | solution.py:42
  704.2 4.0 convert_add_fusion
  713.6 7.9 %collective-permute-done.76 = bf16[128,2048]{1,0:T(8,128)(2,1)S(1)} collective-permute-done((bf16[128,2048]{1,0:T(8,128)(2,1)S(1)}, bf16[128,2048]{1,0:T(8,128)(2,1)S(1)}, u32[]{:S(2)}, u32[]{:S(2)}) %collective-permute-start.76) | collective-permute-done | bytes 524320 | tf_op jit(solution)/shard_map/ppermute | solution.py:42
  731.5 8.0 %moments.1 = (f32[16,8,256]{2,1,0:T(8,128)}, f32[16,8,256]{2,1,0:T(8,128)}, f32[16,8,256]{2,1,0:T(8,128)}, f32[16,8,256]{2,1,0:T(8,128)}) custom-call(f32[512,256]{1,0:T(8,128)} %add.369.grad, f32[16,8,256]{2,1,0:T(8,128)} %broadcast_in_dim.199.step_re, f32[16,8,256]{2,1,0:T(8,128)} %broadcast_in_dim.200.step_im), custom_call_target="tpu_custom_call" | custom-call | flops 31457280 | bytes 524288 | tf_op jit(solution)/shard_map/moments/pallas_call | solution.py:337
  742.4 11.4 %collective-permute-done.84 = f32[2,4,2,64]{3,1,2,0:T(4,128)S(1)} collective-permute-done((f32[2,4,2,64]{3,1,2,0:T(4,128)S(1)}, f32[2,4,2,64]{3,1,2,0:T(4,128)S(1)}, u32[]{:S(2)}, u32[]{:S(2)}) %collective-permute-start.84) | collective-permute-done | bytes 4128 | tf_op jit(solution)/shard_map/ppermute | solution.py:42
  757.4 9.2 %collective-permute-done.82 = bf16[192,2048]{1,0:T(8,128)(2,1)} collective-permute-done((bf16[192,2048]{1,0:T(8,128)(2,1)}, bf16[192,2048]{1,0:T(8,128)(2,1)}, u32[]{:S(2)}, u32[]{:S(2)}) %collective-permute-start.82) | collective-permute-done | bytes 786464 | tf_op jit(solution)/shard_map/ppermute | solution.py:64
  766.7 3.3 fusion.16
  774.4 2.9 collective-permute-start.87
  (592 shorter events, 250.4 us)
Async XLA Ops:
  0.7 65.1 %collective-permute-start.1 = (bf16[256,2048]{1,0:T(8,128)(2,1)}, bf16[256,2048]{1,0:T(8,128)(2,1)}, u32[]{:S(2)}, u32[]{:S(2)}) collective-permute-start(bf16[256,2048]{1,0:T(8,128)(2,1)} %bitcast.216), channel_id=1, source_target_pairs={{0,4},{4,0},{8,12},{12,8},{16,20},{20,16},{24,28},{28,24},{1,5},{5... | collective-permute-start | bytes 3145736 | tf_op jit(solution)/shard_map/ppermute | solution.py:42
  3.7 62.0 %collective-permute-start = (bf16[256,2048]{1,0:T(8,128)(2,1)}, bf16[256,2048]{1,0:T(8,128)(2,1)}, u32[]{:S(2)}, u32[]{:S(2)}) collective-permute-start(bf16[256,2048]{1,0:T(8,128)(2,1)} %bitcast.217), channel_id=1, source_target_pairs={{0,2},{1,3},{2,0},{3,1},{4,6},{5,7},{6,4},{7,5},{8,10},{9,11},{10,... | collective-permute-start | bytes 3145736 | tf_op jit(solution)/shard_map/ppermute | solution.py:42
  11.7 50.7 %collective-permute-start.9 = (bf16[192,2048]{1,0:T(8,128)(2,1)}, bf16[192,2048]{1,0:T(8,128)(2,1)}, u32[]{:S(2)}, u32[]{:S(2)}) collective-permute-start(bf16[192,2048]{1,0:T(8,128)(2,1)} %bitcast.246), channel_id=1, source_target_pairs={{0,16},{4,20},{16,24},{20,28},{24,8},{28,12},{8,0},{12,4},{1,17},{... | collective-permute-start | bytes 2359304 | tf_op jit(solution)/shard_map/ppermute | solution.py:64
  13.2 50.2 %collective-permute-start.10 = (bf16[192,2048]{1,0:T(8,128)(2,1)}, bf16[192,2048]{1,0:T(8,128)(2,1)}, u32[]{:S(2)}, u32[]{:S(2)}) collective-permute-start(bf16[192,2048]{1,0:T(8,128)(2,1)} %bitcast.247), channel_id=1, source_target_pairs={{0,8},{4,12},{16,0},{20,4},{24,16},{28,20},{8,24},{12,28},{1,9},{5... | collective-permute-start | bytes 2359304 | tf_op jit(solution)/shard_map/ppermute | solution.py:64
  24.3 23.3 %collective-permute-start.4 = (bf16[75,64]{1,0:T(8,128)(2,1)S(1)}, bf16[75,64]{1,0:T(8,128)(2,1)S(1)}, u32[]{:S(2)}, u32[]{:S(2)}) collective-permute-start(bf16[75,64]{1,0:T(8,128)(2,1)S(1)} %collective-permute-done.3), channel_id=1, source_target_pairs={{0,16},{4,20},{16,24},{20,28},{24,8},{28,12},{8,0},{12,4},{1,17},{... | collective-permute-start | bytes 28808 | tf_op jit(solution)/shard_map/ppermute | solution.py:64
  68.2 24.1 %collective-permute-start.14 = (bf16[128,2048]{1,0:T(8,128)(2,1)}, bf16[128,2048]{1,0:T(8,128)(2,1)}, u32[]{:S(2)}, u32[]{:S(2)}) collective-permute-start(bf16[128,2048]{1,0:T(8,128)(2,1)} %slice.792), channel_id=1, source_target_pairs={{0,2},{1,3},{2,0},{3,1},{4,6},{5,7},{6,4},{7,5},{8,10},{9,11},{10,... | collective-permute-start | bytes 1572872 | tf_op jit(solution)/shard_map/ppermute | solution.py:42
  72.5 17.9 %collective-permute-start.13 = (bf16[128,2048]{1,0:T(8,128)(2,1)}, bf16[128,2048]{1,0:T(8,128)(2,1)}, u32[]{:S(2)}, u32[]{:S(2)}) collective-permute-start(bf16[128,2048]{1,0:T(8,128)(2,1)} %slice.791), channel_id=1, source_target_pairs={{0,4},{4,0},{8,12},{12,8},{16,20},{20,16},{24,28},{28,24},{1,5},{5... | collective-permute-start | bytes 1572872 | tf_op jit(solution)/shard_map/ppermute | solution.py:42
  73.0 21.2 %collective-permute-start.11 = (bf16[160,2048]{1,0:T(8,128)(2,1)}, bf16[160,2048]{1,0:T(8,128)(2,1)}, u32[]{:S(2)}, u32[]{:S(2)}) collective-permute-start(bf16[160,2048]{1,0:T(8,128)(2,1)} %get-tuple-element.100), channel_id=1, source_target_pairs={{0,16},{4,20},{16,24},{20,28},{24,8},{28,12},{8,0},{12,4},{1,17},{... | collective-permute-start | bytes 1966088 | tf_op jit(solution)/shard_map/ppermute | solution.py:64
  81.3 19.9 %collective-permute-start.12 = (bf16[160,2048]{1,0:T(8,128)(2,1)}, bf16[160,2048]{1,0:T(8,128)(2,1)}, u32[]{:S(2)}, u32[]{:S(2)}) collective-permute-start(bf16[160,2048]{1,0:T(8,128)(2,1)} %get-tuple-element.101), channel_id=1, source_target_pairs={{0,8},{4,12},{16,0},{20,4},{24,16},{28,20},{8,24},{12,28},{1,9},{5... | collective-permute-start | bytes 1966088 | tf_op jit(solution)/shard_map/ppermute | solution.py:64
  88.0 58.3 %collective-permute-start.2 = (bf16[512,2048]{1,0:T(8,128)(2,1)}, bf16[512,2048]{1,0:T(8,128)(2,1)}, u32[]{:S(2)}, u32[]{:S(2)}) collective-permute-start(bf16[512,2048]{1,0:T(8,128)(2,1)} %pad_maximum_fusion.2.refs_0_), channel_id=1, source_target_pairs={{0,1},{1,0},{2,3},{3,2},{4,5},{5,4},{6,7},{7,6},{8,9},{9,8},{10,11... | collective-permute-start | bytes 6291464 | tf_op jit(solution)/shard_map/ppermute | solution.py:42
  94.2 60.5 %collective-permute-start.19 = (bf16[512,2048]{1,0:T(8,128)(2,1)}, bf16[512,2048]{1,0:T(8,128)(2,1)}, u32[]{:S(2)}, u32[]{:S(2)}) collective-permute-start(bf16[512,2048]{1,0:T(8,128)(2,1)} %constant_dynamic-update-slice_fusion.1.refs_0_), channel_id=1, source_target_pairs={{0,1},{1,0},{2,3},{3,2},{4,5},{5,4},{6,7},{7,6},{8,9},{9,8},{10,11... | collective-permute-start | bytes 6291464 | tf_op jit(solution)/shard_map/ppermute | solution.py:42
  102.4 20.0 %collective-permute-start.15 = (bf16[208,2048]{1,0:T(8,128)(2,1)S(1)}, bf16[208,2048]{1,0:T(8,128)(2,1)S(1)}, u32[]{:S(2)}, u32[]{:S(2)}) collective-permute-start(bf16[208,2048]{1,0:T(8,128)(2,1)S(1)} %get-tuple-element.103), channel_id=1, source_target_pairs={{0,16},{4,20},{16,24},{20,28},{24,8},{28,12},{8,0},{12,4},{1,17},{... | collective-permute-start | bytes 2555912 | tf_op jit(solution)/shard_map/ppermute | solution.py:64
  103.0 40.2 %collective-permute-start.16 = (bf16[208,2048]{1,0:T(8,128)(2,1)S(1)}, bf16[208,2048]{1,0:T(8,128)(2,1)S(1)}, u32[]{:S(2)}, u32[]{:S(2)}) collective-permute-start(bf16[208,2048]{1,0:T(8,128)(2,1)S(1)} %get-tuple-element.104), channel_id=1, source_target_pairs={{0,8},{4,12},{16,0},{20,4},{24,16},{28,20},{8,24},{12,28},{1,9},{5... | collective-permute-start | bytes 2555912 | tf_op jit(solution)/shard_map/ppermute | solution.py:64
  178.7 41.7 %collective-permute-start.20 = (bf16[512,2048]{1,0:T(8,128)(2,1)}, bf16[512,2048]{1,0:T(8,128)(2,1)S(1)}, u32[]{:S(2)}, u32[]{:S(2)}) collective-permute-start(bf16[512,2048]{1,0:T(8,128)(2,1)} %convolution_convert_fusion.3), channel_id=1, source_target_pairs={{0,1},{1,0},{2,3},{3,2},{4,5},{5,4},{6,7},{7,6},{8,9},{9,8},{10,11... | collective-permute-start | bytes 6291464 | tf_op jit(solution)/shard_map/ppermute | solution.py:42
  190.6 25.1 %collective-permute-start.39 = (bf16[256,2048]{1,0:T(8,128)(2,1)S(1)}, bf16[256,2048]{1,0:T(8,128)(2,1)S(1)}, u32[]{:S(2)}, u32[]{:S(2)}) collective-permute-start(bf16[256,2048]{1,0:T(8,128)(2,1)S(1)} %bitcast.219), channel_id=1, source_target_pairs={{0,4},{4,0},{8,12},{12,8},{16,20},{20,16},{24,28},{28,24},{1,5},{5... | collective-permute-start | bytes 3145736 | tf_op jit(solution)/shard_map/ppermute | solution.py:42
  192.2 25.2 %collective-permute-start.37 = (bf16[256,2048]{1,0:T(8,128)(2,1)S(1)}, bf16[256,2048]{1,0:T(8,128)(2,1)S(1)}, u32[]{:S(2)}, u32[]{:S(2)}) collective-permute-start(bf16[256,2048]{1,0:T(8,128)(2,1)S(1)} %bitcast.220), channel_id=1, source_target_pairs={{0,2},{1,3},{2,0},{3,1},{4,6},{5,7},{6,4},{7,5},{8,10},{9,11},{10,... | collective-permute-start | bytes 3145736 | tf_op jit(solution)/shard_map/ppermute | solution.py:42
  194.4 36.6 %collective-permute-start.17 = (bf16[512,2048]{1,0:T(8,128)(2,1)S(1)}, bf16[512,2048]{1,0:T(8,128)(2,1)S(1)}, u32[]{:S(2)}, u32[]{:S(2)}) collective-permute-start(bf16[512,2048]{1,0:T(8,128)(2,1)S(1)} %convolution_convert_fusion.5), channel_id=1, source_target_pairs={{0,1},{1,0},{2,3},{3,2},{4,5},{5,4},{6,7},{7,6},{8,9},{9,8},{10,11... | collective-permute-start | bytes 6291464 | tf_op jit(solution)/shard_map/ppermute | solution.py:42
  219.2 34.7 %collective-permute-start.38 = (bf16[512,2048]{1,0:T(8,128)(2,1)S(1)}, bf16[512,2048]{1,0:T(8,128)(2,1)S(1)}, u32[]{:S(2)}, u32[]{:S(2)}) collective-permute-start(bf16[512,2048]{1,0:T(8,128)(2,1)S(1)} %pad_maximum_fusion.5), channel_id=1, source_target_pairs={{0,1},{1,0},{2,3},{3,2},{4,5},{5,4},{6,7},{7,6},{8,9},{9,8},{10,11... | collective-permute-start | bytes 6291464 | tf_op jit(solution)/shard_map/ppermute | solution.py:42
  221.3 18.7 %collective-permute-start.22 = (bf16[128,2048]{1,0:T(8,128)(2,1)S(1)}, bf16[128,2048]{1,0:T(8,128)(2,1)S(1)}, u32[]{:S(2)}, u32[]{:S(2)}) collective-permute-start(bf16[128,2048]{1,0:T(8,128)(2,1)S(1)} %get-tuple-element.244), channel_id=1, source_target_pairs={{0,2},{1,3},{2,0},{3,1},{4,6},{5,7},{6,4},{7,5},{8,10},{9,11},{10,... | collective-permute-start | bytes 1572872 | tf_op jit(solution)/shard_map/ppermute | solution.py:42
  230.9 59.6 %collective-permute-start.42 = (bf16[512,2048]{1,0:T(8,128)(2,1)S(1)}, bf16[512,2048]{1,0:T(8,128)(2,1)S(1)}, u32[]{:S(2)}, u32[]{:S(2)}) collective-permute-start(bf16[512,2048]{1,0:T(8,128)(2,1)S(1)} %pad_maximum_fusion.6), channel_id=1, source_target_pairs={{0,1},{1,0},{2,3},{3,2},{4,5},{5,4},{6,7},{7,6},{8,9},{9,8},{10,11... | collective-permute-start | bytes 6291464 | tf_op jit(solution)/shard_map/ppermute | solution.py:42
  231.8 50.4 %collective-permute-start.26 = (bf16[256,2048]{1,0:T(8,128)(2,1)S(1)}, bf16[256,2048]{1,0:T(8,128)(2,1)S(1)}, u32[]{:S(2)}, u32[]{:S(2)}) collective-permute-start(bf16[256,2048]{1,0:T(8,128)(2,1)S(1)} %pad_maximum_fusion.17), channel_id=1, source_target_pairs={{0,8},{4,12},{16,0},{20,4},{24,16},{28,20},{8,24},{12,28},{1,9},{5... | collective-permute-start | bytes 3145736 | tf_op jit(solution)/shard_map/ppermute | solution.py:64
  232.2 48.3 %collective-permute-start.25 = (bf16[272,2048]{1,0:T(8,128)(2,1)S(1)}, bf16[272,2048]{1,0:T(8,128)(2,1)S(1)}, u32[]{:S(2)}, u32[]{:S(2)}) collective-permute-start(bf16[272,2048]{1,0:T(8,128)(2,1)S(1)} %copy-done.70), channel_id=1, source_target_pairs={{0,16},{4,20},{16,24},{20,28},{24,8},{28,12},{8,0},{12,4},{1,17},{... | collective-permute-start | bytes 3342344 | tf_op jit(solution)/shard_map/ppermute | solution.py:64
  252.4 30.8 %collective-permute-start.23 = (bf16[256,2048]{1,0:T(8,128)(2,1)S(1)}, bf16[256,2048]{1,0:T(8,128)(2,1)S(1)}, u32[]{:S(2)}, u32[]{:S(2)}) collective-permute-start(bf16[256,2048]{1,0:T(8,128)(2,1)S(1)} %pad_maximum_fusion.15), channel_id=1, source_target_pairs={{0,2},{1,3},{2,0},{3,1},{4,6},{5,7},{6,4},{7,5},{8,10},{9,11},{10,... | collective-permute-start | bytes 3145736 | tf_op jit(solution)/shard_map/ppermute | solution.py:42
  254.0 29.3 %collective-permute-start.24 = (bf16[256,2048]{1,0:T(8,128)(2,1)S(1)}, bf16[256,2048]{1,0:T(8,128)(2,1)S(1)}, u32[]{:S(2)}, u32[]{:S(2)}) collective-permute-start(bf16[256,2048]{1,0:T(8,128)(2,1)S(1)} %pad_maximum_fusion.16), channel_id=1, source_target_pairs={{0,4},{4,0},{8,12},{12,8},{16,20},{20,16},{24,28},{28,24},{1,5},{5... | collective-permute-start | bytes 3145736 | tf_op jit(solution)/shard_map/ppermute | solution.py:42
  285.3 24.7 %collective-permute-start.31 = (bf16[256,2048]{1,0:T(8,128)(2,1)S(1)}, bf16[256,2048]{1,0:T(8,128)(2,1)S(1)}, u32[]{:S(2)}, u32[]{:S(2)}) collective-permute-start(bf16[256,2048]{1,0:T(8,128)(2,1)S(1)} %get-tuple-element.200), channel_id=1, source_target_pairs={{0,4},{4,0},{8,12},{12,8},{16,20},{20,16},{24,28},{28,24},{1,5},{5... | collective-permute-start | bytes 3145736 | tf_op jit(solution)/shard_map/ppermute | solution.py:42
  286.8 24.8 %collective-permute-start.29 = (bf16[256,2048]{1,0:T(8,128)(2,1)S(1)}, bf16[256,2048]{1,0:T(8,128)(2,1)S(1)}, u32[]{:S(2)}, u32[]{:S(2)}) collective-permute-start(bf16[256,2048]{1,0:T(8,128)(2,1)S(1)} %get-tuple-element.200), channel_id=1, source_target_pairs={{0,2},{1,3},{2,0},{3,1},{4,6},{5,7},{6,4},{7,5},{8,10},{9,11},{10,... | collective-permute-start | bytes 3145736 | tf_op jit(solution)/shard_map/ppermute | solution.py:42
  288.3 26.4 %collective-permute-start.27 = (bf16[272,2048]{1,0:T(8,128)(2,1)S(1)}, bf16[272,2048]{1,0:T(8,128)(2,1)S(1)}, u32[]{:S(2)}, u32[]{:S(2)}) collective-permute-start(bf16[272,2048]{1,0:T(8,128)(2,1)S(1)} %pad_maximum_fusion.14), channel_id=1, source_target_pairs={{0,16},{4,20},{16,24},{20,28},{24,8},{28,12},{8,0},{12,4},{1,17},{... | collective-permute-start | bytes 3342344 | tf_op jit(solution)/shard_map/ppermute | solution.py:64
  289.7 47.4 %collective-permute-start.28 = (bf16[256,2048]{1,0:T(8,128)(2,1)S(1)}, bf16[256,2048]{1,0:T(8,128)(2,1)S(1)}, u32[]{:S(2)}, u32[]{:S(2)}) collective-permute-start(bf16[256,2048]{1,0:T(8,128)(2,1)S(1)} %pad_maximum_fusion.18), channel_id=1, source_target_pairs={{0,8},{4,12},{16,0},{20,4},{24,16},{28,20},{8,24},{12,28},{1,9},{5... | collective-permute-start | bytes 3145736 | tf_op jit(solution)/shard_map/ppermute | solution.py:64
  310.0 27.1 %collective-permute-start.33 = (bf16[128,2048]{1,0:T(8,128)(2,1)S(1)}, bf16[128,2048]{1,0:T(8,128)(2,1)S(1)}, u32[]{:S(2)}, u32[]{:S(2)}) collective-permute-start(bf16[128,2048]{1,0:T(8,128)(2,1)S(1)} %slice.812), channel_id=1, source_target_pairs={{0,2},{1,3},{2,0},{3,1},{4,6},{5,7},{6,4},{7,5},{8,10},{9,11},{10,... | collective-permute-start | bytes 1572872 | tf_op jit(solution)/shard_map/ppermute | solution.py:42
  311.6 25.5 %collective-permute-start.32 = (bf16[128,2048]{1,0:T(8,128)(2,1)S(1)}, bf16[128,2048]{1,0:T(8,128)(2,1)S(1)}, u32[]{:S(2)}, u32[]{:S(2)}) collective-permute-start(bf16[128,2048]{1,0:T(8,128)(2,1)S(1)} %slice.811), channel_id=1, source_target_pairs={{0,4},{4,0},{8,12},{12,8},{16,20},{20,16},{24,28},{28,24},{1,5},{5... | collective-permute-start | bytes 1572872 | tf_op jit(solution)/shard_map/ppermute | solution.py:42
  313.4 42.8 %collective-permute-start.30 = (bf16[512,2048]{1,0:T(8,128)(2,1)S(1)}, bf16[512,2048]{1,0:T(8,128)(2,1)S(1)}, u32[]{:S(2)}, u32[]{:S(2)}) collective-permute-start(bf16[512,2048]{1,0:T(8,128)(2,1)S(1)} %pad_maximum_fusion.3), channel_id=1, source_target_pairs={{0,1},{1,0},{2,3},{3,2},{4,5},{5,4},{6,7},{7,6},{8,9},{9,8},{10,11... | collective-permute-start | bytes 6291464 | tf_op jit(solution)/shard_map/ppermute | solution.py:42
  338.1 18.1 %collective-permute-start.35 = (bf16[96,2048]{1,0:T(8,128)(2,1)S(1)}, bf16[96,2048]{1,0:T(8,128)(2,1)S(1)}, u32[]{:S(2)}, u32[]{:S(2)}) collective-permute-start(bf16[96,2048]{1,0:T(8,128)(2,1)S(1)} %get-tuple-element.112), channel_id=1, source_target_pairs={{0,16},{4,20},{16,24},{20,28},{24,8},{28,12},{8,0},{12,4},{1,17},{... | collective-permute-start | bytes 1179656 | tf_op jit(solution)/shard_map/ppermute | solution.py:64
  340.4 20.3 %collective-permute-start.34 = (bf16[512,2048]{1,0:T(8,128)(2,1)S(1)}, bf16[512,2048]{1,0:T(8,128)(2,1)S(1)}, u32[]{:S(2)}, u32[]{:S(2)}) collective-permute-start(bf16[512,2048]{1,0:T(8,128)(2,1)S(1)} %pad_maximum_fusion.4), channel_id=1, source_target_pairs={{0,1},{1,0},{2,3},{3,2},{4,5},{5,4},{6,7},{7,6},{8,9},{9,8},{10,11... | collective-permute-start | bytes 6291464 | tf_op jit(solution)/shard_map/ppermute | solution.py:42
  404.9 19.1 %collective-permute-start.44 = (bf16[80,2048]{1,0:T(8,128)(2,1)S(1)}, bf16[80,2048]{1,0:T(8,128)(2,1)S(1)}, u32[]{:S(2)}, u32[]{:S(2)}) collective-permute-start(bf16[80,2048]{1,0:T(8,128)(2,1)S(1)} %get-tuple-element.122), channel_id=1, source_target_pairs={{0,8},{4,12},{16,0},{20,4},{24,16},{28,20},{8,24},{12,28},{1,9},{5... | collective-permute-start | bytes 983048 | tf_op jit(solution)/shard_map/ppermute | solution.py:64
  405.5 19.4 %collective-permute-start.43 = (bf16[96,2048]{1,0:T(8,128)(2,1)S(1)}, bf16[96,2048]{1,0:T(8,128)(2,1)S(1)}, u32[]{:S(2)}, u32[]{:S(2)}) collective-permute-start(bf16[96,2048]{1,0:T(8,128)(2,1)S(1)} %get-tuple-element.121), channel_id=1, source_target_pairs={{0,16},{4,20},{16,24},{20,28},{24,8},{28,12},{8,0},{12,4},{1,17},{... | collective-permute-start | bytes 1179656 | tf_op jit(solution)/shard_map/ppermute | solution.py:64
  409.8 19.8 %collective-permute-start.45 = (bf16[512,2048]{1,0:T(8,128)(2,1)S(1)}, bf16[512,2048]{1,0:T(8,128)(2,1)S(1)}, u32[]{:S(2)}, u32[]{:S(2)}) collective-permute-start(bf16[512,2048]{1,0:T(8,128)(2,1)S(1)} %add_convert_fusion.3), channel_id=1, source_target_pairs={{0,1},{1,0},{2,3},{3,2},{4,5},{5,4},{6,7},{7,6},{8,9},{9,8},{10,11... | collective-permute-start | bytes 6291464 | tf_op jit(solution)/shard_map/ppermute | solution.py:42
  411.9 17.8 %collective-permute-start.48 = (bf16[512,2048]{1,0:T(8,128)(2,1)S(1)}, bf16[512,2048]{1,0:T(8,128)(2,1)S(1)}, u32[]{:S(2)}, u32[]{:S(2)}) collective-permute-start(bf16[512,2048]{1,0:T(8,128)(2,1)S(1)} %add_convert_fusion.2), channel_id=1, source_target_pairs={{0,1},{1,0},{2,3},{3,2},{4,5},{5,4},{6,7},{7,6},{8,9},{9,8},{10,11... | collective-permute-start | bytes 6291464 | tf_op jit(solution)/shard_map/ppermute | solution.py:42
  444.1 17.5 %collective-permute-start.47 = (bf16[128,2048]{1,0:T(8,128)(2,1)S(1)}, bf16[128,2048]{1,0:T(8,128)(2,1)S(1)}, u32[]{:S(2)}, u32[]{:S(2)}) collective-permute-start(bf16[128,2048]{1,0:T(8,128)(2,1)S(1)} %get-tuple-element.241), channel_id=1, source_target_pairs={{0,2},{1,3},{2,0},{3,1},{4,6},{5,7},{6,4},{7,5},{8,10},{9,11},{10,... | collective-permute-start | bytes 1572872 | tf_op jit(solution)/shard_map/ppermute | solution.py:42
  444.7 15.8 %collective-permute-start.46 = (bf16[128,2048]{1,0:T(8,128)(2,1)}, bf16[128,2048]{1,0:T(8,128)(2,1)}, u32[]{:S(2)}, u32[]{:S(2)}) collective-permute-start(bf16[128,2048]{1,0:T(8,128)(2,1)} %get-tuple-element.242), channel_id=1, source_target_pairs={{0,4},{4,0},{8,12},{12,8},{16,20},{20,16},{24,28},{28,24},{1,5},{5... | collective-permute-start | bytes 1572872 | tf_op jit(solution)/shard_map/ppermute | solution.py:42
  454.7 17.9 %collective-permute-start.49 = (bf16[176,2048]{1,0:T(8,128)(2,1)}, bf16[176,2048]{1,0:T(8,128)(2,1)S(1)}, u32[]{:S(2)}, u32[]{:S(2)}) collective-permute-start(bf16[176,2048]{1,0:T(8,128)(2,1)} %pad_maximum_fusion.34), channel_id=1, source_target_pairs={{0,16},{4,20},{16,24},{20,28},{24,8},{28,12},{8,0},{12,4},{1,17},{... | collective-permute-start | bytes 2162696 | tf_op jit(solution)/shard_map/ppermute | solution.py:64
  454.8 30.9 %collective-permute-start.50 = (bf16[176,2048]{1,0:T(8,128)(2,1)}, bf16[176,2048]{1,0:T(8,128)(2,1)S(1)}, u32[]{:S(2)}, u32[]{:S(2)}) collective-permute-start(bf16[176,2048]{1,0:T(8,128)(2,1)} %pad_maximum_fusion.35), channel_id=1, source_target_pairs={{0,8},{4,12},{16,0},{20,4},{24,16},{28,20},{8,24},{12,28},{1,9},{5... | collective-permute-start | bytes 2162696 | tf_op jit(solution)/shard_map/ppermute | solution.py:64
  463.8 32.1 %collective-permute-start.51 = (bf16[256,2048]{1,0:T(8,128)(2,1)S(1)}, bf16[256,2048]{1,0:T(8,128)(2,1)S(1)}, u32[]{:S(2)}, u32[]{:S(2)}) collective-permute-start(bf16[256,2048]{1,0:T(8,128)(2,1)S(1)} %pad_maximum_fusion.19), channel_id=1, source_target_pairs={{0,2},{1,3},{2,0},{3,1},{4,6},{5,7},{6,4},{7,5},{8,10},{9,11},{10,... | collective-permute-start | bytes 3145736 | tf_op jit(solution)/shard_map/ppermute | solution.py:42
  465.4 30.6 %collective-permute-start.52 = (bf16[256,2048]{1,0:T(8,128)(2,1)S(1)}, bf16[256,2048]{1,0:T(8,128)(2,1)S(1)}, u32[]{:S(2)}, u32[]{:S(2)}) collective-permute-start(bf16[256,2048]{1,0:T(8,128)(2,1)S(1)} %pad_maximum_fusion.20), channel_id=1, source_target_pairs={{0,4},{4,0},{8,12},{12,8},{16,20},{20,16},{24,28},{28,24},{1,5},{5... | collective-permute-start | bytes 3145736 | tf_op jit(solution)/shard_map/ppermute | solution.py:42
  499.4 25.1 %collective-permute-start.53 = (bf16[256,2048]{1,0:T(8,128)(2,1)S(1)}, bf16[256,2048]{1,0:T(8,128)(2,1)S(1)}, u32[]{:S(2)}, u32[]{:S(2)}) collective-permute-start(bf16[256,2048]{1,0:T(8,128)(2,1)S(1)} %get-tuple-element.197), channel_id=1, source_target_pairs={{0,2},{1,3},{2,0},{3,1},{4,6},{5,7},{6,4},{7,5},{8,10},{9,11},{10,... | collective-permute-start | bytes 3145736 | tf_op jit(solution)/shard_map/ppermute | solution.py:42
  505.8 34.2 %collective-permute-start.67 = (bf16[160,2048]{1,0:T(8,128)(2,1)S(1)}, bf16[160,2048]{1,0:T(8,128)(2,1)S(1)}, u32[]{:S(2)}, u32[]{:S(2)}) collective-permute-start(bf16[160,2048]{1,0:T(8,128)(2,1)S(1)} %pad_maximum_fusion.36), channel_id=1, source_target_pairs={{0,8},{4,12},{16,0},{20,4},{24,16},{28,20},{8,24},{12,28},{1,9},{5... | collective-permute-start | bytes 1966088 | tf_op jit(solution)/shard_map/ppermute | solution.py:64
  507.7 33.8 %collective-permute-start.55 = (bf16[256,2048]{1,0:T(8,128)(2,1)S(1)}, bf16[256,2048]{1,0:T(8,128)(2,1)S(1)}, u32[]{:S(2)}, u32[]{:S(2)}) collective-permute-start(bf16[256,2048]{1,0:T(8,128)(2,1)S(1)} %get-tuple-element.197), channel_id=1, source_target_pairs={{0,4},{4,0},{8,12},{12,8},{16,20},{20,16},{24,28},{28,24},{1,5},{5... | collective-permute-start | bytes 3145736 | tf_op jit(solution)/shard_map/ppermute | solution.py:42
  514.0 30.1 %collective-permute-start.66 = (bf16[192,2048]{1,0:T(8,128)(2,1)S(1)}, bf16[192,2048]{1,0:T(8,128)(2,1)S(1)}, u32[]{:S(2)}, u32[]{:S(2)}) collective-permute-start(bf16[192,2048]{1,0:T(8,128)(2,1)S(1)} %pad_maximum_fusion.28), channel_id=1, source_target_pairs={{0,16},{4,20},{16,24},{20,28},{24,8},{28,12},{8,0},{12,4},{1,17},{... | collective-permute-start | bytes 2359304 | tf_op jit(solution)/shard_map/ppermute | solution.py:64
  524.7 31.0 %collective-permute-start.54 = (bf16[512,2048]{1,0:T(8,128)(2,1)S(1)}, bf16[512,2048]{1,0:T(8,128)(2,1)S(1)}, u32[]{:S(2)}, u32[]{:S(2)}) collective-permute-start(bf16[512,2048]{1,0:T(8,128)(2,1)S(1)} %pad_maximum_fusion.7), channel_id=1, source_target_pairs={{0,1},{1,0},{2,3},{3,2},{4,5},{5,4},{6,7},{7,6},{8,9},{9,8},{10,11... | collective-permute-start | bytes 6291464 | tf_op jit(solution)/shard_map/ppermute | solution.py:42
  545.7 36.9 %collective-permute-start.68 = (bf16[352,2048]{1,0:T(8,128)(2,1)}, bf16[352,2048]{1,0:T(8,128)(2,1)}, u32[]{:S(2)}, u32[]{:S(2)}) collective-permute-start(bf16[352,2048]{1,0:T(8,128)(2,1)} %pad_maximum_fusion.11), channel_id=1, source_target_pairs={{0,16},{4,20},{16,24},{20,28},{24,8},{28,12},{8,0},{12,4},{1,17},{... | collective-permute-start | bytes 4325384 | tf_op jit(solution)/shard_map/ppermute | solution.py:64
  545.7 60.1 %collective-permute-start.69 = (bf16[352,2048]{1,0:T(8,128)(2,1)}, bf16[352,2048]{1,0:T(8,128)(2,1)}, u32[]{:S(2)}, u32[]{:S(2)}) collective-permute-start(bf16[352,2048]{1,0:T(8,128)(2,1)} %pad_maximum_fusion.12), channel_id=1, source_target_pairs={{0,8},{4,12},{16,0},{20,4},{24,16},{28,20},{8,24},{12,28},{1,9},{5... | collective-permute-start | bytes 4325384 | tf_op jit(solution)/shard_map/ppermute | solution.py:64
  553.5 24.5 %collective-permute-start.58 = (bf16[512,2048]{1,0:T(8,128)(2,1)}, bf16[512,2048]{1,0:T(8,128)(2,1)S(1)}, u32[]{:S(2)}, u32[]{:S(2)}) collective-permute-start(bf16[512,2048]{1,0:T(8,128)(2,1)} %pad_maximum_fusion.8), channel_id=1, source_target_pairs={{0,1},{1,0},{2,3},{3,2},{4,5},{5,4},{6,7},{7,6},{8,9},{9,8},{10,11... | collective-permute-start | bytes 6291464 | tf_op jit(solution)/shard_map/ppermute | solution.py:42
  577.4 52.0 %collective-permute-start.65 = (bf16[512,2048]{1,0:T(8,128)(2,1)S(1)}, bf16[512,2048]{1,0:T(8,128)(2,1)S(1)}, u32[]{:S(2)}, u32[]{:S(2)}) collective-permute-start(bf16[512,2048]{1,0:T(8,128)(2,1)S(1)} %convolution_convert_fusion.9), channel_id=1, source_target_pairs={{0,1},{1,0},{2,3},{3,2},{4,5},{5,4},{6,7},{7,6},{8,9},{9,8},{10,11... | collective-permute-start | bytes 6291464 | tf_op jit(solution)/shard_map/ppermute | solution.py:42
  612.4 27.9 %collective-permute-start.59 = (bf16[512,2048]{1,0:T(8,128)(2,1)S(1)}, bf16[512,2048]{1,0:T(8,128)(2,1)S(1)}, u32[]{:S(2)}, u32[]{:S(2)}) collective-permute-start(bf16[512,2048]{1,0:T(8,128)(2,1)S(1)} %copy-done.94), channel_id=1, source_target_pairs={{0,1},{1,0},{2,3},{3,2},{4,5},{5,4},{6,7},{7,6},{8,9},{9,8},{10,11... | collective-permute-start | bytes 6291464 | tf_op jit(solution)/shard_map/ppermute | solution.py:42
  612.4 21.1 %collective-permute-start.60 = (bf16[512,2048]{1,0:T(8,128)(2,1)S(1)}, bf16[512,2048]{1,0:T(8,128)(2,1)S(1)}, u32[]{:S(2)}, u32[]{:S(2)}) collective-permute-start(bf16[512,2048]{1,0:T(8,128)(2,1)S(1)} %copy-done.93), channel_id=1, source_target_pairs={{0,1},{1,0},{2,3},{3,2},{4,5},{5,4},{6,7},{7,6},{8,9},{9,8},{10,11... | collective-permute-start | bytes 6291464 | tf_op jit(solution)/shard_map/ppermute | solution.py:42
  637.8 21.5 %collective-permute-start.62 = (bf16[128,2048]{1,0:T(8,128)(2,1)}, bf16[128,2048]{1,0:T(8,128)(2,1)}, u32[]{:S(2)}, u32[]{:S(2)}) collective-permute-start(bf16[128,2048]{1,0:T(8,128)(2,1)} %get-tuple-element.238), channel_id=1, source_target_pairs={{0,2},{1,3},{2,0},{3,1},{4,6},{5,7},{6,4},{7,5},{8,10},{9,11},{10,... | collective-permute-start | bytes 1572872 | tf_op jit(solution)/shard_map/ppermute | solution.py:42
  638.9 20.4 %collective-permute-start.61 = (bf16[128,2048]{1,0:T(8,128)(2,1)}, bf16[128,2048]{1,0:T(8,128)(2,1)}, u32[]{:S(2)}, u32[]{:S(2)}) collective-permute-start(bf16[128,2048]{1,0:T(8,128)(2,1)} %get-tuple-element.239), channel_id=1, source_target_pairs={{0,4},{4,0},{8,12},{12,8},{16,20},{20,16},{24,28},{28,24},{1,5},{5... | collective-permute-start | bytes 1572872 | tf_op jit(solution)/shard_map/ppermute | solution.py:42
  663.4 40.9 %collective-permute-start.72 = (bf16[512,2048]{1,0:T(8,128)(2,1)S(1)}, bf16[512,2048]{1,0:T(8,128)(2,1)S(1)}, u32[]{:S(2)}, u32[]{:S(2)}) collective-permute-start(bf16[512,2048]{1,0:T(8,128)(2,1)S(1)} %convolution_convert_fusion.8), channel_id=1, source_target_pairs={{0,1},{1,0},{2,3},{3,2},{4,5},{5,4},{6,7},{7,6},{8,9},{9,8},{10,11... | collective-permute-start | bytes 6291464 | tf_op jit(solution)/shard_map/ppermute | solution.py:42
  676.3 25.6 %collective-permute-start.63 = (bf16[256,2048]{1,0:T(8,128)(2,1)S(1)}, bf16[256,2048]{1,0:T(8,128)(2,1)S(1)}, u32[]{:S(2)}, u32[]{:S(2)}) collective-permute-start(bf16[256,2048]{1,0:T(8,128)(2,1)S(1)} %pad_maximum_fusion.21), channel_id=1, source_target_pairs={{0,2},{1,3},{2,0},{3,1},{4,6},{5,7},{6,4},{7,5},{8,10},{9,11},{10,... | collective-permute-start | bytes 3145736 | tf_op jit(solution)/shard_map/ppermute | solution.py:42
  677.3 25.3 %collective-permute-start.64 = (bf16[256,2048]{1,0:T(8,128)(2,1)S(1)}, bf16[256,2048]{1,0:T(8,128)(2,1)S(1)}, u32[]{:S(2)}, u32[]{:S(2)}) collective-permute-start(bf16[256,2048]{1,0:T(8,128)(2,1)S(1)} %pad_maximum_fusion.22), channel_id=1, source_target_pairs={{0,4},{4,0},{8,12},{12,8},{16,20},{20,16},{24,28},{28,24},{1,5},{5... | collective-permute-start | bytes 3145736 | tf_op jit(solution)/shard_map/ppermute | solution.py:42
  722.9 16.6 %collective-permute-start.83 = (f32[2,2,4,2,64]{4,2,3,1,0:T(4,128)S(1)}, f32[2,2,4,2,64]{4,2,3,1,0:T(4,128)S(1)}, u32[]{:S(2)}, u32[]{:S(2)}) collective-permute-start(f32[2,2,4,2,64]{4,2,3,1,0:T(4,128)S(1)} %slice.889), channel_id=1, source_target_pairs={{0,1},{1,0},{2,3},{3,2},{4,5},{5,4},{6,7},{7,6},{8,9},{9,8},{10,11... | collective-permute-start | bytes 24584 | tf_op jit(solution)/shard_map/ppermute | solution.py:42
  727.9 42.1 %collective-permute-start.77 = (bf16[256,2048]{1,0:T(8,128)(2,1)}, bf16[256,2048]{1,0:T(8,128)(2,1)S(1)}, u32[]{:S(2)}, u32[]{:S(2)}) collective-permute-start(bf16[256,2048]{1,0:T(8,128)(2,1)} %pad_maximum_fusion.23), channel_id=1, source_target_pairs={{0,2},{1,3},{2,0},{3,1},{4,6},{5,7},{6,4},{7,5},{8,10},{9,11},{10,... | collective-permute-start | bytes 3145736 | tf_op jit(solution)/shard_map/ppermute | solution.py:42
  728.8 41.2 %collective-permute-start.78 = (bf16[256,2048]{1,0:T(8,128)(2,1)}, bf16[256,2048]{1,0:T(8,128)(2,1)S(1)}, u32[]{:S(2)}, u32[]{:S(2)}) collective-permute-start(bf16[256,2048]{1,0:T(8,128)(2,1)} %pad_maximum_fusion.24), channel_id=1, source_target_pairs={{0,4},{4,0},{8,12},{12,8},{16,20},{20,16},{24,28},{28,24},{1,5},{5... | collective-permute-start | bytes 3145736 | tf_op jit(solution)/shard_map/ppermute | solution.py:42
  729.4 28.0 %collective-permute-start.81 = (bf16[192,2048]{1,0:T(8,128)(2,1)}, bf16[192,2048]{1,0:T(8,128)(2,1)}, u32[]{:S(2)}, u32[]{:S(2)}) collective-permute-start(bf16[192,2048]{1,0:T(8,128)(2,1)} %pad_maximum_fusion.29), channel_id=1, source_target_pairs={{0,16},{4,20},{16,24},{20,28},{24,8},{28,12},{8,0},{12,4},{1,17},{... | collective-permute-start | bytes 2359304 | tf_op jit(solution)/shard_map/ppermute | solution.py:64
  730.1 36.6 %collective-permute-start.82 = (bf16[192,2048]{1,0:T(8,128)(2,1)}, bf16[192,2048]{1,0:T(8,128)(2,1)}, u32[]{:S(2)}, u32[]{:S(2)}) collective-permute-start(bf16[192,2048]{1,0:T(8,128)(2,1)} %pad_maximum_fusion.30), channel_id=1, source_target_pairs={{0,8},{4,12},{16,0},{20,4},{24,16},{28,20},{8,24},{12,28},{1,9},{5... | collective-permute-start | bytes 2359304 | tf_op jit(solution)/shard_map/ppermute | solution.py:64
  (130 other events, 2303.6 us)

commit v5 on v4

--- a/solution.py
+++ b/solution.py
@@ -137,11 +137,11 @@
             self.total = self.total + got + back
 
 
-def ring_step(items, tokens=()):
+def ring_step(items, tokens=(), arrive=()):
     sends = [item.sends() for item in items]
     ways = [one[0] if len(one) == 1 else jnp.concatenate(one, axis=0) for one in zip(*sends)]
     ways = after(ways, list(tokens)) if tokens else lax.optimization_barrier(tuple(ways))
-    got, back = along(ways[0], 1), along(ways[1], -1)
+    got, back = after([along(ways[0], 1), along(ways[1], -1)], list(arrive))
     at = [0, 0]
     for item, (ahead, behind) in zip(items, sends):
         ends = [at[0] + ahead.shape[0], at[1] + behind.shape[0]]
@@ -152,11 +152,7 @@
 
 def gather_small(own):
     outer = lax.axis_size("wide") // 2
-    pieces = [own]
-    for _ in range(1, outer):
-        pieces.append(along(pieces[-1], 1))
-    order = [-offset % outer for offset in ring_offsets(outer)]
-    return jnp.concatenate([pieces[k] for k in order], axis=1)
+    return [own] + [along(own, -offset) for offset in ring_offsets(outer)[1:]]
 
 
 def scatter_small(chunks):
@@ -167,13 +163,15 @@
     return total
 
 
-def gather_rows(own, tokens=()):
+def gather_rows(own, tokens=(), later=()):
     size = lax.axis_size("narrow")
     half = own.shape[0] // 2
     [own] = after([own], tokens)
     across = [swap(own, "narrow", k) for k in range(2, size, 2)]
     beside = swap(own, "wide", 1)
     stage_one = across + [beside]
+    if later:
+        *across, beside = after(across + [beside], later)
     parts, stage_two = [beside], []
     for n, k in enumerate(range(2, size, 2)):
         ends = [swap(across[n][:half], "wide", 1), swap(beside[half:], "narrow", k)]
@@ -185,7 +183,7 @@
     return ([even, odd], [other_even, other_odd]), (stage_one, stage_two, [odd, other_odd])
 
 
-def scatter_rows(even, odd, other_even, other_odd, tokens=()):
+def scatter_rows(even, odd, other_even, other_odd, tokens=(), later=()):
     size = lax.axis_size("narrow")
     rows = even.shape[0] // (size // 2)
     half = rows // 2
@@ -211,7 +209,7 @@
             ).astype(bf16)
         )
     spread.append(jnp.concatenate([beside_top, beside_bottom], axis=0).astype(bf16))
-    spread = lax.optimization_barrier(tuple(spread))
+    spread = after(spread, later) if later else lax.optimization_barrier(tuple(spread))
     for n, k in enumerate(range(2, size, 2)):
         stage_three.append(swap(spread[n], "narrow", k))
         out = out + stage_three[-1].astype(f32)
@@ -245,11 +243,7 @@
     return pl.pallas_call(
         norm_kernel,
         out_shape=jax.ShapeDtypeStruct((rows * len(pieces), width), bf16),
-        cost_estimate=pl.CostEstimate(
-            flops=6 * rows * len(pieces) * width,
-            bytes_accessed=4 * rows * len(pieces) * width,
-            transcendentals=0,
-        ),
+        cost_estimate=light,
         name="norm",
     )(*pieces, gain.reshape(1, width))
 
@@ -258,6 +252,9 @@
     a = grad * gain
     inner = jnp.mean(a * values, axis=-1, keepdims=True)
     return rate * a - values * (rate * rate * rate) * inner
+
+
+light = pl.CostEstimate(flops=1024, bytes_accessed=1024, transcendentals=0)
 
 
 def filter_kernel(base_re, base_im, step_re, step_im, out):
@@ -290,9 +287,7 @@
     return pl.pallas_call(
         filter_kernel,
         out_shape=jax.ShapeDtypeStruct((SPAN, width), f32),
-        cost_estimate=pl.CostEstimate(
-            flops=16 * 7 * SPAN * width, bytes_accessed=4 * SPAN * width, transcendentals=0
-        ),
+        cost_estimate=light,
         name="taps",
     )(base_re, base_im, step_re, step_im)
 
@@ -329,6 +324,48 @@
                 sum_im[j0 + n, :, lanes] = state[4 * n + 1]
                 mom_re[j0 + n, :, lanes] = state[4 * n + 2]
                 mom_im[j0 + n, :, lanes] = state[4 * n + 3]
+
+
+SIDE = 512
+
+
+def product_kernel(a, b, out, turned=None, *, kind):
+    if kind == "tn":
+
+        @pl.when(pl.program_id(0) == 0)
+        def _():
+            turned[...] = a[...].T
+
+        value = nn(turned[...], b[...])
+    else:
+        value = (nn if kind == "nn" else nt)(a[...], b[...])
+    out[...] = value.astype(out.dtype)
+
+
+def product(a, b, kind, dtype, at=0):
+    if kind == "tn":
+        depth, rows = a.shape[0], SIDE
+        a_spec = pl.BlockSpec((depth, SIDE), lambda i: (0, at))
+        scratch = [pltpu.VMEM((SIDE, depth), a.dtype)]
+    else:
+        rows, depth = a.shape
+        a_spec = pl.BlockSpec((rows, depth), lambda i: (0, 0))
+        scratch = []
+    columns = b.shape[0] if kind == "nt" else b.shape[1]
+    if kind == "nt":
+        b_spec = pl.BlockSpec((SIDE, depth), lambda i: (i, 0))
+    else:
+        b_spec = pl.BlockSpec((depth, SIDE), lambda i: (0, i))
+    return pl.pallas_call(
+        partial(product_kernel, kind=kind),
+        grid=(columns // SIDE,),
+        out_shape=jax.ShapeDtypeStruct((rows, columns), dtype),
+        in_specs=[a_spec, b_spec],
+        out_specs=pl.BlockSpec((rows, SIDE), lambda i: (0, i)),
+        scratch_shapes=scratch,
+        cost_estimate=light,
+        name="product",
+    )(a, b)
 
 
 def filter_moments(grad, step_re, step_im):
@@ -528,11 +565,7 @@
             pltpu.VMEM((SPAN, width), bf16),
         ],
         compiler_params=pltpu.CompilerParams(vmem_limit_bytes=40 * 2**20),
-        cost_estimate=pl.CostEstimate(
-            flops=docs * 8 * FREQ * SPAN * width,
-            bytes_accessed=slots * three * 4 + 8 * slots * width,
-            transcendentals=0,
-        ),
+        cost_estimate=light,
         name="mixer_forward",
     )(order, first, count, proj, taps, table, spectrum, fwd, inv)
 
@@ -561,11 +594,7 @@
             pltpu.VMEM((2 * FREQ, width), f32),
         ],
         compiler_params=pltpu.CompilerParams(vmem_limit_bytes=48 * 2**20),
-        cost_estimate=pl.CostEstimate(
-            flops=docs * 10 * FREQ * SPAN * width,
-            bytes_accessed=slots * three * 8 + 8 * slots * width,
-            transcendentals=0,
-        ),
+        cost_estimate=light,
         name="mixer_backward",
     )(order, first, count, proj, d_gated, long_out, seen, taps, table, spectrum, fwd, inv)
 
@@ -621,8 +650,6 @@
     order = picked(jnp.arange(narrow) ^ narrow_at, narrow, jnp.asarray(place_of, jnp.int32))
     narrow_of = jnp.asarray(offsets, jnp.int32) ^ narrow_at
 
-    (first_own, first_other), first_stages = gather_rows(tokens[0])
-
     small = jnp.concatenate(
         [
             short_kernel.reshape(9, own),
@@ -634,9 +661,10 @@
         ],
         axis=0,
     )
-    small_all = gather_small(small)
+    small_pieces = gather_small(small)
+    small_all = jnp.concatenate(small_pieces, axis=1)
+    (first_own, first_other), first_stages = gather_rows(tokens[0], small_pieces[1:])
     gains = small_all[small.shape[0] - 2 :].reshape(2, outer, own)
-    [gains] = after([gains], first_stages[0])
     gains = jnp.stack([gains, swap(gains, "wide", 1)])
     gains = jnp.stack([gains] + [swap(gains, "narrow", k) for k in range(2, narrow, 2)])
     gains = jnp.concatenate([gains, swap(gains, "narrow", 1)], axis=0).astype(f32)
@@ -661,26 +689,28 @@
         return scatter_small([summed[j] for j in range(outer)])
 
     documents = jnp.concatenate([doc_blocks, doc_pad], axis=0)
-    [documents] = after([documents], first_stages[0])
+    [documents] = after([documents], small_pieces[1:])
     documents = (documents, swap(documents, "wide", 1))
     tables = [layout(rules[0], rules[1], slots) for rules in documents]
 
     shards = [w_in.transpose(0, 2, 1).reshape(3 * own, width), w_out, w_down.T, w_gate.T, w_up.T]
     weights = [Gather(shard) for shard in shards]
+    in_all, out_all, down_all, gate_all, up_all = weights
     steps = outer // 2
-
-    def weight_step(at, tokens):
-        active = [weights[i] for i in range(len(weights)) if 0 <= at - i < steps]
-        return ring_step(active, tokens)
-
     last = []
     for at in range(steps - 1):
-        last = weight_step(at, last)
-    last = weight_step(steps - 1, last + first_stages[0])
-    last = weight_step(steps, last + first_stages[1])
-    rows_first = [normed_rows(first_own, gain_first), normed_rows(first_other, gain_first)]
+        last = ring_step([in_all], last)
+    last = ring_step([in_all, out_all], last + first_stages[0])
+    for at in range(1, steps):
+        last = ring_step([out_all], last)
+
+    def normed(pieces):
+        values = jnp.concatenate(pieces, axis=0).astype(f32)
+        return (values * inverse_rms(values) * gain_first).astype(bf16)
+
+    rows_first = [normed(first_own), normed(first_other)]
     rate_first = inverse_rms(source)
-    (upstream_own, upstream_other), _ = gather_rows(upstream_low, first_stages[2])
+    (upstream_own, upstream_other), upstream_stages = gather_rows(upstream_low, first_stages[2])
 
     matrix = transform()
     fwd = jnp.asarray(matrix, bf16)
@@ -714,7 +744,7 @@
     )
     res_re, res_im = res_re[:, 0], -res_im[:, 0]
 
-    in_pieces = [piece.reshape(3, own, width) for piece in weights[0].pieces()]
+    in_pieces = [piece.reshape(3, own, width) for piece in in_all.pieces()]
     in_all = jnp.concatenate(in_pieces, axis=1).reshape(3 * channels, width)
     mixed = []
     for r in range(2):
@@ -724,28 +754,39 @@
             order, first, documents[r][0], proj, taps, table, spectrum, fwd, inv
         )
         mixed.append((proj, gated.reshape(slots, channels), long_out, seen))
-    out_all = jnp.concatenate(weights[1].pieces(), axis=0)
+    out_last = last
+    out_all = jnp.concatenate(out_all.pieces(), axis=0)
     parts = [slice(0, even), slice(even, slots)]
-    shares = [nn(mixed[r][1][p], out_all).astype(bf16) for r in range(2) for p in parts]
-    cores = [swap(shares[n], "narrow", 1) for n in (1, 3)]
-    mixer_out, stages = scatter_rows(shares[0], cores[0], shares[2], cores[1])
+    odds = [nn(mixed[r][1][parts[1]], out_all).astype(bf16) for r in range(2)]
+    cores = [swap(odd, "narrow", 1) for odd in odds]
+    for at in range(steps - 1):
+        last = ring_step([down_all], last)
+    ready = after([mixed[0][1], mixed[1][1]], last + upstream_stages[0])
+    evens = [nn(ready[r][parts[0]], out_all).astype(bf16) for r in range(2)]
+    last_two = last
+    for at in range(1, steps):
+        last_two = ring_step([down_all], last_two, cores)
+    last_three = ring_step([gate_all], last_two)
+    for at in range(1, steps - 1):
+        last_three = ring_step([gate_all], last_three)
+    mixer_out, stages = scatter_rows(
+        evens[0], cores[0], evens[1], cores[1], upstream_stages[1], last_two
+    )
     middle = source + mixer_out
     rate_last = inverse_rms(middle)
     rows_upstream = jnp.concatenate(upstream_own + upstream_other, axis=0)
-    (second_own, second_other), second_stages = gather_rows(
-        (middle * rate_last * gain_last).astype(bf16)
-    )
+    low_second = (middle * rate_last * gain_last).astype(bf16)
+    last_four = ring_step([gate_all], last_three + stages[1])
+    (second_own, second_other), second_stages = gather_rows(low_second, last_three, last_four)
     rows_second = jnp.concatenate(second_own + second_other, axis=0)
-    last = weight_step(steps + 1, last + cores)
-    last = weight_step(steps + 2, last + stages[1])
-    last = weight_step(steps + 3, last + second_stages[1])
-    for at in range(steps + 4, steps + len(weights) - 1):
-        last = weight_step(at, last)
-
-    down_all, gate_all = [jnp.concatenate(weights[i].pieces(), axis=0) for i in (2, 3)]
-    d_hidden = nt(down_all, rows_upstream)
-    gate_pre = nt(gate_all, rows_second)
-    up_pieces = after(weights[4].pieces(), [d_hidden, gate_pre])
+    last = ring_step([up_all], last_four + second_stages[0], second_stages[2])
+    for at in range(1, steps):
+        last = ring_step([up_all], last)
+
+    down_all, gate_all = [jnp.concatenate(w.pieces(), axis=0) for w in (down_all, gate_all)]
+    d_hidden = product(down_all, rows_upstream, "nt", f32)
+    gate_pre = product(gate_all, rows_second, "nt", f32)
+    up_pieces = after(up_all.pieces(), [d_hidden, gate_pre])
     up_all = jnp.concatenate(up_pieces, axis=0)
     up_pre = nt(up_all, rows_second)
     sig = jax.nn.sigmoid(gate_pre)
@@ -753,11 +794,11 @@
     hidden = (silu * up_pre).astype(bf16)
     d_gate = (d_hidden * up_pre * sig * (1.0 + gate_pre * (1.0 - sig))).astype(bf16)
     d_up = (d_hidden * silu).astype(bf16)
-    grad_down = nn(hidden, rows_upstream).astype(bf16)
+    grad_down = product(hidden, rows_upstream, "nn", bf16)
     d_gate, d_up = after([d_gate, d_up], [grad_down])
+    parts = [slice(p, p + even) for p in range(0, 2 * slots, even)]
     grads = [Scatter(jnp.split(grad_down, outer, axis=0))]
     last = ring_step(grads)
-    parts = [slice(p, p + even) for p in range(0, 2 * slots, even)]
 
     def second_share(n, tokens=()):
         one, two = after([d_gate, d_up], tokens)
@@ -766,23 +807,28 @@
 
     odds = [second_share(n) for n in (1, 3)]
     cores = [swap(odd, "narrow", 1) for odd in odds]
-    evens = [second_share(n, last) for n in (0, 2)]
+    evens = [second_share(0), second_share(2, last)]
     d_second, stages = scatter_rows(evens[0], cores[0], evens[1], cores[1])
     upstream = upstream_low.astype(f32)
     d_middle = upstream + norm_back(middle, rate_last, gain_last, d_second)
     (middle_own, middle_other), middle_stages = gather_rows(d_middle.astype(bf16))
     rows_dmiddle = [jnp.concatenate(middle_own, axis=0), jnp.concatenate(middle_other, axis=0)]
-    d_gate, d_up = after([d_gate, d_up], cores)
-    for d in (d_gate, d_up):
-        grads.append(Scatter(jnp.split(nn(d, rows_second).astype(bf16), outer, axis=0)))
+    [d_gate] = after([d_gate], cores + evens)
+    grad_gate = product(d_gate, rows_second, "nn", bf16)
+    [d_up] = after([d_up], stages[0] + [grad_gate])
+    grad_up = product(d_up, rows_second, "nn", bf16)
+    [hidden] = after([hidden], [grad_up])
+    down_shares = [product(hidden, down_all, "tn", bf16, n) for n in (0, 1)]
     for at in range(1, steps):
-        last = ring_step(grads[:1], last + cores)
-    down_last = last
-    last = ring_step(grads[1:], last + stages[0])
+        last = ring_step(grads, last, down_shares)
+    [hidden] = after([hidden], last)
+    down_shares += [product(hidden, down_all, "tn", bf16, n) for n in (2, 3)]
+    pair = [Scatter(jnp.split(grad, outer, axis=0)) for grad in (grad_gate, grad_up)]
+    grads += pair
+    last = ring_step(pair, list(last) + down_shares[:2], middle_stages[0])
     for at in range(1, steps):
-        last = ring_step(grads[1:], last + stages[1])
-    [hidden] = after([hidden], stages[0] + down_last)
-    down_shares = [tn(hidden[:, p], down_all).astype(bf16) for p in parts]
+        last = ring_step(pair, last, middle_stages[2])
+    pair_last = last
     down_shares = after(down_shares, middle_stages[2])
     down_cores = [swap(down_shares[n], "narrow", 1) for n in (1, 3)]
     down_out, down_stages = scatter_rows(
@@ -812,7 +858,8 @@
         d_rows[r] = dz.reshape(slots, 3 * channels)
         d_filter, d_taps = d_filter + d_filter_row, d_taps + d_taps_row
         if r == 0:
-            shares[r] = [nn(d_rows[r][p], in_all).astype(bf16) for p in halves]
+            [ready] = after([d_rows[r]], pair_last)
+            shares[r] = [nn(ready[p], in_all).astype(bf16) for p in halves]
     [ready] = after([d_rows[1]], out_last[0] + down_stages[0])
     odd = nn(ready[halves[1]], in_all).astype(bf16)
     cores = [swap(shares[0][1], "narrow", 1), swap(odd, "narrow", 1)]
@@ -830,8 +877,6 @@
     in_sum = Scatter([chunks[:, j].reshape(3 * own, width) for j in range(outer)])
     last = ring_step([in_sum], last)
     d_filter, *_ = after([d_filter], last + stages[0])
-    for at in range(1, steps):
-        last = ring_step([in_sum], last + stages[0])
     gain_grads = after([jnp.stack([grad_gain_one / gain_first, grad_gain_two])], stages[0])
     gain_share = reduce_gain(gain_grads[0], stages[1])
 
@@ -854,6 +899,9 @@
     ).astype(bf16)
     [small_grad] = after([small_grad], stages[1])
     small_share = scatter_small(jnp.split(small_grad, outer, axis=1))
+
+    for at in range(1, steps):
+        last = ring_step([in_sum], last + stages[0], [gain_share, small_share])
 
     at = 9 + poles
     return (

time: 796 us -> 805 us (1.011)
  Pallas kernels: 74.9 us -> 136 us
  matrix products: 147 us -> 90.8 us
  waiting for transfers between devices: 318 us -> 271 us
  other arithmetic: 70.1 us -> 112 us
  local copies, waits for them, and re-layouts: 74.6 us -> 90 us
    pallas_call x2 -> x9, Pallas kernels: 16.8 us -> 75.7 us  [product(): pl.pallas_call(partial(product_kernel, kind=kind), grid=(columns // SIDE,...]
    ppermute x37 -> x43, waiting for transfers between devices: 212 us -> 164 us  [along(): return lax.ppermute(values, 'wide', pairs)]
    dot_general x11 -> x8, matrix products: 45.5 us -> 22.1 us  [nn(): lax.dot_general(a, b, (((1,), (0,)), ((), ())), preferred_element_type=f32)]
    dot_general x7 -> x5, matrix products: 49.7 us -> 29.8 us  [nt(): lax.dot_general(a, b, (((1,), (1,)), ((), ())), preferred_element_type=f32)]
    dot_general x16 -> x12, matrix products: 47.9 us -> 35.4 us  [tn(): lax.dot_general(a, b, (((0,), (0,)), ((), ())), preferred_element_type=f32)]
    convert_element_type x0 -> x2, other arithmetic: none -> 11.9 us  [the longest x1 11.6 us: normed(): return (values * inverse_rms(values) * gain_first).astype(bf16)]
    unnamed x228 -> x200, local copies, waits for them, and re-layouts: 35.8 us -> 38.6 us
    ppermute x37 -> x43, starting transfers between devices: 51.1 us -> 51.9 us  [along(): return lax.ppermute(values, 'wide', pairs)]
  transfers between devices with their start and end apart: 92 -> 98, of which waited for: 37 -> 42; matrix products, arithmetic and copies ran while one was open for 25% -> 30% of each run, Pallas kernels for 8% -> 16%
where the time goes in v5:
time: 805 us; the launch traced here: 796 us
  waiting for transfers between devices  271 us (34%)
  Pallas kernels  136 us (17%)
  other arithmetic  112 us (14%)
  starting transfers between devices  94.2 us (12%)
  matrix products  90.8 us (11%)
  local copies, waits for them, and re-layouts  90 us (11%)
    ppermute x43, waiting for transfers between devices, along(): return lax.ppermute(values, 'wide', pairs)  164 us
    ppermute x55, waiting for transfers between devices, swap(): return lax.ppermute(values, axis, [(i, i ^ shift) for i in range(size)])  107 us
    pallas_call x9, Pallas kernels, product(): pl.pallas_call(partial(product_kernel, kind=kind), grid=(columns // SIDE,...  75.7 us
    ppermute x43, starting transfers between devices, along(): return lax.ppermute(values, 'wide', pairs)  51.9 us
    ppermute x55, starting transfers between devices, swap(): return lax.ppermute(values, axis, [(i, i ^ shift) for i in range(size)])  42.3 us
    unnamed x200, local copies, waits for them, and re-layouts  38.6 us
    dot_general x12, matrix products, tn(): lax.dot_general(a, b, (((0,), (0,)), ((), ())), preferred_element_type=f32)  35.4 us
    pallas_call x2, Pallas kernels, mixer_backward(): pl.pallas_call(backward_kernel, out_shape=(jax.ShapeDtypeStruct((pieces,...  33.3 us
  transfers between devices with their start and end apart: 98, of which 42 were waited for; matrix products, arithmetic and copies ran while one was open for 30% of the time, Pallas kernels for 16%

profile of v5, /device:TPU:0, one launch (start us, length us, event | category | flops | bytes accessed | tf_op | source)
XLA Modules:
  0.0 796.3 jit_solution(16358299472232538799)
XLA Ops:
  4.5 4.1 collective-permute-start
  28.1 4.1 taps.1
  32.2 3.5 fusion.89.spectrum
  35.7 9.4 %collective-permute-done.13 = s32[2,3]{1,0:T(2,128)S(1)} collective-permute-done((s32[2,3]{1,0:T(2,128)S(1)}, s32[2,3]{1,0:T(2,128)S(1)}, u32[]{:S(2)}, u32[]{:S(2)}) %collective-permute-start.13) | collective-permute-done | bytes 56 | tf_op jit(solution)/shard_map/ppermute | solution.py:42
  69.9 3.8 collective-permute-done.15
  78.7 16.3 %collective-permute-done.11 = bf16[160,2048]{1,0:T(8,128)(2,1)} collective-permute-done((bf16[160,2048]{1,0:T(8,128)(2,1)}, bf16[160,2048]{1,0:T(8,128)(2,1)}, u32[]{:S(2)}, u32[]{:S(2)}) %collective-permute-start.11) | collective-permute-done | bytes 655392 | tf_op jit(solution)/shard_map/ppermute | solution.py:64
  114.3 11.6 %fusion.5 = (bf16[1024,2048]{1,0:T(8,128)(2,1)S(1)}, bf16[1024,2048]{1,0:T(8,128)(2,1)S(1)}) fusion(f32[1024]{0:T(1024)S(1)} %add_rsqrt_fusion, f32[2048]{0:T(1024)S(1)} %mul.468, bf16[512,2048]{1,0:T(8,128)(2,1)S(1)} %collective-permute-done.16, bf16[128,2048]{1,0:T(8,128)(2,1)} %collective-permute-done.15, bf16[128,2048]{1,0:T(8,128)(2,1)} %collective-permute-done.14, ...), kind=kLoop, calls=%fused_computation.9 | loop fusion | flops 41943040 | bytes 16793600 | tf_op jit(solution)/shard_map/convert_element_type | solution.py:709
  126.0 3.5 fusion.90.proj
  129.6 7.1 mixer_forward.3
  139.1 3.5 fusion.88.proj
  142.6 7.3 mixer_forward.2
  169.5 6.5 collective-permute-done.25
  185.1 6.4 collective-permute-done.27
  191.7 4.6 collective-permute-done.28
  208.8 10.7 %collective-permute-done.32 = bf16[256,2048]{1,0:T(8,128)(2,1)S(1)} collective-permute-done((bf16[256,2048]{1,0:T(8,128)(2,1)S(1)}, bf16[256,2048]{1,0:T(8,128)(2,1)S(1)}, u32[]{:S(2)}, u32[]{:S(2)}) %collective-permute-start.32) | collective-permute-done | bytes 1048608 | tf_op jit(solution)/shard_map/ppermute | solution.py:42
  221.8 20.2 %collective-permute-done.33 = bf16[176,2048]{1,0:T(8,128)(2,1)S(1)} collective-permute-done((bf16[176,2048]{1,0:T(8,128)(2,1)S(1)}, bf16[176,2048]{1,0:T(8,128)(2,1)S(1)}, u32[]{:S(2)}, u32[]{:S(2)}) %collective-permute-start.33) | collective-permute-done | bytes 720928 | tf_op jit(solution)/shard_map/ppermute | solution.py:64
  250.1 13.5 %collective-permute-done.36 = bf16[80,2048]{1,0:T(8,128)(2,1)S(1)} collective-permute-done((bf16[80,2048]{1,0:T(8,128)(2,1)S(1)}, bf16[80,2048]{1,0:T(8,128)(2,1)S(1)}, u32[]{:S(2)}, u32[]{:S(2)}) %collective-permute-start.36) | collective-permute-done | bytes 327712 | tf_op jit(solution)/shard_map/ppermute | solution.py:64
  263.6 3.3 collective-permute-done.37
  272.9 7.0 collective-permute-done.40
  292.3 12.0 %collective-permute-done.43 = bf16[176,2048]{1,0:T(8,128)(2,1)S(1)} collective-permute-done((bf16[176,2048]{1,0:T(8,128)(2,1)S(1)}, bf16[176,2048]{1,0:T(8,128)(2,1)S(1)}, u32[]{:S(2)}, u32[]{:S(2)}) %collective-permute-start.43) | collective-permute-done | bytes 720928 | tf_op jit(solution)/shard_map/ppermute | solution.py:64
  304.3 16.1 %collective-permute-done.44 = bf16[176,2048]{1,0:T(8,128)(2,1)S(1)} collective-permute-done((bf16[176,2048]{1,0:T(8,128)(2,1)S(1)}, bf16[176,2048]{1,0:T(8,128)(2,1)S(1)}, u32[]{:S(2)}, u32[]{:S(2)}) %collective-permute-start.44) | collective-permute-done | bytes 720928 | tf_op jit(solution)/shard_map/ppermute | solution.py:64
  327.4 11.3 %product.10 = f32[704,2048]{1,0:T(8,128)} custom-call(bf16[704,2048]{1,0:T(8,128)(2,1)} %constant_dynamic-update-slice_fusion.15.a.b, bf16[2048,2048]{1,0:T(8,128)(2,1)} %constant_dynamic-update-slice_fusion.20.b), custom_call_target="tpu_custom_call" | custom-call | flops 1024 | bytes 1024 | tf_op jit(solution)/shard_map/product/pallas_call | solution.py:359
  338.7 11.0 %product.9 = f32[704,2048]{1,0:T(8,128)} custom-call(bf16[704,2048]{1,0:T(8,128)(2,1)} %constant_dynamic-update-slice_fusion.3.a, bf16[2048,2048]{1,0:T(8,128)(2,1)} %constant_dynamic-update-slice_fusion.8.b), custom_call_target="tpu_custom_call" | custom-call | flops 1024 | bytes 1024 | tf_op jit(solution)/shard_map/product/pallas_call | solution.py:359
  353.2 15.8 %multiply_convert_fusion = (bf16[704,2048]{1,0:T(8,128)(2,1)}, bf16[704,2048]{1,0:T(8,128)(2,1)}, bf16[704,2048]{1,0:T(8,128)(2,1)}) fusion(f32[704,2048]{1,0:T(8,128)S(1)} %copy-done.48, f32[704,2048]{1,0:T(8,128)} %product.9, bf16[704,2048]{1,0:T(8,128)(2,1)S(1)} %constant_dynamic-update-slice_fusion.27, ...), kind=kOutput, calls=%fused_computation.11 | convolution fusion | flops 5927206912 | bytes 31457280 | tf_op jit(solution)/shard_map/dot_general | solution.py:33
  369.0 10.4 %product.11 = bf16[704,2048]{1,0:T(8,128)(2,1)} custom-call(bf16[704,2048]{1,0:T(8,128)(2,1)} %get-tuple-element.174.a, bf16[2048,2048]{1,0:T(8,128)(2,1)} %constant_dynamic-update-slice_fusion.20.b), custom_call_target="tpu_custom_call" | custom-call | flops 1024 | bytes 1024 | tf_op jit(solution)/shard_map/product/pallas_call | solution.py:359
  381.9 3.1 fusion.43
  395.7 14.5 %collective-permute-done.50 = bf16[80,2048]{1,0:T(8,128)(2,1)S(1)} collective-permute-done((bf16[80,2048]{1,0:T(8,128)(2,1)S(1)}, bf16[80,2048]{1,0:T(8,128)(2,1)S(1)}, u32[]{:S(2)}, u32[]{:S(2)}) %collective-permute-start.50) | collective-permute-done | bytes 327712 | tf_op jit(solution)/shard_map/ppermute | solution.py:64
  418.4 4.1 convert_add_fusion.5
  426.6 4.1 convert_add_fusion.4
  430.7 10.3 %product.12 = bf16[704,2048]{1,0:T(8,128)(2,1)} custom-call(bf16[704,2048]{1,0:T(8,128)(2,1)} %get-tuple-element.167.a, bf16[2048,2048]{1,0:T(8,128)(2,1)} %constant_dynamic-update-slice_fusion.8.b), custom_call_target="tpu_custom_call" | custom-call | flops 1024 | bytes 1024 | tf_op jit(solution)/shard_map/product/pallas_call | solution.py:359
  450.3 10.3 %product.13 = bf16[704,2048]{1,0:T(8,128)(2,1)} custom-call(bf16[704,2048]{1,0:T(8,128)(2,1)} %get-tuple-element.168.a, bf16[2048,2048]{1,0:T(8,128)(2,1)} %constant_dynamic-update-slice_fusion.8.b), custom_call_target="tpu_custom_call" | custom-call | flops 1024 | bytes 1024 | tf_op jit(solution)/shard_map/product/pallas_call | solution.py:359
  462.6 9.3 %collective-permute-done.58 = bf16[256,2048]{1,0:T(8,128)(2,1)} collective-permute-done((bf16[256,2048]{1,0:T(8,128)(2,1)}, bf16[256,2048]{1,0:T(8,128)(2,1)}, u32[]{:S(2)}, u32[]{:S(2)}) %collective-permute-start.58) | collective-permute-done | bytes 1048608 | tf_op jit(solution)/shard_map/ppermute | solution.py:42
  472.1 3.7 multiply_reduce_fusion.4
  475.8 4.5 fusion.68
  485.3 5.6 product.14
  490.9 5.6 product.15
  500.1 3.5 collective-permute-done.59
  511.0 18.6 %collective-permute-done.72 = bf16[160,2048]{1,0:T(8,128)(2,1)} collective-permute-done((bf16[160,2048]{1,0:T(8,128)(2,1)}, bf16[160,2048]{1,0:T(8,128)(2,1)}, u32[]{:S(2)}, u32[]{:S(2)}) %collective-permute-start.72) | collective-permute-done | bytes 655392 | tf_op jit(solution)/shard_map/ppermute | solution.py:64
  532.9 3.2 pad_maximum_fusion.11
  543.7 5.6 product.16
  549.3 5.6 product.17
  560.0 3.6 fusion.21
  563.6 16.0 %mixer_backward.2 = (bf16[4,256,768]{2,1,0:T(8,128)(2,1)}, f32[512,256]{1,0:T(8,128)S(1)}, f32[8,768]{1,0:T(8,128)S(1)}) custom-call(s32[4]{0:T(128)S(1)} %select_reduce_fusion.7.order, s32[3]{0:T(128)S(1)} %get-tuple-element.257.first, s32[3]{0:T(128)S(1)} %get-tuple-element.354.count, f32[4,256,768]{2,1,0:T(8,128)} %copy-done.3, ...), custom_call_target="tpu_custom_call" | custom-call | flops 1024 | bytes 1024 | tf_op jit(solution)/shard_map/mixer_backward/pallas_call | solution.py:578
  580.1 24.0 %collective-permute-done.74 = bf16[352,2048]{1,0:T(8,128)(2,1)} collective-permute-done((bf16[352,2048]{1,0:T(8,128)(2,1)}, bf16[352,2048]{1,0:T(8,128)(2,1)}, u32[]{:S(2)}, u32[]{:S(2)}) %collective-permute-start.74) | collective-permute-done | bytes 1441824 | tf_op jit(solution)/shard_map/ppermute | solution.py:64
  604.2 4.5 add_bitcast_fusion.1
  608.7 3.2 constant_dynamic-update-slice_fusion.31
  611.9 3.5 fusion.92
  615.4 3.6 fusion.7
  630.1 3.5 fusion.91
  633.6 8.0 %collective-permute-done.79 = bf16[64,2048]{1,0:T(8,128)(2,1)S(1)} collective-permute-done((bf16[64,2048]{1,0:T(8,128)(2,1)S(1)}, bf16[64,2048]{1,0:T(8,128)(2,1)S(1)}, u32[]{:S(2)}, u32[]{:S(2)}) %collective-permute-start.79) | collective-permute-done | bytes 262176 | tf_op jit(solution)/shard_map/ppermute | solution.py:64
  651.7 3.2 convert_add_fusion.1
  654.8 17.3 %mixer_backward.3 = (bf16[4,256,768]{2,1,0:T(8,128)(2,1)}, f32[512,256]{1,0:T(8,128)S(1)}, f32[8,768]{1,0:T(8,128)S(1)}) custom-call(s32[4]{0:T(128)S(1)} %select_reduce_fusion.7.order, s32[3]{0:T(128)S(1)} %get-tuple-element.253.first, s32[3]{0:T(128)S(1)} %get-tuple-element.352.count, f32[4,256,768]{2,1,0:T(8,128)} %copy-done.2, ...), custom_call_target="tpu_custom_call" | custom-call | flops 1024 | bytes 1024 | tf_op jit(solution)/shard_map/mixer_backward/pallas_call | solution.py:578
  674.5 4.1 convolution_convert_fusion.5
  678.7 3.5 fusion.93
  682.2 3.9 add_convert_fusion
  694.8 4.3 collective-permute-done.85
  700.1 7.9 collective-permute-done.86
  709.1 7.9 collective-permute-done.70
  719.9 3.9 convert_add_fusion
  728.7 8.5 %collective-permute-done.81 = bf16[128,2048]{1,0:T(8,128)(2,1)S(1)} collective-permute-done((bf16[128,2048]{1,0:T(8,128)(2,1)S(1)}, bf16[128,2048]{1,0:T(8,128)(2,1)S(1)}, u32[]{:S(2)}, u32[]{:S(2)}) %collective-permute-start.81) | collective-permute-done | bytes 524320 | tf_op jit(solution)/shard_map/ppermute | solution.py:42
  747.0 8.2 %moments.1 = (f32[16,8,256]{2,1,0:T(8,128)}, f32[16,8,256]{2,1,0:T(8,128)}, f32[16,8,256]{2,1,0:T(8,128)}, f32[16,8,256]{2,1,0:T(8,128)}) custom-call(f32[512,256]{1,0:T(8,128)} %add.391.grad, f32[16,8,256]{2,1,0:T(8,128)} %broadcast_in_dim.201.step_re, f32[16,8,256]{2,1,0:T(8,128)} %broadcast_in_dim.202.step_im), custom_call_target="tpu_custom_call" | custom-call | flops 31457280 | bytes 524288 | tf_op jit(solution)/shard_map/moments/pallas_call | solution.py:374
  758.5 11.6 %collective-permute-done.90 = f32[2,4,2,64]{3,1,2,0:T(4,128)S(1)} collective-permute-done((f32[2,4,2,64]{3,1,2,0:T(4,128)S(1)}, f32[2,4,2,64]{3,1,2,0:T(4,128)S(1)}, u32[]{:S(2)}, u32[]{:S(2)}) %collective-permute-start.90) | collective-permute-done | bytes 4128 | tf_op jit(solution)/shard_map/ppermute | solution.py:42
  781.0 3.4 fusion.24
  792.9 3.1 fusion.22
  (574 shorter events, 297.8 us)
Async XLA Ops:
  11.6 43.5 %collective-permute-start.9 = (bf16[192,2048]{1,0:T(8,128)(2,1)}, bf16[192,2048]{1,0:T(8,128)(2,1)}, u32[]{:S(2)}, u32[]{:S(2)}) collective-permute-start(bf16[192,2048]{1,0:T(8,128)(2,1)} %bitcast.213), channel_id=1, source_target_pairs={{0,8},{4,12},{16,0},{20,4},{24,16},{28,20},{8,24},{12,28},{1,9},{5... | collective-permute-start | bytes 2359304 | tf_op jit(solution)/shard_map/ppermute | solution.py:64
  12.0 44.2 %collective-permute-start.8 = (bf16[192,2048]{1,0:T(8,128)(2,1)}, bf16[192,2048]{1,0:T(8,128)(2,1)}, u32[]{:S(2)}, u32[]{:S(2)}) collective-permute-start(bf16[192,2048]{1,0:T(8,128)(2,1)} %bitcast.214), channel_id=1, source_target_pairs={{0,16},{4,20},{16,24},{20,28},{24,8},{28,12},{8,0},{12,4},{1,17},{... | collective-permute-start | bytes 2359304 | tf_op jit(solution)/shard_map/ppermute | solution.py:64
  21.2 36.0 %collective-permute-start.10 = (bf16[256,2048]{1,0:T(8,128)(2,1)}, bf16[256,2048]{1,0:T(8,128)(2,1)}, u32[]{:S(2)}, u32[]{:S(2)}) collective-permute-start(bf16[256,2048]{1,0:T(8,128)(2,1)} %bitcast.188), channel_id=1, source_target_pairs={{0,4},{4,0},{8,12},{12,8},{16,20},{20,16},{24,28},{28,24},{1,5},{5... | collective-permute-start | bytes 3145736 | tf_op jit(solution)/shard_map/ppermute | solution.py:42
  22.8 37.8 %collective-permute-start.3 = (bf16[256,2048]{1,0:T(8,128)(2,1)}, bf16[256,2048]{1,0:T(8,128)(2,1)}, u32[]{:S(2)}, u32[]{:S(2)}) collective-permute-start(bf16[256,2048]{1,0:T(8,128)(2,1)} %bitcast.189), channel_id=1, source_target_pairs={{0,2},{1,3},{2,0},{3,1},{4,6},{5,7},{6,4},{7,5},{8,10},{9,11},{10,... | collective-permute-start | bytes 3145736 | tf_op jit(solution)/shard_map/ppermute | solution.py:42
  24.6 20.5 %collective-permute-start.13 = (s32[2,3]{1,0:T(2,128)S(1)}, s32[2,3]{1,0:T(2,128)S(1)}, u32[]{:S(2)}, u32[]{:S(2)}) collective-permute-start(s32[2,3]{1,0:T(2,128)S(1)} %pad_add_fusion), channel_id=1, source_target_pairs={{0,4},{4,0},{8,12},{12,8},{16,20},{20,16},{24,28},{28,24},{1,5},{5... | collective-permute-start | bytes 80 | tf_op jit(solution)/shard_map/ppermute | solution.py:42
  65.3 31.9 %collective-permute-start.12 = (bf16[160,2048]{1,0:T(8,128)(2,1)}, bf16[160,2048]{1,0:T(8,128)(2,1)}, u32[]{:S(2)}, u32[]{:S(2)}) collective-permute-start(bf16[160,2048]{1,0:T(8,128)(2,1)} %get-tuple-element.127), channel_id=1, source_target_pairs={{0,8},{4,12},{16,0},{20,4},{24,16},{28,20},{8,24},{12,28},{1,9},{5... | collective-permute-start | bytes 1966088 | tf_op jit(solution)/shard_map/ppermute | solution.py:64
  65.3 29.8 %collective-permute-start.11 = (bf16[160,2048]{1,0:T(8,128)(2,1)}, bf16[160,2048]{1,0:T(8,128)(2,1)}, u32[]{:S(2)}, u32[]{:S(2)}) collective-permute-start(bf16[160,2048]{1,0:T(8,128)(2,1)} %get-tuple-element.126), channel_id=1, source_target_pairs={{0,16},{4,20},{16,24},{20,28},{24,8},{28,12},{8,0},{12,4},{1,17},{... | collective-permute-start | bytes 1966088 | tf_op jit(solution)/shard_map/ppermute | solution.py:64
  69.9 38.7 %collective-permute-start.4 = (bf16[512,2048]{1,0:T(8,128)(2,1)S(1)}, bf16[512,2048]{1,0:T(8,128)(2,1)S(1)}, u32[]{:S(2)}, u32[]{:S(2)}) collective-permute-start(bf16[512,2048]{1,0:T(8,128)(2,1)S(1)} %pad_maximum_fusion.4), channel_id=1, source_target_pairs={{0,1},{1,0},{2,3},{3,2},{4,5},{5,4},{6,7},{7,6},{8,9},{9,8},{10,11... | collective-permute-start | bytes 6291464 | tf_op jit(solution)/shard_map/ppermute | solution.py:42
  78.7 32.3 %collective-permute-start.16 = (bf16[512,2048]{1,0:T(8,128)(2,1)S(1)}, bf16[512,2048]{1,0:T(8,128)(2,1)S(1)}, u32[]{:S(2)}, u32[]{:S(2)}) collective-permute-start(bf16[512,2048]{1,0:T(8,128)(2,1)S(1)} %pad_maximum_fusion.5), channel_id=1, source_target_pairs={{0,1},{1,0},{2,3},{3,2},{4,5},{5,4},{6,7},{7,6},{8,9},{9,8},{10,11... | collective-permute-start | bytes 6291464 | tf_op jit(solution)/shard_map/ppermute | solution.py:42
  106.5 45.6 %collective-permute-start.19 = (bf16[176,2048]{1,0:T(8,128)(2,1)}, bf16[176,2048]{1,0:T(8,128)(2,1)S(1)}, u32[]{:S(2)}, u32[]{:S(2)}) collective-permute-start(bf16[176,2048]{1,0:T(8,128)(2,1)} %bitcast.38), channel_id=1, source_target_pairs={{0,16},{4,20},{16,24},{20,28},{24,8},{28,12},{8,0},{12,4},{1,17},{... | collective-permute-start | bytes 2162696 | tf_op jit(solution)/shard_map/ppermute | solution.py:64
  108.1 49.1 %collective-permute-start.20 = (bf16[176,2048]{1,0:T(8,128)(2,1)}, bf16[176,2048]{1,0:T(8,128)(2,1)}, u32[]{:S(2)}, u32[]{:S(2)}) collective-permute-start(bf16[176,2048]{1,0:T(8,128)(2,1)} %bitcast.38), channel_id=1, source_target_pairs={{0,8},{4,12},{16,0},{20,4},{24,16},{28,20},{8,24},{12,28},{1,9},{5... | collective-permute-start | bytes 2162696 | tf_op jit(solution)/shard_map/ppermute | solution.py:64
  111.0 49.8 %collective-permute-start.21 = (bf16[256,2048]{1,0:T(8,128)(2,1)}, bf16[256,2048]{1,0:T(8,128)(2,1)}, u32[]{:S(2)}, u32[]{:S(2)}) collective-permute-start(bf16[256,2048]{1,0:T(8,128)(2,1)} %bitcast.39), channel_id=1, source_target_pairs={{0,2},{1,3},{2,0},{3,1},{4,6},{5,7},{6,4},{7,5},{8,10},{9,11},{10,... | collective-permute-start | bytes 3145736 | tf_op jit(solution)/shard_map/ppermute | solution.py:42
  111.6 51.9 %collective-permute-start.22 = (bf16[256,2048]{1,0:T(8,128)(2,1)}, bf16[256,2048]{1,0:T(8,128)(2,1)}, u32[]{:S(2)}, u32[]{:S(2)}) collective-permute-start(bf16[256,2048]{1,0:T(8,128)(2,1)} %bitcast.39), channel_id=1, source_target_pairs={{0,4},{4,0},{8,12},{12,8},{16,20},{20,16},{24,28},{28,24},{1,5},{5... | collective-permute-start | bytes 3145736 | tf_op jit(solution)/shard_map/ppermute | solution.py:42
  139.1 28.0 %collective-permute-start.24 = (bf16[512,2048]{1,0:T(8,128)(2,1)}, bf16[512,2048]{1,0:T(8,128)(2,1)}, u32[]{:S(2)}, u32[]{:S(2)}) collective-permute-start(bf16[512,2048]{1,0:T(8,128)(2,1)} %convolution_convert_fusion), channel_id=1, source_target_pairs={{0,1},{1,0},{2,3},{3,2},{4,5},{5,4},{6,7},{7,6},{8,9},{9,8},{10,11... | collective-permute-start | bytes 6291464 | tf_op jit(solution)/shard_map/ppermute | solution.py:42
  152.2 29.0 %collective-permute-start.23 = (bf16[512,2048]{1,0:T(8,128)(2,1)}, bf16[512,2048]{1,0:T(8,128)(2,1)}, u32[]{:S(2)}, u32[]{:S(2)}) collective-permute-start(bf16[512,2048]{1,0:T(8,128)(2,1)} %convolution_convert_fusion.2), channel_id=1, source_target_pairs={{0,1},{1,0},{2,3},{3,2},{4,5},{5,4},{6,7},{7,6},{8,9},{9,8},{10,11... | collective-permute-start | bytes 6291464 | tf_op jit(solution)/shard_map/ppermute | solution.py:42
  158.3 26.8 %collective-permute-start.29 = (bf16[96,2048]{1,0:T(8,128)(2,1)S(1)}, bf16[96,2048]{1,0:T(8,128)(2,1)S(1)}, u32[]{:S(2)}, u32[]{:S(2)}) collective-permute-start(bf16[96,2048]{1,0:T(8,128)(2,1)S(1)} %slice.713), channel_id=1, source_target_pairs={{0,16},{4,20},{16,24},{20,28},{24,8},{28,12},{8,0},{12,4},{1,17},{... | collective-permute-start | bytes 1179656 | tf_op jit(solution)/shard_map/ppermute | solution.py:64
  167.1 18.0 %collective-permute-start.30 = (bf16[80,2048]{1,0:T(8,128)(2,1)S(1)}, bf16[80,2048]{1,0:T(8,128)(2,1)S(1)}, u32[]{:S(2)}, u32[]{:S(2)}) collective-permute-start(bf16[80,2048]{1,0:T(8,128)(2,1)S(1)} %slice.714), channel_id=1, source_target_pairs={{0,8},{4,12},{16,0},{20,4},{24,16},{28,20},{8,24},{12,28},{1,9},{5... | collective-permute-start | bytes 983048 | tf_op jit(solution)/shard_map/ppermute | solution.py:64
  196.5 23.1 %collective-permute-start.32 = (bf16[256,2048]{1,0:T(8,128)(2,1)S(1)}, bf16[256,2048]{1,0:T(8,128)(2,1)S(1)}, u32[]{:S(2)}, u32[]{:S(2)}) collective-permute-start(bf16[256,2048]{1,0:T(8,128)(2,1)S(1)} %pad_maximum_fusion.17), channel_id=1, source_target_pairs={{0,4},{4,0},{8,12},{12,8},{16,20},{20,16},{24,28},{28,24},{1,5},{5... | collective-permute-start | bytes 3145736 | tf_op jit(solution)/shard_map/ppermute | solution.py:42
  198.0 22.7 %collective-permute-start.31 = (bf16[256,2048]{1,0:T(8,128)(2,1)S(1)}, bf16[256,2048]{1,0:T(8,128)(2,1)S(1)}, u32[]{:S(2)}, u32[]{:S(2)}) collective-permute-start(bf16[256,2048]{1,0:T(8,128)(2,1)S(1)} %pad_maximum_fusion.16), channel_id=1, source_target_pairs={{0,2},{1,3},{2,0},{3,1},{4,6},{5,7},{6,4},{7,5},{8,10},{9,11},{10,... | collective-permute-start | bytes 3145736 | tf_op jit(solution)/shard_map/ppermute | solution.py:42
  203.7 42.4 %collective-permute-start.47 = (bf16[512,2048]{1,0:T(8,128)(2,1)S(1)}, bf16[512,2048]{1,0:T(8,128)(2,1)S(1)}, u32[]{:S(2)}, u32[]{:S(2)}) collective-permute-start(bf16[512,2048]{1,0:T(8,128)(2,1)S(1)} %pad_maximum_fusion.8), channel_id=1, source_target_pairs={{0,1},{1,0},{2,3},{3,2},{4,5},{5,4},{6,7},{7,6},{8,9},{9,8},{10,11... | collective-permute-start | bytes 6291464 | tf_op jit(solution)/shard_map/ppermute | solution.py:42
  207.9 74.6 %collective-permute-start.48 = (bf16[512,2048]{1,0:T(8,128)(2,1)S(1)}, bf16[512,2048]{1,0:T(8,128)(2,1)S(1)}, u32[]{:S(2)}, u32[]{:S(2)}) collective-permute-start(bf16[512,2048]{1,0:T(8,128)(2,1)S(1)} %pad_maximum_fusion.9), channel_id=1, source_target_pairs={{0,1},{1,0},{2,3},{3,2},{4,5},{5,4},{6,7},{7,6},{8,9},{9,8},{10,11... | collective-permute-start | bytes 6291464 | tf_op jit(solution)/shard_map/ppermute | solution.py:42
  208.3 33.6 %collective-permute-start.33 = (bf16[176,2048]{1,0:T(8,128)(2,1)S(1)}, bf16[176,2048]{1,0:T(8,128)(2,1)S(1)}, u32[]{:S(2)}, u32[]{:S(2)}) collective-permute-start(bf16[176,2048]{1,0:T(8,128)(2,1)S(1)} %bitcast.216), channel_id=1, source_target_pairs={{0,16},{4,20},{16,24},{20,28},{24,8},{28,12},{8,0},{12,4},{1,17},{... | collective-permute-start | bytes 2162696 | tf_op jit(solution)/shard_map/ppermute | solution.py:64
  219.5 22.4 %collective-permute-start.34 = (bf16[176,2048]{1,0:T(8,128)(2,1)S(1)}, bf16[176,2048]{1,0:T(8,128)(2,1)S(1)}, u32[]{:S(2)}, u32[]{:S(2)}) collective-permute-start(bf16[176,2048]{1,0:T(8,128)(2,1)S(1)} %bitcast.217), channel_id=1, source_target_pairs={{0,8},{4,12},{16,0},{20,4},{24,16},{28,20},{8,24},{12,28},{1,9},{5... | collective-permute-start | bytes 2162696 | tf_op jit(solution)/shard_map/ppermute | solution.py:64
  242.0 25.0 %collective-permute-start.37 = (bf16[256,2048]{1,0:T(8,128)(2,1)S(1)}, bf16[256,2048]{1,0:T(8,128)(2,1)S(1)}, u32[]{:S(2)}, u32[]{:S(2)}) collective-permute-start(bf16[256,2048]{1,0:T(8,128)(2,1)S(1)} %multiply_convert_fusion.3), channel_id=1, source_target_pairs={{0,2},{1,3},{2,0},{3,1},{4,6},{5,7},{6,4},{7,5},{8,10},{9,11},{10,... | collective-permute-start | bytes 3145736 | tf_op jit(solution)/shard_map/ppermute | solution.py:42
  242.5 24.7 %collective-permute-start.38 = (bf16[256,2048]{1,0:T(8,128)(2,1)S(1)}, bf16[256,2048]{1,0:T(8,128)(2,1)S(1)}, u32[]{:S(2)}, u32[]{:S(2)}) collective-permute-start(bf16[256,2048]{1,0:T(8,128)(2,1)S(1)} %multiply_convert_fusion.3), channel_id=1, source_target_pairs={{0,4},{4,0},{8,12},{12,8},{16,20},{20,16},{24,28},{28,24},{1,5},{5... | collective-permute-start | bytes 3145736 | tf_op jit(solution)/shard_map/ppermute | solution.py:42
  245.5 18.1 %collective-permute-start.35 = (bf16[96,2048]{1,0:T(8,128)(2,1)S(1)}, bf16[96,2048]{1,0:T(8,128)(2,1)S(1)}, u32[]{:S(2)}, u32[]{:S(2)}) collective-permute-start(bf16[96,2048]{1,0:T(8,128)(2,1)S(1)} %slice.715), channel_id=1, source_target_pairs={{0,16},{4,20},{16,24},{20,28},{24,8},{28,12},{8,0},{12,4},{1,17},{... | collective-permute-start | bytes 1179656 | tf_op jit(solution)/shard_map/ppermute | solution.py:64
  269.6 19.1 %collective-permute-start.39 = (bf16[512,2048]{1,0:T(8,128)(2,1)S(1)}, bf16[512,2048]{1,0:T(8,128)(2,1)S(1)}, u32[]{:S(2)}, u32[]{:S(2)}) collective-permute-start(bf16[512,2048]{1,0:T(8,128)(2,1)S(1)} %pad_maximum_fusion.6), channel_id=1, source_target_pairs={{0,1},{1,0},{2,3},{3,2},{4,5},{5,4},{6,7},{7,6},{8,9},{9,8},{10,11... | collective-permute-start | bytes 6291464 | tf_op jit(solution)/shard_map/ppermute | solution.py:42
  280.5 39.9 %collective-permute-start.42 = (bf16[512,2048]{1,0:T(8,128)(2,1)S(1)}, bf16[512,2048]{1,0:T(8,128)(2,1)S(1)}, u32[]{:S(2)}, u32[]{:S(2)}) collective-permute-start(bf16[512,2048]{1,0:T(8,128)(2,1)S(1)} %pad_maximum_fusion.7), channel_id=1, source_target_pairs={{0,1},{1,0},{2,3},{3,2},{4,5},{5,4},{6,7},{7,6},{8,9},{9,8},{10,11... | collective-permute-start | bytes 6291464 | tf_op jit(solution)/shard_map/ppermute | solution.py:42
  285.7 18.6 %collective-permute-start.43 = (bf16[176,2048]{1,0:T(8,128)(2,1)S(1)}, bf16[176,2048]{1,0:T(8,128)(2,1)S(1)}, u32[]{:S(2)}, u32[]{:S(2)}) collective-permute-start(bf16[176,2048]{1,0:T(8,128)(2,1)S(1)} %bitcast.219), channel_id=1, source_target_pairs={{0,16},{4,20},{16,24},{20,28},{24,8},{28,12},{8,0},{12,4},{1,17},{... | collective-permute-start | bytes 2162696 | tf_op jit(solution)/shard_map/ppermute | solution.py:64
  285.7 34.7 %collective-permute-start.44 = (bf16[176,2048]{1,0:T(8,128)(2,1)S(1)}, bf16[176,2048]{1,0:T(8,128)(2,1)S(1)}, u32[]{:S(2)}, u32[]{:S(2)}) collective-permute-start(bf16[176,2048]{1,0:T(8,128)(2,1)S(1)} %bitcast.220), channel_id=1, source_target_pairs={{0,8},{4,12},{16,0},{20,4},{24,16},{28,20},{8,24},{12,28},{1,9},{5... | collective-permute-start | bytes 2162696 | tf_op jit(solution)/shard_map/ppermute | solution.py:64
  322.0 27.7 %collective-permute-start.46 = (bf16[80,2048]{1,0:T(8,128)(2,1)}, bf16[80,2048]{1,0:T(8,128)(2,1)}, u32[]{:S(2)}, u32[]{:S(2)}) collective-permute-start(bf16[80,2048]{1,0:T(8,128)(2,1)} %slice.579), channel_id=1, source_target_pairs={{0,8},{4,12},{16,0},{20,4},{24,16},{28,20},{8,24},{12,28},{1,9},{5... | collective-permute-start | bytes 983048 | tf_op jit(solution)/shard_map/ppermute | solution.py:64
  322.0 27.7 %collective-permute-start.45 = (bf16[96,2048]{1,0:T(8,128)(2,1)}, bf16[96,2048]{1,0:T(8,128)(2,1)}, u32[]{:S(2)}, u32[]{:S(2)}) collective-permute-start(bf16[96,2048]{1,0:T(8,128)(2,1)} %slice.578), channel_id=1, source_target_pairs={{0,16},{4,20},{16,24},{20,28},{24,8},{28,12},{8,0},{12,4},{1,17},{... | collective-permute-start | bytes 1179656 | tf_op jit(solution)/shard_map/ppermute | solution.py:64
  391.6 26.8 %collective-permute-start.51 = (bf16[512,2048]{1,0:T(8,128)(2,1)S(1)}, bf16[512,2048]{1,0:T(8,128)(2,1)S(1)}, u32[]{:S(2)}, u32[]{:S(2)}) collective-permute-start(bf16[512,2048]{1,0:T(8,128)(2,1)S(1)} %add_convert_fusion.3), channel_id=1, source_target_pairs={{0,1},{1,0},{2,3},{3,2},{4,5},{5,4},{6,7},{7,6},{8,9},{9,8},{10,11... | collective-permute-start | bytes 6291464 | tf_op jit(solution)/shard_map/ppermute | solution.py:42
  391.7 20.5 %collective-permute-start.49 = (bf16[96,2048]{1,0:T(8,128)(2,1)S(1)}, bf16[96,2048]{1,0:T(8,128)(2,1)S(1)}, u32[]{:S(2)}, u32[]{:S(2)}) collective-permute-start(bf16[96,2048]{1,0:T(8,128)(2,1)S(1)} %get-tuple-element.163), channel_id=1, source_target_pairs={{0,16},{4,20},{16,24},{20,28},{24,8},{28,12},{8,0},{12,4},{1,17},{... | collective-permute-start | bytes 1179656 | tf_op jit(solution)/shard_map/ppermute | solution.py:64
  391.8 18.5 %collective-permute-start.50 = (bf16[80,2048]{1,0:T(8,128)(2,1)S(1)}, bf16[80,2048]{1,0:T(8,128)(2,1)S(1)}, u32[]{:S(2)}, u32[]{:S(2)}) collective-permute-start(bf16[80,2048]{1,0:T(8,128)(2,1)S(1)} %get-tuple-element.164), channel_id=1, source_target_pairs={{0,8},{4,12},{16,0},{20,4},{24,16},{28,20},{8,24},{12,28},{1,9},{5... | collective-permute-start | bytes 983048 | tf_op jit(solution)/shard_map/ppermute | solution.py:64
  395.7 30.9 %collective-permute-start.54 = (bf16[512,2048]{1,0:T(8,128)(2,1)S(1)}, bf16[512,2048]{1,0:T(8,128)(2,1)S(1)}, u32[]{:S(2)}, u32[]{:S(2)}) collective-permute-start(bf16[512,2048]{1,0:T(8,128)(2,1)S(1)} %add_convert_fusion.2), channel_id=1, source_target_pairs={{0,1},{1,0},{2,3},{3,2},{4,5},{5,4},{6,7},{7,6},{8,9},{9,8},{10,11... | collective-permute-start | bytes 6291464 | tf_op jit(solution)/shard_map/ppermute | solution.py:42
  414.3 82.3 %collective-permute-start.55 = (bf16[176,2048]{1,0:T(8,128)(2,1)}, bf16[176,2048]{1,0:T(8,128)(2,1)}, u32[]{:S(2)}, u32[]{:S(2)}) collective-permute-start(bf16[176,2048]{1,0:T(8,128)(2,1)} %pad_maximum_fusion.31), channel_id=1, source_target_pairs={{0,16},{4,20},{16,24},{20,28},{24,8},{28,12},{8,0},{12,4},{1,17},{... | collective-permute-start | bytes 2162696 | tf_op jit(solution)/shard_map/ppermute | solution.py:64
  414.9 81.7 %collective-permute-start.56 = (bf16[176,2048]{1,0:T(8,128)(2,1)}, bf16[176,2048]{1,0:T(8,128)(2,1)}, u32[]{:S(2)}, u32[]{:S(2)}) collective-permute-start(bf16[176,2048]{1,0:T(8,128)(2,1)} %pad_maximum_fusion.32), channel_id=1, source_target_pairs={{0,8},{4,12},{16,0},{20,4},{24,16},{28,20},{8,24},{12,28},{1,9},{5... | collective-permute-start | bytes 2162696 | tf_op jit(solution)/shard_map/ppermute | solution.py:64
  423.6 18.7 %collective-permute-start.52 = (bf16[128,2048]{1,0:T(8,128)(2,1)}, bf16[128,2048]{1,0:T(8,128)(2,1)}, u32[]{:S(2)}, u32[]{:S(2)}) collective-permute-start(bf16[128,2048]{1,0:T(8,128)(2,1)} %get-tuple-element.294), channel_id=1, source_target_pairs={{0,4},{4,0},{8,12},{12,8},{16,20},{20,16},{24,28},{28,24},{1,5},{5... | collective-permute-start | bytes 1572872 | tf_op jit(solution)/shard_map/ppermute | solution.py:42
  425.1 19.7 %collective-permute-start.53 = (bf16[128,2048]{1,0:T(8,128)(2,1)}, bf16[128,2048]{1,0:T(8,128)(2,1)}, u32[]{:S(2)}, u32[]{:S(2)}) collective-permute-start(bf16[128,2048]{1,0:T(8,128)(2,1)} %get-tuple-element.293), channel_id=1, source_target_pairs={{0,2},{1,3},{2,0},{3,1},{4,6},{5,7},{6,4},{7,5},{8,10},{9,11},{10,... | collective-permute-start | bytes 1572872 | tf_op jit(solution)/shard_map/ppermute | solution.py:42
  447.5 24.3 %collective-permute-start.58 = (bf16[256,2048]{1,0:T(8,128)(2,1)}, bf16[256,2048]{1,0:T(8,128)(2,1)}, u32[]{:S(2)}, u32[]{:S(2)}) collective-permute-start(bf16[256,2048]{1,0:T(8,128)(2,1)} %pad_maximum_fusion.19), channel_id=1, source_target_pairs={{0,4},{4,0},{8,12},{12,8},{16,20},{20,16},{24,28},{28,24},{1,5},{5... | collective-permute-start | bytes 3145736 | tf_op jit(solution)/shard_map/ppermute | solution.py:42
  448.0 24.0 %collective-permute-start.57 = (bf16[256,2048]{1,0:T(8,128)(2,1)}, bf16[256,2048]{1,0:T(8,128)(2,1)}, u32[]{:S(2)}, u32[]{:S(2)}) collective-permute-start(bf16[256,2048]{1,0:T(8,128)(2,1)} %pad_maximum_fusion.18), channel_id=1, source_target_pairs={{0,2},{1,3},{2,0},{3,1},{4,6},{5,7},{6,4},{7,5},{8,10},{9,11},{10,... | collective-permute-start | bytes 3145736 | tf_op jit(solution)/shard_map/ppermute | solution.py:42
  480.4 23.2 %collective-permute-start.59 = (bf16[256,2048]{1,0:T(8,128)(2,1)}, bf16[256,2048]{1,0:T(8,128)(2,1)}, u32[]{:S(2)}, u32[]{:S(2)}) collective-permute-start(bf16[256,2048]{1,0:T(8,128)(2,1)} %get-tuple-element.249), channel_id=1, source_target_pairs={{0,2},{1,3},{2,0},{3,1},{4,6},{5,7},{6,4},{7,5},{8,10},{9,11},{10,... | collective-permute-start | bytes 3145736 | tf_op jit(solution)/shard_map/ppermute | solution.py:42
  482.8 23.9 %collective-permute-start.61 = (bf16[256,2048]{1,0:T(8,128)(2,1)}, bf16[256,2048]{1,0:T(8,128)(2,1)}, u32[]{:S(2)}, u32[]{:S(2)}) collective-permute-start(bf16[256,2048]{1,0:T(8,128)(2,1)} %get-tuple-element.249), channel_id=1, source_target_pairs={{0,4},{4,0},{8,12},{12,8},{16,20},{20,16},{24,28},{28,24},{1,5},{5... | collective-permute-start | bytes 3145736 | tf_op jit(solution)/shard_map/ppermute | solution.py:42
  497.5 32.2 %collective-permute-start.71 = (bf16[192,2048]{1,0:T(8,128)(2,1)}, bf16[192,2048]{1,0:T(8,128)(2,1)}, u32[]{:S(2)}, u32[]{:S(2)}) collective-permute-start(bf16[192,2048]{1,0:T(8,128)(2,1)} %pad_maximum_fusion.25), channel_id=1, source_target_pairs={{0,16},{4,20},{16,24},{20,28},{24,8},{28,12},{8,0},{12,4},{1,17},{... | collective-permute-start | bytes 2359304 | tf_op jit(solution)/shard_map/ppermute | solution.py:64
  498.8 30.9 %collective-permute-start.72 = (bf16[160,2048]{1,0:T(8,128)(2,1)}, bf16[160,2048]{1,0:T(8,128)(2,1)}, u32[]{:S(2)}, u32[]{:S(2)}) collective-permute-start(bf16[160,2048]{1,0:T(8,128)(2,1)} %pad_maximum_fusion.33), channel_id=1, source_target_pairs={{0,8},{4,12},{16,0},{20,4},{24,16},{28,20},{8,24},{12,28},{1,9},{5... | collective-permute-start | bytes 1966088 | tf_op jit(solution)/shard_map/ppermute | solution.py:64
  506.7 53.3 %collective-permute-start.60 = (bf16[512,2048]{1,0:T(8,128)(2,1)}, bf16[512,2048]{1,0:T(8,128)(2,1)}, u32[]{:S(2)}, u32[]{:S(2)}) collective-permute-start(bf16[512,2048]{1,0:T(8,128)(2,1)} %pad_maximum_fusion.10), channel_id=1, source_target_pairs={{0,1},{1,0},{2,3},{3,2},{4,5},{5,4},{6,7},{7,6},{8,9},{9,8},{10,11... | collective-permute-start | bytes 6291464 | tf_op jit(solution)/shard_map/ppermute | solution.py:42
  507.8 25.1 %collective-permute-start.63 = (bf16[128,2048]{1,0:T(8,128)(2,1)S(1)}, bf16[128,2048]{1,0:T(8,128)(2,1)S(1)}, u32[]{:S(2)}, u32[]{:S(2)}) collective-permute-start(bf16[128,2048]{1,0:T(8,128)(2,1)S(1)} %slice.732), channel_id=1, source_target_pairs={{0,2},{1,3},{2,0},{3,1},{4,6},{5,7},{6,4},{7,5},{8,10},{9,11},{10,... | collective-permute-start | bytes 1572872 | tf_op jit(solution)/shard_map/ppermute | solution.py:42
  509.5 23.4 %collective-permute-start.62 = (bf16[128,2048]{1,0:T(8,128)(2,1)S(1)}, bf16[128,2048]{1,0:T(8,128)(2,1)S(1)}, u32[]{:S(2)}, u32[]{:S(2)}) collective-permute-start(bf16[128,2048]{1,0:T(8,128)(2,1)S(1)} %slice.731), channel_id=1, source_target_pairs={{0,4},{4,0},{8,12},{12,8},{16,20},{20,16},{24,28},{28,24},{1,5},{5... | collective-permute-start | bytes 1572872 | tf_op jit(solution)/shard_map/ppermute | solution.py:42
  536.1 43.5 %collective-permute-start.64 = (bf16[512,2048]{1,0:T(8,128)(2,1)}, bf16[512,2048]{1,0:T(8,128)(2,1)}, u32[]{:S(2)}, u32[]{:S(2)}) collective-permute-start(bf16[512,2048]{1,0:T(8,128)(2,1)} %pad_maximum_fusion.11), channel_id=1, source_target_pairs={{0,1},{1,0},{2,3},{3,2},{4,5},{5,4},{6,7},{7,6},{8,9},{9,8},{10,11... | collective-permute-start | bytes 6291464 | tf_op jit(solution)/shard_map/ppermute | solution.py:42
  538.7 41.5 %collective-permute-start.73 = (bf16[352,2048]{1,0:T(8,128)(2,1)}, bf16[352,2048]{1,0:T(8,128)(2,1)}, u32[]{:S(2)}, u32[]{:S(2)}) collective-permute-start(bf16[352,2048]{1,0:T(8,128)(2,1)} %pad_maximum_fusion.14), channel_id=1, source_target_pairs={{0,16},{4,20},{16,24},{20,28},{24,8},{28,12},{8,0},{12,4},{1,17},{... | collective-permute-start | bytes 4325384 | tf_op jit(solution)/shard_map/ppermute | solution.py:64
  539.3 64.9 %collective-permute-start.74 = (bf16[352,2048]{1,0:T(8,128)(2,1)}, bf16[352,2048]{1,0:T(8,128)(2,1)}, u32[]{:S(2)}, u32[]{:S(2)}) collective-permute-start(bf16[352,2048]{1,0:T(8,128)(2,1)} %pad_maximum_fusion.15), channel_id=1, source_target_pairs={{0,8},{4,12},{16,0},{20,4},{24,16},{28,20},{8,24},{12,28},{1,9},{5... | collective-permute-start | bytes 4325384 | tf_op jit(solution)/shard_map/ppermute | solution.py:64
  579.6 69.2 %collective-permute-start.65 = (bf16[512,2048]{1,0:T(8,128)(2,1)}, bf16[512,2048]{1,0:T(8,128)(2,1)S(1)}, u32[]{:S(2)}, u32[]{:S(2)}) collective-permute-start(bf16[512,2048]{1,0:T(8,128)(2,1)} %product.15), channel_id=1, source_target_pairs={{0,1},{1,0},{2,3},{3,2},{4,5},{5,4},{6,7},{7,6},{8,9},{9,8},{10,11... | collective-permute-start | bytes 6291464 | tf_op jit(solution)/shard_map/ppermute | solution.py:42
  579.6 62.8 %collective-permute-start.66 = (bf16[512,2048]{1,0:T(8,128)(2,1)S(1)}, bf16[512,2048]{1,0:T(8,128)(2,1)S(1)}, u32[]{:S(2)}, u32[]{:S(2)}) collective-permute-start(bf16[512,2048]{1,0:T(8,128)(2,1)S(1)} %copy-done.53), channel_id=1, source_target_pairs={{0,1},{1,0},{2,3},{3,2},{4,5},{5,4},{6,7},{7,6},{8,9},{9,8},{10,11... | collective-permute-start | bytes 6291464 | tf_op jit(solution)/shard_map/ppermute | solution.py:42
  623.0 28.7 %collective-permute-start.75 = (bf16[512,2048]{1,0:T(8,128)(2,1)S(1)}, bf16[512,2048]{1,0:T(8,128)(2,1)S(1)}, u32[]{:S(2)}, u32[]{:S(2)}) collective-permute-start(bf16[512,2048]{1,0:T(8,128)(2,1)S(1)} %convolution_convert_fusion.6), channel_id=1, source_target_pairs={{0,1},{1,0},{2,3},{3,2},{4,5},{5,4},{6,7},{7,6},{8,9},{9,8},{10,11... | collective-permute-start | bytes 6291464 | tf_op jit(solution)/shard_map/ppermute | solution.py:42
  646.8 27.7 %collective-permute-start.67 = (bf16[128,2048]{1,0:T(8,128)(2,1)}, bf16[128,2048]{1,0:T(8,128)(2,1)}, u32[]{:S(2)}, u32[]{:S(2)}) collective-permute-start(bf16[128,2048]{1,0:T(8,128)(2,1)} %get-tuple-element.291), channel_id=1, source_target_pairs={{0,4},{4,0},{8,12},{12,8},{16,20},{20,16},{24,28},{28,24},{1,5},{5... | collective-permute-start | bytes 1572872 | tf_op jit(solution)/shard_map/ppermute | solution.py:42
  647.4 27.1 %collective-permute-start.68 = (bf16[128,2048]{1,0:T(8,128)(2,1)}, bf16[128,2048]{1,0:T(8,128)(2,1)}, u32[]{:S(2)}, u32[]{:S(2)}) collective-permute-start(bf16[128,2048]{1,0:T(8,128)(2,1)} %get-tuple-element.290), channel_id=1, source_target_pairs={{0,2},{1,3},{2,0},{3,1},{4,6},{5,7},{6,4},{7,5},{8,10},{9,11},{10,... | collective-permute-start | bytes 1572872 | tf_op jit(solution)/shard_map/ppermute | solution.py:42
  678.6 41.3 %collective-permute-start.78 = (bf16[512,2048]{1,0:T(8,128)(2,1)S(1)}, bf16[512,2048]{1,0:T(8,128)(2,1)S(1)}, u32[]{:S(2)}, u32[]{:S(2)}) collective-permute-start(bf16[512,2048]{1,0:T(8,128)(2,1)S(1)} %convolution_convert_fusion.5), channel_id=1, source_target_pairs={{0,1},{1,0},{2,3},{3,2},{4,5},{5,4},{6,7},{7,6},{8,9},{9,8},{10,11... | collective-permute-start | bytes 6291464 | tf_op jit(solution)/shard_map/ppermute | solution.py:42
  691.4 25.6 %collective-permute-start.70 = (bf16[256,2048]{1,0:T(8,128)(2,1)S(1)}, bf16[256,2048]{1,0:T(8,128)(2,1)S(1)}, u32[]{:S(2)}, u32[]{:S(2)}) collective-permute-start(bf16[256,2048]{1,0:T(8,128)(2,1)S(1)} %pad_maximum_fusion.21), channel_id=1, source_target_pairs={{0,4},{4,0},{8,12},{12,8},{16,20},{20,16},{24,28},{28,24},{1,5},{5... | collective-permute-start | bytes 3145736 | tf_op jit(solution)/shard_map/ppermute | solution.py:42
  693.0 25.3 %collective-permute-start.69 = (bf16[256,2048]{1,0:T(8,128)(2,1)S(1)}, bf16[256,2048]{1,0:T(8,128)(2,1)S(1)}, u32[]{:S(2)}, u32[]{:S(2)}) collective-permute-start(bf16[256,2048]{1,0:T(8,128)(2,1)S(1)} %pad_maximum_fusion.20), channel_id=1, source_target_pairs={{0,2},{1,3},{2,0},{3,1},{4,6},{5,7},{6,4},{7,5},{8,10},{9,11},{10,... | collective-permute-start | bytes 3145736 | tf_op jit(solution)/shard_map/ppermute | solution.py:42
  743.0 30.8 %collective-permute-start.84 = (bf16[256,2048]{1,0:T(8,128)(2,1)}, bf16[256,2048]{1,0:T(8,128)(2,1)}, u32[]{:S(2)}, u32[]{:S(2)}) collective-permute-start(bf16[256,2048]{1,0:T(8,128)(2,1)} %pad_maximum_fusion.23), channel_id=1, source_target_pairs={{0,4},{4,0},{8,12},{12,8},{16,20},{20,16},{24,28},{28,24},{1,5},{5... | collective-permute-start | bytes 3145736 | tf_op jit(solution)/shard_map/ppermute | solution.py:42
  744.4 29.3 %collective-permute-start.83 = (bf16[256,2048]{1,0:T(8,128)(2,1)}, bf16[256,2048]{1,0:T(8,128)(2,1)}, u32[]{:S(2)}, u32[]{:S(2)}) collective-permute-start(bf16[256,2048]{1,0:T(8,128)(2,1)} %pad_maximum_fusion.22), channel_id=1, source_target_pairs={{0,2},{1,3},{2,0},{3,1},{4,6},{5,7},{6,4},{7,5},{8,10},{9,11},{10,... | collective-permute-start | bytes 3145736 | tf_op jit(solution)/shard_map/ppermute | solution.py:42
  745.0 47.3 %collective-permute-start.87 = (bf16[192,2048]{1,0:T(8,128)(2,1)}, bf16[192,2048]{1,0:T(8,128)(2,1)}, u32[]{:S(2)}, u32[]{:S(2)}) collective-permute-start(bf16[192,2048]{1,0:T(8,128)(2,1)} %pad_maximum_fusion.26), channel_id=1, source_target_pairs={{0,16},{4,20},{16,24},{20,28},{24,8},{28,12},{8,0},{12,4},{1,17},{... | collective-permute-start | bytes 2359304 | tf_op jit(solution)/shard_map/ppermute | solution.py:64
  745.9 46.4 %collective-permute-start.88 = (bf16[192,2048]{1,0:T(8,128)(2,1)}, bf16[192,2048]{1,0:T(8,128)(2,1)}, u32[]{:S(2)}, u32[]{:S(2)}) collective-permute-start(bf16[192,2048]{1,0:T(8,128)(2,1)} %pad_maximum_fusion.27), channel_id=1, source_target_pairs={{0,8},{4,12},{16,0},{20,4},{24,16},{28,20},{8,24},{12,28},{1,9},{5... | collective-permute-start | bytes 2359304 | tf_op jit(solution)/shard_map/ppermute | solution.py:64
  (119 other events, 1273.1 us)

commit v6 on v5

--- a/solution.py
+++ b/solution.py
@@ -163,7 +163,7 @@
     return total
 
 
-def gather_rows(own, tokens=(), later=()):
+def gather_rows(own, tokens=(), later=(), single=False):
     size = lax.axis_size("narrow")
     half = own.shape[0] // 2
     [own] = after([own], tokens)
@@ -179,7 +179,10 @@
         stage_two += ends
     even = jnp.concatenate([own] + across, axis=0)
     other_even = jnp.concatenate(parts, axis=0)
-    odd, other_odd = swap(even, "narrow", 1), swap(other_even, "narrow", 1)
+    odd = swap(even, "narrow", 1)
+    if single:
+        [other_even] = after([other_even], [odd])
+    other_odd = swap(other_even, "narrow", 1)
     return ([even, odd], [other_even, other_odd]), (stage_one, stage_two, [odd, other_odd])
 
 
@@ -342,26 +345,27 @@
     out[...] = value.astype(out.dtype)
 
 
-def product(a, b, kind, dtype, at=0):
+def product(a, b, kind, dtype, at=None):
     if kind == "tn":
         depth, rows = a.shape[0], SIDE
         a_spec = pl.BlockSpec((depth, SIDE), lambda i: (0, at))
         scratch = [pltpu.VMEM((SIDE, depth), a.dtype)]
     else:
-        rows, depth = a.shape
-        a_spec = pl.BlockSpec((rows, depth), lambda i: (0, 0))
+        rows, depth = a.shape if at is None else (SIDE, a.shape[1])
+        a_spec = pl.BlockSpec((rows, depth), lambda i: (at or 0, 0))
         scratch = []
     columns = b.shape[0] if kind == "nt" else b.shape[1]
+    side = max(s for s in (512, 384, 256, 128, columns) if columns % s == 0 and s <= 512)
     if kind == "nt":
-        b_spec = pl.BlockSpec((SIDE, depth), lambda i: (i, 0))
+        b_spec = pl.BlockSpec((side, depth), lambda i: (i, 0))
     else:
-        b_spec = pl.BlockSpec((depth, SIDE), lambda i: (0, i))
+        b_spec = pl.BlockSpec((depth, side), lambda i: (0, i))
     return pl.pallas_call(
         partial(product_kernel, kind=kind),
-        grid=(columns // SIDE,),
+        grid=(columns // side,),
         out_shape=jax.ShapeDtypeStruct((rows, columns), dtype),
         in_specs=[a_spec, b_spec],
-        out_specs=pl.BlockSpec((rows, SIDE), lambda i: (0, i)),
+        out_specs=pl.BlockSpec((rows, side), lambda i: (0, i)),
         scratch_shapes=scratch,
         cost_estimate=light,
         name="product",
@@ -663,7 +667,7 @@
     )
     small_pieces = gather_small(small)
     small_all = jnp.concatenate(small_pieces, axis=1)
-    (first_own, first_other), first_stages = gather_rows(tokens[0], small_pieces[1:])
+    (first_own, first_other), first_stages = gather_rows(tokens[0])
     gains = small_all[small.shape[0] - 2 :].reshape(2, outer, own)
     gains = jnp.stack([gains, swap(gains, "wide", 1)])
     gains = jnp.stack([gains] + [swap(gains, "narrow", k) for k in range(2, narrow, 2)])
@@ -697,10 +701,10 @@
     weights = [Gather(shard) for shard in shards]
     in_all, out_all, down_all, gate_all, up_all = weights
     steps = outer // 2
-    last = []
+    last = small_pieces[1:]
     for at in range(steps - 1):
         last = ring_step([in_all], last)
-    last = ring_step([in_all, out_all], last + first_stages[0])
+    last = ring_step([in_all, out_all], last)
     for at in range(1, steps):
         last = ring_step([out_all], last)
 
@@ -710,7 +714,9 @@
 
     rows_first = [normed(first_own), normed(first_other)]
     rate_first = inverse_rms(source)
-    (upstream_own, upstream_other), upstream_stages = gather_rows(upstream_low, first_stages[2])
+    (upstream_own, upstream_other), upstream_stages = gather_rows(
+        upstream_low, first_stages[2], (), True
+    )
 
     matrix = transform()
     fwd = jnp.asarray(matrix, bf16)
@@ -749,7 +755,8 @@
     mixed = []
     for r in range(2):
         table, first = tables[r]
-        proj = nt(rows_first[r], in_all).reshape(narrow, local_rows, 3 * channels)
+        proj = product(rows_first[r], in_all, "nt", f32)
+        proj = proj.reshape(narrow, local_rows, 3 * channels)
         gated, long_out, seen = mixer_forward(
             order, first, documents[r][0], proj, taps, table, spectrum, fwd, inv
         )
@@ -757,7 +764,7 @@
     out_last = last
     out_all = jnp.concatenate(out_all.pieces(), axis=0)
     parts = [slice(0, even), slice(even, slots)]
-    odds = [nn(mixed[r][1][parts[1]], out_all).astype(bf16) for r in range(2)]
+    odds = [product(mixed[r][1], out_all, "nn", bf16, 1) for r in range(2)]
     cores = [swap(odd, "narrow", 1) for odd in odds]
     for at in range(steps - 1):
         last = ring_step([down_all], last)
@@ -798,16 +805,15 @@
     d_gate, d_up = after([d_gate, d_up], [grad_down])
     parts = [slice(p, p + even) for p in range(0, 2 * slots, even)]
     grads = [Scatter(jnp.split(grad_down, outer, axis=0))]
-    last = ring_step(grads)
-
-    def second_share(n, tokens=()):
-        one, two = after([d_gate, d_up], tokens)
+
+    def second_share(n):
         p = parts[n]
-        return (tn(one[:, p], gate_all) + tn(two[:, p], up_all)).astype(bf16)
+        return (tn(d_gate[:, p], gate_all) + tn(d_up[:, p], up_all)).astype(bf16)
 
     odds = [second_share(n) for n in (1, 3)]
     cores = [swap(odd, "narrow", 1) for odd in odds]
-    evens = [second_share(0), second_share(2, last)]
+    evens = [second_share(0), second_share(2)]
+    last = ring_step(grads, (), evens)
     d_second, stages = scatter_rows(evens[0], cores[0], evens[1], cores[1])
     upstream = upstream_low.astype(f32)
     d_middle = upstream + norm_back(middle, rate_last, gain_last, d_second)
@@ -820,37 +826,30 @@
     [hidden] = after([hidden], [grad_up])
     down_shares = [product(hidden, down_all, "tn", bf16, n) for n in (0, 1)]
     for at in range(1, steps):
-        last = ring_step(grads, last, down_shares)
-    [hidden] = after([hidden], last)
+        last = ring_step(grads, last, [grad_up])
     down_shares += [product(hidden, down_all, "tn", bf16, n) for n in (2, 3)]
     pair = [Scatter(jnp.split(grad, outer, axis=0)) for grad in (grad_gate, grad_up)]
     grads += pair
-    last = ring_step(pair, list(last) + down_shares[:2], middle_stages[0])
-    for at in range(1, steps):
-        last = ring_step(pair, last, middle_stages[2])
-    pair_last = last
-    down_shares = after(down_shares, middle_stages[2])
+    last = ring_step(pair, last, middle_stages[0])
     down_cores = [swap(down_shares[n], "narrow", 1) for n in (1, 3)]
     down_out, down_stages = scatter_rows(
-        down_shares[0], down_cores[0], down_shares[2], down_cores[1]
+        down_shares[0], down_cores[0], down_shares[2], down_cores[1], middle_stages[1]
     )
     block_output = (middle + down_out).astype(bf16)
     grad_gain_two = jnp.sum(d_second * middle * rate_last, axis=0)
 
     grad_out = sum(tn(mixed[r][1], rows_dmiddle[r]) for r in range(2)).astype(bf16)
-    out_sum = Scatter(jnp.split(grad_out, outer, axis=0))
-    out_last = []
-    for at in range(steps):
-        last = ring_step([out_sum], last)
-        out_last.append(last)
     halves = (slice(0, even), slice(even, slots))
     shares, d_rows, grad_gain_one, d_filter, d_taps = [None, None], [None, None], 0.0, 0.0, 0.0
     for r in range(2):
         proj, gated, long_out, seen = mixed[r]
         table, first = tables[r]
         d_gated = nt(rows_dmiddle[r], out_all).reshape(narrow, local_rows, channels)
+        if r == 0:
+            for at in range(1, steps):
+                last = ring_step(pair[:1], last, [d_gated])
         if r == 1:
-            [d_gated] = after([d_gated], [grad_out, *shares[0], *down_cores])
+            [d_gated] = after([d_gated], [grad_out, *shares[0], *down_stages[1]])
         dz, d_filter_row, d_taps_row = mixer_backward(
             order, first, documents[r][0], proj, d_gated, long_out, seen, taps, table,
             spectrum, fwd, inv,
@@ -858,14 +857,18 @@
         d_rows[r] = dz.reshape(slots, 3 * channels)
         d_filter, d_taps = d_filter + d_filter_row, d_taps + d_taps_row
         if r == 0:
-            [ready] = after([d_rows[r]], pair_last)
+            [ready] = after([d_rows[r]], down_stages[0])
             shares[r] = [nn(ready[p], in_all).astype(bf16) for p in halves]
-    [ready] = after([d_rows[1]], out_last[0] + down_stages[0])
-    odd = nn(ready[halves[1]], in_all).astype(bf16)
+    for at in range(1, steps):
+        last = ring_step(pair[1:], last, [d_rows[1]])
+    out_sum = Scatter(jnp.split(grad_out, outer, axis=0))
+    for at in range(steps):
+        last = ring_step([out_sum], last)
+    odd = nn(d_rows[1][halves[1]], in_all).astype(bf16)
     cores = [swap(shares[0][1], "narrow", 1), swap(odd, "narrow", 1)]
     ready = after(d_rows, [odd])
     grad_in = sum(tn(ready[r], rows_first[r]) for r in range(2)).astype(bf16)
-    [ready] = after([d_rows[1]], [grad_in] + cores + out_last[-1] + down_stages[1])
+    [ready] = after([d_rows[1]], [grad_in] + cores)
     shares[1] = [nn(ready[halves[0]], in_all).astype(bf16), odd]
     d_normed, stages = scatter_rows(shares[0][0], cores[0], shares[1][0], cores[1])
     input_grad = (d_middle + norm_back(source, rate_first, gain_first, d_normed)).astype(bf16)
@@ -875,7 +878,7 @@
             grad_gain_one = grad_gain_one + jnp.sum(share.astype(f32) * rows.astype(f32), axis=0)
     chunks = grad_in.reshape(3, outer, own, width)
     in_sum = Scatter([chunks[:, j].reshape(3 * own, width) for j in range(outer)])
-    last = ring_step([in_sum], last)
+    last = ring_step([in_sum], last, stages[0])
     d_filter, *_ = after([d_filter], last + stages[0])
     gain_grads = after([jnp.stack([grad_gain_one / gain_first, grad_gain_two])], stages[0])
     gain_share = reduce_gain(gain_grads[0], stages[1])
@@ -901,7 +904,7 @@
     small_share = scatter_small(jnp.split(small_grad, outer, axis=1))
 
     for at in range(1, steps):
-        last = ring_step([in_sum], last + stages[0], [gain_share, small_share])
+        last = ring_step([in_sum], last, [gain_share, small_share])
 
     at = 9 + poles
     return (

time: 805 us -> 773 us (0.960)
  waiting for transfers between devices: 271 us -> 206 us
  Pallas kernels: 136 us -> 159 us
  local copies, waits for them, and re-layouts: 90 us -> 108 us
  matrix products: 90.8 us -> 76.3 us
    ppermute x43 -> x45, waiting for transfers between devices: 164 us -> 131 us  [along(): return lax.ppermute(values, 'wide', pairs)]
    ppermute x55, waiting for transfers between devices: 107 us -> 75 us  [swap(): return lax.ppermute(values, axis, [(i, i ^ shift) for i in range(size)])]
    pallas_call x9 -> x13, Pallas kernels: 75.7 us -> 101 us  [product(): pl.pallas_call(partial(product_kernel, kind=kind), grid=(columns // side,...]
    unnamed x200 -> x238, local copies, waits for them, and re-layouts: 38.6 us -> 52.7 us
    dot_general x5 -> x3, matrix products: 29.8 us -> 20.7 us  [nt(): lax.dot_general(a, b, (((1,), (1,)), ((), ())), preferred_element_type=f32)]
    ppermute x43 -> x45, starting transfers between devices: 51.9 us -> 58.1 us  [along(): return lax.ppermute(values, 'wide', pairs)]
    dot_general x8 -> x6, matrix products: 22.1 us -> 17.4 us  [nn(): lax.dot_general(a, b, (((1,), (0,)), ((), ())), preferred_element_type=f32)]
  transfers between devices with their start and end apart: 98 -> 100, of which waited for: 42 -> 29; matrix products, arithmetic and copies ran while one was open for 30% -> 30% of each run, Pallas kernels for 16% -> 17%
where the time goes in v6:
time: 773 us; the launch traced here: 762 us
  waiting for transfers between devices  206 us (27%)
  Pallas kernels  159 us (21%)
  other arithmetic  109 us (14%)
  local copies, waits for them, and re-layouts  108 us (14%)
  starting transfers between devices  100 us (13%)
  matrix products  76.3 us (10%)
    ppermute x45, waiting for transfers between devices, along(): return lax.ppermute(values, 'wide', pairs)  131 us
    pallas_call x13, Pallas kernels, product(): pl.pallas_call(partial(product_kernel, kind=kind), grid=(columns // side,...  101 us
    ppermute x55, waiting for transfers between devices, swap(): return lax.ppermute(values, axis, [(i, i ^ shift) for i in range(size)])  75 us
    ppermute x45, starting transfers between devices, along(): return lax.ppermute(values, 'wide', pairs)  58.1 us
    unnamed x238, local copies, waits for them, and re-layouts  52.7 us
    ppermute x55, starting transfers between devices, swap(): return lax.ppermute(values, axis, [(i, i ^ shift) for i in range(size)])  42.3 us
    dot_general x12, matrix products, tn(): lax.dot_general(a, b, (((0,), (0,)), ((), ())), preferred_element_type=f32)  34.7 us
    pallas_call x2, Pallas kernels, mixer_backward(): pl.pallas_call(backward_kernel, out_shape=(jax.ShapeDtypeStruct((pieces,...  31.4 us
  transfers between devices with their start and end apart: 100, of which 29 were waited for; matrix products, arithmetic and copies ran while one was open for 30% of the time, Pallas kernels for 17%

profile of v6, /device:TPU:0, one launch (start us, length us, event | category | flops | bytes accessed | tf_op | source)
XLA Modules:
  0.0 761.7 jit_solution(10844286648478870052)
XLA Ops:
  1.3 3.1 concatenate.212
  4.5 4.1 collective-permute-start
  8.6 3.0 collective-permute-start.2
  27.1 4.1 taps.1
  31.2 3.5 fusion.87.spectrum
  38.3 2.9 collective-permute-done.6
  42.6 16.5 %collective-permute-done.9 = bf16[192,2048]{1,0:T(8,128)(2,1)S(1)} collective-permute-done((bf16[192,2048]{1,0:T(8,128)(2,1)}, bf16[192,2048]{1,0:T(8,128)(2,1)S(1)}, u32[]{:S(2)}, u32[]{:S(2)}) %collective-permute-start.9) | collective-permute-done | bytes 786464 | tf_op jit(solution)/shard_map/ppermute | solution.py:64
  62.5 2.9 collective-permute-start.10
  72.8 18.9 %collective-permute-done.10 = bf16[160,2048]{1,0:T(8,128)(2,1)} collective-permute-done((bf16[160,2048]{1,0:T(8,128)(2,1)}, bf16[160,2048]{1,0:T(8,128)(2,1)}, u32[]{:S(2)}, u32[]{:S(2)}) %collective-permute-start.10) | collective-permute-done | bytes 655392 | tf_op jit(solution)/shard_map/ppermute | solution.py:64
  101.8 2.9 pad_maximum_fusion.3
  109.4 5.7 fusion.5
  115.1 8.7 %product.14 = f32[1024,768]{1,0:T(8,128)} custom-call(bf16[1024,2048]{1,0:T(8,128)(2,1)} %get-tuple-element.327.a, bf16[768,2048]{1,0:T(8,128)(2,1)} %bitcast.183), custom_call_target="tpu_custom_call" | custom-call | flops 1024 | bytes 1024 | tf_op jit(solution)/shard_map/product/pallas_call | solution.py:363
  126.7 7.1 mixer_forward.3
  136.7 4.3 product.16
  147.2 8.6 %product.13 = f32[1024,768]{1,0:T(8,128)} custom-call(bf16[1024,2048]{1,0:T(8,128)(2,1)} %get-tuple-element.328.a, bf16[768,2048]{1,0:T(8,128)(2,1)} %bitcast.184), custom_call_target="tpu_custom_call" | custom-call | flops 1024 | bytes 1024 | tf_op jit(solution)/shard_map/product/pallas_call | solution.py:363
  158.7 7.1 mixer_forward.2
  168.7 4.3 product.15
  184.7 6.1 collective-permute-done.25
  201.8 14.7 %collective-permute-done.30 = bf16[80,2048]{1,0:T(8,128)(2,1)S(1)} collective-permute-done((bf16[80,2048]{1,0:T(8,128)(2,1)S(1)}, bf16[80,2048]{1,0:T(8,128)(2,1)S(1)}, u32[]{:S(2)}, u32[]{:S(2)}) %collective-permute-start.30) | collective-permute-done | bytes 327712 | tf_op jit(solution)/shard_map/ppermute | solution.py:64
  233.4 10.8 %collective-permute-done.32 = bf16[256,2048]{1,0:T(8,128)(2,1)} collective-permute-done((bf16[256,2048]{1,0:T(8,128)(2,1)}, bf16[256,2048]{1,0:T(8,128)(2,1)}, u32[]{:S(2)}, u32[]{:S(2)}) %collective-permute-start.32) | collective-permute-done | bytes 1048608 | tf_op jit(solution)/shard_map/ppermute | solution.py:42
  249.4 15.9 %collective-permute-done.33 = bf16[176,2048]{1,0:T(8,128)(2,1)S(1)} collective-permute-done((bf16[176,2048]{1,0:T(8,128)(2,1)S(1)}, bf16[176,2048]{1,0:T(8,128)(2,1)S(1)}, u32[]{:S(2)}, u32[]{:S(2)}) %collective-permute-start.33) | collective-permute-done | bytes 720928 | tf_op jit(solution)/shard_map/ppermute | solution.py:64
  274.7 14.4 %collective-permute-done.36 = bf16[80,2048]{1,0:T(8,128)(2,1)S(1)} collective-permute-done((bf16[80,2048]{1,0:T(8,128)(2,1)S(1)}, bf16[80,2048]{1,0:T(8,128)(2,1)S(1)}, u32[]{:S(2)}, u32[]{:S(2)}) %collective-permute-start.36) | collective-permute-done | bytes 327712 | tf_op jit(solution)/shard_map/ppermute | solution.py:64
  295.6 7.6 %collective-permute-done.40 = bf16[128,2048]{1,0:T(8,128)(2,1)S(1)} collective-permute-done((bf16[128,2048]{1,0:T(8,128)(2,1)S(1)}, bf16[128,2048]{1,0:T(8,128)(2,1)S(1)}, u32[]{:S(2)}, u32[]{:S(2)}) %collective-permute-start.40) | collective-permute-done | bytes 524320 | tf_op jit(solution)/shard_map/ppermute | solution.py:42
  317.5 25.7 %collective-permute-done.43 = bf16[176,2048]{1,0:T(8,128)(2,1)S(1)} collective-permute-done((bf16[176,2048]{1,0:T(8,128)(2,1)S(1)}, bf16[176,2048]{1,0:T(8,128)(2,1)S(1)}, u32[]{:S(2)}, u32[]{:S(2)}) %collective-permute-start.43) | collective-permute-done | bytes 720928 | tf_op jit(solution)/shard_map/ppermute | solution.py:64
  350.4 10.9 %product.18 = f32[704,2048]{1,0:T(8,128)} custom-call(bf16[704,2048]{1,0:T(8,128)(2,1)} %constant_dynamic-update-slice_fusion.15.a.b, bf16[2048,2048]{1,0:T(8,128)(2,1)} %constant_dynamic-update-slice_fusion.20.b), custom_call_target="tpu_custom_call" | custom-call | flops 1024 | bytes 1024 | tf_op jit(solution)/shard_map/product/pallas_call | solution.py:363
  361.3 10.9 %product.17 = f32[704,2048]{1,0:T(8,128)} custom-call(bf16[704,2048]{1,0:T(8,128)(2,1)} %constant_dynamic-update-slice_fusion.3.a, bf16[2048,2048]{1,0:T(8,128)(2,1)} %constant_dynamic-update-slice_fusion.8.b), custom_call_target="tpu_custom_call" | custom-call | flops 1024 | bytes 1024 | tf_op jit(solution)/shard_map/product/pallas_call | solution.py:363
  376.8 15.8 %multiply_convert_fusion = (bf16[704,2048]{1,0:T(8,128)(2,1)}, bf16[704,2048]{1,0:T(8,128)(2,1)}, bf16[704,2048]{1,0:T(8,128)(2,1)}) fusion(f32[704,2048]{1,0:T(8,128)S(1)} %copy-done.52, f32[704,2048]{1,0:T(8,128)} %product.17, bf16[704,2048]{1,0:T(8,128)(2,1)S(1)} %constant_dynamic-update-slice_fusion.25, ...), kind=kOutput, calls=%fused_computation.11 | convolution fusion | flops 5927206912 | bytes 31457280 | tf_op jit(solution)/shard_map/dot_general | solution.py:33
  392.6 10.4 %product.19 = bf16[704,2048]{1,0:T(8,128)(2,1)} custom-call(bf16[704,2048]{1,0:T(8,128)(2,1)} %get-tuple-element.166.a, bf16[2048,2048]{1,0:T(8,128)(2,1)} %constant_dynamic-update-slice_fusion.20.b), custom_call_target="tpu_custom_call" | custom-call | flops 1024 | bytes 1024 | tf_op jit(solution)/shard_map/product/pallas_call | solution.py:363
  403.1 4.0 fusion.42
  422.3 4.2 convert_add_fusion.5
  430.5 4.1 convert_add_fusion.2
  434.6 10.2 %product.20 = bf16[704,2048]{1,0:T(8,128)(2,1)} custom-call(bf16[704,2048]{1,0:T(8,128)(2,1)} %get-tuple-element.164.a, bf16[2048,2048]{1,0:T(8,128)(2,1)} %constant_dynamic-update-slice_fusion.8.b), custom_call_target="tpu_custom_call" | custom-call | flops 1024 | bytes 1024 | tf_op jit(solution)/shard_map/product/pallas_call | solution.py:363
  457.7 10.3 %product.21 = bf16[704,2048]{1,0:T(8,128)(2,1)} custom-call(bf16[704,2048]{1,0:T(8,128)(2,1)} %get-tuple-element.165.a, bf16[2048,2048]{1,0:T(8,128)(2,1)} %constant_dynamic-update-slice_fusion.8.b), custom_call_target="tpu_custom_call" | custom-call | flops 1024 | bytes 1024 | tf_op jit(solution)/shard_map/product/pallas_call | solution.py:363
  477.5 5.6 product.23
  483.1 5.6 product.22
  488.7 5.6 product.25
  494.3 5.6 product.24
  503.6 3.0 add_bitcast_fusion
  511.1 4.0 fusion.67
  521.4 18.4 %collective-permute-done.57 = bf16[256,2048]{1,0:T(8,128)(2,1)S(1)} collective-permute-done((bf16[256,2048]{1,0:T(8,128)(2,1)S(1)}, bf16[256,2048]{1,0:T(8,128)(2,1)S(1)}, u32[]{:S(2)}, u32[]{:S(2)}) %collective-permute-start.57) | collective-permute-done | bytes 1048608 | tf_op jit(solution)/shard_map/ppermute | solution.py:42
  559.4 8.2 %collective-permute-done.61 = bf16[128,2048]{1,0:T(8,128)(2,1)S(1)} collective-permute-done((bf16[128,2048]{1,0:T(8,128)(2,1)S(1)}, bf16[128,2048]{1,0:T(8,128)(2,1)S(1)}, u32[]{:S(2)}, u32[]{:S(2)}) %collective-permute-start.61) | collective-permute-done | bytes 524320 | tf_op jit(solution)/shard_map/ppermute | solution.py:42
  573.0 15.8 %mixer_backward.2 = (bf16[4,256,768]{2,1,0:T(8,128)(2,1)}, f32[512,256]{1,0:T(8,128)S(1)}, f32[8,768]{1,0:T(8,128)S(1)}) custom-call(s32[4]{0:T(128)S(1)} %select_reduce_fusion.7.order, s32[3]{0:T(128)S(1)} %get-tuple-element.259.first, s32[3]{0:T(128)S(1)} %get-tuple-element.353.count, f32[4,256,768]{2,1,0:T(8,128)} %bitcast.173, ...), custom_call_target="tpu_custom_call" | custom-call | flops 1024 | bytes 1024 | tf_op jit(solution)/shard_map/mixer_backward/pallas_call | solution.py:582
  588.8 2.9 convolution_convert_fusion.4
  594.6 3.0 add_bitcast_fusion.2
  600.8 3.3 constant_dynamic-update-slice_fusion.29
  604.0 3.5 fusion.89
  607.7 3.6 fusion.88
  614.8 4.5 convert_add_fusion.1
  619.3 15.6 %mixer_backward.3 = (bf16[4,256,768]{2,1,0:T(8,128)(2,1)}, f32[512,256]{1,0:T(8,128)S(1)}, f32[8,768]{1,0:T(8,128)S(1)}) custom-call(s32[4]{0:T(128)S(1)} %select_reduce_fusion.7.order, s32[3]{0:T(128)S(1)} %get-tuple-element.255.first, s32[3]{0:T(128)S(1)} %get-tuple-element.351.count, f32[4,256,768]{2,1,0:T(8,128)} %bitcast.171, ...), custom_call_target="tpu_custom_call" | custom-call | flops 1024 | bytes 1024 | tf_op jit(solution)/shard_map/mixer_backward/pallas_call | solution.py:582
  636.2 3.2 convolution_convert_fusion.3
  639.4 3.6 fusion.90
  643.0 4.0 add_convert_fusion
  651.9 3.0 add_bitcast_fusion.1
  668.0 6.7 collective-permute-done.85
  674.7 6.7 collective-permute-done.86
  685.5 3.6 convert_add_fusion
  691.7 3.6 multiply_reduce_fusion.1
  697.2 5.4 collective-permute-done.69
  713.5 8.2 %moments.1 = (f32[16,8,256]{2,1,0:T(8,128)}, f32[16,8,256]{2,1,0:T(8,128)}, f32[16,8,256]{2,1,0:T(8,128)}, f32[16,8,256]{2,1,0:T(8,128)}) custom-call(f32[512,256]{1,0:T(8,128)} %add.383.grad, f32[16,8,256]{2,1,0:T(8,128)} %broadcast_in_dim.201.step_re, f32[16,8,256]{2,1,0:T(8,128)} %broadcast_in_dim.202.step_im), custom_call_target="tpu_custom_call" | custom-call | flops 31457280 | bytes 524288 | tf_op jit(solution)/shard_map/moments/pallas_call | solution.py:378
  724.1 7.0 collective-permute-done.92
  734.7 3.0 fusion.8
  741.8 3.4 fusion.24
  745.4 4.1 collective-permute-done.96
  758.1 3.1 fusion.22
  (620 shorter events, 297.6 us)
Async XLA Ops:
  11.6 53.9 %collective-permute-start.13 = (bf16[256,2048]{1,0:T(8,128)(2,1)}, bf16[256,2048]{1,0:T(8,128)(2,1)}, u32[]{:S(2)}, u32[]{:S(2)}) collective-permute-start(bf16[256,2048]{1,0:T(8,128)(2,1)} %bitcast.189), channel_id=1, source_target_pairs={{0,4},{4,0},{8,12},{12,8},{16,20},{20,16},{24,28},{28,24},{1,5},{5... | collective-permute-start | bytes 3145736 | tf_op jit(solution)/shard_map/ppermute | solution.py:42
  13.1 54.8 %collective-permute-start.3 = (bf16[256,2048]{1,0:T(8,128)(2,1)}, bf16[256,2048]{1,0:T(8,128)(2,1)}, u32[]{:S(2)}, u32[]{:S(2)}) collective-permute-start(bf16[256,2048]{1,0:T(8,128)(2,1)} %bitcast.190), channel_id=1, source_target_pairs={{0,2},{1,3},{2,0},{3,1},{4,6},{5,7},{6,4},{7,5},{8,10},{9,11},{10,... | collective-permute-start | bytes 3145736 | tf_op jit(solution)/shard_map/ppermute | solution.py:42
  23.9 35.3 %collective-permute-start.9 = (bf16[192,2048]{1,0:T(8,128)(2,1)}, bf16[192,2048]{1,0:T(8,128)(2,1)S(1)}, u32[]{:S(2)}, u32[]{:S(2)}) collective-permute-start(bf16[192,2048]{1,0:T(8,128)(2,1)} %bitcast.209), channel_id=1, source_target_pairs={{0,8},{4,12},{16,0},{20,4},{24,16},{28,20},{8,24},{12,28},{1,9},{5... | collective-permute-start | bytes 2359304 | tf_op jit(solution)/shard_map/ppermute | solution.py:64
  36.0 24.1 %collective-permute-start.8 = (bf16[192,2048]{1,0:T(8,128)(2,1)}, bf16[192,2048]{1,0:T(8,128)(2,1)}, u32[]{:S(2)}, u32[]{:S(2)}) collective-permute-start(bf16[192,2048]{1,0:T(8,128)(2,1)} %bitcast.210), channel_id=1, source_target_pairs={{0,16},{4,20},{16,24},{20,28},{24,8},{28,12},{8,0},{12,4},{1,17},{... | collective-permute-start | bytes 2359304 | tf_op jit(solution)/shard_map/ppermute | solution.py:64
  62.5 30.2 %collective-permute-start.11 = (bf16[160,2048]{1,0:T(8,128)(2,1)}, bf16[160,2048]{1,0:T(8,128)(2,1)}, u32[]{:S(2)}, u32[]{:S(2)}) collective-permute-start(bf16[160,2048]{1,0:T(8,128)(2,1)} %get-tuple-element.127), channel_id=1, source_target_pairs={{0,8},{4,12},{16,0},{20,4},{24,16},{28,20},{8,24},{12,28},{1,9},{5... | collective-permute-start | bytes 1966088 | tf_op jit(solution)/shard_map/ppermute | solution.py:64
  62.5 29.3 %collective-permute-start.10 = (bf16[160,2048]{1,0:T(8,128)(2,1)}, bf16[160,2048]{1,0:T(8,128)(2,1)}, u32[]{:S(2)}, u32[]{:S(2)}) collective-permute-start(bf16[160,2048]{1,0:T(8,128)(2,1)} %get-tuple-element.126), channel_id=1, source_target_pairs={{0,16},{4,20},{16,24},{20,28},{24,8},{28,12},{8,0},{12,4},{1,17},{... | collective-permute-start | bytes 1966088 | tf_op jit(solution)/shard_map/ppermute | solution.py:64
  67.4 28.3 %collective-permute-start.15 = (bf16[128,2048]{1,0:T(8,128)(2,1)}, bf16[128,2048]{1,0:T(8,128)(2,1)}, u32[]{:S(2)}, u32[]{:S(2)}) collective-permute-start(bf16[128,2048]{1,0:T(8,128)(2,1)} %slice.673), channel_id=1, source_target_pairs={{0,2},{1,3},{2,0},{3,1},{4,6},{5,7},{6,4},{7,5},{8,10},{9,11},{10,... | collective-permute-start | bytes 1572872 | tf_op jit(solution)/shard_map/ppermute | solution.py:42
  69.8 25.9 %collective-permute-start.14 = (bf16[128,2048]{1,0:T(8,128)(2,1)}, bf16[128,2048]{1,0:T(8,128)(2,1)}, u32[]{:S(2)}, u32[]{:S(2)}) collective-permute-start(bf16[128,2048]{1,0:T(8,128)(2,1)} %slice.672), channel_id=1, source_target_pairs={{0,4},{4,0},{8,12},{12,8},{16,20},{20,16},{24,28},{28,24},{1,5},{5... | collective-permute-start | bytes 1572872 | tf_op jit(solution)/shard_map/ppermute | solution.py:42
  72.7 32.0 %collective-permute-start.4 = (bf16[512,2048]{1,0:T(8,128)(2,1)S(1)}, bf16[512,2048]{1,0:T(8,128)(2,1)S(1)}, u32[]{:S(2)}, u32[]{:S(2)}) collective-permute-start(bf16[512,2048]{1,0:T(8,128)(2,1)S(1)} %pad_maximum_fusion.4), channel_id=1, source_target_pairs={{0,1},{1,0},{2,3},{3,2},{4,5},{5,4},{6,7},{7,6},{8,9},{9,8},{10,11... | collective-permute-start | bytes 6291464 | tf_op jit(solution)/shard_map/ppermute | solution.py:42
  141.0 41.2 %collective-permute-start.24 = (bf16[512,2048]{1,0:T(8,128)(2,1)}, bf16[512,2048]{1,0:T(8,128)(2,1)}, u32[]{:S(2)}, u32[]{:S(2)}) collective-permute-start(bf16[512,2048]{1,0:T(8,128)(2,1)} %product.16), channel_id=1, source_target_pairs={{0,1},{1,0},{2,3},{3,2},{4,5},{5,4},{6,7},{7,6},{8,9},{9,8},{10,11... | collective-permute-start | bytes 6291464 | tf_op jit(solution)/shard_map/ppermute | solution.py:42
  141.4 31.5 %collective-permute-start.21 = (bf16[256,2048]{1,0:T(8,128)(2,1)}, bf16[256,2048]{1,0:T(8,128)(2,1)}, u32[]{:S(2)}, u32[]{:S(2)}) collective-permute-start(bf16[256,2048]{1,0:T(8,128)(2,1)} %bitcast.194), channel_id=1, source_target_pairs={{0,2},{1,3},{2,0},{3,1},{4,6},{5,7},{6,4},{7,5},{8,10},{9,11},{10,... | collective-permute-start | bytes 3145736 | tf_op jit(solution)/shard_map/ppermute | solution.py:42
  141.7 34.6 %collective-permute-start.22 = (bf16[256,2048]{1,0:T(8,128)(2,1)}, bf16[256,2048]{1,0:T(8,128)(2,1)}, u32[]{:S(2)}, u32[]{:S(2)}) collective-permute-start(bf16[256,2048]{1,0:T(8,128)(2,1)} %bitcast.195), channel_id=1, source_target_pairs={{0,4},{4,0},{8,12},{12,8},{16,20},{20,16},{24,28},{28,24},{1,5},{5... | collective-permute-start | bytes 3145736 | tf_op jit(solution)/shard_map/ppermute | solution.py:42
  141.8 37.6 %collective-permute-start.19 = (bf16[176,2048]{1,0:T(8,128)(2,1)}, bf16[176,2048]{1,0:T(8,128)(2,1)}, u32[]{:S(2)}, u32[]{:S(2)}) collective-permute-start(bf16[176,2048]{1,0:T(8,128)(2,1)} %bitcast.213), channel_id=1, source_target_pairs={{0,16},{4,20},{16,24},{20,28},{24,8},{28,12},{8,0},{12,4},{1,17},{... | collective-permute-start | bytes 2162696 | tf_op jit(solution)/shard_map/ppermute | solution.py:64
  146.9 35.3 %collective-permute-start.20 = (bf16[176,2048]{1,0:T(8,128)(2,1)}, bf16[176,2048]{1,0:T(8,128)(2,1)}, u32[]{:S(2)}, u32[]{:S(2)}) collective-permute-start(bf16[176,2048]{1,0:T(8,128)(2,1)} %bitcast.214), channel_id=1, source_target_pairs={{0,8},{4,12},{16,0},{20,4},{24,16},{28,20},{8,24},{12,28},{1,9},{5... | collective-permute-start | bytes 2162696 | tf_op jit(solution)/shard_map/ppermute | solution.py:64
  173.0 26.2 %collective-permute-start.23 = (bf16[512,2048]{1,0:T(8,128)(2,1)}, bf16[512,2048]{1,0:T(8,128)(2,1)S(1)}, u32[]{:S(2)}, u32[]{:S(2)}) collective-permute-start(bf16[512,2048]{1,0:T(8,128)(2,1)} %product.15), channel_id=1, source_target_pairs={{0,1},{1,0},{2,3},{3,2},{4,5},{5,4},{6,7},{7,6},{8,9},{9,8},{10,11... | collective-permute-start | bytes 6291464 | tf_op jit(solution)/shard_map/ppermute | solution.py:42
  194.2 22.3 %collective-permute-start.27 = (bf16[128,2048]{1,0:T(8,128)(2,1)S(1)}, bf16[128,2048]{1,0:T(8,128)(2,1)S(1)}, u32[]{:S(2)}, u32[]{:S(2)}) collective-permute-start(bf16[128,2048]{1,0:T(8,128)(2,1)S(1)} %get-tuple-element.301), channel_id=1, source_target_pairs={{0,4},{4,0},{8,12},{12,8},{16,20},{20,16},{24,28},{28,24},{1,5},{5... | collective-permute-start | bytes 1572872 | tf_op jit(solution)/shard_map/ppermute | solution.py:42
  196.5 19.9 %collective-permute-start.29 = (bf16[96,2048]{1,0:T(8,128)(2,1)S(1)}, bf16[96,2048]{1,0:T(8,128)(2,1)S(1)}, u32[]{:S(2)}, u32[]{:S(2)}) collective-permute-start(bf16[96,2048]{1,0:T(8,128)(2,1)S(1)} %slice.686), channel_id=1, source_target_pairs={{0,16},{4,20},{16,24},{20,28},{24,8},{28,12},{8,0},{12,4},{1,17},{... | collective-permute-start | bytes 1179656 | tf_op jit(solution)/shard_map/ppermute | solution.py:64
  199.0 17.4 %collective-permute-start.30 = (bf16[80,2048]{1,0:T(8,128)(2,1)S(1)}, bf16[80,2048]{1,0:T(8,128)(2,1)S(1)}, u32[]{:S(2)}, u32[]{:S(2)}) collective-permute-start(bf16[80,2048]{1,0:T(8,128)(2,1)S(1)} %slice.687), channel_id=1, source_target_pairs={{0,8},{4,12},{16,0},{20,4},{24,16},{28,20},{8,24},{12,28},{1,9},{5... | collective-permute-start | bytes 983048 | tf_op jit(solution)/shard_map/ppermute | solution.py:64
  200.0 17.7 %collective-permute-start.28 = (bf16[128,2048]{1,0:T(8,128)(2,1)S(1)}, bf16[128,2048]{1,0:T(8,128)(2,1)S(1)}, u32[]{:S(2)}, u32[]{:S(2)}) collective-permute-start(bf16[128,2048]{1,0:T(8,128)(2,1)S(1)} %get-tuple-element.300), channel_id=1, source_target_pairs={{0,2},{1,3},{2,0},{3,1},{4,6},{5,7},{6,4},{7,5},{8,10},{9,11},{10,... | collective-permute-start | bytes 1572872 | tf_op jit(solution)/shard_map/ppermute | solution.py:42
  218.9 25.4 %collective-permute-start.32 = (bf16[256,2048]{1,0:T(8,128)(2,1)}, bf16[256,2048]{1,0:T(8,128)(2,1)}, u32[]{:S(2)}, u32[]{:S(2)}) collective-permute-start(bf16[256,2048]{1,0:T(8,128)(2,1)} %pad_maximum_fusion.15), channel_id=1, source_target_pairs={{0,4},{4,0},{8,12},{12,8},{16,20},{20,16},{24,28},{28,24},{1,5},{5... | collective-permute-start | bytes 3145736 | tf_op jit(solution)/shard_map/ppermute | solution.py:42
  220.6 25.1 %collective-permute-start.31 = (bf16[256,2048]{1,0:T(8,128)(2,1)}, bf16[256,2048]{1,0:T(8,128)(2,1)}, u32[]{:S(2)}, u32[]{:S(2)}) collective-permute-start(bf16[256,2048]{1,0:T(8,128)(2,1)} %pad_maximum_fusion.14), channel_id=1, source_target_pairs={{0,2},{1,3},{2,0},{3,1},{4,6},{5,7},{6,4},{7,5},{8,10},{9,11},{10,... | collective-permute-start | bytes 3145736 | tf_op jit(solution)/shard_map/ppermute | solution.py:42
  231.3 43.4 %collective-permute-start.47 = (bf16[512,2048]{1,0:T(8,128)(2,1)S(1)}, bf16[512,2048]{1,0:T(8,128)(2,1)S(1)}, u32[]{:S(2)}, u32[]{:S(2)}) collective-permute-start(bf16[512,2048]{1,0:T(8,128)(2,1)S(1)} %pad_maximum_fusion.8), channel_id=1, source_target_pairs={{0,1},{1,0},{2,3},{3,2},{4,5},{5,4},{6,7},{7,6},{8,9},{9,8},{10,11... | collective-permute-start | bytes 6291464 | tf_op jit(solution)/shard_map/ppermute | solution.py:42
  231.4 34.0 %collective-permute-start.33 = (bf16[176,2048]{1,0:T(8,128)(2,1)S(1)}, bf16[176,2048]{1,0:T(8,128)(2,1)S(1)}, u32[]{:S(2)}, u32[]{:S(2)}) collective-permute-start(bf16[176,2048]{1,0:T(8,128)(2,1)S(1)} %bitcast.215), channel_id=1, source_target_pairs={{0,16},{4,20},{16,24},{20,28},{24,8},{28,12},{8,0},{12,4},{1,17},{... | collective-permute-start | bytes 2162696 | tf_op jit(solution)/shard_map/ppermute | solution.py:64
  232.0 33.3 %collective-permute-start.34 = (bf16[176,2048]{1,0:T(8,128)(2,1)S(1)}, bf16[176,2048]{1,0:T(8,128)(2,1)S(1)}, u32[]{:S(2)}, u32[]{:S(2)}) collective-permute-start(bf16[176,2048]{1,0:T(8,128)(2,1)S(1)} %bitcast.216), channel_id=1, source_target_pairs={{0,8},{4,12},{16,0},{20,4},{24,16},{28,20},{8,24},{12,28},{1,9},{5... | collective-permute-start | bytes 2162696 | tf_op jit(solution)/shard_map/ppermute | solution.py:64
  265.3 24.9 %collective-permute-start.37 = (bf16[256,2048]{1,0:T(8,128)(2,1)S(1)}, bf16[256,2048]{1,0:T(8,128)(2,1)S(1)}, u32[]{:S(2)}, u32[]{:S(2)}) collective-permute-start(bf16[256,2048]{1,0:T(8,128)(2,1)S(1)} %multiply_convert_fusion.3), channel_id=1, source_target_pairs={{0,2},{1,3},{2,0},{3,1},{4,6},{5,7},{6,4},{7,5},{8,10},{9,11},{10,... | collective-permute-start | bytes 3145736 | tf_op jit(solution)/shard_map/ppermute | solution.py:42
  265.7 24.6 %collective-permute-start.38 = (bf16[256,2048]{1,0:T(8,128)(2,1)S(1)}, bf16[256,2048]{1,0:T(8,128)(2,1)S(1)}, u32[]{:S(2)}, u32[]{:S(2)}) collective-permute-start(bf16[256,2048]{1,0:T(8,128)(2,1)S(1)} %multiply_convert_fusion.3), channel_id=1, source_target_pairs={{0,4},{4,0},{8,12},{12,8},{16,20},{20,16},{24,28},{28,24},{1,5},{5... | collective-permute-start | bytes 3145736 | tf_op jit(solution)/shard_map/ppermute | solution.py:42
  270.9 18.2 %collective-permute-start.35 = (bf16[96,2048]{1,0:T(8,128)(2,1)S(1)}, bf16[96,2048]{1,0:T(8,128)(2,1)S(1)}, u32[]{:S(2)}, u32[]{:S(2)}) collective-permute-start(bf16[96,2048]{1,0:T(8,128)(2,1)S(1)} %slice.688), channel_id=1, source_target_pairs={{0,16},{4,20},{16,24},{20,28},{24,8},{28,12},{8,0},{12,4},{1,17},{... | collective-permute-start | bytes 1179656 | tf_op jit(solution)/shard_map/ppermute | solution.py:64
  271.5 17.7 %collective-permute-start.36 = (bf16[80,2048]{1,0:T(8,128)(2,1)S(1)}, bf16[80,2048]{1,0:T(8,128)(2,1)S(1)}, u32[]{:S(2)}, u32[]{:S(2)}) collective-permute-start(bf16[80,2048]{1,0:T(8,128)(2,1)S(1)} %slice.689), channel_id=1, source_target_pairs={{0,8},{4,12},{16,0},{20,4},{24,16},{28,20},{8,24},{12,28},{1,9},{5... | collective-permute-start | bytes 983048 | tf_op jit(solution)/shard_map/ppermute | solution.py:64
  274.7 37.7 %collective-permute-start.48 = (bf16[512,2048]{1,0:T(8,128)(2,1)S(1)}, bf16[512,2048]{1,0:T(8,128)(2,1)S(1)}, u32[]{:S(2)}, u32[]{:S(2)}) collective-permute-start(bf16[512,2048]{1,0:T(8,128)(2,1)S(1)} %pad_maximum_fusion.9), channel_id=1, source_target_pairs={{0,1},{1,0},{2,3},{3,2},{4,5},{5,4},{6,7},{7,6},{8,9},{9,8},{10,11... | collective-permute-start | bytes 6291464 | tf_op jit(solution)/shard_map/ppermute | solution.py:42
  293.0 21.0 %collective-permute-start.39 = (bf16[512,2048]{1,0:T(8,128)(2,1)S(1)}, bf16[512,2048]{1,0:T(8,128)(2,1)S(1)}, u32[]{:S(2)}, u32[]{:S(2)}) collective-permute-start(bf16[512,2048]{1,0:T(8,128)(2,1)S(1)} %pad_maximum_fusion.6), channel_id=1, source_target_pairs={{0,1},{1,0},{2,3},{3,2},{4,5},{5,4},{6,7},{7,6},{8,9},{9,8},{10,11... | collective-permute-start | bytes 6291464 | tf_op jit(solution)/shard_map/ppermute | solution.py:42
  304.9 38.4 %collective-permute-start.42 = (bf16[512,2048]{1,0:T(8,128)(2,1)S(1)}, bf16[512,2048]{1,0:T(8,128)(2,1)S(1)}, u32[]{:S(2)}, u32[]{:S(2)}) collective-permute-start(bf16[512,2048]{1,0:T(8,128)(2,1)S(1)} %pad_maximum_fusion.7), channel_id=1, source_target_pairs={{0,1},{1,0},{2,3},{3,2},{4,5},{5,4},{6,7},{7,6},{8,9},{9,8},{10,11... | collective-permute-start | bytes 6291464 | tf_op jit(solution)/shard_map/ppermute | solution.py:42
  309.2 34.0 %collective-permute-start.43 = (bf16[176,2048]{1,0:T(8,128)(2,1)S(1)}, bf16[176,2048]{1,0:T(8,128)(2,1)S(1)}, u32[]{:S(2)}, u32[]{:S(2)}) collective-permute-start(bf16[176,2048]{1,0:T(8,128)(2,1)S(1)} %bitcast.218), channel_id=1, source_target_pairs={{0,16},{4,20},{16,24},{20,28},{24,8},{28,12},{8,0},{12,4},{1,17},{... | collective-permute-start | bytes 2162696 | tf_op jit(solution)/shard_map/ppermute | solution.py:64
  309.3 34.0 %collective-permute-start.44 = (bf16[176,2048]{1,0:T(8,128)(2,1)S(1)}, bf16[176,2048]{1,0:T(8,128)(2,1)S(1)}, u32[]{:S(2)}, u32[]{:S(2)}) collective-permute-start(bf16[176,2048]{1,0:T(8,128)(2,1)S(1)} %bitcast.219), channel_id=1, source_target_pairs={{0,8},{4,12},{16,0},{20,4},{24,16},{28,20},{8,24},{12,28},{1,9},{5... | collective-permute-start | bytes 2162696 | tf_op jit(solution)/shard_map/ppermute | solution.py:64
  344.2 28.1 %collective-permute-start.46 = (bf16[80,2048]{1,0:T(8,128)(2,1)S(1)}, bf16[80,2048]{1,0:T(8,128)(2,1)}, u32[]{:S(2)}, u32[]{:S(2)}) collective-permute-start(bf16[80,2048]{1,0:T(8,128)(2,1)S(1)} %slice.554), channel_id=1, source_target_pairs={{0,8},{4,12},{16,0},{20,4},{24,16},{28,20},{8,24},{12,28},{1,9},{5... | collective-permute-start | bytes 983048 | tf_op jit(solution)/shard_map/ppermute | solution.py:64
  344.5 27.8 %collective-permute-start.45 = (bf16[96,2048]{1,0:T(8,128)(2,1)}, bf16[96,2048]{1,0:T(8,128)(2,1)}, u32[]{:S(2)}, u32[]{:S(2)}) collective-permute-start(bf16[96,2048]{1,0:T(8,128)(2,1)} %slice.553), channel_id=1, source_target_pairs={{0,16},{4,20},{16,24},{20,28},{24,8},{28,12},{8,0},{12,4},{1,17},{... | collective-permute-start | bytes 1179656 | tf_op jit(solution)/shard_map/ppermute | solution.py:64
  416.2 30.6 %collective-permute-start.73 = (bf16[96,2048]{1,0:T(8,128)(2,1)}, bf16[96,2048]{1,0:T(8,128)(2,1)}, u32[]{:S(2)}, u32[]{:S(2)}) collective-permute-start(bf16[96,2048]{1,0:T(8,128)(2,1)} %get-tuple-element.185), channel_id=1, source_target_pairs={{0,16},{4,20},{16,24},{20,28},{24,8},{28,12},{8,0},{12,4},{1,17},{... | collective-permute-start | bytes 1179656 | tf_op jit(solution)/shard_map/ppermute | solution.py:64
  416.3 30.5 %collective-permute-start.74 = (bf16[80,2048]{1,0:T(8,128)(2,1)}, bf16[80,2048]{1,0:T(8,128)(2,1)}, u32[]{:S(2)}, u32[]{:S(2)}) collective-permute-start(bf16[80,2048]{1,0:T(8,128)(2,1)} %get-tuple-element.186), channel_id=1, source_target_pairs={{0,8},{4,12},{16,0},{20,4},{24,16},{28,20},{8,24},{12,28},{1,9},{5... | collective-permute-start | bytes 983048 | tf_op jit(solution)/shard_map/ppermute | solution.py:64
  427.7 30.0 %collective-permute-start.50 = (bf16[128,2048]{1,0:T(8,128)(2,1)}, bf16[128,2048]{1,0:T(8,128)(2,1)}, u32[]{:S(2)}, u32[]{:S(2)}) collective-permute-start(bf16[128,2048]{1,0:T(8,128)(2,1)} %get-tuple-element.291), channel_id=1, source_target_pairs={{0,4},{4,0},{8,12},{12,8},{16,20},{20,16},{24,28},{28,24},{1,5},{5... | collective-permute-start | bytes 1572872 | tf_op jit(solution)/shard_map/ppermute | solution.py:42
  429.1 28.6 %collective-permute-start.51 = (bf16[128,2048]{1,0:T(8,128)(2,1)}, bf16[128,2048]{1,0:T(8,128)(2,1)}, u32[]{:S(2)}, u32[]{:S(2)}) collective-permute-start(bf16[128,2048]{1,0:T(8,128)(2,1)} %get-tuple-element.290), channel_id=1, source_target_pairs={{0,2},{1,3},{2,0},{3,1},{4,6},{5,7},{6,4},{7,5},{8,10},{9,11},{10,... | collective-permute-start | bytes 1572872 | tf_op jit(solution)/shard_map/ppermute | solution.py:42
  453.1 49.9 %collective-permute-start.75 = (bf16[176,2048]{1,0:T(8,128)(2,1)}, bf16[176,2048]{1,0:T(8,128)(2,1)}, u32[]{:S(2)}, u32[]{:S(2)}) collective-permute-start(bf16[176,2048]{1,0:T(8,128)(2,1)} %pad_maximum_fusion.29), channel_id=1, source_target_pairs={{0,16},{4,20},{16,24},{20,28},{24,8},{28,12},{8,0},{12,4},{1,17},{... | collective-permute-start | bytes 2162696 | tf_op jit(solution)/shard_map/ppermute | solution.py:64
  454.1 49.6 %collective-permute-start.76 = (bf16[176,2048]{1,0:T(8,128)(2,1)}, bf16[176,2048]{1,0:T(8,128)(2,1)}, u32[]{:S(2)}, u32[]{:S(2)}) collective-permute-start(bf16[176,2048]{1,0:T(8,128)(2,1)} %pad_maximum_fusion.30), channel_id=1, source_target_pairs={{0,8},{4,12},{16,0},{20,4},{24,16},{28,20},{8,24},{12,28},{1,9},{5... | collective-permute-start | bytes 2162696 | tf_op jit(solution)/shard_map/ppermute | solution.py:64
  474.4 34.0 %collective-permute-start.56 = (bf16[256,2048]{1,0:T(8,128)(2,1)}, bf16[256,2048]{1,0:T(8,128)(2,1)}, u32[]{:S(2)}, u32[]{:S(2)}) collective-permute-start(bf16[256,2048]{1,0:T(8,128)(2,1)} %pad_maximum_fusion.17), channel_id=1, source_target_pairs={{0,4},{4,0},{8,12},{12,8},{16,20},{20,16},{24,28},{28,24},{1,5},{5... | collective-permute-start | bytes 3145736 | tf_op jit(solution)/shard_map/ppermute | solution.py:42
  475.3 33.4 %collective-permute-start.55 = (bf16[256,2048]{1,0:T(8,128)(2,1)}, bf16[256,2048]{1,0:T(8,128)(2,1)}, u32[]{:S(2)}, u32[]{:S(2)}) collective-permute-start(bf16[256,2048]{1,0:T(8,128)(2,1)} %pad_maximum_fusion.16), channel_id=1, source_target_pairs={{0,2},{1,3},{2,0},{3,1},{4,6},{5,7},{6,4},{7,5},{8,10},{9,11},{10,... | collective-permute-start | bytes 3145736 | tf_op jit(solution)/shard_map/ppermute | solution.py:42
  499.9 17.0 %collective-permute-start.54 = (bf16[512,2048]{1,0:T(8,128)(2,1)}, bf16[512,2048]{1,0:T(8,128)(2,1)S(1)}, u32[]{:S(2)}, u32[]{:S(2)}) collective-permute-start(bf16[512,2048]{1,0:T(8,128)(2,1)} %product.25), channel_id=1, source_target_pairs={{0,1},{1,0},{2,3},{3,2},{4,5},{5,4},{6,7},{7,6},{8,9},{9,8},{10,11... | collective-permute-start | bytes 6291464 | tf_op jit(solution)/shard_map/ppermute | solution.py:42
  506.6 36.6 %collective-permute-start.77 = (bf16[192,2048]{1,0:T(8,128)(2,1)S(1)}, bf16[192,2048]{1,0:T(8,128)(2,1)S(1)}, u32[]{:S(2)}, u32[]{:S(2)}) collective-permute-start(bf16[192,2048]{1,0:T(8,128)(2,1)S(1)} %pad_maximum_fusion.23), channel_id=1, source_target_pairs={{0,16},{4,20},{16,24},{20,28},{24,8},{28,12},{8,0},{12,4},{1,17},{... | collective-permute-start | bytes 2359304 | tf_op jit(solution)/shard_map/ppermute | solution.py:64
  508.4 34.8 %collective-permute-start.78 = (bf16[160,2048]{1,0:T(8,128)(2,1)S(1)}, bf16[160,2048]{1,0:T(8,128)(2,1)S(1)}, u32[]{:S(2)}, u32[]{:S(2)}) collective-permute-start(bf16[160,2048]{1,0:T(8,128)(2,1)S(1)} %pad_maximum_fusion.35), channel_id=1, source_target_pairs={{0,8},{4,12},{16,0},{20,4},{24,16},{28,20},{8,24},{12,28},{1,9},{5... | collective-permute-start | bytes 1966088 | tf_op jit(solution)/shard_map/ppermute | solution.py:64
  515.2 24.6 %collective-permute-start.57 = (bf16[256,2048]{1,0:T(8,128)(2,1)S(1)}, bf16[256,2048]{1,0:T(8,128)(2,1)S(1)}, u32[]{:S(2)}, u32[]{:S(2)}) collective-permute-start(bf16[256,2048]{1,0:T(8,128)(2,1)S(1)} %get-tuple-element.251), channel_id=1, source_target_pairs={{0,2},{1,3},{2,0},{3,1},{4,6},{5,7},{6,4},{7,5},{8,10},{9,11},{10,... | collective-permute-start | bytes 3145736 | tf_op jit(solution)/shard_map/ppermute | solution.py:42
  516.8 24.4 %collective-permute-start.59 = (bf16[256,2048]{1,0:T(8,128)(2,1)S(1)}, bf16[256,2048]{1,0:T(8,128)(2,1)S(1)}, u32[]{:S(2)}, u32[]{:S(2)}) collective-permute-start(bf16[256,2048]{1,0:T(8,128)(2,1)S(1)} %get-tuple-element.251), channel_id=1, source_target_pairs={{0,4},{4,0},{8,12},{12,8},{16,20},{20,16},{24,28},{28,24},{1,5},{5... | collective-permute-start | bytes 3145736 | tf_op jit(solution)/shard_map/ppermute | solution.py:42
  543.1 27.8 %collective-permute-start.65 = (bf16[512,2048]{1,0:T(8,128)(2,1)S(1)}, bf16[512,2048]{1,0:T(8,128)(2,1)S(1)}, u32[]{:S(2)}, u32[]{:S(2)}) collective-permute-start(bf16[512,2048]{1,0:T(8,128)(2,1)S(1)} %pad_maximum_fusion.10), channel_id=1, source_target_pairs={{0,1},{1,0},{2,3},{3,2},{4,5},{5,4},{6,7},{7,6},{8,9},{9,8},{10,11... | collective-permute-start | bytes 6291464 | tf_op jit(solution)/shard_map/ppermute | solution.py:42
  547.8 44.0 %collective-permute-start.79 = (bf16[176,2048]{1,0:T(8,128)(2,1)}, bf16[176,2048]{1,0:T(8,128)(2,1)}, u32[]{:S(2)}, u32[]{:S(2)}) collective-permute-start(bf16[176,2048]{1,0:T(8,128)(2,1)} %pad_maximum_fusion.33), channel_id=1, source_target_pairs={{0,16},{4,20},{16,24},{20,28},{24,8},{28,12},{8,0},{12,4},{1,17},{... | collective-permute-start | bytes 2162696 | tf_op jit(solution)/shard_map/ppermute | solution.py:64
  550.4 41.5 %collective-permute-start.80 = (bf16[176,2048]{1,0:T(8,128)(2,1)}, bf16[176,2048]{1,0:T(8,128)(2,1)}, u32[]{:S(2)}, u32[]{:S(2)}) collective-permute-start(bf16[176,2048]{1,0:T(8,128)(2,1)} %pad_maximum_fusion.34), channel_id=1, source_target_pairs={{0,8},{4,12},{16,0},{20,4},{24,16},{28,20},{8,24},{12,28},{1,9},{5... | collective-permute-start | bytes 2162696 | tf_op jit(solution)/shard_map/ppermute | solution.py:64
  567.6 33.1 %collective-permute-start.67 = (bf16[512,2048]{1,0:T(8,128)(2,1)}, bf16[512,2048]{1,0:T(8,128)(2,1)}, u32[]{:S(2)}, u32[]{:S(2)}) collective-permute-start(bf16[512,2048]{1,0:T(8,128)(2,1)} %pad_maximum_fusion.11), channel_id=1, source_target_pairs={{0,1},{1,0},{2,3},{3,2},{4,5},{5,4},{6,7},{7,6},{8,9},{9,8},{10,11... | collective-permute-start | bytes 6291464 | tf_op jit(solution)/shard_map/ppermute | solution.py:42
  570.0 27.5 %collective-permute-start.64 = (bf16[256,2048]{1,0:T(8,128)(2,1)}, bf16[256,2048]{1,0:T(8,128)(2,1)S(1)}, u32[]{:S(2)}, u32[]{:S(2)}) collective-permute-start(bf16[256,2048]{1,0:T(8,128)(2,1)} %pad_maximum_fusion.19), channel_id=1, source_target_pairs={{0,4},{4,0},{8,12},{12,8},{16,20},{20,16},{24,28},{28,24},{1,5},{5... | collective-permute-start | bytes 3145736 | tf_op jit(solution)/shard_map/ppermute | solution.py:42
  570.9 27.0 %collective-permute-start.63 = (bf16[256,2048]{1,0:T(8,128)(2,1)}, bf16[256,2048]{1,0:T(8,128)(2,1)}, u32[]{:S(2)}, u32[]{:S(2)}) collective-permute-start(bf16[256,2048]{1,0:T(8,128)(2,1)} %pad_maximum_fusion.18), channel_id=1, source_target_pairs={{0,2},{1,3},{2,0},{3,1},{4,6},{5,7},{6,4},{7,5},{8,10},{9,11},{10,... | collective-permute-start | bytes 3145736 | tf_op jit(solution)/shard_map/ppermute | solution.py:42
  591.8 23.0 %collective-permute-start.66 = (bf16[512,2048]{1,0:T(8,128)(2,1)S(1)}, bf16[512,2048]{1,0:T(8,128)(2,1)S(1)}, u32[]{:S(2)}, u32[]{:S(2)}) collective-permute-start(bf16[512,2048]{1,0:T(8,128)(2,1)S(1)} %convolution_convert_fusion.4), channel_id=1, source_target_pairs={{0,1},{1,0},{2,3},{3,2},{4,5},{5,4},{6,7},{7,6},{8,9},{9,8},{10,11... | collective-permute-start | bytes 6291464 | tf_op jit(solution)/shard_map/ppermute | solution.py:42
  591.9 60.0 %collective-permute-start.81 = (bf16[176,2048]{1,0:T(8,128)(2,1)}, bf16[176,2048]{1,0:T(8,128)(2,1)}, u32[]{:S(2)}, u32[]{:S(2)}) collective-permute-start(bf16[176,2048]{1,0:T(8,128)(2,1)} %pad_maximum_fusion.31), channel_id=1, source_target_pairs={{0,16},{4,20},{16,24},{20,28},{24,8},{28,12},{8,0},{12,4},{1,17},{... | collective-permute-start | bytes 2162696 | tf_op jit(solution)/shard_map/ppermute | solution.py:64
  597.6 54.3 %collective-permute-start.82 = (bf16[176,2048]{1,0:T(8,128)(2,1)}, bf16[176,2048]{1,0:T(8,128)(2,1)}, u32[]{:S(2)}, u32[]{:S(2)}) collective-permute-start(bf16[176,2048]{1,0:T(8,128)(2,1)} %pad_maximum_fusion.32), channel_id=1, source_target_pairs={{0,8},{4,12},{16,0},{20,4},{24,16},{28,20},{8,24},{12,28},{1,9},{5... | collective-permute-start | bytes 2162696 | tf_op jit(solution)/shard_map/ppermute | solution.py:64
  639.4 46.1 %collective-permute-start.68 = (bf16[512,2048]{1,0:T(8,128)(2,1)}, bf16[512,2048]{1,0:T(8,128)(2,1)}, u32[]{:S(2)}, u32[]{:S(2)}) collective-permute-start(bf16[512,2048]{1,0:T(8,128)(2,1)} %convolution_convert_fusion.3), channel_id=1, source_target_pairs={{0,1},{1,0},{2,3},{3,2},{4,5},{5,4},{6,7},{7,6},{8,9},{9,8},{10,11... | collective-permute-start | bytes 6291464 | tf_op jit(solution)/shard_map/ppermute | solution.py:42
  681.4 27.3 %collective-permute-start.87 = (bf16[96,2048]{1,0:T(8,128)(2,1)S(1)}, bf16[96,2048]{1,0:T(8,128)(2,1)S(1)}, u32[]{:S(2)}, u32[]{:S(2)}) collective-permute-start(bf16[96,2048]{1,0:T(8,128)(2,1)S(1)} %get-tuple-element.209), channel_id=1, source_target_pairs={{0,16},{4,20},{16,24},{20,28},{24,8},{28,12},{8,0},{12,4},{1,17},{... | collective-permute-start | bytes 1179656 | tf_op jit(solution)/shard_map/ppermute | solution.py:64
  682.0 26.7 %collective-permute-start.88 = (bf16[96,2048]{1,0:T(8,128)(2,1)S(1)}, bf16[96,2048]{1,0:T(8,128)(2,1)S(1)}, u32[]{:S(2)}, u32[]{:S(2)}) collective-permute-start(bf16[96,2048]{1,0:T(8,128)(2,1)S(1)} %get-tuple-element.210), channel_id=1, source_target_pairs={{0,8},{4,12},{16,0},{20,4},{24,16},{28,20},{8,24},{12,28},{1,9},{5... | collective-permute-start | bytes 1179656 | tf_op jit(solution)/shard_map/ppermute | solution.py:64
  706.3 28.4 %collective-permute-start.72 = (bf16[256,2048]{1,0:T(8,128)(2,1)}, bf16[256,2048]{1,0:T(8,128)(2,1)}, u32[]{:S(2)}, u32[]{:S(2)}) collective-permute-start(bf16[256,2048]{1,0:T(8,128)(2,1)} %pad_maximum_fusion.21), channel_id=1, source_target_pairs={{0,4},{4,0},{8,12},{12,8},{16,20},{20,16},{24,28},{28,24},{1,5},{5... | collective-permute-start | bytes 3145736 | tf_op jit(solution)/shard_map/ppermute | solution.py:42
  707.3 27.4 %collective-permute-start.71 = (bf16[256,2048]{1,0:T(8,128)(2,1)}, bf16[256,2048]{1,0:T(8,128)(2,1)}, u32[]{:S(2)}, u32[]{:S(2)}) collective-permute-start(bf16[256,2048]{1,0:T(8,128)(2,1)} %pad_maximum_fusion.20), channel_id=1, source_target_pairs={{0,2},{1,3},{2,0},{3,1},{4,6},{5,7},{6,4},{7,5},{8,10},{9,11},{10,... | collective-permute-start | bytes 3145736 | tf_op jit(solution)/shard_map/ppermute | solution.py:42
  711.4 46.1 %collective-permute-start.89 = (bf16[192,2048]{1,0:T(8,128)(2,1)}, bf16[192,2048]{1,0:T(8,128)(2,1)}, u32[]{:S(2)}, u32[]{:S(2)}) collective-permute-start(bf16[192,2048]{1,0:T(8,128)(2,1)} %pad_maximum_fusion.24), channel_id=1, source_target_pairs={{0,16},{4,20},{16,24},{20,28},{24,8},{28,12},{8,0},{12,4},{1,17},{... | collective-permute-start | bytes 2359304 | tf_op jit(solution)/shard_map/ppermute | solution.py:64
  712.6 44.9 %collective-permute-start.90 = (bf16[192,2048]{1,0:T(8,128)(2,1)}, bf16[192,2048]{1,0:T(8,128)(2,1)}, u32[]{:S(2)}, u32[]{:S(2)}) collective-permute-start(bf16[192,2048]{1,0:T(8,128)(2,1)} %pad_maximum_fusion.25), channel_id=1, source_target_pairs={{0,8},{4,12},{16,0},{20,4},{24,16},{28,20},{8,24},{12,28},{1,9},{5... | collective-permute-start | bytes 2359304 | tf_op jit(solution)/shard_map/ppermute | solution.py:64
  (141 other events, 1306.0 us)

commit v7 on v6

--- a/solution.py
+++ b/solution.py
@@ -702,17 +702,14 @@
     in_all, out_all, down_all, gate_all, up_all = weights
     steps = outer // 2
     last = small_pieces[1:]
-    for at in range(steps - 1):
-        last = ring_step([in_all], last)
-    last = ring_step([in_all, out_all], last)
-    for at in range(1, steps):
-        last = ring_step([out_all], last)
+    for at in range(steps):
+        last = ring_step([in_all, out_all], last)
 
     def normed(pieces):
         values = jnp.concatenate(pieces, axis=0).astype(f32)
         return (values * inverse_rms(values) * gain_first).astype(bf16)
 
-    rows_first = [normed(first_own), normed(first_other)]
+    rows_first = lax.optimization_barrier([normed(first_own), normed(first_other)])
     rate_first = inverse_rms(source)
     (upstream_own, upstream_other), upstream_stages = gather_rows(
         upstream_low, first_stages[2], (), True
@@ -755,8 +752,7 @@
     mixed = []
     for r in range(2):
         table, first = tables[r]
-        proj = product(rows_first[r], in_all, "nt", f32)
-        proj = proj.reshape(narrow, local_rows, 3 * channels)
+        proj = nt(rows_first[r], in_all).reshape(narrow, local_rows, 3 * channels)
         gated, long_out, seen = mixer_forward(
             order, first, documents[r][0], proj, taps, table, spectrum, fwd, inv
         )
@@ -764,37 +760,31 @@
     out_last = last
     out_all = jnp.concatenate(out_all.pieces(), axis=0)
     parts = [slice(0, even), slice(even, slots)]
-    odds = [product(mixed[r][1], out_all, "nn", bf16, 1) for r in range(2)]
+    ready = [mixed[0][1], after([mixed[1][1]], upstream_stages[0])[0]]
+    odds = [nn(ready[r][parts[1]], out_all).astype(bf16) for r in range(2)]
     cores = [swap(odd, "narrow", 1) for odd in odds]
     for at in range(steps - 1):
-        last = ring_step([down_all], last)
-    ready = after([mixed[0][1], mixed[1][1]], last + upstream_stages[0])
+        last = ring_step([down_all, gate_all], last, odds)
+    last_two = last
+    for at in range(steps - 1):
+        last_two = ring_step([up_all], last_two)
+    ready = after([mixed[0][1], mixed[1][1]], upstream_stages[0])
     evens = [nn(ready[r][parts[0]], out_all).astype(bf16) for r in range(2)]
-    last_two = last
-    for at in range(1, steps):
-        last_two = ring_step([down_all], last_two, cores)
-    last_three = ring_step([gate_all], last_two)
-    for at in range(1, steps - 1):
-        last_three = ring_step([gate_all], last_three)
     mixer_out, stages = scatter_rows(
-        evens[0], cores[0], evens[1], cores[1], upstream_stages[1], last_two
+        evens[0], cores[0], evens[1], cores[1], upstream_stages[1] + last
     )
     middle = source + mixer_out
     rate_last = inverse_rms(middle)
     rows_upstream = jnp.concatenate(upstream_own + upstream_other, axis=0)
     low_second = (middle * rate_last * gain_last).astype(bf16)
-    last_four = ring_step([gate_all], last_three + stages[1])
-    (second_own, second_other), second_stages = gather_rows(low_second, last_three, last_four)
+    (second_own, second_other), second_stages = gather_rows(low_second, last_two + upstream_stages[2])
     rows_second = jnp.concatenate(second_own + second_other, axis=0)
-    last = ring_step([up_all], last_four + second_stages[0], second_stages[2])
-    for at in range(1, steps):
-        last = ring_step([up_all], last)
+    last = ring_step([down_all, gate_all, up_all], last_two + stages[1], second_stages[1])
 
     down_all, gate_all = [jnp.concatenate(w.pieces(), axis=0) for w in (down_all, gate_all)]
-    d_hidden = product(down_all, rows_upstream, "nt", f32)
-    gate_pre = product(gate_all, rows_second, "nt", f32)
-    up_pieces = after(up_all.pieces(), [d_hidden, gate_pre])
-    up_all = jnp.concatenate(up_pieces, axis=0)
+    up_all = jnp.concatenate(up_all.pieces(), axis=0)
+    d_hidden = nt(down_all, rows_upstream)
+    gate_pre = nt(gate_all, rows_second)
     up_pre = nt(up_all, rows_second)
     sig = jax.nn.sigmoid(gate_pre)
     silu = gate_pre * sig
@@ -813,7 +803,6 @@
     odds = [second_share(n) for n in (1, 3)]
     cores = [swap(odd, "narrow", 1) for odd in odds]
     evens = [second_share(0), second_share(2)]
-    last = ring_step(grads, (), evens)
     d_second, stages = scatter_rows(evens[0], cores[0], evens[1], cores[1])
     upstream = upstream_low.astype(f32)
     d_middle = upstream + norm_back(middle, rate_last, gain_last, d_second)
@@ -825,15 +814,14 @@
     grad_up = product(d_up, rows_second, "nn", bf16)
     [hidden] = after([hidden], [grad_up])
     down_shares = [product(hidden, down_all, "tn", bf16, n) for n in (0, 1)]
-    for at in range(1, steps):
-        last = ring_step(grads, last, [grad_up])
     down_shares += [product(hidden, down_all, "tn", bf16, n) for n in (2, 3)]
     pair = [Scatter(jnp.split(grad, outer, axis=0)) for grad in (grad_gate, grad_up)]
     grads += pair
-    last = ring_step(pair, last, middle_stages[0])
+    last = ring_step(grads, (), middle_stages[0])
+    down_shares = after(down_shares, middle_stages[1])
     down_cores = [swap(down_shares[n], "narrow", 1) for n in (1, 3)]
     down_out, down_stages = scatter_rows(
-        down_shares[0], down_cores[0], down_shares[2], down_cores[1], middle_stages[1]
+        down_shares[0], down_cores[0], down_shares[2], down_cores[1]
     )
     block_output = (middle + down_out).astype(bf16)
     grad_gain_two = jnp.sum(d_second * middle * rate_last, axis=0)
@@ -845,11 +833,8 @@
         proj, gated, long_out, seen = mixed[r]
         table, first = tables[r]
         d_gated = nt(rows_dmiddle[r], out_all).reshape(narrow, local_rows, channels)
-        if r == 0:
-            for at in range(1, steps):
-                last = ring_step(pair[:1], last, [d_gated])
         if r == 1:
-            [d_gated] = after([d_gated], [grad_out, *shares[0], *down_stages[1]])
+            [d_gated] = after([d_gated], [grad_out, *shares[0], *down_stages[0]])
         dz, d_filter_row, d_taps_row = mixer_backward(
             order, first, documents[r][0], proj, d_gated, long_out, seen, taps, table,
             spectrum, fwd, inv,
@@ -857,17 +842,14 @@
         d_rows[r] = dz.reshape(slots, 3 * channels)
         d_filter, d_taps = d_filter + d_filter_row, d_taps + d_taps_row
         if r == 0:
-            [ready] = after([d_rows[r]], down_stages[0])
-            shares[r] = [nn(ready[p], in_all).astype(bf16) for p in halves]
-    for at in range(1, steps):
-        last = ring_step(pair[1:], last, [d_rows[1]])
-    out_sum = Scatter(jnp.split(grad_out, outer, axis=0))
-    for at in range(steps):
-        last = ring_step([out_sum], last)
-    odd = nn(d_rows[1][halves[1]], in_all).astype(bf16)
+            shares[r] = [nn(d_rows[r][p], in_all).astype(bf16) for p in halves]
+    [ready] = after([d_rows[1]], down_stages[1])
+    odd = nn(ready[halves[1]], in_all).astype(bf16)
     cores = [swap(shares[0][1], "narrow", 1), swap(odd, "narrow", 1)]
     ready = after(d_rows, [odd])
     grad_in = sum(tn(ready[r], rows_first[r]) for r in range(2)).astype(bf16)
+    for at in range(1, steps):
+        last = ring_step(grads, last, [grad_in])
     [ready] = after([d_rows[1]], [grad_in] + cores)
     shares[1] = [nn(ready[halves[0]], in_all).astype(bf16), odd]
     d_normed, stages = scatter_rows(shares[0][0], cores[0], shares[1][0], cores[1])
@@ -878,7 +860,8 @@
             grad_gain_one = grad_gain_one + jnp.sum(share.astype(f32) * rows.astype(f32), axis=0)
     chunks = grad_in.reshape(3, outer, own, width)
     in_sum = Scatter([chunks[:, j].reshape(3 * own, width) for j in range(outer)])
-    last = ring_step([in_sum], last, stages[0])
+    out_sum = Scatter(jnp.split(grad_out, outer, axis=0))
+    last = ring_step([in_sum, out_sum], last, stages[0])
     d_filter, *_ = after([d_filter], last + stages[0])
     gain_grads = after([jnp.stack([grad_gain_one / gain_first, grad_gain_two])], stages[0])
     gain_share = reduce_gain(gain_grads[0], stages[1])
@@ -904,7 +887,7 @@
     small_share = scatter_small(jnp.split(small_grad, outer, axis=1))
 
     for at in range(1, steps):
-        last = ring_step([in_sum], last, [gain_share, small_share])
+        last = ring_step([in_sum, out_sum], last, [gain_share, small_share])
 
     at = 9 + poles
     return (

time: 773 us -> 673 us (0.87)
  Pallas kernels: 159 us -> 112 us
  local copies, waits for them, and re-layouts: 108 us -> 73.8 us
  starting transfers between devices: 100 us -> 74.7 us
  matrix products: 76.3 us -> 101 us
  waiting for transfers between devices: 206 us -> 183 us
    pallas_call x13 -> x7, Pallas kernels: 101 us -> 53.4 us  [product(): pl.pallas_call(partial(product_kernel, kind=kind), grid=(columns // side,...]
    ppermute x45 -> x27, waiting for transfers between devices: 131 us -> 95.8 us  [along(): return lax.ppermute(values, 'wide', pairs)]
    dot_general x3 -> x7, matrix products: 20.7 us -> 45.6 us  [nt(): lax.dot_general(a, b, (((1,), (1,)), ((), ())), preferred_element_type=f32)]
    unnamed x238 -> x235, local copies, waits for them, and re-layouts: 52.7 us -> 29.5 us
    ppermute x45 -> x27, starting transfers between devices: 58.1 us -> 36 us  [along(): return lax.ppermute(values, 'wide', pairs)]
    ppermute x55, waiting for transfers between devices: 75 us -> 87.1 us  [swap(): return lax.ppermute(values, axis, [(i, i ^ shift) for i in range(size)])]
    unnamed x0 -> x5, other arithmetic: none -> 9.98 us
    dot_general x6 -> x8, matrix products: 17.4 us -> 18.8 us  [nn(): lax.dot_general(a, b, (((1,), (0,)), ((), ())), preferred_element_type=f32)]
  transfers between devices with their start and end apart: 100 -> 82, of which waited for: 29 -> 26; matrix products, arithmetic and copies ran while one was open for 30% -> 35% of each run, Pallas kernels for 17% -> 15%
where the time goes in v7:
time: 673 us; the launch traced here: 665 us
  waiting for transfers between devices  183 us (27%)
  other arithmetic  116 us (17%)
  Pallas kernels  112 us (17%)
  matrix products  101 us (15%)
  starting transfers between devices  74.7 us (11%)
  local copies, waits for them, and re-layouts  73.8 us (11%)
    ppermute x27, waiting for transfers between devices, along(): return lax.ppermute(values, 'wide', pairs)  95.8 us
    ppermute x55, waiting for transfers between devices, swap(): return lax.ppermute(values, axis, [(i, i ^ shift) for i in range(size)])  87.1 us
    pallas_call x7, Pallas kernels, product(): pl.pallas_call(partial(product_kernel, kind=kind), grid=(columns // side,...  53.4 us
    dot_general x7, matrix products, nt(): lax.dot_general(a, b, (((1,), (1,)), ((), ())), preferred_element_type=f32)  45.6 us
    ppermute x55, starting transfers between devices, swap(): return lax.ppermute(values, axis, [(i, i ^ shift) for i in range(size)])  38.7 us
    ppermute x27, starting transfers between devices, along(): return lax.ppermute(values, 'wide', pairs)  36 us
    dot_general x12, matrix products, tn(): lax.dot_general(a, b, (((0,), (0,)), ((), ())), preferred_element_type=f32)  33.4 us
    pallas_call x2, Pallas kernels, mixer_backward(): pl.pallas_call(backward_kernel, out_shape=(jax.ShapeDtypeStruct((pieces,...  31.9 us
  transfers between devices with their start and end apart: 82, of which 26 were waited for; matrix products, arithmetic and copies ran while one was open for 35% of the time, Pallas kernels for 15%

profile of v7, /device:TPU:0, one launch (start us, length us, event | category | flops | bytes accessed | tf_op | source)
XLA Modules:
  0.0 664.6 jit_solution(2898416456315790667)
XLA Ops:
  1.5 3.1 concatenate.225
  4.6 5.1 collective-permute-start.2
  9.7 2.9 collective-permute-start
  34.8 4.1 taps.1
  38.9 3.5 fusion.91.spectrum
  45.5 3.1 collective-permute-done.6
  56.7 21.3 %collective-permute-done.12 = bf16[256,2048]{1,0:T(8,128)(2,1)} collective-permute-done((bf16[256,2048]{1,0:T(8,128)(2,1)}, bf16[256,2048]{1,0:T(8,128)(2,1)}, u32[]{:S(2)}, u32[]{:S(2)}) %collective-permute-start.12) | collective-permute-done | bytes 1048608 | tf_op jit(solution)/shard_map/ppermute | solution.py:64
  90.3 5.3 collective-permute-done.14
  95.6 9.9 %collective-permute-done.15 = bf16[128,2048]{1,0:T(8,128)(2,1)S(1)} collective-permute-done((bf16[128,2048]{1,0:T(8,128)(2,1)S(1)}, bf16[128,2048]{1,0:T(8,128)(2,1)S(1)}, u32[]{:S(2)}, u32[]{:S(2)}) %collective-permute-start.15) | collective-permute-done | bytes 524320 | tf_op jit(solution)/shard_map/ppermute | solution.py:64
  108.4 2.8 fusion
  114.4 13.1 %fusion.5 = (bf16[1024,2048]{1,0:T(8,128)(2,1)S(1)}, bf16[1024,2048]{1,0:T(8,128)(2,1)S(1)}) fusion(f32[1024]{0:T(1024)S(1)} %add_rsqrt_fusion, f32[2048]{0:T(1024)S(1)} %mul.420, bf16[512,2048]{1,0:T(8,128)(2,1)S(1)} %collective-permute-done.11, bf16[128,2048]{1,0:T(8,128)(2,1)S(1)} %collective-permute-done.10, ...), kind=kLoop, calls=%fused_computation.9 | loop fusion | flops 41943040 | bytes 16793600 | tf_op jit(solution)/shard_map/convert_element_type | solution.py:710
  127.6 3.5 fusion.90.proj
  131.1 7.1 %mixer_forward.2 = (bf16[4,256,256]{2,1,0:T(8,128)(2,1)S(1)}, f32[1024,256]{1,0:T(8,128)S(1)}, bf16[3,1024,256]{2,1,0:T(8,128)(2,1)S(1)}) custom-call(s32[4]{0:T(128)S(1)} %select_reduce_fusion.7.order, s32[3]{0:T(128)S(1)} %get-tuple-element.211.first, s32[3]{0:T(128)S(1)} %get-tuple-element.321.count, f32[4,256,768]{2,1,0:T(8,128)S(1)} %fusion.90.proj, ...), custom_call_target="tpu_custom_call" | custom-call | flops 1024 | bytes 1024 | tf_op jit(solution)/shard_map/mixer_forward/pallas_call | solution.py:556
  140.7 3.5 fusion.92.proj
  144.2 7.5 %mixer_forward.3 = (bf16[4,256,256]{2,1,0:T(8,128)(2,1)S(1)}, f32[1024,256]{1,0:T(8,128)S(1)}, bf16[3,1024,256]{2,1,0:T(8,128)(2,1)S(1)}) custom-call(s32[4]{0:T(128)S(1)} %select_reduce_fusion.7.order, s32[3]{0:T(128)S(1)} %get-tuple-element.207.first, s32[3]{0:T(128)S(1)} %get-tuple-element.319.count, f32[4,256,768]{2,1,0:T(8,128)S(1)} %fusion.92.proj, ...), custom_call_target="tpu_custom_call" | custom-call | flops 1024 | bytes 1024 | tf_op jit(solution)/shard_map/mixer_forward/pallas_call | solution.py:556
  158.3 11.9 %collective-permute-done.23 = bf16[352,2048]{1,0:T(8,128)(2,1)} collective-permute-done((bf16[352,2048]{1,0:T(8,128)(2,1)}, bf16[352,2048]{1,0:T(8,128)(2,1)}, u32[]{:S(2)}, u32[]{:S(2)}) %collective-permute-start.23) | collective-permute-done | bytes 1441824 | tf_op jit(solution)/shard_map/ppermute | solution.py:64
  184.9 9.1 %collective-permute-done.26 = bf16[128,2048]{1,0:T(8,128)(2,1)S(1)} collective-permute-done((bf16[128,2048]{1,0:T(8,128)(2,1)S(1)}, bf16[128,2048]{1,0:T(8,128)(2,1)S(1)}, u32[]{:S(2)}, u32[]{:S(2)}) %collective-permute-start.26) | collective-permute-done | bytes 524320 | tf_op jit(solution)/shard_map/ppermute | solution.py:42
  194.3 2.6 collective-permute-done.25
  204.8 16.4 %collective-permute-done.27 = bf16[256,2048]{1,0:T(8,128)(2,1)S(1)} collective-permute-done((bf16[256,2048]{1,0:T(8,128)(2,1)S(1)}, bf16[256,2048]{1,0:T(8,128)(2,1)S(1)}, u32[]{:S(2)}, u32[]{:S(2)}) %collective-permute-start.27) | collective-permute-done | bytes 1048608 | tf_op jit(solution)/shard_map/ppermute | solution.py:42
  234.1 12.2 %collective-permute-done.35 = bf16[256,2048]{1,0:T(8,128)(2,1)S(1)} collective-permute-done((bf16[256,2048]{1,0:T(8,128)(2,1)S(1)}, bf16[256,2048]{1,0:T(8,128)(2,1)S(1)}, u32[]{:S(2)}, u32[]{:S(2)}) %collective-permute-start.35) | collective-permute-done | bytes 1048608 | tf_op jit(solution)/shard_map/ppermute | solution.py:42
  247.7 3.2 collective-permute-done.37
  254.9 6.9 %collective-permute-done.38 = bf16[128,2048]{1,0:T(8,128)(2,1)S(1)} collective-permute-done((bf16[128,2048]{1,0:T(8,128)(2,1)S(1)}, bf16[128,2048]{1,0:T(8,128)(2,1)S(1)}, u32[]{:S(2)}, u32[]{:S(2)}) %collective-permute-start.38) | collective-permute-done | bytes 524320 | tf_op jit(solution)/shard_map/ppermute | solution.py:42
  261.8 2.7 collective-permute-done.36
  264.9 15.4 %collective-permute-done.32 = bf16[240,2048]{1,0:T(8,128)(2,1)} collective-permute-done((bf16[240,2048]{1,0:T(8,128)(2,1)}, bf16[240,2048]{1,0:T(8,128)(2,1)}, u32[]{:S(2)}, u32[]{:S(2)}) %collective-permute-start.32) | collective-permute-done | bytes 983072 | tf_op jit(solution)/shard_map/ppermute | solution.py:64
  283.8 2.7 copy-done.64
  286.5 8.1 %fusion.94 = f32[704,2048]{1,0:T(8,128)} fusion(bf16[704,2048]{1,0:T(8,128)(2,1)S(1)} %get-tuple-element.274, bf16[2048,2048]{1,0:T(8,128)(2,1)S(1)} %constant_dynamic-update-slice_fusion.2.b), kind=kOutput, calls=%fused_computation.347 | convolution fusion | flops 5905580032 | bytes 17039360 | tf_op jit(solution)/shard_map/dot_general | solution.py:33
  294.6 8.0 %fusion.93 = f32[704,2048]{1,0:T(8,128)} fusion(bf16[704,2048]{1,0:T(8,128)(2,1)S(1)} %get-tuple-element.275, bf16[2048,2048]{1,0:T(8,128)(2,1)S(1)} %constant_dynamic-update-slice_fusion.2.b), kind=kOutput, calls=%fused_computation.346 | convolution fusion | flops 5905580032 | bytes 17039360 | tf_op jit(solution)/shard_map/dot_general | solution.py:33
  302.6 15.5 %multiply_convert_fusion = (bf16[704,2048]{1,0:T(8,128)(2,1)}, bf16[704,2048]{1,0:T(8,128)(2,1)}, bf16[704,2048]{1,0:T(8,128)(2,1)}) fusion(f32[704,2048]{1,0:T(8,128)} %fusion.93, f32[704,2048]{1,0:T(8,128)} %fusion.94, bf16[704,2048]{1,0:T(8,128)(2,1)S(1)} %get-tuple-element.273.b, bf16[2048,2048]{1,0:T(8,128)(2,1)} %constant_dynamic-update-slice_fusion.13.b), kind=kOutput, calls=%fused_computation.11 | convolution fusion | flops 5927206912 | bytes 31457280 | tf_op jit(solution)/shard_map/dot_general | solution.py:33
  318.1 10.5 %product.7 = bf16[704,2048]{1,0:T(8,128)(2,1)} custom-call(bf16[704,2048]{1,0:T(8,128)(2,1)} %get-tuple-element.131.a, bf16[2048,2048]{1,0:T(8,128)(2,1)} %constant_dynamic-update-slice_fusion.13.b), custom_call_target="tpu_custom_call" | custom-call | flops 1024 | bytes 1024 | tf_op jit(solution)/shard_map/product/pallas_call | solution.py:363
  328.5 4.0 fusion.42
  346.0 2.5 convert_add_fusion.4
  349.0 10.7 %collective-permute-done.43 = bf16[128,2048]{1,0:T(8,128)(2,1)S(1)} collective-permute-done((bf16[128,2048]{1,0:T(8,128)(2,1)S(1)}, bf16[128,2048]{1,0:T(8,128)(2,1)S(1)}, u32[]{:S(2)}, u32[]{:S(2)}) %collective-permute-start.43) | collective-permute-done | bytes 524320 | tf_op jit(solution)/shard_map/ppermute | solution.py:42
  366.7 10.3 %product.8 = bf16[704,2048]{1,0:T(8,128)(2,1)} custom-call(bf16[704,2048]{1,0:T(8,128)(2,1)} %get-tuple-element.129.a, bf16[2048,2048]{1,0:T(8,128)(2,1)} %copy-done.28), custom_call_target="tpu_custom_call" | custom-call | flops 1024 | bytes 1024 | tf_op jit(solution)/shard_map/product/pallas_call | solution.py:363
  378.7 10.3 %product.9 = bf16[704,2048]{1,0:T(8,128)(2,1)} custom-call(bf16[704,2048]{1,0:T(8,128)(2,1)} %get-tuple-element.130.a, bf16[2048,2048]{1,0:T(8,128)(2,1)} %copy-done.28), custom_call_target="tpu_custom_call" | custom-call | flops 1024 | bytes 1024 | tf_op jit(solution)/shard_map/product/pallas_call | solution.py:363
  393.9 3.4 multiply_reduce_fusion.4
  397.4 4.2 fusion.74
  405.2 5.6 product.13
  410.8 5.6 product.12
  416.4 5.6 product.11
  422.0 5.6 product.10
  431.9 10.6 %collective-permute-done.66 = bf16[240,2048]{1,0:T(8,128)(2,1)} collective-permute-done((bf16[240,2048]{1,0:T(8,128)(2,1)}, bf16[240,2048]{1,0:T(8,128)(2,1)}, u32[]{:S(2)}, u32[]{:S(2)}) %collective-permute-start.66) | collective-permute-done | bytes 983072 | tf_op jit(solution)/shard_map/ppermute | solution.py:64
  462.8 3.0 pad_maximum_fusion.11
  465.9 3.6 fusion.21
  469.6 15.9 %mixer_backward.2 = (bf16[4,256,768]{2,1,0:T(8,128)(2,1)}, f32[512,256]{1,0:T(8,128)S(1)}, f32[8,768]{1,0:T(8,128)S(1)}) custom-call(s32[4]{0:T(128)S(1)} %select_reduce_fusion.7.order, s32[3]{0:T(128)S(1)} %copy-done.17, s32[3]{0:T(128)S(1)} %copy-done.19, f32[4,256,768]{2,1,0:T(8,128)} %copy-done.4, f32[4,256,256]{2,1,0:T(8,128)S(1)} %bitcast.197, ...), custom_call_target="tpu_custom_call" | custom-call | flops 1024 | bytes 1024 | tf_op jit(solution)/shard_map/mixer_backward/pallas_call | solution.py:582
  492.3 3.2 constant_dynamic-update-slice_fusion.18
  495.5 3.6 fusion.96
  503.1 4.3 fusion.7
  509.7 3.5 collective-permute-done.53
  517.4 3.5 fusion.95
  520.9 4.5 convert_add_fusion.1
  525.4 16.0 %mixer_backward.3 = (bf16[4,256,768]{2,1,0:T(8,128)(2,1)}, f32[512,256]{1,0:T(8,128)S(1)}, f32[8,768]{1,0:T(8,128)S(1)}) custom-call(s32[4]{0:T(128)S(1)} %select_reduce_fusion.7.order, s32[3]{0:T(128)S(1)} %get-tuple-element.207.first, s32[3]{0:T(128)S(1)} %get-tuple-element.319.count, f32[4,256,768]{2,1,0:T(8,128)} %copy-done.3, ...), custom_call_target="tpu_custom_call" | custom-call | flops 1024 | bytes 1024 | tf_op jit(solution)/shard_map/mixer_backward/pallas_call | solution.py:582
  545.5 4.1 convolution_convert_fusion.5
  549.7 3.5 fusion.97
  553.2 3.7 add_convert_fusion
  561.8 3.2 fusion.23
  565.0 4.7 add_bitcast_fusion
  569.8 3.9 convert_add_fusion
  578.8 7.2 %collective-permute-done.70 = bf16[128,2048]{1,0:T(8,128)(2,1)S(1)} collective-permute-done((bf16[128,2048]{1,0:T(8,128)(2,1)S(1)}, bf16[128,2048]{1,0:T(8,128)(2,1)S(1)}, u32[]{:S(2)}, u32[]{:S(2)}) %collective-permute-start.70) | collective-permute-done | bytes 524320 | tf_op jit(solution)/shard_map/ppermute | solution.py:64
  603.5 7.9 %moments.1 = (f32[16,8,256]{2,1,0:T(8,128)}, f32[16,8,256]{2,1,0:T(8,128)}, f32[16,8,256]{2,1,0:T(8,128)}, f32[16,8,256]{2,1,0:T(8,128)}) custom-call(f32[512,256]{1,0:T(8,128)} %add.383.grad, f32[16,8,256]{2,1,0:T(8,128)} %broadcast_in_dim.201.step_re, f32[16,8,256]{2,1,0:T(8,128)} %broadcast_in_dim.202.step_im), custom_call_target="tpu_custom_call" | custom-call | flops 31457280 | bytes 524288 | tf_op jit(solution)/shard_map/moments/pallas_call | solution.py:378
  613.9 9.5 %collective-permute-done.74 = f32[2,4,2,64]{3,1,2,0:T(4,128)S(1)} collective-permute-done((f32[2,4,2,64]{3,1,2,0:T(4,128)S(1)}, f32[2,4,2,64]{3,1,2,0:T(4,128)S(1)}, u32[]{:S(2)}, u32[]{:S(2)}) %collective-permute-start.74) | collective-permute-done | bytes 4128 | tf_op jit(solution)/shard_map/ppermute | solution.py:42
  627.0 2.7 fusion.8
  634.2 3.7 fusion.24
  638.0 12.5 %collective-permute-done.78 = f32[2,64]{1,0:T(2,128)S(1)} collective-permute-done((f32[2,64]{1,0:T(2,128)S(1)}, f32[2,64]{1,0:T(2,128)S(1)}, u32[]{:S(2)}, u32[]{:S(2)}) %collective-permute-start.78) | collective-permute-done | bytes 544 | tf_op jit(solution)/shard_map/ppermute | solution.py:64
  661.2 3.0 fusion.22
  (580 shorter events, 231.1 us)
Async XLA Ops:
  4.6 24.7 %collective-permute-start.2 = (bf16[75,64]{1,0:T(8,128)(2,1)S(1)}, bf16[75,64]{1,0:T(8,128)(2,1)S(1)}, u32[]{:S(2)}, u32[]{:S(2)}) collective-permute-start(bf16[75,64]{1,0:T(8,128)(2,1)S(1)} %concatenate.225), channel_id=1, source_target_pairs={{0,24},{4,28},{16,8},{20,12},{24,0},{28,4},{8,16},{12,20},{1,25},{... | collective-permute-start | bytes 28808 | tf_op jit(solution)/shard_map/ppermute | solution.py:64
  9.7 19.6 %collective-permute-start.1 = (bf16[75,64]{1,0:T(8,128)(2,1)S(1)}, bf16[75,64]{1,0:T(8,128)(2,1)S(1)}, u32[]{:S(2)}, u32[]{:S(2)}) collective-permute-start(bf16[75,64]{1,0:T(8,128)(2,1)S(1)} %concatenate.225), channel_id=1, source_target_pairs={{0,8},{4,12},{16,0},{20,4},{24,16},{28,20},{8,24},{12,28},{1,9},{5... | collective-permute-start | bytes 28808 | tf_op jit(solution)/shard_map/ppermute | solution.py:64
  9.7 19.6 %collective-permute-start = (bf16[75,64]{1,0:T(8,128)(2,1)S(1)}, bf16[75,64]{1,0:T(8,128)(2,1)S(1)}, u32[]{:S(2)}, u32[]{:S(2)}) collective-permute-start(bf16[75,64]{1,0:T(8,128)(2,1)S(1)} %concatenate.225), channel_id=1, source_target_pairs={{0,16},{4,20},{16,24},{20,28},{24,8},{28,12},{8,0},{12,4},{1,17},{... | collective-permute-start | bytes 28808 | tf_op jit(solution)/shard_map/ppermute | solution.py:64
  12.6 39.0 %collective-permute-start.8 = (bf16[256,2048]{1,0:T(8,128)(2,1)}, bf16[256,2048]{1,0:T(8,128)(2,1)}, u32[]{:S(2)}, u32[]{:S(2)}) collective-permute-start(bf16[256,2048]{1,0:T(8,128)(2,1)} %bitcast.204), channel_id=1, source_target_pairs={{0,4},{4,0},{8,12},{12,8},{16,20},{20,16},{24,28},{28,24},{1,5},{5... | collective-permute-start | bytes 3145736 | tf_op jit(solution)/shard_map/ppermute | solution.py:42
  14.2 39.2 %collective-permute-start.3 = (bf16[256,2048]{1,0:T(8,128)(2,1)}, bf16[256,2048]{1,0:T(8,128)(2,1)}, u32[]{:S(2)}, u32[]{:S(2)}) collective-permute-start(bf16[256,2048]{1,0:T(8,128)(2,1)} %bitcast.205), channel_id=1, source_target_pairs={{0,2},{1,3},{2,0},{3,1},{4,6},{5,7},{6,4},{7,5},{8,10},{9,11},{10,... | collective-permute-start | bytes 3145736 | tf_op jit(solution)/shard_map/ppermute | solution.py:42
  30.5 14.3 %collective-permute-start.5 = (bf16[2,4,64]{2,1,0:T(4,128)(2,1)S(1)}, bf16[2,4,64]{2,1,0:T(4,128)(2,1)S(1)}, u32[]{:S(2)}, u32[]{:S(2)}) collective-permute-start(bf16[2,4,64]{2,1,0:T(4,128)(2,1)S(1)} %reshape.523), channel_id=1, source_target_pairs={{0,4},{4,0},{8,12},{12,8},{16,20},{20,16},{24,28},{28,24},{1,5},{5... | collective-permute-start | bytes 3080 | tf_op jit(solution)/shard_map/ppermute | solution.py:42
  32.2 45.8 %collective-permute-start.12 = (bf16[256,2048]{1,0:T(8,128)(2,1)}, bf16[256,2048]{1,0:T(8,128)(2,1)}, u32[]{:S(2)}, u32[]{:S(2)}) collective-permute-start(bf16[256,2048]{1,0:T(8,128)(2,1)} %pad_maximum_fusion.17), channel_id=1, source_target_pairs={{0,16},{4,20},{16,24},{20,28},{24,8},{28,12},{8,0},{12,4},{1,17},{... | collective-permute-start | bytes 3145736 | tf_op jit(solution)/shard_map/ppermute | solution.py:64
  42.3 37.6 %collective-permute-start.13 = (bf16[256,2048]{1,0:T(8,128)(2,1)}, bf16[256,2048]{1,0:T(8,128)(2,1)}, u32[]{:S(2)}, u32[]{:S(2)}) collective-permute-start(bf16[256,2048]{1,0:T(8,128)(2,1)} %pad_maximum_fusion.17), channel_id=1, source_target_pairs={{0,8},{4,12},{16,0},{20,4},{24,16},{28,20},{8,24},{12,28},{1,9},{5... | collective-permute-start | bytes 3145736 | tf_op jit(solution)/shard_map/ppermute | solution.py:64
  52.7 32.3 %collective-permute-start.10 = (bf16[128,2048]{1,0:T(8,128)(2,1)S(1)}, bf16[128,2048]{1,0:T(8,128)(2,1)S(1)}, u32[]{:S(2)}, u32[]{:S(2)}) collective-permute-start(bf16[128,2048]{1,0:T(8,128)(2,1)S(1)} %slice.805), channel_id=1, source_target_pairs={{0,2},{1,3},{2,0},{3,1},{4,6},{5,7},{6,4},{7,5},{8,10},{9,11},{10,... | collective-permute-start | bytes 1572872 | tf_op jit(solution)/shard_map/ppermute | solution.py:42
  54.4 30.6 %collective-permute-start.9 = (bf16[128,2048]{1,0:T(8,128)(2,1)S(1)}, bf16[128,2048]{1,0:T(8,128)(2,1)S(1)}, u32[]{:S(2)}, u32[]{:S(2)}) collective-permute-start(bf16[128,2048]{1,0:T(8,128)(2,1)S(1)} %slice.804), channel_id=1, source_target_pairs={{0,4},{4,0},{8,12},{12,8},{16,20},{20,16},{24,28},{28,24},{1,5},{5... | collective-permute-start | bytes 1572872 | tf_op jit(solution)/shard_map/ppermute | solution.py:42
  56.6 51.8 %collective-permute-start.4 = (bf16[512,2048]{1,0:T(8,128)(2,1)S(1)}, bf16[512,2048]{1,0:T(8,128)(2,1)S(1)}, u32[]{:S(2)}, u32[]{:S(2)}) collective-permute-start(bf16[512,2048]{1,0:T(8,128)(2,1)S(1)} %pad_maximum_fusion.4), channel_id=1, source_target_pairs={{0,1},{1,0},{2,3},{3,2},{4,5},{5,4},{6,7},{7,6},{8,9},{9,8},{10,11... | collective-permute-start | bytes 6291464 | tf_op jit(solution)/shard_map/ppermute | solution.py:42
  82.0 23.4 %collective-permute-start.15 = (bf16[128,2048]{1,0:T(8,128)(2,1)S(1)}, bf16[128,2048]{1,0:T(8,128)(2,1)S(1)}, u32[]{:S(2)}, u32[]{:S(2)}) collective-permute-start(bf16[128,2048]{1,0:T(8,128)(2,1)S(1)} %pad_maximum_fusion.32), channel_id=1, source_target_pairs={{0,8},{4,12},{16,0},{20,4},{24,16},{28,20},{8,24},{12,28},{1,9},{5... | collective-permute-start | bytes 1572872 | tf_op jit(solution)/shard_map/ppermute | solution.py:64
  86.7 24.5 %collective-permute-start.11 = (bf16[512,2048]{1,0:T(8,128)(2,1)S(1)}, bf16[512,2048]{1,0:T(8,128)(2,1)S(1)}, u32[]{:S(2)}, u32[]{:S(2)}) collective-permute-start(bf16[512,2048]{1,0:T(8,128)(2,1)S(1)} %pad_maximum_fusion.5), channel_id=1, source_target_pairs={{0,1},{1,0},{2,3},{3,2},{4,5},{5,4},{6,7},{7,6},{8,9},{9,8},{10,11... | collective-permute-start | bytes 6291464 | tf_op jit(solution)/shard_map/ppermute | solution.py:42
  105.4 64.7 %collective-permute-start.23 = (bf16[352,2048]{1,0:T(8,128)(2,1)}, bf16[352,2048]{1,0:T(8,128)(2,1)}, u32[]{:S(2)}, u32[]{:S(2)}) collective-permute-start(bf16[352,2048]{1,0:T(8,128)(2,1)} %pad_maximum_fusion.14), channel_id=1, source_target_pairs={{0,16},{4,20},{16,24},{20,28},{24,8},{28,12},{8,0},{12,4},{1,17},{... | collective-permute-start | bytes 4325384 | tf_op jit(solution)/shard_map/ppermute | solution.py:64
  106.0 64.6 %collective-permute-start.24 = (bf16[352,2048]{1,0:T(8,128)(2,1)}, bf16[352,2048]{1,0:T(8,128)(2,1)}, u32[]{:S(2)}, u32[]{:S(2)}) collective-permute-start(bf16[352,2048]{1,0:T(8,128)(2,1)} %pad_maximum_fusion.14), channel_id=1, source_target_pairs={{0,8},{4,12},{16,0},{20,4},{24,16},{28,20},{8,24},{12,28},{1,9},{5... | collective-permute-start | bytes 4325384 | tf_op jit(solution)/shard_map/ppermute | solution.py:64
  111.3 40.5 %collective-permute-start.18 = (bf16[256,2048]{1,0:T(8,128)(2,1)S(1)}, bf16[256,2048]{1,0:T(8,128)(2,1)}, u32[]{:S(2)}, u32[]{:S(2)}) collective-permute-start(bf16[256,2048]{1,0:T(8,128)(2,1)S(1)} %bitcast.216), channel_id=1, source_target_pairs={{0,4},{4,0},{8,12},{12,8},{16,20},{20,16},{24,28},{28,24},{1,5},{5... | collective-permute-start | bytes 3145736 | tf_op jit(solution)/shard_map/ppermute | solution.py:42
  111.9 43.0 %collective-permute-start.17 = (bf16[256,2048]{1,0:T(8,128)(2,1)S(1)}, bf16[256,2048]{1,0:T(8,128)(2,1)S(1)}, u32[]{:S(2)}, u32[]{:S(2)}) collective-permute-start(bf16[256,2048]{1,0:T(8,128)(2,1)S(1)} %bitcast.217), channel_id=1, source_target_pairs={{0,2},{1,3},{2,0},{3,1},{4,6},{5,7},{6,4},{7,5},{8,10},{9,11},{10,... | collective-permute-start | bytes 3145736 | tf_op jit(solution)/shard_map/ppermute | solution.py:42
  140.7 40.1 %collective-permute-start.19 = (bf16[512,2048]{1,0:T(8,128)(2,1)}, bf16[512,2048]{1,0:T(8,128)(2,1)}, u32[]{:S(2)}, u32[]{:S(2)}) collective-permute-start(bf16[512,2048]{1,0:T(8,128)(2,1)} %convolution_convert_fusion.2), channel_id=1, source_target_pairs={{0,1},{1,0},{2,3},{3,2},{4,5},{5,4},{6,7},{7,6},{8,9},{9,8},{10,11... | collective-permute-start | bytes 6291464 | tf_op jit(solution)/shard_map/ppermute | solution.py:42
  153.3 24.7 %collective-permute-start.22 = (bf16[128,2048]{1,0:T(8,128)(2,1)S(1)}, bf16[128,2048]{1,0:T(8,128)(2,1)}, u32[]{:S(2)}, u32[]{:S(2)}) collective-permute-start(bf16[128,2048]{1,0:T(8,128)(2,1)S(1)} %slice.827), channel_id=1, source_target_pairs={{0,2},{1,3},{2,0},{3,1},{4,6},{5,7},{6,4},{7,5},{8,10},{9,11},{10,... | collective-permute-start | bytes 1572872 | tf_op jit(solution)/shard_map/ppermute | solution.py:42
  155.6 21.2 %collective-permute-start.20 = (bf16[512,2048]{1,0:T(8,128)(2,1)S(1)}, bf16[512,2048]{1,0:T(8,128)(2,1)S(1)}, u32[]{:S(2)}, u32[]{:S(2)}) collective-permute-start(bf16[512,2048]{1,0:T(8,128)(2,1)S(1)} %convolution_convert_fusion), channel_id=1, source_target_pairs={{0,1},{1,0},{2,3},{3,2},{4,5},{5,4},{6,7},{7,6},{8,9},{9,8},{10,11... | collective-permute-start | bytes 6291464 | tf_op jit(solution)/shard_map/ppermute | solution.py:42
  170.7 31.3 %collective-permute-start.33 = (bf16[512,2048]{1,0:T(8,128)(2,1)}, bf16[512,2048]{1,0:T(8,128)(2,1)}, u32[]{:S(2)}, u32[]{:S(2)}) collective-permute-start(bf16[512,2048]{1,0:T(8,128)(2,1)} %pad_maximum_fusion.6), channel_id=1, source_target_pairs={{0,1},{1,0},{2,3},{3,2},{4,5},{5,4},{6,7},{7,6},{8,9},{9,8},{10,11... | collective-permute-start | bytes 6291464 | tf_op jit(solution)/shard_map/ppermute | solution.py:42
  176.8 46.6 %collective-permute-start.29 = (bf16[176,2048]{1,0:T(8,128)(2,1)}, bf16[176,2048]{1,0:T(8,128)(2,1)S(1)}, u32[]{:S(2)}, u32[]{:S(2)}) collective-permute-start(bf16[176,2048]{1,0:T(8,128)(2,1)} %bitcast.42), channel_id=1, source_target_pairs={{0,16},{4,20},{16,24},{20,28},{24,8},{28,12},{8,0},{12,4},{1,17},{... | collective-permute-start | bytes 2162696 | tf_op jit(solution)/shard_map/ppermute | solution.py:64
  178.1 45.3 %collective-permute-start.30 = (bf16[176,2048]{1,0:T(8,128)(2,1)}, bf16[176,2048]{1,0:T(8,128)(2,1)}, u32[]{:S(2)}, u32[]{:S(2)}) collective-permute-start(bf16[176,2048]{1,0:T(8,128)(2,1)} %bitcast.42), channel_id=1, source_target_pairs={{0,8},{4,12},{16,0},{20,4},{24,16},{28,20},{8,24},{12,28},{1,9},{5... | collective-permute-start | bytes 2162696 | tf_op jit(solution)/shard_map/ppermute | solution.py:64
  197.1 24.0 %collective-permute-start.27 = (bf16[256,2048]{1,0:T(8,128)(2,1)S(1)}, bf16[256,2048]{1,0:T(8,128)(2,1)S(1)}, u32[]{:S(2)}, u32[]{:S(2)}) collective-permute-start(bf16[256,2048]{1,0:T(8,128)(2,1)S(1)} %pad_maximum_fusion.18), channel_id=1, source_target_pairs={{0,2},{1,3},{2,0},{3,1},{4,6},{5,7},{6,4},{7,5},{8,10},{9,11},{10,... | collective-permute-start | bytes 3145736 | tf_op jit(solution)/shard_map/ppermute | solution.py:42
  198.7 23.7 %collective-permute-start.28 = (bf16[256,2048]{1,0:T(8,128)(2,1)S(1)}, bf16[256,2048]{1,0:T(8,128)(2,1)S(1)}, u32[]{:S(2)}, u32[]{:S(2)}) collective-permute-start(bf16[256,2048]{1,0:T(8,128)(2,1)S(1)} %pad_maximum_fusion.19), channel_id=1, source_target_pairs={{0,4},{4,0},{8,12},{12,8},{16,20},{20,16},{24,28},{28,24},{1,5},{5... | collective-permute-start | bytes 3145736 | tf_op jit(solution)/shard_map/ppermute | solution.py:42
  202.0 21.4 %collective-permute-start.34 = (bf16[512,2048]{1,0:T(8,128)(2,1)S(1)}, bf16[512,2048]{1,0:T(8,128)(2,1)S(1)}, u32[]{:S(2)}, u32[]{:S(2)}) collective-permute-start(bf16[512,2048]{1,0:T(8,128)(2,1)S(1)} %pad_maximum_fusion.7), channel_id=1, source_target_pairs={{0,1},{1,0},{2,3},{3,2},{4,5},{5,4},{6,7},{7,6},{8,9},{9,8},{10,11... | collective-permute-start | bytes 6291464 | tf_op jit(solution)/shard_map/ppermute | solution.py:42
  223.4 22.9 %collective-permute-start.35 = (bf16[256,2048]{1,0:T(8,128)(2,1)S(1)}, bf16[256,2048]{1,0:T(8,128)(2,1)S(1)}, u32[]{:S(2)}, u32[]{:S(2)}) collective-permute-start(bf16[256,2048]{1,0:T(8,128)(2,1)S(1)} %multiply_convert_fusion.3), channel_id=1, source_target_pairs={{0,2},{1,3},{2,0},{3,1},{4,6},{5,7},{6,4},{7,5},{8,10},{9,11},{10,... | collective-permute-start | bytes 3145736 | tf_op jit(solution)/shard_map/ppermute | solution.py:42
  228.0 22.9 %collective-permute-start.37 = (bf16[256,2048]{1,0:T(8,128)(2,1)S(1)}, bf16[256,2048]{1,0:T(8,128)(2,1)S(1)}, u32[]{:S(2)}, u32[]{:S(2)}) collective-permute-start(bf16[256,2048]{1,0:T(8,128)(2,1)S(1)} %multiply_convert_fusion.3), channel_id=1, source_target_pairs={{0,4},{4,0},{8,12},{12,8},{16,20},{20,16},{24,28},{28,24},{1,5},{5... | collective-permute-start | bytes 3145736 | tf_op jit(solution)/shard_map/ppermute | solution.py:42
  232.6 47.8 %collective-permute-start.31 = (bf16[288,2048]{1,0:T(8,128)(2,1)S(1)}, bf16[288,2048]{1,0:T(8,128)(2,1)}, u32[]{:S(2)}, u32[]{:S(2)}) collective-permute-start(bf16[288,2048]{1,0:T(8,128)(2,1)S(1)} %pad_maximum_fusion.15), channel_id=1, source_target_pairs={{0,16},{4,20},{16,24},{20,28},{24,8},{28,12},{8,0},{12,4},{1,17},{... | collective-permute-start | bytes 3538952 | tf_op jit(solution)/shard_map/ppermute | solution.py:64
  246.6 36.5 %collective-permute-start.39 = (bf16[512,2048]{1,0:T(8,128)(2,1)S(1)}, bf16[512,2048]{1,0:T(8,128)(2,1)S(1)}, u32[]{:S(2)}, u32[]{:S(2)}) collective-permute-start(bf16[512,2048]{1,0:T(8,128)(2,1)S(1)} %pad_maximum_fusion.8), channel_id=1, source_target_pairs={{0,1},{1,0},{2,3},{3,2},{4,5},{5,4},{6,7},{7,6},{8,9},{9,8},{10,11... | collective-permute-start | bytes 6291464 | tf_op jit(solution)/shard_map/ppermute | solution.py:42
  246.9 33.5 %collective-permute-start.32 = (bf16[240,2048]{1,0:T(8,128)(2,1)}, bf16[240,2048]{1,0:T(8,128)(2,1)}, u32[]{:S(2)}, u32[]{:S(2)}) collective-permute-start(bf16[240,2048]{1,0:T(8,128)(2,1)} %pad_maximum_fusion.28), channel_id=1, source_target_pairs={{0,8},{4,12},{16,0},{20,4},{24,16},{28,20},{8,24},{12,28},{1,9},{5... | collective-permute-start | bytes 2949128 | tf_op jit(solution)/shard_map/ppermute | solution.py:64
  264.8 18.7 %collective-permute-start.40 = (bf16[512,2048]{1,0:T(8,128)(2,1)S(1)}, bf16[512,2048]{1,0:T(8,128)(2,1)S(1)}, u32[]{:S(2)}, u32[]{:S(2)}) collective-permute-start(bf16[512,2048]{1,0:T(8,128)(2,1)S(1)} %pad_maximum_fusion.9), channel_id=1, source_target_pairs={{0,1},{1,0},{2,3},{3,2},{4,5},{5,4},{6,7},{7,6},{8,9},{9,8},{10,11... | collective-permute-start | bytes 6291464 | tf_op jit(solution)/shard_map/ppermute | solution.py:42
  345.3 14.3 %collective-permute-start.43 = (bf16[128,2048]{1,0:T(8,128)(2,1)S(1)}, bf16[128,2048]{1,0:T(8,128)(2,1)S(1)}, u32[]{:S(2)}, u32[]{:S(2)}) collective-permute-start(bf16[128,2048]{1,0:T(8,128)(2,1)S(1)} %get-tuple-element.250), channel_id=1, source_target_pairs={{0,2},{1,3},{2,0},{3,1},{4,6},{5,7},{6,4},{7,5},{8,10},{9,11},{10,... | collective-permute-start | bytes 1572872 | tf_op jit(solution)/shard_map/ppermute | solution.py:42
  363.9 30.0 %collective-permute-start.45 = (bf16[256,2048]{1,0:T(8,128)(2,1)}, bf16[256,2048]{1,0:T(8,128)(2,1)}, u32[]{:S(2)}, u32[]{:S(2)}) collective-permute-start(bf16[256,2048]{1,0:T(8,128)(2,1)} %pad_maximum_fusion.20), channel_id=1, source_target_pairs={{0,2},{1,3},{2,0},{3,1},{4,6},{5,7},{6,4},{7,5},{8,10},{9,11},{10,... | collective-permute-start | bytes 3145736 | tf_op jit(solution)/shard_map/ppermute | solution.py:42
  365.3 28.6 %collective-permute-start.46 = (bf16[256,2048]{1,0:T(8,128)(2,1)}, bf16[256,2048]{1,0:T(8,128)(2,1)}, u32[]{:S(2)}, u32[]{:S(2)}) collective-permute-start(bf16[256,2048]{1,0:T(8,128)(2,1)} %pad_maximum_fusion.21), channel_id=1, source_target_pairs={{0,4},{4,0},{8,12},{12,8},{16,20},{20,16},{24,28},{28,24},{1,5},{5... | collective-permute-start | bytes 3145736 | tf_op jit(solution)/shard_map/ppermute | solution.py:42
  393.3 49.1 %collective-permute-start.65 = (bf16[288,2048]{1,0:T(8,128)(2,1)}, bf16[288,2048]{1,0:T(8,128)(2,1)}, u32[]{:S(2)}, u32[]{:S(2)}) collective-permute-start(bf16[288,2048]{1,0:T(8,128)(2,1)} %pad_maximum_fusion.16), channel_id=1, source_target_pairs={{0,16},{4,20},{16,24},{20,28},{24,8},{28,12},{8,0},{12,4},{1,17},{... | collective-permute-start | bytes 3538952 | tf_op jit(solution)/shard_map/ppermute | solution.py:64
  401.6 26.0 %collective-permute-start.49 = (bf16[256,2048]{1,0:T(8,128)(2,1)}, bf16[256,2048]{1,0:T(8,128)(2,1)}, u32[]{:S(2)}, u32[]{:S(2)}) collective-permute-start(bf16[256,2048]{1,0:T(8,128)(2,1)} %get-tuple-element.203), channel_id=1, source_target_pairs={{0,4},{4,0},{8,12},{12,8},{16,20},{20,16},{24,28},{28,24},{1,5},{5... | collective-permute-start | bytes 3145736 | tf_op jit(solution)/shard_map/ppermute | solution.py:42
  403.2 27.0 %collective-permute-start.47 = (bf16[256,2048]{1,0:T(8,128)(2,1)}, bf16[256,2048]{1,0:T(8,128)(2,1)}, u32[]{:S(2)}, u32[]{:S(2)}) collective-permute-start(bf16[256,2048]{1,0:T(8,128)(2,1)} %get-tuple-element.203), channel_id=1, source_target_pairs={{0,2},{1,3},{2,0},{3,1},{4,6},{5,7},{6,4},{7,5},{8,10},{9,11},{10,... | collective-permute-start | bytes 3145736 | tf_op jit(solution)/shard_map/ppermute | solution.py:42
  403.8 38.6 %collective-permute-start.66 = (bf16[240,2048]{1,0:T(8,128)(2,1)}, bf16[240,2048]{1,0:T(8,128)(2,1)}, u32[]{:S(2)}, u32[]{:S(2)}) collective-permute-start(bf16[240,2048]{1,0:T(8,128)(2,1)} %pad_maximum_fusion.29), channel_id=1, source_target_pairs={{0,8},{4,12},{16,0},{20,4},{24,16},{28,20},{8,24},{12,28},{1,9},{5... | collective-permute-start | bytes 2949128 | tf_op jit(solution)/shard_map/ppermute | solution.py:64
  428.7 29.6 %collective-permute-start.50 = (bf16[128,2048]{1,0:T(8,128)(2,1)S(1)}, bf16[128,2048]{1,0:T(8,128)(2,1)S(1)}, u32[]{:S(2)}, u32[]{:S(2)}) collective-permute-start(bf16[128,2048]{1,0:T(8,128)(2,1)S(1)} %slice.844), channel_id=1, source_target_pairs={{0,2},{1,3},{2,0},{3,1},{4,6},{5,7},{6,4},{7,5},{8,10},{9,11},{10,... | collective-permute-start | bytes 1572872 | tf_op jit(solution)/shard_map/ppermute | solution.py:42
  431.3 27.0 %collective-permute-start.48 = (bf16[128,2048]{1,0:T(8,128)(2,1)S(1)}, bf16[128,2048]{1,0:T(8,128)(2,1)S(1)}, u32[]{:S(2)}, u32[]{:S(2)}) collective-permute-start(bf16[128,2048]{1,0:T(8,128)(2,1)S(1)} %slice.843), channel_id=1, source_target_pairs={{0,4},{4,0},{8,12},{12,8},{16,20},{20,16},{24,28},{28,24},{1,5},{5... | collective-permute-start | bytes 1572872 | tf_op jit(solution)/shard_map/ppermute | solution.py:42
  444.2 21.6 %collective-permute-start.57 = (bf16[512,2048]{1,0:T(8,128)(2,1)S(1)}, bf16[512,2048]{1,0:T(8,128)(2,1)S(1)}, u32[]{:S(2)}, u32[]{:S(2)}) collective-permute-start(bf16[512,2048]{1,0:T(8,128)(2,1)S(1)} %pad_maximum_fusion.10), channel_id=1, source_target_pairs={{0,1},{1,0},{2,3},{3,2},{4,5},{5,4},{6,7},{7,6},{8,9},{9,8},{10,11... | collective-permute-start | bytes 6291464 | tf_op jit(solution)/shard_map/ppermute | solution.py:42
  456.2 100.7 %collective-permute-start.67 = (bf16[528,2048]{1,0:T(8,128)(2,1)}, bf16[528,2048]{1,0:T(8,128)(2,1)}, u32[]{:S(2)}, u32[]{:S(2)}) collective-permute-start(bf16[528,2048]{1,0:T(8,128)(2,1)} %get-tuple-element.157), channel_id=1, source_target_pairs={{0,16},{4,20},{16,24},{20,28},{24,8},{28,12},{8,0},{12,4},{1,17},{... | collective-permute-start | bytes 6488072 | tf_op jit(solution)/shard_map/ppermute | solution.py:64
  456.8 100.1 %collective-permute-start.68 = (bf16[528,2048]{1,0:T(8,128)(2,1)}, bf16[528,2048]{1,0:T(8,128)(2,1)}, u32[]{:S(2)}, u32[]{:S(2)}) collective-permute-start(bf16[528,2048]{1,0:T(8,128)(2,1)} %get-tuple-element.158), channel_id=1, source_target_pairs={{0,8},{4,12},{16,0},{20,4},{24,16},{28,20},{8,24},{12,28},{1,9},{5... | collective-permute-start | bytes 6488072 | tf_op jit(solution)/shard_map/ppermute | solution.py:64
  458.3 31.7 %collective-permute-start.52 = (bf16[512,2048]{1,0:T(8,128)(2,1)S(1)}, bf16[512,2048]{1,0:T(8,128)(2,1)S(1)}, u32[]{:S(2)}, u32[]{:S(2)}) collective-permute-start(bf16[512,2048]{1,0:T(8,128)(2,1)S(1)} %copy-done.71), channel_id=1, source_target_pairs={{0,1},{1,0},{2,3},{3,2},{4,5},{5,4},{6,7},{7,6},{8,9},{9,8},{10,11... | collective-permute-start | bytes 6291464 | tf_op jit(solution)/shard_map/ppermute | solution.py:42
  460.7 38.5 %collective-permute-start.51 = (bf16[512,2048]{1,0:T(8,128)(2,1)}, bf16[512,2048]{1,0:T(8,128)(2,1)}, u32[]{:S(2)}, u32[]{:S(2)}) collective-permute-start(bf16[512,2048]{1,0:T(8,128)(2,1)} %product.11), channel_id=1, source_target_pairs={{0,1},{1,0},{2,3},{3,2},{4,5},{5,4},{6,7},{7,6},{8,9},{9,8},{10,11... | collective-permute-start | bytes 6291464 | tf_op jit(solution)/shard_map/ppermute | solution.py:42
  465.8 25.9 %collective-permute-start.59 = (bf16[512,2048]{1,0:T(8,128)(2,1)}, bf16[512,2048]{1,0:T(8,128)(2,1)}, u32[]{:S(2)}, u32[]{:S(2)}) collective-permute-start(bf16[512,2048]{1,0:T(8,128)(2,1)} %pad_maximum_fusion.11), channel_id=1, source_target_pairs={{0,1},{1,0},{2,3},{3,2},{4,5},{5,4},{6,7},{7,6},{8,9},{9,8},{10,11... | collective-permute-start | bytes 6291464 | tf_op jit(solution)/shard_map/ppermute | solution.py:42
  489.9 31.0 %collective-permute-start.58 = (bf16[512,2048]{1,0:T(8,128)(2,1)S(1)}, bf16[512,2048]{1,0:T(8,128)(2,1)S(1)}, u32[]{:S(2)}, u32[]{:S(2)}) collective-permute-start(bf16[512,2048]{1,0:T(8,128)(2,1)S(1)} %convolution_convert_fusion.6), channel_id=1, source_target_pairs={{0,1},{1,0},{2,3},{3,2},{4,5},{5,4},{6,7},{7,6},{8,9},{9,8},{10,11... | collective-permute-start | bytes 6291464 | tf_op jit(solution)/shard_map/ppermute | solution.py:42
  491.7 16.7 %collective-permute-start.54 = (bf16[128,2048]{1,0:T(8,128)(2,1)S(1)}, bf16[128,2048]{1,0:T(8,128)(2,1)S(1)}, u32[]{:S(2)}, u32[]{:S(2)}) collective-permute-start(bf16[128,2048]{1,0:T(8,128)(2,1)S(1)} %get-tuple-element.247), channel_id=1, source_target_pairs={{0,2},{1,3},{2,0},{3,1},{4,6},{5,7},{6,4},{7,5},{8,10},{9,11},{10,... | collective-permute-start | bytes 1572872 | tf_op jit(solution)/shard_map/ppermute | solution.py:42
  499.2 14.1 %collective-permute-start.53 = (bf16[128,2048]{1,0:T(8,128)(2,1)S(1)}, bf16[128,2048]{1,0:T(8,128)(2,1)S(1)}, u32[]{:S(2)}, u32[]{:S(2)}) collective-permute-start(bf16[128,2048]{1,0:T(8,128)(2,1)S(1)} %get-tuple-element.248), channel_id=1, source_target_pairs={{0,4},{4,0},{8,12},{12,8},{16,20},{20,16},{24,28},{28,24},{1,5},{5... | collective-permute-start | bytes 1572872 | tf_op jit(solution)/shard_map/ppermute | solution.py:42
  514.4 31.1 %collective-permute-start.55 = (bf16[256,2048]{1,0:T(8,128)(2,1)}, bf16[256,2048]{1,0:T(8,128)(2,1)}, u32[]{:S(2)}, u32[]{:S(2)}) collective-permute-start(bf16[256,2048]{1,0:T(8,128)(2,1)} %pad_maximum_fusion.22), channel_id=1, source_target_pairs={{0,2},{1,3},{2,0},{3,1},{4,6},{5,7},{6,4},{7,5},{8,10},{9,11},{10,... | collective-permute-start | bytes 3145736 | tf_op jit(solution)/shard_map/ppermute | solution.py:42
  515.9 29.6 %collective-permute-start.56 = (bf16[256,2048]{1,0:T(8,128)(2,1)}, bf16[256,2048]{1,0:T(8,128)(2,1)}, u32[]{:S(2)}, u32[]{:S(2)}) collective-permute-start(bf16[256,2048]{1,0:T(8,128)(2,1)} %pad_maximum_fusion.23), channel_id=1, source_target_pairs={{0,4},{4,0},{8,12},{12,8},{16,20},{20,16},{24,28},{28,24},{1,5},{5... | collective-permute-start | bytes 3145736 | tf_op jit(solution)/shard_map/ppermute | solution.py:42
  549.6 20.2 %collective-permute-start.60 = (bf16[512,2048]{1,0:T(8,128)(2,1)S(1)}, bf16[512,2048]{1,0:T(8,128)(2,1)S(1)}, u32[]{:S(2)}, u32[]{:S(2)}) collective-permute-start(bf16[512,2048]{1,0:T(8,128)(2,1)S(1)} %convolution_convert_fusion.5), channel_id=1, source_target_pairs={{0,1},{1,0},{2,3},{3,2},{4,5},{5,4},{6,7},{7,6},{8,9},{9,8},{10,11... | collective-permute-start | bytes 6291464 | tf_op jit(solution)/shard_map/ppermute | solution.py:42
  559.5 19.2 %collective-permute-start.69 = (bf16[128,2048]{1,0:T(8,128)(2,1)S(1)}, bf16[128,2048]{1,0:T(8,128)(2,1)S(1)}, u32[]{:S(2)}, u32[]{:S(2)}) collective-permute-start(bf16[128,2048]{1,0:T(8,128)(2,1)S(1)} %pad_maximum_fusion.33), channel_id=1, source_target_pairs={{0,16},{4,20},{16,24},{20,28},{24,8},{28,12},{8,0},{12,4},{1,17},{... | collective-permute-start | bytes 1572872 | tf_op jit(solution)/shard_map/ppermute | solution.py:64
  561.0 25.0 %collective-permute-start.70 = (bf16[128,2048]{1,0:T(8,128)(2,1)S(1)}, bf16[128,2048]{1,0:T(8,128)(2,1)S(1)}, u32[]{:S(2)}, u32[]{:S(2)}) collective-permute-start(bf16[128,2048]{1,0:T(8,128)(2,1)S(1)} %pad_maximum_fusion.34), channel_id=1, source_target_pairs={{0,8},{4,12},{16,0},{20,4},{24,16},{28,20},{8,24},{12,28},{1,9},{5... | collective-permute-start | bytes 1572872 | tf_op jit(solution)/shard_map/ppermute | solution.py:64
  573.8 14.3 %collective-permute-start.62 = (bf16[128,2048]{1,0:T(8,128)(2,1)S(1)}, bf16[128,2048]{1,0:T(8,128)(2,1)S(1)}, u32[]{:S(2)}, u32[]{:S(2)}) collective-permute-start(bf16[128,2048]{1,0:T(8,128)(2,1)S(1)} %get-tuple-element.244), channel_id=1, source_target_pairs={{0,2},{1,3},{2,0},{3,1},{4,6},{5,7},{6,4},{7,5},{8,10},{9,11},{10,... | collective-permute-start | bytes 1572872 | tf_op jit(solution)/shard_map/ppermute | solution.py:42
  592.3 19.2 %collective-permute-start.73 = (f32[2,2,4,2,64]{4,2,3,1,0:T(4,128)S(1)}, f32[2,2,4,2,64]{4,2,3,1,0:T(4,128)S(1)}, u32[]{:S(2)}, u32[]{:S(2)}) collective-permute-start(f32[2,2,4,2,64]{4,2,3,1,0:T(4,128)S(1)} %slice.894), channel_id=1, source_target_pairs={{0,1},{1,0},{2,3},{3,2},{4,5},{5,4},{6,7},{7,6},{8,9},{9,8},{10,11... | collective-permute-start | bytes 24584 | tf_op jit(solution)/shard_map/ppermute | solution.py:42
  597.4 29.6 %collective-permute-start.63 = (bf16[256,2048]{1,0:T(8,128)(2,1)}, bf16[256,2048]{1,0:T(8,128)(2,1)S(1)}, u32[]{:S(2)}, u32[]{:S(2)}) collective-permute-start(bf16[256,2048]{1,0:T(8,128)(2,1)} %pad_maximum_fusion.24), channel_id=1, source_target_pairs={{0,2},{1,3},{2,0},{3,1},{4,6},{5,7},{6,4},{7,5},{8,10},{9,11},{10,... | collective-permute-start | bytes 3145736 | tf_op jit(solution)/shard_map/ppermute | solution.py:42
  598.9 28.1 %collective-permute-start.64 = (bf16[256,2048]{1,0:T(8,128)(2,1)}, bf16[256,2048]{1,0:T(8,128)(2,1)}, u32[]{:S(2)}, u32[]{:S(2)}) collective-permute-start(bf16[256,2048]{1,0:T(8,128)(2,1)} %pad_maximum_fusion.25), channel_id=1, source_target_pairs={{0,4},{4,0},{8,12},{12,8},{16,20},{20,16},{24,28},{28,24},{1,5},{5... | collective-permute-start | bytes 3145736 | tf_op jit(solution)/shard_map/ppermute | solution.py:42
  601.5 57.7 %collective-permute-start.71 = (bf16[256,2048]{1,0:T(8,128)(2,1)}, bf16[256,2048]{1,0:T(8,128)(2,1)}, u32[]{:S(2)}, u32[]{:S(2)}) collective-permute-start(bf16[256,2048]{1,0:T(8,128)(2,1)} %pad_maximum_fusion.26), channel_id=1, source_target_pairs={{0,16},{4,20},{16,24},{20,28},{24,8},{28,12},{8,0},{12,4},{1,17},{... | collective-permute-start | bytes 3145736 | tf_op jit(solution)/shard_map/ppermute | solution.py:64
  603.5 55.7 %collective-permute-start.72 = (bf16[256,2048]{1,0:T(8,128)(2,1)}, bf16[256,2048]{1,0:T(8,128)(2,1)}, u32[]{:S(2)}, u32[]{:S(2)}) collective-permute-start(bf16[256,2048]{1,0:T(8,128)(2,1)} %pad_maximum_fusion.27), channel_id=1, source_target_pairs={{0,8},{4,12},{16,0},{20,4},{24,16},{28,20},{8,24},{12,28},{1,9},{5... | collective-permute-start | bytes 3145736 | tf_op jit(solution)/shard_map/ppermute | solution.py:64
  629.8 20.8 %collective-permute-start.78 = (f32[2,64]{1,0:T(2,128)S(1)}, f32[2,64]{1,0:T(2,128)S(1)}, u32[]{:S(2)}, u32[]{:S(2)}) collective-permute-start(f32[2,64]{1,0:T(2,128)S(1)} %bitcast.261), channel_id=1, source_target_pairs={{0,24},{4,28},{16,8},{20,12},{24,0},{28,4},{8,16},{12,20},{1,25},{... | collective-permute-start | bytes 1544 | tf_op jit(solution)/shard_map/ppermute | solution.py:64
  631.3 19.8 %collective-permute-start.76 = (f32[2,64]{1,0:T(2,128)S(1)}, f32[2,64]{1,0:T(2,128)S(1)}, u32[]{:S(2)}, u32[]{:S(2)}) collective-permute-start(f32[2,64]{1,0:T(2,128)S(1)} %bitcast.260), channel_id=1, source_target_pairs={{0,8},{4,12},{16,0},{20,4},{24,16},{28,20},{8,24},{12,28},{1,9},{5... | collective-permute-start | bytes 1544 | tf_op jit(solution)/shard_map/ppermute | solution.py:64
  632.3 21.2 %collective-permute-start.77 = (f32[2,64]{1,0:T(2,128)S(1)}, f32[2,64]{1,0:T(2,128)S(1)}, u32[]{:S(2)}, u32[]{:S(2)}) collective-permute-start(f32[2,64]{1,0:T(2,128)S(1)} %bitcast.259), channel_id=1, source_target_pairs={{0,16},{4,20},{16,24},{20,28},{24,8},{28,12},{8,0},{12,4},{1,17},{... | collective-permute-start | bytes 1544 | tf_op jit(solution)/shard_map/ppermute | solution.py:64
  (126 other events, 1358.9 us)

commit v8 on v7

--- a/solution.py
+++ b/solution.py
@@ -378,9 +378,7 @@
     return pl.pallas_call(
         moment_kernel,
         out_shape=(shape,) * 4,
-        cost_estimate=pl.CostEstimate(
-            flops=16 * 15 * SPAN * width, bytes_accessed=4 * SPAN * width, transcendentals=0
-        ),
+        cost_estimate=light,
         name="moments",
     )(grad, step_re, step_im)
 
@@ -667,7 +665,7 @@
     )
     small_pieces = gather_small(small)
     small_all = jnp.concatenate(small_pieces, axis=1)
-    (first_own, first_other), first_stages = gather_rows(tokens[0])
+    (first_own, first_other), first_stages = gather_rows(tokens[0], small_pieces[1:])
     gains = small_all[small.shape[0] - 2 :].reshape(2, outer, own)
     gains = jnp.stack([gains, swap(gains, "wide", 1)])
     gains = jnp.stack([gains] + [swap(gains, "narrow", k) for k in range(2, narrow, 2)])
@@ -679,7 +677,7 @@
     gain_all = gains.transpose(3, 0, 1, 2, 4).reshape(2, width)
     gain_first, gain_last = gain_all[0], gain_all[1]
 
-    def reduce_gain(values, tokens):
+    def place_gain(values):
         values = values.reshape(2, outer, 2, narrow, own).transpose(1, 2, 3, 0, 4)
         values = picked(piece_outer, outer, values).transpose(1, 0, 2, 3, 4)
         values = picked(sides, 2, values).transpose(2, 0, 1, 3, 4)
@@ -689,8 +687,7 @@
         for k in range(1, narrow // 2):
             summed = summed + swap(total[k], "narrow", 2 * k)
         summed = summed[0] + swap(summed[1], "wide", 1)
-        [summed] = after([summed], tokens)
-        return scatter_small([summed[j] for j in range(outer)])
+        return summed
 
     documents = jnp.concatenate([doc_blocks, doc_pad], axis=0)
     [documents] = after([documents], small_pieces[1:])
@@ -701,7 +698,7 @@
     weights = [Gather(shard) for shard in shards]
     in_all, out_all, down_all, gate_all, up_all = weights
     steps = outer // 2
-    last = small_pieces[1:]
+    last = []
     for at in range(steps):
         last = ring_step([in_all, out_all], last)
 
@@ -767,7 +764,7 @@
         last = ring_step([down_all, gate_all], last, odds)
     last_two = last
     for at in range(steps - 1):
-        last_two = ring_step([up_all], last_two)
+        last_two = ring_step([up_all] if at else [down_all, up_all], last_two)
     ready = after([mixed[0][1], mixed[1][1]], upstream_stages[0])
     evens = [nn(ready[r][parts[0]], out_all).astype(bf16) for r in range(2)]
     mixer_out, stages = scatter_rows(
@@ -779,7 +776,7 @@
     low_second = (middle * rate_last * gain_last).astype(bf16)
     (second_own, second_other), second_stages = gather_rows(low_second, last_two + upstream_stages[2])
     rows_second = jnp.concatenate(second_own + second_other, axis=0)
-    last = ring_step([down_all, gate_all, up_all], last_two + stages[1], second_stages[1])
+    last = ring_step([gate_all, up_all], last_two, second_stages[1])
 
     down_all, gate_all = [jnp.concatenate(w.pieces(), axis=0) for w in (down_all, gate_all)]
     up_all = jnp.concatenate(up_all.pieces(), axis=0)
@@ -791,11 +788,7 @@
     hidden = (silu * up_pre).astype(bf16)
     d_gate = (d_hidden * up_pre * sig * (1.0 + gate_pre * (1.0 - sig))).astype(bf16)
     d_up = (d_hidden * silu).astype(bf16)
-    grad_down = product(hidden, rows_upstream, "nn", bf16)
-    d_gate, d_up = after([d_gate, d_up], [grad_down])
     parts = [slice(p, p + even) for p in range(0, 2 * slots, even)]
-    grads = [Scatter(jnp.split(grad_down, outer, axis=0))]
-
     def second_share(n):
         p = parts[n]
         return (tn(d_gate[:, p], gate_all) + tn(d_up[:, p], up_all)).astype(bf16)
@@ -808,9 +801,12 @@
     d_middle = upstream + norm_back(middle, rate_last, gain_last, d_second)
     (middle_own, middle_other), middle_stages = gather_rows(d_middle.astype(bf16))
     rows_dmiddle = [jnp.concatenate(middle_own, axis=0), jnp.concatenate(middle_other, axis=0)]
-    [d_gate] = after([d_gate], cores + evens)
+    [hidden] = after([hidden], cores + evens)
+    grad_down = product(hidden, rows_upstream, "nn", bf16)
+    grads = [Scatter(jnp.split(grad_down, outer, axis=0))]
+    [d_gate] = after([d_gate], stages[0])
     grad_gate = product(d_gate, rows_second, "nn", bf16)
-    [d_up] = after([d_up], stages[0] + [grad_gate])
+    [d_up] = after([d_up], [grad_gate])
     grad_up = product(d_up, rows_second, "nn", bf16)
     [hidden] = after([hidden], [grad_up])
     down_shares = [product(hidden, down_all, "tn", bf16, n) for n in (0, 1)]
@@ -861,11 +857,8 @@
     chunks = grad_in.reshape(3, outer, own, width)
     in_sum = Scatter([chunks[:, j].reshape(3 * own, width) for j in range(outer)])
     out_sum = Scatter(jnp.split(grad_out, outer, axis=0))
-    last = ring_step([in_sum, out_sum], last, stages[0])
-    d_filter, *_ = after([d_filter], last + stages[0])
-    gain_grads = after([jnp.stack([grad_gain_one / gain_first, grad_gain_two])], stages[0])
-    gain_share = reduce_gain(gain_grads[0], stages[1])
-
+    d_filter, *_ = after([d_filter], last + [grad_in])
+    gain_grads = jnp.stack([grad_gain_one / gain_first, grad_gain_two])
     sum_re, sum_im, mom_re, mom_im = filter_moments(d_filter, step_re, step_im)
     full_re = lag * sum_re + 8.0 * mom_re
     full_im = lag * sum_im + 8.0 * mom_im
@@ -883,11 +876,18 @@
         ],
         axis=0,
     ).astype(bf16)
-    [small_grad] = after([small_grad], stages[1])
+    last = ring_step([in_sum, out_sum], last, stages[0] + [gain_grads, small_grad])
+    gain_sums = place_gain(gain_grads).transpose(1, 0, 2).reshape(2, channels)
+    gain_high = gain_sums.astype(bf16)
+    gain_low = (gain_sums - gain_high.astype(f32)).astype(bf16)
+    small_grad = jnp.concatenate([small_grad, gain_high, gain_low], axis=0)
+    for at in range(1, steps):
+        last = ring_step([in_sum], last)
+    [small_grad] = after([small_grad], last)
     small_share = scatter_small(jnp.split(small_grad, outer, axis=1))
-
+    gain_share = small_share[-4:-2] + small_share[-2:]
     for at in range(1, steps):
-        last = ring_step([in_sum, out_sum], last, [gain_share, small_share])
+        last = ring_step([out_sum], last)
 
     at = 9 + poles
     return (
@@ -899,7 +899,7 @@
         small_share[:9].reshape(3, 3, own),
         small_share[9:at].T,
         small_share[at : at + poles].T,
-        small_share[at + poles :].T,
+        small_share[at + poles : at + 3 * poles].T,
         gain_share[1],
         grads[1].total.T,
         grads[2].total.T,

time: 673 us -> 686 us (1.019)
    ppermute x27 -> x26, waiting for transfers between devices: 95.8 us -> 98.2 us  [along(): return lax.ppermute(values, 'wide', pairs)]
    unnamed x235 -> x236, local copies, waits for them, and re-layouts: 29.5 us -> 30.1 us
    ppermute x27 -> x26, starting transfers between devices: 36 us -> 35.5 us  [along(): return lax.ppermute(values, 'wide', pairs)]
  transfers between devices with their start and end apart: 82 -> 81, of which waited for: 26 -> 25; matrix products, arithmetic and copies ran while one was open for 35% -> 35% of each run, Pallas kernels for 15% -> 16%
where the time goes in v8:
time: 686 us; the launch traced here: 678 us
  waiting for transfers between devices  189 us (28%)
  other arithmetic  118 us (17%)
  Pallas kernels  112 us (16%)
  matrix products  104 us (15%)
  starting transfers between devices  76.7 us (11%)
  local copies, waits for them, and re-layouts  75.5 us (11%)
    ppermute x26, waiting for transfers between devices, along(): return lax.ppermute(values, 'wide', pairs)  98.2 us
    ppermute x55, waiting for transfers between devices, swap(): return lax.ppermute(values, axis, [(i, i ^ shift) for i in range(size)])  91 us
    pallas_call x7, Pallas kernels, product(): pl.pallas_call(partial(product_kernel, kind=kind), grid=(columns // side,...  53.2 us
    dot_general x7, matrix products, nt(): lax.dot_general(a, b, (((1,), (1,)), ((), ())), preferred_element_type=f32)  45.6 us
    ppermute x55, starting transfers between devices, swap(): return lax.ppermute(values, axis, [(i, i ^ shift) for i in range(size)])  41.2 us
    ppermute x26, starting transfers between devices, along(): return lax.ppermute(values, 'wide', pairs)  35.5 us
    pallas_call x2, Pallas kernels, mixer_backward(): pl.pallas_call(backward_kernel, out_shape=(jax.ShapeDtypeStruct((pieces,...  32.2 us
    dot_general x12, matrix products, tn(): lax.dot_general(a, b, (((0,), (0,)), ((), ())), preferred_element_type=f32)  32.2 us
  transfers between devices with their start and end apart: 81, of which 25 were waited for; matrix products, arithmetic and copies ran while one was open for 35% of the time, Pallas kernels for 16%

profile of v8, /device:TPU:0, one launch (start us, length us, event | category | flops | bytes accessed | tf_op | source)
XLA Modules:
  0.0 678.1 jit_solution(14275413608639504589)
XLA Ops:
  1.5 3.1 concatenate.234
  4.6 5.1 collective-permute-start.2
  9.7 2.9 collective-permute-start
  23.9 2.5 constant_dynamic-update-slice_fusion.1
  26.5 2.5 pad_maximum_fusion.14
  35.9 4.1 taps.1
  39.9 3.5 fusion.91.spectrum
  45.4 9.0 %collective-permute-done.5 = bf16[2,4,64]{2,1,0:T(4,128)(2,1)S(1)} collective-permute-done((bf16[2,4,64]{2,1,0:T(4,128)(2,1)S(1)}, bf16[2,4,64]{2,1,0:T(4,128)(2,1)S(1)}, u32[]{:S(2)}, u32[]{:S(2)}) %collective-permute-start.5) | collective-permute-done | bytes 1056 | tf_op jit(solution)/shard_map/ppermute | solution.py:42
  76.0 6.8 %collective-permute-done.10 = bf16[128,2048]{1,0:T(8,128)(2,1)S(1)} collective-permute-done((bf16[128,2048]{1,0:T(8,128)(2,1)S(1)}, bf16[128,2048]{1,0:T(8,128)(2,1)S(1)}, u32[]{:S(2)}, u32[]{:S(2)}) %collective-permute-start.10) | collective-permute-done | bytes 524320 | tf_op jit(solution)/shard_map/ppermute | solution.py:42
  82.8 2.4 collective-permute-done.9
  95.2 3.6 fusion
  102.9 12.4 %fusion.5 = (bf16[1024,2048]{1,0:T(8,128)(2,1)S(1)}, bf16[1024,2048]{1,0:T(8,128)(2,1)S(1)}) fusion(f32[1024]{0:T(1024)S(1)} %add_rsqrt_fusion, f32[2048]{0:T(1024)S(1)} %mul.420, bf16[512,2048]{1,0:T(8,128)(2,1)S(1)} %collective-permute-done.11, bf16[128,2048]{1,0:T(8,128)(2,1)S(1)} %collective-permute-done.10, ...), kind=kLoop, calls=%fused_computation.9 | loop fusion | flops 41943040 | bytes 16793600 | tf_op jit(solution)/shard_map/convert_element_type | solution.py:707
  115.3 3.5 fusion.90.proj
  118.9 7.3 %mixer_forward.2 = (bf16[4,256,256]{2,1,0:T(8,128)(2,1)S(1)}, f32[1024,256]{1,0:T(8,128)S(1)}, bf16[3,1024,256]{2,1,0:T(8,128)(2,1)S(1)}) custom-call(s32[4]{0:T(128)S(1)} %select_reduce_fusion.7.order, s32[3]{0:T(128)S(1)} %get-tuple-element.209.first, s32[3]{0:T(128)S(1)} %get-tuple-element.317.count, f32[4,256,768]{2,1,0:T(8,128)S(1)} %fusion.90.proj, ...), custom_call_target="tpu_custom_call" | custom-call | flops 1024 | bytes 1024 | tf_op jit(solution)/shard_map/mixer_forward/pallas_call | solution.py:554
  128.6 3.5 fusion.92.proj
  132.1 7.1 %mixer_forward.3 = (bf16[4,256,256]{2,1,0:T(8,128)(2,1)S(1)}, f32[1024,256]{1,0:T(8,128)S(1)}, bf16[3,1024,256]{2,1,0:T(8,128)(2,1)S(1)}) custom-call(s32[4]{0:T(128)S(1)} %select_reduce_fusion.7.order, s32[3]{0:T(128)S(1)} %get-tuple-element.205.first, s32[3]{0:T(128)S(1)} %get-tuple-element.315.count, f32[4,256,768]{2,1,0:T(8,128)S(1)} %fusion.92.proj, ...), custom_call_target="tpu_custom_call" | custom-call | flops 1024 | bytes 1024 | tf_op jit(solution)/shard_map/mixer_forward/pallas_call | solution.py:554
  144.8 12.6 %collective-permute-done.24 = bf16[352,2048]{1,0:T(8,128)(2,1)} collective-permute-done((bf16[352,2048]{1,0:T(8,128)(2,1)}, bf16[352,2048]{1,0:T(8,128)(2,1)}, u32[]{:S(2)}, u32[]{:S(2)}) %collective-permute-start.24) | collective-permute-done | bytes 1441824 | tf_op jit(solution)/shard_map/ppermute | solution.py:64
  168.3 2.5 collective-permute-start.29
  177.9 10.6 %collective-permute-done.25 = bf16[128,2048]{1,0:T(8,128)(2,1)S(1)} collective-permute-done((bf16[128,2048]{1,0:T(8,128)(2,1)S(1)}, bf16[128,2048]{1,0:T(8,128)(2,1)S(1)}, u32[]{:S(2)}, u32[]{:S(2)}) %collective-permute-start.25) | collective-permute-done | bytes 524320 | tf_op jit(solution)/shard_map/ppermute | solution.py:42
  190.1 27.5 %collective-permute-done.29 = bf16[272,2048]{1,0:T(8,128)(2,1)S(1)} collective-permute-done((bf16[272,2048]{1,0:T(8,128)(2,1)S(1)}, bf16[272,2048]{1,0:T(8,128)(2,1)S(1)}, u32[]{:S(2)}, u32[]{:S(2)}) %collective-permute-start.29) | collective-permute-done | bytes 1114144 | tf_op jit(solution)/shard_map/ppermute | solution.py:64
  222.0 2.9 collective-permute-start.31
  232.7 18.6 %collective-permute-done.35 = bf16[256,2048]{1,0:T(8,128)(2,1)S(1)} collective-permute-done((bf16[256,2048]{1,0:T(8,128)(2,1)S(1)}, bf16[256,2048]{1,0:T(8,128)(2,1)S(1)}, u32[]{:S(2)}, u32[]{:S(2)}) %collective-permute-start.35) | collective-permute-done | bytes 1048608 | tf_op jit(solution)/shard_map/ppermute | solution.py:42
  257.5 10.1 %collective-permute-done.38 = bf16[128,2048]{1,0:T(8,128)(2,1)S(1)} collective-permute-done((bf16[128,2048]{1,0:T(8,128)(2,1)S(1)}, bf16[128,2048]{1,0:T(8,128)(2,1)S(1)}, u32[]{:S(2)}, u32[]{:S(2)}) %collective-permute-start.38) | collective-permute-done | bytes 524320 | tf_op jit(solution)/shard_map/ppermute | solution.py:42
  271.0 2.4 collective-permute-done.40
  273.6 8.1 %fusion.94 = f32[704,2048]{1,0:T(8,128)} fusion(bf16[704,2048]{1,0:T(8,128)(2,1)S(1)} %get-tuple-element.277, bf16[2048,2048]{1,0:T(8,128)(2,1)S(1)} %constant_dynamic-update-slice_fusion.2.b), kind=kOutput, calls=%fused_computation.353 | convolution fusion | flops 5905580032 | bytes 17039360 | tf_op jit(solution)/shard_map/dot_general | solution.py:33
  281.7 8.1 %fusion.93 = f32[704,2048]{1,0:T(8,128)} fusion(bf16[704,2048]{1,0:T(8,128)(2,1)S(1)} %get-tuple-element.276, bf16[2048,2048]{1,0:T(8,128)(2,1)S(1)} %constant_dynamic-update-slice_fusion.2.b), kind=kOutput, calls=%fused_computation.352 | convolution fusion | flops 5905580032 | bytes 17039360 | tf_op jit(solution)/shard_map/dot_general | solution.py:33
  289.8 15.4 %multiply_convert_fusion = (bf16[704,2048]{1,0:T(8,128)(2,1)}, bf16[704,2048]{1,0:T(8,128)(2,1)S(1)}, bf16[704,2048]{1,0:T(8,128)(2,1)}) fusion(f32[704,2048]{1,0:T(8,128)} %fusion.93, f32[704,2048]{1,0:T(8,128)} %fusion.94, bf16[704,2048]{1,0:T(8,128)(2,1)S(1)} %get-tuple-element.268.b, bf16[2048,2048]{1,0:T(8,128)(2,1)} %constant_dynamic-update-slice_fusion.11.b), kind=kOutput, calls=%fused_computation.11 | convolution fusion | flops 5927206912 | bytes 31457280 | tf_op jit(solution)/shard_map/dot_general | solution.py:33
  325.1 10.5 %collective-permute-done.44 = bf16[128,2048]{1,0:T(8,128)(2,1)S(1)} collective-permute-done((bf16[128,2048]{1,0:T(8,128)(2,1)S(1)}, bf16[128,2048]{1,0:T(8,128)(2,1)S(1)}, u32[]{:S(2)}, u32[]{:S(2)}) %collective-permute-start.44) | collective-permute-done | bytes 524320 | tf_op jit(solution)/shard_map/ppermute | solution.py:42
  341.4 10.3 %product.13 = bf16[704,2048]{1,0:T(8,128)(2,1)} custom-call(bf16[704,2048]{1,0:T(8,128)(2,1)} %get-tuple-element.129.a, bf16[2048,2048]{1,0:T(8,128)(2,1)} %constant_dynamic-update-slice_fusion.11.b), custom_call_target="tpu_custom_call" | custom-call | flops 1024 | bytes 1024 | tf_op jit(solution)/shard_map/product/pallas_call | solution.py:363
  353.7 10.2 %product.7 = bf16[704,2048]{1,0:T(8,128)(2,1)} custom-call(bf16[704,2048]{1,0:T(8,128)(2,1)} %copy-done.48, bf16[2048,2048]{1,0:T(8,128)(2,1)} %copy-done.26), custom_call_target="tpu_custom_call" | custom-call | flops 1024 | bytes 1024 | tf_op jit(solution)/shard_map/product/pallas_call | solution.py:363
  364.0 10.2 %product.8 = bf16[704,2048]{1,0:T(8,128)(2,1)} custom-call(bf16[704,2048]{1,0:T(8,128)(2,1)} %get-tuple-element.128.a, bf16[2048,2048]{1,0:T(8,128)(2,1)} %copy-done.26), custom_call_target="tpu_custom_call" | custom-call | flops 1024 | bytes 1024 | tf_op jit(solution)/shard_map/product/pallas_call | solution.py:363
  377.5 3.3 multiply_reduce_fusion.4
  381.2 4.3 fusion.75
  390.8 5.6 product.12
  396.5 5.6 product.11
  402.0 5.7 product.10
  407.7 5.6 product.9
  419.7 16.6 %collective-permute-done.66 = bf16[240,2048]{1,0:T(8,128)(2,1)} collective-permute-done((bf16[240,2048]{1,0:T(8,128)(2,1)}, bf16[240,2048]{1,0:T(8,128)(2,1)}, u32[]{:S(2)}, u32[]{:S(2)}) %collective-permute-start.66) | collective-permute-done | bytes 983072 | tf_op jit(solution)/shard_map/ppermute | solution.py:64
  454.9 2.9 pad_maximum_fusion.11
  458.0 3.6 fusion.21
  461.7 16.0 %mixer_backward.2 = (bf16[4,256,768]{2,1,0:T(8,128)(2,1)}, f32[512,256]{1,0:T(8,128)S(1)}, f32[8,768]{1,0:T(8,128)S(1)}) custom-call(s32[4]{0:T(128)S(1)} %select_reduce_fusion.7.order, s32[3]{0:T(128)S(1)} %copy-done.17, s32[3]{0:T(128)S(1)} %copy-done.19, f32[4,256,768]{2,1,0:T(8,128)} %copy-done.4, f32[4,256,256]{2,1,0:T(8,128)S(1)} %bitcast.191, ...), custom_call_target="tpu_custom_call" | custom-call | flops 1024 | bytes 1024 | tf_op jit(solution)/shard_map/mixer_backward/pallas_call | solution.py:580
  485.0 3.2 constant_dynamic-update-slice_fusion.16
  488.2 3.6 fusion.96
  492.4 2.5 convert_add_fusion.3
  494.9 4.3 fusion.7
  501.4 4.5 collective-permute-done.53
  508.6 3.5 fusion.95
  512.1 4.5 convert_add_fusion.1
  516.6 16.2 %mixer_backward.3 = (bf16[4,256,768]{2,1,0:T(8,128)(2,1)}, f32[512,256]{1,0:T(8,128)S(1)}, f32[8,768]{1,0:T(8,128)S(1)}) custom-call(s32[4]{0:T(128)S(1)} %select_reduce_fusion.7.order, s32[3]{0:T(128)S(1)} %get-tuple-element.205.first, s32[3]{0:T(128)S(1)} %get-tuple-element.315.count, f32[4,256,768]{2,1,0:T(8,128)} %copy-done.3, ...), custom_call_target="tpu_custom_call" | custom-call | flops 1024 | bytes 1024 | tf_op jit(solution)/shard_map/mixer_backward/pallas_call | solution.py:580
  536.9 5.4 convolution_convert_fusion.5
  542.4 3.6 fusion.97
  546.0 4.9 add_convert_fusion
  550.9 7.9 %moments.1 = (f32[16,8,256]{2,1,0:T(8,128)}, f32[16,8,256]{2,1,0:T(8,128)}, f32[16,8,256]{2,1,0:T(8,128)}, f32[16,8,256]{2,1,0:T(8,128)}) custom-call(f32[512,256]{1,0:T(8,128)} %add.374.grad, f32[16,8,256]{2,1,0:T(8,128)} %broadcast_in_dim.201.step_re, f32[16,8,256]{2,1,0:T(8,128)} %broadcast_in_dim.202.step_im), custom_call_target="tpu_custom_call" | custom-call | flops 1024 | bytes 1024 | tf_op jit(solution)/shard_map/moments/pallas_call | solution.py:378
  558.9 3.1 fusion.77
  566.0 3.2 fusion.23
  569.2 4.7 add_bitcast_fusion
  574.0 6.2 convert_add_fusion
  582.5 3.0 multiply_reduce_fusion.1
  596.2 8.5 %collective-permute-done.77 = f32[4,2,64]{2,0,1:T(4,128)S(1)} collective-permute-done((f32[4,2,64]{2,0,1:T(4,128)S(1)}, f32[4,2,64]{2,0,1:T(4,128)S(1)}, u32[]{:S(2)}, u32[]{:S(2)}) %collective-permute-start.77) | collective-permute-done | bytes 2080 | tf_op jit(solution)/shard_map/ppermute | solution.py:42
  620.8 16.7 %collective-permute-done.71 = bf16[192,2048]{1,0:T(8,128)(2,1)S(1)} collective-permute-done((bf16[192,2048]{1,0:T(8,128)(2,1)S(1)}, bf16[192,2048]{1,0:T(8,128)(2,1)S(1)}, u32[]{:S(2)}, u32[]{:S(2)}) %collective-permute-start.71) | collective-permute-done | bytes 786464 | tf_op jit(solution)/shard_map/ppermute | solution.py:64
  637.5 16.0 %collective-permute-done.72 = bf16[192,2048]{1,0:T(8,128)(2,1)S(1)} collective-permute-done((bf16[192,2048]{1,0:T(8,128)(2,1)S(1)}, bf16[192,2048]{1,0:T(8,128)(2,1)S(1)}, u32[]{:S(2)}, u32[]{:S(2)}) %collective-permute-start.72) | collective-permute-done | bytes 786464 | tf_op jit(solution)/shard_map/ppermute | solution.py:64
  663.6 2.9 fusion.8
  667.5 5.5 collective-permute-done.74
  674.7 3.1 fusion.24
  (585 shorter events, 229.2 us)
Async XLA Ops:
  4.6 24.4 %collective-permute-start.2 = (bf16[75,64]{1,0:T(8,128)(2,1)S(1)}, bf16[75,64]{1,0:T(8,128)(2,1)S(1)}, u32[]{:S(2)}, u32[]{:S(2)}) collective-permute-start(bf16[75,64]{1,0:T(8,128)(2,1)S(1)} %concatenate.234), channel_id=1, source_target_pairs={{0,24},{4,28},{16,8},{20,12},{24,0},{28,4},{8,16},{12,20},{1,25},{... | collective-permute-start | bytes 28808 | tf_op jit(solution)/shard_map/ppermute | solution.py:64
  9.7 19.2 %collective-permute-start.1 = (bf16[75,64]{1,0:T(8,128)(2,1)S(1)}, bf16[75,64]{1,0:T(8,128)(2,1)S(1)}, u32[]{:S(2)}, u32[]{:S(2)}) collective-permute-start(bf16[75,64]{1,0:T(8,128)(2,1)S(1)} %concatenate.234), channel_id=1, source_target_pairs={{0,8},{4,12},{16,0},{20,4},{24,16},{28,20},{8,24},{12,28},{1,9},{5... | collective-permute-start | bytes 28808 | tf_op jit(solution)/shard_map/ppermute | solution.py:64
  9.7 19.3 %collective-permute-start = (bf16[75,64]{1,0:T(8,128)(2,1)S(1)}, bf16[75,64]{1,0:T(8,128)(2,1)S(1)}, u32[]{:S(2)}, u32[]{:S(2)}) collective-permute-start(bf16[75,64]{1,0:T(8,128)(2,1)S(1)} %concatenate.234), channel_id=1, source_target_pairs={{0,16},{4,20},{16,24},{20,28},{24,8},{28,12},{8,0},{12,4},{1,17},{... | collective-permute-start | bytes 28808 | tf_op jit(solution)/shard_map/ppermute | solution.py:64
  14.9 46.9 %collective-permute-start.12 = (bf16[256,2048]{1,0:T(8,128)(2,1)}, bf16[256,2048]{1,0:T(8,128)(2,1)}, u32[]{:S(2)}, u32[]{:S(2)}) collective-permute-start(bf16[256,2048]{1,0:T(8,128)(2,1)} %pad_maximum_fusion.17), channel_id=1, source_target_pairs={{0,16},{4,20},{16,24},{20,28},{24,8},{28,12},{8,0},{12,4},{1,17},{... | collective-permute-start | bytes 3145736 | tf_op jit(solution)/shard_map/ppermute | solution.py:64
  14.9 48.8 %collective-permute-start.13 = (bf16[256,2048]{1,0:T(8,128)(2,1)}, bf16[256,2048]{1,0:T(8,128)(2,1)}, u32[]{:S(2)}, u32[]{:S(2)}) collective-permute-start(bf16[256,2048]{1,0:T(8,128)(2,1)} %pad_maximum_fusion.17), channel_id=1, source_target_pairs={{0,8},{4,12},{16,0},{20,4},{24,16},{28,20},{8,24},{12,28},{1,9},{5... | collective-permute-start | bytes 3145736 | tf_op jit(solution)/shard_map/ppermute | solution.py:64
  29.0 14.4 %collective-permute-start.16 = (s32[2,3]{1,0:T(2,128)S(1)}, s32[2,3]{1,0:T(2,128)S(1)}, u32[]{:S(2)}, u32[]{:S(2)}) collective-permute-start(s32[2,3]{1,0:T(2,128)S(1)} %pad_add_fusion), channel_id=1, source_target_pairs={{0,4},{4,0},{8,12},{12,8},{16,20},{20,16},{24,28},{28,24},{1,5},{5... | collective-permute-start | bytes 80 | tf_op jit(solution)/shard_map/ppermute | solution.py:42
  30.9 37.0 %collective-permute-start.8 = (bf16[256,2048]{1,0:T(8,128)(2,1)}, bf16[256,2048]{1,0:T(8,128)(2,1)}, u32[]{:S(2)}, u32[]{:S(2)}) collective-permute-start(bf16[256,2048]{1,0:T(8,128)(2,1)} %bitcast), channel_id=1, source_target_pairs={{0,4},{4,0},{8,12},{12,8},{16,20},{20,16},{24,28},{28,24},{1,5},{5... | collective-permute-start | bytes 3145736 | tf_op jit(solution)/shard_map/ppermute | solution.py:42
  31.4 39.2 %collective-permute-start.3 = (bf16[256,2048]{1,0:T(8,128)(2,1)}, bf16[256,2048]{1,0:T(8,128)(2,1)}, u32[]{:S(2)}, u32[]{:S(2)}) collective-permute-start(bf16[256,2048]{1,0:T(8,128)(2,1)} %bitcast), channel_id=1, source_target_pairs={{0,2},{1,3},{2,0},{3,1},{4,6},{5,7},{6,4},{7,5},{8,10},{9,11},{10,... | collective-permute-start | bytes 3145736 | tf_op jit(solution)/shard_map/ppermute | solution.py:42
  65.8 24.6 %collective-permute-start.14 = (bf16[128,2048]{1,0:T(8,128)(2,1)S(1)}, bf16[128,2048]{1,0:T(8,128)(2,1)S(1)}, u32[]{:S(2)}, u32[]{:S(2)}) collective-permute-start(bf16[128,2048]{1,0:T(8,128)(2,1)S(1)} %pad_maximum_fusion.33), channel_id=1, source_target_pairs={{0,16},{4,20},{16,24},{20,28},{24,8},{28,12},{8,0},{12,4},{1,17},{... | collective-permute-start | bytes 1572872 | tf_op jit(solution)/shard_map/ppermute | solution.py:64
  67.1 25.0 %collective-permute-start.15 = (bf16[128,2048]{1,0:T(8,128)(2,1)S(1)}, bf16[128,2048]{1,0:T(8,128)(2,1)S(1)}, u32[]{:S(2)}, u32[]{:S(2)}) collective-permute-start(bf16[128,2048]{1,0:T(8,128)(2,1)S(1)} %pad_maximum_fusion.34), channel_id=1, source_target_pairs={{0,8},{4,12},{16,0},{20,4},{24,16},{28,20},{8,24},{12,28},{1,9},{5... | collective-permute-start | bytes 1572872 | tf_op jit(solution)/shard_map/ppermute | solution.py:64
  69.0 13.8 %collective-permute-start.10 = (bf16[128,2048]{1,0:T(8,128)(2,1)S(1)}, bf16[128,2048]{1,0:T(8,128)(2,1)S(1)}, u32[]{:S(2)}, u32[]{:S(2)}) collective-permute-start(bf16[128,2048]{1,0:T(8,128)(2,1)S(1)} %slice.791), channel_id=1, source_target_pairs={{0,2},{1,3},{2,0},{3,1},{4,6},{5,7},{6,4},{7,5},{8,10},{9,11},{10,... | collective-permute-start | bytes 1572872 | tf_op jit(solution)/shard_map/ppermute | solution.py:42
  71.6 13.5 %collective-permute-start.9 = (bf16[128,2048]{1,0:T(8,128)(2,1)S(1)}, bf16[128,2048]{1,0:T(8,128)(2,1)S(1)}, u32[]{:S(2)}, u32[]{:S(2)}) collective-permute-start(bf16[128,2048]{1,0:T(8,128)(2,1)S(1)} %slice.790), channel_id=1, source_target_pairs={{0,4},{4,0},{8,12},{12,8},{16,20},{20,16},{24,28},{28,24},{1,5},{5... | collective-permute-start | bytes 1572872 | tf_op jit(solution)/shard_map/ppermute | solution.py:42
  75.9 19.3 %collective-permute-start.4 = (bf16[512,2048]{1,0:T(8,128)(2,1)S(1)}, bf16[512,2048]{1,0:T(8,128)(2,1)S(1)}, u32[]{:S(2)}, u32[]{:S(2)}) collective-permute-start(bf16[512,2048]{1,0:T(8,128)(2,1)S(1)} %pad_maximum_fusion.4), channel_id=1, source_target_pairs={{0,1},{1,0},{2,3},{3,2},{4,5},{5,4},{6,7},{7,6},{8,9},{9,8},{10,11... | collective-permute-start | bytes 6291464 | tf_op jit(solution)/shard_map/ppermute | solution.py:42
  92.0 52.7 %collective-permute-start.23 = (bf16[352,2048]{1,0:T(8,128)(2,1)}, bf16[352,2048]{1,0:T(8,128)(2,1)}, u32[]{:S(2)}, u32[]{:S(2)}) collective-permute-start(bf16[352,2048]{1,0:T(8,128)(2,1)} %pad_maximum_fusion.14), channel_id=1, source_target_pairs={{0,16},{4,20},{16,24},{20,28},{24,8},{28,12},{8,0},{12,4},{1,17},{... | collective-permute-start | bytes 4325384 | tf_op jit(solution)/shard_map/ppermute | solution.py:64
  92.7 64.8 %collective-permute-start.24 = (bf16[352,2048]{1,0:T(8,128)(2,1)}, bf16[352,2048]{1,0:T(8,128)(2,1)}, u32[]{:S(2)}, u32[]{:S(2)}) collective-permute-start(bf16[352,2048]{1,0:T(8,128)(2,1)} %pad_maximum_fusion.14), channel_id=1, source_target_pairs={{0,8},{4,12},{16,0},{20,4},{24,16},{28,20},{8,24},{12,28},{1,9},{5... | collective-permute-start | bytes 4325384 | tf_op jit(solution)/shard_map/ppermute | solution.py:64
  98.8 41.6 %collective-permute-start.18 = (bf16[256,2048]{1,0:T(8,128)(2,1)S(1)}, bf16[256,2048]{1,0:T(8,128)(2,1)}, u32[]{:S(2)}, u32[]{:S(2)}) collective-permute-start(bf16[256,2048]{1,0:T(8,128)(2,1)S(1)} %bitcast.205), channel_id=1, source_target_pairs={{0,4},{4,0},{8,12},{12,8},{16,20},{20,16},{24,28},{28,24},{1,5},{5... | collective-permute-start | bytes 3145736 | tf_op jit(solution)/shard_map/ppermute | solution.py:42
  99.4 42.7 %collective-permute-start.17 = (bf16[256,2048]{1,0:T(8,128)(2,1)S(1)}, bf16[256,2048]{1,0:T(8,128)(2,1)S(1)}, u32[]{:S(2)}, u32[]{:S(2)}) collective-permute-start(bf16[256,2048]{1,0:T(8,128)(2,1)S(1)} %bitcast.206), channel_id=1, source_target_pairs={{0,2},{1,3},{2,0},{3,1},{4,6},{5,7},{6,4},{7,5},{8,10},{9,11},{10,... | collective-permute-start | bytes 3145736 | tf_op jit(solution)/shard_map/ppermute | solution.py:42
  128.6 46.5 %collective-permute-start.19 = (bf16[512,2048]{1,0:T(8,128)(2,1)}, bf16[512,2048]{1,0:T(8,128)(2,1)}, u32[]{:S(2)}, u32[]{:S(2)}) collective-permute-start(bf16[512,2048]{1,0:T(8,128)(2,1)} %convolution_convert_fusion.2), channel_id=1, source_target_pairs={{0,1},{1,0},{2,3},{3,2},{4,5},{5,4},{6,7},{7,6},{8,9},{9,8},{10,11... | collective-permute-start | bytes 6291464 | tf_op jit(solution)/shard_map/ppermute | solution.py:42
  141.5 26.3 %collective-permute-start.22 = (bf16[128,2048]{1,0:T(8,128)(2,1)S(1)}, bf16[128,2048]{1,0:T(8,128)(2,1)S(1)}, u32[]{:S(2)}, u32[]{:S(2)}) collective-permute-start(bf16[128,2048]{1,0:T(8,128)(2,1)S(1)} %slice.813), channel_id=1, source_target_pairs={{0,2},{1,3},{2,0},{3,1},{4,6},{5,7},{6,4},{7,5},{8,10},{9,11},{10,... | collective-permute-start | bytes 1572872 | tf_op jit(solution)/shard_map/ppermute | solution.py:42
  142.2 26.1 %collective-permute-start.21 = (bf16[128,2048]{1,0:T(8,128)(2,1)S(1)}, bf16[128,2048]{1,0:T(8,128)(2,1)S(1)}, u32[]{:S(2)}, u32[]{:S(2)}) collective-permute-start(bf16[128,2048]{1,0:T(8,128)(2,1)S(1)} %slice.812), channel_id=1, source_target_pairs={{0,4},{4,0},{8,12},{12,8},{16,20},{20,16},{24,28},{28,24},{1,5},{5... | collective-permute-start | bytes 1572872 | tf_op jit(solution)/shard_map/ppermute | solution.py:42
  144.8 72.9 %collective-permute-start.33 = (bf16[512,2048]{1,0:T(8,128)(2,1)S(1)}, bf16[512,2048]{1,0:T(8,128)(2,1)S(1)}, u32[]{:S(2)}, u32[]{:S(2)}) collective-permute-start(bf16[512,2048]{1,0:T(8,128)(2,1)S(1)} %pad_maximum_fusion.6), channel_id=1, source_target_pairs={{0,1},{1,0},{2,3},{3,2},{4,5},{5,4},{6,7},{7,6},{8,9},{9,8},{10,11... | collective-permute-start | bytes 6291464 | tf_op jit(solution)/shard_map/ppermute | solution.py:42
  157.4 14.9 %collective-permute-start.20 = (bf16[512,2048]{1,0:T(8,128)(2,1)S(1)}, bf16[512,2048]{1,0:T(8,128)(2,1)S(1)}, u32[]{:S(2)}, u32[]{:S(2)}) collective-permute-start(bf16[512,2048]{1,0:T(8,128)(2,1)S(1)} %convolution_convert_fusion), channel_id=1, source_target_pairs={{0,1},{1,0},{2,3},{3,2},{4,5},{5,4},{6,7},{7,6},{8,9},{9,8},{10,11... | collective-permute-start | bytes 6291464 | tf_op jit(solution)/shard_map/ppermute | solution.py:42
  167.8 50.7 %collective-permute-start.30 = (bf16[256,2048]{1,0:T(8,128)(2,1)}, bf16[256,2048]{1,0:T(8,128)(2,1)}, u32[]{:S(2)}, u32[]{:S(2)}) collective-permute-start(bf16[256,2048]{1,0:T(8,128)(2,1)} %pad_maximum_fusion.20), channel_id=1, source_target_pairs={{0,8},{4,12},{16,0},{20,4},{24,16},{28,20},{8,24},{12,28},{1,9},{5... | collective-permute-start | bytes 3145736 | tf_op jit(solution)/shard_map/ppermute | solution.py:64
  168.3 49.3 %collective-permute-start.29 = (bf16[272,2048]{1,0:T(8,128)(2,1)S(1)}, bf16[272,2048]{1,0:T(8,128)(2,1)S(1)}, u32[]{:S(2)}, u32[]{:S(2)}) collective-permute-start(bf16[272,2048]{1,0:T(8,128)(2,1)S(1)} %pad_maximum_fusion.16), channel_id=1, source_target_pairs={{0,16},{4,20},{16,24},{20,28},{24,8},{28,12},{8,0},{12,4},{1,17},{... | collective-permute-start | bytes 3342344 | tf_op jit(solution)/shard_map/ppermute | solution.py:64
  173.5 15.2 %collective-permute-start.26 = (bf16[128,2048]{1,0:T(8,128)(2,1)S(1)}, bf16[128,2048]{1,0:T(8,128)(2,1)S(1)}, u32[]{:S(2)}, u32[]{:S(2)}) collective-permute-start(bf16[128,2048]{1,0:T(8,128)(2,1)S(1)} %get-tuple-element.270), channel_id=1, source_target_pairs={{0,2},{1,3},{2,0},{3,1},{4,6},{5,7},{6,4},{7,5},{8,10},{9,11},{10,... | collective-permute-start | bytes 1572872 | tf_op jit(solution)/shard_map/ppermute | solution.py:42
  175.0 13.5 %collective-permute-start.25 = (bf16[128,2048]{1,0:T(8,128)(2,1)S(1)}, bf16[128,2048]{1,0:T(8,128)(2,1)S(1)}, u32[]{:S(2)}, u32[]{:S(2)}) collective-permute-start(bf16[128,2048]{1,0:T(8,128)(2,1)S(1)} %get-tuple-element.271), channel_id=1, source_target_pairs={{0,4},{4,0},{8,12},{12,8},{16,20},{20,16},{24,28},{28,24},{1,5},{5... | collective-permute-start | bytes 1572872 | tf_op jit(solution)/shard_map/ppermute | solution.py:42
  189.0 35.8 %collective-permute-start.27 = (bf16[256,2048]{1,0:T(8,128)(2,1)S(1)}, bf16[256,2048]{1,0:T(8,128)(2,1)S(1)}, u32[]{:S(2)}, u32[]{:S(2)}) collective-permute-start(bf16[256,2048]{1,0:T(8,128)(2,1)S(1)} %pad_maximum_fusion.18), channel_id=1, source_target_pairs={{0,2},{1,3},{2,0},{3,1},{4,6},{5,7},{6,4},{7,5},{8,10},{9,11},{10,... | collective-permute-start | bytes 3145736 | tf_op jit(solution)/shard_map/ppermute | solution.py:42
  189.6 35.2 %collective-permute-start.28 = (bf16[256,2048]{1,0:T(8,128)(2,1)S(1)}, bf16[256,2048]{1,0:T(8,128)(2,1)S(1)}, u32[]{:S(2)}, u32[]{:S(2)}) collective-permute-start(bf16[256,2048]{1,0:T(8,128)(2,1)S(1)} %pad_maximum_fusion.19), channel_id=1, source_target_pairs={{0,4},{4,0},{8,12},{12,8},{16,20},{20,16},{24,28},{28,24},{1,5},{5... | collective-permute-start | bytes 3145736 | tf_op jit(solution)/shard_map/ppermute | solution.py:42
  221.7 47.6 %collective-permute-start.32 = (bf16[160,2048]{1,0:T(8,128)(2,1)}, bf16[160,2048]{1,0:T(8,128)(2,1)}, u32[]{:S(2)}, u32[]{:S(2)}) collective-permute-start(bf16[160,2048]{1,0:T(8,128)(2,1)} %pad_maximum_fusion.32), channel_id=1, source_target_pairs={{0,8},{4,12},{16,0},{20,4},{24,16},{28,20},{8,24},{12,28},{1,9},{5... | collective-permute-start | bytes 1966088 | tf_op jit(solution)/shard_map/ppermute | solution.py:64
  222.0 47.3 %collective-permute-start.31 = (bf16[192,2048]{1,0:T(8,128)(2,1)}, bf16[192,2048]{1,0:T(8,128)(2,1)S(1)}, u32[]{:S(2)}, u32[]{:S(2)}) collective-permute-start(bf16[192,2048]{1,0:T(8,128)(2,1)} %pad_maximum_fusion.29), channel_id=1, source_target_pairs={{0,16},{4,20},{16,24},{20,28},{24,8},{28,12},{8,0},{12,4},{1,17},{... | collective-permute-start | bytes 2359304 | tf_op jit(solution)/shard_map/ppermute | solution.py:64
  227.1 24.3 %collective-permute-start.35 = (bf16[256,2048]{1,0:T(8,128)(2,1)S(1)}, bf16[256,2048]{1,0:T(8,128)(2,1)S(1)}, u32[]{:S(2)}, u32[]{:S(2)}) collective-permute-start(bf16[256,2048]{1,0:T(8,128)(2,1)S(1)} %multiply_convert_fusion.3), channel_id=1, source_target_pairs={{0,2},{1,3},{2,0},{3,1},{4,6},{5,7},{6,4},{7,5},{8,10},{9,11},{10,... | collective-permute-start | bytes 3145736 | tf_op jit(solution)/shard_map/ppermute | solution.py:42
  229.4 24.3 %collective-permute-start.37 = (bf16[256,2048]{1,0:T(8,128)(2,1)S(1)}, bf16[256,2048]{1,0:T(8,128)(2,1)S(1)}, u32[]{:S(2)}, u32[]{:S(2)}) collective-permute-start(bf16[256,2048]{1,0:T(8,128)(2,1)S(1)} %multiply_convert_fusion.3), channel_id=1, source_target_pairs={{0,4},{4,0},{8,12},{12,8},{16,20},{20,16},{24,28},{28,24},{1,5},{5... | collective-permute-start | bytes 3145736 | tf_op jit(solution)/shard_map/ppermute | solution.py:42
  251.6 18.9 %collective-permute-start.39 = (bf16[512,2048]{1,0:T(8,128)(2,1)S(1)}, bf16[512,2048]{1,0:T(8,128)(2,1)S(1)}, u32[]{:S(2)}, u32[]{:S(2)}) collective-permute-start(bf16[512,2048]{1,0:T(8,128)(2,1)S(1)} %pad_maximum_fusion.8), channel_id=1, source_target_pairs={{0,1},{1,0},{2,3},{3,2},{4,5},{5,4},{6,7},{7,6},{8,9},{9,8},{10,11... | collective-permute-start | bytes 6291464 | tf_op jit(solution)/shard_map/ppermute | solution.py:42
  253.7 13.9 %collective-permute-start.38 = (bf16[128,2048]{1,0:T(8,128)(2,1)S(1)}, bf16[128,2048]{1,0:T(8,128)(2,1)S(1)}, u32[]{:S(2)}, u32[]{:S(2)}) collective-permute-start(bf16[128,2048]{1,0:T(8,128)(2,1)S(1)} %slice.821), channel_id=1, source_target_pairs={{0,2},{1,3},{2,0},{3,1},{4,6},{5,7},{6,4},{7,5},{8,10},{9,11},{10,... | collective-permute-start | bytes 1572872 | tf_op jit(solution)/shard_map/ppermute | solution.py:42
  255.3 13.6 %collective-permute-start.36 = (bf16[128,2048]{1,0:T(8,128)(2,1)S(1)}, bf16[128,2048]{1,0:T(8,128)(2,1)S(1)}, u32[]{:S(2)}, u32[]{:S(2)}) collective-permute-start(bf16[128,2048]{1,0:T(8,128)(2,1)S(1)} %slice.820), channel_id=1, source_target_pairs={{0,4},{4,0},{8,12},{12,8},{16,20},{20,16},{24,28},{28,24},{1,5},{5... | collective-permute-start | bytes 1572872 | tf_op jit(solution)/shard_map/ppermute | solution.py:42
  321.6 14.0 %collective-permute-start.44 = (bf16[128,2048]{1,0:T(8,128)(2,1)S(1)}, bf16[128,2048]{1,0:T(8,128)(2,1)S(1)}, u32[]{:S(2)}, u32[]{:S(2)}) collective-permute-start(bf16[128,2048]{1,0:T(8,128)(2,1)S(1)} %get-tuple-element.248), channel_id=1, source_target_pairs={{0,2},{1,3},{2,0},{3,1},{4,6},{5,7},{6,4},{7,5},{8,10},{9,11},{10,... | collective-permute-start | bytes 1572872 | tf_op jit(solution)/shard_map/ppermute | solution.py:42
  324.5 13.7 %collective-permute-start.43 = (bf16[128,2048]{1,0:T(8,128)(2,1)S(1)}, bf16[128,2048]{1,0:T(8,128)(2,1)S(1)}, u32[]{:S(2)}, u32[]{:S(2)}) collective-permute-start(bf16[128,2048]{1,0:T(8,128)(2,1)S(1)} %get-tuple-element.249), channel_id=1, source_target_pairs={{0,4},{4,0},{8,12},{12,8},{16,20},{20,16},{24,28},{28,24},{1,5},{5... | collective-permute-start | bytes 1572872 | tf_op jit(solution)/shard_map/ppermute | solution.py:42
  339.5 38.0 %collective-permute-start.45 = (bf16[256,2048]{1,0:T(8,128)(2,1)}, bf16[256,2048]{1,0:T(8,128)(2,1)}, u32[]{:S(2)}, u32[]{:S(2)}) collective-permute-start(bf16[256,2048]{1,0:T(8,128)(2,1)} %pad_maximum_fusion.21), channel_id=1, source_target_pairs={{0,2},{1,3},{2,0},{3,1},{4,6},{5,7},{6,4},{7,5},{8,10},{9,11},{10,... | collective-permute-start | bytes 3145736 | tf_op jit(solution)/shard_map/ppermute | solution.py:42
  340.9 36.6 %collective-permute-start.46 = (bf16[256,2048]{1,0:T(8,128)(2,1)}, bf16[256,2048]{1,0:T(8,128)(2,1)}, u32[]{:S(2)}, u32[]{:S(2)}) collective-permute-start(bf16[256,2048]{1,0:T(8,128)(2,1)} %pad_maximum_fusion.22), channel_id=1, source_target_pairs={{0,4},{4,0},{8,12},{12,8},{16,20},{20,16},{24,28},{28,24},{1,5},{5... | collective-permute-start | bytes 3145736 | tf_op jit(solution)/shard_map/ppermute | solution.py:42
  385.5 27.8 %collective-permute-start.49 = (bf16[256,2048]{1,0:T(8,128)(2,1)}, bf16[256,2048]{1,0:T(8,128)(2,1)}, u32[]{:S(2)}, u32[]{:S(2)}) collective-permute-start(bf16[256,2048]{1,0:T(8,128)(2,1)} %get-tuple-element.201), channel_id=1, source_target_pairs={{0,4},{4,0},{8,12},{12,8},{16,20},{20,16},{24,28},{28,24},{1,5},{5... | collective-permute-start | bytes 3145736 | tf_op jit(solution)/shard_map/ppermute | solution.py:42
  387.1 28.9 %collective-permute-start.47 = (bf16[256,2048]{1,0:T(8,128)(2,1)}, bf16[256,2048]{1,0:T(8,128)(2,1)}, u32[]{:S(2)}, u32[]{:S(2)}) collective-permute-start(bf16[256,2048]{1,0:T(8,128)(2,1)} %get-tuple-element.201), channel_id=1, source_target_pairs={{0,2},{1,3},{2,0},{3,1},{4,6},{5,7},{6,4},{7,5},{8,10},{9,11},{10,... | collective-permute-start | bytes 3145736 | tf_op jit(solution)/shard_map/ppermute | solution.py:42
  388.7 47.6 %collective-permute-start.65 = (bf16[288,2048]{1,0:T(8,128)(2,1)}, bf16[288,2048]{1,0:T(8,128)(2,1)}, u32[]{:S(2)}, u32[]{:S(2)}) collective-permute-start(bf16[288,2048]{1,0:T(8,128)(2,1)} %pad_maximum_fusion.15), channel_id=1, source_target_pairs={{0,16},{4,20},{16,24},{20,28},{24,8},{28,12},{8,0},{12,4},{1,17},{... | collective-permute-start | bytes 3538952 | tf_op jit(solution)/shard_map/ppermute | solution.py:64
  389.2 47.1 %collective-permute-start.66 = (bf16[240,2048]{1,0:T(8,128)(2,1)}, bf16[240,2048]{1,0:T(8,128)(2,1)}, u32[]{:S(2)}, u32[]{:S(2)}) collective-permute-start(bf16[240,2048]{1,0:T(8,128)(2,1)} %pad_maximum_fusion.27), channel_id=1, source_target_pairs={{0,8},{4,12},{16,0},{20,4},{24,16},{28,20},{8,24},{12,28},{1,9},{5... | collective-permute-start | bytes 2949128 | tf_op jit(solution)/shard_map/ppermute | solution.py:64
  414.5 35.9 %collective-permute-start.50 = (bf16[128,2048]{1,0:T(8,128)(2,1)S(1)}, bf16[128,2048]{1,0:T(8,128)(2,1)S(1)}, u32[]{:S(2)}, u32[]{:S(2)}) collective-permute-start(bf16[128,2048]{1,0:T(8,128)(2,1)S(1)} %slice.842), channel_id=1, source_target_pairs={{0,2},{1,3},{2,0},{3,1},{4,6},{5,7},{6,4},{7,5},{8,10},{9,11},{10,... | collective-permute-start | bytes 1572872 | tf_op jit(solution)/shard_map/ppermute | solution.py:42
  417.0 33.3 %collective-permute-start.48 = (bf16[128,2048]{1,0:T(8,128)(2,1)S(1)}, bf16[128,2048]{1,0:T(8,128)(2,1)S(1)}, u32[]{:S(2)}, u32[]{:S(2)}) collective-permute-start(bf16[128,2048]{1,0:T(8,128)(2,1)S(1)} %slice.841), channel_id=1, source_target_pairs={{0,4},{4,0},{8,12},{12,8},{16,20},{20,16},{24,28},{28,24},{1,5},{5... | collective-permute-start | bytes 1572872 | tf_op jit(solution)/shard_map/ppermute | solution.py:42
  419.6 38.2 %collective-permute-start.57 = (bf16[512,2048]{1,0:T(8,128)(2,1)S(1)}, bf16[512,2048]{1,0:T(8,128)(2,1)S(1)}, u32[]{:S(2)}, u32[]{:S(2)}) collective-permute-start(bf16[512,2048]{1,0:T(8,128)(2,1)S(1)} %pad_maximum_fusion.10), channel_id=1, source_target_pairs={{0,1},{1,0},{2,3},{3,2},{4,5},{5,4},{6,7},{7,6},{8,9},{9,8},{10,11... | collective-permute-start | bytes 6291464 | tf_op jit(solution)/shard_map/ppermute | solution.py:42
  448.3 102.6 %collective-permute-start.67 = (bf16[528,2048]{1,0:T(8,128)(2,1)}, bf16[528,2048]{1,0:T(8,128)(2,1)}, u32[]{:S(2)}, u32[]{:S(2)}) collective-permute-start(bf16[528,2048]{1,0:T(8,128)(2,1)} %get-tuple-element.155), channel_id=1, source_target_pairs={{0,16},{4,20},{16,24},{20,28},{24,8},{28,12},{8,0},{12,4},{1,17},{... | collective-permute-start | bytes 6488072 | tf_op jit(solution)/shard_map/ppermute | solution.py:64
  449.0 102.0 %collective-permute-start.68 = (bf16[528,2048]{1,0:T(8,128)(2,1)}, bf16[528,2048]{1,0:T(8,128)(2,1)}, u32[]{:S(2)}, u32[]{:S(2)}) collective-permute-start(bf16[528,2048]{1,0:T(8,128)(2,1)} %get-tuple-element.156), channel_id=1, source_target_pairs={{0,8},{4,12},{16,0},{20,4},{24,16},{28,20},{8,24},{12,28},{1,9},{5... | collective-permute-start | bytes 6488072 | tf_op jit(solution)/shard_map/ppermute | solution.py:64
  450.4 31.7 %collective-permute-start.52 = (bf16[512,2048]{1,0:T(8,128)(2,1)S(1)}, bf16[512,2048]{1,0:T(8,128)(2,1)S(1)}, u32[]{:S(2)}, u32[]{:S(2)}) collective-permute-start(bf16[512,2048]{1,0:T(8,128)(2,1)S(1)} %copy-done.74), channel_id=1, source_target_pairs={{0,1},{1,0},{2,3},{3,2},{4,5},{5,4},{6,7},{7,6},{8,9},{9,8},{10,11... | collective-permute-start | bytes 6291464 | tf_op jit(solution)/shard_map/ppermute | solution.py:42
  452.8 39.1 %collective-permute-start.51 = (bf16[512,2048]{1,0:T(8,128)(2,1)}, bf16[512,2048]{1,0:T(8,128)(2,1)}, u32[]{:S(2)}, u32[]{:S(2)}) collective-permute-start(bf16[512,2048]{1,0:T(8,128)(2,1)} %product.10), channel_id=1, source_target_pairs={{0,1},{1,0},{2,3},{3,2},{4,5},{5,4},{6,7},{7,6},{8,9},{9,8},{10,11... | collective-permute-start | bytes 6291464 | tf_op jit(solution)/shard_map/ppermute | solution.py:42
  457.9 26.0 %collective-permute-start.59 = (bf16[512,2048]{1,0:T(8,128)(2,1)}, bf16[512,2048]{1,0:T(8,128)(2,1)}, u32[]{:S(2)}, u32[]{:S(2)}) collective-permute-start(bf16[512,2048]{1,0:T(8,128)(2,1)} %pad_maximum_fusion.11), channel_id=1, source_target_pairs={{0,1},{1,0},{2,3},{3,2},{4,5},{5,4},{6,7},{7,6},{8,9},{9,8},{10,11... | collective-permute-start | bytes 6291464 | tf_op jit(solution)/shard_map/ppermute | solution.py:42
  482.1 30.0 %collective-permute-start.58 = (bf16[512,2048]{1,0:T(8,128)(2,1)S(1)}, bf16[512,2048]{1,0:T(8,128)(2,1)S(1)}, u32[]{:S(2)}, u32[]{:S(2)}) collective-permute-start(bf16[512,2048]{1,0:T(8,128)(2,1)S(1)} %convolution_convert_fusion.6), channel_id=1, source_target_pairs={{0,1},{1,0},{2,3},{3,2},{4,5},{5,4},{6,7},{7,6},{8,9},{9,8},{10,11... | collective-permute-start | bytes 6291464 | tf_op jit(solution)/shard_map/ppermute | solution.py:42
  483.8 16.4 %collective-permute-start.54 = (bf16[128,2048]{1,0:T(8,128)(2,1)S(1)}, bf16[128,2048]{1,0:T(8,128)(2,1)S(1)}, u32[]{:S(2)}, u32[]{:S(2)}) collective-permute-start(bf16[128,2048]{1,0:T(8,128)(2,1)S(1)} %get-tuple-element.245), channel_id=1, source_target_pairs={{0,2},{1,3},{2,0},{3,1},{4,6},{5,7},{6,4},{7,5},{8,10},{9,11},{10,... | collective-permute-start | bytes 1572872 | tf_op jit(solution)/shard_map/ppermute | solution.py:42
  491.9 14.1 %collective-permute-start.53 = (bf16[128,2048]{1,0:T(8,128)(2,1)S(1)}, bf16[128,2048]{1,0:T(8,128)(2,1)S(1)}, u32[]{:S(2)}, u32[]{:S(2)}) collective-permute-start(bf16[128,2048]{1,0:T(8,128)(2,1)S(1)} %get-tuple-element.246), channel_id=1, source_target_pairs={{0,4},{4,0},{8,12},{12,8},{16,20},{20,16},{24,28},{28,24},{1,5},{5... | collective-permute-start | bytes 1572872 | tf_op jit(solution)/shard_map/ppermute | solution.py:42
  507.1 29.8 %collective-permute-start.55 = (bf16[256,2048]{1,0:T(8,128)(2,1)}, bf16[256,2048]{1,0:T(8,128)(2,1)}, u32[]{:S(2)}, u32[]{:S(2)}) collective-permute-start(bf16[256,2048]{1,0:T(8,128)(2,1)} %pad_maximum_fusion.23), channel_id=1, source_target_pairs={{0,2},{1,3},{2,0},{3,1},{4,6},{5,7},{6,4},{7,5},{8,10},{9,11},{10,... | collective-permute-start | bytes 3145736 | tf_op jit(solution)/shard_map/ppermute | solution.py:42
  508.0 28.9 %collective-permute-start.56 = (bf16[256,2048]{1,0:T(8,128)(2,1)}, bf16[256,2048]{1,0:T(8,128)(2,1)}, u32[]{:S(2)}, u32[]{:S(2)}) collective-permute-start(bf16[256,2048]{1,0:T(8,128)(2,1)} %pad_maximum_fusion.24), channel_id=1, source_target_pairs={{0,4},{4,0},{8,12},{12,8},{16,20},{20,16},{24,28},{28,24},{1,5},{5... | collective-permute-start | bytes 3145736 | tf_op jit(solution)/shard_map/ppermute | solution.py:42
  542.4 31.6 %collective-permute-start.60 = (bf16[512,2048]{1,0:T(8,128)(2,1)}, bf16[512,2048]{1,0:T(8,128)(2,1)}, u32[]{:S(2)}, u32[]{:S(2)}) collective-permute-start(bf16[512,2048]{1,0:T(8,128)(2,1)} %convolution_convert_fusion.5), channel_id=1, source_target_pairs={{0,1},{1,0},{2,3},{3,2},{4,5},{5,4},{6,7},{7,6},{8,9},{9,8},{10,11... | collective-permute-start | bytes 6291464 | tf_op jit(solution)/shard_map/ppermute | solution.py:42
  563.8 50.9 %collective-permute-start.69 = (bf16[128,2048]{1,0:T(8,128)(2,1)}, bf16[128,2048]{1,0:T(8,128)(2,1)}, u32[]{:S(2)}, u32[]{:S(2)}) collective-permute-start(bf16[128,2048]{1,0:T(8,128)(2,1)} %pad_maximum_fusion.35), channel_id=1, source_target_pairs={{0,16},{4,20},{16,24},{20,28},{24,8},{28,12},{8,0},{12,4},{1,17},{... | collective-permute-start | bytes 1572872 | tf_op jit(solution)/shard_map/ppermute | solution.py:64
  565.3 49.4 %collective-permute-start.70 = (bf16[128,2048]{1,0:T(8,128)(2,1)}, bf16[128,2048]{1,0:T(8,128)(2,1)}, u32[]{:S(2)}, u32[]{:S(2)}) collective-permute-start(bf16[128,2048]{1,0:T(8,128)(2,1)} %pad_maximum_fusion.36), channel_id=1, source_target_pairs={{0,8},{4,12},{16,0},{20,4},{24,16},{28,20},{8,24},{12,28},{1,9},{5... | collective-permute-start | bytes 1572872 | tf_op jit(solution)/shard_map/ppermute | solution.py:64
  590.7 14.6 %collective-permute-start.61 = (bf16[128,2048]{1,0:T(8,128)(2,1)S(1)}, bf16[128,2048]{1,0:T(8,128)(2,1)}, u32[]{:S(2)}, u32[]{:S(2)}) collective-permute-start(bf16[128,2048]{1,0:T(8,128)(2,1)S(1)} %get-tuple-element.243), channel_id=1, source_target_pairs={{0,4},{4,0},{8,12},{12,8},{16,20},{20,16},{24,28},{28,24},{1,5},{5... | collective-permute-start | bytes 1572872 | tf_op jit(solution)/shard_map/ppermute | solution.py:42
  612.2 51.4 %collective-permute-start.63 = (bf16[256,2048]{1,0:T(8,128)(2,1)}, bf16[256,2048]{1,0:T(8,128)(2,1)S(1)}, u32[]{:S(2)}, u32[]{:S(2)}) collective-permute-start(bf16[256,2048]{1,0:T(8,128)(2,1)} %pad_maximum_fusion.25), channel_id=1, source_target_pairs={{0,2},{1,3},{2,0},{3,1},{4,6},{5,7},{6,4},{7,5},{8,10},{9,11},{10,... | collective-permute-start | bytes 3145736 | tf_op jit(solution)/shard_map/ppermute | solution.py:42
  613.2 50.4 %collective-permute-start.64 = (bf16[256,2048]{1,0:T(8,128)(2,1)}, bf16[256,2048]{1,0:T(8,128)(2,1)S(1)}, u32[]{:S(2)}, u32[]{:S(2)}) collective-permute-start(bf16[256,2048]{1,0:T(8,128)(2,1)} %pad_maximum_fusion.26), channel_id=1, source_target_pairs={{0,4},{4,0},{8,12},{12,8},{16,20},{20,16},{24,28},{28,24},{1,5},{5... | collective-permute-start | bytes 3145736 | tf_op jit(solution)/shard_map/ppermute | solution.py:42
  617.2 20.3 %collective-permute-start.71 = (bf16[192,2048]{1,0:T(8,128)(2,1)S(1)}, bf16[192,2048]{1,0:T(8,128)(2,1)S(1)}, u32[]{:S(2)}, u32[]{:S(2)}) collective-permute-start(bf16[192,2048]{1,0:T(8,128)(2,1)S(1)} %pad_maximum_fusion.30), channel_id=1, source_target_pairs={{0,16},{4,20},{16,24},{20,28},{24,8},{28,12},{8,0},{12,4},{1,17},{... | collective-permute-start | bytes 2359304 | tf_op jit(solution)/shard_map/ppermute | solution.py:64
  619.6 33.9 %collective-permute-start.72 = (bf16[192,2048]{1,0:T(8,128)(2,1)S(1)}, bf16[192,2048]{1,0:T(8,128)(2,1)S(1)}, u32[]{:S(2)}, u32[]{:S(2)}) collective-permute-start(bf16[192,2048]{1,0:T(8,128)(2,1)S(1)} %pad_maximum_fusion.31), channel_id=1, source_target_pairs={{0,8},{4,12},{16,0},{20,4},{24,16},{28,20},{8,24},{12,28},{1,9},{5... | collective-permute-start | bytes 2359304 | tf_op jit(solution)/shard_map/ppermute | solution.py:64
  (127 other events, 1315.4 us)

commit v9 on v8

--- a/solution.py
+++ b/solution.py
@@ -796,13 +796,13 @@
     odds = [second_share(n) for n in (1, 3)]
     cores = [swap(odd, "narrow", 1) for odd in odds]
     evens = [second_share(0), second_share(2)]
-    d_second, stages = scatter_rows(evens[0], cores[0], evens[1], cores[1])
+    [ready] = after([hidden], cores + evens)
+    grad_down = product(ready, rows_upstream, "nn", bf16)
+    d_second, stages = scatter_rows(evens[0], cores[0], evens[1], cores[1], (), [grad_down])
     upstream = upstream_low.astype(f32)
     d_middle = upstream + norm_back(middle, rate_last, gain_last, d_second)
     (middle_own, middle_other), middle_stages = gather_rows(d_middle.astype(bf16))
     rows_dmiddle = [jnp.concatenate(middle_own, axis=0), jnp.concatenate(middle_other, axis=0)]
-    [hidden] = after([hidden], cores + evens)
-    grad_down = product(hidden, rows_upstream, "nn", bf16)
     grads = [Scatter(jnp.split(grad_down, outer, axis=0))]
     [d_gate] = after([d_gate], stages[0])
     grad_gate = product(d_gate, rows_second, "nn", bf16)
@@ -857,8 +857,10 @@
     chunks = grad_in.reshape(3, outer, own, width)
     in_sum = Scatter([chunks[:, j].reshape(3 * own, width) for j in range(outer)])
     out_sum = Scatter(jnp.split(grad_out, outer, axis=0))
-    d_filter, *_ = after([d_filter], last + [grad_in])
+    last = ring_step([in_sum, out_sum], last)
+    d_filter, *_ = after([d_filter], last + stages[0])
     gain_grads = jnp.stack([grad_gain_one / gain_first, grad_gain_two])
+    [gain_grads] = after([gain_grads], stages[0])
     sum_re, sum_im, mom_re, mom_im = filter_moments(d_filter, step_re, step_im)
     full_re = lag * sum_re + 8.0 * mom_re
     full_im = lag * sum_im + 8.0 * mom_im
@@ -876,18 +878,15 @@
         ],
         axis=0,
     ).astype(bf16)
-    last = ring_step([in_sum, out_sum], last, stages[0] + [gain_grads, small_grad])
     gain_sums = place_gain(gain_grads).transpose(1, 0, 2).reshape(2, channels)
     gain_high = gain_sums.astype(bf16)
     gain_low = (gain_sums - gain_high.astype(f32)).astype(bf16)
     small_grad = jnp.concatenate([small_grad, gain_high, gain_low], axis=0)
-    for at in range(1, steps):
-        last = ring_step([in_sum], last)
-    [small_grad] = after([small_grad], last)
+    [small_grad] = after([small_grad], stages[1])
     small_share = scatter_small(jnp.split(small_grad, outer, axis=1))
     gain_share = small_share[-4:-2] + small_share[-2:]
     for at in range(1, steps):
-        last = ring_step([out_sum], last)
+        last = ring_step([in_sum, out_sum], last, [small_share])
 
     at = 9 + poles
     return (

time: 686 us -> 697 us (1.016)
  waiting for transfers between devices: 189 us -> 201 us
    ppermute x55, waiting for transfers between devices: 91 us -> 108 us  [swap(): return lax.ppermute(values, axis, [(i, i ^ shift) for i in range(size)])]
    ppermute x26 -> x24, waiting for transfers between devices: 98.2 us -> 93.6 us  [along(): return lax.ppermute(values, 'wide', pairs)]
    ppermute x26 -> x24, starting transfers between devices: 35.5 us -> 32.7 us  [along(): return lax.ppermute(values, 'wide', pairs)]
    concatenate x13 -> x15, other arithmetic: 14.9 us -> 15.5 us  [ring_step(): jnp.concatenate(one, axis=0)]
    unnamed x236 -> x228, local copies, waits for them, and re-layouts: 30.1 us -> 30.4 us
  transfers between devices with their start and end apart: 81 -> 79, of which waited for: 25 -> 22; matrix products, arithmetic and copies ran while one was open for 35% -> 35% of each run, Pallas kernels for 16% -> 16%
where the time goes in v9:
time: 697 us; the launch traced here: 689 us
  waiting for transfers between devices  201 us (29%)
  other arithmetic  121 us (17%)
  Pallas kernels  112 us (16%)
  matrix products  105 us (15%)
  starting transfers between devices  75.4 us (11%)
  local copies, waits for them, and re-layouts  71.5 us (10%)
    ppermute x55, waiting for transfers between devices, swap(): return lax.ppermute(values, axis, [(i, i ^ shift) for i in range(size)])  108 us
    ppermute x24, waiting for transfers between devices, along(): return lax.ppermute(values, 'wide', pairs)  93.6 us
    pallas_call x7, Pallas kernels, product(): pl.pallas_call(partial(product_kernel, kind=kind), grid=(columns // side,...  53.2 us
    dot_general x7, matrix products, nt(): lax.dot_general(a, b, (((1,), (1,)), ((), ())), preferred_element_type=f32)  45.8 us
    ppermute x55, starting transfers between devices, swap(): return lax.ppermute(values, axis, [(i, i ^ shift) for i in range(size)])  42.6 us
    dot_general x12, matrix products, tn(): lax.dot_general(a, b, (((0,), (0,)), ((), ())), preferred_element_type=f32)  36.7 us
    ppermute x24, starting transfers between devices, along(): return lax.ppermute(values, 'wide', pairs)  32.7 us
    pallas_call x2, Pallas kernels, mixer_backward(): pl.pallas_call(backward_kernel, out_shape=(jax.ShapeDtypeStruct((pieces,...  31.9 us
  transfers between devices with their start and end apart: 79, of which 22 were waited for; matrix products, arithmetic and copies ran while one was open for 35% of the time, Pallas kernels for 16%

profile of v9, /device:TPU:0, one launch (start us, length us, event | category | flops | bytes accessed | tf_op | source)
XLA Modules:
  0.0 688.8 jit_solution(7928748302243054218)
XLA Ops:
  1.5 3.1 concatenate.233
  4.6 5.1 collective-permute-start.2
  9.7 2.9 collective-permute-start
  24.6 2.6 constant_dynamic-update-slice_fusion.1
  27.2 2.5 pad_maximum_fusion.14
  36.7 4.1 taps.1
  40.7 3.5 fusion.91.spectrum
  46.2 8.8 %collective-permute-done.5 = bf16[2,4,64]{2,1,0:T(4,128)(2,1)S(1)} collective-permute-done((bf16[2,4,64]{2,1,0:T(4,128)(2,1)S(1)}, bf16[2,4,64]{2,1,0:T(4,128)(2,1)S(1)}, u32[]{:S(2)}, u32[]{:S(2)}) %collective-permute-start.5) | collective-permute-done | bytes 1056 | tf_op jit(solution)/shard_map/ppermute | solution.py:42
  75.9 7.0 %collective-permute-done.10 = bf16[128,2048]{1,0:T(8,128)(2,1)S(1)} collective-permute-done((bf16[128,2048]{1,0:T(8,128)(2,1)S(1)}, bf16[128,2048]{1,0:T(8,128)(2,1)S(1)}, u32[]{:S(2)}, u32[]{:S(2)}) %collective-permute-start.10) | collective-permute-done | bytes 524320 | tf_op jit(solution)/shard_map/ppermute | solution.py:42
  82.9 2.4 collective-permute-done.9
  95.1 2.8 fusion
  102.1 13.1 %fusion.5 = (bf16[1024,2048]{1,0:T(8,128)(2,1)S(1)}, bf16[1024,2048]{1,0:T(8,128)(2,1)S(1)}) fusion(f32[1024]{0:T(1024)S(1)} %add_rsqrt_fusion, f32[2048]{0:T(1024)S(1)} %mul.420, bf16[512,2048]{1,0:T(8,128)(2,1)S(1)} %collective-permute-done.11, bf16[128,2048]{1,0:T(8,128)(2,1)S(1)} %collective-permute-done.10, ...), kind=kLoop, calls=%fused_computation.9 | loop fusion | flops 41943040 | bytes 16793600 | tf_op jit(solution)/shard_map/convert_element_type | solution.py:707
  115.2 3.5 fusion.90.proj
  118.8 7.1 %mixer_forward.2 = (bf16[4,256,256]{2,1,0:T(8,128)(2,1)S(1)}, f32[1024,256]{1,0:T(8,128)S(1)}, bf16[3,1024,256]{2,1,0:T(8,128)(2,1)S(1)}) custom-call(s32[4]{0:T(128)S(1)} %select_reduce_fusion.7.order, s32[3]{0:T(128)S(1)} %get-tuple-element.207.first, s32[3]{0:T(128)S(1)} %get-tuple-element.315.count, f32[4,256,768]{2,1,0:T(8,128)S(1)} %fusion.90.proj, ...), custom_call_target="tpu_custom_call" | custom-call | flops 1024 | bytes 1024 | tf_op jit(solution)/shard_map/mixer_forward/pallas_call | solution.py:554
  128.2 3.5 fusion.92.proj
  131.7 7.5 %mixer_forward.3 = (bf16[4,256,256]{2,1,0:T(8,128)(2,1)S(1)}, f32[1024,256]{1,0:T(8,128)S(1)}, bf16[3,1024,256]{2,1,0:T(8,128)(2,1)S(1)}) custom-call(s32[4]{0:T(128)S(1)} %select_reduce_fusion.7.order, s32[3]{0:T(128)S(1)} %get-tuple-element.203.first, s32[3]{0:T(128)S(1)} %get-tuple-element.313.count, f32[4,256,768]{2,1,0:T(8,128)S(1)} %fusion.92.proj, ...), custom_call_target="tpu_custom_call" | custom-call | flops 1024 | bytes 1024 | tf_op jit(solution)/shard_map/mixer_forward/pallas_call | solution.py:554
  145.5 12.0 %collective-permute-done.24 = bf16[352,2048]{1,0:T(8,128)(2,1)} collective-permute-done((bf16[352,2048]{1,0:T(8,128)(2,1)}, bf16[352,2048]{1,0:T(8,128)(2,1)}, u32[]{:S(2)}, u32[]{:S(2)}) %collective-permute-start.24) | collective-permute-done | bytes 1441824 | tf_op jit(solution)/shard_map/ppermute | solution.py:64
  167.8 2.5 collective-permute-start.29
  176.8 40.6 %collective-permute-done.29 = bf16[272,2048]{1,0:T(8,128)(2,1)} collective-permute-done((bf16[272,2048]{1,0:T(8,128)(2,1)}, bf16[272,2048]{1,0:T(8,128)(2,1)}, u32[]{:S(2)}, u32[]{:S(2)}) %collective-permute-start.29) | collective-permute-done | bytes 1114144 | tf_op jit(solution)/shard_map/ppermute | solution.py:64
  219.5 12.9 %collective-permute-done.25 = bf16[128,2048]{1,0:T(8,128)(2,1)S(1)} collective-permute-done((bf16[128,2048]{1,0:T(8,128)(2,1)S(1)}, bf16[128,2048]{1,0:T(8,128)(2,1)S(1)}, u32[]{:S(2)}, u32[]{:S(2)}) %collective-permute-start.25) | collective-permute-done | bytes 524320 | tf_op jit(solution)/shard_map/ppermute | solution.py:42
  240.2 16.6 %collective-permute-done.27 = bf16[256,2048]{1,0:T(8,128)(2,1)S(1)} collective-permute-done((bf16[256,2048]{1,0:T(8,128)(2,1)S(1)}, bf16[256,2048]{1,0:T(8,128)(2,1)S(1)}, u32[]{:S(2)}, u32[]{:S(2)}) %collective-permute-start.27) | collective-permute-done | bytes 1048608 | tf_op jit(solution)/shard_map/ppermute | solution.py:42
  264.1 17.6 %collective-permute-done.37 = bf16[256,2048]{1,0:T(8,128)(2,1)S(1)} collective-permute-done((bf16[256,2048]{1,0:T(8,128)(2,1)S(1)}, bf16[256,2048]{1,0:T(8,128)(2,1)S(1)}, u32[]{:S(2)}, u32[]{:S(2)}) %collective-permute-start.37) | collective-permute-done | bytes 1048608 | tf_op jit(solution)/shard_map/ppermute | solution.py:42
  285.8 8.3 %fusion.94 = f32[704,2048]{1,0:T(8,128)} fusion(bf16[704,2048]{1,0:T(8,128)(2,1)S(1)} %get-tuple-element.266.b, bf16[2048,2048]{1,0:T(8,128)(2,1)S(1)} %constant_dynamic-update-slice_fusion.11.b), kind=kOutput, calls=%fused_computation.350 | convolution fusion | flops 5905580032 | bytes 17039360 | tf_op jit(solution)/shard_map/dot_general | solution.py:33
  300.5 8.0 %fusion.93 = f32[704,2048]{1,0:T(8,128)} fusion(bf16[704,2048]{1,0:T(8,128)(2,1)S(1)} %get-tuple-element.275, bf16[2048,2048]{1,0:T(8,128)(2,1)S(1)} %constant_dynamic-update-slice_fusion.2.b), kind=kOutput, calls=%fused_computation.349 | convolution fusion | flops 5905580032 | bytes 17039360 | tf_op jit(solution)/shard_map/dot_general | solution.py:33
  308.5 15.5 %multiply_convert_fusion = (bf16[704,2048]{1,0:T(8,128)(2,1)S(1)}, bf16[704,2048]{1,0:T(8,128)(2,1)S(1)}, bf16[704,2048]{1,0:T(8,128)(2,1)}) fusion(f32[704,2048]{1,0:T(8,128)} %fusion.94, f32[704,2048]{1,0:T(8,128)} %fusion.93, bf16[704,2048]{1,0:T(8,128)(2,1)S(1)} %get-tuple-element.274, bf16[2048,2048]{1,0:T(8,128)(2,1)} %copy-done.26), kind=kOutput, calls=%fused_computation.11 | convolution fusion | flops 5927206912 | bytes 31457280 | tf_op jit(solution)/shard_map/dot_general | solution.py:33
  336.3 3.1 fusion.45
  339.5 4.4 convert_add_fusion.5
  345.8 4.5 convert_add_fusion.4
  350.3 10.3 %product.13 = bf16[704,2048]{1,0:T(8,128)(2,1)} custom-call(bf16[704,2048]{1,0:T(8,128)(2,1)} %get-tuple-element.128.a, bf16[2048,2048]{1,0:T(8,128)(2,1)} %copy-done.51), custom_call_target="tpu_custom_call" | custom-call | flops 1024 | bytes 1024 | tf_op jit(solution)/shard_map/product/pallas_call | solution.py:363
  365.2 10.7 %collective-permute-done.42 = bf16[128,2048]{1,0:T(8,128)(2,1)S(1)} collective-permute-done((bf16[128,2048]{1,0:T(8,128)(2,1)}, bf16[128,2048]{1,0:T(8,128)(2,1)S(1)}, u32[]{:S(2)}, u32[]{:S(2)}) %collective-permute-start.42) | collective-permute-done | bytes 524320 | tf_op jit(solution)/shard_map/ppermute | solution.py:42
  381.2 10.3 %product.7 = bf16[704,2048]{1,0:T(8,128)(2,1)} custom-call(bf16[704,2048]{1,0:T(8,128)(2,1)} %copy-done.50, bf16[2048,2048]{1,0:T(8,128)(2,1)} %copy-done.26), custom_call_target="tpu_custom_call" | custom-call | flops 1024 | bytes 1024 | tf_op jit(solution)/shard_map/product/pallas_call | solution.py:363
  391.5 10.3 %product.8 = bf16[704,2048]{1,0:T(8,128)(2,1)} custom-call(bf16[704,2048]{1,0:T(8,128)(2,1)} %copy-done.63, bf16[2048,2048]{1,0:T(8,128)(2,1)} %copy-done.26), custom_call_target="tpu_custom_call" | custom-call | flops 1024 | bytes 1024 | tf_op jit(solution)/shard_map/product/pallas_call | solution.py:363
  405.0 3.3 multiply_reduce_fusion.4
  408.8 4.3 fusion.75
  418.5 5.6 product.12
  424.1 5.6 product.11
  429.7 5.6 product.10
  435.3 5.6 product.9
  447.1 17.2 %collective-permute-done.66 = bf16[240,2048]{1,0:T(8,128)(2,1)} collective-permute-done((bf16[240,2048]{1,0:T(8,128)(2,1)}, bf16[240,2048]{1,0:T(8,128)(2,1)}, u32[]{:S(2)}, u32[]{:S(2)}) %collective-permute-start.66) | collective-permute-done | bytes 983072 | tf_op jit(solution)/shard_map/ppermute | solution.py:64
  483.0 2.9 pad_maximum_fusion.11
  486.0 3.6 fusion.21
  489.7 15.9 %mixer_backward.2 = (bf16[4,256,768]{2,1,0:T(8,128)(2,1)}, f32[512,256]{1,0:T(8,128)S(1)}, f32[8,768]{1,0:T(8,128)S(1)}) custom-call(s32[4]{0:T(128)S(1)} %select_reduce_fusion.7.order, s32[3]{0:T(128)S(1)} %copy-done.17, s32[3]{0:T(128)S(1)} %copy-done.19, f32[4,256,768]{2,1,0:T(8,128)} %copy-done.4, f32[4,256,256]{2,1,0:T(8,128)S(1)} %bitcast.197, ...), custom_call_target="tpu_custom_call" | custom-call | flops 1024 | bytes 1024 | tf_op jit(solution)/shard_map/mixer_backward/pallas_call | solution.py:580
  513.3 3.2 constant_dynamic-update-slice_fusion.16
  516.5 3.6 fusion.96
  520.5 2.4 convert_add_fusion.3
  523.0 4.3 fusion.7
  529.5 4.8 collective-permute-done.53
  536.5 3.5 fusion.95
  540.0 4.5 convert_add_fusion.1
  544.5 16.0 %mixer_backward.3 = (bf16[4,256,768]{2,1,0:T(8,128)(2,1)}, f32[512,256]{1,0:T(8,128)S(1)}, f32[8,768]{1,0:T(8,128)S(1)}) custom-call(s32[4]{0:T(128)S(1)} %select_reduce_fusion.7.order, s32[3]{0:T(128)S(1)} %get-tuple-element.203.first, s32[3]{0:T(128)S(1)} %get-tuple-element.313.count, f32[4,256,768]{2,1,0:T(8,128)} %copy-done.3, ...), custom_call_target="tpu_custom_call" | custom-call | flops 1024 | bytes 1024 | tf_op jit(solution)/shard_map/mixer_backward/pallas_call | solution.py:580
  564.6 4.1 convolution_convert_fusion.5
  568.8 3.5 fusion.97
  572.3 3.7 add_convert_fusion
  578.7 4.7 add_bitcast_fusion
  585.6 3.1 fusion.23
  588.9 9.1 %collective-permute-done.69 = bf16[128,2048]{1,0:T(8,128)(2,1)S(1)} collective-permute-done((bf16[128,2048]{1,0:T(8,128)(2,1)S(1)}, bf16[128,2048]{1,0:T(8,128)(2,1)S(1)}, u32[]{:S(2)}, u32[]{:S(2)}) %collective-permute-start.69) | collective-permute-done | bytes 524320 | tf_op jit(solution)/shard_map/ppermute | solution.py:64
  598.0 13.0 %collective-permute-done.70 = bf16[128,2048]{1,0:T(8,128)(2,1)S(1)} collective-permute-done((bf16[128,2048]{1,0:T(8,128)(2,1)S(1)}, bf16[128,2048]{1,0:T(8,128)(2,1)S(1)}, u32[]{:S(2)}, u32[]{:S(2)}) %collective-permute-start.70) | collective-permute-done | bytes 524320 | tf_op jit(solution)/shard_map/ppermute | solution.py:64
  616.7 4.0 convert_add_fusion
  626.8 7.3 %collective-permute-done.62 = bf16[128,2048]{1,0:T(8,128)(2,1)S(1)} collective-permute-done((bf16[128,2048]{1,0:T(8,128)(2,1)S(1)}, bf16[128,2048]{1,0:T(8,128)(2,1)S(1)}, u32[]{:S(2)}, u32[]{:S(2)}) %collective-permute-start.62) | collective-permute-done | bytes 524320 | tf_op jit(solution)/shard_map/ppermute | solution.py:42
  643.4 7.9 %moments.1 = (f32[16,8,256]{2,1,0:T(8,128)}, f32[16,8,256]{2,1,0:T(8,128)}, f32[16,8,256]{2,1,0:T(8,128)}, f32[16,8,256]{2,1,0:T(8,128)}) custom-call(f32[512,256]{1,0:T(8,128)} %add.367.grad, f32[16,8,256]{2,1,0:T(8,128)} %broadcast_in_dim.201.step_re, f32[16,8,256]{2,1,0:T(8,128)} %broadcast_in_dim.202.step_im), custom_call_target="tpu_custom_call" | custom-call | flops 1024 | bytes 1024 | tf_op jit(solution)/shard_map/moments/pallas_call | solution.py:378
  654.0 12.1 %collective-permute-done.74 = f32[2,4,2,64]{3,1,2,0:T(4,128)S(1)} collective-permute-done((f32[2,4,2,64]{3,1,2,0:T(4,128)S(1)}, f32[2,4,2,64]{3,1,2,0:T(4,128)S(1)}, u32[]{:S(2)}, u32[]{:S(2)}) %collective-permute-start.74) | collective-permute-done | bytes 4128 | tf_op jit(solution)/shard_map/ppermute | solution.py:42
  670.4 2.9 fusion.8
  677.3 3.7 fusion.24
  685.4 3.0 fusion.22
  (571 shorter events, 224.4 us)
Async XLA Ops:
  4.6 25.1 %collective-permute-start.2 = (bf16[75,64]{1,0:T(8,128)(2,1)S(1)}, bf16[75,64]{1,0:T(8,128)(2,1)S(1)}, u32[]{:S(2)}, u32[]{:S(2)}) collective-permute-start(bf16[75,64]{1,0:T(8,128)(2,1)S(1)} %concatenate.233), channel_id=1, source_target_pairs={{0,24},{4,28},{16,8},{20,12},{24,0},{28,4},{8,16},{12,20},{1,25},{... | collective-permute-start | bytes 28808 | tf_op jit(solution)/shard_map/ppermute | solution.py:64
  9.7 20.0 %collective-permute-start.1 = (bf16[75,64]{1,0:T(8,128)(2,1)S(1)}, bf16[75,64]{1,0:T(8,128)(2,1)S(1)}, u32[]{:S(2)}, u32[]{:S(2)}) collective-permute-start(bf16[75,64]{1,0:T(8,128)(2,1)S(1)} %concatenate.233), channel_id=1, source_target_pairs={{0,8},{4,12},{16,0},{20,4},{24,16},{28,20},{8,24},{12,28},{1,9},{5... | collective-permute-start | bytes 28808 | tf_op jit(solution)/shard_map/ppermute | solution.py:64
  9.7 20.0 %collective-permute-start = (bf16[75,64]{1,0:T(8,128)(2,1)S(1)}, bf16[75,64]{1,0:T(8,128)(2,1)S(1)}, u32[]{:S(2)}, u32[]{:S(2)}) collective-permute-start(bf16[75,64]{1,0:T(8,128)(2,1)S(1)} %concatenate.233), channel_id=1, source_target_pairs={{0,16},{4,20},{16,24},{20,28},{24,8},{28,12},{8,0},{12,4},{1,17},{... | collective-permute-start | bytes 28808 | tf_op jit(solution)/shard_map/ppermute | solution.py:64
  14.9 46.9 %collective-permute-start.12 = (bf16[256,2048]{1,0:T(8,128)(2,1)}, bf16[256,2048]{1,0:T(8,128)(2,1)}, u32[]{:S(2)}, u32[]{:S(2)}) collective-permute-start(bf16[256,2048]{1,0:T(8,128)(2,1)} %pad_maximum_fusion.17), channel_id=1, source_target_pairs={{0,16},{4,20},{16,24},{20,28},{24,8},{28,12},{8,0},{12,4},{1,17},{... | collective-permute-start | bytes 3145736 | tf_op jit(solution)/shard_map/ppermute | solution.py:64
  14.9 48.9 %collective-permute-start.13 = (bf16[256,2048]{1,0:T(8,128)(2,1)}, bf16[256,2048]{1,0:T(8,128)(2,1)}, u32[]{:S(2)}, u32[]{:S(2)}) collective-permute-start(bf16[256,2048]{1,0:T(8,128)(2,1)} %pad_maximum_fusion.17), channel_id=1, source_target_pairs={{0,8},{4,12},{16,0},{20,4},{24,16},{28,20},{8,24},{12,28},{1,9},{5... | collective-permute-start | bytes 3145736 | tf_op jit(solution)/shard_map/ppermute | solution.py:64
  29.7 14.5 %collective-permute-start.16 = (s32[2,3]{1,0:T(2,128)S(1)}, s32[2,3]{1,0:T(2,128)S(1)}, u32[]{:S(2)}, u32[]{:S(2)}) collective-permute-start(s32[2,3]{1,0:T(2,128)S(1)} %pad_add_fusion), channel_id=1, source_target_pairs={{0,4},{4,0},{8,12},{12,8},{16,20},{20,16},{24,28},{28,24},{1,5},{5... | collective-permute-start | bytes 80 | tf_op jit(solution)/shard_map/ppermute | solution.py:42
  31.6 36.4 %collective-permute-start.8 = (bf16[256,2048]{1,0:T(8,128)(2,1)S(1)}, bf16[256,2048]{1,0:T(8,128)(2,1)}, u32[]{:S(2)}, u32[]{:S(2)}) collective-permute-start(bf16[256,2048]{1,0:T(8,128)(2,1)S(1)} %bitcast.204), channel_id=1, source_target_pairs={{0,4},{4,0},{8,12},{12,8},{16,20},{20,16},{24,28},{28,24},{1,5},{5... | collective-permute-start | bytes 3145736 | tf_op jit(solution)/shard_map/ppermute | solution.py:42
  32.1 38.5 %collective-permute-start.3 = (bf16[256,2048]{1,0:T(8,128)(2,1)S(1)}, bf16[256,2048]{1,0:T(8,128)(2,1)}, u32[]{:S(2)}, u32[]{:S(2)}) collective-permute-start(bf16[256,2048]{1,0:T(8,128)(2,1)S(1)} %bitcast.205), channel_id=1, source_target_pairs={{0,2},{1,3},{2,0},{3,1},{4,6},{5,7},{6,4},{7,5},{8,10},{9,11},{10,... | collective-permute-start | bytes 3145736 | tf_op jit(solution)/shard_map/ppermute | solution.py:42
  65.9 24.6 %collective-permute-start.14 = (bf16[128,2048]{1,0:T(8,128)(2,1)S(1)}, bf16[128,2048]{1,0:T(8,128)(2,1)S(1)}, u32[]{:S(2)}, u32[]{:S(2)}) collective-permute-start(bf16[128,2048]{1,0:T(8,128)(2,1)S(1)} %pad_maximum_fusion.33), channel_id=1, source_target_pairs={{0,16},{4,20},{16,24},{20,28},{24,8},{28,12},{8,0},{12,4},{1,17},{... | collective-permute-start | bytes 1572872 | tf_op jit(solution)/shard_map/ppermute | solution.py:64
  67.1 25.0 %collective-permute-start.15 = (bf16[128,2048]{1,0:T(8,128)(2,1)S(1)}, bf16[128,2048]{1,0:T(8,128)(2,1)S(1)}, u32[]{:S(2)}, u32[]{:S(2)}) collective-permute-start(bf16[128,2048]{1,0:T(8,128)(2,1)S(1)} %pad_maximum_fusion.34), channel_id=1, source_target_pairs={{0,8},{4,12},{16,0},{20,4},{24,16},{28,20},{8,24},{12,28},{1,9},{5... | collective-permute-start | bytes 1572872 | tf_op jit(solution)/shard_map/ppermute | solution.py:64
  69.1 13.8 %collective-permute-start.10 = (bf16[128,2048]{1,0:T(8,128)(2,1)S(1)}, bf16[128,2048]{1,0:T(8,128)(2,1)S(1)}, u32[]{:S(2)}, u32[]{:S(2)}) collective-permute-start(bf16[128,2048]{1,0:T(8,128)(2,1)S(1)} %slice.807), channel_id=1, source_target_pairs={{0,2},{1,3},{2,0},{3,1},{4,6},{5,7},{6,4},{7,5},{8,10},{9,11},{10,... | collective-permute-start | bytes 1572872 | tf_op jit(solution)/shard_map/ppermute | solution.py:42
  71.7 13.5 %collective-permute-start.9 = (bf16[128,2048]{1,0:T(8,128)(2,1)S(1)}, bf16[128,2048]{1,0:T(8,128)(2,1)S(1)}, u32[]{:S(2)}, u32[]{:S(2)}) collective-permute-start(bf16[128,2048]{1,0:T(8,128)(2,1)S(1)} %slice.806), channel_id=1, source_target_pairs={{0,4},{4,0},{8,12},{12,8},{16,20},{20,16},{24,28},{28,24},{1,5},{5... | collective-permute-start | bytes 1572872 | tf_op jit(solution)/shard_map/ppermute | solution.py:42
  75.8 19.2 %collective-permute-start.4 = (bf16[512,2048]{1,0:T(8,128)(2,1)S(1)}, bf16[512,2048]{1,0:T(8,128)(2,1)S(1)}, u32[]{:S(2)}, u32[]{:S(2)}) collective-permute-start(bf16[512,2048]{1,0:T(8,128)(2,1)S(1)} %pad_maximum_fusion.4), channel_id=1, source_target_pairs={{0,1},{1,0},{2,3},{3,2},{4,5},{5,4},{6,7},{7,6},{8,9},{9,8},{10,11... | collective-permute-start | bytes 6291464 | tf_op jit(solution)/shard_map/ppermute | solution.py:42
  92.1 53.2 %collective-permute-start.23 = (bf16[352,2048]{1,0:T(8,128)(2,1)}, bf16[352,2048]{1,0:T(8,128)(2,1)}, u32[]{:S(2)}, u32[]{:S(2)}) collective-permute-start(bf16[352,2048]{1,0:T(8,128)(2,1)} %pad_maximum_fusion.14), channel_id=1, source_target_pairs={{0,16},{4,20},{16,24},{20,28},{24,8},{28,12},{8,0},{12,4},{1,17},{... | collective-permute-start | bytes 4325384 | tf_op jit(solution)/shard_map/ppermute | solution.py:64
  92.7 64.8 %collective-permute-start.24 = (bf16[352,2048]{1,0:T(8,128)(2,1)}, bf16[352,2048]{1,0:T(8,128)(2,1)}, u32[]{:S(2)}, u32[]{:S(2)}) collective-permute-start(bf16[352,2048]{1,0:T(8,128)(2,1)} %pad_maximum_fusion.14), channel_id=1, source_target_pairs={{0,8},{4,12},{16,0},{20,4},{24,16},{28,20},{8,24},{12,28},{1,9},{5... | collective-permute-start | bytes 4325384 | tf_op jit(solution)/shard_map/ppermute | solution.py:64
  98.0 41.3 %collective-permute-start.18 = (bf16[256,2048]{1,0:T(8,128)(2,1)S(1)}, bf16[256,2048]{1,0:T(8,128)(2,1)}, u32[]{:S(2)}, u32[]{:S(2)}) collective-permute-start(bf16[256,2048]{1,0:T(8,128)(2,1)S(1)} %bitcast.216), channel_id=1, source_target_pairs={{0,4},{4,0},{8,12},{12,8},{16,20},{20,16},{24,28},{28,24},{1,5},{5... | collective-permute-start | bytes 3145736 | tf_op jit(solution)/shard_map/ppermute | solution.py:42
  98.5 42.9 %collective-permute-start.17 = (bf16[256,2048]{1,0:T(8,128)(2,1)S(1)}, bf16[256,2048]{1,0:T(8,128)(2,1)S(1)}, u32[]{:S(2)}, u32[]{:S(2)}) collective-permute-start(bf16[256,2048]{1,0:T(8,128)(2,1)S(1)} %bitcast.217), channel_id=1, source_target_pairs={{0,2},{1,3},{2,0},{3,1},{4,6},{5,7},{6,4},{7,5},{8,10},{9,11},{10,... | collective-permute-start | bytes 3145736 | tf_op jit(solution)/shard_map/ppermute | solution.py:42
  128.2 46.3 %collective-permute-start.19 = (bf16[512,2048]{1,0:T(8,128)(2,1)}, bf16[512,2048]{1,0:T(8,128)(2,1)}, u32[]{:S(2)}, u32[]{:S(2)}) collective-permute-start(bf16[512,2048]{1,0:T(8,128)(2,1)} %convolution_convert_fusion.2), channel_id=1, source_target_pairs={{0,1},{1,0},{2,3},{3,2},{4,5},{5,4},{6,7},{7,6},{8,9},{9,8},{10,11... | collective-permute-start | bytes 6291464 | tf_op jit(solution)/shard_map/ppermute | solution.py:42
  140.8 26.5 %collective-permute-start.22 = (bf16[128,2048]{1,0:T(8,128)(2,1)S(1)}, bf16[128,2048]{1,0:T(8,128)(2,1)S(1)}, u32[]{:S(2)}, u32[]{:S(2)}) collective-permute-start(bf16[128,2048]{1,0:T(8,128)(2,1)S(1)} %slice.829), channel_id=1, source_target_pairs={{0,2},{1,3},{2,0},{3,1},{4,6},{5,7},{6,4},{7,5},{8,10},{9,11},{10,... | collective-permute-start | bytes 1572872 | tf_op jit(solution)/shard_map/ppermute | solution.py:42
  141.5 26.3 %collective-permute-start.21 = (bf16[128,2048]{1,0:T(8,128)(2,1)S(1)}, bf16[128,2048]{1,0:T(8,128)(2,1)S(1)}, u32[]{:S(2)}, u32[]{:S(2)}) collective-permute-start(bf16[128,2048]{1,0:T(8,128)(2,1)S(1)} %slice.828), channel_id=1, source_target_pairs={{0,4},{4,0},{8,12},{12,8},{16,20},{20,16},{24,28},{28,24},{1,5},{5... | collective-permute-start | bytes 1572872 | tf_op jit(solution)/shard_map/ppermute | solution.py:42
  145.4 89.5 %collective-permute-start.33 = (bf16[512,2048]{1,0:T(8,128)(2,1)}, bf16[512,2048]{1,0:T(8,128)(2,1)}, u32[]{:S(2)}, u32[]{:S(2)}) collective-permute-start(bf16[512,2048]{1,0:T(8,128)(2,1)} %pad_maximum_fusion.6), channel_id=1, source_target_pairs={{0,1},{1,0},{2,3},{3,2},{4,5},{5,4},{6,7},{7,6},{8,9},{9,8},{10,11... | collective-permute-start | bytes 6291464 | tf_op jit(solution)/shard_map/ppermute | solution.py:42
  157.5 14.3 %collective-permute-start.20 = (bf16[512,2048]{1,0:T(8,128)(2,1)S(1)}, bf16[512,2048]{1,0:T(8,128)(2,1)S(1)}, u32[]{:S(2)}, u32[]{:S(2)}) collective-permute-start(bf16[512,2048]{1,0:T(8,128)(2,1)S(1)} %convolution_convert_fusion), channel_id=1, source_target_pairs={{0,1},{1,0},{2,3},{3,2},{4,5},{5,4},{6,7},{7,6},{8,9},{9,8},{10,11... | collective-permute-start | bytes 6291464 | tf_op jit(solution)/shard_map/ppermute | solution.py:42
  167.3 66.1 %collective-permute-start.30 = (bf16[256,2048]{1,0:T(8,128)(2,1)}, bf16[256,2048]{1,0:T(8,128)(2,1)}, u32[]{:S(2)}, u32[]{:S(2)}) collective-permute-start(bf16[256,2048]{1,0:T(8,128)(2,1)} %pad_maximum_fusion.20), channel_id=1, source_target_pairs={{0,8},{4,12},{16,0},{20,4},{24,16},{28,20},{8,24},{12,28},{1,9},{5... | collective-permute-start | bytes 3145736 | tf_op jit(solution)/shard_map/ppermute | solution.py:64
  167.8 49.7 %collective-permute-start.29 = (bf16[272,2048]{1,0:T(8,128)(2,1)}, bf16[272,2048]{1,0:T(8,128)(2,1)}, u32[]{:S(2)}, u32[]{:S(2)}) collective-permute-start(bf16[272,2048]{1,0:T(8,128)(2,1)} %pad_maximum_fusion.16), channel_id=1, source_target_pairs={{0,16},{4,20},{16,24},{20,28},{24,8},{28,12},{8,0},{12,4},{1,17},{... | collective-permute-start | bytes 3342344 | tf_op jit(solution)/shard_map/ppermute | solution.py:64
  173.0 46.3 %collective-permute-start.26 = (bf16[128,2048]{1,0:T(8,128)(2,1)S(1)}, bf16[128,2048]{1,0:T(8,128)(2,1)S(1)}, u32[]{:S(2)}, u32[]{:S(2)}) collective-permute-start(bf16[128,2048]{1,0:T(8,128)(2,1)S(1)} %get-tuple-element.268), channel_id=1, source_target_pairs={{0,2},{1,3},{2,0},{3,1},{4,6},{5,7},{6,4},{7,5},{8,10},{9,11},{10,... | collective-permute-start | bytes 1572872 | tf_op jit(solution)/shard_map/ppermute | solution.py:42
  218.7 13.7 %collective-permute-start.25 = (bf16[128,2048]{1,0:T(8,128)(2,1)S(1)}, bf16[128,2048]{1,0:T(8,128)(2,1)S(1)}, u32[]{:S(2)}, u32[]{:S(2)}) collective-permute-start(bf16[128,2048]{1,0:T(8,128)(2,1)S(1)} %get-tuple-element.269), channel_id=1, source_target_pairs={{0,4},{4,0},{8,12},{12,8},{16,20},{20,16},{24,28},{28,24},{1,5},{5... | collective-permute-start | bytes 1572872 | tf_op jit(solution)/shard_map/ppermute | solution.py:42
  232.6 24.1 %collective-permute-start.27 = (bf16[256,2048]{1,0:T(8,128)(2,1)S(1)}, bf16[256,2048]{1,0:T(8,128)(2,1)S(1)}, u32[]{:S(2)}, u32[]{:S(2)}) collective-permute-start(bf16[256,2048]{1,0:T(8,128)(2,1)S(1)} %pad_maximum_fusion.18), channel_id=1, source_target_pairs={{0,2},{1,3},{2,0},{3,1},{4,6},{5,7},{6,4},{7,5},{8,10},{9,11},{10,... | collective-permute-start | bytes 3145736 | tf_op jit(solution)/shard_map/ppermute | solution.py:42
  232.9 23.9 %collective-permute-start.28 = (bf16[256,2048]{1,0:T(8,128)(2,1)S(1)}, bf16[256,2048]{1,0:T(8,128)(2,1)S(1)}, u32[]{:S(2)}, u32[]{:S(2)}) collective-permute-start(bf16[256,2048]{1,0:T(8,128)(2,1)S(1)} %pad_maximum_fusion.19), channel_id=1, source_target_pairs={{0,4},{4,0},{8,12},{12,8},{16,20},{20,16},{24,28},{28,24},{1,5},{5... | collective-permute-start | bytes 3145736 | tf_op jit(solution)/shard_map/ppermute | solution.py:42
  234.8 23.6 %collective-permute-start.34 = (bf16[512,2048]{1,0:T(8,128)(2,1)S(1)}, bf16[512,2048]{1,0:T(8,128)(2,1)S(1)}, u32[]{:S(2)}, u32[]{:S(2)}) collective-permute-start(bf16[512,2048]{1,0:T(8,128)(2,1)S(1)} %pad_maximum_fusion.7), channel_id=1, source_target_pairs={{0,1},{1,0},{2,3},{3,2},{4,5},{5,4},{6,7},{7,6},{8,9},{9,8},{10,11... | collective-permute-start | bytes 6291464 | tf_op jit(solution)/shard_map/ppermute | solution.py:42
  236.0 60.1 %collective-permute-start.32 = (bf16[160,2048]{1,0:T(8,128)(2,1)}, bf16[160,2048]{1,0:T(8,128)(2,1)S(1)}, u32[]{:S(2)}, u32[]{:S(2)}) collective-permute-start(bf16[160,2048]{1,0:T(8,128)(2,1)} %pad_maximum_fusion.32), channel_id=1, source_target_pairs={{0,8},{4,12},{16,0},{20,4},{24,16},{28,20},{8,24},{12,28},{1,9},{5... | collective-permute-start | bytes 1966088 | tf_op jit(solution)/shard_map/ppermute | solution.py:64
  237.0 59.2 %collective-permute-start.31 = (bf16[192,2048]{1,0:T(8,128)(2,1)S(1)}, bf16[192,2048]{1,0:T(8,128)(2,1)}, u32[]{:S(2)}, u32[]{:S(2)}) collective-permute-start(bf16[192,2048]{1,0:T(8,128)(2,1)S(1)} %pad_maximum_fusion.31), channel_id=1, source_target_pairs={{0,16},{4,20},{16,24},{20,28},{24,8},{28,12},{8,0},{12,4},{1,17},{... | collective-permute-start | bytes 2359304 | tf_op jit(solution)/shard_map/ppermute | solution.py:64
  258.4 23.3 %collective-permute-start.37 = (bf16[256,2048]{1,0:T(8,128)(2,1)S(1)}, bf16[256,2048]{1,0:T(8,128)(2,1)S(1)}, u32[]{:S(2)}, u32[]{:S(2)}) collective-permute-start(bf16[256,2048]{1,0:T(8,128)(2,1)S(1)} %multiply_convert_fusion.3), channel_id=1, source_target_pairs={{0,4},{4,0},{8,12},{12,8},{16,20},{20,16},{24,28},{28,24},{1,5},{5... | collective-permute-start | bytes 3145736 | tf_op jit(solution)/shard_map/ppermute | solution.py:42
  259.1 24.9 %collective-permute-start.35 = (bf16[256,2048]{1,0:T(8,128)(2,1)S(1)}, bf16[256,2048]{1,0:T(8,128)(2,1)S(1)}, u32[]{:S(2)}, u32[]{:S(2)}) collective-permute-start(bf16[256,2048]{1,0:T(8,128)(2,1)S(1)} %multiply_convert_fusion.3), channel_id=1, source_target_pairs={{0,2},{1,3},{2,0},{3,1},{4,6},{5,7},{6,4},{7,5},{8,10},{9,11},{10,... | collective-permute-start | bytes 3145736 | tf_op jit(solution)/shard_map/ppermute | solution.py:42
  345.0 17.7 %collective-permute-start.43 = (bf16[128,2048]{1,0:T(8,128)(2,1)}, bf16[128,2048]{1,0:T(8,128)(2,1)}, u32[]{:S(2)}, u32[]{:S(2)}) collective-permute-start(bf16[128,2048]{1,0:T(8,128)(2,1)} %get-tuple-element.246), channel_id=1, source_target_pairs={{0,2},{1,3},{2,0},{3,1},{4,6},{5,7},{6,4},{7,5},{8,10},{9,11},{10,... | collective-permute-start | bytes 1572872 | tf_op jit(solution)/shard_map/ppermute | solution.py:42
  361.9 14.0 %collective-permute-start.42 = (bf16[128,2048]{1,0:T(8,128)(2,1)}, bf16[128,2048]{1,0:T(8,128)(2,1)S(1)}, u32[]{:S(2)}, u32[]{:S(2)}) collective-permute-start(bf16[128,2048]{1,0:T(8,128)(2,1)} %get-tuple-element.247), channel_id=1, source_target_pairs={{0,4},{4,0},{8,12},{12,8},{16,20},{20,16},{24,28},{28,24},{1,5},{5... | collective-permute-start | bytes 1572872 | tf_op jit(solution)/shard_map/ppermute | solution.py:42
  378.3 26.6 %collective-permute-start.45 = (bf16[256,2048]{1,0:T(8,128)(2,1)}, bf16[256,2048]{1,0:T(8,128)(2,1)}, u32[]{:S(2)}, u32[]{:S(2)}) collective-permute-start(bf16[256,2048]{1,0:T(8,128)(2,1)} %pad_maximum_fusion.21), channel_id=1, source_target_pairs={{0,2},{1,3},{2,0},{3,1},{4,6},{5,7},{6,4},{7,5},{8,10},{9,11},{10,... | collective-permute-start | bytes 3145736 | tf_op jit(solution)/shard_map/ppermute | solution.py:42
  379.6 25.4 %collective-permute-start.46 = (bf16[256,2048]{1,0:T(8,128)(2,1)}, bf16[256,2048]{1,0:T(8,128)(2,1)}, u32[]{:S(2)}, u32[]{:S(2)}) collective-permute-start(bf16[256,2048]{1,0:T(8,128)(2,1)} %pad_maximum_fusion.22), channel_id=1, source_target_pairs={{0,4},{4,0},{8,12},{12,8},{16,20},{20,16},{24,28},{28,24},{1,5},{5... | collective-permute-start | bytes 3145736 | tf_op jit(solution)/shard_map/ppermute | solution.py:42
  413.0 27.9 %collective-permute-start.49 = (bf16[256,2048]{1,0:T(8,128)(2,1)}, bf16[256,2048]{1,0:T(8,128)(2,1)}, u32[]{:S(2)}, u32[]{:S(2)}) collective-permute-start(bf16[256,2048]{1,0:T(8,128)(2,1)} %get-tuple-element.199), channel_id=1, source_target_pairs={{0,4},{4,0},{8,12},{12,8},{16,20},{20,16},{24,28},{28,24},{1,5},{5... | collective-permute-start | bytes 3145736 | tf_op jit(solution)/shard_map/ppermute | solution.py:42
  414.4 28.9 %collective-permute-start.47 = (bf16[256,2048]{1,0:T(8,128)(2,1)}, bf16[256,2048]{1,0:T(8,128)(2,1)}, u32[]{:S(2)}, u32[]{:S(2)}) collective-permute-start(bf16[256,2048]{1,0:T(8,128)(2,1)} %get-tuple-element.199), channel_id=1, source_target_pairs={{0,2},{1,3},{2,0},{3,1},{4,6},{5,7},{6,4},{7,5},{8,10},{9,11},{10,... | collective-permute-start | bytes 3145736 | tf_op jit(solution)/shard_map/ppermute | solution.py:42
  416.3 48.1 %collective-permute-start.65 = (bf16[288,2048]{1,0:T(8,128)(2,1)}, bf16[288,2048]{1,0:T(8,128)(2,1)}, u32[]{:S(2)}, u32[]{:S(2)}) collective-permute-start(bf16[288,2048]{1,0:T(8,128)(2,1)} %pad_maximum_fusion.15), channel_id=1, source_target_pairs={{0,16},{4,20},{16,24},{20,28},{24,8},{28,12},{8,0},{12,4},{1,17},{... | collective-permute-start | bytes 3538952 | tf_op jit(solution)/shard_map/ppermute | solution.py:64
  418.0 46.3 %collective-permute-start.66 = (bf16[240,2048]{1,0:T(8,128)(2,1)}, bf16[240,2048]{1,0:T(8,128)(2,1)}, u32[]{:S(2)}, u32[]{:S(2)}) collective-permute-start(bf16[240,2048]{1,0:T(8,128)(2,1)} %pad_maximum_fusion.29), channel_id=1, source_target_pairs={{0,8},{4,12},{16,0},{20,4},{24,16},{28,20},{8,24},{12,28},{1,9},{5... | collective-permute-start | bytes 2949128 | tf_op jit(solution)/shard_map/ppermute | solution.py:64
  442.0 36.4 %collective-permute-start.50 = (bf16[128,2048]{1,0:T(8,128)(2,1)S(1)}, bf16[128,2048]{1,0:T(8,128)(2,1)S(1)}, u32[]{:S(2)}, u32[]{:S(2)}) collective-permute-start(bf16[128,2048]{1,0:T(8,128)(2,1)S(1)} %slice.858), channel_id=1, source_target_pairs={{0,2},{1,3},{2,0},{3,1},{4,6},{5,7},{6,4},{7,5},{8,10},{9,11},{10,... | collective-permute-start | bytes 1572872 | tf_op jit(solution)/shard_map/ppermute | solution.py:42
  444.4 34.0 %collective-permute-start.48 = (bf16[128,2048]{1,0:T(8,128)(2,1)S(1)}, bf16[128,2048]{1,0:T(8,128)(2,1)S(1)}, u32[]{:S(2)}, u32[]{:S(2)}) collective-permute-start(bf16[128,2048]{1,0:T(8,128)(2,1)S(1)} %slice.857), channel_id=1, source_target_pairs={{0,4},{4,0},{8,12},{12,8},{16,20},{20,16},{24,28},{28,24},{1,5},{5... | collective-permute-start | bytes 1572872 | tf_op jit(solution)/shard_map/ppermute | solution.py:42
  447.1 38.8 %collective-permute-start.57 = (bf16[512,2048]{1,0:T(8,128)(2,1)S(1)}, bf16[512,2048]{1,0:T(8,128)(2,1)S(1)}, u32[]{:S(2)}, u32[]{:S(2)}) collective-permute-start(bf16[512,2048]{1,0:T(8,128)(2,1)S(1)} %pad_maximum_fusion.10), channel_id=1, source_target_pairs={{0,1},{1,0},{2,3},{3,2},{4,5},{5,4},{6,7},{7,6},{8,9},{9,8},{10,11... | collective-permute-start | bytes 6291464 | tf_op jit(solution)/shard_map/ppermute | solution.py:42
  476.4 99.6 %collective-permute-start.67 = (bf16[528,2048]{1,0:T(8,128)(2,1)}, bf16[528,2048]{1,0:T(8,128)(2,1)}, u32[]{:S(2)}, u32[]{:S(2)}) collective-permute-start(bf16[528,2048]{1,0:T(8,128)(2,1)} %get-tuple-element.154), channel_id=1, source_target_pairs={{0,16},{4,20},{16,24},{20,28},{24,8},{28,12},{8,0},{12,4},{1,17},{... | collective-permute-start | bytes 6488072 | tf_op jit(solution)/shard_map/ppermute | solution.py:64
  477.0 99.0 %collective-permute-start.68 = (bf16[528,2048]{1,0:T(8,128)(2,1)}, bf16[528,2048]{1,0:T(8,128)(2,1)}, u32[]{:S(2)}, u32[]{:S(2)}) collective-permute-start(bf16[528,2048]{1,0:T(8,128)(2,1)} %get-tuple-element.155), channel_id=1, source_target_pairs={{0,8},{4,12},{16,0},{20,4},{24,16},{28,20},{8,24},{12,28},{1,9},{5... | collective-permute-start | bytes 6488072 | tf_op jit(solution)/shard_map/ppermute | solution.py:64
  478.4 31.6 %collective-permute-start.52 = (bf16[512,2048]{1,0:T(8,128)(2,1)S(1)}, bf16[512,2048]{1,0:T(8,128)(2,1)S(1)}, u32[]{:S(2)}, u32[]{:S(2)}) collective-permute-start(bf16[512,2048]{1,0:T(8,128)(2,1)S(1)} %copy-done.72), channel_id=1, source_target_pairs={{0,1},{1,0},{2,3},{3,2},{4,5},{5,4},{6,7},{7,6},{8,9},{9,8},{10,11... | collective-permute-start | bytes 6291464 | tf_op jit(solution)/shard_map/ppermute | solution.py:42
  480.8 39.3 %collective-permute-start.51 = (bf16[512,2048]{1,0:T(8,128)(2,1)}, bf16[512,2048]{1,0:T(8,128)(2,1)}, u32[]{:S(2)}, u32[]{:S(2)}) collective-permute-start(bf16[512,2048]{1,0:T(8,128)(2,1)} %product.10), channel_id=1, source_target_pairs={{0,1},{1,0},{2,3},{3,2},{4,5},{5,4},{6,7},{7,6},{8,9},{9,8},{10,11... | collective-permute-start | bytes 6291464 | tf_op jit(solution)/shard_map/ppermute | solution.py:42
  485.9 25.9 %collective-permute-start.59 = (bf16[512,2048]{1,0:T(8,128)(2,1)}, bf16[512,2048]{1,0:T(8,128)(2,1)}, u32[]{:S(2)}, u32[]{:S(2)}) collective-permute-start(bf16[512,2048]{1,0:T(8,128)(2,1)} %pad_maximum_fusion.11), channel_id=1, source_target_pairs={{0,1},{1,0},{2,3},{3,2},{4,5},{5,4},{6,7},{7,6},{8,9},{9,8},{10,11... | collective-permute-start | bytes 6291464 | tf_op jit(solution)/shard_map/ppermute | solution.py:42
  510.0 30.0 %collective-permute-start.58 = (bf16[512,2048]{1,0:T(8,128)(2,1)S(1)}, bf16[512,2048]{1,0:T(8,128)(2,1)S(1)}, u32[]{:S(2)}, u32[]{:S(2)}) collective-permute-start(bf16[512,2048]{1,0:T(8,128)(2,1)S(1)} %convolution_convert_fusion.6), channel_id=1, source_target_pairs={{0,1},{1,0},{2,3},{3,2},{4,5},{5,4},{6,7},{7,6},{8,9},{9,8},{10,11... | collective-permute-start | bytes 6291464 | tf_op jit(solution)/shard_map/ppermute | solution.py:42
  511.8 16.5 %collective-permute-start.54 = (bf16[128,2048]{1,0:T(8,128)(2,1)S(1)}, bf16[128,2048]{1,0:T(8,128)(2,1)S(1)}, u32[]{:S(2)}, u32[]{:S(2)}) collective-permute-start(bf16[128,2048]{1,0:T(8,128)(2,1)S(1)} %get-tuple-element.243), channel_id=1, source_target_pairs={{0,2},{1,3},{2,0},{3,1},{4,6},{5,7},{6,4},{7,5},{8,10},{9,11},{10,... | collective-permute-start | bytes 1572872 | tf_op jit(solution)/shard_map/ppermute | solution.py:42
  520.2 14.1 %collective-permute-start.53 = (bf16[128,2048]{1,0:T(8,128)(2,1)S(1)}, bf16[128,2048]{1,0:T(8,128)(2,1)S(1)}, u32[]{:S(2)}, u32[]{:S(2)}) collective-permute-start(bf16[128,2048]{1,0:T(8,128)(2,1)S(1)} %get-tuple-element.244), channel_id=1, source_target_pairs={{0,4},{4,0},{8,12},{12,8},{16,20},{20,16},{24,28},{28,24},{1,5},{5... | collective-permute-start | bytes 1572872 | tf_op jit(solution)/shard_map/ppermute | solution.py:42
  535.4 29.2 %collective-permute-start.55 = (bf16[256,2048]{1,0:T(8,128)(2,1)}, bf16[256,2048]{1,0:T(8,128)(2,1)}, u32[]{:S(2)}, u32[]{:S(2)}) collective-permute-start(bf16[256,2048]{1,0:T(8,128)(2,1)} %pad_maximum_fusion.23), channel_id=1, source_target_pairs={{0,2},{1,3},{2,0},{3,1},{4,6},{5,7},{6,4},{7,5},{8,10},{9,11},{10,... | collective-permute-start | bytes 3145736 | tf_op jit(solution)/shard_map/ppermute | solution.py:42
  536.0 28.6 %collective-permute-start.56 = (bf16[256,2048]{1,0:T(8,128)(2,1)}, bf16[256,2048]{1,0:T(8,128)(2,1)}, u32[]{:S(2)}, u32[]{:S(2)}) collective-permute-start(bf16[256,2048]{1,0:T(8,128)(2,1)} %pad_maximum_fusion.24), channel_id=1, source_target_pairs={{0,4},{4,0},{8,12},{12,8},{16,20},{20,16},{24,28},{28,24},{1,5},{5... | collective-permute-start | bytes 3145736 | tf_op jit(solution)/shard_map/ppermute | solution.py:42
  568.7 48.0 %collective-permute-start.60 = (bf16[512,2048]{1,0:T(8,128)(2,1)S(1)}, bf16[512,2048]{1,0:T(8,128)(2,1)S(1)}, u32[]{:S(2)}, u32[]{:S(2)}) collective-permute-start(bf16[512,2048]{1,0:T(8,128)(2,1)S(1)} %convolution_convert_fusion.5), channel_id=1, source_target_pairs={{0,1},{1,0},{2,3},{3,2},{4,5},{5,4},{6,7},{7,6},{8,9},{9,8},{10,11... | collective-permute-start | bytes 6291464 | tf_op jit(solution)/shard_map/ppermute | solution.py:42
  583.6 14.4 %collective-permute-start.69 = (bf16[128,2048]{1,0:T(8,128)(2,1)S(1)}, bf16[128,2048]{1,0:T(8,128)(2,1)S(1)}, u32[]{:S(2)}, u32[]{:S(2)}) collective-permute-start(bf16[128,2048]{1,0:T(8,128)(2,1)S(1)} %pad_maximum_fusion.35), channel_id=1, source_target_pairs={{0,16},{4,20},{16,24},{20,28},{24,8},{28,12},{8,0},{12,4},{1,17},{... | collective-permute-start | bytes 1572872 | tf_op jit(solution)/shard_map/ppermute | solution.py:64
  585.1 25.9 %collective-permute-start.70 = (bf16[128,2048]{1,0:T(8,128)(2,1)S(1)}, bf16[128,2048]{1,0:T(8,128)(2,1)S(1)}, u32[]{:S(2)}, u32[]{:S(2)}) collective-permute-start(bf16[128,2048]{1,0:T(8,128)(2,1)S(1)} %pad_maximum_fusion.36), channel_id=1, source_target_pairs={{0,8},{4,12},{16,0},{20,4},{24,16},{28,20},{8,24},{12,28},{1,9},{5... | collective-permute-start | bytes 1572872 | tf_op jit(solution)/shard_map/ppermute | solution.py:64
  614.4 69.0 %collective-permute-start.71 = (bf16[256,2048]{1,0:T(8,128)(2,1)}, bf16[256,2048]{1,0:T(8,128)(2,1)}, u32[]{:S(2)}, u32[]{:S(2)}) collective-permute-start(bf16[256,2048]{1,0:T(8,128)(2,1)} %pad_maximum_fusion.27), channel_id=1, source_target_pairs={{0,16},{4,20},{16,24},{20,28},{24,8},{28,12},{8,0},{12,4},{1,17},{... | collective-permute-start | bytes 3145736 | tf_op jit(solution)/shard_map/ppermute | solution.py:64
  615.0 68.4 %collective-permute-start.72 = (bf16[256,2048]{1,0:T(8,128)(2,1)}, bf16[256,2048]{1,0:T(8,128)(2,1)}, u32[]{:S(2)}, u32[]{:S(2)}) collective-permute-start(bf16[256,2048]{1,0:T(8,128)(2,1)} %pad_maximum_fusion.28), channel_id=1, source_target_pairs={{0,8},{4,12},{16,0},{20,4},{24,16},{28,20},{8,24},{12,28},{1,9},{5... | collective-permute-start | bytes 3145736 | tf_op jit(solution)/shard_map/ppermute | solution.py:64
  620.8 13.4 %collective-permute-start.62 = (bf16[128,2048]{1,0:T(8,128)(2,1)S(1)}, bf16[128,2048]{1,0:T(8,128)(2,1)S(1)}, u32[]{:S(2)}, u32[]{:S(2)}) collective-permute-start(bf16[128,2048]{1,0:T(8,128)(2,1)S(1)} %get-tuple-element.240), channel_id=1, source_target_pairs={{0,2},{1,3},{2,0},{3,1},{4,6},{5,7},{6,4},{7,5},{8,10},{9,11},{10,... | collective-permute-start | bytes 1572872 | tf_op jit(solution)/shard_map/ppermute | solution.py:42
  635.1 16.2 %collective-permute-start.73 = (f32[2,2,4,2,64]{4,2,3,1,0:T(4,128)S(1)}, f32[2,2,4,2,64]{4,2,3,1,0:T(4,128)S(1)}, u32[]{:S(2)}, u32[]{:S(2)}) collective-permute-start(f32[2,2,4,2,64]{4,2,3,1,0:T(4,128)S(1)} %slice.914), channel_id=1, source_target_pairs={{0,1},{1,0},{2,3},{3,2},{4,5},{5,4},{6,7},{7,6},{8,9},{9,8},{10,11... | collective-permute-start | bytes 24584 | tf_op jit(solution)/shard_map/ppermute | solution.py:42
  640.4 29.9 %collective-permute-start.63 = (bf16[256,2048]{1,0:T(8,128)(2,1)}, bf16[256,2048]{1,0:T(8,128)(2,1)S(1)}, u32[]{:S(2)}, u32[]{:S(2)}) collective-permute-start(bf16[256,2048]{1,0:T(8,128)(2,1)} %pad_maximum_fusion.25), channel_id=1, source_target_pairs={{0,2},{1,3},{2,0},{3,1},{4,6},{5,7},{6,4},{7,5},{8,10},{9,11},{10,... | collective-permute-start | bytes 3145736 | tf_op jit(solution)/shard_map/ppermute | solution.py:42
  641.6 28.7 %collective-permute-start.64 = (bf16[256,2048]{1,0:T(8,128)(2,1)}, bf16[256,2048]{1,0:T(8,128)(2,1)}, u32[]{:S(2)}, u32[]{:S(2)}) collective-permute-start(bf16[256,2048]{1,0:T(8,128)(2,1)} %pad_maximum_fusion.26), channel_id=1, source_target_pairs={{0,4},{4,0},{8,12},{12,8},{16,20},{20,16},{24,28},{28,24},{1,5},{5... | collective-permute-start | bytes 3145736 | tf_op jit(solution)/shard_map/ppermute | solution.py:42
  651.3 14.8 %collective-permute-start.74 = (f32[2,4,2,64]{3,1,2,0:T(4,128)S(1)}, f32[2,4,2,64]{3,1,2,0:T(4,128)S(1)}, u32[]{:S(2)}, u32[]{:S(2)}) collective-permute-start(f32[2,4,2,64]{3,1,2,0:T(4,128)S(1)} %slice_bitcast_fusion.3), channel_id=1, source_target_pairs={{0,2},{1,3},{2,0},{3,1},{4,6},{5,7},{6,4},{7,5},{8,10},{9,11},{10,... | collective-permute-start | bytes 12296 | tf_op jit(solution)/shard_map/ppermute | solution.py:42
  (121 other events, 1373.7 us)

commit v10 on v9

--- a/solution.py
+++ b/solution.py
@@ -378,7 +378,9 @@
     return pl.pallas_call(
         moment_kernel,
         out_shape=(shape,) * 4,
-        cost_estimate=light,
+        cost_estimate=pl.CostEstimate(
+            flops=16 * 15 * SPAN * width, bytes_accessed=4 * SPAN * width, transcendentals=0
+        ),
         name="moments",
     )(grad, step_re, step_im)
 
@@ -788,7 +790,10 @@
     hidden = (silu * up_pre).astype(bf16)
     d_gate = (d_hidden * up_pre * sig * (1.0 + gate_pre * (1.0 - sig))).astype(bf16)
     d_up = (d_hidden * silu).astype(bf16)
+    grad_down = product(hidden, rows_upstream, "nn", bf16)
+    d_gate, d_up = after([d_gate, d_up], [grad_down])
     parts = [slice(p, p + even) for p in range(0, 2 * slots, even)]
+
     def second_share(n):
         p = parts[n]
         return (tn(d_gate[:, p], gate_all) + tn(d_up[:, p], up_all)).astype(bf16)
@@ -796,24 +801,22 @@
     odds = [second_share(n) for n in (1, 3)]
     cores = [swap(odd, "narrow", 1) for odd in odds]
     evens = [second_share(0), second_share(2)]
-    [ready] = after([hidden], cores + evens)
-    grad_down = product(ready, rows_upstream, "nn", bf16)
-    d_second, stages = scatter_rows(evens[0], cores[0], evens[1], cores[1], (), [grad_down])
+    d_second, stages = scatter_rows(evens[0], cores[0], evens[1], cores[1])
     upstream = upstream_low.astype(f32)
     d_middle = upstream + norm_back(middle, rate_last, gain_last, d_second)
     (middle_own, middle_other), middle_stages = gather_rows(d_middle.astype(bf16))
     rows_dmiddle = [jnp.concatenate(middle_own, axis=0), jnp.concatenate(middle_other, axis=0)]
     grads = [Scatter(jnp.split(grad_down, outer, axis=0))]
-    [d_gate] = after([d_gate], stages[0])
+    [d_gate] = after([d_gate], cores + evens)
     grad_gate = product(d_gate, rows_second, "nn", bf16)
-    [d_up] = after([d_up], [grad_gate])
+    [d_up] = after([d_up], stages[0] + [grad_gate])
     grad_up = product(d_up, rows_second, "nn", bf16)
     [hidden] = after([hidden], [grad_up])
     down_shares = [product(hidden, down_all, "tn", bf16, n) for n in (0, 1)]
     down_shares += [product(hidden, down_all, "tn", bf16, n) for n in (2, 3)]
     pair = [Scatter(jnp.split(grad, outer, axis=0)) for grad in (grad_gate, grad_up)]
     grads += pair
-    last = ring_step(grads, (), middle_stages[0])
+    last = ring_step(grads, (), middle_stages[1])
     down_shares = after(down_shares, middle_stages[1])
     down_cores = [swap(down_shares[n], "narrow", 1) for n in (1, 3)]
     down_out, down_stages = scatter_rows(
@@ -857,7 +860,7 @@
     chunks = grad_in.reshape(3, outer, own, width)
     in_sum = Scatter([chunks[:, j].reshape(3 * own, width) for j in range(outer)])
     out_sum = Scatter(jnp.split(grad_out, outer, axis=0))
-    last = ring_step([in_sum, out_sum], last)
+    last = ring_step([in_sum, out_sum], last, stages[0])
     d_filter, *_ = after([d_filter], last + stages[0])
     gain_grads = jnp.stack([grad_gain_one / gain_first, grad_gain_two])
     [gain_grads] = after([gain_grads], stages[0])

time: 697 us -> 656 us (0.941)
  waiting for transfers between devices: 201 us -> 170 us
    ppermute x24, waiting for transfers between devices: 93.6 us -> 76.8 us  [along(): return lax.ppermute(values, 'wide', pairs)]
    ppermute x55, waiting for transfers between devices: 108 us -> 92.8 us  [swap(): return lax.ppermute(values, axis, [(i, i ^ shift) for i in range(size)])]
    unnamed x228 -> x240, local copies, waits for them, and re-layouts: 30.4 us -> 27.5 us
  transfers between devices with their start and end apart: 79 -> 79, of which waited for: 22 -> 28; matrix products, arithmetic and copies ran while one was open for 35% -> 33% of each run, Pallas kernels for 16% -> 16%
where the time goes in v10:
time: 656 us; the launch traced here: 648 us
  waiting for transfers between devices  170 us (26%)
  other arithmetic  120 us (18%)
  Pallas kernels  112 us (17%)
  matrix products  98.5 us (15%)
  starting transfers between devices  78.3 us (12%)
  local copies, waits for them, and re-layouts  66.5 us (10%)
    ppermute x55, waiting for transfers between devices, swap(): return lax.ppermute(values, axis, [(i, i ^ shift) for i in range(size)])  92.8 us
    ppermute x24, waiting for transfers between devices, along(): return lax.ppermute(values, 'wide', pairs)  76.8 us
    pallas_call x7, Pallas kernels, product(): pl.pallas_call(partial(product_kernel, kind=kind), grid=(columns // side,...  53.4 us
    ppermute x55, starting transfers between devices, swap(): return lax.ppermute(values, axis, [(i, i ^ shift) for i in range(size)])  47.3 us
    dot_general x7, matrix products, nt(): lax.dot_general(a, b, (((1,), (1,)), ((), ())), preferred_element_type=f32)  45.1 us
    pallas_call x2, Pallas kernels, mixer_backward(): pl.pallas_call(backward_kernel, out_shape=(jax.ShapeDtypeStruct((pieces,...  32 us
    dot_general x12, matrix products, tn(): lax.dot_general(a, b, (((0,), (0,)), ((), ())), preferred_element_type=f32)  31.1 us
    ppermute x24, starting transfers between devices, along(): return lax.ppermute(values, 'wide', pairs)  31 us
  transfers between devices with their start and end apart: 79, of which 28 were waited for; matrix products, arithmetic and copies ran while one was open for 33% of the time, Pallas kernels for 16%

profile of v10, /device:TPU:0, one launch (start us, length us, event | category | flops | bytes accessed | tf_op | source)
XLA Modules:
  0.0 647.9 jit_solution(14376482007447457947)
XLA Ops:
  1.5 3.1 concatenate.233
  4.6 4.1 collective-permute-start
  8.7 3.0 collective-permute-start.2
  23.7 2.6 constant_dynamic-update-slice_fusion.1
  26.3 2.5 pad_maximum_fusion.14
  35.7 4.1 taps.1
  39.7 3.5 fusion.91.spectrum
  43.2 9.3 %collective-permute-done.16 = s32[2,3]{1,0:T(2,128)S(1)} collective-permute-done((s32[2,3]{1,0:T(2,128)S(1)}, s32[2,3]{1,0:T(2,128)S(1)}, u32[]{:S(2)}, u32[]{:S(2)}) %collective-permute-start.16) | collective-permute-done | bytes 56 | tf_op jit(solution)/shard_map/ppermute | solution.py:42
  77.0 6.9 %collective-permute-done.10 = bf16[128,2048]{1,0:T(8,128)(2,1)S(1)} collective-permute-done((bf16[128,2048]{1,0:T(8,128)(2,1)S(1)}, bf16[128,2048]{1,0:T(8,128)(2,1)S(1)}, u32[]{:S(2)}, u32[]{:S(2)}) %collective-permute-start.10) | collective-permute-done | bytes 524320 | tf_op jit(solution)/shard_map/ppermute | solution.py:42
  84.0 2.4 collective-permute-done.9
  91.6 2.7 collective-permute-done.15
  97.2 2.8 fusion
  105.2 13.1 %fusion.5 = (bf16[1024,2048]{1,0:T(8,128)(2,1)S(1)}, bf16[1024,2048]{1,0:T(8,128)(2,1)S(1)}) fusion(f32[1024]{0:T(1024)S(1)} %add_rsqrt_fusion, f32[2048]{0:T(1024)S(1)} %mul.420, bf16[512,2048]{1,0:T(8,128)(2,1)S(1)} %collective-permute-done.11, bf16[128,2048]{1,0:T(8,128)(2,1)S(1)} %collective-permute-done.10, ...), kind=kLoop, calls=%fused_computation.9 | loop fusion | flops 41943040 | bytes 16793600 | tf_op jit(solution)/shard_map/convert_element_type | solution.py:709
  118.4 3.5 fusion.90.proj
  121.9 7.0 %mixer_forward.2 = (bf16[4,256,256]{2,1,0:T(8,128)(2,1)S(1)}, f32[1024,256]{1,0:T(8,128)S(1)}, bf16[3,1024,256]{2,1,0:T(8,128)(2,1)S(1)}) custom-call(s32[4]{0:T(128)S(1)} %select_reduce_fusion.7.order, s32[3]{0:T(128)S(1)} %get-tuple-element.213.first, s32[3]{0:T(128)S(1)} %get-tuple-element.321.count, f32[4,256,768]{2,1,0:T(8,128)S(1)} %fusion.90.proj, ...), custom_call_target="tpu_custom_call" | custom-call | flops 1024 | bytes 1024 | tf_op jit(solution)/shard_map/mixer_forward/pallas_call | solution.py:556
  129.0 2.3 convolution_convert_fusion.2
  131.4 3.5 fusion.92.proj
  134.8 7.4 %mixer_forward.3 = (bf16[4,256,256]{2,1,0:T(8,128)(2,1)S(1)}, f32[1024,256]{1,0:T(8,128)S(1)}, bf16[3,1024,256]{2,1,0:T(8,128)(2,1)S(1)}) custom-call(s32[4]{0:T(128)S(1)} %select_reduce_fusion.7.order, s32[3]{0:T(128)S(1)} %get-tuple-element.209.first, s32[3]{0:T(128)S(1)} %get-tuple-element.319.count, f32[4,256,768]{2,1,0:T(8,128)S(1)} %fusion.92.proj, ...), custom_call_target="tpu_custom_call" | custom-call | flops 1024 | bytes 1024 | tf_op jit(solution)/shard_map/mixer_forward/pallas_call | solution.py:556
  149.2 10.3 %collective-permute-done.24 = bf16[352,2048]{1,0:T(8,128)(2,1)} collective-permute-done((bf16[352,2048]{1,0:T(8,128)(2,1)}, bf16[352,2048]{1,0:T(8,128)(2,1)}, u32[]{:S(2)}, u32[]{:S(2)}) %collective-permute-start.24) | collective-permute-done | bytes 1441824 | tf_op jit(solution)/shard_map/ppermute | solution.py:64
  167.3 2.4 constant_dynamic-update-slice_fusion.14
  181.4 9.1 %collective-permute-done.25 = bf16[128,2048]{1,0:T(8,128)(2,1)S(1)} collective-permute-done((bf16[128,2048]{1,0:T(8,128)(2,1)S(1)}, bf16[128,2048]{1,0:T(8,128)(2,1)S(1)}, u32[]{:S(2)}, u32[]{:S(2)}) %collective-permute-start.25) | collective-permute-done | bytes 524320 | tf_op jit(solution)/shard_map/ppermute | solution.py:42
  193.5 4.9 collective-permute-done.29
  198.6 22.3 %collective-permute-done.30 = bf16[256,2048]{1,0:T(8,128)(2,1)} collective-permute-done((bf16[256,2048]{1,0:T(8,128)(2,1)}, bf16[256,2048]{1,0:T(8,128)(2,1)}, u32[]{:S(2)}, u32[]{:S(2)}) %collective-permute-start.30) | collective-permute-done | bytes 1048608 | tf_op jit(solution)/shard_map/ppermute | solution.py:64
  233.9 17.9 %collective-permute-done.35 = bf16[256,2048]{1,0:T(8,128)(2,1)S(1)} collective-permute-done((bf16[256,2048]{1,0:T(8,128)(2,1)S(1)}, bf16[256,2048]{1,0:T(8,128)(2,1)S(1)}, u32[]{:S(2)}, u32[]{:S(2)}) %collective-permute-start.35) | collective-permute-done | bytes 1048608 | tf_op jit(solution)/shard_map/ppermute | solution.py:42
  258.6 9.5 %collective-permute-done.36 = bf16[128,2048]{1,0:T(8,128)(2,1)S(1)} collective-permute-done((bf16[128,2048]{1,0:T(8,128)(2,1)S(1)}, bf16[128,2048]{1,0:T(8,128)(2,1)S(1)}, u32[]{:S(2)}, u32[]{:S(2)}) %collective-permute-start.36) | collective-permute-done | bytes 524320 | tf_op jit(solution)/shard_map/ppermute | solution.py:42
  271.5 2.4 collective-permute-done.40
  274.2 8.3 %fusion.94 = f32[704,2048]{1,0:T(8,128)} fusion(bf16[704,2048]{1,0:T(8,128)(2,1)S(1)} %get-tuple-element.281, bf16[2048,2048]{1,0:T(8,128)(2,1)S(1)} %constant_dynamic-update-slice_fusion.2.b), kind=kOutput, calls=%fused_computation.350 | convolution fusion | flops 5905580032 | bytes 17039360 | tf_op jit(solution)/shard_map/dot_general | solution.py:33
  282.4 8.1 %fusion.93 = f32[704,2048]{1,0:T(8,128)} fusion(bf16[704,2048]{1,0:T(8,128)(2,1)S(1)} %get-tuple-element.280, bf16[2048,2048]{1,0:T(8,128)(2,1)S(1)} %constant_dynamic-update-slice_fusion.2.b), kind=kOutput, calls=%fused_computation.349 | convolution fusion | flops 5905580032 | bytes 17039360 | tf_op jit(solution)/shard_map/dot_general | solution.py:33
  290.5 15.5 %multiply_convert_fusion = (bf16[704,2048]{1,0:T(8,128)(2,1)}, bf16[704,2048]{1,0:T(8,128)(2,1)}, bf16[704,2048]{1,0:T(8,128)(2,1)}) fusion(f32[704,2048]{1,0:T(8,128)} %fusion.93, f32[704,2048]{1,0:T(8,128)} %fusion.94, bf16[704,2048]{1,0:T(8,128)(2,1)S(1)} %get-tuple-element.272.b, bf16[2048,2048]{1,0:T(8,128)(2,1)} %constant_dynamic-update-slice_fusion.11.b), kind=kOutput, calls=%fused_computation.11 | convolution fusion | flops 5927206912 | bytes 31457280 | tf_op jit(solution)/shard_map/dot_general | solution.py:33
  306.0 10.5 %product.7 = bf16[704,2048]{1,0:T(8,128)(2,1)} custom-call(bf16[704,2048]{1,0:T(8,128)(2,1)} %get-tuple-element.132.a, bf16[2048,2048]{1,0:T(8,128)(2,1)} %constant_dynamic-update-slice_fusion.11.b), custom_call_target="tpu_custom_call" | custom-call | flops 1024 | bytes 1024 | tf_op jit(solution)/shard_map/product/pallas_call | solution.py:363
  316.5 4.0 fusion.42
  335.4 2.5 convert_add_fusion.4
  338.0 9.8 %collective-permute-done.43 = bf16[128,2048]{1,0:T(8,128)(2,1)S(1)} collective-permute-done((bf16[128,2048]{1,0:T(8,128)(2,1)S(1)}, bf16[128,2048]{1,0:T(8,128)(2,1)S(1)}, u32[]{:S(2)}, u32[]{:S(2)}) %collective-permute-start.43) | collective-permute-done | bytes 524320 | tf_op jit(solution)/shard_map/ppermute | solution.py:42
  354.2 10.3 %product.8 = bf16[704,2048]{1,0:T(8,128)(2,1)} custom-call(bf16[704,2048]{1,0:T(8,128)(2,1)} %get-tuple-element.130.a, bf16[2048,2048]{1,0:T(8,128)(2,1)} %copy-done.28), custom_call_target="tpu_custom_call" | custom-call | flops 1024 | bytes 1024 | tf_op jit(solution)/shard_map/product/pallas_call | solution.py:363
  364.5 10.3 %product.9 = bf16[704,2048]{1,0:T(8,128)(2,1)} custom-call(bf16[704,2048]{1,0:T(8,128)(2,1)} %get-tuple-element.131.a, bf16[2048,2048]{1,0:T(8,128)(2,1)} %copy-done.28), custom_call_target="tpu_custom_call" | custom-call | flops 1024 | bytes 1024 | tf_op jit(solution)/shard_map/product/pallas_call | solution.py:363
  376.1 4.3 multiply_reduce_fusion.4
  380.5 4.3 fusion.75
  390.7 5.6 product.13
  396.3 5.6 product.12
  401.9 5.7 product.11
  407.6 5.6 product.10
  421.4 15.7 %collective-permute-done.66 = bf16[240,2048]{1,0:T(8,128)(2,1)} collective-permute-done((bf16[240,2048]{1,0:T(8,128)(2,1)}, bf16[240,2048]{1,0:T(8,128)(2,1)}, u32[]{:S(2)}, u32[]{:S(2)}) %collective-permute-start.66) | collective-permute-done | bytes 983072 | tf_op jit(solution)/shard_map/ppermute | solution.py:64
  451.1 3.0 pad_maximum_fusion.11
  454.8 5.1 fusion.21
  459.9 16.0 %mixer_backward.2 = (bf16[4,256,768]{2,1,0:T(8,128)(2,1)}, f32[512,256]{1,0:T(8,128)S(1)}, f32[8,768]{1,0:T(8,128)S(1)}) custom-call(s32[4]{0:T(128)S(1)} %select_reduce_fusion.7.order, s32[3]{0:T(128)S(1)} %copy-done.17, s32[3]{0:T(128)S(1)} %copy-done.19, f32[4,256,768]{2,1,0:T(8,128)} %copy-done.4, f32[4,256,256]{2,1,0:T(8,128)S(1)} %bitcast.197, ...), custom_call_target="tpu_custom_call" | custom-call | flops 1024 | bytes 1024 | tf_op jit(solution)/shard_map/mixer_backward/pallas_call | solution.py:582
  489.7 4.3 fusion.7
  495.0 5.2 collective-permute-done.54
  505.6 4.5 convert_add_fusion.1
  510.1 16.1 %mixer_backward.3 = (bf16[4,256,768]{2,1,0:T(8,128)(2,1)}, f32[512,256]{1,0:T(8,128)S(1)}, f32[8,768]{1,0:T(8,128)S(1)}) custom-call(s32[4]{0:T(128)S(1)} %select_reduce_fusion.7.order, s32[3]{0:T(128)S(1)} %get-tuple-element.209.first, s32[3]{0:T(128)S(1)} %get-tuple-element.319.count, f32[4,256,768]{2,1,0:T(8,128)} %copy-done.3, ...), custom_call_target="tpu_custom_call" | custom-call | flops 1024 | bytes 1024 | tf_op jit(solution)/shard_map/mixer_backward/pallas_call | solution.py:582
  530.3 4.1 convolution_convert_fusion.5
  534.5 3.5 fusion.97
  538.0 3.7 add_convert_fusion
  541.7 3.7 collective-permute-done.68
  550.3 3.4 fusion.23
  553.7 4.7 add_bitcast_fusion
  558.4 3.9 convert_add_fusion
  567.8 4.0 collective-permute-done.70
  571.8 4.0 collective-permute-done.61
  592.1 7.9 %moments.1 = (f32[16,8,256]{2,1,0:T(8,128)}, f32[16,8,256]{2,1,0:T(8,128)}, f32[16,8,256]{2,1,0:T(8,128)}, f32[16,8,256]{2,1,0:T(8,128)}) custom-call(f32[512,256]{1,0:T(8,128)} %add.367.grad, f32[16,8,256]{2,1,0:T(8,128)} %broadcast_in_dim.201.step_re, f32[16,8,256]{2,1,0:T(8,128)} %broadcast_in_dim.202.step_im), custom_call_target="tpu_custom_call" | custom-call | flops 31457280 | bytes 524288 | tf_op jit(solution)/shard_map/moments/pallas_call | solution.py:378
  602.7 8.3 %collective-permute-done.74 = f32[2,4,2,64]{3,1,2,0:T(4,128)S(1)} collective-permute-done((f32[2,4,2,64]{3,1,2,0:T(4,128)S(1)}, f32[2,4,2,64]{3,1,2,0:T(4,128)S(1)}, u32[]{:S(2)}, u32[]{:S(2)}) %collective-permute-start.74) | collective-permute-done | bytes 4128 | tf_op jit(solution)/shard_map/ppermute | solution.py:42
  620.4 2.7 fusion.8
  623.2 3.7 fusion.24
  626.9 12.8 %collective-permute-done.76 = bf16[77,64]{1,0:T(8,128)(2,1)S(1)} collective-permute-done((bf16[77,64]{1,0:T(8,128)(2,1)S(1)}, bf16[77,64]{1,0:T(8,128)(2,1)S(1)}, u32[]{:S(2)}, u32[]{:S(2)}) %collective-permute-start.76) | collective-permute-done | bytes 9888 | tf_op jit(solution)/shard_map/ppermute | solution.py:64
  643.4 3.0 fusion.22
  (583 shorter events, 228.2 us)
Async XLA Ops:
  4.6 24.2 %collective-permute-start = (bf16[75,64]{1,0:T(8,128)(2,1)S(1)}, bf16[75,64]{1,0:T(8,128)(2,1)S(1)}, u32[]{:S(2)}, u32[]{:S(2)}) collective-permute-start(bf16[75,64]{1,0:T(8,128)(2,1)S(1)} %concatenate.233), channel_id=1, source_target_pairs={{0,16},{4,20},{16,24},{20,28},{24,8},{28,12},{8,0},{12,4},{1,17},{... | collective-permute-start | bytes 28808 | tf_op jit(solution)/shard_map/ppermute | solution.py:64
  8.7 20.1 %collective-permute-start.1 = (bf16[75,64]{1,0:T(8,128)(2,1)S(1)}, bf16[75,64]{1,0:T(8,128)(2,1)S(1)}, u32[]{:S(2)}, u32[]{:S(2)}) collective-permute-start(bf16[75,64]{1,0:T(8,128)(2,1)S(1)} %concatenate.233), channel_id=1, source_target_pairs={{0,8},{4,12},{16,0},{20,4},{24,16},{28,20},{8,24},{12,28},{1,9},{5... | collective-permute-start | bytes 28808 | tf_op jit(solution)/shard_map/ppermute | solution.py:64
  8.7 20.1 %collective-permute-start.2 = (bf16[75,64]{1,0:T(8,128)(2,1)S(1)}, bf16[75,64]{1,0:T(8,128)(2,1)S(1)}, u32[]{:S(2)}, u32[]{:S(2)}) collective-permute-start(bf16[75,64]{1,0:T(8,128)(2,1)S(1)} %concatenate.233), channel_id=1, source_target_pairs={{0,24},{4,28},{16,8},{20,12},{24,0},{28,4},{8,16},{12,20},{1,25},{... | collective-permute-start | bytes 28808 | tf_op jit(solution)/shard_map/ppermute | solution.py:64
  14.0 48.9 %collective-permute-start.12 = (bf16[256,2048]{1,0:T(8,128)(2,1)}, bf16[256,2048]{1,0:T(8,128)(2,1)}, u32[]{:S(2)}, u32[]{:S(2)}) collective-permute-start(bf16[256,2048]{1,0:T(8,128)(2,1)} %pad_maximum_fusion.17), channel_id=1, source_target_pairs={{0,16},{4,20},{16,24},{20,28},{24,8},{28,12},{8,0},{12,4},{1,17},{... | collective-permute-start | bytes 3145736 | tf_op jit(solution)/shard_map/ppermute | solution.py:64
  14.4 50.6 %collective-permute-start.13 = (bf16[256,2048]{1,0:T(8,128)(2,1)}, bf16[256,2048]{1,0:T(8,128)(2,1)}, u32[]{:S(2)}, u32[]{:S(2)}) collective-permute-start(bf16[256,2048]{1,0:T(8,128)(2,1)} %pad_maximum_fusion.17), channel_id=1, source_target_pairs={{0,8},{4,12},{16,0},{20,4},{24,16},{28,20},{8,24},{12,28},{1,9},{5... | collective-permute-start | bytes 3145736 | tf_op jit(solution)/shard_map/ppermute | solution.py:64
  28.8 40.3 %collective-permute-start.8 = (bf16[256,2048]{1,0:T(8,128)(2,1)S(1)}, bf16[256,2048]{1,0:T(8,128)(2,1)}, u32[]{:S(2)}, u32[]{:S(2)}) collective-permute-start(bf16[256,2048]{1,0:T(8,128)(2,1)S(1)} %bitcast.204), channel_id=1, source_target_pairs={{0,4},{4,0},{8,12},{12,8},{16,20},{20,16},{24,28},{28,24},{1,5},{5... | collective-permute-start | bytes 3145736 | tf_op jit(solution)/shard_map/ppermute | solution.py:42
  30.4 41.3 %collective-permute-start.3 = (bf16[256,2048]{1,0:T(8,128)(2,1)S(1)}, bf16[256,2048]{1,0:T(8,128)(2,1)}, u32[]{:S(2)}, u32[]{:S(2)}) collective-permute-start(bf16[256,2048]{1,0:T(8,128)(2,1)S(1)} %bitcast.205), channel_id=1, source_target_pairs={{0,2},{1,3},{2,0},{3,1},{4,6},{5,7},{6,4},{7,5},{8,10},{9,11},{10,... | collective-permute-start | bytes 3145736 | tf_op jit(solution)/shard_map/ppermute | solution.py:42
  32.2 20.3 %collective-permute-start.16 = (s32[2,3]{1,0:T(2,128)S(1)}, s32[2,3]{1,0:T(2,128)S(1)}, u32[]{:S(2)}, u32[]{:S(2)}) collective-permute-start(s32[2,3]{1,0:T(2,128)S(1)} %pad_add_fusion), channel_id=1, source_target_pairs={{0,4},{4,0},{8,12},{12,8},{16,20},{20,16},{24,28},{28,24},{1,5},{5... | collective-permute-start | bytes 80 | tf_op jit(solution)/shard_map/ppermute | solution.py:42
  67.0 24.6 %collective-permute-start.14 = (bf16[128,2048]{1,0:T(8,128)(2,1)S(1)}, bf16[128,2048]{1,0:T(8,128)(2,1)S(1)}, u32[]{:S(2)}, u32[]{:S(2)}) collective-permute-start(bf16[128,2048]{1,0:T(8,128)(2,1)S(1)} %pad_maximum_fusion.33), channel_id=1, source_target_pairs={{0,16},{4,20},{16,24},{20,28},{24,8},{28,12},{8,0},{12,4},{1,17},{... | collective-permute-start | bytes 1572872 | tf_op jit(solution)/shard_map/ppermute | solution.py:64
  68.3 26.0 %collective-permute-start.15 = (bf16[128,2048]{1,0:T(8,128)(2,1)S(1)}, bf16[128,2048]{1,0:T(8,128)(2,1)S(1)}, u32[]{:S(2)}, u32[]{:S(2)}) collective-permute-start(bf16[128,2048]{1,0:T(8,128)(2,1)S(1)} %pad_maximum_fusion.34), channel_id=1, source_target_pairs={{0,8},{4,12},{16,0},{20,4},{24,16},{28,20},{8,24},{12,28},{1,9},{5... | collective-permute-start | bytes 1572872 | tf_op jit(solution)/shard_map/ppermute | solution.py:64
  77.0 20.2 %collective-permute-start.4 = (bf16[512,2048]{1,0:T(8,128)(2,1)S(1)}, bf16[512,2048]{1,0:T(8,128)(2,1)S(1)}, u32[]{:S(2)}, u32[]{:S(2)}) collective-permute-start(bf16[512,2048]{1,0:T(8,128)(2,1)S(1)} %pad_maximum_fusion.4), channel_id=1, source_target_pairs={{0,1},{1,0},{2,3},{3,2},{4,5},{5,4},{6,7},{7,6},{8,9},{9,8},{10,11... | collective-permute-start | bytes 6291464 | tf_op jit(solution)/shard_map/ppermute | solution.py:42
  94.3 54.8 %collective-permute-start.23 = (bf16[352,2048]{1,0:T(8,128)(2,1)}, bf16[352,2048]{1,0:T(8,128)(2,1)}, u32[]{:S(2)}, u32[]{:S(2)}) collective-permute-start(bf16[352,2048]{1,0:T(8,128)(2,1)} %pad_maximum_fusion.14), channel_id=1, source_target_pairs={{0,16},{4,20},{16,24},{20,28},{24,8},{28,12},{8,0},{12,4},{1,17},{... | collective-permute-start | bytes 4325384 | tf_op jit(solution)/shard_map/ppermute | solution.py:64
  94.9 64.6 %collective-permute-start.24 = (bf16[352,2048]{1,0:T(8,128)(2,1)}, bf16[352,2048]{1,0:T(8,128)(2,1)}, u32[]{:S(2)}, u32[]{:S(2)}) collective-permute-start(bf16[352,2048]{1,0:T(8,128)(2,1)} %pad_maximum_fusion.14), channel_id=1, source_target_pairs={{0,8},{4,12},{16,0},{20,4},{24,16},{28,20},{8,24},{12,28},{1,9},{5... | collective-permute-start | bytes 4325384 | tf_op jit(solution)/shard_map/ppermute | solution.py:64
  100.2 43.4 %collective-permute-start.17 = (bf16[256,2048]{1,0:T(8,128)(2,1)S(1)}, bf16[256,2048]{1,0:T(8,128)(2,1)}, u32[]{:S(2)}, u32[]{:S(2)}) collective-permute-start(bf16[256,2048]{1,0:T(8,128)(2,1)S(1)} %bitcast.216), channel_id=1, source_target_pairs={{0,2},{1,3},{2,0},{3,1},{4,6},{5,7},{6,4},{7,5},{8,10},{9,11},{10,... | collective-permute-start | bytes 3145736 | tf_op jit(solution)/shard_map/ppermute | solution.py:42
  101.7 43.5 %collective-permute-start.18 = (bf16[256,2048]{1,0:T(8,128)(2,1)S(1)}, bf16[256,2048]{1,0:T(8,128)(2,1)}, u32[]{:S(2)}, u32[]{:S(2)}) collective-permute-start(bf16[256,2048]{1,0:T(8,128)(2,1)S(1)} %bitcast.217), channel_id=1, source_target_pairs={{0,4},{4,0},{8,12},{12,8},{16,20},{20,16},{24,28},{28,24},{1,5},{5... | collective-permute-start | bytes 3145736 | tf_op jit(solution)/shard_map/ppermute | solution.py:42
  131.3 46.1 %collective-permute-start.19 = (bf16[512,2048]{1,0:T(8,128)(2,1)}, bf16[512,2048]{1,0:T(8,128)(2,1)}, u32[]{:S(2)}, u32[]{:S(2)}) collective-permute-start(bf16[512,2048]{1,0:T(8,128)(2,1)} %convolution_convert_fusion.2), channel_id=1, source_target_pairs={{0,1},{1,0},{2,3},{3,2},{4,5},{5,4},{6,7},{7,6},{8,9},{9,8},{10,11... | collective-permute-start | bytes 6291464 | tf_op jit(solution)/shard_map/ppermute | solution.py:42
  144.6 26.5 %collective-permute-start.21 = (bf16[128,2048]{1,0:T(8,128)(2,1)S(1)}, bf16[128,2048]{1,0:T(8,128)(2,1)S(1)}, u32[]{:S(2)}, u32[]{:S(2)}) collective-permute-start(bf16[128,2048]{1,0:T(8,128)(2,1)S(1)} %slice.828), channel_id=1, source_target_pairs={{0,4},{4,0},{8,12},{12,8},{16,20},{20,16},{24,28},{28,24},{1,5},{5... | collective-permute-start | bytes 1572872 | tf_op jit(solution)/shard_map/ppermute | solution.py:42
  146.3 25.5 %collective-permute-start.22 = (bf16[128,2048]{1,0:T(8,128)(2,1)S(1)}, bf16[128,2048]{1,0:T(8,128)(2,1)S(1)}, u32[]{:S(2)}, u32[]{:S(2)}) collective-permute-start(bf16[128,2048]{1,0:T(8,128)(2,1)S(1)} %slice.829), channel_id=1, source_target_pairs={{0,2},{1,3},{2,0},{3,1},{4,6},{5,7},{6,4},{7,5},{8,10},{9,11},{10,... | collective-permute-start | bytes 1572872 | tf_op jit(solution)/shard_map/ppermute | solution.py:42
  149.1 49.4 %collective-permute-start.33 = (bf16[512,2048]{1,0:T(8,128)(2,1)S(1)}, bf16[512,2048]{1,0:T(8,128)(2,1)S(1)}, u32[]{:S(2)}, u32[]{:S(2)}) collective-permute-start(bf16[512,2048]{1,0:T(8,128)(2,1)S(1)} %pad_maximum_fusion.6), channel_id=1, source_target_pairs={{0,1},{1,0},{2,3},{3,2},{4,5},{5,4},{6,7},{7,6},{8,9},{9,8},{10,11... | collective-permute-start | bytes 6291464 | tf_op jit(solution)/shard_map/ppermute | solution.py:42
  159.5 15.2 %collective-permute-start.20 = (bf16[512,2048]{1,0:T(8,128)(2,1)S(1)}, bf16[512,2048]{1,0:T(8,128)(2,1)S(1)}, u32[]{:S(2)}, u32[]{:S(2)}) collective-permute-start(bf16[512,2048]{1,0:T(8,128)(2,1)S(1)} %convolution_convert_fusion), channel_id=1, source_target_pairs={{0,1},{1,0},{2,3},{3,2},{4,5},{5,4},{6,7},{7,6},{8,9},{9,8},{10,11... | collective-permute-start | bytes 6291464 | tf_op jit(solution)/shard_map/ppermute | solution.py:42
  171.1 27.3 %collective-permute-start.29 = (bf16[272,2048]{1,0:T(8,128)(2,1)S(1)}, bf16[272,2048]{1,0:T(8,128)(2,1)S(1)}, u32[]{:S(2)}, u32[]{:S(2)}) collective-permute-start(bf16[272,2048]{1,0:T(8,128)(2,1)S(1)} %pad_maximum_fusion.16), channel_id=1, source_target_pairs={{0,16},{4,20},{16,24},{20,28},{24,8},{28,12},{8,0},{12,4},{1,17},{... | collective-permute-start | bytes 3342344 | tf_op jit(solution)/shard_map/ppermute | solution.py:64
  171.8 49.2 %collective-permute-start.30 = (bf16[256,2048]{1,0:T(8,128)(2,1)}, bf16[256,2048]{1,0:T(8,128)(2,1)}, u32[]{:S(2)}, u32[]{:S(2)}) collective-permute-start(bf16[256,2048]{1,0:T(8,128)(2,1)} %pad_maximum_fusion.20), channel_id=1, source_target_pairs={{0,8},{4,12},{16,0},{20,4},{24,16},{28,20},{8,24},{12,28},{1,9},{5... | collective-permute-start | bytes 3145736 | tf_op jit(solution)/shard_map/ppermute | solution.py:64
  175.9 14.8 %collective-permute-start.26 = (bf16[128,2048]{1,0:T(8,128)(2,1)S(1)}, bf16[128,2048]{1,0:T(8,128)(2,1)S(1)}, u32[]{:S(2)}, u32[]{:S(2)}) collective-permute-start(bf16[128,2048]{1,0:T(8,128)(2,1)S(1)} %get-tuple-element.274), channel_id=1, source_target_pairs={{0,2},{1,3},{2,0},{3,1},{4,6},{5,7},{6,4},{7,5},{8,10},{9,11},{10,... | collective-permute-start | bytes 1572872 | tf_op jit(solution)/shard_map/ppermute | solution.py:42
  191.0 35.2 %collective-permute-start.27 = (bf16[256,2048]{1,0:T(8,128)(2,1)S(1)}, bf16[256,2048]{1,0:T(8,128)(2,1)S(1)}, u32[]{:S(2)}, u32[]{:S(2)}) collective-permute-start(bf16[256,2048]{1,0:T(8,128)(2,1)S(1)} %pad_maximum_fusion.18), channel_id=1, source_target_pairs={{0,2},{1,3},{2,0},{3,1},{4,6},{5,7},{6,4},{7,5},{8,10},{9,11},{10,... | collective-permute-start | bytes 3145736 | tf_op jit(solution)/shard_map/ppermute | solution.py:42
  192.0 34.1 %collective-permute-start.28 = (bf16[256,2048]{1,0:T(8,128)(2,1)S(1)}, bf16[256,2048]{1,0:T(8,128)(2,1)S(1)}, u32[]{:S(2)}, u32[]{:S(2)}) collective-permute-start(bf16[256,2048]{1,0:T(8,128)(2,1)S(1)} %pad_maximum_fusion.19), channel_id=1, source_target_pairs={{0,4},{4,0},{8,12},{12,8},{16,20},{20,16},{24,28},{28,24},{1,5},{5... | collective-permute-start | bytes 3145736 | tf_op jit(solution)/shard_map/ppermute | solution.py:42
  198.5 28.7 %collective-permute-start.34 = (bf16[512,2048]{1,0:T(8,128)(2,1)S(1)}, bf16[512,2048]{1,0:T(8,128)(2,1)S(1)}, u32[]{:S(2)}, u32[]{:S(2)}) collective-permute-start(bf16[512,2048]{1,0:T(8,128)(2,1)S(1)} %pad_maximum_fusion.7), channel_id=1, source_target_pairs={{0,1},{1,0},{2,3},{3,2},{4,5},{5,4},{6,7},{7,6},{8,9},{9,8},{10,11... | collective-permute-start | bytes 6291464 | tf_op jit(solution)/shard_map/ppermute | solution.py:42
  224.1 45.8 %collective-permute-start.31 = (bf16[192,2048]{1,0:T(8,128)(2,1)}, bf16[192,2048]{1,0:T(8,128)(2,1)S(1)}, u32[]{:S(2)}, u32[]{:S(2)}) collective-permute-start(bf16[192,2048]{1,0:T(8,128)(2,1)} %pad_maximum_fusion.31), channel_id=1, source_target_pairs={{0,16},{4,20},{16,24},{20,28},{24,8},{28,12},{8,0},{12,4},{1,17},{... | collective-permute-start | bytes 2359304 | tf_op jit(solution)/shard_map/ppermute | solution.py:64
  224.7 45.1 %collective-permute-start.32 = (bf16[160,2048]{1,0:T(8,128)(2,1)}, bf16[160,2048]{1,0:T(8,128)(2,1)}, u32[]{:S(2)}, u32[]{:S(2)}) collective-permute-start(bf16[160,2048]{1,0:T(8,128)(2,1)} %pad_maximum_fusion.32), channel_id=1, source_target_pairs={{0,8},{4,12},{16,0},{20,4},{24,16},{28,20},{8,24},{12,28},{1,9},{5... | collective-permute-start | bytes 1966088 | tf_op jit(solution)/shard_map/ppermute | solution.py:64
  227.2 24.6 %collective-permute-start.35 = (bf16[256,2048]{1,0:T(8,128)(2,1)S(1)}, bf16[256,2048]{1,0:T(8,128)(2,1)S(1)}, u32[]{:S(2)}, u32[]{:S(2)}) collective-permute-start(bf16[256,2048]{1,0:T(8,128)(2,1)S(1)} %multiply_convert_fusion.3), channel_id=1, source_target_pairs={{0,2},{1,3},{2,0},{3,1},{4,6},{5,7},{6,4},{7,5},{8,10},{9,11},{10,... | collective-permute-start | bytes 3145736 | tf_op jit(solution)/shard_map/ppermute | solution.py:42
  229.5 25.7 %collective-permute-start.37 = (bf16[256,2048]{1,0:T(8,128)(2,1)S(1)}, bf16[256,2048]{1,0:T(8,128)(2,1)S(1)}, u32[]{:S(2)}, u32[]{:S(2)}) collective-permute-start(bf16[256,2048]{1,0:T(8,128)(2,1)S(1)} %multiply_convert_fusion.3), channel_id=1, source_target_pairs={{0,4},{4,0},{8,12},{12,8},{16,20},{20,16},{24,28},{28,24},{1,5},{5... | collective-permute-start | bytes 3145736 | tf_op jit(solution)/shard_map/ppermute | solution.py:42
  252.0 19.1 %collective-permute-start.39 = (bf16[512,2048]{1,0:T(8,128)(2,1)S(1)}, bf16[512,2048]{1,0:T(8,128)(2,1)S(1)}, u32[]{:S(2)}, u32[]{:S(2)}) collective-permute-start(bf16[512,2048]{1,0:T(8,128)(2,1)S(1)} %pad_maximum_fusion.8), channel_id=1, source_target_pairs={{0,1},{1,0},{2,3},{3,2},{4,5},{5,4},{6,7},{7,6},{8,9},{9,8},{10,11... | collective-permute-start | bytes 6291464 | tf_op jit(solution)/shard_map/ppermute | solution.py:42
  253.7 14.4 %collective-permute-start.36 = (bf16[128,2048]{1,0:T(8,128)(2,1)S(1)}, bf16[128,2048]{1,0:T(8,128)(2,1)S(1)}, u32[]{:S(2)}, u32[]{:S(2)}) collective-permute-start(bf16[128,2048]{1,0:T(8,128)(2,1)S(1)} %slice.836), channel_id=1, source_target_pairs={{0,4},{4,0},{8,12},{12,8},{16,20},{20,16},{24,28},{28,24},{1,5},{5... | collective-permute-start | bytes 1572872 | tf_op jit(solution)/shard_map/ppermute | solution.py:42
  255.3 14.1 %collective-permute-start.38 = (bf16[128,2048]{1,0:T(8,128)(2,1)S(1)}, bf16[128,2048]{1,0:T(8,128)(2,1)S(1)}, u32[]{:S(2)}, u32[]{:S(2)}) collective-permute-start(bf16[128,2048]{1,0:T(8,128)(2,1)S(1)} %slice.837), channel_id=1, source_target_pairs={{0,2},{1,3},{2,0},{3,1},{4,6},{5,7},{6,4},{7,5},{8,10},{9,11},{10,... | collective-permute-start | bytes 1572872 | tf_op jit(solution)/shard_map/ppermute | solution.py:42
  333.4 15.7 %collective-permute-start.42 = (bf16[128,2048]{1,0:T(8,128)(2,1)S(1)}, bf16[128,2048]{1,0:T(8,128)(2,1)S(1)}, u32[]{:S(2)}, u32[]{:S(2)}) collective-permute-start(bf16[128,2048]{1,0:T(8,128)(2,1)S(1)} %get-tuple-element.253), channel_id=1, source_target_pairs={{0,4},{4,0},{8,12},{12,8},{16,20},{20,16},{24,28},{28,24},{1,5},{5... | collective-permute-start | bytes 1572872 | tf_op jit(solution)/shard_map/ppermute | solution.py:42
  333.9 13.9 %collective-permute-start.43 = (bf16[128,2048]{1,0:T(8,128)(2,1)S(1)}, bf16[128,2048]{1,0:T(8,128)(2,1)S(1)}, u32[]{:S(2)}, u32[]{:S(2)}) collective-permute-start(bf16[128,2048]{1,0:T(8,128)(2,1)S(1)} %get-tuple-element.252), channel_id=1, source_target_pairs={{0,2},{1,3},{2,0},{3,1},{4,6},{5,7},{6,4},{7,5},{8,10},{9,11},{10,... | collective-permute-start | bytes 1572872 | tf_op jit(solution)/shard_map/ppermute | solution.py:42
  350.3 24.6 %collective-permute-start.45 = (bf16[256,2048]{1,0:T(8,128)(2,1)}, bf16[256,2048]{1,0:T(8,128)(2,1)}, u32[]{:S(2)}, u32[]{:S(2)}) collective-permute-start(bf16[256,2048]{1,0:T(8,128)(2,1)} %pad_maximum_fusion.21), channel_id=1, source_target_pairs={{0,2},{1,3},{2,0},{3,1},{4,6},{5,7},{6,4},{7,5},{8,10},{9,11},{10,... | collective-permute-start | bytes 3145736 | tf_op jit(solution)/shard_map/ppermute | solution.py:42
  351.8 24.3 %collective-permute-start.46 = (bf16[256,2048]{1,0:T(8,128)(2,1)}, bf16[256,2048]{1,0:T(8,128)(2,1)}, u32[]{:S(2)}, u32[]{:S(2)}) collective-permute-start(bf16[256,2048]{1,0:T(8,128)(2,1)} %pad_maximum_fusion.22), channel_id=1, source_target_pairs={{0,4},{4,0},{8,12},{12,8},{16,20},{20,16},{24,28},{28,24},{1,5},{5... | collective-permute-start | bytes 3145736 | tf_op jit(solution)/shard_map/ppermute | solution.py:42
  384.9 28.3 %collective-permute-start.47 = (bf16[256,2048]{1,0:T(8,128)(2,1)}, bf16[256,2048]{1,0:T(8,128)(2,1)}, u32[]{:S(2)}, u32[]{:S(2)}) collective-permute-start(bf16[256,2048]{1,0:T(8,128)(2,1)} %get-tuple-element.205), channel_id=1, source_target_pairs={{0,2},{1,3},{2,0},{3,1},{4,6},{5,7},{6,4},{7,5},{8,10},{9,11},{10,... | collective-permute-start | bytes 3145736 | tf_op jit(solution)/shard_map/ppermute | solution.py:42
  385.3 30.0 %collective-permute-start.49 = (bf16[256,2048]{1,0:T(8,128)(2,1)}, bf16[256,2048]{1,0:T(8,128)(2,1)}, u32[]{:S(2)}, u32[]{:S(2)}) collective-permute-start(bf16[256,2048]{1,0:T(8,128)(2,1)} %get-tuple-element.205), channel_id=1, source_target_pairs={{0,4},{4,0},{8,12},{12,8},{16,20},{20,16},{24,28},{28,24},{1,5},{5... | collective-permute-start | bytes 3145736 | tf_op jit(solution)/shard_map/ppermute | solution.py:42
  388.5 48.6 %collective-permute-start.65 = (bf16[288,2048]{1,0:T(8,128)(2,1)}, bf16[288,2048]{1,0:T(8,128)(2,1)}, u32[]{:S(2)}, u32[]{:S(2)}) collective-permute-start(bf16[288,2048]{1,0:T(8,128)(2,1)} %pad_maximum_fusion.15), channel_id=1, source_target_pairs={{0,16},{4,20},{16,24},{20,28},{24,8},{28,12},{8,0},{12,4},{1,17},{... | collective-permute-start | bytes 3538952 | tf_op jit(solution)/shard_map/ppermute | solution.py:64
  389.7 47.3 %collective-permute-start.66 = (bf16[240,2048]{1,0:T(8,128)(2,1)}, bf16[240,2048]{1,0:T(8,128)(2,1)}, u32[]{:S(2)}, u32[]{:S(2)}) collective-permute-start(bf16[240,2048]{1,0:T(8,128)(2,1)} %pad_maximum_fusion.29), channel_id=1, source_target_pairs={{0,8},{4,12},{16,0},{20,4},{24,16},{28,20},{8,24},{12,28},{1,9},{5... | collective-permute-start | bytes 2949128 | tf_op jit(solution)/shard_map/ppermute | solution.py:64
  414.2 22.9 %collective-permute-start.48 = (bf16[128,2048]{1,0:T(8,128)(2,1)S(1)}, bf16[128,2048]{1,0:T(8,128)(2,1)S(1)}, u32[]{:S(2)}, u32[]{:S(2)}) collective-permute-start(bf16[128,2048]{1,0:T(8,128)(2,1)S(1)} %slice.849), channel_id=1, source_target_pairs={{0,4},{4,0},{8,12},{12,8},{16,20},{20,16},{24,28},{28,24},{1,5},{5... | collective-permute-start | bytes 1572872 | tf_op jit(solution)/shard_map/ppermute | solution.py:42
  416.4 20.6 %collective-permute-start.50 = (bf16[128,2048]{1,0:T(8,128)(2,1)S(1)}, bf16[128,2048]{1,0:T(8,128)(2,1)S(1)}, u32[]{:S(2)}, u32[]{:S(2)}) collective-permute-start(bf16[128,2048]{1,0:T(8,128)(2,1)S(1)} %slice.850), channel_id=1, source_target_pairs={{0,2},{1,3},{2,0},{3,1},{4,6},{5,7},{6,4},{7,5},{8,10},{9,11},{10,... | collective-permute-start | bytes 1572872 | tf_op jit(solution)/shard_map/ppermute | solution.py:42
  419.8 34.4 %collective-permute-start.57 = (bf16[512,2048]{1,0:T(8,128)(2,1)S(1)}, bf16[512,2048]{1,0:T(8,128)(2,1)S(1)}, u32[]{:S(2)}, u32[]{:S(2)}) collective-permute-start(bf16[512,2048]{1,0:T(8,128)(2,1)S(1)} %pad_maximum_fusion.10), channel_id=1, source_target_pairs={{0,1},{1,0},{2,3},{3,2},{4,5},{5,4},{6,7},{7,6},{8,9},{9,8},{10,11... | collective-permute-start | bytes 6291464 | tf_op jit(solution)/shard_map/ppermute | solution.py:42
  439.0 41.3 %collective-permute-start.52 = (bf16[512,2048]{1,0:T(8,128)(2,1)S(1)}, bf16[512,2048]{1,0:T(8,128)(2,1)S(1)}, u32[]{:S(2)}, u32[]{:S(2)}) collective-permute-start(bf16[512,2048]{1,0:T(8,128)(2,1)S(1)} %copy-done.71), channel_id=1, source_target_pairs={{0,1},{1,0},{2,3},{3,2},{4,5},{5,4},{6,7},{7,6},{8,9},{9,8},{10,11... | collective-permute-start | bytes 6291464 | tf_op jit(solution)/shard_map/ppermute | solution.py:42
  449.0 92.7 %collective-permute-start.67 = (bf16[528,2048]{1,0:T(8,128)(2,1)}, bf16[528,2048]{1,0:T(8,128)(2,1)}, u32[]{:S(2)}, u32[]{:S(2)}) collective-permute-start(bf16[528,2048]{1,0:T(8,128)(2,1)} %get-tuple-element.158), channel_id=1, source_target_pairs={{0,16},{4,20},{16,24},{20,28},{24,8},{28,12},{8,0},{12,4},{1,17},{... | collective-permute-start | bytes 6488072 | tf_op jit(solution)/shard_map/ppermute | solution.py:64
  449.6 95.8 %collective-permute-start.68 = (bf16[528,2048]{1,0:T(8,128)(2,1)}, bf16[528,2048]{1,0:T(8,128)(2,1)}, u32[]{:S(2)}, u32[]{:S(2)}) collective-permute-start(bf16[528,2048]{1,0:T(8,128)(2,1)} %get-tuple-element.159), channel_id=1, source_target_pairs={{0,8},{4,12},{16,0},{20,4},{24,16},{28,20},{8,24},{12,28},{1,9},{5... | collective-permute-start | bytes 6488072 | tf_op jit(solution)/shard_map/ppermute | solution.py:64
  454.0 28.1 %collective-permute-start.59 = (bf16[512,2048]{1,0:T(8,128)(2,1)}, bf16[512,2048]{1,0:T(8,128)(2,1)}, u32[]{:S(2)}, u32[]{:S(2)}) collective-permute-start(bf16[512,2048]{1,0:T(8,128)(2,1)} %pad_maximum_fusion.11), channel_id=1, source_target_pairs={{0,1},{1,0},{2,3},{3,2},{4,5},{5,4},{6,7},{7,6},{8,9},{9,8},{10,11... | collective-permute-start | bytes 6291464 | tf_op jit(solution)/shard_map/ppermute | solution.py:42
  454.2 32.2 %collective-permute-start.51 = (bf16[512,2048]{1,0:T(8,128)(2,1)}, bf16[512,2048]{1,0:T(8,128)(2,1)}, u32[]{:S(2)}, u32[]{:S(2)}) collective-permute-start(bf16[512,2048]{1,0:T(8,128)(2,1)} %product.11), channel_id=1, source_target_pairs={{0,1},{1,0},{2,3},{3,2},{4,5},{5,4},{6,7},{7,6},{8,9},{9,8},{10,11... | collective-permute-start | bytes 6291464 | tf_op jit(solution)/shard_map/ppermute | solution.py:42
  480.3 25.3 %collective-permute-start.58 = (bf16[512,2048]{1,0:T(8,128)(2,1)S(1)}, bf16[512,2048]{1,0:T(8,128)(2,1)S(1)}, u32[]{:S(2)}, u32[]{:S(2)}) collective-permute-start(bf16[512,2048]{1,0:T(8,128)(2,1)S(1)} %convolution_convert_fusion.6), channel_id=1, source_target_pairs={{0,1},{1,0},{2,3},{3,2},{4,5},{5,4},{6,7},{7,6},{8,9},{9,8},{10,11... | collective-permute-start | bytes 6291464 | tf_op jit(solution)/shard_map/ppermute | solution.py:42
  482.1 19.3 %collective-permute-start.53 = (bf16[128,2048]{1,0:T(8,128)(2,1)S(1)}, bf16[128,2048]{1,0:T(8,128)(2,1)S(1)}, u32[]{:S(2)}, u32[]{:S(2)}) collective-permute-start(bf16[128,2048]{1,0:T(8,128)(2,1)S(1)} %get-tuple-element.250), channel_id=1, source_target_pairs={{0,4},{4,0},{8,12},{12,8},{16,20},{20,16},{24,28},{28,24},{1,5},{5... | collective-permute-start | bytes 1572872 | tf_op jit(solution)/shard_map/ppermute | solution.py:42
  502.6 27.7 %collective-permute-start.55 = (bf16[256,2048]{1,0:T(8,128)(2,1)}, bf16[256,2048]{1,0:T(8,128)(2,1)}, u32[]{:S(2)}, u32[]{:S(2)}) collective-permute-start(bf16[256,2048]{1,0:T(8,128)(2,1)} %pad_maximum_fusion.23), channel_id=1, source_target_pairs={{0,2},{1,3},{2,0},{3,1},{4,6},{5,7},{6,4},{7,5},{8,10},{9,11},{10,... | collective-permute-start | bytes 3145736 | tf_op jit(solution)/shard_map/ppermute | solution.py:42
  503.5 26.8 %collective-permute-start.56 = (bf16[256,2048]{1,0:T(8,128)(2,1)}, bf16[256,2048]{1,0:T(8,128)(2,1)}, u32[]{:S(2)}, u32[]{:S(2)}) collective-permute-start(bf16[256,2048]{1,0:T(8,128)(2,1)} %pad_maximum_fusion.24), channel_id=1, source_target_pairs={{0,4},{4,0},{8,12},{12,8},{16,20},{20,16},{24,28},{28,24},{1,5},{5... | collective-permute-start | bytes 3145736 | tf_op jit(solution)/shard_map/ppermute | solution.py:42
  534.4 24.0 %collective-permute-start.60 = (bf16[512,2048]{1,0:T(8,128)(2,1)S(1)}, bf16[512,2048]{1,0:T(8,128)(2,1)S(1)}, u32[]{:S(2)}, u32[]{:S(2)}) collective-permute-start(bf16[512,2048]{1,0:T(8,128)(2,1)S(1)} %convolution_convert_fusion.5), channel_id=1, source_target_pairs={{0,1},{1,0},{2,3},{3,2},{4,5},{5,4},{6,7},{7,6},{8,9},{9,8},{10,11... | collective-permute-start | bytes 6291464 | tf_op jit(solution)/shard_map/ppermute | solution.py:42
  546.4 21.4 %collective-permute-start.69 = (bf16[128,2048]{1,0:T(8,128)(2,1)S(1)}, bf16[128,2048]{1,0:T(8,128)(2,1)S(1)}, u32[]{:S(2)}, u32[]{:S(2)}) collective-permute-start(bf16[128,2048]{1,0:T(8,128)(2,1)S(1)} %pad_maximum_fusion.35), channel_id=1, source_target_pairs={{0,16},{4,20},{16,24},{20,28},{24,8},{28,12},{8,0},{12,4},{1,17},{... | collective-permute-start | bytes 1572872 | tf_op jit(solution)/shard_map/ppermute | solution.py:64
  547.1 24.7 %collective-permute-start.70 = (bf16[128,2048]{1,0:T(8,128)(2,1)S(1)}, bf16[128,2048]{1,0:T(8,128)(2,1)S(1)}, u32[]{:S(2)}, u32[]{:S(2)}) collective-permute-start(bf16[128,2048]{1,0:T(8,128)(2,1)S(1)} %pad_maximum_fusion.36), channel_id=1, source_target_pairs={{0,8},{4,12},{16,0},{20,4},{24,16},{28,20},{8,24},{12,28},{1,9},{5... | collective-permute-start | bytes 1572872 | tf_op jit(solution)/shard_map/ppermute | solution.py:64
  580.0 20.1 %collective-permute-start.73 = (f32[2,2,4,2,64]{4,2,3,1,0:T(4,128)S(1)}, f32[2,2,4,2,64]{4,2,3,1,0:T(4,128)S(1)}, u32[]{:S(2)}, u32[]{:S(2)}) collective-permute-start(f32[2,2,4,2,64]{4,2,3,1,0:T(4,128)S(1)} %slice.902), channel_id=1, source_target_pairs={{0,1},{1,0},{2,3},{3,2},{4,5},{5,4},{6,7},{7,6},{8,9},{9,8},{10,11... | collective-permute-start | bytes 24584 | tf_op jit(solution)/shard_map/ppermute | solution.py:42
  585.1 30.2 %collective-permute-start.63 = (bf16[256,2048]{1,0:T(8,128)(2,1)}, bf16[256,2048]{1,0:T(8,128)(2,1)S(1)}, u32[]{:S(2)}, u32[]{:S(2)}) collective-permute-start(bf16[256,2048]{1,0:T(8,128)(2,1)} %pad_maximum_fusion.25), channel_id=1, source_target_pairs={{0,2},{1,3},{2,0},{3,1},{4,6},{5,7},{6,4},{7,5},{8,10},{9,11},{10,... | collective-permute-start | bytes 3145736 | tf_op jit(solution)/shard_map/ppermute | solution.py:42
  586.4 28.8 %collective-permute-start.64 = (bf16[256,2048]{1,0:T(8,128)(2,1)}, bf16[256,2048]{1,0:T(8,128)(2,1)}, u32[]{:S(2)}, u32[]{:S(2)}) collective-permute-start(bf16[256,2048]{1,0:T(8,128)(2,1)} %pad_maximum_fusion.26), channel_id=1, source_target_pairs={{0,4},{4,0},{8,12},{12,8},{16,20},{20,16},{24,28},{28,24},{1,5},{5... | collective-permute-start | bytes 3145736 | tf_op jit(solution)/shard_map/ppermute | solution.py:42
  590.1 51.3 %collective-permute-start.71 = (bf16[256,2048]{1,0:T(8,128)(2,1)}, bf16[256,2048]{1,0:T(8,128)(2,1)}, u32[]{:S(2)}, u32[]{:S(2)}) collective-permute-start(bf16[256,2048]{1,0:T(8,128)(2,1)} %pad_maximum_fusion.27), channel_id=1, source_target_pairs={{0,16},{4,20},{16,24},{20,28},{24,8},{28,12},{8,0},{12,4},{1,17},{... | collective-permute-start | bytes 3145736 | tf_op jit(solution)/shard_map/ppermute | solution.py:64
  591.4 50.0 %collective-permute-start.72 = (bf16[256,2048]{1,0:T(8,128)(2,1)}, bf16[256,2048]{1,0:T(8,128)(2,1)}, u32[]{:S(2)}, u32[]{:S(2)}) collective-permute-start(bf16[256,2048]{1,0:T(8,128)(2,1)} %pad_maximum_fusion.28), channel_id=1, source_target_pairs={{0,8},{4,12},{16,0},{20,4},{24,16},{28,20},{8,24},{12,28},{1,9},{5... | collective-permute-start | bytes 3145736 | tf_op jit(solution)/shard_map/ppermute | solution.py:64
  615.4 24.3 %collective-permute-start.76 = (bf16[77,64]{1,0:T(8,128)(2,1)S(1)}, bf16[77,64]{1,0:T(8,128)(2,1)S(1)}, u32[]{:S(2)}, u32[]{:S(2)}) collective-permute-start(bf16[77,64]{1,0:T(8,128)(2,1)S(1)} %get-tuple-element.292), channel_id=1, source_target_pairs={{0,8},{4,12},{16,0},{20,4},{24,16},{28,20},{8,24},{12,28},{1,9},{5... | collective-permute-start | bytes 29576 | tf_op jit(solution)/shard_map/ppermute | solution.py:64
  616.4 23.4 %collective-permute-start.77 = (bf16[77,64]{1,0:T(8,128)(2,1)S(1)}, bf16[77,64]{1,0:T(8,128)(2,1)S(1)}, u32[]{:S(2)}, u32[]{:S(2)}) collective-permute-start(bf16[77,64]{1,0:T(8,128)(2,1)S(1)} %get-tuple-element.294), channel_id=1, source_target_pairs={{0,16},{4,20},{16,24},{20,28},{24,8},{28,12},{8,0},{12,4},{1,17},{... | collective-permute-start | bytes 29576 | tf_op jit(solution)/shard_map/ppermute | solution.py:64
  618.3 21.8 %collective-permute-start.78 = (bf16[77,64]{1,0:T(8,128)(2,1)S(1)}, bf16[77,64]{1,0:T(8,128)(2,1)S(1)}, u32[]{:S(2)}, u32[]{:S(2)}) collective-permute-start(bf16[77,64]{1,0:T(8,128)(2,1)S(1)} %get-tuple-element.293), channel_id=1, source_target_pairs={{0,24},{4,28},{16,8},{20,12},{24,0},{28,4},{8,16},{12,20},{1,25},{... | collective-permute-start | bytes 29576 | tf_op jit(solution)/shard_map/ppermute | solution.py:64
  (127 other events, 1422.2 us)

commit v11 on v10

--- a/solution.py
+++ b/solution.py
@@ -766,7 +766,7 @@
         last = ring_step([down_all, gate_all], last, odds)
     last_two = last
     for at in range(steps - 1):
-        last_two = ring_step([up_all] if at else [down_all, up_all], last_two)
+        last_two = ring_step([up_all], last_two)
     ready = after([mixed[0][1], mixed[1][1]], upstream_stages[0])
     evens = [nn(ready[r][parts[0]], out_all).astype(bf16) for r in range(2)]
     mixer_out, stages = scatter_rows(
@@ -778,7 +778,7 @@
     low_second = (middle * rate_last * gain_last).astype(bf16)
     (second_own, second_other), second_stages = gather_rows(low_second, last_two + upstream_stages[2])
     rows_second = jnp.concatenate(second_own + second_other, axis=0)
-    last = ring_step([gate_all, up_all], last_two, second_stages[1])
+    last = ring_step([down_all, gate_all, up_all], last_two, second_stages[1])
 
     down_all, gate_all = [jnp.concatenate(w.pieces(), axis=0) for w in (down_all, gate_all)]
     up_all = jnp.concatenate(up_all.pieces(), axis=0)

time: 656 us -> 654 us (level)
  starting transfers between devices: 78.3 us -> 89 us
  waiting for transfers between devices: 170 us -> 163 us
    ppermute x24, waiting for transfers between devices: 76.8 us -> 45.2 us  [along(): return lax.ppermute(values, 'wide', pairs)]
    ppermute x55, waiting for transfers between devices: 92.8 us -> 118 us  [swap(): return lax.ppermute(values, axis, [(i, i ^ shift) for i in range(size)])]
    ppermute x55, starting transfers between devices: 47.3 us -> 59.1 us  [swap(): return lax.ppermute(values, axis, [(i, i ^ shift) for i in range(size)])]
    unnamed x240 -> x245, local copies, waits for them, and re-layouts: 27.5 us -> 22.9 us
    concatenate x15 -> x13, other arithmetic: 14.4 us -> 12.1 us  [ring_step(): jnp.concatenate(one, axis=0)]
  transfers between devices with their start and end apart: 79 -> 79, of which waited for: 28 -> 30; matrix products, arithmetic and copies ran while one was open for 33% -> 33% of each run, Pallas kernels for 16% -> 16%
where the time goes in v11:
time: 654 us; the launch traced here: 646 us
  waiting for transfers between devices  163 us (25%)
  other arithmetic  119 us (18%)
  Pallas kernels  112 us (17%)
  matrix products  98.3 us (15%)
  starting transfers between devices  89 us (14%)
  local copies, waits for them, and re-layouts  61.8 us (9%)
    ppermute x55, waiting for transfers between devices, swap(): return lax.ppermute(values, axis, [(i, i ^ shift) for i in range(size)])  118 us
    ppermute x55, starting transfers between devices, swap(): return lax.ppermute(values, axis, [(i, i ^ shift) for i in range(size)])  59.1 us
    pallas_call x7, Pallas kernels, product(): pl.pallas_call(partial(product_kernel, kind=kind), grid=(columns // side,...  53.3 us
    ppermute x24, waiting for transfers between devices, along(): return lax.ppermute(values, 'wide', pairs)  45.2 us
    dot_general x7, matrix products, nt(): lax.dot_general(a, b, (((1,), (1,)), ((), ())), preferred_element_type=f32)  45 us
    pallas_call x2, Pallas kernels, mixer_backward(): pl.pallas_call(backward_kernel, out_shape=(jax.ShapeDtypeStruct((pieces,...  32.1 us
    dot_general x12, matrix products, tn(): lax.dot_general(a, b, (((0,), (0,)), ((), ())), preferred_element_type=f32)  31.1 us
    ppermute x24, starting transfers between devices, along(): return lax.ppermute(values, 'wide', pairs)  29.9 us
  transfers between devices with their start and end apart: 79, of which 30 were waited for; matrix products, arithmetic and copies ran while one was open for 33% of the time, Pallas kernels for 16%

profile of v11, /device:TPU:0, one launch (start us, length us, event | category | flops | bytes accessed | tf_op | source)
XLA Modules:
  0.0 646.2 jit_solution(17544672170390855490)
XLA Ops:
  1.5 3.1 concatenate.227
  4.6 4.1 collective-permute-start
  8.7 3.0 collective-permute-start.2
  34.3 4.1 taps.1
  38.4 3.5 fusion.91.spectrum
  41.9 9.3 %collective-permute-done.16 = s32[2,3]{1,0:T(2,128)S(1)} collective-permute-done((s32[2,3]{1,0:T(2,128)S(1)}, s32[2,3]{1,0:T(2,128)S(1)}, u32[]{:S(2)}, u32[]{:S(2)}) %collective-permute-start.16) | collective-permute-done | bytes 56 | tf_op jit(solution)/shard_map/ppermute | solution.py:42
  75.7 6.9 %collective-permute-done.10 = bf16[128,2048]{1,0:T(8,128)(2,1)S(1)} collective-permute-done((bf16[128,2048]{1,0:T(8,128)(2,1)S(1)}, bf16[128,2048]{1,0:T(8,128)(2,1)S(1)}, u32[]{:S(2)}, u32[]{:S(2)}) %collective-permute-start.10) | collective-permute-done | bytes 524320 | tf_op jit(solution)/shard_map/ppermute | solution.py:42
  82.6 2.4 collective-permute-done.9
  90.2 2.7 collective-permute-done.15
  95.8 2.8 fusion
  103.8 13.1 %fusion.5 = (bf16[1024,2048]{1,0:T(8,128)(2,1)S(1)}, bf16[1024,2048]{1,0:T(8,128)(2,1)S(1)}) fusion(f32[1024]{0:T(1024)S(1)} %add_rsqrt_fusion, f32[2048]{0:T(1024)S(1)} %mul.420, bf16[512,2048]{1,0:T(8,128)(2,1)S(1)} %collective-permute-done.11, bf16[128,2048]{1,0:T(8,128)(2,1)S(1)} %collective-permute-done.10, ...), kind=kLoop, calls=%fused_computation.9 | loop fusion | flops 41943040 | bytes 16793600 | tf_op jit(solution)/shard_map/convert_element_type | solution.py:709
  117.0 3.5 fusion.90.proj
  120.5 7.0 %mixer_forward.2 = (bf16[4,256,256]{2,1,0:T(8,128)(2,1)S(1)}, f32[1024,256]{1,0:T(8,128)S(1)}, bf16[3,1024,256]{2,1,0:T(8,128)(2,1)S(1)}) custom-call(s32[4]{0:T(128)S(1)} %select_reduce_fusion.7.order, s32[3]{0:T(128)S(1)} %get-tuple-element.213.first, s32[3]{0:T(128)S(1)} %get-tuple-element.319.count, f32[4,256,768]{2,1,0:T(8,128)S(1)} %fusion.90.proj, ...), custom_call_target="tpu_custom_call" | custom-call | flops 1024 | bytes 1024 | tf_op jit(solution)/shard_map/mixer_forward/pallas_call | solution.py:556
  127.6 2.4 convolution_convert_fusion.2
  130.0 3.5 fusion.92.proj
  133.5 7.4 %mixer_forward.3 = (bf16[4,256,256]{2,1,0:T(8,128)(2,1)S(1)}, f32[1024,256]{1,0:T(8,128)S(1)}, bf16[3,1024,256]{2,1,0:T(8,128)(2,1)S(1)}) custom-call(s32[4]{0:T(128)S(1)} %select_reduce_fusion.7.order, s32[3]{0:T(128)S(1)} %get-tuple-element.209.first, s32[3]{0:T(128)S(1)} %get-tuple-element.317.count, f32[4,256,768]{2,1,0:T(8,128)S(1)} %fusion.92.proj, ...), custom_call_target="tpu_custom_call" | custom-call | flops 1024 | bytes 1024 | tf_op jit(solution)/shard_map/mixer_forward/pallas_call | solution.py:556
  145.6 13.5 %collective-permute-start.22 = (bf16[128,2048]{1,0:T(8,128)(2,1)S(1)}, bf16[128,2048]{1,0:T(8,128)(2,1)S(1)}, u32[]{:S(2)}, u32[]{:S(2)}) collective-permute-start(bf16[128,2048]{1,0:T(8,128)(2,1)S(1)} %slice.819), channel_id=1, source_target_pairs={{0,2},{1,3},{2,0},{3,1},{4,6},{5,7},{6,4},{7,5},{8,10},{9,11},{10,... | collective-permute-start | bytes 1572872 | tf_op jit(solution)/shard_map/ppermute | solution.py:42
  167.8 2.6 convert_add_fusion.6
  176.7 6.2 collective-permute-done.26
  183.2 6.3 collective-permute-done.25
  195.9 18.4 %collective-permute-done.27 = bf16[256,2048]{1,0:T(8,128)(2,1)S(1)} collective-permute-done((bf16[256,2048]{1,0:T(8,128)(2,1)S(1)}, bf16[256,2048]{1,0:T(8,128)(2,1)S(1)}, u32[]{:S(2)}, u32[]{:S(2)}) %collective-permute-start.27) | collective-permute-done | bytes 1048608 | tf_op jit(solution)/shard_map/ppermute | solution.py:42
  224.6 14.8 %collective-permute-done.35 = bf16[256,2048]{1,0:T(8,128)(2,1)S(1)} collective-permute-done((bf16[256,2048]{1,0:T(8,128)(2,1)S(1)}, bf16[256,2048]{1,0:T(8,128)(2,1)S(1)}, u32[]{:S(2)}, u32[]{:S(2)}) %collective-permute-start.35) | collective-permute-done | bytes 1048608 | tf_op jit(solution)/shard_map/ppermute | solution.py:42
  241.6 3.9 collective-permute-done.37
  248.1 7.4 %collective-permute-done.36 = bf16[128,2048]{1,0:T(8,128)(2,1)S(1)} collective-permute-done((bf16[128,2048]{1,0:T(8,128)(2,1)S(1)}, bf16[128,2048]{1,0:T(8,128)(2,1)S(1)}, u32[]{:S(2)}, u32[]{:S(2)}) %collective-permute-start.36) | collective-permute-done | bytes 524320 | tf_op jit(solution)/shard_map/ppermute | solution.py:42
  258.0 8.9 %collective-permute-done.32 = bf16[240,2048]{1,0:T(8,128)(2,1)} collective-permute-done((bf16[240,2048]{1,0:T(8,128)(2,1)}, bf16[240,2048]{1,0:T(8,128)(2,1)}, u32[]{:S(2)}, u32[]{:S(2)}) %collective-permute-start.32) | collective-permute-done | bytes 983072 | tf_op jit(solution)/shard_map/ppermute | solution.py:64
  270.3 2.7 copy-done.66
  273.0 8.1 %fusion.94 = f32[704,2048]{1,0:T(8,128)} fusion(bf16[704,2048]{1,0:T(8,128)(2,1)S(1)} %get-tuple-element.276, bf16[2048,2048]{1,0:T(8,128)(2,1)S(1)} %constant_dynamic-update-slice_fusion.2.b), kind=kOutput, calls=%fused_computation.348 | convolution fusion | flops 5905580032 | bytes 17039360 | tf_op jit(solution)/shard_map/dot_general | solution.py:33
  281.2 8.0 %fusion.93 = f32[704,2048]{1,0:T(8,128)} fusion(bf16[704,2048]{1,0:T(8,128)(2,1)S(1)} %get-tuple-element.277, bf16[2048,2048]{1,0:T(8,128)(2,1)S(1)} %constant_dynamic-update-slice_fusion.2.b), kind=kOutput, calls=%fused_computation.347 | convolution fusion | flops 5905580032 | bytes 17039360 | tf_op jit(solution)/shard_map/dot_general | solution.py:33
  289.1 15.5 %multiply_convert_fusion = (bf16[704,2048]{1,0:T(8,128)(2,1)}, bf16[704,2048]{1,0:T(8,128)(2,1)}, bf16[704,2048]{1,0:T(8,128)(2,1)}) fusion(f32[704,2048]{1,0:T(8,128)} %fusion.93, f32[704,2048]{1,0:T(8,128)} %fusion.94, bf16[704,2048]{1,0:T(8,128)(2,1)S(1)} %get-tuple-element.275.b, bf16[2048,2048]{1,0:T(8,128)(2,1)} %constant_dynamic-update-slice_fusion.13.b), kind=kOutput, calls=%fused_computation.11 | convolution fusion | flops 5927206912 | bytes 31457280 | tf_op jit(solution)/shard_map/dot_general | solution.py:33
  304.7 10.5 %product.7 = bf16[704,2048]{1,0:T(8,128)(2,1)} custom-call(bf16[704,2048]{1,0:T(8,128)(2,1)} %get-tuple-element.132.a, bf16[2048,2048]{1,0:T(8,128)(2,1)} %constant_dynamic-update-slice_fusion.13.b), custom_call_target="tpu_custom_call" | custom-call | flops 1024 | bytes 1024 | tf_op jit(solution)/shard_map/product/pallas_call | solution.py:363
  315.2 4.0 fusion.42
  334.6 2.5 convert_add_fusion.4
  337.2 10.3 %collective-permute-done.43 = bf16[128,2048]{1,0:T(8,128)(2,1)S(1)} collective-permute-done((bf16[128,2048]{1,0:T(8,128)(2,1)S(1)}, bf16[128,2048]{1,0:T(8,128)(2,1)S(1)}, u32[]{:S(2)}, u32[]{:S(2)}) %collective-permute-start.43) | collective-permute-done | bytes 524320 | tf_op jit(solution)/shard_map/ppermute | solution.py:42
  352.5 10.3 %product.8 = bf16[704,2048]{1,0:T(8,128)(2,1)} custom-call(bf16[704,2048]{1,0:T(8,128)(2,1)} %get-tuple-element.130.a, bf16[2048,2048]{1,0:T(8,128)(2,1)} %copy-done.28), custom_call_target="tpu_custom_call" | custom-call | flops 1024 | bytes 1024 | tf_op jit(solution)/shard_map/product/pallas_call | solution.py:363
  362.8 10.2 %product.9 = bf16[704,2048]{1,0:T(8,128)(2,1)} custom-call(bf16[704,2048]{1,0:T(8,128)(2,1)} %get-tuple-element.131.a, bf16[2048,2048]{1,0:T(8,128)(2,1)} %copy-done.28), custom_call_target="tpu_custom_call" | custom-call | flops 1024 | bytes 1024 | tf_op jit(solution)/shard_map/product/pallas_call | solution.py:363
  375.5 3.7 multiply_reduce_fusion.4
  379.3 4.3 fusion.75
  390.1 5.6 product.13
  395.7 5.6 product.12
  401.3 5.6 product.11
  406.9 5.6 product.10
  420.4 14.9 %collective-permute-done.66 = bf16[240,2048]{1,0:T(8,128)(2,1)} collective-permute-done((bf16[240,2048]{1,0:T(8,128)(2,1)}, bf16[240,2048]{1,0:T(8,128)(2,1)}, u32[]{:S(2)}, u32[]{:S(2)}) %collective-permute-start.66) | collective-permute-done | bytes 983072 | tf_op jit(solution)/shard_map/ppermute | solution.py:64
  449.2 3.0 pad_maximum_fusion.11
  453.0 5.1 fusion.21
  458.1 16.0 %mixer_backward.2 = (bf16[4,256,768]{2,1,0:T(8,128)(2,1)}, f32[512,256]{1,0:T(8,128)S(1)}, f32[8,768]{1,0:T(8,128)S(1)}) custom-call(s32[4]{0:T(128)S(1)} %select_reduce_fusion.7.order, s32[3]{0:T(128)S(1)} %copy-done.17, s32[3]{0:T(128)S(1)} %copy-done.19, f32[4,256,768]{2,1,0:T(8,128)} %copy-done.4, f32[4,256,256]{2,1,0:T(8,128)S(1)} %bitcast.197, ...), custom_call_target="tpu_custom_call" | custom-call | flops 1024 | bytes 1024 | tf_op jit(solution)/shard_map/mixer_backward/pallas_call | solution.py:582
  488.3 4.3 fusion.7
  493.6 5.0 collective-permute-done.54
  504.6 4.5 convert_add_fusion.1
  509.1 16.1 %mixer_backward.3 = (bf16[4,256,768]{2,1,0:T(8,128)(2,1)}, f32[512,256]{1,0:T(8,128)S(1)}, f32[8,768]{1,0:T(8,128)S(1)}) custom-call(s32[4]{0:T(128)S(1)} %select_reduce_fusion.7.order, s32[3]{0:T(128)S(1)} %get-tuple-element.209.first, s32[3]{0:T(128)S(1)} %get-tuple-element.317.count, f32[4,256,768]{2,1,0:T(8,128)} %copy-done.3, ...), custom_call_target="tpu_custom_call" | custom-call | flops 1024 | bytes 1024 | tf_op jit(solution)/shard_map/mixer_backward/pallas_call | solution.py:582
  529.3 4.1 convolution_convert_fusion.5
  533.5 3.5 fusion.97
  537.0 3.7 add_convert_fusion
  540.7 2.7 collective-permute-done.68
  548.3 3.4 fusion.23
  551.7 4.7 add_bitcast_fusion
  556.4 3.9 convert_add_fusion
  566.4 3.5 collective-permute-done.70
  570.0 3.8 collective-permute-done.61
  589.9 7.9 %moments.1 = (f32[16,8,256]{2,1,0:T(8,128)}, f32[16,8,256]{2,1,0:T(8,128)}, f32[16,8,256]{2,1,0:T(8,128)}, f32[16,8,256]{2,1,0:T(8,128)}) custom-call(f32[512,256]{1,0:T(8,128)} %add.367.grad, f32[16,8,256]{2,1,0:T(8,128)} %broadcast_in_dim.201.step_re, f32[16,8,256]{2,1,0:T(8,128)} %broadcast_in_dim.202.step_im), custom_call_target="tpu_custom_call" | custom-call | flops 31457280 | bytes 524288 | tf_op jit(solution)/shard_map/moments/pallas_call | solution.py:378
  600.7 9.3 %collective-permute-done.74 = f32[2,4,2,64]{3,1,2,0:T(4,128)S(1)} collective-permute-done((f32[2,4,2,64]{3,1,2,0:T(4,128)S(1)}, f32[2,4,2,64]{3,1,2,0:T(4,128)S(1)}, u32[]{:S(2)}, u32[]{:S(2)}) %collective-permute-start.74) | collective-permute-done | bytes 4128 | tf_op jit(solution)/shard_map/ppermute | solution.py:42
  619.5 2.7 fusion.8
  622.2 3.7 fusion.24
  626.0 12.1 %collective-permute-done.76 = bf16[77,64]{1,0:T(8,128)(2,1)S(1)} collective-permute-done((bf16[77,64]{1,0:T(8,128)(2,1)S(1)}, bf16[77,64]{1,0:T(8,128)(2,1)S(1)}, u32[]{:S(2)}, u32[]{:S(2)}) %collective-permute-start.76) | collective-permute-done | bytes 9888 | tf_op jit(solution)/shard_map/ppermute | solution.py:64
  641.7 3.0 fusion.22
  (587 shorter events, 228.4 us)
Async XLA Ops:
  4.6 22.8 %collective-permute-start = (bf16[75,64]{1,0:T(8,128)(2,1)S(1)}, bf16[75,64]{1,0:T(8,128)(2,1)S(1)}, u32[]{:S(2)}, u32[]{:S(2)}) collective-permute-start(bf16[75,64]{1,0:T(8,128)(2,1)S(1)} %concatenate.227), channel_id=1, source_target_pairs={{0,16},{4,20},{16,24},{20,28},{24,8},{28,12},{8,0},{12,4},{1,17},{... | collective-permute-start | bytes 28808 | tf_op jit(solution)/shard_map/ppermute | solution.py:64
  8.7 18.7 %collective-permute-start.1 = (bf16[75,64]{1,0:T(8,128)(2,1)S(1)}, bf16[75,64]{1,0:T(8,128)(2,1)S(1)}, u32[]{:S(2)}, u32[]{:S(2)}) collective-permute-start(bf16[75,64]{1,0:T(8,128)(2,1)S(1)} %concatenate.227), channel_id=1, source_target_pairs={{0,8},{4,12},{16,0},{20,4},{24,16},{28,20},{8,24},{12,28},{1,9},{5... | collective-permute-start | bytes 28808 | tf_op jit(solution)/shard_map/ppermute | solution.py:64
  8.7 18.7 %collective-permute-start.2 = (bf16[75,64]{1,0:T(8,128)(2,1)S(1)}, bf16[75,64]{1,0:T(8,128)(2,1)S(1)}, u32[]{:S(2)}, u32[]{:S(2)}) collective-permute-start(bf16[75,64]{1,0:T(8,128)(2,1)S(1)} %concatenate.227), channel_id=1, source_target_pairs={{0,24},{4,28},{16,8},{20,12},{24,0},{28,4},{8,16},{12,20},{1,25},{... | collective-permute-start | bytes 28808 | tf_op jit(solution)/shard_map/ppermute | solution.py:64
  14.0 47.5 %collective-permute-start.12 = (bf16[256,2048]{1,0:T(8,128)(2,1)}, bf16[256,2048]{1,0:T(8,128)(2,1)}, u32[]{:S(2)}, u32[]{:S(2)}) collective-permute-start(bf16[256,2048]{1,0:T(8,128)(2,1)} %pad_maximum_fusion.17), channel_id=1, source_target_pairs={{0,16},{4,20},{16,24},{20,28},{24,8},{28,12},{8,0},{12,4},{1,17},{... | collective-permute-start | bytes 3145736 | tf_op jit(solution)/shard_map/ppermute | solution.py:64
  14.4 49.2 %collective-permute-start.13 = (bf16[256,2048]{1,0:T(8,128)(2,1)}, bf16[256,2048]{1,0:T(8,128)(2,1)}, u32[]{:S(2)}, u32[]{:S(2)}) collective-permute-start(bf16[256,2048]{1,0:T(8,128)(2,1)} %pad_maximum_fusion.17), channel_id=1, source_target_pairs={{0,8},{4,12},{16,0},{20,4},{24,16},{28,20},{8,24},{12,28},{1,9},{5... | collective-permute-start | bytes 3145736 | tf_op jit(solution)/shard_map/ppermute | solution.py:64
  27.4 40.3 %collective-permute-start.8 = (bf16[256,2048]{1,0:T(8,128)(2,1)S(1)}, bf16[256,2048]{1,0:T(8,128)(2,1)}, u32[]{:S(2)}, u32[]{:S(2)}) collective-permute-start(bf16[256,2048]{1,0:T(8,128)(2,1)S(1)} %bitcast.204), channel_id=1, source_target_pairs={{0,4},{4,0},{8,12},{12,8},{16,20},{20,16},{24,28},{28,24},{1,5},{5... | collective-permute-start | bytes 3145736 | tf_op jit(solution)/shard_map/ppermute | solution.py:42
  29.0 41.3 %collective-permute-start.3 = (bf16[256,2048]{1,0:T(8,128)(2,1)S(1)}, bf16[256,2048]{1,0:T(8,128)(2,1)}, u32[]{:S(2)}, u32[]{:S(2)}) collective-permute-start(bf16[256,2048]{1,0:T(8,128)(2,1)S(1)} %bitcast.205), channel_id=1, source_target_pairs={{0,2},{1,3},{2,0},{3,1},{4,6},{5,7},{6,4},{7,5},{8,10},{9,11},{10,... | collective-permute-start | bytes 3145736 | tf_op jit(solution)/shard_map/ppermute | solution.py:42
  30.8 20.3 %collective-permute-start.16 = (s32[2,3]{1,0:T(2,128)S(1)}, s32[2,3]{1,0:T(2,128)S(1)}, u32[]{:S(2)}, u32[]{:S(2)}) collective-permute-start(s32[2,3]{1,0:T(2,128)S(1)} %pad_add_fusion), channel_id=1, source_target_pairs={{0,4},{4,0},{8,12},{12,8},{16,20},{20,16},{24,28},{28,24},{1,5},{5... | collective-permute-start | bytes 80 | tf_op jit(solution)/shard_map/ppermute | solution.py:42
  65.6 24.6 %collective-permute-start.14 = (bf16[128,2048]{1,0:T(8,128)(2,1)S(1)}, bf16[128,2048]{1,0:T(8,128)(2,1)S(1)}, u32[]{:S(2)}, u32[]{:S(2)}) collective-permute-start(bf16[128,2048]{1,0:T(8,128)(2,1)S(1)} %pad_maximum_fusion.31), channel_id=1, source_target_pairs={{0,16},{4,20},{16,24},{20,28},{24,8},{28,12},{8,0},{12,4},{1,17},{... | collective-permute-start | bytes 1572872 | tf_op jit(solution)/shard_map/ppermute | solution.py:64
  66.9 26.0 %collective-permute-start.15 = (bf16[128,2048]{1,0:T(8,128)(2,1)S(1)}, bf16[128,2048]{1,0:T(8,128)(2,1)S(1)}, u32[]{:S(2)}, u32[]{:S(2)}) collective-permute-start(bf16[128,2048]{1,0:T(8,128)(2,1)S(1)} %pad_maximum_fusion.32), channel_id=1, source_target_pairs={{0,8},{4,12},{16,0},{20,4},{24,16},{28,20},{8,24},{12,28},{1,9},{5... | collective-permute-start | bytes 1572872 | tf_op jit(solution)/shard_map/ppermute | solution.py:64
  68.8 13.8 %collective-permute-start.10 = (bf16[128,2048]{1,0:T(8,128)(2,1)S(1)}, bf16[128,2048]{1,0:T(8,128)(2,1)S(1)}, u32[]{:S(2)}, u32[]{:S(2)}) collective-permute-start(bf16[128,2048]{1,0:T(8,128)(2,1)S(1)} %slice.797), channel_id=1, source_target_pairs={{0,2},{1,3},{2,0},{3,1},{4,6},{5,7},{6,4},{7,5},{8,10},{9,11},{10,... | collective-permute-start | bytes 1572872 | tf_op jit(solution)/shard_map/ppermute | solution.py:42
  75.6 20.2 %collective-permute-start.4 = (bf16[512,2048]{1,0:T(8,128)(2,1)S(1)}, bf16[512,2048]{1,0:T(8,128)(2,1)S(1)}, u32[]{:S(2)}, u32[]{:S(2)}) collective-permute-start(bf16[512,2048]{1,0:T(8,128)(2,1)S(1)} %pad_maximum_fusion.4), channel_id=1, source_target_pairs={{0,1},{1,0},{2,3},{3,2},{4,5},{5,4},{6,7},{7,6},{8,9},{9,8},{10,11... | collective-permute-start | bytes 6291464 | tf_op jit(solution)/shard_map/ppermute | solution.py:42
  92.9 52.7 %collective-permute-start.23 = (bf16[352,2048]{1,0:T(8,128)(2,1)}, bf16[352,2048]{1,0:T(8,128)(2,1)}, u32[]{:S(2)}, u32[]{:S(2)}) collective-permute-start(bf16[352,2048]{1,0:T(8,128)(2,1)} %pad_maximum_fusion.14), channel_id=1, source_target_pairs={{0,16},{4,20},{16,24},{20,28},{24,8},{28,12},{8,0},{12,4},{1,17},{... | collective-permute-start | bytes 4325384 | tf_op jit(solution)/shard_map/ppermute | solution.py:64
  93.5 65.6 %collective-permute-start.24 = (bf16[352,2048]{1,0:T(8,128)(2,1)}, bf16[352,2048]{1,0:T(8,128)(2,1)}, u32[]{:S(2)}, u32[]{:S(2)}) collective-permute-start(bf16[352,2048]{1,0:T(8,128)(2,1)} %pad_maximum_fusion.14), channel_id=1, source_target_pairs={{0,8},{4,12},{16,0},{20,4},{24,16},{28,20},{8,24},{12,28},{1,9},{5... | collective-permute-start | bytes 4325384 | tf_op jit(solution)/shard_map/ppermute | solution.py:64
  98.8 42.3 %collective-permute-start.17 = (bf16[256,2048]{1,0:T(8,128)(2,1)S(1)}, bf16[256,2048]{1,0:T(8,128)(2,1)S(1)}, u32[]{:S(2)}, u32[]{:S(2)}) collective-permute-start(bf16[256,2048]{1,0:T(8,128)(2,1)S(1)} %bitcast.216), channel_id=1, source_target_pairs={{0,2},{1,3},{2,0},{3,1},{4,6},{5,7},{6,4},{7,5},{8,10},{9,11},{10,... | collective-permute-start | bytes 3145736 | tf_op jit(solution)/shard_map/ppermute | solution.py:42
  100.3 41.4 %collective-permute-start.18 = (bf16[256,2048]{1,0:T(8,128)(2,1)S(1)}, bf16[256,2048]{1,0:T(8,128)(2,1)}, u32[]{:S(2)}, u32[]{:S(2)}) collective-permute-start(bf16[256,2048]{1,0:T(8,128)(2,1)S(1)} %bitcast.217), channel_id=1, source_target_pairs={{0,4},{4,0},{8,12},{12,8},{16,20},{20,16},{24,28},{28,24},{1,5},{5... | collective-permute-start | bytes 3145736 | tf_op jit(solution)/shard_map/ppermute | solution.py:42
  130.0 42.7 %collective-permute-start.19 = (bf16[512,2048]{1,0:T(8,128)(2,1)}, bf16[512,2048]{1,0:T(8,128)(2,1)}, u32[]{:S(2)}, u32[]{:S(2)}) collective-permute-start(bf16[512,2048]{1,0:T(8,128)(2,1)} %convolution_convert_fusion.2), channel_id=1, source_target_pairs={{0,1},{1,0},{2,3},{3,2},{4,5},{5,4},{6,7},{7,6},{8,9},{9,8},{10,11... | collective-permute-start | bytes 6291464 | tf_op jit(solution)/shard_map/ppermute | solution.py:42
  141.2 23.0 %collective-permute-start.21 = (bf16[128,2048]{1,0:T(8,128)(2,1)S(1)}, bf16[128,2048]{1,0:T(8,128)(2,1)S(1)}, u32[]{:S(2)}, u32[]{:S(2)}) collective-permute-start(bf16[128,2048]{1,0:T(8,128)(2,1)S(1)} %slice.818), channel_id=1, source_target_pairs={{0,4},{4,0},{8,12},{12,8},{16,20},{20,16},{24,28},{28,24},{1,5},{5... | collective-permute-start | bytes 1572872 | tf_op jit(solution)/shard_map/ppermute | solution.py:42
  142.5 25.3 %collective-permute-start.20 = (bf16[512,2048]{1,0:T(8,128)(2,1)S(1)}, bf16[512,2048]{1,0:T(8,128)(2,1)}, u32[]{:S(2)}, u32[]{:S(2)}) collective-permute-start(bf16[512,2048]{1,0:T(8,128)(2,1)S(1)} %convolution_convert_fusion), channel_id=1, source_target_pairs={{0,1},{1,0},{2,3},{3,2},{4,5},{5,4},{6,7},{7,6},{8,9},{9,8},{10,11... | collective-permute-start | bytes 6291464 | tf_op jit(solution)/shard_map/ppermute | solution.py:42
  145.6 20.7 %collective-permute-start.22 = (bf16[128,2048]{1,0:T(8,128)(2,1)S(1)}, bf16[128,2048]{1,0:T(8,128)(2,1)S(1)}, u32[]{:S(2)}, u32[]{:S(2)}) collective-permute-start(bf16[128,2048]{1,0:T(8,128)(2,1)S(1)} %slice.819), channel_id=1, source_target_pairs={{0,2},{1,3},{2,0},{3,1},{4,6},{5,7},{6,4},{7,5},{8,10},{9,11},{10,... | collective-permute-start | bytes 1572872 | tf_op jit(solution)/shard_map/ppermute | solution.py:42
  159.1 15.9 %collective-permute-start.33 = (bf16[512,2048]{1,0:T(8,128)(2,1)}, bf16[512,2048]{1,0:T(8,128)(2,1)S(1)}, u32[]{:S(2)}, u32[]{:S(2)}) collective-permute-start(bf16[512,2048]{1,0:T(8,128)(2,1)} %pad_maximum_fusion.6), channel_id=1, source_target_pairs={{0,1},{1,0},{2,3},{3,2},{4,5},{5,4},{6,7},{7,6},{8,9},{9,8},{10,11... | collective-permute-start | bytes 6291464 | tf_op jit(solution)/shard_map/ppermute | solution.py:42
  164.1 30.8 %collective-permute-start.30 = (bf16[176,2048]{1,0:T(8,128)(2,1)}, bf16[176,2048]{1,0:T(8,128)(2,1)}, u32[]{:S(2)}, u32[]{:S(2)}) collective-permute-start(bf16[176,2048]{1,0:T(8,128)(2,1)} %bitcast.42), channel_id=1, source_target_pairs={{0,8},{4,12},{16,0},{20,4},{24,16},{28,20},{8,24},{12,28},{1,9},{5... | collective-permute-start | bytes 2162696 | tf_op jit(solution)/shard_map/ppermute | solution.py:64
  175.1 40.5 %collective-permute-start.34 = (bf16[512,2048]{1,0:T(8,128)(2,1)S(1)}, bf16[512,2048]{1,0:T(8,128)(2,1)S(1)}, u32[]{:S(2)}, u32[]{:S(2)}) collective-permute-start(bf16[512,2048]{1,0:T(8,128)(2,1)S(1)} %pad_maximum_fusion.7), channel_id=1, source_target_pairs={{0,1},{1,0},{2,3},{3,2},{4,5},{5,4},{6,7},{7,6},{8,9},{9,8},{10,11... | collective-permute-start | bytes 6291464 | tf_op jit(solution)/shard_map/ppermute | solution.py:42
  175.1 14.3 %collective-permute-start.25 = (bf16[128,2048]{1,0:T(8,128)(2,1)S(1)}, bf16[128,2048]{1,0:T(8,128)(2,1)S(1)}, u32[]{:S(2)}, u32[]{:S(2)}) collective-permute-start(bf16[128,2048]{1,0:T(8,128)(2,1)S(1)} %get-tuple-element.274), channel_id=1, source_target_pairs={{0,4},{4,0},{8,12},{12,8},{16,20},{20,16},{24,28},{28,24},{1,5},{5... | collective-permute-start | bytes 1572872 | tf_op jit(solution)/shard_map/ppermute | solution.py:42
  189.7 24.7 %collective-permute-start.27 = (bf16[256,2048]{1,0:T(8,128)(2,1)S(1)}, bf16[256,2048]{1,0:T(8,128)(2,1)S(1)}, u32[]{:S(2)}, u32[]{:S(2)}) collective-permute-start(bf16[256,2048]{1,0:T(8,128)(2,1)S(1)} %pad_maximum_fusion.18), channel_id=1, source_target_pairs={{0,2},{1,3},{2,0},{3,1},{4,6},{5,7},{6,4},{7,5},{8,10},{9,11},{10,... | collective-permute-start | bytes 3145736 | tf_op jit(solution)/shard_map/ppermute | solution.py:42
  189.8 24.7 %collective-permute-start.28 = (bf16[256,2048]{1,0:T(8,128)(2,1)S(1)}, bf16[256,2048]{1,0:T(8,128)(2,1)S(1)}, u32[]{:S(2)}, u32[]{:S(2)}) collective-permute-start(bf16[256,2048]{1,0:T(8,128)(2,1)S(1)} %pad_maximum_fusion.19), channel_id=1, source_target_pairs={{0,4},{4,0},{8,12},{12,8},{16,20},{20,16},{24,28},{28,24},{1,5},{5... | collective-permute-start | bytes 3145736 | tf_op jit(solution)/shard_map/ppermute | solution.py:42
  192.5 23.0 %collective-permute-start.29 = (bf16[176,2048]{1,0:T(8,128)(2,1)}, bf16[176,2048]{1,0:T(8,128)(2,1)S(1)}, u32[]{:S(2)}, u32[]{:S(2)}) collective-permute-start(bf16[176,2048]{1,0:T(8,128)(2,1)} %bitcast.42), channel_id=1, source_target_pairs={{0,16},{4,20},{16,24},{20,28},{24,8},{28,12},{8,0},{12,4},{1,17},{... | collective-permute-start | bytes 2162696 | tf_op jit(solution)/shard_map/ppermute | solution.py:64
  215.5 23.8 %collective-permute-start.35 = (bf16[256,2048]{1,0:T(8,128)(2,1)S(1)}, bf16[256,2048]{1,0:T(8,128)(2,1)S(1)}, u32[]{:S(2)}, u32[]{:S(2)}) collective-permute-start(bf16[256,2048]{1,0:T(8,128)(2,1)S(1)} %multiply_convert_fusion.3), channel_id=1, source_target_pairs={{0,2},{1,3},{2,0},{3,1},{4,6},{5,7},{6,4},{7,5},{8,10},{9,11},{10,... | collective-permute-start | bytes 3145736 | tf_op jit(solution)/shard_map/ppermute | solution.py:42
  219.5 47.4 %collective-permute-start.31 = (bf16[288,2048]{1,0:T(8,128)(2,1)}, bf16[288,2048]{1,0:T(8,128)(2,1)}, u32[]{:S(2)}, u32[]{:S(2)}) collective-permute-start(bf16[288,2048]{1,0:T(8,128)(2,1)} %pad_maximum_fusion.15), channel_id=1, source_target_pairs={{0,16},{4,20},{16,24},{20,28},{24,8},{28,12},{8,0},{12,4},{1,17},{... | collective-permute-start | bytes 3538952 | tf_op jit(solution)/shard_map/ppermute | solution.py:64
  219.5 47.4 %collective-permute-start.32 = (bf16[240,2048]{1,0:T(8,128)(2,1)}, bf16[240,2048]{1,0:T(8,128)(2,1)}, u32[]{:S(2)}, u32[]{:S(2)}) collective-permute-start(bf16[240,2048]{1,0:T(8,128)(2,1)} %pad_maximum_fusion.28), channel_id=1, source_target_pairs={{0,8},{4,12},{16,0},{20,4},{24,16},{28,20},{8,24},{12,28},{1,9},{5... | collective-permute-start | bytes 2949128 | tf_op jit(solution)/shard_map/ppermute | solution.py:64
  221.6 23.9 %collective-permute-start.37 = (bf16[256,2048]{1,0:T(8,128)(2,1)S(1)}, bf16[256,2048]{1,0:T(8,128)(2,1)S(1)}, u32[]{:S(2)}, u32[]{:S(2)}) collective-permute-start(bf16[256,2048]{1,0:T(8,128)(2,1)S(1)} %multiply_convert_fusion.3), channel_id=1, source_target_pairs={{0,4},{4,0},{8,12},{12,8},{16,20},{20,16},{24,28},{28,24},{1,5},{5... | collective-permute-start | bytes 3145736 | tf_op jit(solution)/shard_map/ppermute | solution.py:42
  239.6 29.9 %collective-permute-start.39 = (bf16[512,2048]{1,0:T(8,128)(2,1)S(1)}, bf16[512,2048]{1,0:T(8,128)(2,1)S(1)}, u32[]{:S(2)}, u32[]{:S(2)}) collective-permute-start(bf16[512,2048]{1,0:T(8,128)(2,1)S(1)} %pad_maximum_fusion.8), channel_id=1, source_target_pairs={{0,1},{1,0},{2,3},{3,2},{4,5},{5,4},{6,7},{7,6},{8,9},{9,8},{10,11... | collective-permute-start | bytes 6291464 | tf_op jit(solution)/shard_map/ppermute | solution.py:42
  240.0 15.5 %collective-permute-start.36 = (bf16[128,2048]{1,0:T(8,128)(2,1)S(1)}, bf16[128,2048]{1,0:T(8,128)(2,1)S(1)}, u32[]{:S(2)}, u32[]{:S(2)}) collective-permute-start(bf16[128,2048]{1,0:T(8,128)(2,1)S(1)} %slice.826), channel_id=1, source_target_pairs={{0,4},{4,0},{8,12},{12,8},{16,20},{20,16},{24,28},{28,24},{1,5},{5... | collective-permute-start | bytes 1572872 | tf_op jit(solution)/shard_map/ppermute | solution.py:42
  331.9 16.8 %collective-permute-start.42 = (bf16[128,2048]{1,0:T(8,128)(2,1)S(1)}, bf16[128,2048]{1,0:T(8,128)(2,1)S(1)}, u32[]{:S(2)}, u32[]{:S(2)}) collective-permute-start(bf16[128,2048]{1,0:T(8,128)(2,1)S(1)} %get-tuple-element.253), channel_id=1, source_target_pairs={{0,4},{4,0},{8,12},{12,8},{16,20},{20,16},{24,28},{28,24},{1,5},{5... | collective-permute-start | bytes 1572872 | tf_op jit(solution)/shard_map/ppermute | solution.py:42
  333.5 14.0 %collective-permute-start.43 = (bf16[128,2048]{1,0:T(8,128)(2,1)S(1)}, bf16[128,2048]{1,0:T(8,128)(2,1)S(1)}, u32[]{:S(2)}, u32[]{:S(2)}) collective-permute-start(bf16[128,2048]{1,0:T(8,128)(2,1)S(1)} %get-tuple-element.252), channel_id=1, source_target_pairs={{0,2},{1,3},{2,0},{3,1},{4,6},{5,7},{6,4},{7,5},{8,10},{9,11},{10,... | collective-permute-start | bytes 1572872 | tf_op jit(solution)/shard_map/ppermute | solution.py:42
  349.9 24.7 %collective-permute-start.45 = (bf16[256,2048]{1,0:T(8,128)(2,1)}, bf16[256,2048]{1,0:T(8,128)(2,1)}, u32[]{:S(2)}, u32[]{:S(2)}) collective-permute-start(bf16[256,2048]{1,0:T(8,128)(2,1)} %pad_maximum_fusion.20), channel_id=1, source_target_pairs={{0,2},{1,3},{2,0},{3,1},{4,6},{5,7},{6,4},{7,5},{8,10},{9,11},{10,... | collective-permute-start | bytes 3145736 | tf_op jit(solution)/shard_map/ppermute | solution.py:42
  351.1 24.5 %collective-permute-start.46 = (bf16[256,2048]{1,0:T(8,128)(2,1)}, bf16[256,2048]{1,0:T(8,128)(2,1)}, u32[]{:S(2)}, u32[]{:S(2)}) collective-permute-start(bf16[256,2048]{1,0:T(8,128)(2,1)} %pad_maximum_fusion.21), channel_id=1, source_target_pairs={{0,4},{4,0},{8,12},{12,8},{16,20},{20,16},{24,28},{28,24},{1,5},{5... | collective-permute-start | bytes 3145736 | tf_op jit(solution)/shard_map/ppermute | solution.py:42
  383.7 28.8 %collective-permute-start.47 = (bf16[256,2048]{1,0:T(8,128)(2,1)}, bf16[256,2048]{1,0:T(8,128)(2,1)}, u32[]{:S(2)}, u32[]{:S(2)}) collective-permute-start(bf16[256,2048]{1,0:T(8,128)(2,1)} %get-tuple-element.205), channel_id=1, source_target_pairs={{0,2},{1,3},{2,0},{3,1},{4,6},{5,7},{6,4},{7,5},{8,10},{9,11},{10,... | collective-permute-start | bytes 3145736 | tf_op jit(solution)/shard_map/ppermute | solution.py:42
  384.6 29.9 %collective-permute-start.49 = (bf16[256,2048]{1,0:T(8,128)(2,1)}, bf16[256,2048]{1,0:T(8,128)(2,1)}, u32[]{:S(2)}, u32[]{:S(2)}) collective-permute-start(bf16[256,2048]{1,0:T(8,128)(2,1)} %get-tuple-element.205), channel_id=1, source_target_pairs={{0,4},{4,0},{8,12},{12,8},{16,20},{20,16},{24,28},{28,24},{1,5},{5... | collective-permute-start | bytes 3145736 | tf_op jit(solution)/shard_map/ppermute | solution.py:42
  387.9 47.3 %collective-permute-start.65 = (bf16[288,2048]{1,0:T(8,128)(2,1)}, bf16[288,2048]{1,0:T(8,128)(2,1)}, u32[]{:S(2)}, u32[]{:S(2)}) collective-permute-start(bf16[288,2048]{1,0:T(8,128)(2,1)} %pad_maximum_fusion.16), channel_id=1, source_target_pairs={{0,16},{4,20},{16,24},{20,28},{24,8},{28,12},{8,0},{12,4},{1,17},{... | collective-permute-start | bytes 3538952 | tf_op jit(solution)/shard_map/ppermute | solution.py:64
  388.5 46.8 %collective-permute-start.66 = (bf16[240,2048]{1,0:T(8,128)(2,1)}, bf16[240,2048]{1,0:T(8,128)(2,1)}, u32[]{:S(2)}, u32[]{:S(2)}) collective-permute-start(bf16[240,2048]{1,0:T(8,128)(2,1)} %pad_maximum_fusion.29), channel_id=1, source_target_pairs={{0,8},{4,12},{16,0},{20,4},{24,16},{28,20},{8,24},{12,28},{1,9},{5... | collective-permute-start | bytes 2949128 | tf_op jit(solution)/shard_map/ppermute | solution.py:64
  413.6 21.7 %collective-permute-start.48 = (bf16[128,2048]{1,0:T(8,128)(2,1)S(1)}, bf16[128,2048]{1,0:T(8,128)(2,1)S(1)}, u32[]{:S(2)}, u32[]{:S(2)}) collective-permute-start(bf16[128,2048]{1,0:T(8,128)(2,1)S(1)} %slice.835), channel_id=1, source_target_pairs={{0,4},{4,0},{8,12},{12,8},{16,20},{20,16},{24,28},{28,24},{1,5},{5... | collective-permute-start | bytes 1572872 | tf_op jit(solution)/shard_map/ppermute | solution.py:42
  415.6 19.7 %collective-permute-start.50 = (bf16[128,2048]{1,0:T(8,128)(2,1)S(1)}, bf16[128,2048]{1,0:T(8,128)(2,1)S(1)}, u32[]{:S(2)}, u32[]{:S(2)}) collective-permute-start(bf16[128,2048]{1,0:T(8,128)(2,1)S(1)} %slice.836), channel_id=1, source_target_pairs={{0,2},{1,3},{2,0},{3,1},{4,6},{5,7},{6,4},{7,5},{8,10},{9,11},{10,... | collective-permute-start | bytes 1572872 | tf_op jit(solution)/shard_map/ppermute | solution.py:42
  418.9 33.5 %collective-permute-start.57 = (bf16[512,2048]{1,0:T(8,128)(2,1)S(1)}, bf16[512,2048]{1,0:T(8,128)(2,1)S(1)}, u32[]{:S(2)}, u32[]{:S(2)}) collective-permute-start(bf16[512,2048]{1,0:T(8,128)(2,1)S(1)} %pad_maximum_fusion.10), channel_id=1, source_target_pairs={{0,1},{1,0},{2,3},{3,2},{4,5},{5,4},{6,7},{7,6},{8,9},{9,8},{10,11... | collective-permute-start | bytes 6291464 | tf_op jit(solution)/shard_map/ppermute | solution.py:42
  437.2 41.3 %collective-permute-start.52 = (bf16[512,2048]{1,0:T(8,128)(2,1)S(1)}, bf16[512,2048]{1,0:T(8,128)(2,1)S(1)}, u32[]{:S(2)}, u32[]{:S(2)}) collective-permute-start(bf16[512,2048]{1,0:T(8,128)(2,1)S(1)} %copy-done.73), channel_id=1, source_target_pairs={{0,1},{1,0},{2,3},{3,2},{4,5},{5,4},{6,7},{7,6},{8,9},{9,8},{10,11... | collective-permute-start | bytes 6291464 | tf_op jit(solution)/shard_map/ppermute | solution.py:42
  447.2 93.5 %collective-permute-start.67 = (bf16[528,2048]{1,0:T(8,128)(2,1)}, bf16[528,2048]{1,0:T(8,128)(2,1)}, u32[]{:S(2)}, u32[]{:S(2)}) collective-permute-start(bf16[528,2048]{1,0:T(8,128)(2,1)} %get-tuple-element.158), channel_id=1, source_target_pairs={{0,16},{4,20},{16,24},{20,28},{24,8},{28,12},{8,0},{12,4},{1,17},{... | collective-permute-start | bytes 6488072 | tf_op jit(solution)/shard_map/ppermute | solution.py:64
  447.8 95.6 %collective-permute-start.68 = (bf16[528,2048]{1,0:T(8,128)(2,1)}, bf16[528,2048]{1,0:T(8,128)(2,1)}, u32[]{:S(2)}, u32[]{:S(2)}) collective-permute-start(bf16[528,2048]{1,0:T(8,128)(2,1)} %get-tuple-element.159), channel_id=1, source_target_pairs={{0,8},{4,12},{16,0},{20,4},{24,16},{28,20},{8,24},{12,28},{1,9},{5... | collective-permute-start | bytes 6488072 | tf_op jit(solution)/shard_map/ppermute | solution.py:64
  452.2 28.1 %collective-permute-start.59 = (bf16[512,2048]{1,0:T(8,128)(2,1)}, bf16[512,2048]{1,0:T(8,128)(2,1)}, u32[]{:S(2)}, u32[]{:S(2)}) collective-permute-start(bf16[512,2048]{1,0:T(8,128)(2,1)} %pad_maximum_fusion.11), channel_id=1, source_target_pairs={{0,1},{1,0},{2,3},{3,2},{4,5},{5,4},{6,7},{7,6},{8,9},{9,8},{10,11... | collective-permute-start | bytes 6291464 | tf_op jit(solution)/shard_map/ppermute | solution.py:42
  452.4 32.5 %collective-permute-start.51 = (bf16[512,2048]{1,0:T(8,128)(2,1)}, bf16[512,2048]{1,0:T(8,128)(2,1)}, u32[]{:S(2)}, u32[]{:S(2)}) collective-permute-start(bf16[512,2048]{1,0:T(8,128)(2,1)} %product.11), channel_id=1, source_target_pairs={{0,1},{1,0},{2,3},{3,2},{4,5},{5,4},{6,7},{7,6},{8,9},{9,8},{10,11... | collective-permute-start | bytes 6291464 | tf_op jit(solution)/shard_map/ppermute | solution.py:42
  478.5 26.1 %collective-permute-start.58 = (bf16[512,2048]{1,0:T(8,128)(2,1)S(1)}, bf16[512,2048]{1,0:T(8,128)(2,1)S(1)}, u32[]{:S(2)}, u32[]{:S(2)}) collective-permute-start(bf16[512,2048]{1,0:T(8,128)(2,1)S(1)} %convolution_convert_fusion.6), channel_id=1, source_target_pairs={{0,1},{1,0},{2,3},{3,2},{4,5},{5,4},{6,7},{7,6},{8,9},{9,8},{10,11... | collective-permute-start | bytes 6291464 | tf_op jit(solution)/shard_map/ppermute | solution.py:42
  480.3 19.5 %collective-permute-start.53 = (bf16[128,2048]{1,0:T(8,128)(2,1)S(1)}, bf16[128,2048]{1,0:T(8,128)(2,1)S(1)}, u32[]{:S(2)}, u32[]{:S(2)}) collective-permute-start(bf16[128,2048]{1,0:T(8,128)(2,1)S(1)} %get-tuple-element.250), channel_id=1, source_target_pairs={{0,4},{4,0},{8,12},{12,8},{16,20},{20,16},{24,28},{28,24},{1,5},{5... | collective-permute-start | bytes 1572872 | tf_op jit(solution)/shard_map/ppermute | solution.py:42
  500.9 28.3 %collective-permute-start.55 = (bf16[256,2048]{1,0:T(8,128)(2,1)}, bf16[256,2048]{1,0:T(8,128)(2,1)}, u32[]{:S(2)}, u32[]{:S(2)}) collective-permute-start(bf16[256,2048]{1,0:T(8,128)(2,1)} %pad_maximum_fusion.22), channel_id=1, source_target_pairs={{0,2},{1,3},{2,0},{3,1},{4,6},{5,7},{6,4},{7,5},{8,10},{9,11},{10,... | collective-permute-start | bytes 3145736 | tf_op jit(solution)/shard_map/ppermute | solution.py:42
  502.0 27.3 %collective-permute-start.56 = (bf16[256,2048]{1,0:T(8,128)(2,1)}, bf16[256,2048]{1,0:T(8,128)(2,1)}, u32[]{:S(2)}, u32[]{:S(2)}) collective-permute-start(bf16[256,2048]{1,0:T(8,128)(2,1)} %pad_maximum_fusion.23), channel_id=1, source_target_pairs={{0,4},{4,0},{8,12},{12,8},{16,20},{20,16},{24,28},{28,24},{1,5},{5... | collective-permute-start | bytes 3145736 | tf_op jit(solution)/shard_map/ppermute | solution.py:42
  533.4 23.1 %collective-permute-start.60 = (bf16[512,2048]{1,0:T(8,128)(2,1)S(1)}, bf16[512,2048]{1,0:T(8,128)(2,1)S(1)}, u32[]{:S(2)}, u32[]{:S(2)}) collective-permute-start(bf16[512,2048]{1,0:T(8,128)(2,1)S(1)} %convolution_convert_fusion.5), channel_id=1, source_target_pairs={{0,1},{1,0},{2,3},{3,2},{4,5},{5,4},{6,7},{7,6},{8,9},{9,8},{10,11... | collective-permute-start | bytes 6291464 | tf_op jit(solution)/shard_map/ppermute | solution.py:42
  544.4 22.0 %collective-permute-start.69 = (bf16[128,2048]{1,0:T(8,128)(2,1)S(1)}, bf16[128,2048]{1,0:T(8,128)(2,1)S(1)}, u32[]{:S(2)}, u32[]{:S(2)}) collective-permute-start(bf16[128,2048]{1,0:T(8,128)(2,1)S(1)} %pad_maximum_fusion.33), channel_id=1, source_target_pairs={{0,16},{4,20},{16,24},{20,28},{24,8},{28,12},{8,0},{12,4},{1,17},{... | collective-permute-start | bytes 1572872 | tf_op jit(solution)/shard_map/ppermute | solution.py:64
  545.1 24.9 %collective-permute-start.70 = (bf16[128,2048]{1,0:T(8,128)(2,1)S(1)}, bf16[128,2048]{1,0:T(8,128)(2,1)S(1)}, u32[]{:S(2)}, u32[]{:S(2)}) collective-permute-start(bf16[128,2048]{1,0:T(8,128)(2,1)S(1)} %pad_maximum_fusion.34), channel_id=1, source_target_pairs={{0,8},{4,12},{16,0},{20,4},{24,16},{28,20},{8,24},{12,28},{1,9},{5... | collective-permute-start | bytes 1572872 | tf_op jit(solution)/shard_map/ppermute | solution.py:64
  579.0 18.9 %collective-permute-start.73 = (f32[2,2,4,2,64]{4,2,3,1,0:T(4,128)S(1)}, f32[2,2,4,2,64]{4,2,3,1,0:T(4,128)S(1)}, u32[]{:S(2)}, u32[]{:S(2)}) collective-permute-start(f32[2,2,4,2,64]{4,2,3,1,0:T(4,128)S(1)} %slice.888), channel_id=1, source_target_pairs={{0,1},{1,0},{2,3},{3,2},{4,5},{5,4},{6,7},{7,6},{8,9},{9,8},{10,11... | collective-permute-start | bytes 24584 | tf_op jit(solution)/shard_map/ppermute | solution.py:42
  584.1 30.2 %collective-permute-start.63 = (bf16[256,2048]{1,0:T(8,128)(2,1)}, bf16[256,2048]{1,0:T(8,128)(2,1)S(1)}, u32[]{:S(2)}, u32[]{:S(2)}) collective-permute-start(bf16[256,2048]{1,0:T(8,128)(2,1)} %pad_maximum_fusion.24), channel_id=1, source_target_pairs={{0,2},{1,3},{2,0},{3,1},{4,6},{5,7},{6,4},{7,5},{8,10},{9,11},{10,... | collective-permute-start | bytes 3145736 | tf_op jit(solution)/shard_map/ppermute | solution.py:42
  585.1 29.2 %collective-permute-start.64 = (bf16[256,2048]{1,0:T(8,128)(2,1)}, bf16[256,2048]{1,0:T(8,128)(2,1)}, u32[]{:S(2)}, u32[]{:S(2)}) collective-permute-start(bf16[256,2048]{1,0:T(8,128)(2,1)} %pad_maximum_fusion.25), channel_id=1, source_target_pairs={{0,4},{4,0},{8,12},{12,8},{16,20},{20,16},{24,28},{28,24},{1,5},{5... | collective-permute-start | bytes 3145736 | tf_op jit(solution)/shard_map/ppermute | solution.py:42
  587.9 51.8 %collective-permute-start.71 = (bf16[256,2048]{1,0:T(8,128)(2,1)}, bf16[256,2048]{1,0:T(8,128)(2,1)}, u32[]{:S(2)}, u32[]{:S(2)}) collective-permute-start(bf16[256,2048]{1,0:T(8,128)(2,1)} %pad_maximum_fusion.26), channel_id=1, source_target_pairs={{0,16},{4,20},{16,24},{20,28},{24,8},{28,12},{8,0},{12,4},{1,17},{... | collective-permute-start | bytes 3145736 | tf_op jit(solution)/shard_map/ppermute | solution.py:64
  589.2 50.6 %collective-permute-start.72 = (bf16[256,2048]{1,0:T(8,128)(2,1)}, bf16[256,2048]{1,0:T(8,128)(2,1)}, u32[]{:S(2)}, u32[]{:S(2)}) collective-permute-start(bf16[256,2048]{1,0:T(8,128)(2,1)} %pad_maximum_fusion.27), channel_id=1, source_target_pairs={{0,8},{4,12},{16,0},{20,4},{24,16},{28,20},{8,24},{12,28},{1,9},{5... | collective-permute-start | bytes 3145736 | tf_op jit(solution)/shard_map/ppermute | solution.py:64
  614.3 23.7 %collective-permute-start.76 = (bf16[77,64]{1,0:T(8,128)(2,1)S(1)}, bf16[77,64]{1,0:T(8,128)(2,1)S(1)}, u32[]{:S(2)}, u32[]{:S(2)}) collective-permute-start(bf16[77,64]{1,0:T(8,128)(2,1)S(1)} %get-tuple-element.290), channel_id=1, source_target_pairs={{0,8},{4,12},{16,0},{20,4},{24,16},{28,20},{8,24},{12,28},{1,9},{5... | collective-permute-start | bytes 29576 | tf_op jit(solution)/shard_map/ppermute | solution.py:64
  615.5 22.6 %collective-permute-start.77 = (bf16[77,64]{1,0:T(8,128)(2,1)S(1)}, bf16[77,64]{1,0:T(8,128)(2,1)S(1)}, u32[]{:S(2)}, u32[]{:S(2)}) collective-permute-start(bf16[77,64]{1,0:T(8,128)(2,1)S(1)} %get-tuple-element.292), channel_id=1, source_target_pairs={{0,16},{4,20},{16,24},{20,28},{24,8},{28,12},{8,0},{12,4},{1,17},{... | collective-permute-start | bytes 29576 | tf_op jit(solution)/shard_map/ppermute | solution.py:64
  617.3 21.2 %collective-permute-start.78 = (bf16[77,64]{1,0:T(8,128)(2,1)S(1)}, bf16[77,64]{1,0:T(8,128)(2,1)S(1)}, u32[]{:S(2)}, u32[]{:S(2)}) collective-permute-start(bf16[77,64]{1,0:T(8,128)(2,1)S(1)} %get-tuple-element.291), channel_id=1, source_target_pairs={{0,24},{4,28},{16,8},{20,12},{24,0},{28,4},{8,16},{12,20},{1,25},{... | collective-permute-start | bytes 29576 | tf_op jit(solution)/shard_map/ppermute | solution.py:64
  (130 other events, 1387.5 us)
